TPU v7x, 32 devices: a whole 2x2x4 slice. The times are simulated.
32 devices in a mesh: segment: 4 (over y, core), expert: 8 (over z, x).
Axes of the slice: x: 2, y: 2, z: 4, core: 2. Of those that a mesh axis runs over, the one named last changes fastest.
Arguments:
- state: bfloat16 [4, 64, 2048], P('segment', 'expert'), may hold values from -24 to 24
- routes: int32 [4, 4, 64, 2], P(None, 'segment', 'expert'), may hold values from 0 to 3, all different within a row; in each aligned block of 8 rows (0 to 7, 8 to 15, ..., all dimensions but the last counted through in order) at most 6 rows name the same one
- gates: float32 [4, 4, 64, 2], P(None, 'segment', 'expert'), may hold values from 0.2 to 1
- norm_gain: float32 [2, 4, 2048], P(None, 'segment'), may hold values from 0.25 to 1.75
- w_gate: bfloat16 [2, 4, 5120, 2048], P(None, 'segment', 'expert'), may hold values from -0.125 to 0.125
- w_up: bfloat16 [2, 4, 5120, 2048], P(None, 'segment', 'expert'), may hold values from -0.125 to 0.125
- w_down: bfloat16 [2, 4, 5120, 2048], P(None, 'segment', 'expert'), may hold values from -0.15625 to 0.15625
- spare_gate: bfloat16 [2, 4, 1280, 2048], P(None, 'segment', 'expert'), may hold values from -0.125 to 0.125
- spare_up: bfloat16 [2, 4, 1280, 2048], P(None, 'segment', 'expert'), may hold values from -0.125 to 0.125
- spare_down: bfloat16 [2, 4, 1280, 2048], P(None, 'segment', 'expert'), may hold values from -0.15625 to 0.15625
Outputs:
- final: bfloat16 [4, 64, 2048], P('segment', 'expert')
Inputs may be any that keep to these rules, and one draw needn't show every extreme that they name: `routes`: each row names 2 different experts. Within the 8 rows of one device at one tick (aligned blocks), no expert is named by more than 6 rows, and some blocks reach 6.
All inputs are finite; a program needn't handle non-finite values.
Results may differ from a plain program's by a relative error of at most 0.012.
Values may be sent and summed in bfloat16 or wider, within the bound.
No kernel may reach another device: no remote copies, remote signals or barrier semaphores. Data moves between devices by JAX's collectives and lax.ppermute only.
A program may use at most 64 MiB of HBM per device.

v0:
```python
import jax
import jax.numpy as jnp
from jax import lax
from jax.sharding import PartitionSpec as P

EXPERTS = 4
TICKS = 4
CAP = 4


EPSILON = 1e-06


def from_behind(value, axis, steps):
    count = lax.axis_size(axis)
    pairs = [(source, (source + steps) % count) for source in range(count)]
    return lax.ppermute(value, axis, pairs)


def rms_normed(rows, norm_scale):
    values = rows.astype(jnp.float32)
    row_scale = lax.rsqrt(jnp.mean(values * values, axis=-1, keepdims=True) + EPSILON)
    return (values * row_scale * norm_scale).astype(jnp.bfloat16)


def expert_rows(rows, gate_block, up_block, down_block):
    contract = (((1,), (1,)), ((), ()))
    gate_pre = lax.dot_general(rows, gate_block, contract, preferred_element_type=jnp.float32)
    up_pre = lax.dot_general(rows, up_block, contract, preferred_element_type=jnp.float32)
    hidden = (jax.nn.silu(gate_pre) * up_pre).astype(jnp.bfloat16)
    return jnp.dot(hidden, down_block, preferred_element_type=jnp.float32).astype(jnp.bfloat16)


def group_of(section, tick_idx, segments):
    start_segment = (section - tick_idx) % segments
    first_group = jnp.where((start_segment % 2 == 1) & (start_segment + TICKS <= segments), 1, 0)
    return (first_group + jnp.where(start_segment + tick_idx >= segments, 1, 0)).astype(jnp.int32)


def spare_served(rows, gate_block, up_block, down_block):
    members = lax.axis_size("expert")
    tok_dev = rows.shape[0]
    model_width = rows.shape[1]
    gathered = expert_rows(
        lax.all_gather(rows, "expert", axis=0, tiled=True), gate_block, up_block, down_block
    )
    returned = lax.all_to_all(
        gathered.reshape(members, tok_dev, model_width),
        "expert",
        split_axis=0,
        concat_axis=0,
        tiled=True,
    )
    return jnp.sum(returned.astype(jnp.float32), axis=0)


def on_device(
    state, routes, gates, norm_gain, w_gate, w_up, w_down, spare_gate, spare_up, spare_down
):
    segments = lax.axis_size("segment")
    segment_idx = lax.axis_index("segment")
    members = lax.axis_size("expert")
    split_count = members // EXPERTS
    tok_dev = state.shape[1]
    model_width = state.shape[2]
    current = state[0]
    labels = jnp.arange(EXPERTS, dtype=jnp.int32)
    for tick_idx in range(TICKS):
        group_idx = group_of(segment_idx, tick_idx, segments)
        spare_group = group_of(segment_idx + segments - 1, tick_idx, segments)
        norm_scale = lax.dynamic_index_in_dim(norm_gain[:, 0], group_idx, 0, keepdims=False)
        gate_block = lax.dynamic_index_in_dim(w_gate[:, 0], group_idx, 0, keepdims=False)
        up_block = lax.dynamic_index_in_dim(w_up[:, 0], group_idx, 0, keepdims=False)
        down_block = lax.dynamic_index_in_dim(w_down[:, 0], group_idx, 0, keepdims=False)
        spare_g = lax.dynamic_index_in_dim(spare_gate[:, 0], spare_group, 0, keepdims=False)
        spare_u = lax.dynamic_index_in_dim(spare_up[:, 0], spare_group, 0, keepdims=False)
        spare_d = lax.dynamic_index_in_dim(spare_down[:, 0], spare_group, 0, keepdims=False)
        normed = rms_normed(current, norm_scale)
        chosen = routes[tick_idx, 0]
        weights = gates[tick_idx, 0]
        matches = chosen[:, :, None] == labels[None, None, :]
        routed = jnp.sum(jnp.where(matches, weights[:, :, None], jnp.float32(0.0)), axis=1)
        member_of = jnp.any(matches, axis=1)
        taken = member_of.astype(jnp.int32)
        position = jnp.cumsum(taken, axis=0, dtype=jnp.int32) - taken
        inside = member_of & (position < CAP)
        spill = jnp.sum(jnp.where(inside, jnp.float32(0.0), routed), axis=1)
        slot_ids = jnp.arange(CAP, dtype=jnp.int32)
        select = inside[:, :, None] & (position[:, :, None] == slot_ids[None, None, :])
        picker = select.astype(jnp.bfloat16)
        outgoing = jnp.einsum(
            "tej,td->ejd", picker, normed, preferred_element_type=jnp.float32
        ).astype(jnp.bfloat16)
        outgoing = jnp.repeat(outgoing, split_count, axis=0)
        arrived = lax.all_to_all(outgoing, "expert", split_axis=0, concat_axis=0, tiled=True)
        slot_count = arrived.shape[1]
        partial_value = expert_rows(
            arrived.reshape(-1, model_width), gate_block, up_block, down_block
        )
        returned = lax.all_to_all(
            partial_value.reshape(members, slot_count, model_width),
            "expert",
            split_axis=0,
            concat_axis=0,
            tiled=True,
        )
        coefficient = jnp.where(select, routed[:, :, None], jnp.float32(0.0))
        coefficient = jnp.repeat(coefficient, split_count, axis=1).reshape(tok_dev, members * CAP)
        combined = jnp.dot(
            coefficient,
            returned.reshape(members * CAP, model_width).astype(jnp.float32),
            precision=lax.Precision.HIGHEST,
        )
        stacked = jnp.stack([spare_g, spare_u, spare_d])
        fetched = from_behind(stacked, "segment", -1)
        spare_out = spare_served(normed, fetched[0], fetched[1], fetched[2])
        combined = combined + spill[:, None] * spare_out
        current = (current.astype(jnp.float32) + combined).astype(jnp.bfloat16)
        if tick_idx + 1 < TICKS:
            current = from_behind(current, "segment", 1)
    return current[None]


def solution(mesh):
    return jax.shard_map(
        on_device,
        mesh=mesh,
        in_specs=(
            P("segment", "expert", None),
            P(None, "segment", "expert", None),
            P(None, "segment", "expert", None),
            P(None, "segment", None),
            P(None, "segment", "expert", None),
            P(None, "segment", "expert", None),
            P(None, "segment", "expert", None),
            P(None, "segment", "expert", None),
            P(None, "segment", "expert", None),
            P(None, "segment", "expert", None),
        ),
        out_specs=P("segment", "expert", None),
        check_vma=False,
    )
```

profile of v0, /device:TPU:0, one launch (start us, length us, event | category | flops | bytes accessed | tf_op | source)
XLA Modules:
  0.0 305.4 jit_solution(5004758579361354189)
XLA Ops:
  0.0 2.1 dynamic-slice_bitcast_fusion.2
  3.2 1.5 pad_maximum_fusion.2
  4.7 2.4 collective-permute-start.4
  7.2 1.5 pad_maximum_fusion.1
  9.4 1.5 pad_maximum_fusion
  12.4 5.8 %all-to-all-start = ((bf16[8,4,2048]{2,1,0:T(4,128)(2,1)}), bf16[8,4,2048]{2,1,0:T(4,128)(2,1)S(1)}, u32[]{:S(2)}, u32[]{:S(2)}) async-start(bf16[8,4,2048]{2,1,0:T(4,128)(2,1)} %bitcast.7), calls=%async_computation | async-start | bytes 262144 | tf_op jit(solution)/shard_map/all_to_all | solution.py:95
  18.2 1.5 pad_maximum_fusion.3
  20.2 31.2 %all_gather.12 = bf16[64,2048]{1,0:T(8,128)(2,1)S(1)} all-gather(bf16[8,2048]{1,0:T(8,128)(2,1)S(1)} %fusion.132), channel_id=1, replica_groups=mesh['segment'=4,'expert'=8] {'expert'}, dimensions={0}, use_global_device_ids=true | all-gather | bytes 294912 | tf_op jit(solution)/shard_map/all_gather | solution.py:45
  51.4 2.6 fusion.22
  54.0 4.1 %fusion.40 = bf16[32,2048]{1,0:T(8,128)(2,1)S(1)} fusion(bf16[2,1,640,2048]{3,2,1,0:T(8,128)(2,1)} %param.16, s32[]{:T(128)S(6)} %select_n.202, bf16[32,2048]{1,0:T(8,128)(2,1)S(1)} %reshape.203, bf16[2,1,640,2048]{3,2,1,0:T(8,128)(2,1)} %param.15, f32[32,640]{1,0:T(8,128)S(1)} %fusion.22), kind=kOutput, calls=%fused_computation.44 | convolution fusion | flops 167960576 | bytes 5587968 | tf_op jit(solution)/shard_map/dot_general | solution.py:31
  58.9 5.3 %all-to-all-start.1 = ((bf16[8,4,2048]{2,1,0:T(4,128)(2,1)}), bf16[8,4,2048]{2,1,0:T(4,128)(2,1)S(1)}, u32[]{:S(2)}, u32[]{:S(2)}) async-start(bf16[8,4,2048]{2,1,0:T(4,128)(2,1)} %reshape.204), calls=%async_computation.1 | async-start | bytes 262144 | tf_op jit(solution)/shard_map/all_to_all | solution.py:100
  64.2 7.6 %collective-permute-done = bf16[3,160,2048]{2,1,0:T(8,128)(2,1)} collective-permute-done((bf16[3,160,2048]{2,1,0:T(8,128)(2,1)}, bf16[3,160,2048]{2,1,0:T(8,128)(2,1)}, u32[]{:S(2)}, u32[]{:S(2)}) %collective-permute-start) | collective-permute-done | bytes 1966112 | tf_op jit(solution)/shard_map/ppermute | solution.py:17
  71.8 1.4 fusion.99
  73.2 2.7 fusion.36
  75.9 5.8 %all-to-all-start.2 = ((bf16[8,8,2048]{2,1,0:T(8,128)(2,1)}), bf16[8,8,2048]{2,1,0:T(8,128)(2,1)S(1)}, u32[]{:S(2)}, u32[]{:S(2)}) async-start(bf16[8,8,2048]{2,1,0:T(8,128)(2,1)} %fusion.36), calls=%async_computation.2 | async-start | bytes 524288 | tf_op jit(solution)/shard_map/all_to_all | solution.py:47
  81.8 9.8 %all-to-all-done.2 = bf16[8,8,2048]{2,1,0:T(8,128)(2,1)S(1)} async-done(((bf16[8,8,2048]{2,1,0:T(8,128)(2,1)}), bf16[8,8,2048]{2,1,0:T(8,128)(2,1)S(1)}, u32[]{:S(2)}, u32[]{:S(2)}) %all-to-all-start.2) | async-done | bytes 262176 | tf_op jit(solution)/shard_map/all_to_all | solution.py:47
  92.0 3.3 %collective-permute-done.1 = bf16[8,2048]{1,0:T(8,128)(2,1)S(1)} collective-permute-done((bf16[8,2048]{1,0:T(8,128)(2,1)S(1)}, bf16[8,2048]{1,0:T(8,128)(2,1)S(1)}, u32[]{:S(2)}, u32[]{:S(2)}) %collective-permute-start.1) | collective-permute-done | bytes 32800 | tf_op jit(solution)/shard_map/ppermute | solution.py:17
  96.4 3.9 %all-to-all-start.3 = ((bf16[8,4,2048]{2,1,0:T(4,128)(2,1)}), bf16[8,4,2048]{2,1,0:T(4,128)(2,1)S(1)}, u32[]{:S(2)}, u32[]{:S(2)}) async-start(bf16[8,4,2048]{2,1,0:T(4,128)(2,1)} %bitcast.23), calls=%async_computation.3 | async-start | bytes 262144 | tf_op jit(solution)/shard_map/all_to_all | solution.py:95
  100.5 31.4 %all_gather.13 = bf16[64,2048]{1,0:T(8,128)(2,1)S(1)} all-gather(bf16[8,2048]{1,0:T(8,128)(2,1)S(1)} %fusion.123), channel_id=1, replica_groups=mesh['segment'=4,'expert'=8] {'expert'}, dimensions={0}, use_global_device_ids=true | all-gather | bytes 294912 | tf_op jit(solution)/shard_map/all_gather | solution.py:45
  132.0 2.6 fusion.16
  134.6 4.1 %fusion.43 = bf16[32,2048]{1,0:T(8,128)(2,1)S(1)} fusion(bf16[2,1,640,2048]{3,2,1,0:T(8,128)(2,1)} %param.16, s32[]{:T(128)S(6)} %select_n.215, bf16[32,2048]{1,0:T(8,128)(2,1)S(1)} %reshape.208, bf16[2,1,640,2048]{3,2,1,0:T(8,128)(2,1)} %param.15, f32[32,640]{1,0:T(8,128)S(1)} %fusion.16), kind=kOutput, calls=%fused_computation.45 | convolution fusion | flops 167960576 | bytes 5587968 | tf_op jit(solution)/shard_map/dot_general | solution.py:31
  139.4 5.5 %all-to-all-start.4 = ((bf16[8,4,2048]{2,1,0:T(4,128)(2,1)}), bf16[8,4,2048]{2,1,0:T(4,128)(2,1)S(1)}, u32[]{:S(2)}, u32[]{:S(2)}) async-start(bf16[8,4,2048]{2,1,0:T(4,128)(2,1)} %reshape.209), calls=%async_computation.4 | async-start | bytes 262144 | tf_op jit(solution)/shard_map/all_to_all | solution.py:100
  144.9 1.4 fusion.97
  146.3 2.7 fusion.37
  149.0 3.6 %all-to-all-done.4 = bf16[8,4,2048]{2,1,0:T(4,128)(2,1)S(1)} async-done(((bf16[8,4,2048]{2,1,0:T(4,128)(2,1)}), bf16[8,4,2048]{2,1,0:T(4,128)(2,1)S(1)}, u32[]{:S(2)}, u32[]{:S(2)}) %all-to-all-start.4) | async-done | bytes 131104 | tf_op jit(solution)/shard_map/all_to_all | solution.py:100
  152.6 3.9 %all-to-all-start.5 = ((bf16[8,8,2048]{2,1,0:T(8,128)(2,1)}), bf16[8,8,2048]{2,1,0:T(8,128)(2,1)S(1)}, u32[]{:S(2)}, u32[]{:S(2)}) async-start(bf16[8,8,2048]{2,1,0:T(8,128)(2,1)} %fusion.37), calls=%async_computation.5 | async-start | bytes 524288 | tf_op jit(solution)/shard_map/all_to_all | solution.py:47
  156.6 8.1 %all-to-all-done.5 = bf16[8,8,2048]{2,1,0:T(8,128)(2,1)S(1)} async-done(((bf16[8,8,2048]{2,1,0:T(8,128)(2,1)}), bf16[8,8,2048]{2,1,0:T(8,128)(2,1)S(1)}, u32[]{:S(2)}, u32[]{:S(2)}) %all-to-all-start.5) | async-done | bytes 262176 | tf_op jit(solution)/shard_map/all_to_all | solution.py:47
  165.3 3.1 %collective-permute-done.3 = bf16[8,2048]{1,0:T(8,128)(2,1)S(1)} collective-permute-done((bf16[8,2048]{1,0:T(8,128)(2,1)S(1)}, bf16[8,2048]{1,0:T(8,128)(2,1)S(1)}, u32[]{:S(2)}, u32[]{:S(2)}) %collective-permute-start.3) | collective-permute-done | bytes 32800 | tf_op jit(solution)/shard_map/ppermute | solution.py:17
  169.5 3.4 %all-to-all-start.6 = ((bf16[8,4,2048]{2,1,0:T(4,128)(2,1)}), bf16[8,4,2048]{2,1,0:T(4,128)(2,1)S(1)}, u32[]{:S(2)}, u32[]{:S(2)}) async-start(bf16[8,4,2048]{2,1,0:T(4,128)(2,1)} %bitcast.39), calls=%async_computation.6 | async-start | bytes 262144 | tf_op jit(solution)/shard_map/all_to_all | solution.py:95
  172.9 31.4 %all_gather.14 = bf16[64,2048]{1,0:T(8,128)(2,1)S(1)} all-gather(bf16[8,2048]{1,0:T(8,128)(2,1)S(1)} %fusion.126), channel_id=1, replica_groups=mesh['segment'=4,'expert'=8] {'expert'}, dimensions={0}, use_global_device_ids=true | all-gather | bytes 294912 | tf_op jit(solution)/shard_map/all_gather | solution.py:45
  204.2 1.4 fusion.95
  205.7 2.7 fusion.38
  208.4 5.3 %all-to-all-start.8 = ((bf16[8,8,2048]{2,1,0:T(8,128)(2,1)}), bf16[8,8,2048]{2,1,0:T(8,128)(2,1)S(1)}, u32[]{:S(2)}, u32[]{:S(2)}) async-start(bf16[8,8,2048]{2,1,0:T(8,128)(2,1)} %fusion.38), calls=%async_computation.8 | async-start | bytes 524288 | tf_op jit(solution)/shard_map/all_to_all | solution.py:47
  213.7 2.6 fusion.10
  216.3 4.1 %fusion.46 = bf16[32,2048]{1,0:T(8,128)(2,1)S(1)} fusion(bf16[2,1,640,2048]{3,2,1,0:T(8,128)(2,1)} %param.16, s32[]{:T(128)S(6)} %select_n.228, bf16[32,2048]{1,0:T(8,128)(2,1)S(1)} %reshape.213, bf16[2,1,640,2048]{3,2,1,0:T(8,128)(2,1)} %param.15, f32[32,640]{1,0:T(8,128)S(1)} %fusion.10), kind=kOutput, calls=%fused_computation.46 | convolution fusion | flops 167960576 | bytes 5587968 | tf_op jit(solution)/shard_map/dot_general | solution.py:31
  221.9 5.3 %all-to-all-start.7 = ((bf16[8,4,2048]{2,1,0:T(4,128)(2,1)}), bf16[8,4,2048]{2,1,0:T(4,128)(2,1)S(1)}, u32[]{:S(2)}, u32[]{:S(2)}) async-start(bf16[8,4,2048]{2,1,0:T(4,128)(2,1)} %reshape.214), calls=%async_computation.7 | async-start | bytes 262144 | tf_op jit(solution)/shard_map/all_to_all | solution.py:100
  227.2 7.3 %all-to-all-done.7 = bf16[8,4,2048]{2,1,0:T(4,128)(2,1)S(1)} async-done(((bf16[8,4,2048]{2,1,0:T(4,128)(2,1)}), bf16[8,4,2048]{2,1,0:T(4,128)(2,1)S(1)}, u32[]{:S(2)}, u32[]{:S(2)}) %all-to-all-start.7) | async-done | bytes 131104 | tf_op jit(solution)/shard_map/all_to_all | solution.py:100
  234.9 3.3 %collective-permute-done.5 = bf16[8,2048]{1,0:T(8,128)(2,1)S(1)} collective-permute-done((bf16[8,2048]{1,0:T(8,128)(2,1)S(1)}, bf16[8,2048]{1,0:T(8,128)(2,1)S(1)}, u32[]{:S(2)}, u32[]{:S(2)}) %collective-permute-start.5) | collective-permute-done | bytes 32800 | tf_op jit(solution)/shard_map/ppermute | solution.py:17
  239.3 3.4 %all-to-all-start.9 = ((bf16[8,4,2048]{2,1,0:T(4,128)(2,1)}), bf16[8,4,2048]{2,1,0:T(4,128)(2,1)S(1)}, u32[]{:S(2)}, u32[]{:S(2)}) async-start(bf16[8,4,2048]{2,1,0:T(4,128)(2,1)} %bitcast.55), calls=%async_computation.9 | async-start | bytes 262144 | tf_op jit(solution)/shard_map/all_to_all | solution.py:95
  242.7 31.3 %all_gather.15 = bf16[64,2048]{1,0:T(8,128)(2,1)S(1)} all-gather(bf16[8,2048]{1,0:T(8,128)(2,1)S(1)} %fusion.129), channel_id=1, replica_groups=mesh['segment'=4,'expert'=8] {'expert'}, dimensions={0}, use_global_device_ids=true | all-gather | bytes 294912 | tf_op jit(solution)/shard_map/all_gather | solution.py:45
  274.0 1.4 fusion.93
  275.4 2.7 fusion.39
  278.1 5.6 %all-to-all-start.11 = ((bf16[8,8,2048]{2,1,0:T(8,128)(2,1)}), bf16[8,8,2048]{2,1,0:T(8,128)(2,1)S(1)}, u32[]{:S(2)}, u32[]{:S(2)}) async-start(bf16[8,8,2048]{2,1,0:T(8,128)(2,1)} %fusion.39), calls=%async_computation.11 | async-start | bytes 524288 | tf_op jit(solution)/shard_map/all_to_all | solution.py:47
  283.7 2.6 fusion.4
  286.3 4.1 %fusion.49 = bf16[32,2048]{1,0:T(8,128)(2,1)S(1)} fusion(bf16[2,1,640,2048]{3,2,1,0:T(8,128)(2,1)} %param.16, s32[]{:T(128)S(6)} %select_n.241, bf16[32,2048]{1,0:T(8,128)(2,1)S(1)} %reshape.218, bf16[2,1,640,2048]{3,2,1,0:T(8,128)(2,1)} %param.15, f32[32,640]{1,0:T(8,128)S(1)} %fusion.4), kind=kOutput, calls=%fused_computation.47 | convolution fusion | flops 167960576 | bytes 5587968 | tf_op jit(solution)/shard_map/dot_general | solution.py:31
  291.9 5.2 %all-to-all-start.10 = ((bf16[8,4,2048]{2,1,0:T(4,128)(2,1)}), bf16[8,4,2048]{2,1,0:T(4,128)(2,1)S(1)}, u32[]{:S(2)}, u32[]{:S(2)}) async-start(bf16[8,4,2048]{2,1,0:T(4,128)(2,1)} %reshape.219), calls=%async_computation.10 | async-start | bytes 262144 | tf_op jit(solution)/shard_map/all_to_all | solution.py:100
  297.2 7.3 %all-to-all-done.10 = bf16[8,4,2048]{2,1,0:T(4,128)(2,1)S(1)} async-done(((bf16[8,4,2048]{2,1,0:T(4,128)(2,1)}), bf16[8,4,2048]{2,1,0:T(4,128)(2,1)S(1)}, u32[]{:S(2)}, u32[]{:S(2)}) %all-to-all-start.10) | async-done | bytes 131104 | tf_op jit(solution)/shard_map/all_to_all | solution.py:100
  304.5 0.9 fusion.60
  (101 shorter events, 13.2 us)
Async XLA Ops:
  0.0 2.1 copy-start
  0.0 2.5 copy-start.1
  4.7 199.5 %collective-permute-start.4 = (bf16[3,160,2048]{2,1,0:T(8,128)(2,1)}, bf16[3,160,2048]{2,1,0:T(8,128)(2,1)}, u32[]{:S(2)}, u32[]{:S(2)}) collective-permute-start(bf16[3,160,2048]{2,1,0:T(8,128)(2,1)} %pad_maximum_fusion.2), channel_id=1, source_target_pairs={{0,24},{8,0},{16,8},{24,16},{1,25},{9,1},{17,9},{25,17},{2,26},{10... | collective-permute-start | bytes 5898248 | tf_op jit(solution)/shard_map/ppermute | solution.py:17
  8.7 136.2 %collective-permute-start.2 = (bf16[3,160,2048]{2,1,0:T(8,128)(2,1)}, bf16[3,160,2048]{2,1,0:T(8,128)(2,1)}, u32[]{:S(2)}, u32[]{:S(2)}) collective-permute-start(bf16[3,160,2048]{2,1,0:T(8,128)(2,1)} %pad_maximum_fusion.1), channel_id=1, source_target_pairs={{0,24},{8,0},{16,8},{24,16},{1,25},{9,1},{17,9},{25,17},{2,26},{10... | collective-permute-start | bytes 5898248 | tf_op jit(solution)/shard_map/ppermute | solution.py:17
  9.3 1.5 copy-start.2
  9.3 1.6 copy-start.4
  9.3 1.6 copy-start.5
  9.3 2.1 copy-start.3
  10.8 61.0 %collective-permute-start = (bf16[3,160,2048]{2,1,0:T(8,128)(2,1)}, bf16[3,160,2048]{2,1,0:T(8,128)(2,1)}, u32[]{:S(2)}, u32[]{:S(2)}) collective-permute-start(bf16[3,160,2048]{2,1,0:T(8,128)(2,1)} %pad_maximum_fusion), channel_id=1, source_target_pairs={{0,24},{8,0},{16,8},{24,16},{1,25},{9,1},{17,9},{25,17},{2,26},{10... | collective-permute-start | bytes 5898248 | tf_op jit(solution)/shard_map/ppermute | solution.py:17
  12.4 39.0 %all-to-all-start = ((bf16[8,4,2048]{2,1,0:T(4,128)(2,1)}), bf16[8,4,2048]{2,1,0:T(4,128)(2,1)S(1)}, u32[]{:S(2)}, u32[]{:S(2)}) async-start(bf16[8,4,2048]{2,1,0:T(4,128)(2,1)} %bitcast.7), calls=%async_computation | async-start | bytes 262144 | tf_op jit(solution)/shard_map/all_to_all | solution.py:95
  19.7 254.3 %collective-permute-start.6 = (bf16[3,160,2048]{2,1,0:T(8,128)(2,1)}, bf16[3,160,2048]{2,1,0:T(8,128)(2,1)}, u32[]{:S(2)}, u32[]{:S(2)}) collective-permute-start(bf16[3,160,2048]{2,1,0:T(8,128)(2,1)} %pad_maximum_fusion.3), channel_id=1, source_target_pairs={{0,24},{8,0},{16,8},{24,16},{1,25},{9,1},{17,9},{25,17},{2,26},{10... | collective-permute-start | bytes 5898248 | tf_op jit(solution)/shard_map/ppermute | solution.py:17
  58.9 17.0 %all-to-all-start.1 = ((bf16[8,4,2048]{2,1,0:T(4,128)(2,1)}), bf16[8,4,2048]{2,1,0:T(4,128)(2,1)S(1)}, u32[]{:S(2)}, u32[]{:S(2)}) async-start(bf16[8,4,2048]{2,1,0:T(4,128)(2,1)} %reshape.204), calls=%async_computation.1 | async-start | bytes 262144 | tf_op jit(solution)/shard_map/all_to_all | solution.py:100
  75.9 15.7 %all-to-all-start.2 = ((bf16[8,8,2048]{2,1,0:T(8,128)(2,1)}), bf16[8,8,2048]{2,1,0:T(8,128)(2,1)S(1)}, u32[]{:S(2)}, u32[]{:S(2)}) async-start(bf16[8,8,2048]{2,1,0:T(8,128)(2,1)} %fusion.36), calls=%async_computation.2 | async-start | bytes 524288 | tf_op jit(solution)/shard_map/all_to_all | solution.py:47
  91.9 3.4 %collective-permute-start.1 = (bf16[8,2048]{1,0:T(8,128)(2,1)S(1)}, bf16[8,2048]{1,0:T(8,128)(2,1)S(1)}, u32[]{:S(2)}, u32[]{:S(2)}) collective-permute-start(bf16[8,2048]{1,0:T(8,128)(2,1)S(1)} %fusion.56), channel_id=1, source_target_pairs={{0,8},{8,16},{16,24},{24,0},{1,9},{9,17},{17,25},{25,1},{2,10},{10... | collective-permute-start | bytes 98312 | tf_op jit(solution)/shard_map/ppermute | solution.py:17
  96.4 35.6 %all-to-all-start.3 = ((bf16[8,4,2048]{2,1,0:T(4,128)(2,1)}), bf16[8,4,2048]{2,1,0:T(4,128)(2,1)S(1)}, u32[]{:S(2)}, u32[]{:S(2)}) async-start(bf16[8,4,2048]{2,1,0:T(4,128)(2,1)} %bitcast.23), calls=%async_computation.3 | async-start | bytes 262144 | tf_op jit(solution)/shard_map/all_to_all | solution.py:95
  139.4 13.2 %all-to-all-start.4 = ((bf16[8,4,2048]{2,1,0:T(4,128)(2,1)}), bf16[8,4,2048]{2,1,0:T(4,128)(2,1)S(1)}, u32[]{:S(2)}, u32[]{:S(2)}) async-start(bf16[8,4,2048]{2,1,0:T(4,128)(2,1)} %reshape.209), calls=%async_computation.4 | async-start | bytes 262144 | tf_op jit(solution)/shard_map/all_to_all | solution.py:100
  152.6 12.2 %all-to-all-start.5 = ((bf16[8,8,2048]{2,1,0:T(8,128)(2,1)}), bf16[8,8,2048]{2,1,0:T(8,128)(2,1)S(1)}, u32[]{:S(2)}, u32[]{:S(2)}) async-start(bf16[8,8,2048]{2,1,0:T(8,128)(2,1)} %fusion.37), calls=%async_computation.5 | async-start | bytes 524288 | tf_op jit(solution)/shard_map/all_to_all | solution.py:47
  165.1 3.4 %collective-permute-start.3 = (bf16[8,2048]{1,0:T(8,128)(2,1)S(1)}, bf16[8,2048]{1,0:T(8,128)(2,1)S(1)}, u32[]{:S(2)}, u32[]{:S(2)}) collective-permute-start(bf16[8,2048]{1,0:T(8,128)(2,1)S(1)} %fusion.57), channel_id=1, source_target_pairs={{0,8},{8,16},{16,24},{24,0},{1,9},{9,17},{17,25},{25,1},{2,10},{10... | collective-permute-start | bytes 98312 | tf_op jit(solution)/shard_map/ppermute | solution.py:17
  169.5 38.8 %all-to-all-start.6 = ((bf16[8,4,2048]{2,1,0:T(4,128)(2,1)}), bf16[8,4,2048]{2,1,0:T(4,128)(2,1)S(1)}, u32[]{:S(2)}, u32[]{:S(2)}) async-start(bf16[8,4,2048]{2,1,0:T(4,128)(2,1)} %bitcast.39), calls=%async_computation.6 | async-start | bytes 262144 | tf_op jit(solution)/shard_map/all_to_all | solution.py:95
  208.4 13.6 %all-to-all-start.8 = ((bf16[8,8,2048]{2,1,0:T(8,128)(2,1)}), bf16[8,8,2048]{2,1,0:T(8,128)(2,1)S(1)}, u32[]{:S(2)}, u32[]{:S(2)}) async-start(bf16[8,8,2048]{2,1,0:T(8,128)(2,1)} %fusion.38), calls=%async_computation.8 | async-start | bytes 524288 | tf_op jit(solution)/shard_map/all_to_all | solution.py:47
  221.9 12.6 %all-to-all-start.7 = ((bf16[8,4,2048]{2,1,0:T(4,128)(2,1)}), bf16[8,4,2048]{2,1,0:T(4,128)(2,1)S(1)}, u32[]{:S(2)}, u32[]{:S(2)}) async-start(bf16[8,4,2048]{2,1,0:T(4,128)(2,1)} %reshape.214), calls=%async_computation.7 | async-start | bytes 262144 | tf_op jit(solution)/shard_map/all_to_all | solution.py:100
  234.8 3.4 %collective-permute-start.5 = (bf16[8,2048]{1,0:T(8,128)(2,1)S(1)}, bf16[8,2048]{1,0:T(8,128)(2,1)S(1)}, u32[]{:S(2)}, u32[]{:S(2)}) collective-permute-start(bf16[8,2048]{1,0:T(8,128)(2,1)S(1)} %fusion.58), channel_id=1, source_target_pairs={{0,8},{8,16},{16,24},{24,0},{1,9},{9,17},{17,25},{25,1},{2,10},{10... | collective-permute-start | bytes 98312 | tf_op jit(solution)/shard_map/ppermute | solution.py:17
  239.3 38.8 %all-to-all-start.9 = ((bf16[8,4,2048]{2,1,0:T(4,128)(2,1)}), bf16[8,4,2048]{2,1,0:T(4,128)(2,1)S(1)}, u32[]{:S(2)}, u32[]{:S(2)}) async-start(bf16[8,4,2048]{2,1,0:T(4,128)(2,1)} %bitcast.55), calls=%async_computation.9 | async-start | bytes 262144 | tf_op jit(solution)/shard_map/all_to_all | solution.py:95
  278.1 13.8 %all-to-all-start.11 = ((bf16[8,8,2048]{2,1,0:T(8,128)(2,1)}), bf16[8,8,2048]{2,1,0:T(8,128)(2,1)S(1)}, u32[]{:S(2)}, u32[]{:S(2)}) async-start(bf16[8,8,2048]{2,1,0:T(8,128)(2,1)} %fusion.39), calls=%async_computation.11 | async-start | bytes 524288 | tf_op jit(solution)/shard_map/all_to_all | solution.py:47
  291.9 12.6 %all-to-all-start.10 = ((bf16[8,4,2048]{2,1,0:T(4,128)(2,1)}), bf16[8,4,2048]{2,1,0:T(4,128)(2,1)S(1)}, u32[]{:S(2)}, u32[]{:S(2)}) async-start(bf16[8,4,2048]{2,1,0:T(4,128)(2,1)} %reshape.219), calls=%async_computation.10 | async-start | bytes 262144 | tf_op jit(solution)/shard_map/all_to_all | solution.py:100
where the time goes:
time: 307 us; the launch traced here: 305 us
  blocking collectives  125 us (41%)
  starting transfers between devices  62.1 us (20%)
  waiting for transfers between devices  55 us (18%)
  matrix products  45.5 us (15%)
  local copies, waits for them, and re-layouts  9.18 us (3%)
  other arithmetic  7.97 us (3%)
    all_gather x4, blocking collectives, spare_served(): lax.all_gather(rows, 'expert', axis=0, tiled=True)  125 us
    dot_general x8, matrix products, expert_rows(): jnp.dot(hidden, down_block, preferred_element_type=jnp.float32)  27.1 us
    all_to_all x4, starting transfers between devices, on_device(): lax.all_to_all(partial_value.reshape(members, slot_count, model_width), '...  21.3 us
    all_to_all x4, starting transfers between devices, spare_served(): lax.all_to_all(gathered.reshape(members, tok_dev, model_width), 'expert',...  20.7 us
    all_to_all x4, waiting for transfers between devices, spare_served(): lax.all_to_all(gathered.reshape(members, tok_dev, model_width), 'expert',...  19.5 us
    all_to_all x4, waiting for transfers between devices, on_device(): lax.all_to_all(partial_value.reshape(members, slot_count, model_width), '...  18.2 us
    ppermute x7, waiting for transfers between devices, from_behind(): return lax.ppermute(value, axis, pairs)  17.3 us
    all_to_all x4, starting transfers between devices, on_device(): lax.all_to_all(outgoing, 'expert', split_axis=0, concat_axis=0, tiled=True)  16.5 us
  transfers between devices with their start and end apart: 19, of which 11 were waited for; matrix products, arithmetic and copies ran while one was open for 19% of the time, Pallas kernels for 0%

commit v1 on v0

v1 whole, which is shorter than its diff:
```python
import functools

import jax
import jax.numpy as jnp
from jax import lax
from jax.experimental import pallas as pl
from jax.experimental.pallas import tpu as pltpu
from jax.sharding import PartitionSpec as P

EXPERTS = 4
TICKS = 4
CAP = 4
LANES = 128


EPSILON = 1e-06


def from_behind(value, axis, steps):
    count = lax.axis_size(axis)
    pairs = [(source, (source + steps) % count) for source in range(count)]
    return lax.ppermute(value, axis, pairs)


def group_of(section, tick_idx, segments):
    start_segment = (section - tick_idx) % segments
    first_group = jnp.where((start_segment % 2 == 1) & (start_segment + TICKS <= segments), 1, 0)
    return (first_group + jnp.where(start_segment + tick_idx >= segments, 1, 0)).astype(jnp.int32)


def groups_at(tick_idx, segments):
    found = set()
    for section in range(segments):
        start = (section - tick_idx) % segments
        first = 1 if start % 2 == 1 and start + TICKS <= segments else 0
        found.add(first + (1 if start + tick_idx >= segments else 0))
    return found


def coefficients(routes, gates):
    labels = jnp.arange(EXPERTS, dtype=jnp.int32)
    matches = routes[..., None] == labels
    routed = jnp.sum(jnp.where(matches, gates[..., None], jnp.float32(0.0)), axis=2)
    member = jnp.any(matches, axis=2)
    rows = routes.shape[1]
    earlier = jnp.arange(rows)[None, :] < jnp.arange(rows)[:, None]
    position = jnp.sum(jnp.where(earlier[None, :, :, None] & member[:, None, :, :], 1, 0), axis=2)
    inside = member & (position < CAP)
    share = jnp.where(inside, routed, jnp.float32(0.0))
    spill = jnp.sum(jnp.where(inside, jnp.float32(0.0), routed), axis=2, keepdims=True)
    table = jnp.concatenate([share, spill], axis=2)
    table = jnp.transpose(table, (1, 0, 2)).reshape(rows, -1)
    high = lax.reduce_precision(table, 8, 7)
    low = table - high
    both = jnp.concatenate([high, low], axis=1).astype(jnp.bfloat16)
    return jnp.pad(both, ((0, 0), (0, LANES - both.shape[1])))


def layer_kernel(
    scalars, x_ref, table_ref, gain_ref, gate_ref, up_ref, down_ref, sg_ref, su_ref, sd_ref, out_ref,
    *, tick_idx, slices, slices_out, tok_dev, with_residual
):
    group, expert, member, spare_group = scalars[0], scalars[1], scalars[2], scalars[3]
    if slices == 1:
        x = x_ref[...]
    else:
        x = jnp.concatenate([x_ref[i] for i in range(slices)], axis=1)
    values = x.astype(jnp.float32)
    row_scale = lax.rsqrt(jnp.mean(values * values, axis=-1, keepdims=True) + EPSILON)
    normed = (values * row_scale * gain_ref[group]).astype(jnp.bfloat16)
    table = table_ref[...].astype(jnp.float32)
    lane = lax.broadcasted_iota(jnp.int32, table.shape, 1)
    width = TICKS * (EXPERTS + 1)

    def column(at):
        return jnp.sum(jnp.where((lane == at) | (lane == at + width), table, 0.0), axis=1, keepdims=True)

    share = column(tick_idx * (EXPERTS + 1) + expert)
    spill = column(tick_idx * (EXPERTS + 1) + EXPERTS)
    contract = (((1,), (1,)), ((), ()))

    def served(gate, up, down):
        gate_pre = lax.dot_general(normed, gate, contract, preferred_element_type=jnp.float32)
        up_pre = lax.dot_general(normed, up, contract, preferred_element_type=jnp.float32)
        hidden = (gate_pre / (1.0 + jnp.exp(-gate_pre)) * up_pre).astype(jnp.bfloat16)
        return jnp.dot(hidden, down, preferred_element_type=jnp.float32)

    total = share * served(gate_ref[group], up_ref[group], down_ref[group])
    total = total + spill * served(sg_ref[spare_group], su_ref[spare_group], sd_ref[spare_group])
    if with_residual:
        row = lax.broadcasted_iota(jnp.int32, (x.shape[0], 1), 0)
        total = total + jnp.where(row // tok_dev == member, values, 0.0)
    total = total.astype(jnp.bfloat16)
    if slices_out == 1:
        out_ref[...] = total
    else:
        part = total.shape[1] // slices_out
        for i in range(slices_out):
            out_ref[i] = total[:, i * part:(i + 1) * part]


def run_layer(scalars, x, table, gain, weights, spares, *, tick_idx, slices_out, tok_dev, with_residual):
    slices = 1 if x.ndim == 2 else x.shape[0]
    rows = table.shape[0]
    width = gain.shape[-1]
    out = (rows, width) if slices_out == 1 else (slices_out, rows, width // slices_out)
    whole = pl.BlockSpec(memory_space=pltpu.VMEM)
    hidden = weights[0].shape[1] + spares[0].shape[1]
    return pl.pallas_call(
        functools.partial(
            layer_kernel, tick_idx=tick_idx, slices=slices, slices_out=slices_out, tok_dev=tok_dev,
            with_residual=with_residual,
        ),
        out_shape=jax.ShapeDtypeStruct(out, jnp.bfloat16),
        in_specs=[pl.BlockSpec(memory_space=pltpu.SMEM)] + [whole] * 9,
        out_specs=whole,
        compiler_params=pltpu.CompilerParams(vmem_limit_bytes=16 * 1024 * 1024),
        cost_estimate=pl.CostEstimate(
            flops=6 * rows * hidden * width, bytes_accessed=6 * hidden * width, transcendentals=rows * hidden
        ),
        name="layer",
    )(scalars, x, table, gain, *weights, *spares)


def on_device(
    state, routes, gates, norm_gain, w_gate, w_up, w_down, spare_gate, spare_up, spare_down
):
    segments = lax.axis_size("segment")
    segment_idx = lax.axis_index("segment")
    members = lax.axis_size("expert")
    member_idx = lax.axis_index("expert")
    split_count = members // EXPERTS
    tok_dev = state.shape[1]
    width = state.shape[2]
    rows = members * tok_dev
    part = width // segments
    everyone = ("segment", "expert")

    spare_stack = [spare_gate[:, 0], spare_up[:, 0], spare_down[:, 0]]
    first = [[from_behind(one[0], "segment", -1) for one in spare_stack]]

    sent = jnp.concatenate([state[0], coefficients(routes[:, 0], gates[:, 0])], axis=1)
    sent = jnp.broadcast_to(sent[None], (members,) + sent.shape)
    arrived = lax.all_to_all(sent, "expert", split_axis=0, concat_axis=0, tiled=True)
    arrived = arrived.reshape(rows, -1)
    x = arrived[:, :width]
    table = arrived[:, width:]

    weights = [w_gate[:, 0], w_up[:, 0], w_down[:, 0]]
    gain = norm_gain
    held = None
    second = None
    for tick_idx in range(TICKS):
        needed = groups_at(tick_idx, segments)
        if second is None and needed != {0}:
            second = [from_behind(one[1], "segment", -1) for one in spare_stack]
        group_idx = group_of(segment_idx, tick_idx, segments)
        if second is None:
            spares = [one[None] for one in first[0]]
            spare_at = jnp.int32(0)
        else:
            spares = [jnp.stack([one, two]) for one, two in zip(first[0], second)]
            spare_at = group_idx
        scalars = jnp.stack(
            [group_idx, (member_idx // split_count).astype(jnp.int32), member_idx.astype(jnp.int32), spare_at]
        )
        last = tick_idx + 1 == TICKS
        partial_sum = run_layer(
            scalars, x, table, gain, weights, spares, tick_idx=tick_idx,
            slices_out=1 if last else segments, tok_dev=tok_dev, with_residual=tick_idx == 0,
        )
        if last:
            returned = lax.all_to_all(
                partial_sum.reshape(members, tok_dev, width), "expert", split_axis=0, concat_axis=0, tiled=True
            )
            mine = x.reshape(segments, members, tok_dev, part)
            mine = lax.dynamic_index_in_dim(mine, member_idx, 1, keepdims=False)
            mine = jnp.transpose(mine, (1, 0, 2)).reshape(tok_dev, width)
            total = jnp.sum(returned.astype(jnp.float32), axis=0) + mine.astype(jnp.float32)
            return total.astype(jnp.bfloat16)[None]
        returned = lax.all_to_all(
            partial_sum.reshape(segments * members, tok_dev, part), everyone, split_axis=0, concat_axis=0, tiled=True
        )
        total = jnp.sum(returned.reshape(segments, members, tok_dev, part).astype(jnp.float32), axis=1)
        if held is not None:
            total = total + held.astype(jnp.float32)
        held = jnp.roll(total.astype(jnp.bfloat16), 1, axis=0)
        sent = jnp.broadcast_to(held[:, None], (segments, members, tok_dev, part))
        x = lax.all_to_all(
            sent.reshape(segments * members, tok_dev, part), everyone, split_axis=0, concat_axis=0, tiled=True
        ).reshape(segments, rows, part)


def solution(mesh):
    return jax.shard_map(
        on_device,
        mesh=mesh,
        in_specs=(
            P("segment", "expert", None),
            P(None, "segment", "expert", None),
            P(None, "segment", "expert", None),
            P(None, "segment", None),
            P(None, "segment", "expert", None),
            P(None, "segment", "expert", None),
            P(None, "segment", "expert", None),
            P(None, "segment", "expert", None),
            P(None, "segment", "expert", None),
            P(None, "segment", "expert", None),
        ),
        out_specs=P("segment", "expert", None),
        check_vma=False,
    )
```

time: 307 us -> 177 us (0.58)
  blocking collectives: 125 us -> 27.8 us
  matrix products: 45.5 us -> 0 us
  starting transfers between devices: 62.1 us -> 28.5 us
  local copies, waits for them, and re-layouts: 9.18 us -> 42 us
  Pallas kernels: 0 us -> 15.3 us
    all_gather x4 -> x0, blocking collectives: 125 us -> none  [spare_served(): lax.all_gather(rows, 'expert', axis=0, tiled=True)]
    dot_general x24 -> x0, matrix products: 45.5 us -> none  [the longest x8 27.1 us: expert_rows(): jnp.dot(hidden, down_block, preferred_element_type=jnp.float32)]
    all_to_all x12 -> x6, starting transfers between devices: 58.5 us -> 23.1 us  [the longest x3 7.75 us: on_device(): lax.all_to_all(sent.reshape(segments * members, tok_dev, part), everyone,...]
    unnamed x12 -> x59, local copies, waits for them, and re-layouts: 0.43 us -> 34.2 us
    all_to_all x0 -> x2, blocking collectives: none -> 27.8 us  [on_device(): lax.all_to_all(partial_sum.reshape(segments * members, tok_dev, part), ev...]
    pallas_call x0 -> x4, Pallas kernels: none -> 15.3 us  [run_layer(): pl.pallas_call(functools.partial(layer_kernel, tick_idx=tick_idx, slices=...]
    all_to_all x12 -> x6, waiting for transfers between devices: 37.7 us -> 46.9 us  [the longest x3 21.6 us: on_device(): lax.all_to_all(sent.reshape(segments * members, tok_dev, part), everyone,...]
    ppermute x7 -> x6, waiting for transfers between devices: 17.3 us -> 8.21 us  [from_behind(): return lax.ppermute(value, axis, pairs)]
  transfers between devices with their start and end apart: 19 -> 12, of which waited for: 11 -> 8; matrix products, arithmetic and copies ran while one was open for 19% -> 6% of each run, Pallas kernels for 0% -> 2%
where the time goes in v1:
time: 177 us; the launch traced here: 176 us
  waiting for transfers between devices  55.2 us (31%)
  local copies, waits for them, and re-layouts  42 us (24%)
  starting transfers between devices  28.5 us (16%)
  blocking collectives  27.8 us (16%)
  Pallas kernels  15.3 us (9%)
  other arithmetic  6.99 us (4%)
    unnamed x59, local copies, waits for them, and re-layouts  34.2 us
    all_to_all x2, blocking collectives, on_device(): lax.all_to_all(partial_sum.reshape(segments * members, tok_dev, part), ev...  27.8 us
    all_to_all x3, waiting for transfers between devices, on_device(): lax.all_to_all(sent.reshape(segments * members, tok_dev, part), everyone,...  21.6 us
    pallas_call x4, Pallas kernels, run_layer(): pl.pallas_call(functools.partial(layer_kernel, tick_idx=tick_idx, slices=...  15.3 us
    all_to_all x1, waiting for transfers between devices, on_device(): lax.all_to_all(sent, 'expert', split_axis=0, concat_axis=0, tiled=True)  9.48 us
    all_to_all x1, waiting for transfers between devices, on_device(): lax.all_to_all(partial_sum.reshape(members, tok_dev, width), 'expert', sp...  9.2 us
    ppermute x6, waiting for transfers between devices, from_behind(): return lax.ppermute(value, axis, pairs)  8.21 us
    all_to_all x3, starting transfers between devices, on_device(): lax.all_to_all(sent.reshape(segments * members, tok_dev, part), everyone,...  7.75 us
  transfers between devices with their start and end apart: 12, of which 8 were waited for; matrix products, arithmetic and copies ran while one was open for 6% of the time, Pallas kernels for 2%

profile of v1, /device:TPU:0, one launch (start us, length us, event | category | flops | bytes accessed | tf_op | source)
XLA Modules:
  0.0 176.1 jit_solution(5428043303533714483)
XLA Ops:
  0.0 2.6 %slice_bitcast_fusion.2 = (bf16[160,2048]{1,0:T(8,128)(2,1)}, bf16[160,2048]{1,0:T(8,128)(2,1)}) fusion(bf16[2,1,160,2048]{3,2,1,0:T(8,128)(2,1)} %param.17), kind=kLoop, calls=%fused_computation.5 | loop fusion | bytes 2621440 | tf_op jit(solution)/shard_map/squeeze | solution.py:156
  2.6 2.4 %collective-permute-start = (bf16[160,2048]{1,0:T(8,128)(2,1)}, bf16[160,2048]{1,0:T(8,128)(2,1)S(1)}, u32[]{:S(2)}, u32[]{:S(2)}) collective-permute-start(bf16[160,2048]{1,0:T(8,128)(2,1)} %get-tuple-element.12), channel_id=1, source_target_pairs={{0,24},{8,0},{16,8},{24,16},{1,25},{9,1},{17,9},{25,17},{2,26},{10... | collective-permute-start | bytes 1966088 | tf_op jit(solution)/shard_map/ppermute | solution.py:22
  5.1 1.0 slice_bitcast_fusion.1
  6.0 0.7 collective-permute-start.1
  6.7 1.2 slice_bitcast_fusion
  8.7 0.7 broadcast_in_dim.77
  9.5 5.8 %all-to-all-start = ((bf16[8,8,2176]{2,1,0:T(8,128)(2,1)}), bf16[8,8,2176]{2,1,0:T(8,128)(2,1)S(1)}, u32[]{:S(2)}, u32[]{:S(2)}) async-start(bf16[8,8,2176]{2,1,0:T(8,128)(2,1)} %broadcast_in_dim.77), calls=%async_computation | async-start | bytes 557056 | tf_op jit(solution)/shard_map/all_to_all | solution.py:144
  15.7 9.5 %all-to-all-done = bf16[8,8,2176]{2,1,0:T(8,128)(2,1)S(1)} async-done(((bf16[8,8,2176]{2,1,0:T(8,128)(2,1)}), bf16[8,8,2176]{2,1,0:T(8,128)(2,1)S(1)}, u32[]{:S(2)}, u32[]{:S(2)}) %all-to-all-start) | async-done | bytes 278560 | tf_op jit(solution)/shard_map/all_to_all | solution.py:144
  25.2 2.3 %collective-permute-done.2 = bf16[160,2048]{1,0:T(8,128)(2,1)S(1)} collective-permute-done((bf16[160,2048]{1,0:T(8,128)(2,1)}, bf16[160,2048]{1,0:T(8,128)(2,1)S(1)}, u32[]{:S(2)}, u32[]{:S(2)}) %collective-permute-start.2) | collective-permute-done | bytes 655392 | tf_op jit(solution)/shard_map/ppermute | solution.py:22
  27.5 2.7 %copy-done = bf16[2,1,640,2048]{3,2,1,0:T(8,128)(2,1)S(1)} copy-done((bf16[2,1,640,2048]{3,2,1,0:T(8,128)(2,1)S(1)}, bf16[2,1,640,2048]{3,2,1,0:T(8,128)(2,1)}, u32[]{:S(2)}) %copy-start) | copy-done | bytes 5242904
  30.2 2.5 %copy-done.4 = bf16[2,1,640,2048]{3,2,1,0:T(8,128)(2,1)S(1)} copy-done((bf16[2,1,640,2048]{3,2,1,0:T(8,128)(2,1)S(1)}, bf16[2,1,640,2048]{3,2,1,0:T(8,128)(2,1)}, u32[]{:S(2)}) %copy-start.4) | copy-done | bytes 5242904
  32.7 2.5 %copy-done.8 = bf16[2,1,640,2048]{3,2,1,0:T(8,128)(2,1)S(1)} copy-done((bf16[2,1,640,2048]{3,2,1,0:T(8,128)(2,1)S(1)}, bf16[2,1,640,2048]{3,2,1,0:T(8,128)(2,1)}, u32[]{:S(2)}) %copy-start.8) | copy-done | bytes 5242904
  35.2 4.2 %layer.4 = bf16[4,64,512]{2,1,0:T(8,128)(2,1)} custom-call(s32[4]{0:T(128)S(1)} %pad_add_fusion.3.scalars, bf16[64,2048]{1,0:T(8,128)(2,1)S(1)} %slice.64.x_ref, bf16[64,128]{1,0:T(8,128)(2,1)S(1)} %slice.65.table_ref, f32[2,1,2048]{2,1,0:T(1,128)S(1)} %copy-done.17, bf16[2,640,2048]{2,1,0:T(8,128)(2,1)S(1)} %bitcast.67, bf16[2,640,2048]{2,1,0:T(8,128)(2,1)S(1)} %bitcast.71, ...), custom_call_target="tpu_custom_call" | custom-call | flops 629145600 | bytes 9830400 | tf_op jit(solution)/shard_map/layer/pallas_call | solution.py:109
  39.4 6.1 %all-to-all-start.1 = ((bf16[32,8,512]{2,1,0:T(8,128)(2,1)}), bf16[32,8,512]{2,1,0:T(8,128)(2,1)S(1)}, u32[]{:S(2)}, u32[]{:S(2)}) async-start(bf16[32,8,512]{2,1,0:T(8,128)(2,1)} %bitcast.21), calls=%async_computation.1 | async-start | bytes 524288 | tf_op jit(solution)/shard_map/all_to_all | solution.py:181
  45.5 1.5 collective-permute-start.4
  48.1 1.2 pad_maximum_fusion.sg_ref
  49.3 6.7 %all-to-all-done.1 = bf16[32,8,512]{2,1,0:T(8,128)(2,1)S(1)} async-done(((bf16[32,8,512]{2,1,0:T(8,128)(2,1)}), bf16[32,8,512]{2,1,0:T(8,128)(2,1)S(1)}, u32[]{:S(2)}, u32[]{:S(2)}) %all-to-all-start.1) | async-done | bytes 262176 | tf_op jit(solution)/shard_map/all_to_all | solution.py:181
  56.1 0.7 broadcast_in_dim.81
  56.8 2.6 %all-to-all-start.2 = ((bf16[32,8,512]{2,1,0:T(8,128)(2,1)}), bf16[32,8,512]{2,1,0:T(8,128)(2,1)S(1)}, u32[]{:S(2)}, u32[]{:S(2)}) async-start(bf16[32,8,512]{2,1,0:T(8,128)(2,1)} %bitcast.23), calls=%async_computation.2 | async-start | bytes 524288 | tf_op jit(solution)/shard_map/all_to_all | solution.py:189
  59.4 1.3 pad_maximum_fusion.1.su_ref
  60.7 5.9 %collective-permute-done.5 = bf16[160,2048]{1,0:T(8,128)(2,1)} collective-permute-done((bf16[160,2048]{1,0:T(8,128)(2,1)}, bf16[160,2048]{1,0:T(8,128)(2,1)}, u32[]{:S(2)}, u32[]{:S(2)}) %collective-permute-start.5) | collective-permute-done | bytes 655392 | tf_op jit(solution)/shard_map/ppermute | solution.py:22
  66.6 2.3 %pad_maximum_fusion.2.sd_ref = bf16[2,160,2048]{2,1,0:T(8,128)(2,1)} fusion(bf16[1,160,2048]{2,1,0:T(8,128)(2,1)} %bitcast.30, bf16[1,160,2048]{2,1,0:T(8,128)(2,1)S(1)} %bitcast.82), kind=kLoop, calls=%fused_computation.2 | loop fusion | flops 655360 | bytes 2621440 | tf_op jit(solution)/shard_map/stack | solution.py:162
  68.9 1.0 all-to-all-done.2
  69.9 2.5 %copy-done.1 = bf16[2,1,640,2048]{3,2,1,0:T(8,128)(2,1)S(1)} copy-done((bf16[2,1,640,2048]{3,2,1,0:T(8,128)(2,1)S(1)}, bf16[2,1,640,2048]{3,2,1,0:T(8,128)(2,1)}, u32[]{:S(2)}) %copy-start.1) | copy-done | bytes 5242904
  72.3 2.5 %copy-done.5 = bf16[2,1,640,2048]{3,2,1,0:T(8,128)(2,1)S(1)} copy-done((bf16[2,1,640,2048]{3,2,1,0:T(8,128)(2,1)S(1)}, bf16[2,1,640,2048]{3,2,1,0:T(8,128)(2,1)}, u32[]{:S(2)}) %copy-start.5) | copy-done | bytes 5242904
  74.8 2.5 %copy-done.9 = bf16[2,1,640,2048]{3,2,1,0:T(8,128)(2,1)S(1)} copy-done((bf16[2,1,640,2048]{3,2,1,0:T(8,128)(2,1)S(1)}, bf16[2,1,640,2048]{3,2,1,0:T(8,128)(2,1)}, u32[]{:S(2)}) %copy-start.9) | copy-done | bytes 5242904
  77.3 1.3 copy-done.12
  78.6 3.5 %layer.5 = bf16[4,64,512]{2,1,0:T(8,128)(2,1)S(1)} custom-call(s32[4]{0:T(128)S(1)} %copy-done.19, bf16[4,64,512]{2,1,0:T(8,128)(2,1)S(1)} %bitcast.88, bf16[64,128]{1,0:T(8,128)(2,1)S(1)} %slice.65.table_ref, f32[2,1,2048]{2,1,0:T(1,128)S(1)} %copy-done.18, bf16[2,640,2048]{2,1,0:T(8,128)(2,1)S(1)} %bitcast.68, bf16[2,640,2048]{2,1,0:T(8,128)(2,1)S(1)} %bitcast.72, ...), custom_call_target="tpu_custom_call" | custom-call | flops 629145600 | bytes 9830400 | tf_op jit(solution)/shard_map/layer/pallas_call | solution.py:109
  82.1 15.0 %all_to_all.40 = bf16[32,8,512]{2,1,0:T(8,128)(2,1)S(1)} all-to-all(bf16[32,8,512]{2,1,0:T(8,128)(2,1)S(1)} %bitcast.89), channel_id=1, replica_groups=mesh['segment'=4,'expert'=8] {'segment','expert'}, dimensions={0} | all-to-all | bytes 524288 | tf_op jit(solution)/shard_map/all_to_all | solution.py:181
  97.3 0.7 broadcast_in_dim.82
  98.0 2.6 %all-to-all-start.4 = ((bf16[32,8,512]{2,1,0:T(8,128)(2,1)}), bf16[32,8,512]{2,1,0:T(8,128)(2,1)S(1)}, u32[]{:S(2)}, u32[]{:S(2)}) async-start(bf16[32,8,512]{2,1,0:T(8,128)(2,1)} %bitcast.33), calls=%async_computation.4 | async-start | bytes 524288 | tf_op jit(solution)/shard_map/all_to_all | solution.py:189
  100.7 10.3 %all-to-all-done.4 = bf16[32,8,512]{2,1,0:T(8,128)(2,1)S(1)} async-done(((bf16[32,8,512]{2,1,0:T(8,128)(2,1)}), bf16[32,8,512]{2,1,0:T(8,128)(2,1)S(1)}, u32[]{:S(2)}, u32[]{:S(2)}) %all-to-all-start.4) | async-done | bytes 262176 | tf_op jit(solution)/shard_map/all_to_all | solution.py:189
  111.0 2.5 %copy-done.2 = bf16[2,1,640,2048]{3,2,1,0:T(8,128)(2,1)S(1)} copy-done((bf16[2,1,640,2048]{3,2,1,0:T(8,128)(2,1)S(1)}, bf16[2,1,640,2048]{3,2,1,0:T(8,128)(2,1)}, u32[]{:S(2)}) %copy-start.2) | copy-done | bytes 5242904
  113.5 2.5 %copy-done.6 = bf16[2,1,640,2048]{3,2,1,0:T(8,128)(2,1)S(1)} copy-done((bf16[2,1,640,2048]{3,2,1,0:T(8,128)(2,1)S(1)}, bf16[2,1,640,2048]{3,2,1,0:T(8,128)(2,1)}, u32[]{:S(2)}) %copy-start.6) | copy-done | bytes 5242904
  116.0 2.5 %copy-done.10 = bf16[2,1,640,2048]{3,2,1,0:T(8,128)(2,1)S(1)} copy-done((bf16[2,1,640,2048]{3,2,1,0:T(8,128)(2,1)S(1)}, bf16[2,1,640,2048]{3,2,1,0:T(8,128)(2,1)}, u32[]{:S(2)}) %copy-start.10) | copy-done | bytes 5242904
  118.5 1.3 copy-done.13
  119.8 3.5 %layer.6 = bf16[4,64,512]{2,1,0:T(8,128)(2,1)S(1)} custom-call(s32[4]{0:T(128)S(1)} %pad_add_fusion.1.scalars, bf16[4,64,512]{2,1,0:T(8,128)(2,1)S(1)} %bitcast.87, bf16[64,128]{1,0:T(8,128)(2,1)S(1)} %slice.65.table_ref, f32[2,1,2048]{2,1,0:T(1,128)S(1)} %copy-done.18, bf16[2,640,2048]{2,1,0:T(8,128)(2,1)S(1)} %bitcast.69, ...), custom_call_target="tpu_custom_call" | custom-call | flops 629145600 | bytes 9830400 | tf_op jit(solution)/shard_map/layer/pallas_call | solution.py:109
  123.3 12.7 %all_to_all.41 = bf16[32,8,512]{2,1,0:T(8,128)(2,1)S(1)} all-to-all(bf16[32,8,512]{2,1,0:T(8,128)(2,1)S(1)} %bitcast.90), channel_id=1, replica_groups=mesh['segment'=4,'expert'=8] {'segment','expert'}, dimensions={0} | all-to-all | bytes 524288 | tf_op jit(solution)/shard_map/all_to_all | solution.py:181
  136.1 0.7 broadcast_in_dim.83
  136.8 2.6 %all-to-all-start.6 = ((bf16[32,8,512]{2,1,0:T(8,128)(2,1)}), bf16[32,8,512]{2,1,0:T(8,128)(2,1)S(1)}, u32[]{:S(2)}, u32[]{:S(2)}) async-start(bf16[32,8,512]{2,1,0:T(8,128)(2,1)} %bitcast.37), calls=%async_computation.6 | async-start | bytes 524288 | tf_op jit(solution)/shard_map/all_to_all | solution.py:189
  139.5 10.3 %all-to-all-done.6 = bf16[32,8,512]{2,1,0:T(8,128)(2,1)S(1)} async-done(((bf16[32,8,512]{2,1,0:T(8,128)(2,1)}), bf16[32,8,512]{2,1,0:T(8,128)(2,1)S(1)}, u32[]{:S(2)}, u32[]{:S(2)}) %all-to-all-start.6) | async-done | bytes 262176 | tf_op jit(solution)/shard_map/all_to_all | solution.py:189
  149.8 2.5 %copy-done.3 = bf16[2,1,640,2048]{3,2,1,0:T(8,128)(2,1)S(1)} copy-done((bf16[2,1,640,2048]{3,2,1,0:T(8,128)(2,1)S(1)}, bf16[2,1,640,2048]{3,2,1,0:T(8,128)(2,1)}, u32[]{:S(2)}) %copy-start.3) | copy-done | bytes 5242904
  152.3 2.5 %copy-done.7 = bf16[2,1,640,2048]{3,2,1,0:T(8,128)(2,1)S(1)} copy-done((bf16[2,1,640,2048]{3,2,1,0:T(8,128)(2,1)S(1)}, bf16[2,1,640,2048]{3,2,1,0:T(8,128)(2,1)}, u32[]{:S(2)}) %copy-start.7) | copy-done | bytes 5242904
  154.8 2.5 %copy-done.11 = bf16[2,1,640,2048]{3,2,1,0:T(8,128)(2,1)S(1)} copy-done((bf16[2,1,640,2048]{3,2,1,0:T(8,128)(2,1)S(1)}, bf16[2,1,640,2048]{3,2,1,0:T(8,128)(2,1)}, u32[]{:S(2)}) %copy-start.11) | copy-done | bytes 5242904
  157.3 1.3 copy-done.14
  158.6 4.2 %layer.7 = bf16[64,2048]{1,0:T(8,128)(2,1)} custom-call(s32[4]{0:T(128)S(1)} %pad_add_fusion.scalars, bf16[4,64,512]{2,1,0:T(8,128)(2,1)S(1)} %bitcast.85, bf16[64,128]{1,0:T(8,128)(2,1)S(1)} %slice.65.table_ref, f32[2,1,2048]{2,1,0:T(1,128)S(1)} %copy-done.18, bf16[2,640,2048]{2,1,0:T(8,128)(2,1)S(1)} %bitcast.70, bf16[2,640,2048]{2,1,0:T(8,128)(2,1)S(1)} %bitcast.74, ...), custom_call_target="tpu_custom_call" | custom-call | flops 629145600 | bytes 9830400 | tf_op jit(solution)/shard_map/layer/pallas_call | solution.py:109
  162.8 3.4 %all-to-all-start.7 = ((bf16[8,8,2048]{2,1,0:T(8,128)(2,1)}), bf16[8,8,2048]{2,1,0:T(8,128)(2,1)S(1)}, u32[]{:S(2)}, u32[]{:S(2)}) async-start(bf16[8,8,2048]{2,1,0:T(8,128)(2,1)} %bitcast.39), calls=%async_computation.7 | async-start | bytes 524288 | tf_op jit(solution)/shard_map/all_to_all | solution.py:173
  166.2 9.2 %all-to-all-done.7 = bf16[8,8,2048]{2,1,0:T(8,128)(2,1)S(1)} async-done(((bf16[8,8,2048]{2,1,0:T(8,128)(2,1)}), bf16[8,8,2048]{2,1,0:T(8,128)(2,1)S(1)}, u32[]{:S(2)}, u32[]{:S(2)}) %all-to-all-start.7) | async-done | bytes 262176 | tf_op jit(solution)/shard_map/all_to_all | solution.py:173
  (87 shorter events, 3.3 us)
Async XLA Ops:
  0.0 5.1 %copy-start.20 = (bf16[2,1,160,2048]{3,2,1,0:T(8,128)(2,1)S(1)}, bf16[2,1,160,2048]{3,2,1,0:T(8,128)(2,1)}, u32[]{:S(2)}) copy-start(bf16[2,1,160,2048]{3,2,1,0:T(8,128)(2,1)} %param.18) | copy-start | bytes 3932164
  2.6 4.1 %copy-start.21 = (bf16[2,1,160,2048]{3,2,1,0:T(8,128)(2,1)S(1)}, bf16[2,1,160,2048]{3,2,1,0:T(8,128)(2,1)}, u32[]{:S(2)}) copy-start(bf16[2,1,160,2048]{3,2,1,0:T(8,128)(2,1)} %param.19) | copy-start | bytes 3932164
  2.6 22.6 %collective-permute-start = (bf16[160,2048]{1,0:T(8,128)(2,1)}, bf16[160,2048]{1,0:T(8,128)(2,1)S(1)}, u32[]{:S(2)}, u32[]{:S(2)}) collective-permute-start(bf16[160,2048]{1,0:T(8,128)(2,1)} %get-tuple-element.12), channel_id=1, source_target_pairs={{0,24},{8,0},{16,8},{24,16},{1,25},{9,1},{17,9},{25,17},{2,26},{10... | collective-permute-start | bytes 1966088 | tf_op jit(solution)/shard_map/ppermute | solution.py:22
  6.0 1.9 %copy-start.27 = (s32[4,1,8,2]{2,3,1,0:T(2,128)S(1)}, s32[4,1,8,2]{2,3,1,0:T(2,128)}, u32[]{:S(2)}) copy-start(s32[4,1,8,2]{2,3,1,0:T(2,128)} %param.11) | copy-start | bytes 772
  6.0 1.9 %copy-start.28 = (f32[4,1,8,2]{2,3,1,0:T(2,128)S(1)}, f32[4,1,8,2]{2,3,1,0:T(2,128)}, u32[]{:S(2)}) copy-start(f32[4,1,8,2]{2,3,1,0:T(2,128)} %param.12) | copy-start | bytes 772
  6.0 2.7 %copy-start.26 = (bf16[1,8,2048]{2,1,0:T(8,128)(2,1)S(1)}, bf16[1,8,2048]{2,1,0:T(8,128)(2,1)}, u32[]{:S(2)}) copy-start(bf16[1,8,2048]{2,1,0:T(8,128)(2,1)} %param.10) | copy-start | bytes 98308
  6.0 19.2 %collective-permute-start.1 = (bf16[160,2048]{1,0:T(8,128)(2,1)}, bf16[160,2048]{1,0:T(8,128)(2,1)S(1)}, u32[]{:S(2)}, u32[]{:S(2)}) collective-permute-start(bf16[160,2048]{1,0:T(8,128)(2,1)} %get-tuple-element.10), channel_id=1, source_target_pairs={{0,24},{8,0},{16,8},{24,16},{1,25},{9,1},{17,9},{25,17},{2,26},{10... | collective-permute-start | bytes 1966088 | tf_op jit(solution)/shard_map/ppermute | solution.py:22
  7.9 19.6 %copy-start.17 = (f32[2,1,2048]{2,1,0:T(1,128)S(1)}, f32[2,1,2048]{2,1,0:T(1,128)}, u32[]{:S(2)}) copy-start(f32[2,1,2048]{2,1,0:T(1,128)} %gain_ref.7) | copy-start | bytes 49156
  7.9 19.6 %collective-permute-start.2 = (bf16[160,2048]{1,0:T(8,128)(2,1)}, bf16[160,2048]{1,0:T(8,128)(2,1)S(1)}, u32[]{:S(2)}, u32[]{:S(2)}) collective-permute-start(bf16[160,2048]{1,0:T(8,128)(2,1)} %get-tuple-element.8), channel_id=1, source_target_pairs={{0,24},{8,0},{16,8},{24,16},{1,25},{9,1},{17,9},{25,17},{2,26},{10... | collective-permute-start | bytes 1966088 | tf_op jit(solution)/shard_map/ppermute | solution.py:22
  9.5 15.7 %all-to-all-start = ((bf16[8,8,2176]{2,1,0:T(8,128)(2,1)}), bf16[8,8,2176]{2,1,0:T(8,128)(2,1)S(1)}, u32[]{:S(2)}, u32[]{:S(2)}) async-start(bf16[8,8,2176]{2,1,0:T(8,128)(2,1)} %broadcast_in_dim.77), calls=%async_computation | async-start | bytes 557056 | tf_op jit(solution)/shard_map/all_to_all | solution.py:144
  15.3 32.8 %collective-permute-start.3 = (bf16[160,2048]{1,0:T(8,128)(2,1)}, bf16[160,2048]{1,0:T(8,128)(2,1)}, u32[]{:S(2)}, u32[]{:S(2)}) collective-permute-start(bf16[160,2048]{1,0:T(8,128)(2,1)} %get-tuple-element.11), channel_id=1, source_target_pairs={{0,24},{8,0},{16,8},{24,16},{1,25},{9,1},{17,9},{25,17},{2,26},{10... | collective-permute-start | bytes 1966088 | tf_op jit(solution)/shard_map/ppermute | solution.py:22
  27.5 11.9 %copy-start.15 = (bf16[160,2048]{1,0:T(8,128)(2,1)}, bf16[160,2048]{1,0:T(8,128)(2,1)S(1)}, u32[]{:S(2)}) copy-start(bf16[160,2048]{1,0:T(8,128)(2,1)S(1)} %collective-permute-done.2) | copy-start | bytes 1966084
  27.5 2.7 %copy-start = (bf16[2,1,640,2048]{3,2,1,0:T(8,128)(2,1)S(1)}, bf16[2,1,640,2048]{3,2,1,0:T(8,128)(2,1)}, u32[]{:S(2)}) copy-start(bf16[2,1,640,2048]{3,2,1,0:T(8,128)(2,1)} %param.14) | copy-start | bytes 15728644
  30.2 2.5 %copy-start.4 = (bf16[2,1,640,2048]{3,2,1,0:T(8,128)(2,1)S(1)}, bf16[2,1,640,2048]{3,2,1,0:T(8,128)(2,1)}, u32[]{:S(2)}) copy-start(bf16[2,1,640,2048]{3,2,1,0:T(8,128)(2,1)} %param.15) | copy-start | bytes 15728644
  32.7 2.5 %copy-start.8 = (bf16[2,1,640,2048]{3,2,1,0:T(8,128)(2,1)S(1)}, bf16[2,1,640,2048]{3,2,1,0:T(8,128)(2,1)}, u32[]{:S(2)}) copy-start(bf16[2,1,640,2048]{3,2,1,0:T(8,128)(2,1)} %param.16) | copy-start | bytes 15728644
  39.4 16.6 %all-to-all-start.1 = ((bf16[32,8,512]{2,1,0:T(8,128)(2,1)}), bf16[32,8,512]{2,1,0:T(8,128)(2,1)S(1)}, u32[]{:S(2)}, u32[]{:S(2)}) async-start(bf16[32,8,512]{2,1,0:T(8,128)(2,1)} %bitcast.21), calls=%async_computation.1 | async-start | bytes 524288 | tf_op jit(solution)/shard_map/all_to_all | solution.py:181
  45.5 13.9 %collective-permute-start.4 = (bf16[160,2048]{1,0:T(8,128)(2,1)S(1)}, bf16[160,2048]{1,0:T(8,128)(2,1)}, u32[]{:S(2)}, u32[]{:S(2)}) collective-permute-start(bf16[160,2048]{1,0:T(8,128)(2,1)S(1)} %get-tuple-element.9), channel_id=1, source_target_pairs={{0,24},{8,0},{16,8},{24,16},{1,25},{9,1},{17,9},{25,17},{2,26},{10... | collective-permute-start | bytes 1966088 | tf_op jit(solution)/shard_map/ppermute | solution.py:22
  47.1 19.5 %collective-permute-start.5 = (bf16[160,2048]{1,0:T(8,128)(2,1)}, bf16[160,2048]{1,0:T(8,128)(2,1)}, u32[]{:S(2)}, u32[]{:S(2)}) collective-permute-start(bf16[160,2048]{1,0:T(8,128)(2,1)} %get-tuple-element.7), channel_id=1, source_target_pairs={{0,24},{8,0},{16,8},{24,16},{1,25},{9,1},{17,9},{25,17},{2,26},{10... | collective-permute-start | bytes 1966088 | tf_op jit(solution)/shard_map/ppermute | solution.py:22
  56.0 0.8 copy-start.22
  56.1 0.8 copy-start.24
  56.8 13.0 %all-to-all-start.2 = ((bf16[32,8,512]{2,1,0:T(8,128)(2,1)}), bf16[32,8,512]{2,1,0:T(8,128)(2,1)S(1)}, u32[]{:S(2)}, u32[]{:S(2)}) async-start(bf16[32,8,512]{2,1,0:T(8,128)(2,1)} %bitcast.23), calls=%async_computation.2 | async-start | bytes 524288 | tf_op jit(solution)/shard_map/all_to_all | solution.py:189
  59.4 7.2 %copy-start.16 = (bf16[160,2048]{1,0:T(8,128)(2,1)S(1)}, bf16[160,2048]{1,0:T(8,128)(2,1)}, u32[]{:S(2)}) copy-start(bf16[160,2048]{1,0:T(8,128)(2,1)} %copy-done.15) | copy-start | bytes 1966084
  66.6 3.3 %copy-start.18 = (f32[2,1,2048]{2,1,0:T(1,128)S(1)}, f32[2,1,2048]{2,1,0:T(1,128)}, u32[]{:S(2)}) copy-start(f32[2,1,2048]{2,1,0:T(1,128)} %gain_ref.7) | copy-start | bytes 49156
  66.6 3.3 %copy-start.19 = (s32[4]{0:T(128)S(1)}, s32[4]{0:T(128)}, u32[]{:S(2)}) copy-start(s32[4]{0:T(128)} %pad_add_fusion.2.scalars) | copy-start | bytes 52
  69.9 2.5 %copy-start.1 = (bf16[2,1,640,2048]{3,2,1,0:T(8,128)(2,1)S(1)}, bf16[2,1,640,2048]{3,2,1,0:T(8,128)(2,1)}, u32[]{:S(2)}) copy-start(bf16[2,1,640,2048]{3,2,1,0:T(8,128)(2,1)} %param.14) | copy-start | bytes 15728644
  72.3 2.5 %copy-start.5 = (bf16[2,1,640,2048]{3,2,1,0:T(8,128)(2,1)S(1)}, bf16[2,1,640,2048]{3,2,1,0:T(8,128)(2,1)}, u32[]{:S(2)}) copy-start(bf16[2,1,640,2048]{3,2,1,0:T(8,128)(2,1)} %param.15) | copy-start | bytes 15728644
  74.8 2.5 %copy-start.9 = (bf16[2,1,640,2048]{3,2,1,0:T(8,128)(2,1)S(1)}, bf16[2,1,640,2048]{3,2,1,0:T(8,128)(2,1)}, u32[]{:S(2)}) copy-start(bf16[2,1,640,2048]{3,2,1,0:T(8,128)(2,1)} %param.16) | copy-start | bytes 15728644
  77.3 1.3 copy-start.12
  78.6 18.6 %copy-start.23 = (bf16[3,8,512]{2,1,0:T(8,128)(2,1)S(1)}, bf16[3,8,512]{2,1,0:T(8,128)(2,1)}, u32[]{:S(2)}) copy-start(bf16[3,8,512]{2,1,0:T(8,128)(2,1)} %copy-done.22) | copy-start | bytes 73732
  78.6 18.6 %copy-start.25 = (bf16[1,8,512]{2,1,0:T(8,128)(2,1)S(1)}, bf16[1,8,512]{2,1,0:T(8,128)(2,1)}, u32[]{:S(2)}) copy-start(bf16[1,8,512]{2,1,0:T(8,128)(2,1)} %copy-done.24) | copy-start | bytes 24580
  98.0 13.0 %all-to-all-start.4 = ((bf16[32,8,512]{2,1,0:T(8,128)(2,1)}), bf16[32,8,512]{2,1,0:T(8,128)(2,1)S(1)}, u32[]{:S(2)}, u32[]{:S(2)}) async-start(bf16[32,8,512]{2,1,0:T(8,128)(2,1)} %bitcast.33), calls=%async_computation.4 | async-start | bytes 524288 | tf_op jit(solution)/shard_map/all_to_all | solution.py:189
  111.0 2.5 %copy-start.2 = (bf16[2,1,640,2048]{3,2,1,0:T(8,128)(2,1)S(1)}, bf16[2,1,640,2048]{3,2,1,0:T(8,128)(2,1)}, u32[]{:S(2)}) copy-start(bf16[2,1,640,2048]{3,2,1,0:T(8,128)(2,1)} %param.14) | copy-start | bytes 15728644
  113.5 2.5 %copy-start.6 = (bf16[2,1,640,2048]{3,2,1,0:T(8,128)(2,1)S(1)}, bf16[2,1,640,2048]{3,2,1,0:T(8,128)(2,1)}, u32[]{:S(2)}) copy-start(bf16[2,1,640,2048]{3,2,1,0:T(8,128)(2,1)} %param.15) | copy-start | bytes 15728644
  116.0 2.5 %copy-start.10 = (bf16[2,1,640,2048]{3,2,1,0:T(8,128)(2,1)S(1)}, bf16[2,1,640,2048]{3,2,1,0:T(8,128)(2,1)}, u32[]{:S(2)}) copy-start(bf16[2,1,640,2048]{3,2,1,0:T(8,128)(2,1)} %param.16) | copy-start | bytes 15728644
  118.5 1.3 copy-start.13
  136.8 13.0 %all-to-all-start.6 = ((bf16[32,8,512]{2,1,0:T(8,128)(2,1)}), bf16[32,8,512]{2,1,0:T(8,128)(2,1)S(1)}, u32[]{:S(2)}, u32[]{:S(2)}) async-start(bf16[32,8,512]{2,1,0:T(8,128)(2,1)} %bitcast.37), calls=%async_computation.6 | async-start | bytes 524288 | tf_op jit(solution)/shard_map/all_to_all | solution.py:189
  149.8 2.5 %copy-start.3 = (bf16[2,1,640,2048]{3,2,1,0:T(8,128)(2,1)S(1)}, bf16[2,1,640,2048]{3,2,1,0:T(8,128)(2,1)}, u32[]{:S(2)}) copy-start(bf16[2,1,640,2048]{3,2,1,0:T(8,128)(2,1)} %param.14) | copy-start | bytes 15728644
  152.3 2.5 %copy-start.7 = (bf16[2,1,640,2048]{3,2,1,0:T(8,128)(2,1)S(1)}, bf16[2,1,640,2048]{3,2,1,0:T(8,128)(2,1)}, u32[]{:S(2)}) copy-start(bf16[2,1,640,2048]{3,2,1,0:T(8,128)(2,1)} %param.15) | copy-start | bytes 15728644
  154.8 2.5 %copy-start.11 = (bf16[2,1,640,2048]{3,2,1,0:T(8,128)(2,1)S(1)}, bf16[2,1,640,2048]{3,2,1,0:T(8,128)(2,1)}, u32[]{:S(2)}) copy-start(bf16[2,1,640,2048]{3,2,1,0:T(8,128)(2,1)} %param.16) | copy-start | bytes 15728644
  157.3 1.3 copy-start.14
  162.8 12.6 %all-to-all-start.7 = ((bf16[8,8,2048]{2,1,0:T(8,128)(2,1)}), bf16[8,8,2048]{2,1,0:T(8,128)(2,1)S(1)}, u32[]{:S(2)}, u32[]{:S(2)}) async-start(bf16[8,8,2048]{2,1,0:T(8,128)(2,1)} %bitcast.39), calls=%async_computation.7 | async-start | bytes 524288 | tf_op jit(solution)/shard_map/all_to_all | solution.py:173

commit v2 on v1

v2 whole, which is shorter than its diff:
```python
import functools

import jax
import jax.numpy as jnp
from jax import lax
from jax.experimental import pallas as pl
from jax.experimental.pallas import tpu as pltpu
from jax.sharding import PartitionSpec as P

EXPERTS = 4
TICKS = 4
CAP = 4
LANES = 128
BOTH = ("segment", "expert")


EPSILON = 1e-06


def moved(value, flip, steps):
    segments, members = lax.axis_size("segment"), lax.axis_size("expert")
    pairs = [
        (section * members + member, (section + steps) % segments * members + (member ^ flip))
        for section in range(segments)
        for member in range(members)
    ]
    return lax.ppermute(value, BOTH, pairs)


def group_of(section, tick_idx, segments):
    start_segment = (section - tick_idx) % segments
    first_group = jnp.where((start_segment % 2 == 1) & (start_segment + TICKS <= segments), 1, 0)
    return (first_group + jnp.where(start_segment + tick_idx >= segments, 1, 0)).astype(jnp.int32)


def groups_at(tick_idx, segments):
    found = set()
    for section in range(segments):
        start = (section - tick_idx) % segments
        first = 1 if start % 2 == 1 and start + TICKS <= segments else 0
        found.add(first + (1 if start + tick_idx >= segments else 0))
    return found


def coefficients(routes, gates):
    labels = jnp.arange(EXPERTS, dtype=jnp.int32)
    matches = routes[..., None] == labels
    routed = jnp.sum(jnp.where(matches, gates[..., None], jnp.float32(0.0)), axis=2)
    member = jnp.any(matches, axis=2)
    rows = routes.shape[1]
    earlier = jnp.arange(rows)[None, :] < jnp.arange(rows)[:, None]
    position = jnp.sum(jnp.where(earlier[None, :, :, None] & member[:, None, :, :], 1, 0), axis=2)
    inside = member & (position < CAP)
    share = jnp.where(inside, routed, jnp.float32(0.0))
    spill = jnp.sum(jnp.where(inside, jnp.float32(0.0), routed), axis=2, keepdims=True)
    table = jnp.concatenate([share, spill], axis=2)
    table = jnp.transpose(table, (1, 0, 2)).reshape(rows, -1)
    high = lax.reduce_precision(table, 8, 7)
    low = table - high
    both = jnp.concatenate([high, low], axis=1).astype(jnp.bfloat16)
    return jnp.pad(both, ((0, 0), (0, LANES - both.shape[1])))


def layer_kernel(scalars, *refs, tick_idx, blocks, spare_count, tok_dev):
    x_refs, refs = refs[:blocks], refs[blocks:]
    table_ref, gain_ref, gate_ref, up_ref, down_ref = refs[:5]
    spare_refs, refs = refs[5:5 + spare_count], refs[5 + spare_count:]
    out_refs, (total_ref,) = refs[:blocks], refs[blocks:]
    group, expert = scalars[0], scalars[1]
    x = jnp.concatenate([x_ref[...] for x_ref in x_refs], axis=0)
    values = x.astype(jnp.float32)
    row_scale = lax.rsqrt(jnp.mean(values * values, axis=-1, keepdims=True) + EPSILON)
    normed = (values * row_scale * gain_ref[group]).astype(jnp.bfloat16)
    table = table_ref[...].astype(jnp.float32)
    lane = lax.broadcasted_iota(jnp.int32, table.shape, 1)
    width = TICKS * (EXPERTS + 1)

    def column(at):
        return jnp.sum(jnp.where((lane == at) | (lane == at + width), table, 0.0), axis=1, keepdims=True)

    share = column(tick_idx * (EXPERTS + 1) + expert)
    spill = column(tick_idx * (EXPERTS + 1) + EXPERTS)
    contract = (((1,), (1,)), ((), ()))

    def served(gate, up, down):
        gate_pre = lax.dot_general(normed, gate, contract, preferred_element_type=jnp.float32)
        up_pre = lax.dot_general(normed, up, contract, preferred_element_type=jnp.float32)
        hidden = (gate_pre / (1.0 + jnp.exp(-gate_pre)) * up_pre).astype(jnp.bfloat16)
        return jnp.dot(hidden, down, preferred_element_type=jnp.float32)

    total_ref[...] = share * served(gate_ref[group], up_ref[group], down_ref[group])
    for at, spare_ref in enumerate(spare_refs):

        def add(spare_ref=spare_ref):
            total_ref[...] += spill * served(spare_ref[0], spare_ref[1], spare_ref[2])

        if spare_count == 1:
            add()
        else:
            pl.when(group == at)(add)
    per = 2 * tok_dev
    first = total_ref[0:per, :]
    row = lax.broadcasted_iota(jnp.int32, (per, 1), 0)
    out_refs[0][...] = first + jnp.where(row < tok_dev, values[0:per], 0.0)
    for i in range(1, blocks):
        out_refs[i][...] = total_ref[i * per:(i + 1) * per, :].astype(jnp.bfloat16)


def run_layer(scalars, x_blocks, table, gain, weights, spares, *, tick_idx, tok_dev):
    blocks = len(x_blocks)
    rows = table.shape[0]
    width = gain.shape[-1]
    per = rows // blocks
    whole = pl.BlockSpec(memory_space=pltpu.VMEM)
    hidden = weights[0].shape[1] + spares[0].shape[1]
    return pl.pallas_call(
        functools.partial(
            layer_kernel, tick_idx=tick_idx, blocks=blocks, spare_count=len(spares), tok_dev=tok_dev
        ),
        out_shape=[jax.ShapeDtypeStruct((per, width), jnp.float32)]
        + [jax.ShapeDtypeStruct((per, width), jnp.bfloat16)] * (blocks - 1),
        in_specs=[pl.BlockSpec(memory_space=pltpu.SMEM)] + [whole] * (blocks + 5 + len(spares)),
        out_specs=[whole] * blocks,
        scratch_shapes=[pltpu.VMEM((rows, width), jnp.float32)],
        compiler_params=pltpu.CompilerParams(vmem_limit_bytes=16 * 1024 * 1024),
        cost_estimate=pl.CostEstimate(
            flops=6 * rows * hidden * width, bytes_accessed=6 * hidden * width, transcendentals=rows * hidden
        ),
        name="layer",
    )(scalars, *x_blocks, table, gain, *weights, *spares)


def pick_kernel(gate_ref, up_ref, down_ref, out_ref, sems, *, group):
    copies = [
        pltpu.make_async_copy(ref.at[group], out_ref.at[i], sems.at[i])
        for i, ref in enumerate((gate_ref, up_ref, down_ref))
    ]
    for copy in copies:
        copy.start()
    for copy in copies:
        copy.wait()


def picked(spares, group):
    return pl.pallas_call(
        functools.partial(pick_kernel, group=group),
        out_shape=jax.ShapeDtypeStruct((3,) + spares[0].shape[1:], spares[0].dtype),
        in_specs=[pl.BlockSpec(memory_space=pl.ANY)] * 3,
        out_specs=pl.BlockSpec(memory_space=pltpu.VMEM),
        scratch_shapes=[pltpu.SemaphoreType.DMA((3,))],
        name="pick",
    )(*spares)


def widest_first(outer):
    return range(outer - 1, 0, -1)


def added(values):
    total = values[0].astype(jnp.float32)
    for value in values[1:]:
        total = total + value.astype(jnp.float32)
    return total


def on_device(
    state, routes, gates, norm_gain, w_gate, w_up, w_down, spare_gate, spare_up, spare_down
):
    segments = lax.axis_size("segment")
    segment_idx = lax.axis_index("segment")
    members = lax.axis_size("expert")
    member_idx = lax.axis_index("expert")
    split_count = members // EXPERTS
    outer = members // 2
    assert outer & (outer - 1) == 0
    tok_dev = state.shape[1]
    width = state.shape[2]

    def spread(value):
        got = {j: moved(value, 2 * j, 0) for j in widest_first(outer)}
        return [value] + [got[j] for j in range(1, outer)]

    weights = [w_gate[:, 0], w_up[:, 0], w_down[:, 0]]
    spare_all = [spare_gate[:, 0], spare_up[:, 0], spare_down[:, 0]]
    spares = [moved(picked(spare_all, 0), 0, -1)]

    own = jnp.concatenate([state[0], coefficients(routes[:, 0], gates[:, 0])], axis=1)
    pair = jnp.concatenate([own, moved(own, 1, 0)], axis=0)
    arrived = spread(pair)
    x_blocks = [one[:, :width] for one in arrived]
    table = jnp.concatenate([one[:, width:] for one in arrived], axis=0)

    early = own
    for tick_idx in range(TICKS):
        group_idx = group_of(segment_idx, tick_idx, segments)
        if len(spares) == 1 and groups_at(tick_idx, segments) != {0}:
            spares.append(moved(picked(lax.optimization_barrier((*spare_all, early))[:3], 1), 0, -1))
        early = x_blocks[0]
        scalars = jnp.stack([group_idx, (member_idx // split_count).astype(jnp.int32)])
        parts = run_layer(
            scalars, x_blocks, table, norm_gain, weights, spares, tick_idx=tick_idx, tok_dev=tok_dev
        )
        got = [moved(parts[j], 2 * j, 0) for j in widest_first(outer)]
        total = added([parts[0]] + got)
        if tick_idx + 1 == TICKS:
            other = moved(total[tok_dev:].astype(jnp.bfloat16), 1, 0)
            return added([total[:tok_dev], other]).astype(jnp.bfloat16)[None]
        total = total.astype(jnp.bfloat16)
        across = moved(total, 1, 1)
        along = moved(total, 0, 1)
        across = jnp.concatenate([across[tok_dev:], across[:tok_dev]], axis=0)
        x_blocks = spread(added([along, across]).astype(jnp.bfloat16))


def solution(mesh):
    return jax.shard_map(
        on_device,
        mesh=mesh,
        in_specs=(
            P("segment", "expert", None),
            P(None, "segment", "expert", None),
            P(None, "segment", "expert", None),
            P(None, "segment", None),
            P(None, "segment", "expert", None),
            P(None, "segment", "expert", None),
            P(None, "segment", "expert", None),
            P(None, "segment", "expert", None),
            P(None, "segment", "expert", None),
            P(None, "segment", "expert", None),
        ),
        out_specs=P("segment", "expert", None),
        check_vma=False,
    )
```

time: 177 us -> 155 us (0.88)
  blocking collectives: 27.8 us -> 0 us
  starting transfers between devices: 28.5 us -> 44.8 us
  local copies, waits for them, and re-layouts: 42 us -> 30.1 us
  Pallas kernels: 15.3 us -> 22.9 us
  other arithmetic: 6.99 us -> 1.66 us
    all_to_all x6 -> x0, waiting for transfers between devices: 46.9 us -> none  [the longest x3 21.6 us: on_device(): lax.all_to_all(sent.reshape(segments * members, tok_dev, part), everyone,...]
    ppermute x6 -> x34, waiting for transfers between devices: 8.21 us -> 54.2 us  [moved(): return lax.ppermute(value, BOTH, pairs)]
    ppermute x6 -> x34, starting transfers between devices: 5.39 us -> 44.8 us  [moved(): return lax.ppermute(value, BOTH, pairs)]
    all_to_all x2 -> x0, blocking collectives: 27.8 us -> none  [on_device(): lax.all_to_all(partial_sum.reshape(segments * members, tok_dev, part), ev...]
    all_to_all x6 -> x0, starting transfers between devices: 23.1 us -> none  [the longest x3 7.75 us: on_device(): lax.all_to_all(sent.reshape(segments * members, tok_dev, part), everyone,...]
    pallas_call x4 -> x6, Pallas kernels: 15.3 us -> 22.9 us  [the longest x4 17.3 us: run_layer(): pl.pallas_call(functools.partial(layer_kernel, tick_idx=tick_idx, blocks=...]
    another operation x8 -> x5, other arithmetic: 5.63 us -> 0.31 us  [the longest x4 0.3 us: on_device(): jnp.stack([group_idx, (member_idx // split_count).astype(jnp.int32)])]
    squeeze x3 -> x0, local copies, waits for them, and re-layouts: 4.76 us -> none  [on_device(): second = [from_behind(one[1], 'segment', -1) for one in spare_stack]]
  transfers between devices with their start and end apart: 12 -> 34, of which waited for: 8 -> 26; matrix products, arithmetic and copies ran while one was open for 6% -> 1% of each run, Pallas kernels for 2% -> 4%
where the time goes in v2:
time: 155 us; the launch traced here: 154 us
  waiting for transfers between devices  54.2 us (35%)
  starting transfers between devices  44.8 us (29%)
  local copies, waits for them, and re-layouts  30.1 us (19%)
  Pallas kernels  22.9 us (15%)
  other arithmetic  1.66 us (1%)
    ppermute x34, waiting for transfers between devices, moved(): return lax.ppermute(value, BOTH, pairs)  54.2 us
    ppermute x34, starting transfers between devices, moved(): return lax.ppermute(value, BOTH, pairs)  44.8 us
    unnamed x33, local copies, waits for them, and re-layouts  29.9 us
    pallas_call x4, Pallas kernels, run_layer(): pl.pallas_call(functools.partial(layer_kernel, tick_idx=tick_idx, blocks=...  17.3 us
    pallas_call x2, Pallas kernels, picked(): pl.pallas_call(functools.partial(pick_kernel, group=group), out_shape=jax...  5.62 us
  transfers between devices with their start and end apart: 34, of which 26 were waited for; matrix products, arithmetic and copies ran while one was open for 1% of the time, Pallas kernels for 4%

profile of v2, /device:TPU:0, one launch (start us, length us, event | category | flops | bytes accessed | tf_op | source)
XLA Modules:
  0.0 154.1 jit_solution(2768267018332180320)
XLA Ops:
  0.0 2.8 %pick.2 = bf16[3,160,2048]{2,1,0:T(8,128)(2,1)} custom-call(bf16[2,160,2048]{2,1,0:T(8,128)(2,1)} %bitcast.33, bf16[2,160,2048]{2,1,0:T(8,128)(2,1)} %bitcast.35, bf16[2,160,2048]{2,1,0:T(8,128)(2,1)} %bitcast.37), custom_call_target="tpu_custom_call" | custom-call | tf_op jit(solution)/shard_map/pick/pallas_call | solution.py:145
  2.8 2.5 %collective-permute-start.4 = (bf16[3,160,2048]{2,1,0:T(8,128)(2,1)}, bf16[3,160,2048]{2,1,0:T(8,128)(2,1)S(1)}, u32[]{:S(2)}, u32[]{:S(2)}) collective-permute-start(bf16[3,160,2048]{2,1,0:T(8,128)(2,1)} %pick.2), channel_id=1, source_target_pairs={{0,24},{1,25},{2,26},{3,27},{4,28},{5,29},{6,30},{7,31},{8,0},{9,1... | collective-permute-start | bytes 5898248 | tf_op jit(solution)/shard_map/ppermute | solution.py:27
  6.2 1.6 %collective-permute-start = (bf16[8,2176]{1,0:T(8,128)(2,1)S(1)}, bf16[8,2176]{1,0:T(8,128)(2,1)S(1)}, u32[]{:S(2)}, u32[]{:S(2)}) collective-permute-start(bf16[8,2176]{1,0:T(8,128)(2,1)S(1)} %pad_maximum_fusion.1), channel_id=1, source_target_pairs={{0,1},{1,0},{2,3},{3,2},{4,5},{5,4},{6,7},{7,6},{8,9},{9,8},{10,11... | collective-permute-start | bytes 104456 | tf_op jit(solution)/shard_map/ppermute | solution.py:27
  7.7 2.4 %collective-permute-done = bf16[8,2176]{1,0:T(8,128)(2,1)S(1)} collective-permute-done((bf16[8,2176]{1,0:T(8,128)(2,1)S(1)}, bf16[8,2176]{1,0:T(8,128)(2,1)S(1)}, u32[]{:S(2)}, u32[]{:S(2)}) %collective-permute-start) | collective-permute-done | bytes 34848 | tf_op jit(solution)/shard_map/ppermute | solution.py:27
  10.2 2.8 %pick.3 = bf16[3,160,2048]{2,1,0:T(8,128)(2,1)} custom-call(bf16[2,160,2048]{2,1,0:T(8,128)(2,1)} %bitcast.34, bf16[2,160,2048]{2,1,0:T(8,128)(2,1)} %bitcast.36, bf16[2,160,2048]{2,1,0:T(8,128)(2,1)} %bitcast.38), custom_call_target="tpu_custom_call" | custom-call | tf_op jit(solution)/shard_map/pick/pallas_call | solution.py:145
  13.1 1.6 %collective-permute-start.1 = (bf16[16,2176]{1,0:T(8,128)(2,1)S(1)}, bf16[16,2176]{1,0:T(8,128)(2,1)S(1)}, u32[]{:S(2)}, u32[]{:S(2)}) collective-permute-start(bf16[16,2176]{1,0:T(8,128)(2,1)S(1)} %pad_maximum_fusion), channel_id=1, source_target_pairs={{0,2},{1,3},{2,0},{3,1},{4,6},{5,7},{6,4},{7,5},{8,10},{9,11},{10,... | collective-permute-start | bytes 208904 | tf_op jit(solution)/shard_map/ppermute | solution.py:27
  14.8 2.6 %collective-permute-start.2 = (bf16[16,2176]{1,0:T(8,128)(2,1)S(1)}, bf16[16,2176]{1,0:T(8,128)(2,1)S(1)}, u32[]{:S(2)}, u32[]{:S(2)}) collective-permute-start(bf16[16,2176]{1,0:T(8,128)(2,1)S(1)} %pad_maximum_fusion), channel_id=1, source_target_pairs={{0,4},{1,5},{2,6},{3,7},{4,0},{5,1},{6,2},{7,3},{8,12},{9,13},{10,... | collective-permute-start | bytes 208904 | tf_op jit(solution)/shard_map/ppermute | solution.py:27
  17.7 5.0 %collective-permute-done.2 = bf16[16,2176]{1,0:T(8,128)(2,1)S(1)} collective-permute-done((bf16[16,2176]{1,0:T(8,128)(2,1)S(1)}, bf16[16,2176]{1,0:T(8,128)(2,1)S(1)}, u32[]{:S(2)}, u32[]{:S(2)}) %collective-permute-start.2) | collective-permute-done | bytes 69664 | tf_op jit(solution)/shard_map/ppermute | solution.py:27
  23.5 4.3 %collective-permute-done.4.refs_9_ = bf16[3,160,2048]{2,1,0:T(8,128)(2,1)S(1)} collective-permute-done((bf16[3,160,2048]{2,1,0:T(8,128)(2,1)}, bf16[3,160,2048]{2,1,0:T(8,128)(2,1)S(1)}, u32[]{:S(2)}, u32[]{:S(2)}) %collective-permute-start.4) | collective-permute-done | bytes 1966112 | tf_op jit(solution)/shard_map/ppermute | solution.py:27
  27.8 2.5 %copy-done = bf16[2,1,640,2048]{3,2,1,0:T(8,128)(2,1)S(1)} copy-done((bf16[2,1,640,2048]{3,2,1,0:T(8,128)(2,1)S(1)}, bf16[2,1,640,2048]{3,2,1,0:T(8,128)(2,1)}, u32[]{:S(2)}) %copy-start) | copy-done | bytes 5242904
  30.3 2.5 %copy-done.4 = bf16[2,1,640,2048]{3,2,1,0:T(8,128)(2,1)S(1)} copy-done((bf16[2,1,640,2048]{3,2,1,0:T(8,128)(2,1)S(1)}, bf16[2,1,640,2048]{3,2,1,0:T(8,128)(2,1)}, u32[]{:S(2)}) %copy-start.4) | copy-done | bytes 5242904
  32.8 2.5 %copy-done.8 = bf16[2,1,640,2048]{3,2,1,0:T(8,128)(2,1)S(1)} copy-done((bf16[2,1,640,2048]{3,2,1,0:T(8,128)(2,1)S(1)}, bf16[2,1,640,2048]{3,2,1,0:T(8,128)(2,1)}, u32[]{:S(2)}) %copy-start.8) | copy-done | bytes 5242904
  35.2 3.4 %layer.4 = (f32[16,2048]{1,0:T(8,128)S(1)}, bf16[16,2048]{1,0:T(8,128)(2,1)S(1)}, bf16[16,2048]{1,0:T(8,128)(2,1)S(1)}, bf16[16,2048]{1,0:T(8,128)(2,1)S(1)}) custom-call(s32[2]{0:T(128)S(1)} %pad_add_fusion.3.scalars, bf16[16,2048]{1,0:T(8,128)(2,1)S(1)} %slice.65.refs_0_, bf16[16,2048]{1,0:T(8,128)(2,1)S(1)} %slice.66.refs_1_, ...), custom_call_target="tpu_custom_call" | custom-call | flops 629145600 | bytes 9830400 | tf_op jit(solution)/shard_map/layer/pallas_call | solution.py:116
  38.7 3.7 %collective-permute-start.5 = (bf16[16,2048]{1,0:T(8,128)(2,1)S(1)}, bf16[16,2048]{1,0:T(8,128)(2,1)S(1)}, u32[]{:S(2)}, u32[]{:S(2)}) collective-permute-start(bf16[16,2048]{1,0:T(8,128)(2,1)S(1)} %get-tuple-element.25), channel_id=1, source_target_pairs={{0,6},{1,7},{2,4},{3,5},{4,2},{5,3},{6,0},{7,1},{8,14},{9,15},{10,... | collective-permute-start | bytes 196616 | tf_op jit(solution)/shard_map/ppermute | solution.py:27
  43.2 2.4 %collective-permute-done.5 = bf16[16,2048]{1,0:T(8,128)(2,1)S(1)} collective-permute-done((bf16[16,2048]{1,0:T(8,128)(2,1)S(1)}, bf16[16,2048]{1,0:T(8,128)(2,1)S(1)}, u32[]{:S(2)}, u32[]{:S(2)}) %collective-permute-start.5) | collective-permute-done | bytes 65568 | tf_op jit(solution)/shard_map/ppermute | solution.py:27
  45.6 3.2 %collective-permute-done.6 = bf16[16,2048]{1,0:T(8,128)(2,1)S(1)} collective-permute-done((bf16[16,2048]{1,0:T(8,128)(2,1)S(1)}, bf16[16,2048]{1,0:T(8,128)(2,1)S(1)}, u32[]{:S(2)}, u32[]{:S(2)}) %collective-permute-start.6) | collective-permute-done | bytes 65568 | tf_op jit(solution)/shard_map/ppermute | solution.py:27
  50.3 3.2 %collective-permute-done.9 = bf16[16,2048]{1,0:T(8,128)(2,1)S(1)} collective-permute-done((bf16[16,2048]{1,0:T(8,128)(2,1)S(1)}, bf16[16,2048]{1,0:T(8,128)(2,1)S(1)}, u32[]{:S(2)}, u32[]{:S(2)}) %collective-permute-start.9) | collective-permute-done | bytes 65568 | tf_op jit(solution)/shard_map/ppermute | solution.py:27
  55.5 1.8 %collective-permute-start.11 = (bf16[16,2048]{1,0:T(8,128)(2,1)S(1)}, bf16[16,2048]{1,0:T(8,128)(2,1)S(1)}, u32[]{:S(2)}, u32[]{:S(2)}) collective-permute-start(bf16[16,2048]{1,0:T(8,128)(2,1)S(1)} %add_convert_fusion.4.refs_0_), channel_id=1, source_target_pairs={{0,4},{1,5},{2,6},{3,7},{4,0},{5,1},{6,2},{7,3},{8,12},{9,13},{10,... | collective-permute-start | bytes 196616 | tf_op jit(solution)/shard_map/ppermute | solution.py:27
  58.8 3.2 %collective-permute-done.11.refs_2_ = bf16[16,2048]{1,0:T(8,128)(2,1)S(1)} collective-permute-done((bf16[16,2048]{1,0:T(8,128)(2,1)S(1)}, bf16[16,2048]{1,0:T(8,128)(2,1)S(1)}, u32[]{:S(2)}, u32[]{:S(2)}) %collective-permute-start.11) | collective-permute-done | bytes 65568 | tf_op jit(solution)/shard_map/ppermute | solution.py:27
  63.4 2.5 %copy-done.1 = bf16[2,1,640,2048]{3,2,1,0:T(8,128)(2,1)S(1)} copy-done((bf16[2,1,640,2048]{3,2,1,0:T(8,128)(2,1)S(1)}, bf16[2,1,640,2048]{3,2,1,0:T(8,128)(2,1)}, u32[]{:S(2)}) %copy-start.1) | copy-done | bytes 5242904
  65.9 2.5 %copy-done.5 = bf16[2,1,640,2048]{3,2,1,0:T(8,128)(2,1)S(1)} copy-done((bf16[2,1,640,2048]{3,2,1,0:T(8,128)(2,1)S(1)}, bf16[2,1,640,2048]{3,2,1,0:T(8,128)(2,1)}, u32[]{:S(2)}) %copy-start.5) | copy-done | bytes 5242904
  68.4 2.5 %copy-done.9 = bf16[2,1,640,2048]{3,2,1,0:T(8,128)(2,1)S(1)} copy-done((bf16[2,1,640,2048]{3,2,1,0:T(8,128)(2,1)S(1)}, bf16[2,1,640,2048]{3,2,1,0:T(8,128)(2,1)}, u32[]{:S(2)}) %copy-start.9) | copy-done | bytes 5242904
  70.9 4.6 %layer.5 = (f32[16,2048]{1,0:T(8,128)S(1)}, bf16[16,2048]{1,0:T(8,128)(2,1)S(1)}, bf16[16,2048]{1,0:T(8,128)(2,1)S(1)}, bf16[16,2048]{1,0:T(8,128)(2,1)S(1)}) custom-call(s32[2]{0:T(128)S(1)} %pad_add_fusion.2.scalars, bf16[16,2048]{1,0:T(8,128)(2,1)S(1)} %add_convert_fusion.4.refs_0_, bf16[16,2048]{1,0:T(8,128)(2,1)S(1)} %collective-permute-done.10.refs_1_, ...), custom_call_target="tpu_custom_call" | custom-call | flops 629145600 | bytes 9830400 | tf_op jit(solution)/shard_map/layer/pallas_call | solution.py:116
  75.5 1.4 collective-permute-start.14
  76.9 3.0 %collective-permute-start.16 = (bf16[16,2048]{1,0:T(8,128)(2,1)S(1)}, bf16[16,2048]{1,0:T(8,128)(2,1)S(1)}, u32[]{:S(2)}, u32[]{:S(2)}) collective-permute-start(bf16[16,2048]{1,0:T(8,128)(2,1)S(1)} %get-tuple-element.34), channel_id=1, source_target_pairs={{0,2},{1,3},{2,0},{3,1},{4,6},{5,7},{6,4},{7,5},{8,10},{9,11},{10,... | collective-permute-start | bytes 196616 | tf_op jit(solution)/shard_map/ppermute | solution.py:27
  80.0 1.7 %collective-permute-done.14 = bf16[16,2048]{1,0:T(8,128)(2,1)S(1)} collective-permute-done((bf16[16,2048]{1,0:T(8,128)(2,1)S(1)}, bf16[16,2048]{1,0:T(8,128)(2,1)S(1)}, u32[]{:S(2)}, u32[]{:S(2)}) %collective-permute-start.14) | collective-permute-done | bytes 65568 | tf_op jit(solution)/shard_map/ppermute | solution.py:27
  84.4 3.4 %collective-permute-done.18 = bf16[16,2048]{1,0:T(8,128)(2,1)S(1)} collective-permute-done((bf16[16,2048]{1,0:T(8,128)(2,1)S(1)}, bf16[16,2048]{1,0:T(8,128)(2,1)S(1)}, u32[]{:S(2)}, u32[]{:S(2)}) %collective-permute-start.18) | collective-permute-done | bytes 65568 | tf_op jit(solution)/shard_map/ppermute | solution.py:27
  90.2 2.0 %collective-permute-start.21 = (bf16[16,2048]{1,0:T(8,128)(2,1)S(1)}, bf16[16,2048]{1,0:T(8,128)(2,1)S(1)}, u32[]{:S(2)}, u32[]{:S(2)}) collective-permute-start(bf16[16,2048]{1,0:T(8,128)(2,1)S(1)} %add_convert_fusion.2.refs_0_), channel_id=1, source_target_pairs={{0,6},{1,7},{2,4},{3,5},{4,2},{5,3},{6,0},{7,1},{8,14},{9,15},{10,... | collective-permute-start | bytes 196616 | tf_op jit(solution)/shard_map/ppermute | solution.py:27
  92.5 2.6 %collective-permute-done.20.refs_2_ = bf16[16,2048]{1,0:T(8,128)(2,1)S(1)} collective-permute-done((bf16[16,2048]{1,0:T(8,128)(2,1)S(1)}, bf16[16,2048]{1,0:T(8,128)(2,1)S(1)}, u32[]{:S(2)}, u32[]{:S(2)}) %collective-permute-start.20) | collective-permute-done | bytes 65568 | tf_op jit(solution)/shard_map/ppermute | solution.py:27
  96.4 2.5 %copy-done.2 = bf16[2,1,640,2048]{3,2,1,0:T(8,128)(2,1)S(1)} copy-done((bf16[2,1,640,2048]{3,2,1,0:T(8,128)(2,1)S(1)}, bf16[2,1,640,2048]{3,2,1,0:T(8,128)(2,1)}, u32[]{:S(2)}) %copy-start.2) | copy-done | bytes 5242904
  98.9 2.5 %copy-done.6 = bf16[2,1,640,2048]{3,2,1,0:T(8,128)(2,1)S(1)} copy-done((bf16[2,1,640,2048]{3,2,1,0:T(8,128)(2,1)S(1)}, bf16[2,1,640,2048]{3,2,1,0:T(8,128)(2,1)}, u32[]{:S(2)}) %copy-start.6) | copy-done | bytes 5242904
  101.4 2.5 %copy-done.10 = bf16[2,1,640,2048]{3,2,1,0:T(8,128)(2,1)S(1)} copy-done((bf16[2,1,640,2048]{3,2,1,0:T(8,128)(2,1)S(1)}, bf16[2,1,640,2048]{3,2,1,0:T(8,128)(2,1)}, u32[]{:S(2)}) %copy-start.10) | copy-done | bytes 5242904
  103.9 4.6 %layer.6 = (f32[16,2048]{1,0:T(8,128)S(1)}, bf16[16,2048]{1,0:T(8,128)(2,1)S(1)}, bf16[16,2048]{1,0:T(8,128)(2,1)S(1)}, bf16[16,2048]{1,0:T(8,128)(2,1)S(1)}) custom-call(s32[2]{0:T(128)S(1)} %pad_add_fusion.1.scalars, bf16[16,2048]{1,0:T(8,128)(2,1)S(1)} %add_convert_fusion.2.refs_0_, bf16[16,2048]{1,0:T(8,128)(2,1)S(1)} %collective-permute-done.19.refs_1_, ...), custom_call_target="tpu_custom_call" | custom-call | flops 629145600 | bytes 9830400 | tf_op jit(solution)/shard_map/layer/pallas_call | solution.py:116
  108.5 2.0 %collective-permute-start.22 = (bf16[16,2048]{1,0:T(8,128)(2,1)S(1)}, bf16[16,2048]{1,0:T(8,128)(2,1)S(1)}, u32[]{:S(2)}, u32[]{:S(2)}) collective-permute-start(bf16[16,2048]{1,0:T(8,128)(2,1)S(1)} %get-tuple-element.36), channel_id=1, source_target_pairs={{0,6},{1,7},{2,4},{3,5},{4,2},{5,3},{6,0},{7,1},{8,14},{9,15},{10,... | collective-permute-start | bytes 196616 | tf_op jit(solution)/shard_map/ppermute | solution.py:27
  110.6 2.3 %collective-permute-start.24 = (bf16[16,2048]{1,0:T(8,128)(2,1)S(1)}, bf16[16,2048]{1,0:T(8,128)(2,1)S(1)}, u32[]{:S(2)}, u32[]{:S(2)}) collective-permute-start(bf16[16,2048]{1,0:T(8,128)(2,1)S(1)} %get-tuple-element.38), channel_id=1, source_target_pairs={{0,2},{1,3},{2,0},{3,1},{4,6},{5,7},{6,4},{7,5},{8,10},{9,11},{10,... | collective-permute-start | bytes 196616 | tf_op jit(solution)/shard_map/ppermute | solution.py:27
  112.9 1.7 %collective-permute-done.22 = bf16[16,2048]{1,0:T(8,128)(2,1)S(1)} collective-permute-done((bf16[16,2048]{1,0:T(8,128)(2,1)S(1)}, bf16[16,2048]{1,0:T(8,128)(2,1)S(1)}, u32[]{:S(2)}, u32[]{:S(2)}) %collective-permute-start.22) | collective-permute-done | bytes 65568 | tf_op jit(solution)/shard_map/ppermute | solution.py:27
  117.5 3.3 %collective-permute-done.26 = bf16[16,2048]{1,0:T(8,128)(2,1)S(1)} collective-permute-done((bf16[16,2048]{1,0:T(8,128)(2,1)S(1)}, bf16[16,2048]{1,0:T(8,128)(2,1)S(1)}, u32[]{:S(2)}, u32[]{:S(2)}) %collective-permute-start.26) | collective-permute-done | bytes 65568 | tf_op jit(solution)/shard_map/ppermute | solution.py:27
  122.2 1.5 %collective-permute-start.28 = (bf16[16,2048]{1,0:T(8,128)(2,1)S(1)}, bf16[16,2048]{1,0:T(8,128)(2,1)S(1)}, u32[]{:S(2)}, u32[]{:S(2)}) collective-permute-start(bf16[16,2048]{1,0:T(8,128)(2,1)S(1)} %add_convert_fusion.refs_0_), channel_id=1, source_target_pairs={{0,4},{1,5},{2,6},{3,7},{4,0},{5,1},{6,2},{7,3},{8,12},{9,13},{10,... | collective-permute-start | bytes 196616 | tf_op jit(solution)/shard_map/ppermute | solution.py:27
  123.7 1.7 %collective-permute-start.29 = (bf16[16,2048]{1,0:T(8,128)(2,1)S(1)}, bf16[16,2048]{1,0:T(8,128)(2,1)S(1)}, u32[]{:S(2)}, u32[]{:S(2)}) collective-permute-start(bf16[16,2048]{1,0:T(8,128)(2,1)S(1)} %add_convert_fusion.refs_0_), channel_id=1, source_target_pairs={{0,6},{1,7},{2,4},{3,5},{4,2},{5,3},{6,0},{7,1},{8,14},{9,15},{10,... | collective-permute-start | bytes 196616 | tf_op jit(solution)/shard_map/ppermute | solution.py:27
  125.5 2.9 %collective-permute-done.28.refs_2_ = bf16[16,2048]{1,0:T(8,128)(2,1)S(1)} collective-permute-done((bf16[16,2048]{1,0:T(8,128)(2,1)S(1)}, bf16[16,2048]{1,0:T(8,128)(2,1)S(1)}, u32[]{:S(2)}, u32[]{:S(2)}) %collective-permute-start.28) | collective-permute-done | bytes 65568 | tf_op jit(solution)/shard_map/ppermute | solution.py:27
  129.8 2.5 %copy-done.3 = bf16[2,1,640,2048]{3,2,1,0:T(8,128)(2,1)S(1)} copy-done((bf16[2,1,640,2048]{3,2,1,0:T(8,128)(2,1)S(1)}, bf16[2,1,640,2048]{3,2,1,0:T(8,128)(2,1)}, u32[]{:S(2)}) %copy-start.3) | copy-done | bytes 5242904
  132.3 2.5 %copy-done.7 = bf16[2,1,640,2048]{3,2,1,0:T(8,128)(2,1)S(1)} copy-done((bf16[2,1,640,2048]{3,2,1,0:T(8,128)(2,1)S(1)}, bf16[2,1,640,2048]{3,2,1,0:T(8,128)(2,1)}, u32[]{:S(2)}) %copy-start.7) | copy-done | bytes 5242904
  134.8 2.5 %copy-done.11 = bf16[2,1,640,2048]{3,2,1,0:T(8,128)(2,1)S(1)} copy-done((bf16[2,1,640,2048]{3,2,1,0:T(8,128)(2,1)S(1)}, bf16[2,1,640,2048]{3,2,1,0:T(8,128)(2,1)}, u32[]{:S(2)}) %copy-start.11) | copy-done | bytes 5242904
  137.3 4.6 %layer.7 = (f32[16,2048]{1,0:T(8,128)S(1)}, bf16[16,2048]{1,0:T(8,128)(2,1)S(1)}, bf16[16,2048]{1,0:T(8,128)(2,1)S(1)}, bf16[16,2048]{1,0:T(8,128)(2,1)S(1)}) custom-call(s32[2]{0:T(128)S(1)} %pad_add_fusion.scalars, bf16[16,2048]{1,0:T(8,128)(2,1)S(1)} %add_convert_fusion.refs_0_, bf16[16,2048]{1,0:T(8,128)(2,1)S(1)} %collective-permute-done.27.refs_1_, ...), custom_call_target="tpu_custom_call" | custom-call | flops 629145600 | bytes 9830400 | tf_op jit(solution)/shard_map/layer/pallas_call | solution.py:116
  141.9 1.8 %collective-permute-start.30 = (bf16[16,2048]{1,0:T(8,128)(2,1)S(1)}, bf16[16,2048]{1,0:T(8,128)(2,1)S(1)}, u32[]{:S(2)}, u32[]{:S(2)}) collective-permute-start(bf16[16,2048]{1,0:T(8,128)(2,1)S(1)} %get-tuple-element.40), channel_id=1, source_target_pairs={{0,6},{1,7},{2,4},{3,5},{4,2},{5,3},{6,0},{7,1},{8,14},{9,15},{10,... | collective-permute-start | bytes 196616 | tf_op jit(solution)/shard_map/ppermute | solution.py:27
  143.7 2.7 %collective-permute-start.32 = (bf16[16,2048]{1,0:T(8,128)(2,1)S(1)}, bf16[16,2048]{1,0:T(8,128)(2,1)S(1)}, u32[]{:S(2)}, u32[]{:S(2)}) collective-permute-start(bf16[16,2048]{1,0:T(8,128)(2,1)S(1)} %get-tuple-element.42), channel_id=1, source_target_pairs={{0,2},{1,3},{2,0},{3,1},{4,6},{5,7},{6,4},{7,5},{8,10},{9,11},{10,... | collective-permute-start | bytes 196616 | tf_op jit(solution)/shard_map/ppermute | solution.py:27
  146.4 1.7 %collective-permute-done.30 = bf16[16,2048]{1,0:T(8,128)(2,1)S(1)} collective-permute-done((bf16[16,2048]{1,0:T(8,128)(2,1)S(1)}, bf16[16,2048]{1,0:T(8,128)(2,1)S(1)}, u32[]{:S(2)}, u32[]{:S(2)}) %collective-permute-start.30) | collective-permute-done | bytes 65568 | tf_op jit(solution)/shard_map/ppermute | solution.py:27
  150.4 3.1 %collective-permute-done.33 = bf16[8,2048]{1,0:T(8,128)(2,1)S(1)} collective-permute-done((bf16[8,2048]{1,0:T(8,128)(2,1)S(1)}, bf16[8,2048]{1,0:T(8,128)(2,1)S(1)}, u32[]{:S(2)}, u32[]{:S(2)}) %collective-permute-start.33) | collective-permute-done | bytes 32800 | tf_op jit(solution)/shard_map/ppermute | solution.py:27
  (98 shorter events, 24.7 us)
Async XLA Ops:
  0.0 5.3 %copy-start.14 = (s32[4,1,8,2]{2,3,1,0:T(2,128)S(1)}, s32[4,1,8,2]{2,3,1,0:T(2,128)}, u32[]{:S(2)}) copy-start(s32[4,1,8,2]{2,3,1,0:T(2,128)} %param.11) | copy-start | bytes 772
  0.0 5.3 %copy-start.15 = (f32[4,1,8,2]{2,3,1,0:T(2,128)S(1)}, f32[4,1,8,2]{2,3,1,0:T(2,128)}, u32[]{:S(2)}) copy-start(f32[4,1,8,2]{2,3,1,0:T(2,128)} %param.12) | copy-start | bytes 772
  0.0 6.1 %copy-start.13 = (bf16[1,8,2048]{2,1,0:T(8,128)(2,1)S(1)}, bf16[1,8,2048]{2,1,0:T(8,128)(2,1)}, u32[]{:S(2)}) copy-start(bf16[1,8,2048]{2,1,0:T(8,128)(2,1)} %param.10) | copy-start | bytes 98308
  2.8 25.0 %collective-permute-start.4 = (bf16[3,160,2048]{2,1,0:T(8,128)(2,1)}, bf16[3,160,2048]{2,1,0:T(8,128)(2,1)S(1)}, u32[]{:S(2)}, u32[]{:S(2)}) collective-permute-start(bf16[3,160,2048]{2,1,0:T(8,128)(2,1)} %pick.2), channel_id=1, source_target_pairs={{0,24},{1,25},{2,26},{3,27},{4,28},{5,29},{6,30},{7,31},{8,0},{9,1... | collective-permute-start | bytes 5898248 | tf_op jit(solution)/shard_map/ppermute | solution.py:27
  6.2 4.0 %collective-permute-start = (bf16[8,2176]{1,0:T(8,128)(2,1)S(1)}, bf16[8,2176]{1,0:T(8,128)(2,1)S(1)}, u32[]{:S(2)}, u32[]{:S(2)}) collective-permute-start(bf16[8,2176]{1,0:T(8,128)(2,1)S(1)} %pad_maximum_fusion.1), channel_id=1, source_target_pairs={{0,1},{1,0},{2,3},{3,2},{4,5},{5,4},{6,7},{7,6},{8,9},{9,8},{10,11... | collective-permute-start | bytes 104456 | tf_op jit(solution)/shard_map/ppermute | solution.py:27
  10.2 17.6 %copy-start.12 = (f32[2,1,2048]{2,1,0:T(1,128)S(1)}, f32[2,1,2048]{2,1,0:T(1,128)}, u32[]{:S(2)}) copy-start(f32[2,1,2048]{2,1,0:T(1,128)} %refs_5_.7) | copy-start | bytes 49156
  13.0 45.7 %collective-permute-start.13 = (bf16[3,160,2048]{2,1,0:T(8,128)(2,1)}, bf16[3,160,2048]{2,1,0:T(8,128)(2,1)}, u32[]{:S(2)}, u32[]{:S(2)}) collective-permute-start(bf16[3,160,2048]{2,1,0:T(8,128)(2,1)} %pick.3), channel_id=1, source_target_pairs={{0,24},{1,25},{2,26},{3,27},{4,28},{5,29},{6,30},{7,31},{8,0},{9,1... | collective-permute-start | bytes 5898248 | tf_op jit(solution)/shard_map/ppermute | solution.py:27
  13.1 4.5 %collective-permute-start.1 = (bf16[16,2176]{1,0:T(8,128)(2,1)S(1)}, bf16[16,2176]{1,0:T(8,128)(2,1)S(1)}, u32[]{:S(2)}, u32[]{:S(2)}) collective-permute-start(bf16[16,2176]{1,0:T(8,128)(2,1)S(1)} %pad_maximum_fusion), channel_id=1, source_target_pairs={{0,2},{1,3},{2,0},{3,1},{4,6},{5,7},{6,4},{7,5},{8,10},{9,11},{10,... | collective-permute-start | bytes 208904 | tf_op jit(solution)/shard_map/ppermute | solution.py:27
  14.8 7.9 %collective-permute-start.2 = (bf16[16,2176]{1,0:T(8,128)(2,1)S(1)}, bf16[16,2176]{1,0:T(8,128)(2,1)S(1)}, u32[]{:S(2)}, u32[]{:S(2)}) collective-permute-start(bf16[16,2176]{1,0:T(8,128)(2,1)S(1)} %pad_maximum_fusion), channel_id=1, source_target_pairs={{0,4},{1,5},{2,6},{3,7},{4,0},{5,1},{6,2},{7,3},{8,12},{9,13},{10,... | collective-permute-start | bytes 208904 | tf_op jit(solution)/shard_map/ppermute | solution.py:27
  17.3 6.1 %collective-permute-start.3 = (bf16[16,2176]{1,0:T(8,128)(2,1)S(1)}, bf16[16,2176]{1,0:T(8,128)(2,1)S(1)}, u32[]{:S(2)}, u32[]{:S(2)}) collective-permute-start(bf16[16,2176]{1,0:T(8,128)(2,1)S(1)} %pad_maximum_fusion), channel_id=1, source_target_pairs={{0,6},{1,7},{2,4},{3,5},{4,2},{5,3},{6,0},{7,1},{8,14},{9,15},{10,... | collective-permute-start | bytes 208904 | tf_op jit(solution)/shard_map/ppermute | solution.py:27
  27.8 2.5 %copy-start = (bf16[2,1,640,2048]{3,2,1,0:T(8,128)(2,1)S(1)}, bf16[2,1,640,2048]{3,2,1,0:T(8,128)(2,1)}, u32[]{:S(2)}) copy-start(bf16[2,1,640,2048]{3,2,1,0:T(8,128)(2,1)} %param.14) | copy-start | bytes 15728644
  30.3 2.5 %copy-start.4 = (bf16[2,1,640,2048]{3,2,1,0:T(8,128)(2,1)S(1)}, bf16[2,1,640,2048]{3,2,1,0:T(8,128)(2,1)}, u32[]{:S(2)}) copy-start(bf16[2,1,640,2048]{3,2,1,0:T(8,128)(2,1)} %param.15) | copy-start | bytes 15728644
  32.8 2.5 %copy-start.8 = (bf16[2,1,640,2048]{3,2,1,0:T(8,128)(2,1)S(1)}, bf16[2,1,640,2048]{3,2,1,0:T(8,128)(2,1)}, u32[]{:S(2)}) copy-start(bf16[2,1,640,2048]{3,2,1,0:T(8,128)(2,1)} %param.16) | copy-start | bytes 15728644
  38.7 6.9 %collective-permute-start.5 = (bf16[16,2048]{1,0:T(8,128)(2,1)S(1)}, bf16[16,2048]{1,0:T(8,128)(2,1)S(1)}, u32[]{:S(2)}, u32[]{:S(2)}) collective-permute-start(bf16[16,2048]{1,0:T(8,128)(2,1)S(1)} %get-tuple-element.25), channel_id=1, source_target_pairs={{0,6},{1,7},{2,4},{3,5},{4,2},{5,3},{6,0},{7,1},{8,14},{9,15},{10,... | collective-permute-start | bytes 196616 | tf_op jit(solution)/shard_map/ppermute | solution.py:27
  42.4 6.4 %collective-permute-start.6 = (bf16[16,2048]{1,0:T(8,128)(2,1)S(1)}, bf16[16,2048]{1,0:T(8,128)(2,1)S(1)}, u32[]{:S(2)}, u32[]{:S(2)}) collective-permute-start(bf16[16,2048]{1,0:T(8,128)(2,1)S(1)} %get-tuple-element.26), channel_id=1, source_target_pairs={{0,4},{1,5},{2,6},{3,7},{4,0},{5,1},{6,2},{7,3},{8,12},{9,13},{10,... | collective-permute-start | bytes 196616 | tf_op jit(solution)/shard_map/ppermute | solution.py:27
  42.4 6.4 %collective-permute-start.7 = (bf16[16,2048]{1,0:T(8,128)(2,1)S(1)}, bf16[16,2048]{1,0:T(8,128)(2,1)S(1)}, u32[]{:S(2)}, u32[]{:S(2)}) collective-permute-start(bf16[16,2048]{1,0:T(8,128)(2,1)S(1)} %get-tuple-element.27), channel_id=1, source_target_pairs={{0,2},{1,3},{2,0},{3,1},{4,6},{5,7},{6,4},{7,5},{8,10},{9,11},{10,... | collective-permute-start | bytes 196616 | tf_op jit(solution)/shard_map/ppermute | solution.py:27
  48.8 4.7 %collective-permute-start.9 = (bf16[16,2048]{1,0:T(8,128)(2,1)S(1)}, bf16[16,2048]{1,0:T(8,128)(2,1)S(1)}, u32[]{:S(2)}, u32[]{:S(2)}) collective-permute-start(bf16[16,2048]{1,0:T(8,128)(2,1)S(1)} %add_convert_fusion.5), channel_id=1, source_target_pairs={{0,9},{1,8},{2,11},{3,10},{4,13},{5,12},{6,15},{7,14},{8,17},{9,16... | collective-permute-start | bytes 196616 | tf_op jit(solution)/shard_map/ppermute | solution.py:27
  49.8 4.4 %collective-permute-start.8 = (bf16[16,2048]{1,0:T(8,128)(2,1)S(1)}, bf16[16,2048]{1,0:T(8,128)(2,1)S(1)}, u32[]{:S(2)}, u32[]{:S(2)}) collective-permute-start(bf16[16,2048]{1,0:T(8,128)(2,1)S(1)} %add_convert_fusion.5), channel_id=1, source_target_pairs={{0,8},{1,9},{2,10},{3,11},{4,12},{5,13},{6,14},{7,15},{8,16},{9,17... | collective-permute-start | bytes 196616 | tf_op jit(solution)/shard_map/ppermute | solution.py:27
  54.2 4.7 %collective-permute-start.10 = (bf16[16,2048]{1,0:T(8,128)(2,1)S(1)}, bf16[16,2048]{1,0:T(8,128)(2,1)S(1)}, u32[]{:S(2)}, u32[]{:S(2)}) collective-permute-start(bf16[16,2048]{1,0:T(8,128)(2,1)S(1)} %add_convert_fusion.4.refs_0_), channel_id=1, source_target_pairs={{0,2},{1,3},{2,0},{3,1},{4,6},{5,7},{6,4},{7,5},{8,10},{9,11},{10,... | collective-permute-start | bytes 196616 | tf_op jit(solution)/shard_map/ppermute | solution.py:27
  55.5 6.6 %collective-permute-start.11 = (bf16[16,2048]{1,0:T(8,128)(2,1)S(1)}, bf16[16,2048]{1,0:T(8,128)(2,1)S(1)}, u32[]{:S(2)}, u32[]{:S(2)}) collective-permute-start(bf16[16,2048]{1,0:T(8,128)(2,1)S(1)} %add_convert_fusion.4.refs_0_), channel_id=1, source_target_pairs={{0,4},{1,5},{2,6},{3,7},{4,0},{5,1},{6,2},{7,3},{8,12},{9,13},{10,... | collective-permute-start | bytes 196616 | tf_op jit(solution)/shard_map/ppermute | solution.py:27
  57.3 6.2 %collective-permute-start.12 = (bf16[16,2048]{1,0:T(8,128)(2,1)S(1)}, bf16[16,2048]{1,0:T(8,128)(2,1)S(1)}, u32[]{:S(2)}, u32[]{:S(2)}) collective-permute-start(bf16[16,2048]{1,0:T(8,128)(2,1)S(1)} %add_convert_fusion.4.refs_0_), channel_id=1, source_target_pairs={{0,6},{1,7},{2,4},{3,5},{4,2},{5,3},{6,0},{7,1},{8,14},{9,15},{10,... | collective-permute-start | bytes 196616 | tf_op jit(solution)/shard_map/ppermute | solution.py:27
  63.4 2.5 %copy-start.1 = (bf16[2,1,640,2048]{3,2,1,0:T(8,128)(2,1)S(1)}, bf16[2,1,640,2048]{3,2,1,0:T(8,128)(2,1)}, u32[]{:S(2)}) copy-start(bf16[2,1,640,2048]{3,2,1,0:T(8,128)(2,1)} %param.14) | copy-start | bytes 15728644
  65.9 2.5 %copy-start.5 = (bf16[2,1,640,2048]{3,2,1,0:T(8,128)(2,1)S(1)}, bf16[2,1,640,2048]{3,2,1,0:T(8,128)(2,1)}, u32[]{:S(2)}) copy-start(bf16[2,1,640,2048]{3,2,1,0:T(8,128)(2,1)} %param.15) | copy-start | bytes 15728644
  75.5 6.2 %collective-permute-start.14 = (bf16[16,2048]{1,0:T(8,128)(2,1)S(1)}, bf16[16,2048]{1,0:T(8,128)(2,1)S(1)}, u32[]{:S(2)}, u32[]{:S(2)}) collective-permute-start(bf16[16,2048]{1,0:T(8,128)(2,1)S(1)} %get-tuple-element.32), channel_id=1, source_target_pairs={{0,6},{1,7},{2,4},{3,5},{4,2},{5,3},{6,0},{7,1},{8,14},{9,15},{10,... | collective-permute-start | bytes 196616 | tf_op jit(solution)/shard_map/ppermute | solution.py:27
  76.9 6.1 %collective-permute-start.15 = (bf16[16,2048]{1,0:T(8,128)(2,1)S(1)}, bf16[16,2048]{1,0:T(8,128)(2,1)S(1)}, u32[]{:S(2)}, u32[]{:S(2)}) collective-permute-start(bf16[16,2048]{1,0:T(8,128)(2,1)S(1)} %get-tuple-element.33), channel_id=1, source_target_pairs={{0,4},{1,5},{2,6},{3,7},{4,0},{5,1},{6,2},{7,3},{8,12},{9,13},{10,... | collective-permute-start | bytes 196616 | tf_op jit(solution)/shard_map/ppermute | solution.py:27
  76.9 6.1 %collective-permute-start.16 = (bf16[16,2048]{1,0:T(8,128)(2,1)S(1)}, bf16[16,2048]{1,0:T(8,128)(2,1)S(1)}, u32[]{:S(2)}, u32[]{:S(2)}) collective-permute-start(bf16[16,2048]{1,0:T(8,128)(2,1)S(1)} %get-tuple-element.34), channel_id=1, source_target_pairs={{0,2},{1,3},{2,0},{3,1},{4,6},{5,7},{6,4},{7,5},{8,10},{9,11},{10,... | collective-permute-start | bytes 196616 | tf_op jit(solution)/shard_map/ppermute | solution.py:27
  83.1 4.7 %collective-permute-start.18 = (bf16[16,2048]{1,0:T(8,128)(2,1)S(1)}, bf16[16,2048]{1,0:T(8,128)(2,1)S(1)}, u32[]{:S(2)}, u32[]{:S(2)}) collective-permute-start(bf16[16,2048]{1,0:T(8,128)(2,1)S(1)} %add_convert_fusion.3), channel_id=1, source_target_pairs={{0,9},{1,8},{2,11},{3,10},{4,13},{5,12},{6,15},{7,14},{8,17},{9,16... | collective-permute-start | bytes 196616 | tf_op jit(solution)/shard_map/ppermute | solution.py:27
  83.2 4.6 %collective-permute-start.17 = (bf16[16,2048]{1,0:T(8,128)(2,1)S(1)}, bf16[16,2048]{1,0:T(8,128)(2,1)S(1)}, u32[]{:S(2)}, u32[]{:S(2)}) collective-permute-start(bf16[16,2048]{1,0:T(8,128)(2,1)S(1)} %add_convert_fusion.3), channel_id=1, source_target_pairs={{0,8},{1,9},{2,10},{3,11},{4,12},{5,13},{6,14},{7,15},{8,16},{9,17... | collective-permute-start | bytes 196616 | tf_op jit(solution)/shard_map/ppermute | solution.py:27
  87.8 4.6 %collective-permute-start.19 = (bf16[16,2048]{1,0:T(8,128)(2,1)S(1)}, bf16[16,2048]{1,0:T(8,128)(2,1)S(1)}, u32[]{:S(2)}, u32[]{:S(2)}) collective-permute-start(bf16[16,2048]{1,0:T(8,128)(2,1)S(1)} %add_convert_fusion.2.refs_0_), channel_id=1, source_target_pairs={{0,2},{1,3},{2,0},{3,1},{4,6},{5,7},{6,4},{7,5},{8,10},{9,11},{10,... | collective-permute-start | bytes 196616 | tf_op jit(solution)/shard_map/ppermute | solution.py:27
  89.1 6.0 %collective-permute-start.20 = (bf16[16,2048]{1,0:T(8,128)(2,1)S(1)}, bf16[16,2048]{1,0:T(8,128)(2,1)S(1)}, u32[]{:S(2)}, u32[]{:S(2)}) collective-permute-start(bf16[16,2048]{1,0:T(8,128)(2,1)S(1)} %add_convert_fusion.2.refs_0_), channel_id=1, source_target_pairs={{0,4},{1,5},{2,6},{3,7},{4,0},{5,1},{6,2},{7,3},{8,12},{9,13},{10,... | collective-permute-start | bytes 196616 | tf_op jit(solution)/shard_map/ppermute | solution.py:27
  90.2 6.2 %collective-permute-start.21 = (bf16[16,2048]{1,0:T(8,128)(2,1)S(1)}, bf16[16,2048]{1,0:T(8,128)(2,1)S(1)}, u32[]{:S(2)}, u32[]{:S(2)}) collective-permute-start(bf16[16,2048]{1,0:T(8,128)(2,1)S(1)} %add_convert_fusion.2.refs_0_), channel_id=1, source_target_pairs={{0,6},{1,7},{2,4},{3,5},{4,2},{5,3},{6,0},{7,1},{8,14},{9,15},{10,... | collective-permute-start | bytes 196616 | tf_op jit(solution)/shard_map/ppermute | solution.py:27
  96.4 2.5 %copy-start.2 = (bf16[2,1,640,2048]{3,2,1,0:T(8,128)(2,1)S(1)}, bf16[2,1,640,2048]{3,2,1,0:T(8,128)(2,1)}, u32[]{:S(2)}) copy-start(bf16[2,1,640,2048]{3,2,1,0:T(8,128)(2,1)} %param.14) | copy-start | bytes 15728644
  98.9 2.5 %copy-start.6 = (bf16[2,1,640,2048]{3,2,1,0:T(8,128)(2,1)S(1)}, bf16[2,1,640,2048]{3,2,1,0:T(8,128)(2,1)}, u32[]{:S(2)}) copy-start(bf16[2,1,640,2048]{3,2,1,0:T(8,128)(2,1)} %param.15) | copy-start | bytes 15728644
  101.4 2.5 %copy-start.10 = (bf16[2,1,640,2048]{3,2,1,0:T(8,128)(2,1)S(1)}, bf16[2,1,640,2048]{3,2,1,0:T(8,128)(2,1)}, u32[]{:S(2)}) copy-start(bf16[2,1,640,2048]{3,2,1,0:T(8,128)(2,1)} %param.16) | copy-start | bytes 15728644
  108.5 6.1 %collective-permute-start.22 = (bf16[16,2048]{1,0:T(8,128)(2,1)S(1)}, bf16[16,2048]{1,0:T(8,128)(2,1)S(1)}, u32[]{:S(2)}, u32[]{:S(2)}) collective-permute-start(bf16[16,2048]{1,0:T(8,128)(2,1)S(1)} %get-tuple-element.36), channel_id=1, source_target_pairs={{0,6},{1,7},{2,4},{3,5},{4,2},{5,3},{6,0},{7,1},{8,14},{9,15},{10,... | collective-permute-start | bytes 196616 | tf_op jit(solution)/shard_map/ppermute | solution.py:27
  110.5 5.5 %collective-permute-start.23 = (bf16[16,2048]{1,0:T(8,128)(2,1)S(1)}, bf16[16,2048]{1,0:T(8,128)(2,1)S(1)}, u32[]{:S(2)}, u32[]{:S(2)}) collective-permute-start(bf16[16,2048]{1,0:T(8,128)(2,1)S(1)} %get-tuple-element.37), channel_id=1, source_target_pairs={{0,4},{1,5},{2,6},{3,7},{4,0},{5,1},{6,2},{7,3},{8,12},{9,13},{10,... | collective-permute-start | bytes 196616 | tf_op jit(solution)/shard_map/ppermute | solution.py:27
  110.6 5.4 %collective-permute-start.24 = (bf16[16,2048]{1,0:T(8,128)(2,1)S(1)}, bf16[16,2048]{1,0:T(8,128)(2,1)S(1)}, u32[]{:S(2)}, u32[]{:S(2)}) collective-permute-start(bf16[16,2048]{1,0:T(8,128)(2,1)S(1)} %get-tuple-element.38), channel_id=1, source_target_pairs={{0,2},{1,3},{2,0},{3,1},{4,6},{5,7},{6,4},{7,5},{8,10},{9,11},{10,... | collective-permute-start | bytes 196616 | tf_op jit(solution)/shard_map/ppermute | solution.py:27
  116.0 4.7 %collective-permute-start.26 = (bf16[16,2048]{1,0:T(8,128)(2,1)S(1)}, bf16[16,2048]{1,0:T(8,128)(2,1)S(1)}, u32[]{:S(2)}, u32[]{:S(2)}) collective-permute-start(bf16[16,2048]{1,0:T(8,128)(2,1)S(1)} %add_convert_fusion.1), channel_id=1, source_target_pairs={{0,9},{1,8},{2,11},{3,10},{4,13},{5,12},{6,15},{7,14},{8,17},{9,16... | collective-permute-start | bytes 196616 | tf_op jit(solution)/shard_map/ppermute | solution.py:27
  116.2 4.8 %collective-permute-start.25 = (bf16[16,2048]{1,0:T(8,128)(2,1)S(1)}, bf16[16,2048]{1,0:T(8,128)(2,1)S(1)}, u32[]{:S(2)}, u32[]{:S(2)}) collective-permute-start(bf16[16,2048]{1,0:T(8,128)(2,1)S(1)} %add_convert_fusion.1), channel_id=1, source_target_pairs={{0,8},{1,9},{2,10},{3,11},{4,12},{5,13},{6,14},{7,15},{8,16},{9,17... | collective-permute-start | bytes 196616 | tf_op jit(solution)/shard_map/ppermute | solution.py:27
  120.9 4.6 %collective-permute-start.27 = (bf16[16,2048]{1,0:T(8,128)(2,1)S(1)}, bf16[16,2048]{1,0:T(8,128)(2,1)S(1)}, u32[]{:S(2)}, u32[]{:S(2)}) collective-permute-start(bf16[16,2048]{1,0:T(8,128)(2,1)S(1)} %add_convert_fusion.refs_0_), channel_id=1, source_target_pairs={{0,2},{1,3},{2,0},{3,1},{4,6},{5,7},{6,4},{7,5},{8,10},{9,11},{10,... | collective-permute-start | bytes 196616 | tf_op jit(solution)/shard_map/ppermute | solution.py:27
  122.2 6.2 %collective-permute-start.28 = (bf16[16,2048]{1,0:T(8,128)(2,1)S(1)}, bf16[16,2048]{1,0:T(8,128)(2,1)S(1)}, u32[]{:S(2)}, u32[]{:S(2)}) collective-permute-start(bf16[16,2048]{1,0:T(8,128)(2,1)S(1)} %add_convert_fusion.refs_0_), channel_id=1, source_target_pairs={{0,4},{1,5},{2,6},{3,7},{4,0},{5,1},{6,2},{7,3},{8,12},{9,13},{10,... | collective-permute-start | bytes 196616 | tf_op jit(solution)/shard_map/ppermute | solution.py:27
  123.7 6.1 %collective-permute-start.29 = (bf16[16,2048]{1,0:T(8,128)(2,1)S(1)}, bf16[16,2048]{1,0:T(8,128)(2,1)S(1)}, u32[]{:S(2)}, u32[]{:S(2)}) collective-permute-start(bf16[16,2048]{1,0:T(8,128)(2,1)S(1)} %add_convert_fusion.refs_0_), channel_id=1, source_target_pairs={{0,6},{1,7},{2,4},{3,5},{4,2},{5,3},{6,0},{7,1},{8,14},{9,15},{10,... | collective-permute-start | bytes 196616 | tf_op jit(solution)/shard_map/ppermute | solution.py:27
  129.8 2.5 %copy-start.3 = (bf16[2,1,640,2048]{3,2,1,0:T(8,128)(2,1)S(1)}, bf16[2,1,640,2048]{3,2,1,0:T(8,128)(2,1)}, u32[]{:S(2)}) copy-start(bf16[2,1,640,2048]{3,2,1,0:T(8,128)(2,1)} %param.14) | copy-start | bytes 15728644
  132.3 2.5 %copy-start.7 = (bf16[2,1,640,2048]{3,2,1,0:T(8,128)(2,1)S(1)}, bf16[2,1,640,2048]{3,2,1,0:T(8,128)(2,1)}, u32[]{:S(2)}) copy-start(bf16[2,1,640,2048]{3,2,1,0:T(8,128)(2,1)} %param.15) | copy-start | bytes 15728644
  141.9 6.1 %collective-permute-start.30 = (bf16[16,2048]{1,0:T(8,128)(2,1)S(1)}, bf16[16,2048]{1,0:T(8,128)(2,1)S(1)}, u32[]{:S(2)}, u32[]{:S(2)}) collective-permute-start(bf16[16,2048]{1,0:T(8,128)(2,1)S(1)} %get-tuple-element.40), channel_id=1, source_target_pairs={{0,6},{1,7},{2,4},{3,5},{4,2},{5,3},{6,0},{7,1},{8,14},{9,15},{10,... | collective-permute-start | bytes 196616 | tf_op jit(solution)/shard_map/ppermute | solution.py:27
  143.7 5.7 %collective-permute-start.31 = (bf16[16,2048]{1,0:T(8,128)(2,1)S(1)}, bf16[16,2048]{1,0:T(8,128)(2,1)S(1)}, u32[]{:S(2)}, u32[]{:S(2)}) collective-permute-start(bf16[16,2048]{1,0:T(8,128)(2,1)S(1)} %get-tuple-element.41), channel_id=1, source_target_pairs={{0,4},{1,5},{2,6},{3,7},{4,0},{5,1},{6,2},{7,3},{8,12},{9,13},{10,... | collective-permute-start | bytes 196616 | tf_op jit(solution)/shard_map/ppermute | solution.py:27
  143.7 5.7 %collective-permute-start.32 = (bf16[16,2048]{1,0:T(8,128)(2,1)S(1)}, bf16[16,2048]{1,0:T(8,128)(2,1)S(1)}, u32[]{:S(2)}, u32[]{:S(2)}) collective-permute-start(bf16[16,2048]{1,0:T(8,128)(2,1)S(1)} %get-tuple-element.42), channel_id=1, source_target_pairs={{0,2},{1,3},{2,0},{3,1},{4,6},{5,7},{6,4},{7,5},{8,10},{9,11},{10,... | collective-permute-start | bytes 196616 | tf_op jit(solution)/shard_map/ppermute | solution.py:27
  149.5 4.0 %collective-permute-start.33 = (bf16[8,2048]{1,0:T(8,128)(2,1)S(1)}, bf16[8,2048]{1,0:T(8,128)(2,1)S(1)}, u32[]{:S(2)}, u32[]{:S(2)}) collective-permute-start(bf16[8,2048]{1,0:T(8,128)(2,1)S(1)} %slice.87), channel_id=1, source_target_pairs={{0,1},{1,0},{2,3},{3,2},{4,5},{5,4},{6,7},{7,6},{8,9},{9,8},{10,11... | collective-permute-start | bytes 98312 | tf_op jit(solution)/shard_map/ppermute | solution.py:27
  (2 other events, 5.0 us)

commit v3 on v2

v3 whole, which is shorter than its diff:
```python
import functools

import jax
import jax.numpy as jnp
from jax import lax
from jax.experimental import pallas as pl
from jax.experimental.pallas import tpu as pltpu
from jax.sharding import PartitionSpec as P

EXPERTS = 4
TICKS = 4
CAP = 4
LANES = 128
BOTH = ("segment", "expert")


EPSILON = 1e-06


def moved(value, flip, steps):
    segments, members = lax.axis_size("segment"), lax.axis_size("expert")
    pairs = [
        (section * members + member, (section + steps) % segments * members + (member ^ flip))
        for section in range(segments)
        for member in range(members)
    ]
    return lax.ppermute(value, BOTH, pairs)


def group_of(section, tick_idx, segments):
    start_segment = (section - tick_idx) % segments
    first_group = jnp.where((start_segment % 2 == 1) & (start_segment + TICKS <= segments), 1, 0)
    return (first_group + jnp.where(start_segment + tick_idx >= segments, 1, 0)).astype(jnp.int32)


def groups_at(tick_idx, segments):
    found = set()
    for section in range(segments):
        start = (section - tick_idx) % segments
        first = 1 if start % 2 == 1 and start + TICKS <= segments else 0
        found.add(first + (1 if start + tick_idx >= segments else 0))
    return found


WHOLE = pl.BlockSpec(memory_space=pltpu.VMEM)


def small(kernel, out_shape, *values):
    return pl.pallas_call(
        kernel,
        out_shape=out_shape,
        in_specs=[WHOLE] * len(values),
        out_specs=WHOLE,
        compiler_params=pltpu.CompilerParams(vmem_limit_bytes=2 * 1024 * 1024),
    )(*values)


def prepare_kernel(state_ref, routes_ref, gates_ref, out_ref):
    rows, width = state_ref.shape
    lane = lax.broadcasted_iota(jnp.int32, (rows, LANES), 1)
    columns = EXPERTS + 1
    routed = jnp.zeros((rows, LANES), jnp.float32)
    member = jnp.zeros((rows, LANES), jnp.float32)
    square = (rows, rows)
    diagonal = lax.broadcasted_iota(jnp.int32, square, 0) == lax.broadcasted_iota(jnp.int32, square, 1)

    def upright(line):
        return jnp.sum(jnp.where(diagonal, line, jnp.zeros_like(line)), axis=1, keepdims=True)

    for tick_idx in range(TICKS):
        for choice in range(routes_ref.shape[1]):
            named = lane == upright(routes_ref[tick_idx, choice:choice + 1, :]) + tick_idx * columns
            routed = routed + jnp.where(named, upright(gates_ref[tick_idx, choice:choice + 1, :]), 0.0)
            member = member + jnp.where(named, 1.0, 0.0)
    row = lax.broadcasted_iota(jnp.int32, (rows, LANES), 0)
    position = jnp.zeros((rows, LANES), jnp.float32)
    for earlier in range(rows - 1):
        position = position + jnp.where(row > earlier, member[earlier:earlier + 1, :], 0.0)
    inside = position < CAP
    table = jnp.where(inside, routed, 0.0)
    over = jnp.where(inside, 0.0, routed)
    for tick_idx in range(TICKS):
        low = tick_idx * columns
        spill = jnp.sum(jnp.where((lane >= low) & (lane < low + EXPERTS), over, 0.0), axis=1, keepdims=True)
        table = jnp.where(lane == low + EXPERTS, spill, table)
    high = table.astype(jnp.bfloat16).astype(jnp.float32)
    both = high + pltpu.roll(table - high, TICKS * columns, 1)
    out_ref[:, :width] = state_ref[...]
    out_ref[:, width:] = both.astype(jnp.bfloat16)


def join_kernel(first_ref, second_ref, out_ref):
    out_ref[...] = jnp.concatenate([first_ref[...], second_ref[...]], axis=0)


def layer_kernel(*refs, tick_idx, blocks, spare_count, tok_dev, width):
    x_refs, first_refs, refs = refs[:blocks], refs[blocks:2 * blocks], refs[2 * blocks:]
    gain_ref, gate_ref, up_ref, down_ref = refs[:4]
    spare_refs, refs = refs[4:4 + spare_count], refs[4 + spare_count:]
    out_refs, (total_ref,) = refs[:blocks], refs[blocks:]
    segments, members = lax.axis_size("segment"), lax.axis_size("expert")
    group = group_of(lax.axis_index("segment"), tick_idx, segments)
    expert = lax.axis_index("expert") // (members // EXPERTS)
    x = jnp.concatenate([x_ref[:, :width] for x_ref in x_refs], axis=0)
    values = x.astype(jnp.float32)
    row_scale = lax.rsqrt(jnp.mean(values * values, axis=-1, keepdims=True) + EPSILON)
    normed = (values * row_scale * gain_ref[group]).astype(jnp.bfloat16)
    table = jnp.concatenate([ref[:, width:] for ref in first_refs], axis=0).astype(jnp.float32)
    lane = lax.broadcasted_iota(jnp.int32, table.shape, 1)
    columns = TICKS * (EXPERTS + 1)

    def column(at):
        return jnp.sum(jnp.where((lane == at) | (lane == at + columns), table, 0.0), axis=1, keepdims=True)

    share = column(tick_idx * (EXPERTS + 1) + expert)
    spill = column(tick_idx * (EXPERTS + 1) + EXPERTS)
    contract = (((1,), (1,)), ((), ()))

    def served(gate, up, down):
        gate_pre = lax.dot_general(normed, gate, contract, preferred_element_type=jnp.float32)
        up_pre = lax.dot_general(normed, up, contract, preferred_element_type=jnp.float32)
        hidden = (gate_pre / (1.0 + jnp.exp(-gate_pre)) * up_pre).astype(jnp.bfloat16)
        return jnp.dot(hidden, down, preferred_element_type=jnp.float32)

    total_ref[...] = share * served(gate_ref[group], up_ref[group], down_ref[group])
    for at, spare_ref in enumerate(spare_refs):

        def add(spare_ref=spare_ref):
            total_ref[...] += spill * served(spare_ref[0], spare_ref[1], spare_ref[2])

        if spare_count == 1:
            add()
        else:
            pl.when(group == at)(add)
    per = 2 * tok_dev
    first = total_ref[0:per, :]
    row = lax.broadcasted_iota(jnp.int32, (per, 1), 0)
    out_refs[0][...] = first + jnp.where(row < tok_dev, values[0:per], 0.0)
    for i in range(1, blocks):
        out_refs[i][...] = total_ref[i * per:(i + 1) * per, :].astype(jnp.bfloat16)


def resident(values):
    return [pltpu.with_memory_space_constraint(value, pltpu.VMEM) for value in values]


def run_layer(x_blocks, first_blocks, gain, weights, spares, *, tick_idx, tok_dev):
    blocks = len(x_blocks)
    width = gain.shape[-1]
    per = 2 * tok_dev
    rows = per * blocks
    hidden = weights[0].shape[1] + spares[0].shape[1]
    return pl.pallas_call(
        functools.partial(
            layer_kernel, tick_idx=tick_idx, blocks=blocks, spare_count=len(spares), tok_dev=tok_dev, width=width
        ),
        out_shape=[jax.ShapeDtypeStruct((per, width), jnp.float32)]
        + [jax.ShapeDtypeStruct((per, width), jnp.bfloat16)] * (blocks - 1),
        in_specs=[WHOLE] * (2 * blocks + 4 + len(spares)),
        out_specs=[WHOLE] * blocks,
        scratch_shapes=[pltpu.VMEM((rows, width), jnp.float32)],
        compiler_params=pltpu.CompilerParams(vmem_limit_bytes=12 * 1024 * 1024),
        cost_estimate=pl.CostEstimate(
            flops=6 * rows * hidden * width, bytes_accessed=6 * hidden * width, transcendentals=rows * hidden
        ),
        name="layer",
    )(*x_blocks, *first_blocks, gain, *resident(weights), *resident(spares))


def sum_kernel(*refs, swap):
    total = refs[0][...].astype(jnp.float32)
    half = total.shape[0] // 2
    for ref in refs[1:-1]:
        value = ref[...].astype(jnp.float32)
        total = total + (jnp.concatenate([value[half:], value[:half]], axis=0) if swap else value)
    refs[-1][...] = total.astype(jnp.bfloat16)


def summed(values, swap=False):
    shape = jax.ShapeDtypeStruct(values[0].shape, jnp.bfloat16)
    return small(functools.partial(sum_kernel, swap=swap), shape, *values)


def fill_kernel(*refs, group):
    count = len(refs) // 2
    ins, outs, sems = refs[:count], refs[count:2 * count], refs[2 * count]
    copies = [
        pltpu.make_async_copy(one if group is None else one.at[group], out, sems.at[i])
        for i, (one, out) in enumerate(zip(ins, outs))
    ]
    for copy in copies:
        copy.start()
    for copy in copies:
        copy.wait()


def filled(values, group=None):
    shapes = [value.shape if group is None else value.shape[1:] for value in values]
    return pl.pallas_call(
        functools.partial(fill_kernel, group=group),
        out_shape=[pltpu.VMEM(shape, value.dtype) for shape, value in zip(shapes, values)],
        in_specs=[pl.BlockSpec(memory_space=pltpu.HBM)] * len(values),
        out_specs=[WHOLE] * len(values),
        scratch_shapes=[pltpu.SemaphoreType.DMA((len(values),))],
        compiler_params=pltpu.CompilerParams(vmem_limit_bytes=1024 * 1024),
        name="fill",
    )(*[pltpu.with_memory_space_constraint(value, pltpu.HBM) for value in values])


def stack_kernel(gate_ref, up_ref, down_ref, out_ref, sems, *, group):
    copies = [
        pltpu.make_async_copy(ref.at[group], out_ref.at[i], sems.at[i])
        for i, ref in enumerate((gate_ref, up_ref, down_ref))
    ]
    for copy in copies:
        copy.start()
    for copy in copies:
        copy.wait()


def stacked(spares, group):
    return pl.pallas_call(
        functools.partial(stack_kernel, group=group),
        out_shape=pltpu.VMEM((3,) + spares[0].shape[1:], spares[0].dtype),
        in_specs=[pl.BlockSpec(memory_space=pltpu.HBM)] * 3,
        out_specs=WHOLE,
        scratch_shapes=[pltpu.SemaphoreType.DMA((3,))],
        compiler_params=pltpu.CompilerParams(vmem_limit_bytes=6 * 1024 * 1024),
        name="stack",
    )(*[pltpu.with_memory_space_constraint(value, pltpu.HBM) for value in spares])


def widest_first(outer):
    return range(outer - 1, 0, -1)


def added(values):
    total = values[0].astype(jnp.float32)
    for value in values[1:]:
        total = total + value.astype(jnp.float32)
    return total


def on_device(
    state, routes, gates, norm_gain, w_gate, w_up, w_down, spare_gate, spare_up, spare_down
):
    segments = lax.axis_size("segment")
    members = lax.axis_size("expert")
    outer = members // 2
    assert outer & (outer - 1) == 0
    tok_dev = state.shape[1]

    def spread(value):
        got = {j: moved(value, 2 * j, 0) for j in widest_first(outer)}
        return [value] + [got[j] for j in range(1, outer)]

    weights = [w_gate[:, 0], w_up[:, 0], w_down[:, 0]]
    spare_all = [spare_gate[:, 0], spare_up[:, 0], spare_down[:, 0]]
    sent, state, routes, gates = lax.optimization_barrier((stacked(spare_all, 0), state, routes, gates))
    spares = [moved(sent, 0, -1)]
    shape = (tok_dev, state.shape[2] + LANES)
    own = small(
        prepare_kernel, jax.ShapeDtypeStruct(shape, state.dtype), state[0],
        jnp.transpose(routes[:, 0], (0, 2, 1)), jnp.transpose(gates[:, 0], (0, 2, 1)),
    )
    other = moved(own, 1, 0)
    pair = small(join_kernel, jax.ShapeDtypeStruct((2 * tok_dev, shape[1]), state.dtype), own, other)
    arrived = spread(pair)
    weights = filled(weights)
    x_blocks = arrived
    late = stacked(lax.optimization_barrier((*spare_all, arrived[1]))[:3], 1)
    for tick_idx in range(TICKS):
        needed = groups_at(tick_idx, segments)
        if tick_idx == 0 and needed != {0}:
            spares.append(moved(late, 0, -1))
        parts = run_layer(x_blocks, arrived, norm_gain, weights, spares, tick_idx=tick_idx, tok_dev=tok_dev)
        got = [moved(parts[j], 2 * j, 0) for j in widest_first(outer)]
        if len(spares) == 1:
            late, _ = lax.optimization_barrier((late, parts[0]))
            spares.append(moved(late, 0, -1))
        if tick_idx + 1 == TICKS:
            total = added([parts[0]] + got)
            other = moved(total[tok_dev:].astype(jnp.bfloat16), 1, 0)
            return added([total[:tok_dev], other]).astype(jnp.bfloat16)[None]
        total = summed([parts[0]] + got)
        across = moved(total, 1, 1)
        along = moved(total, 0, 1)
        x_blocks = spread(summed([along, across], swap=True))


def solution(mesh):
    return jax.shard_map(
        on_device,
        mesh=mesh,
        in_specs=(
            P("segment", "expert", None),
            P(None, "segment", "expert", None),
            P(None, "segment", "expert", None),
            P(None, "segment", None),
            P(None, "segment", "expert", None),
            P(None, "segment", "expert", None),
            P(None, "segment", "expert", None),
            P(None, "segment", "expert", None),
            P(None, "segment", "expert", None),
            P(None, "segment", "expert", None),
        ),
        out_specs=P("segment", "expert", None),
        check_vma=False,
    )
```

time: 155 us -> 123 us (0.79)
  local copies, waits for them, and re-layouts: 30.1 us -> 0.02 us
  starting transfers between devices: 44.8 us -> 47.1 us
  Pallas kernels: 22.9 us -> 21.1 us
    unnamed x33 -> x8, local copies, waits for them, and re-layouts: 29.9 us -> 0.02 us
    pallas_call x4, Pallas kernels: 17.3 us -> 12.1 us  [run_layer(): pl.pallas_call(functools.partial(layer_kernel, tick_idx=tick_idx, blocks=...]
    pallas_call x2 -> x11, Pallas kernels: 5.62 us -> 9.03 us  [the longest x1 5.57 us: filled(): pl.pallas_call(functools.partial(fill_kernel, group=group), out_shape=[pl...]
    ppermute x34, starting transfers between devices: 44.8 us -> 47.1 us  [moved(): return lax.ppermute(value, BOTH, pairs)]
  transfers between devices with their start and end apart: 34 -> 34, of which waited for: 26 -> 24; matrix products, arithmetic and copies ran while one was open for 1% -> 0% of each run, Pallas kernels for 4% -> 6%
where the time goes in v3:
time: 123 us
  waiting for transfers between devices  53.8 us (44%)
  starting transfers between devices  47.1 us (38%)
  Pallas kernels  21.1 us (17%)
    ppermute x34, waiting for transfers between devices, moved(): return lax.ppermute(value, BOTH, pairs)  53.8 us
    ppermute x34, starting transfers between devices, moved(): return lax.ppermute(value, BOTH, pairs)  47.1 us
    pallas_call x4, Pallas kernels, run_layer(): pl.pallas_call(functools.partial(layer_kernel, tick_idx=tick_idx, blocks=...  12.1 us
    pallas_call x1, Pallas kernels, filled(): pl.pallas_call(functools.partial(fill_kernel, group=group), out_shape=[pl...  5.57 us
    pallas_call x2, Pallas kernels, stacked(): pl.pallas_call(functools.partial(stack_kernel, group=group), out_shape=pl...  3.03 us
  transfers between devices with their start and end apart: 34, of which 24 were waited for; matrix products, arithmetic and copies ran while one was open for 0% of the time, Pallas kernels for 6%

profile of v3, /device:TPU:0, one launch (start us, length us, event | category | flops | bytes accessed | tf_op | source)
XLA Modules:
  0.0 122.8 jit_solution(14632936252291132553)
XLA Ops:
  0.0 1.5 %stack.2 = bf16[3,160,2048]{2,1,0:T(8,128)(2,1)S(1)} custom-call(bf16[2,160,2048]{2,1,0:T(8,128)(2,1)} %bitcast.21, bf16[2,160,2048]{2,1,0:T(8,128)(2,1)} %bitcast.23, bf16[2,160,2048]{2,1,0:T(8,128)(2,1)} %bitcast.25), custom_call_target="tpu_custom_call" | custom-call | tf_op jit(solution)/shard_map/stack/pallas_call | solution.py:222
  1.5 2.5 %collective-permute-start.4 = (bf16[3,160,2048]{2,1,0:T(8,128)(2,1)S(1)}, bf16[3,160,2048]{2,1,0:T(8,128)(2,1)S(1)}, u32[]{:S(2)}, u32[]{:S(2)}) collective-permute-start(bf16[3,160,2048]{2,1,0:T(8,128)(2,1)S(1)} %stack.2), channel_id=1, source_target_pairs={{0,24},{1,25},{2,26},{3,27},{4,28},{5,29},{6,30},{7,31},{8,0},{9,1... | collective-permute-start | bytes 5898248 | tf_op jit(solution)/shard_map/ppermute | solution.py:27
  4.3 1.5 %collective-permute-start = (bf16[8,2176]{1,0:T(8,128)(2,1)S(1)}, bf16[8,2176]{1,0:T(8,128)(2,1)S(1)}, u32[]{:S(2)}, u32[]{:S(2)}) collective-permute-start(bf16[8,2176]{1,0:T(8,128)(2,1)S(1)} %shard_map.100.first_ref), channel_id=1, source_target_pairs={{0,1},{1,0},{2,3},{3,2},{4,5},{5,4},{6,7},{7,6},{8,9},{9,8},{10,11... | collective-permute-start | bytes 104456 | tf_op jit(solution)/shard_map/ppermute | solution.py:27
  5.8 2.4 %collective-permute-done.second_ref = bf16[8,2176]{1,0:T(8,128)(2,1)S(1)} collective-permute-done((bf16[8,2176]{1,0:T(8,128)(2,1)S(1)}, bf16[8,2176]{1,0:T(8,128)(2,1)S(1)}, u32[]{:S(2)}, u32[]{:S(2)}) %collective-permute-start) | collective-permute-done | bytes 34848 | tf_op jit(solution)/shard_map/ppermute | solution.py:27
  8.3 1.6 %collective-permute-start.1 = (bf16[16,2176]{1,0:T(8,128)(2,1)S(1)}, bf16[16,2176]{1,0:T(8,128)(2,1)S(1)}, u32[]{:S(2)}, u32[]{:S(2)}) collective-permute-start(bf16[16,2176]{1,0:T(8,128)(2,1)S(1)} %shard_map.101.refs_0_.refs_4_), channel_id=1, source_target_pairs={{0,2},{1,3},{2,0},{3,1},{4,6},{5,7},{6,4},{7,5},{8,10},{9,11},{10,... | collective-permute-start | bytes 208904 | tf_op jit(solution)/shard_map/ppermute | solution.py:27
  9.9 2.5 %collective-permute-start.3 = (bf16[16,2176]{1,0:T(8,128)(2,1)S(1)}, bf16[16,2176]{1,0:T(8,128)(2,1)S(1)}, u32[]{:S(2)}, u32[]{:S(2)}) collective-permute-start(bf16[16,2176]{1,0:T(8,128)(2,1)S(1)} %shard_map.101.refs_0_.refs_4_), channel_id=1, source_target_pairs={{0,6},{1,7},{2,4},{3,5},{4,2},{5,3},{6,0},{7,1},{8,14},{9,15},{10,... | collective-permute-start | bytes 208904 | tf_op jit(solution)/shard_map/ppermute | solution.py:27
  12.5 5.6 %fill.1 = (bf16[2,640,2048]{2,1,0:T(8,128)(2,1)S(1)}, bf16[2,640,2048]{2,1,0:T(8,128)(2,1)S(1)}, bf16[2,640,2048]{2,1,0:T(8,128)(2,1)S(1)}) custom-call(bf16[2,640,2048]{2,1,0:T(8,128)(2,1)} %bitcast.18, bf16[2,640,2048]{2,1,0:T(8,128)(2,1)} %bitcast.19, bf16[2,640,2048]{2,1,0:T(8,128)(2,1)} %bitcast.20), custom_call_target="tpu_custom_call" | custom-call | tf_op jit(solution)/shard_map/fill/pallas_call | solution.py:199
  18.1 1.5 %stack.3 = bf16[3,160,2048]{2,1,0:T(8,128)(2,1)S(1)} custom-call(bf16[2,160,2048]{2,1,0:T(8,128)(2,1)} %bitcast.22, bf16[2,160,2048]{2,1,0:T(8,128)(2,1)} %bitcast.24, bf16[2,160,2048]{2,1,0:T(8,128)(2,1)} %bitcast.26), custom_call_target="tpu_custom_call" | custom-call | tf_op jit(solution)/shard_map/stack/pallas_call | solution.py:222
  19.7 6.5 %collective-permute-done.4.refs_12_ = bf16[3,160,2048]{2,1,0:T(8,128)(2,1)S(1)} collective-permute-done((bf16[3,160,2048]{2,1,0:T(8,128)(2,1)S(1)}, bf16[3,160,2048]{2,1,0:T(8,128)(2,1)S(1)}, u32[]{:S(2)}, u32[]{:S(2)}) %collective-permute-start.4) | collective-permute-done | bytes 1966112 | tf_op jit(solution)/shard_map/ppermute | solution.py:27
  26.2 2.9 %layer.4 = (f32[16,2048]{1,0:T(8,128)S(1)}, bf16[16,2048]{1,0:T(8,128)(2,1)S(1)}, bf16[16,2048]{1,0:T(8,128)(2,1)S(1)}, bf16[16,2048]{1,0:T(8,128)(2,1)S(1)}) custom-call(bf16[16,2176]{1,0:T(8,128)(2,1)S(1)} %shard_map.101.refs_0_.refs_4_, bf16[16,2176]{1,0:T(8,128)(2,1)S(1)} %collective-permute-done.1.refs_1_.refs_5_, ...), custom_call_target="tpu_custom_call" | custom-call | flops 629145600 | bytes 9830400 | tf_op jit(solution)/shard_map/layer/pallas_call | solution.py:153
  29.1 2.0 %collective-permute-start.13 = (bf16[3,160,2048]{2,1,0:T(8,128)(2,1)S(1)}, bf16[3,160,2048]{2,1,0:T(8,128)(2,1)S(1)}, u32[]{:S(2)}, u32[]{:S(2)}) collective-permute-start(bf16[3,160,2048]{2,1,0:T(8,128)(2,1)S(1)} %stack.3), channel_id=1, source_target_pairs={{0,24},{1,25},{2,26},{3,27},{4,28},{5,29},{6,30},{7,31},{8,0},{9,1... | collective-permute-start | bytes 5898248 | tf_op jit(solution)/shard_map/ppermute | solution.py:27
  31.1 3.6 %collective-permute-start.5 = (bf16[16,2048]{1,0:T(8,128)(2,1)S(1)}, bf16[16,2048]{1,0:T(8,128)(2,1)S(1)}, u32[]{:S(2)}, u32[]{:S(2)}) collective-permute-start(bf16[16,2048]{1,0:T(8,128)(2,1)S(1)} %get-tuple-element.40), channel_id=1, source_target_pairs={{0,6},{1,7},{2,4},{3,5},{4,2},{5,3},{6,0},{7,1},{8,14},{9,15},{10,... | collective-permute-start | bytes 196616 | tf_op jit(solution)/shard_map/ppermute | solution.py:27
  35.5 2.0 %collective-permute-done.5.refs_1_ = bf16[16,2048]{1,0:T(8,128)(2,1)S(1)} collective-permute-done((bf16[16,2048]{1,0:T(8,128)(2,1)S(1)}, bf16[16,2048]{1,0:T(8,128)(2,1)S(1)}, u32[]{:S(2)}, u32[]{:S(2)}) %collective-permute-start.5) | collective-permute-done | bytes 65568 | tf_op jit(solution)/shard_map/ppermute | solution.py:27
  37.4 2.6 %collective-permute-done.6.refs_2_ = bf16[16,2048]{1,0:T(8,128)(2,1)S(1)} collective-permute-done((bf16[16,2048]{1,0:T(8,128)(2,1)S(1)}, bf16[16,2048]{1,0:T(8,128)(2,1)S(1)}, u32[]{:S(2)}, u32[]{:S(2)}) %collective-permute-start.6) | collective-permute-done | bytes 65568 | tf_op jit(solution)/shard_map/ppermute | solution.py:27
  40.2 1.9 %collective-permute-start.8 = (bf16[16,2048]{1,0:T(8,128)(2,1)S(1)}, bf16[16,2048]{1,0:T(8,128)(2,1)S(1)}, u32[]{:S(2)}, u32[]{:S(2)}) collective-permute-start(bf16[16,2048]{1,0:T(8,128)(2,1)S(1)} %shard_map.102), channel_id=1, source_target_pairs={{0,8},{1,9},{2,10},{3,11},{4,12},{5,13},{6,14},{7,15},{8,16},{9,17... | collective-permute-start | bytes 196616 | tf_op jit(solution)/shard_map/ppermute | solution.py:27
  42.1 2.9 %collective-permute-done.9.refs_1_ = bf16[16,2048]{1,0:T(8,128)(2,1)S(1)} collective-permute-done((bf16[16,2048]{1,0:T(8,128)(2,1)S(1)}, bf16[16,2048]{1,0:T(8,128)(2,1)S(1)}, u32[]{:S(2)}, u32[]{:S(2)}) %collective-permute-start.9) | collective-permute-done | bytes 65568 | tf_op jit(solution)/shard_map/ppermute | solution.py:27
  45.0 1.2 collective-permute-done.8.refs_0_
  46.2 2.3 %collective-permute-start.12 = (bf16[16,2048]{1,0:T(8,128)(2,1)S(1)}, bf16[16,2048]{1,0:T(8,128)(2,1)S(1)}, u32[]{:S(2)}, u32[]{:S(2)}) collective-permute-start(bf16[16,2048]{1,0:T(8,128)(2,1)S(1)} %shard_map.103.refs_0_), channel_id=1, source_target_pairs={{0,6},{1,7},{2,4},{3,5},{4,2},{5,3},{6,0},{7,1},{8,14},{9,15},{10,... | collective-permute-start | bytes 196616 | tf_op jit(solution)/shard_map/ppermute | solution.py:27
  48.5 2.1 %collective-permute-start.10 = (bf16[16,2048]{1,0:T(8,128)(2,1)S(1)}, bf16[16,2048]{1,0:T(8,128)(2,1)S(1)}, u32[]{:S(2)}, u32[]{:S(2)}) collective-permute-start(bf16[16,2048]{1,0:T(8,128)(2,1)S(1)} %shard_map.103.refs_0_), channel_id=1, source_target_pairs={{0,2},{1,3},{2,0},{3,1},{4,6},{5,7},{6,4},{7,5},{8,10},{9,11},{10,... | collective-permute-start | bytes 196616 | tf_op jit(solution)/shard_map/ppermute | solution.py:27
  50.6 2.1 %collective-permute-done.12.refs_3_ = bf16[16,2048]{1,0:T(8,128)(2,1)S(1)} collective-permute-done((bf16[16,2048]{1,0:T(8,128)(2,1)S(1)}, bf16[16,2048]{1,0:T(8,128)(2,1)S(1)}, u32[]{:S(2)}, u32[]{:S(2)}) %collective-permute-start.12) | collective-permute-done | bytes 65568 | tf_op jit(solution)/shard_map/ppermute | solution.py:27
  52.8 1.5 %collective-permute-done.11.refs_2_ = bf16[16,2048]{1,0:T(8,128)(2,1)S(1)} collective-permute-done((bf16[16,2048]{1,0:T(8,128)(2,1)S(1)}, bf16[16,2048]{1,0:T(8,128)(2,1)S(1)}, u32[]{:S(2)}, u32[]{:S(2)}) %collective-permute-start.11) | collective-permute-done | bytes 65568 | tf_op jit(solution)/shard_map/ppermute | solution.py:27
  54.6 3.1 %layer.5 = (f32[16,2048]{1,0:T(8,128)S(1)}, bf16[16,2048]{1,0:T(8,128)(2,1)S(1)}, bf16[16,2048]{1,0:T(8,128)(2,1)S(1)}, bf16[16,2048]{1,0:T(8,128)(2,1)S(1)}) custom-call(bf16[16,2048]{1,0:T(8,128)(2,1)S(1)} %shard_map.103.refs_0_, bf16[16,2048]{1,0:T(8,128)(2,1)S(1)} %collective-permute-done.10.refs_1_, ...), custom_call_target="tpu_custom_call" | custom-call | flops 629145600 | bytes 9830400 | tf_op jit(solution)/shard_map/layer/pallas_call | solution.py:153
  57.7 3.7 %collective-permute-start.14 = (bf16[16,2048]{1,0:T(8,128)(2,1)S(1)}, bf16[16,2048]{1,0:T(8,128)(2,1)S(1)}, u32[]{:S(2)}, u32[]{:S(2)}) collective-permute-start(bf16[16,2048]{1,0:T(8,128)(2,1)S(1)} %get-tuple-element.48), channel_id=1, source_target_pairs={{0,6},{1,7},{2,4},{3,5},{4,2},{5,3},{6,0},{7,1},{8,14},{9,15},{10,... | collective-permute-start | bytes 196616 | tf_op jit(solution)/shard_map/ppermute | solution.py:27
  62.1 2.5 %collective-permute-done.14.refs_1_ = bf16[16,2048]{1,0:T(8,128)(2,1)S(1)} collective-permute-done((bf16[16,2048]{1,0:T(8,128)(2,1)S(1)}, bf16[16,2048]{1,0:T(8,128)(2,1)S(1)}, u32[]{:S(2)}, u32[]{:S(2)}) %collective-permute-start.14) | collective-permute-done | bytes 65568 | tf_op jit(solution)/shard_map/ppermute | solution.py:27
  64.6 3.2 %collective-permute-done.15.refs_2_ = bf16[16,2048]{1,0:T(8,128)(2,1)S(1)} collective-permute-done((bf16[16,2048]{1,0:T(8,128)(2,1)S(1)}, bf16[16,2048]{1,0:T(8,128)(2,1)S(1)}, u32[]{:S(2)}, u32[]{:S(2)}) %collective-permute-start.15) | collective-permute-done | bytes 65568 | tf_op jit(solution)/shard_map/ppermute | solution.py:27
  67.8 1.1 collective-permute-start.18
  69.3 3.2 %collective-permute-done.18.refs_1_ = bf16[16,2048]{1,0:T(8,128)(2,1)S(1)} collective-permute-done((bf16[16,2048]{1,0:T(8,128)(2,1)S(1)}, bf16[16,2048]{1,0:T(8,128)(2,1)S(1)}, u32[]{:S(2)}, u32[]{:S(2)}) %collective-permute-start.18) | collective-permute-done | bytes 65568 | tf_op jit(solution)/shard_map/ppermute | solution.py:27
  73.2 2.6 %collective-permute-start.21 = (bf16[16,2048]{1,0:T(8,128)(2,1)S(1)}, bf16[16,2048]{1,0:T(8,128)(2,1)S(1)}, u32[]{:S(2)}, u32[]{:S(2)}) collective-permute-start(bf16[16,2048]{1,0:T(8,128)(2,1)S(1)} %shard_map.105.refs_0_), channel_id=1, source_target_pairs={{0,6},{1,7},{2,4},{3,5},{4,2},{5,3},{6,0},{7,1},{8,14},{9,15},{10,... | collective-permute-start | bytes 196616 | tf_op jit(solution)/shard_map/ppermute | solution.py:27
  76.0 1.7 %collective-permute-start.19 = (bf16[16,2048]{1,0:T(8,128)(2,1)S(1)}, bf16[16,2048]{1,0:T(8,128)(2,1)S(1)}, u32[]{:S(2)}, u32[]{:S(2)}) collective-permute-start(bf16[16,2048]{1,0:T(8,128)(2,1)S(1)} %shard_map.105.refs_0_), channel_id=1, source_target_pairs={{0,2},{1,3},{2,0},{3,1},{4,6},{5,7},{6,4},{7,5},{8,10},{9,11},{10,... | collective-permute-start | bytes 196616 | tf_op jit(solution)/shard_map/ppermute | solution.py:27
  77.7 1.9 %collective-permute-done.21.refs_3_ = bf16[16,2048]{1,0:T(8,128)(2,1)S(1)} collective-permute-done((bf16[16,2048]{1,0:T(8,128)(2,1)S(1)}, bf16[16,2048]{1,0:T(8,128)(2,1)S(1)}, u32[]{:S(2)}, u32[]{:S(2)}) %collective-permute-start.21) | collective-permute-done | bytes 65568 | tf_op jit(solution)/shard_map/ppermute | solution.py:27
  79.6 2.0 %collective-permute-done.20.refs_2_ = bf16[16,2048]{1,0:T(8,128)(2,1)S(1)} collective-permute-done((bf16[16,2048]{1,0:T(8,128)(2,1)S(1)}, bf16[16,2048]{1,0:T(8,128)(2,1)S(1)}, u32[]{:S(2)}, u32[]{:S(2)}) %collective-permute-start.20) | collective-permute-done | bytes 65568 | tf_op jit(solution)/shard_map/ppermute | solution.py:27
  81.6 3.1 %layer.6 = (f32[16,2048]{1,0:T(8,128)S(1)}, bf16[16,2048]{1,0:T(8,128)(2,1)S(1)}, bf16[16,2048]{1,0:T(8,128)(2,1)S(1)}, bf16[16,2048]{1,0:T(8,128)(2,1)S(1)}) custom-call(bf16[16,2048]{1,0:T(8,128)(2,1)S(1)} %shard_map.105.refs_0_, bf16[16,2048]{1,0:T(8,128)(2,1)S(1)} %collective-permute-done.19.refs_1_, ...), custom_call_target="tpu_custom_call" | custom-call | flops 629145600 | bytes 9830400 | tf_op jit(solution)/shard_map/layer/pallas_call | solution.py:153
  84.7 2.0 %collective-permute-start.22 = (bf16[16,2048]{1,0:T(8,128)(2,1)S(1)}, bf16[16,2048]{1,0:T(8,128)(2,1)S(1)}, u32[]{:S(2)}, u32[]{:S(2)}) collective-permute-start(bf16[16,2048]{1,0:T(8,128)(2,1)S(1)} %get-tuple-element.52), channel_id=1, source_target_pairs={{0,6},{1,7},{2,4},{3,5},{4,2},{5,3},{6,0},{7,1},{8,14},{9,15},{10,... | collective-permute-start | bytes 196616 | tf_op jit(solution)/shard_map/ppermute | solution.py:27
  86.7 2.4 %collective-permute-start.24 = (bf16[16,2048]{1,0:T(8,128)(2,1)S(1)}, bf16[16,2048]{1,0:T(8,128)(2,1)S(1)}, u32[]{:S(2)}, u32[]{:S(2)}) collective-permute-start(bf16[16,2048]{1,0:T(8,128)(2,1)S(1)} %get-tuple-element.54), channel_id=1, source_target_pairs={{0,2},{1,3},{2,0},{3,1},{4,6},{5,7},{6,4},{7,5},{8,10},{9,11},{10,... | collective-permute-start | bytes 196616 | tf_op jit(solution)/shard_map/ppermute | solution.py:27
  89.1 1.9 %collective-permute-done.22.refs_1_ = bf16[16,2048]{1,0:T(8,128)(2,1)S(1)} collective-permute-done((bf16[16,2048]{1,0:T(8,128)(2,1)S(1)}, bf16[16,2048]{1,0:T(8,128)(2,1)S(1)}, u32[]{:S(2)}, u32[]{:S(2)}) %collective-permute-start.22) | collective-permute-done | bytes 65568 | tf_op jit(solution)/shard_map/ppermute | solution.py:27
  91.1 1.9 %collective-permute-done.23.refs_2_ = bf16[16,2048]{1,0:T(8,128)(2,1)S(1)} collective-permute-done((bf16[16,2048]{1,0:T(8,128)(2,1)S(1)}, bf16[16,2048]{1,0:T(8,128)(2,1)S(1)}, u32[]{:S(2)}, u32[]{:S(2)}) %collective-permute-start.23) | collective-permute-done | bytes 65568 | tf_op jit(solution)/shard_map/ppermute | solution.py:27
  94.2 3.5 %collective-permute-done.26.refs_1_ = bf16[16,2048]{1,0:T(8,128)(2,1)S(1)} collective-permute-done((bf16[16,2048]{1,0:T(8,128)(2,1)S(1)}, bf16[16,2048]{1,0:T(8,128)(2,1)S(1)}, u32[]{:S(2)}, u32[]{:S(2)}) %collective-permute-start.26) | collective-permute-done | bytes 65568 | tf_op jit(solution)/shard_map/ppermute | solution.py:27
  98.4 2.3 %collective-permute-start.29 = (bf16[16,2048]{1,0:T(8,128)(2,1)S(1)}, bf16[16,2048]{1,0:T(8,128)(2,1)S(1)}, u32[]{:S(2)}, u32[]{:S(2)}) collective-permute-start(bf16[16,2048]{1,0:T(8,128)(2,1)S(1)} %shard_map.107.refs_0_), channel_id=1, source_target_pairs={{0,6},{1,7},{2,4},{3,5},{4,2},{5,3},{6,0},{7,1},{8,14},{9,15},{10,... | collective-permute-start | bytes 196616 | tf_op jit(solution)/shard_map/ppermute | solution.py:27
  100.6 2.2 %collective-permute-start.27 = (bf16[16,2048]{1,0:T(8,128)(2,1)S(1)}, bf16[16,2048]{1,0:T(8,128)(2,1)S(1)}, u32[]{:S(2)}, u32[]{:S(2)}) collective-permute-start(bf16[16,2048]{1,0:T(8,128)(2,1)S(1)} %shard_map.107.refs_0_), channel_id=1, source_target_pairs={{0,2},{1,3},{2,0},{3,1},{4,6},{5,7},{6,4},{7,5},{8,10},{9,11},{10,... | collective-permute-start | bytes 196616 | tf_op jit(solution)/shard_map/ppermute | solution.py:27
  102.8 2.1 %collective-permute-done.29.refs_3_ = bf16[16,2048]{1,0:T(8,128)(2,1)S(1)} collective-permute-done((bf16[16,2048]{1,0:T(8,128)(2,1)S(1)}, bf16[16,2048]{1,0:T(8,128)(2,1)S(1)}, u32[]{:S(2)}, u32[]{:S(2)}) %collective-permute-start.29) | collective-permute-done | bytes 65568 | tf_op jit(solution)/shard_map/ppermute | solution.py:27
  104.9 1.9 %collective-permute-done.28.refs_2_ = bf16[16,2048]{1,0:T(8,128)(2,1)S(1)} collective-permute-done((bf16[16,2048]{1,0:T(8,128)(2,1)S(1)}, bf16[16,2048]{1,0:T(8,128)(2,1)S(1)}, u32[]{:S(2)}, u32[]{:S(2)}) %collective-permute-start.28) | collective-permute-done | bytes 65568 | tf_op jit(solution)/shard_map/ppermute | solution.py:27
  106.8 3.1 %layer.7 = (f32[16,2048]{1,0:T(8,128)S(1)}, bf16[16,2048]{1,0:T(8,128)(2,1)S(1)}, bf16[16,2048]{1,0:T(8,128)(2,1)S(1)}, bf16[16,2048]{1,0:T(8,128)(2,1)S(1)}) custom-call(bf16[16,2048]{1,0:T(8,128)(2,1)S(1)} %shard_map.107.refs_0_, bf16[16,2048]{1,0:T(8,128)(2,1)S(1)} %collective-permute-done.27.refs_1_, ...), custom_call_target="tpu_custom_call" | custom-call | flops 629145600 | bytes 9830400 | tf_op jit(solution)/shard_map/layer/pallas_call | solution.py:153
  109.8 1.8 %collective-permute-start.30 = (bf16[16,2048]{1,0:T(8,128)(2,1)S(1)}, bf16[16,2048]{1,0:T(8,128)(2,1)S(1)}, u32[]{:S(2)}, u32[]{:S(2)}) collective-permute-start(bf16[16,2048]{1,0:T(8,128)(2,1)S(1)} %get-tuple-element.56), channel_id=1, source_target_pairs={{0,6},{1,7},{2,4},{3,5},{4,2},{5,3},{6,0},{7,1},{8,14},{9,15},{10,... | collective-permute-start | bytes 196616 | tf_op jit(solution)/shard_map/ppermute | solution.py:27
  111.7 2.6 %collective-permute-start.32 = (bf16[16,2048]{1,0:T(8,128)(2,1)S(1)}, bf16[16,2048]{1,0:T(8,128)(2,1)S(1)}, u32[]{:S(2)}, u32[]{:S(2)}) collective-permute-start(bf16[16,2048]{1,0:T(8,128)(2,1)S(1)} %get-tuple-element.58), channel_id=1, source_target_pairs={{0,2},{1,3},{2,0},{3,1},{4,6},{5,7},{6,4},{7,5},{8,10},{9,11},{10,... | collective-permute-start | bytes 196616 | tf_op jit(solution)/shard_map/ppermute | solution.py:27
  114.3 2.4 %collective-permute-done.30 = bf16[16,2048]{1,0:T(8,128)(2,1)S(1)} collective-permute-done((bf16[16,2048]{1,0:T(8,128)(2,1)S(1)}, bf16[16,2048]{1,0:T(8,128)(2,1)S(1)}, u32[]{:S(2)}, u32[]{:S(2)}) %collective-permute-start.30) | collective-permute-done | bytes 65568 | tf_op jit(solution)/shard_map/ppermute | solution.py:27
  116.7 1.5 %collective-permute-done.31 = bf16[16,2048]{1,0:T(8,128)(2,1)S(1)} collective-permute-done((bf16[16,2048]{1,0:T(8,128)(2,1)S(1)}, bf16[16,2048]{1,0:T(8,128)(2,1)S(1)}, u32[]{:S(2)}, u32[]{:S(2)}) %collective-permute-start.31) | collective-permute-done | bytes 65568 | tf_op jit(solution)/shard_map/ppermute | solution.py:27
  118.2 1.2 collective-permute-start.33
  119.4 2.8 %collective-permute-done.33 = bf16[8,2048]{1,0:T(8,128)(2,1)S(1)} collective-permute-done((bf16[8,2048]{1,0:T(8,128)(2,1)S(1)}, bf16[8,2048]{1,0:T(8,128)(2,1)S(1)}, u32[]{:S(2)}, u32[]{:S(2)}) %collective-permute-start.33) | collective-permute-done | bytes 32800 | tf_op jit(solution)/shard_map/ppermute | solution.py:27
  (46 shorter events, 6.3 us)
Async XLA Ops:
  0.0 4.1 %copy-start.1 = (bf16[1,8,2048]{2,1,0:T(8,128)(2,1)S(1)}, bf16[1,8,2048]{2,1,0:T(8,128)(2,1)}, u32[]{:S(2)}) copy-start(bf16[1,8,2048]{2,1,0:T(8,128)(2,1)} %param.10) | copy-start | bytes 98308
  0.0 4.1 %copy-start.2 = (s32[4,1,8,2]{2,3,1,0:T(2,128)S(1)}, s32[4,1,8,2]{2,3,1,0:T(2,128)}, u32[]{:S(2)}) copy-start(s32[4,1,8,2]{2,3,1,0:T(2,128)} %param.11) | copy-start | bytes 772
  0.0 4.1 %copy-start.3 = (f32[4,1,8,2]{2,3,1,0:T(2,128)S(1)}, f32[4,1,8,2]{2,3,1,0:T(2,128)}, u32[]{:S(2)}) copy-start(f32[4,1,8,2]{2,3,1,0:T(2,128)} %param.12) | copy-start | bytes 772
  1.5 24.7 %collective-permute-start.4 = (bf16[3,160,2048]{2,1,0:T(8,128)(2,1)S(1)}, bf16[3,160,2048]{2,1,0:T(8,128)(2,1)S(1)}, u32[]{:S(2)}, u32[]{:S(2)}) collective-permute-start(bf16[3,160,2048]{2,1,0:T(8,128)(2,1)S(1)} %stack.2), channel_id=1, source_target_pairs={{0,24},{1,25},{2,26},{3,27},{4,28},{5,29},{6,30},{7,31},{8,0},{9,1... | collective-permute-start | bytes 5898248 | tf_op jit(solution)/shard_map/ppermute | solution.py:27
  4.3 3.9 %collective-permute-start = (bf16[8,2176]{1,0:T(8,128)(2,1)S(1)}, bf16[8,2176]{1,0:T(8,128)(2,1)S(1)}, u32[]{:S(2)}, u32[]{:S(2)}) collective-permute-start(bf16[8,2176]{1,0:T(8,128)(2,1)S(1)} %shard_map.100.first_ref), channel_id=1, source_target_pairs={{0,1},{1,0},{2,3},{3,2},{4,5},{5,4},{6,7},{7,6},{8,9},{9,8},{10,11... | collective-permute-start | bytes 104456 | tf_op jit(solution)/shard_map/ppermute | solution.py:27
  8.3 9.8 %collective-permute-start.1 = (bf16[16,2176]{1,0:T(8,128)(2,1)S(1)}, bf16[16,2176]{1,0:T(8,128)(2,1)S(1)}, u32[]{:S(2)}, u32[]{:S(2)}) collective-permute-start(bf16[16,2176]{1,0:T(8,128)(2,1)S(1)} %shard_map.101.refs_0_.refs_4_), channel_id=1, source_target_pairs={{0,2},{1,3},{2,0},{3,1},{4,6},{5,7},{6,4},{7,5},{8,10},{9,11},{10,... | collective-permute-start | bytes 208904 | tf_op jit(solution)/shard_map/ppermute | solution.py:27
  9.9 9.7 %collective-permute-start.3 = (bf16[16,2176]{1,0:T(8,128)(2,1)S(1)}, bf16[16,2176]{1,0:T(8,128)(2,1)S(1)}, u32[]{:S(2)}, u32[]{:S(2)}) collective-permute-start(bf16[16,2176]{1,0:T(8,128)(2,1)S(1)} %shard_map.101.refs_0_.refs_4_), channel_id=1, source_target_pairs={{0,6},{1,7},{2,4},{3,5},{4,2},{5,3},{6,0},{7,1},{8,14},{9,15},{10,... | collective-permute-start | bytes 208904 | tf_op jit(solution)/shard_map/ppermute | solution.py:27
  12.4 7.3 %collective-permute-start.2 = (bf16[16,2176]{1,0:T(8,128)(2,1)S(1)}, bf16[16,2176]{1,0:T(8,128)(2,1)S(1)}, u32[]{:S(2)}, u32[]{:S(2)}) collective-permute-start(bf16[16,2176]{1,0:T(8,128)(2,1)S(1)} %shard_map.101.refs_0_.refs_4_), channel_id=1, source_target_pairs={{0,4},{1,5},{2,6},{3,7},{4,0},{5,1},{6,2},{7,3},{8,12},{9,13},{10,... | collective-permute-start | bytes 208904 | tf_op jit(solution)/shard_map/ppermute | solution.py:27
  18.1 8.1 %copy-start = (f32[2,1,2048]{2,1,0:T(1,128)S(1)}, f32[2,1,2048]{2,1,0:T(1,128)}, u32[]{:S(2)}) copy-start(f32[2,1,2048]{2,1,0:T(1,128)} %refs_8_.7) | copy-start | bytes 49156
  29.1 25.5 %collective-permute-start.13 = (bf16[3,160,2048]{2,1,0:T(8,128)(2,1)S(1)}, bf16[3,160,2048]{2,1,0:T(8,128)(2,1)S(1)}, u32[]{:S(2)}, u32[]{:S(2)}) collective-permute-start(bf16[3,160,2048]{2,1,0:T(8,128)(2,1)S(1)} %stack.3), channel_id=1, source_target_pairs={{0,24},{1,25},{2,26},{3,27},{4,28},{5,29},{6,30},{7,31},{8,0},{9,1... | collective-permute-start | bytes 5898248 | tf_op jit(solution)/shard_map/ppermute | solution.py:27
  31.1 6.3 %collective-permute-start.5 = (bf16[16,2048]{1,0:T(8,128)(2,1)S(1)}, bf16[16,2048]{1,0:T(8,128)(2,1)S(1)}, u32[]{:S(2)}, u32[]{:S(2)}) collective-permute-start(bf16[16,2048]{1,0:T(8,128)(2,1)S(1)} %get-tuple-element.40), channel_id=1, source_target_pairs={{0,6},{1,7},{2,4},{3,5},{4,2},{5,3},{6,0},{7,1},{8,14},{9,15},{10,... | collective-permute-start | bytes 196616 | tf_op jit(solution)/shard_map/ppermute | solution.py:27
  34.7 5.4 %collective-permute-start.6 = (bf16[16,2048]{1,0:T(8,128)(2,1)S(1)}, bf16[16,2048]{1,0:T(8,128)(2,1)S(1)}, u32[]{:S(2)}, u32[]{:S(2)}) collective-permute-start(bf16[16,2048]{1,0:T(8,128)(2,1)S(1)} %get-tuple-element.41), channel_id=1, source_target_pairs={{0,4},{1,5},{2,6},{3,7},{4,0},{5,1},{6,2},{7,3},{8,12},{9,13},{10,... | collective-permute-start | bytes 196616 | tf_op jit(solution)/shard_map/ppermute | solution.py:27
  34.7 5.4 %collective-permute-start.7 = (bf16[16,2048]{1,0:T(8,128)(2,1)S(1)}, bf16[16,2048]{1,0:T(8,128)(2,1)S(1)}, u32[]{:S(2)}, u32[]{:S(2)}) collective-permute-start(bf16[16,2048]{1,0:T(8,128)(2,1)S(1)} %get-tuple-element.42), channel_id=1, source_target_pairs={{0,2},{1,3},{2,0},{3,1},{4,6},{5,7},{6,4},{7,5},{8,10},{9,11},{10,... | collective-permute-start | bytes 196616 | tf_op jit(solution)/shard_map/ppermute | solution.py:27
  40.1 4.9 %collective-permute-start.9 = (bf16[16,2048]{1,0:T(8,128)(2,1)S(1)}, bf16[16,2048]{1,0:T(8,128)(2,1)S(1)}, u32[]{:S(2)}, u32[]{:S(2)}) collective-permute-start(bf16[16,2048]{1,0:T(8,128)(2,1)S(1)} %shard_map.102), channel_id=1, source_target_pairs={{0,9},{1,8},{2,11},{3,10},{4,13},{5,12},{6,15},{7,14},{8,17},{9,16... | collective-permute-start | bytes 196616 | tf_op jit(solution)/shard_map/ppermute | solution.py:27
  40.2 6.0 %collective-permute-start.8 = (bf16[16,2048]{1,0:T(8,128)(2,1)S(1)}, bf16[16,2048]{1,0:T(8,128)(2,1)S(1)}, u32[]{:S(2)}, u32[]{:S(2)}) collective-permute-start(bf16[16,2048]{1,0:T(8,128)(2,1)S(1)} %shard_map.102), channel_id=1, source_target_pairs={{0,8},{1,9},{2,10},{3,11},{4,12},{5,13},{6,14},{7,15},{8,16},{9,17... | collective-permute-start | bytes 196616 | tf_op jit(solution)/shard_map/ppermute | solution.py:27
  46.2 6.6 %collective-permute-start.12 = (bf16[16,2048]{1,0:T(8,128)(2,1)S(1)}, bf16[16,2048]{1,0:T(8,128)(2,1)S(1)}, u32[]{:S(2)}, u32[]{:S(2)}) collective-permute-start(bf16[16,2048]{1,0:T(8,128)(2,1)S(1)} %shard_map.103.refs_0_), channel_id=1, source_target_pairs={{0,6},{1,7},{2,4},{3,5},{4,2},{5,3},{6,0},{7,1},{8,14},{9,15},{10,... | collective-permute-start | bytes 196616 | tf_op jit(solution)/shard_map/ppermute | solution.py:27
  48.5 5.8 %collective-permute-start.11 = (bf16[16,2048]{1,0:T(8,128)(2,1)S(1)}, bf16[16,2048]{1,0:T(8,128)(2,1)S(1)}, u32[]{:S(2)}, u32[]{:S(2)}) collective-permute-start(bf16[16,2048]{1,0:T(8,128)(2,1)S(1)} %shard_map.103.refs_0_), channel_id=1, source_target_pairs={{0,4},{1,5},{2,6},{3,7},{4,0},{5,1},{6,2},{7,3},{8,12},{9,13},{10,... | collective-permute-start | bytes 196616 | tf_op jit(solution)/shard_map/ppermute | solution.py:27
  48.5 5.8 %collective-permute-start.10 = (bf16[16,2048]{1,0:T(8,128)(2,1)S(1)}, bf16[16,2048]{1,0:T(8,128)(2,1)S(1)}, u32[]{:S(2)}, u32[]{:S(2)}) collective-permute-start(bf16[16,2048]{1,0:T(8,128)(2,1)S(1)} %shard_map.103.refs_0_), channel_id=1, source_target_pairs={{0,2},{1,3},{2,0},{3,1},{4,6},{5,7},{6,4},{7,5},{8,10},{9,11},{10,... | collective-permute-start | bytes 196616 | tf_op jit(solution)/shard_map/ppermute | solution.py:27
  57.7 6.9 %collective-permute-start.14 = (bf16[16,2048]{1,0:T(8,128)(2,1)S(1)}, bf16[16,2048]{1,0:T(8,128)(2,1)S(1)}, u32[]{:S(2)}, u32[]{:S(2)}) collective-permute-start(bf16[16,2048]{1,0:T(8,128)(2,1)S(1)} %get-tuple-element.48), channel_id=1, source_target_pairs={{0,6},{1,7},{2,4},{3,5},{4,2},{5,3},{6,0},{7,1},{8,14},{9,15},{10,... | collective-permute-start | bytes 196616 | tf_op jit(solution)/shard_map/ppermute | solution.py:27
  61.4 6.4 %collective-permute-start.15 = (bf16[16,2048]{1,0:T(8,128)(2,1)S(1)}, bf16[16,2048]{1,0:T(8,128)(2,1)S(1)}, u32[]{:S(2)}, u32[]{:S(2)}) collective-permute-start(bf16[16,2048]{1,0:T(8,128)(2,1)S(1)} %get-tuple-element.49), channel_id=1, source_target_pairs={{0,4},{1,5},{2,6},{3,7},{4,0},{5,1},{6,2},{7,3},{8,12},{9,13},{10,... | collective-permute-start | bytes 196616 | tf_op jit(solution)/shard_map/ppermute | solution.py:27
  61.4 6.4 %collective-permute-start.16 = (bf16[16,2048]{1,0:T(8,128)(2,1)S(1)}, bf16[16,2048]{1,0:T(8,128)(2,1)S(1)}, u32[]{:S(2)}, u32[]{:S(2)}) collective-permute-start(bf16[16,2048]{1,0:T(8,128)(2,1)S(1)} %get-tuple-element.50), channel_id=1, source_target_pairs={{0,2},{1,3},{2,0},{3,1},{4,6},{5,7},{6,4},{7,5},{8,10},{9,11},{10,... | collective-permute-start | bytes 196616 | tf_op jit(solution)/shard_map/ppermute | solution.py:27
  67.8 4.7 %collective-permute-start.18 = (bf16[16,2048]{1,0:T(8,128)(2,1)S(1)}, bf16[16,2048]{1,0:T(8,128)(2,1)S(1)}, u32[]{:S(2)}, u32[]{:S(2)}) collective-permute-start(bf16[16,2048]{1,0:T(8,128)(2,1)S(1)} %shard_map.104), channel_id=1, source_target_pairs={{0,9},{1,8},{2,11},{3,10},{4,13},{5,12},{6,15},{7,14},{8,17},{9,16... | collective-permute-start | bytes 196616 | tf_op jit(solution)/shard_map/ppermute | solution.py:27
  68.9 4.2 %collective-permute-start.17 = (bf16[16,2048]{1,0:T(8,128)(2,1)S(1)}, bf16[16,2048]{1,0:T(8,128)(2,1)S(1)}, u32[]{:S(2)}, u32[]{:S(2)}) collective-permute-start(bf16[16,2048]{1,0:T(8,128)(2,1)S(1)} %shard_map.104), channel_id=1, source_target_pairs={{0,8},{1,9},{2,10},{3,11},{4,12},{5,13},{6,14},{7,15},{8,16},{9,17... | collective-permute-start | bytes 196616 | tf_op jit(solution)/shard_map/ppermute | solution.py:27
  73.2 6.4 %collective-permute-start.21 = (bf16[16,2048]{1,0:T(8,128)(2,1)S(1)}, bf16[16,2048]{1,0:T(8,128)(2,1)S(1)}, u32[]{:S(2)}, u32[]{:S(2)}) collective-permute-start(bf16[16,2048]{1,0:T(8,128)(2,1)S(1)} %shard_map.105.refs_0_), channel_id=1, source_target_pairs={{0,6},{1,7},{2,4},{3,5},{4,2},{5,3},{6,0},{7,1},{8,14},{9,15},{10,... | collective-permute-start | bytes 196616 | tf_op jit(solution)/shard_map/ppermute | solution.py:27
  75.8 5.9 %collective-permute-start.20 = (bf16[16,2048]{1,0:T(8,128)(2,1)S(1)}, bf16[16,2048]{1,0:T(8,128)(2,1)S(1)}, u32[]{:S(2)}, u32[]{:S(2)}) collective-permute-start(bf16[16,2048]{1,0:T(8,128)(2,1)S(1)} %shard_map.105.refs_0_), channel_id=1, source_target_pairs={{0,4},{1,5},{2,6},{3,7},{4,0},{5,1},{6,2},{7,3},{8,12},{9,13},{10,... | collective-permute-start | bytes 196616 | tf_op jit(solution)/shard_map/ppermute | solution.py:27
  76.0 5.6 %collective-permute-start.19 = (bf16[16,2048]{1,0:T(8,128)(2,1)S(1)}, bf16[16,2048]{1,0:T(8,128)(2,1)S(1)}, u32[]{:S(2)}, u32[]{:S(2)}) collective-permute-start(bf16[16,2048]{1,0:T(8,128)(2,1)S(1)} %shard_map.105.refs_0_), channel_id=1, source_target_pairs={{0,2},{1,3},{2,0},{3,1},{4,6},{5,7},{6,4},{7,5},{8,10},{9,11},{10,... | collective-permute-start | bytes 196616 | tf_op jit(solution)/shard_map/ppermute | solution.py:27
  84.7 6.4 %collective-permute-start.22 = (bf16[16,2048]{1,0:T(8,128)(2,1)S(1)}, bf16[16,2048]{1,0:T(8,128)(2,1)S(1)}, u32[]{:S(2)}, u32[]{:S(2)}) collective-permute-start(bf16[16,2048]{1,0:T(8,128)(2,1)S(1)} %get-tuple-element.52), channel_id=1, source_target_pairs={{0,6},{1,7},{2,4},{3,5},{4,2},{5,3},{6,0},{7,1},{8,14},{9,15},{10,... | collective-permute-start | bytes 196616 | tf_op jit(solution)/shard_map/ppermute | solution.py:27
  86.7 6.3 %collective-permute-start.23 = (bf16[16,2048]{1,0:T(8,128)(2,1)S(1)}, bf16[16,2048]{1,0:T(8,128)(2,1)S(1)}, u32[]{:S(2)}, u32[]{:S(2)}) collective-permute-start(bf16[16,2048]{1,0:T(8,128)(2,1)S(1)} %get-tuple-element.53), channel_id=1, source_target_pairs={{0,4},{1,5},{2,6},{3,7},{4,0},{5,1},{6,2},{7,3},{8,12},{9,13},{10,... | collective-permute-start | bytes 196616 | tf_op jit(solution)/shard_map/ppermute | solution.py:27
  86.7 6.3 %collective-permute-start.24 = (bf16[16,2048]{1,0:T(8,128)(2,1)S(1)}, bf16[16,2048]{1,0:T(8,128)(2,1)S(1)}, u32[]{:S(2)}, u32[]{:S(2)}) collective-permute-start(bf16[16,2048]{1,0:T(8,128)(2,1)S(1)} %get-tuple-element.54), channel_id=1, source_target_pairs={{0,2},{1,3},{2,0},{3,1},{4,6},{5,7},{6,4},{7,5},{8,10},{9,11},{10,... | collective-permute-start | bytes 196616 | tf_op jit(solution)/shard_map/ppermute | solution.py:27
  93.0 4.7 %collective-permute-start.26 = (bf16[16,2048]{1,0:T(8,128)(2,1)S(1)}, bf16[16,2048]{1,0:T(8,128)(2,1)S(1)}, u32[]{:S(2)}, u32[]{:S(2)}) collective-permute-start(bf16[16,2048]{1,0:T(8,128)(2,1)S(1)} %shard_map.106), channel_id=1, source_target_pairs={{0,9},{1,8},{2,11},{3,10},{4,13},{5,12},{6,15},{7,14},{8,17},{9,16... | collective-permute-start | bytes 196616 | tf_op jit(solution)/shard_map/ppermute | solution.py:27
  94.1 4.3 %collective-permute-start.25 = (bf16[16,2048]{1,0:T(8,128)(2,1)S(1)}, bf16[16,2048]{1,0:T(8,128)(2,1)S(1)}, u32[]{:S(2)}, u32[]{:S(2)}) collective-permute-start(bf16[16,2048]{1,0:T(8,128)(2,1)S(1)} %shard_map.106), channel_id=1, source_target_pairs={{0,8},{1,9},{2,10},{3,11},{4,12},{5,13},{6,14},{7,15},{8,16},{9,17... | collective-permute-start | bytes 196616 | tf_op jit(solution)/shard_map/ppermute | solution.py:27
  98.4 6.5 %collective-permute-start.29 = (bf16[16,2048]{1,0:T(8,128)(2,1)S(1)}, bf16[16,2048]{1,0:T(8,128)(2,1)S(1)}, u32[]{:S(2)}, u32[]{:S(2)}) collective-permute-start(bf16[16,2048]{1,0:T(8,128)(2,1)S(1)} %shard_map.107.refs_0_), channel_id=1, source_target_pairs={{0,6},{1,7},{2,4},{3,5},{4,2},{5,3},{6,0},{7,1},{8,14},{9,15},{10,... | collective-permute-start | bytes 196616 | tf_op jit(solution)/shard_map/ppermute | solution.py:27
  100.6 6.1 %collective-permute-start.28 = (bf16[16,2048]{1,0:T(8,128)(2,1)S(1)}, bf16[16,2048]{1,0:T(8,128)(2,1)S(1)}, u32[]{:S(2)}, u32[]{:S(2)}) collective-permute-start(bf16[16,2048]{1,0:T(8,128)(2,1)S(1)} %shard_map.107.refs_0_), channel_id=1, source_target_pairs={{0,4},{1,5},{2,6},{3,7},{4,0},{5,1},{6,2},{7,3},{8,12},{9,13},{10,... | collective-permute-start | bytes 196616 | tf_op jit(solution)/shard_map/ppermute | solution.py:27
  100.6 6.1 %collective-permute-start.27 = (bf16[16,2048]{1,0:T(8,128)(2,1)S(1)}, bf16[16,2048]{1,0:T(8,128)(2,1)S(1)}, u32[]{:S(2)}, u32[]{:S(2)}) collective-permute-start(bf16[16,2048]{1,0:T(8,128)(2,1)S(1)} %shard_map.107.refs_0_), channel_id=1, source_target_pairs={{0,2},{1,3},{2,0},{3,1},{4,6},{5,7},{6,4},{7,5},{8,10},{9,11},{10,... | collective-permute-start | bytes 196616 | tf_op jit(solution)/shard_map/ppermute | solution.py:27
  109.8 6.8 %collective-permute-start.30 = (bf16[16,2048]{1,0:T(8,128)(2,1)S(1)}, bf16[16,2048]{1,0:T(8,128)(2,1)S(1)}, u32[]{:S(2)}, u32[]{:S(2)}) collective-permute-start(bf16[16,2048]{1,0:T(8,128)(2,1)S(1)} %get-tuple-element.56), channel_id=1, source_target_pairs={{0,6},{1,7},{2,4},{3,5},{4,2},{5,3},{6,0},{7,1},{8,14},{9,15},{10,... | collective-permute-start | bytes 196616 | tf_op jit(solution)/shard_map/ppermute | solution.py:27
  111.7 6.5 %collective-permute-start.31 = (bf16[16,2048]{1,0:T(8,128)(2,1)S(1)}, bf16[16,2048]{1,0:T(8,128)(2,1)S(1)}, u32[]{:S(2)}, u32[]{:S(2)}) collective-permute-start(bf16[16,2048]{1,0:T(8,128)(2,1)S(1)} %get-tuple-element.57), channel_id=1, source_target_pairs={{0,4},{1,5},{2,6},{3,7},{4,0},{5,1},{6,2},{7,3},{8,12},{9,13},{10,... | collective-permute-start | bytes 196616 | tf_op jit(solution)/shard_map/ppermute | solution.py:27
  111.7 6.5 %collective-permute-start.32 = (bf16[16,2048]{1,0:T(8,128)(2,1)S(1)}, bf16[16,2048]{1,0:T(8,128)(2,1)S(1)}, u32[]{:S(2)}, u32[]{:S(2)}) collective-permute-start(bf16[16,2048]{1,0:T(8,128)(2,1)S(1)} %get-tuple-element.58), channel_id=1, source_target_pairs={{0,2},{1,3},{2,0},{3,1},{4,6},{5,7},{6,4},{7,5},{8,10},{9,11},{10,... | collective-permute-start | bytes 196616 | tf_op jit(solution)/shard_map/ppermute | solution.py:27
  118.2 4.0 %collective-permute-start.33 = (bf16[8,2048]{1,0:T(8,128)(2,1)S(1)}, bf16[8,2048]{1,0:T(8,128)(2,1)S(1)}, u32[]{:S(2)}, u32[]{:S(2)}) collective-permute-start(bf16[8,2048]{1,0:T(8,128)(2,1)S(1)} %slice.17), channel_id=1, source_target_pairs={{0,1},{1,0},{2,3},{3,2},{4,5},{5,4},{6,7},{7,6},{8,9},{9,8},{10,11... | collective-permute-start | bytes 98312 | tf_op jit(solution)/shard_map/ppermute | solution.py:27

commit v4 on v3

--- a/solution.py
+++ b/solution.py
@@ -93,11 +93,25 @@
     out_ref[...] = jnp.concatenate([first_ref[...], second_ref[...]], axis=0)
 
 
-def layer_kernel(*refs, tick_idx, blocks, spare_count, tok_dev, width):
+def served(normed, gate, up, down):
+    contract = (((1,), (1,)), ((), ()))
+    gate_pre = lax.dot_general(normed, gate, contract, preferred_element_type=jnp.float32)
+    up_pre = lax.dot_general(normed, up, contract, preferred_element_type=jnp.float32)
+    hidden = (gate_pre / (1.0 + jnp.exp(-gate_pre)) * up_pre).astype(jnp.bfloat16)
+    return jnp.dot(hidden, down, preferred_element_type=jnp.float32)
+
+
+def layer_kernel(*refs, tick_idx, blocks, spare_counts, tok_dev, width, carried, ends):
     x_refs, first_refs, refs = refs[:blocks], refs[blocks:2 * blocks], refs[2 * blocks:]
-    gain_ref, gate_ref, up_ref, down_ref = refs[:4]
-    spare_refs, refs = refs[4:4 + spare_count], refs[4 + spare_count:]
-    out_refs, (total_ref,) = refs[:blocks], refs[blocks:]
+    gain_ref, refs = refs[0], refs[1:]
+    if carried:
+        carried_ref, refs = refs[0], refs[1:]
+    else:
+        (gate_ref, up_ref, down_ref), refs = refs[:3], refs[3:]
+    spare_refs = []
+    for count in spare_counts:
+        spare_refs.append(refs[:count] if count > 1 else [refs[0].at[i] for i in range(refs[0].shape[0])])
+        refs = refs[count:]
     segments, members = lax.axis_size("segment"), lax.axis_size("expert")
     group = group_of(lax.axis_index("segment"), tick_idx, segments)
     expert = lax.axis_index("expert") // (members // EXPERTS)
@@ -112,30 +126,28 @@
     def column(at):
         return jnp.sum(jnp.where((lane == at) | (lane == at + columns), table, 0.0), axis=1, keepdims=True)
 
-    share = column(tick_idx * (EXPERTS + 1) + expert)
-    spill = column(tick_idx * (EXPERTS + 1) + EXPERTS)
-    contract = (((1,), (1,)), ((), ()))
-
-    def served(gate, up, down):
-        gate_pre = lax.dot_general(normed, gate, contract, preferred_element_type=jnp.float32)
-        up_pre = lax.dot_general(normed, up, contract, preferred_element_type=jnp.float32)
-        hidden = (gate_pre / (1.0 + jnp.exp(-gate_pre)) * up_pre).astype(jnp.bfloat16)
-        return jnp.dot(hidden, down, preferred_element_type=jnp.float32)
-
-    total_ref[...] = share * served(gate_ref[group], up_ref[group], down_ref[group])
+    total_ref = refs[0] if not ends else refs[-1]
+    if carried:
+        total_ref[...] = carried_ref[...]
+    else:
+        share = column(tick_idx * (EXPERTS + 1) + expert)
+        total_ref[...] = share * served(normed, gate_ref[group], up_ref[group], down_ref[group])
     for at, spare_ref in enumerate(spare_refs):
 
         def add(spare_ref=spare_ref):
-            total_ref[...] += spill * served(spare_ref[0], spare_ref[1], spare_ref[2])
-
-        if spare_count == 1:
+            spill = column(tick_idx * (EXPERTS + 1) + EXPERTS)
+            total_ref[...] += spill * served(normed, *[ref[...] for ref in spare_ref])
+
+        if len(spare_refs) == 1:
             add()
         else:
             pl.when(group == at)(add)
+    if not ends:
+        return
+    out_refs = refs[:blocks]
     per = 2 * tok_dev
-    first = total_ref[0:per, :]
     row = lax.broadcasted_iota(jnp.int32, (per, 1), 0)
-    out_refs[0][...] = first + jnp.where(row < tok_dev, values[0:per], 0.0)
+    out_refs[0][...] = total_ref[0:per, :] + jnp.where(row < tok_dev, values[0:per], 0.0)
     for i in range(1, blocks):
         out_refs[i][...] = total_ref[i * per:(i + 1) * per, :].astype(jnp.bfloat16)
 
@@ -144,27 +156,34 @@
     return [pltpu.with_memory_space_constraint(value, pltpu.VMEM) for value in values]
 
 
-def run_layer(x_blocks, first_blocks, gain, weights, spares, *, tick_idx, tok_dev):
+def run_layer(x_blocks, first_blocks, gain, weights, spares, *, tick_idx, tok_dev, carried=None, ends=True):
     blocks = len(x_blocks)
     width = gain.shape[-1]
     per = 2 * tok_dev
     rows = per * blocks
-    hidden = weights[0].shape[1] + spares[0].shape[1]
+    values = [*x_blocks, *first_blocks, gain]
+    values += [carried] if carried is not None else resident(weights)
+    for spare in spares:
+        values += resident(spare)
+    hidden = (0 if carried is not None else weights[0].shape[1]) + (spares[0][0].shape[0] if spares else 0)
+    whole = jax.ShapeDtypeStruct((rows, width), jnp.float32)
+    parts = [jax.ShapeDtypeStruct((per, width), jnp.float32)]
+    parts += [jax.ShapeDtypeStruct((per, width), jnp.bfloat16)] * (blocks - 1)
     return pl.pallas_call(
         functools.partial(
-            layer_kernel, tick_idx=tick_idx, blocks=blocks, spare_count=len(spares), tok_dev=tok_dev, width=width
+            layer_kernel, tick_idx=tick_idx, blocks=blocks, spare_counts=[len(spare) for spare in spares],
+            tok_dev=tok_dev, width=width, carried=carried is not None, ends=ends,
         ),
-        out_shape=[jax.ShapeDtypeStruct((per, width), jnp.float32)]
-        + [jax.ShapeDtypeStruct((per, width), jnp.bfloat16)] * (blocks - 1),
-        in_specs=[WHOLE] * (2 * blocks + 4 + len(spares)),
-        out_specs=[WHOLE] * blocks,
-        scratch_shapes=[pltpu.VMEM((rows, width), jnp.float32)],
+        out_shape=parts if ends else whole,
+        in_specs=[WHOLE] * len(values),
+        out_specs=[WHOLE] * blocks if ends else WHOLE,
+        scratch_shapes=[pltpu.VMEM((rows, width), jnp.float32)] if ends else [],
         compiler_params=pltpu.CompilerParams(vmem_limit_bytes=12 * 1024 * 1024),
         cost_estimate=pl.CostEstimate(
             flops=6 * rows * hidden * width, bytes_accessed=6 * hidden * width, transcendentals=rows * hidden
         ),
         name="layer",
-    )(*x_blocks, *first_blocks, gain, *resident(weights), *resident(spares))
+    )(*values)
 
 
 def sum_kernel(*refs, swap):
@@ -207,27 +226,26 @@
     )(*[pltpu.with_memory_space_constraint(value, pltpu.HBM) for value in values])
 
 
-def stack_kernel(gate_ref, up_ref, down_ref, out_ref, sems, *, group):
-    copies = [
-        pltpu.make_async_copy(ref.at[group], out_ref.at[i], sems.at[i])
-        for i, ref in enumerate((gate_ref, up_ref, down_ref))
-    ]
+def stack_kernel(*refs, group):
+    ins, out, sems = refs[:-2], refs[-2], refs[-1]
+    copies = [pltpu.make_async_copy(one.at[group], out.at[i], sems.at[i]) for i, one in enumerate(ins)]
     for copy in copies:
         copy.start()
     for copy in copies:
         copy.wait()
 
 
-def stacked(spares, group):
+def stacked(values, group):
+    shape = (len(values),) + values[0].shape[1:]
     return pl.pallas_call(
         functools.partial(stack_kernel, group=group),
-        out_shape=pltpu.VMEM((3,) + spares[0].shape[1:], spares[0].dtype),
-        in_specs=[pl.BlockSpec(memory_space=pltpu.HBM)] * 3,
+        out_shape=pltpu.VMEM(shape, values[0].dtype),
+        in_specs=[pl.BlockSpec(memory_space=pltpu.HBM)] * len(values),
         out_specs=WHOLE,
-        scratch_shapes=[pltpu.SemaphoreType.DMA((3,))],
+        scratch_shapes=[pltpu.SemaphoreType.DMA((len(values),))],
         compiler_params=pltpu.CompilerParams(vmem_limit_bytes=6 * 1024 * 1024),
         name="stack",
-    )(*[pltpu.with_memory_space_constraint(value, pltpu.HBM) for value in spares])
+    )(*[pltpu.with_memory_space_constraint(value, pltpu.HBM) for value in values])
 
 
 def widest_first(outer):
@@ -256,8 +274,13 @@
 
     weights = [w_gate[:, 0], w_up[:, 0], w_down[:, 0]]
     spare_all = [spare_gate[:, 0], spare_up[:, 0], spare_down[:, 0]]
-    sent, state, routes, gates = lax.optimization_barrier((stacked(spare_all, 0), state, routes, gates))
-    spares = [moved(sent, 0, -1)]
+
+    def fetched(values):
+        return [moved(value, 0, -1) for value in values]
+
+    head = filled(spare_all[:1], 0)
+    head, rest, state, routes, gates = lax.optimization_barrier((head, spare_all[1:], state, routes, gates))
+    spares = [fetched(head + filled(rest, 0))]
     shape = (tok_dev, state.shape[2] + LANES)
     own = small(
         prepare_kernel, jax.ShapeDtypeStruct(shape, state.dtype), state[0],
@@ -267,17 +290,22 @@
     pair = small(join_kernel, jax.ShapeDtypeStruct((2 * tok_dev, shape[1]), state.dtype), own, other)
     arrived = spread(pair)
     weights = filled(weights)
+    late = stacked(lax.optimization_barrier((*spare_all, arrived[1]))[:3], 1)
+    before = run_layer(
+        arrived, arrived, norm_gain, weights, [], tick_idx=0, tok_dev=tok_dev, ends=False
+    )
+    late = moved(late, 0, -1)
+    spares.append([late])
+
     x_blocks = arrived
-    late = stacked(lax.optimization_barrier((*spare_all, arrived[1]))[:3], 1)
     for tick_idx in range(TICKS):
-        needed = groups_at(tick_idx, segments)
-        if tick_idx == 0 and needed != {0}:
-            spares.append(moved(late, 0, -1))
-        parts = run_layer(x_blocks, arrived, norm_gain, weights, spares, tick_idx=tick_idx, tok_dev=tok_dev)
+        used = sorted(groups_at(tick_idx, segments))
+        assert used in ([0], [0, 1])
+        parts = run_layer(
+            x_blocks, arrived, norm_gain, weights, spares[:len(used)], tick_idx=tick_idx, tok_dev=tok_dev,
+            carried=before if tick_idx == 0 else None,
+        )
         got = [moved(parts[j], 2 * j, 0) for j in widest_first(outer)]
-        if len(spares) == 1:
-            late, _ = lax.optimization_barrier((late, parts[0]))
-            spares.append(moved(late, 0, -1))
         if tick_idx + 1 == TICKS:
             total = added([parts[0]] + got)
             other = moved(total[tok_dev:].astype(jnp.bfloat16), 1, 0)

time: 123 us -> 149 us (1.21)
  waiting for transfers between devices: 53.8 us -> 72.1 us
  starting transfers between devices: 47.1 us -> 51.8 us
  local copies, waits for them, and re-layouts: 0.02 us -> 2.14 us
    ppermute x34 -> x36, waiting for transfers between devices: 53.8 us -> 72.1 us  [moved(): return lax.ppermute(value, BOTH, pairs)]
    ppermute x34 -> x36, starting transfers between devices: 47.1 us -> 51.8 us  [moved(): return lax.ppermute(value, BOTH, pairs)]
    pallas_call x1 -> x3, Pallas kernels: 5.57 us -> 7.97 us  [filled(): pl.pallas_call(functools.partial(fill_kernel, group=group), out_shape=[pl...]
    unnamed x8, local copies, waits for them, and re-layouts: 0.02 us -> 2.13 us
    pallas_call x2 -> x1, Pallas kernels: 3.03 us -> 1.51 us  [stacked(): pl.pallas_call(functools.partial(stack_kernel, group=group), out_shape=pl...]
    pallas_call x4 -> x5, Pallas kernels: 12.1 us -> 12.3 us  [run_layer(): pl.pallas_call(functools.partial(layer_kernel, tick_idx=tick_idx, blocks=...]
  transfers between devices with their start and end apart: 34 -> 36, of which waited for: 24 -> 25; matrix products, arithmetic and copies ran while one was open for 0% -> 0% of each run, Pallas kernels for 6% -> 7%
where the time goes in v4:
time: 149 us
  waiting for transfers between devices  72.1 us (48%)
  starting transfers between devices  51.8 us (35%)
  Pallas kernels  22.2 us (15%)
  local copies, waits for them, and re-layouts  2.14 us (1%)
    ppermute x36, waiting for transfers between devices, moved(): return lax.ppermute(value, BOTH, pairs)  72.1 us
    ppermute x36, starting transfers between devices, moved(): return lax.ppermute(value, BOTH, pairs)  51.8 us
    pallas_call x5, Pallas kernels, run_layer(): pl.pallas_call(functools.partial(layer_kernel, tick_idx=tick_idx, blocks=...  12.3 us
    pallas_call x3, Pallas kernels, filled(): pl.pallas_call(functools.partial(fill_kernel, group=group), out_shape=[pl...  7.97 us
  transfers between devices with their start and end apart: 36, of which 25 were waited for; matrix products, arithmetic and copies ran while one was open for 0% of the time, Pallas kernels for 7%

profile of v4, /device:TPU:0, one launch (start us, length us, event | category | flops | bytes accessed | tf_op | source)
XLA Modules:
  0.0 149.0 jit_solution(17379347315777803574)
XLA Ops:
  3.5 3.0 %collective-permute-start = (bf16[8,2176]{1,0:T(8,128)(2,1)S(1)}, bf16[8,2176]{1,0:T(8,128)(2,1)S(1)}, u32[]{:S(2)}, u32[]{:S(2)}) collective-permute-start(bf16[8,2176]{1,0:T(8,128)(2,1)S(1)} %shard_map.100.first_ref), channel_id=1, source_target_pairs={{0,1},{1,0},{2,3},{3,2},{4,5},{5,4},{6,7},{7,6},{8,9},{9,8},{10,11... | collective-permute-start | bytes 104456 | tf_op jit(solution)/shard_map/ppermute | solution.py:27
  6.5 1.9 %collective-permute-done.second_ref = bf16[8,2176]{1,0:T(8,128)(2,1)S(1)} collective-permute-done((bf16[8,2176]{1,0:T(8,128)(2,1)S(1)}, bf16[8,2176]{1,0:T(8,128)(2,1)S(1)}, u32[]{:S(2)}, u32[]{:S(2)}) %collective-permute-start) | collective-permute-done | bytes 34848 | tf_op jit(solution)/shard_map/ppermute | solution.py:27
  8.4 2.2 %collective-permute-start.1 = (bf16[16,2176]{1,0:T(8,128)(2,1)S(1)}, bf16[16,2176]{1,0:T(8,128)(2,1)S(1)}, u32[]{:S(2)}, u32[]{:S(2)}) collective-permute-start(bf16[16,2176]{1,0:T(8,128)(2,1)S(1)} %shard_map.101.refs_0_.refs_4_), channel_id=1, source_target_pairs={{0,2},{1,3},{2,0},{3,1},{4,6},{5,7},{6,4},{7,5},{8,10},{9,11},{10,... | collective-permute-start | bytes 208904 | tf_op jit(solution)/shard_map/ppermute | solution.py:27
  10.6 2.3 %collective-permute-done.1.refs_1_.refs_5_ = bf16[16,2176]{1,0:T(8,128)(2,1)S(1)} collective-permute-done((bf16[16,2176]{1,0:T(8,128)(2,1)S(1)}, bf16[16,2176]{1,0:T(8,128)(2,1)S(1)}, u32[]{:S(2)}, u32[]{:S(2)}) %collective-permute-start.1) | collective-permute-done | bytes 69664 | tf_op jit(solution)/shard_map/ppermute | solution.py:27
  14.4 2.1 %collective-permute-start.4 = (bf16[160,2048]{1,0:T(8,128)(2,1)S(1)}, bf16[160,2048]{1,0:T(8,128)(2,1)S(1)}, u32[]{:S(2)}, u32[]{:S(2)}) collective-permute-start(bf16[160,2048]{1,0:T(8,128)(2,1)S(1)} %fill.3), channel_id=1, source_target_pairs={{0,24},{1,25},{2,26},{3,27},{4,28},{5,29},{6,30},{7,31},{8,0},{9,1... | collective-permute-start | bytes 1966088 | tf_op jit(solution)/shard_map/ppermute | solution.py:27
  18.0 4.0 %collective-permute-start.3 = (bf16[16,2176]{1,0:T(8,128)(2,1)S(1)}, bf16[16,2176]{1,0:T(8,128)(2,1)S(1)}, u32[]{:S(2)}, u32[]{:S(2)}) collective-permute-start(bf16[16,2176]{1,0:T(8,128)(2,1)S(1)} %shard_map.101.refs_0_.refs_4_), channel_id=1, source_target_pairs={{0,6},{1,7},{2,4},{3,5},{4,2},{5,3},{6,0},{7,1},{8,14},{9,15},{10,... | collective-permute-start | bytes 208904 | tf_op jit(solution)/shard_map/ppermute | solution.py:27
  22.1 2.4 %collective-permute-done.3.refs_3_.refs_7_ = bf16[16,2176]{1,0:T(8,128)(2,1)S(1)} collective-permute-done((bf16[16,2176]{1,0:T(8,128)(2,1)S(1)}, bf16[16,2176]{1,0:T(8,128)(2,1)S(1)}, u32[]{:S(2)}, u32[]{:S(2)}) %collective-permute-start.3) | collective-permute-done | bytes 69664 | tf_op jit(solution)/shard_map/ppermute | solution.py:27
  25.4 5.6 %fill.4 = (bf16[2,640,2048]{2,1,0:T(8,128)(2,1)S(1)}, bf16[2,640,2048]{2,1,0:T(8,128)(2,1)S(1)}, bf16[2,640,2048]{2,1,0:T(8,128)(2,1)S(1)}) custom-call(bf16[2,640,2048]{2,1,0:T(8,128)(2,1)} %bitcast.22, bf16[2,640,2048]{2,1,0:T(8,128)(2,1)} %bitcast.23, bf16[2,640,2048]{2,1,0:T(8,128)(2,1)} %bitcast.24), custom_call_target="tpu_custom_call" | custom-call | tf_op jit(solution)/shard_map/fill/pallas_call | solution.py:218
  31.0 2.2 %layer.5.refs_9_ = f32[64,2048]{1,0:T(8,128)S(1)} custom-call(bf16[16,2176]{1,0:T(8,128)(2,1)S(1)} %shard_map.101.refs_0_.refs_4_, bf16[16,2176]{1,0:T(8,128)(2,1)S(1)} %collective-permute-done.1.refs_1_.refs_5_, bf16[16,2176]{1,0:T(8,128)(2,1)S(1)} %collective-permute-done.2.refs_2_.refs_6_, bf16[16,2176]{1,0:T(8,128)(2,1)S(1)} %collective-permute-done.3.refs_3_.refs_7_, ...), custom_call_target="tpu_custom_call" | custom-call | flops 503316480 | bytes 7864320 | tf_op jit(solution)/shard_map/layer/pallas_call | solution.py:172
  33.3 10.4 %collective-permute-done.4.refs_10_.refs_12_ = bf16[160,2048]{1,0:T(8,128)(2,1)S(1)} collective-permute-done((bf16[160,2048]{1,0:T(8,128)(2,1)S(1)}, bf16[160,2048]{1,0:T(8,128)(2,1)S(1)}, u32[]{:S(2)}, u32[]{:S(2)}) %collective-permute-start.4) | collective-permute-done | bytes 655392 | tf_op jit(solution)/shard_map/ppermute | solution.py:27
  43.6 7.0 %collective-permute-done.5.refs_11_.refs_13_ = bf16[160,2048]{1,0:T(8,128)(2,1)S(1)} collective-permute-done((bf16[160,2048]{1,0:T(8,128)(2,1)S(1)}, bf16[160,2048]{1,0:T(8,128)(2,1)S(1)}, u32[]{:S(2)}, u32[]{:S(2)}) %collective-permute-start.5) | collective-permute-done | bytes 655392 | tf_op jit(solution)/shard_map/ppermute | solution.py:27
  50.6 7.0 %collective-permute-done.6.refs_12_.refs_14_ = bf16[160,2048]{1,0:T(8,128)(2,1)S(1)} collective-permute-done((bf16[160,2048]{1,0:T(8,128)(2,1)S(1)}, bf16[160,2048]{1,0:T(8,128)(2,1)S(1)}, u32[]{:S(2)}, u32[]{:S(2)}) %collective-permute-start.6) | collective-permute-done | bytes 655392 | tf_op jit(solution)/shard_map/ppermute | solution.py:27
  58.5 4.1 %collective-permute-start.7 = (bf16[16,2048]{1,0:T(8,128)(2,1)S(1)}, bf16[16,2048]{1,0:T(8,128)(2,1)S(1)}, u32[]{:S(2)}, u32[]{:S(2)}) collective-permute-start(bf16[16,2048]{1,0:T(8,128)(2,1)S(1)} %get-tuple-element.47), channel_id=1, source_target_pairs={{0,6},{1,7},{2,4},{3,5},{4,2},{5,3},{6,0},{7,1},{8,14},{9,15},{10,... | collective-permute-start | bytes 196616 | tf_op jit(solution)/shard_map/ppermute | solution.py:27
  63.3 1.7 %collective-permute-done.7.refs_1_ = bf16[16,2048]{1,0:T(8,128)(2,1)S(1)} collective-permute-done((bf16[16,2048]{1,0:T(8,128)(2,1)S(1)}, bf16[16,2048]{1,0:T(8,128)(2,1)S(1)}, u32[]{:S(2)}, u32[]{:S(2)}) %collective-permute-start.7) | collective-permute-done | bytes 65568 | tf_op jit(solution)/shard_map/ppermute | solution.py:27
  65.0 3.9 %collective-permute-done.8.refs_2_ = bf16[16,2048]{1,0:T(8,128)(2,1)S(1)} collective-permute-done((bf16[16,2048]{1,0:T(8,128)(2,1)S(1)}, bf16[16,2048]{1,0:T(8,128)(2,1)S(1)}, u32[]{:S(2)}, u32[]{:S(2)}) %collective-permute-start.8) | collective-permute-done | bytes 65568 | tf_op jit(solution)/shard_map/ppermute | solution.py:27
  71.7 2.3 %collective-permute-done.11.refs_1_ = bf16[16,2048]{1,0:T(8,128)(2,1)S(1)} collective-permute-done((bf16[16,2048]{1,0:T(8,128)(2,1)S(1)}, bf16[16,2048]{1,0:T(8,128)(2,1)S(1)}, u32[]{:S(2)}, u32[]{:S(2)}) %collective-permute-start.11) | collective-permute-done | bytes 65568 | tf_op jit(solution)/shard_map/ppermute | solution.py:27
  74.4 2.4 %collective-permute-start.14 = (bf16[16,2048]{1,0:T(8,128)(2,1)S(1)}, bf16[16,2048]{1,0:T(8,128)(2,1)S(1)}, u32[]{:S(2)}, u32[]{:S(2)}) collective-permute-start(bf16[16,2048]{1,0:T(8,128)(2,1)S(1)} %shard_map.103.refs_0_), channel_id=1, source_target_pairs={{0,6},{1,7},{2,4},{3,5},{4,2},{5,3},{6,0},{7,1},{8,14},{9,15},{10,... | collective-permute-start | bytes 196616 | tf_op jit(solution)/shard_map/ppermute | solution.py:27
  76.8 2.0 %collective-permute-start.12 = (bf16[16,2048]{1,0:T(8,128)(2,1)S(1)}, bf16[16,2048]{1,0:T(8,128)(2,1)S(1)}, u32[]{:S(2)}, u32[]{:S(2)}) collective-permute-start(bf16[16,2048]{1,0:T(8,128)(2,1)S(1)} %shard_map.103.refs_0_), channel_id=1, source_target_pairs={{0,2},{1,3},{2,0},{3,1},{4,6},{5,7},{6,4},{7,5},{8,10},{9,11},{10,... | collective-permute-start | bytes 196616 | tf_op jit(solution)/shard_map/ppermute | solution.py:27
  78.8 1.7 %collective-permute-done.14.refs_3_ = bf16[16,2048]{1,0:T(8,128)(2,1)S(1)} collective-permute-done((bf16[16,2048]{1,0:T(8,128)(2,1)S(1)}, bf16[16,2048]{1,0:T(8,128)(2,1)S(1)}, u32[]{:S(2)}, u32[]{:S(2)}) %collective-permute-start.14) | collective-permute-done | bytes 65568 | tf_op jit(solution)/shard_map/ppermute | solution.py:27
  80.5 2.5 %collective-permute-done.13.refs_2_ = bf16[16,2048]{1,0:T(8,128)(2,1)S(1)} collective-permute-done((bf16[16,2048]{1,0:T(8,128)(2,1)S(1)}, bf16[16,2048]{1,0:T(8,128)(2,1)S(1)}, u32[]{:S(2)}, u32[]{:S(2)}) %collective-permute-start.13) | collective-permute-done | bytes 65568 | tf_op jit(solution)/shard_map/ppermute | solution.py:27
  83.0 3.1 %layer.7 = (f32[16,2048]{1,0:T(8,128)S(1)}, bf16[16,2048]{1,0:T(8,128)(2,1)S(1)}, bf16[16,2048]{1,0:T(8,128)(2,1)S(1)}, bf16[16,2048]{1,0:T(8,128)(2,1)S(1)}) custom-call(bf16[16,2048]{1,0:T(8,128)(2,1)S(1)} %shard_map.103.refs_0_, bf16[16,2048]{1,0:T(8,128)(2,1)S(1)} %collective-permute-done.12.refs_1_, ...), custom_call_target="tpu_custom_call" | custom-call | flops 629145600 | bytes 9830400 | tf_op jit(solution)/shard_map/layer/pallas_call | solution.py:172
  86.0 2.4 %collective-permute-start.16 = (bf16[16,2048]{1,0:T(8,128)(2,1)S(1)}, bf16[16,2048]{1,0:T(8,128)(2,1)S(1)}, u32[]{:S(2)}, u32[]{:S(2)}) collective-permute-start(bf16[16,2048]{1,0:T(8,128)(2,1)S(1)} %get-tuple-element.54), channel_id=1, source_target_pairs={{0,6},{1,7},{2,4},{3,5},{4,2},{5,3},{6,0},{7,1},{8,14},{9,15},{10,... | collective-permute-start | bytes 196616 | tf_op jit(solution)/shard_map/ppermute | solution.py:27
  88.4 2.0 %collective-permute-start.18 = (bf16[16,2048]{1,0:T(8,128)(2,1)S(1)}, bf16[16,2048]{1,0:T(8,128)(2,1)S(1)}, u32[]{:S(2)}, u32[]{:S(2)}) collective-permute-start(bf16[16,2048]{1,0:T(8,128)(2,1)S(1)} %get-tuple-element.56), channel_id=1, source_target_pairs={{0,2},{1,3},{2,0},{3,1},{4,6},{5,7},{6,4},{7,5},{8,10},{9,11},{10,... | collective-permute-start | bytes 196616 | tf_op jit(solution)/shard_map/ppermute | solution.py:27
  90.5 1.7 %collective-permute-done.16.refs_1_ = bf16[16,2048]{1,0:T(8,128)(2,1)S(1)} collective-permute-done((bf16[16,2048]{1,0:T(8,128)(2,1)S(1)}, bf16[16,2048]{1,0:T(8,128)(2,1)S(1)}, u32[]{:S(2)}, u32[]{:S(2)}) %collective-permute-start.16) | collective-permute-done | bytes 65568 | tf_op jit(solution)/shard_map/ppermute | solution.py:27
  92.2 2.0 %collective-permute-done.17.refs_2_ = bf16[16,2048]{1,0:T(8,128)(2,1)S(1)} collective-permute-done((bf16[16,2048]{1,0:T(8,128)(2,1)S(1)}, bf16[16,2048]{1,0:T(8,128)(2,1)S(1)}, u32[]{:S(2)}, u32[]{:S(2)}) %collective-permute-start.17) | collective-permute-done | bytes 65568 | tf_op jit(solution)/shard_map/ppermute | solution.py:27
  94.9 1.8 %collective-permute-start.19 = (bf16[16,2048]{1,0:T(8,128)(2,1)S(1)}, bf16[16,2048]{1,0:T(8,128)(2,1)S(1)}, u32[]{:S(2)}, u32[]{:S(2)}) collective-permute-start(bf16[16,2048]{1,0:T(8,128)(2,1)S(1)} %shard_map.104), channel_id=1, source_target_pairs={{0,8},{1,9},{2,10},{3,11},{4,12},{5,13},{6,14},{7,15},{8,16},{9,17... | collective-permute-start | bytes 196616 | tf_op jit(solution)/shard_map/ppermute | solution.py:27
  96.7 2.7 %collective-permute-done.20.refs_1_ = bf16[16,2048]{1,0:T(8,128)(2,1)S(1)} collective-permute-done((bf16[16,2048]{1,0:T(8,128)(2,1)S(1)}, bf16[16,2048]{1,0:T(8,128)(2,1)S(1)}, u32[]{:S(2)}, u32[]{:S(2)}) %collective-permute-start.20) | collective-permute-done | bytes 65568 | tf_op jit(solution)/shard_map/ppermute | solution.py:27
  99.4 2.6 %collective-permute-start.23 = (bf16[16,2048]{1,0:T(8,128)(2,1)S(1)}, bf16[16,2048]{1,0:T(8,128)(2,1)S(1)}, u32[]{:S(2)}, u32[]{:S(2)}) collective-permute-start(bf16[16,2048]{1,0:T(8,128)(2,1)S(1)} %shard_map.105.refs_0_), channel_id=1, source_target_pairs={{0,6},{1,7},{2,4},{3,5},{4,2},{5,3},{6,0},{7,1},{8,14},{9,15},{10,... | collective-permute-start | bytes 196616 | tf_op jit(solution)/shard_map/ppermute | solution.py:27
  102.1 1.8 %collective-permute-start.21 = (bf16[16,2048]{1,0:T(8,128)(2,1)S(1)}, bf16[16,2048]{1,0:T(8,128)(2,1)S(1)}, u32[]{:S(2)}, u32[]{:S(2)}) collective-permute-start(bf16[16,2048]{1,0:T(8,128)(2,1)S(1)} %shard_map.105.refs_0_), channel_id=1, source_target_pairs={{0,2},{1,3},{2,0},{3,1},{4,6},{5,7},{6,4},{7,5},{8,10},{9,11},{10,... | collective-permute-start | bytes 196616 | tf_op jit(solution)/shard_map/ppermute | solution.py:27
  103.9 2.0 %collective-permute-done.23.refs_3_ = bf16[16,2048]{1,0:T(8,128)(2,1)S(1)} collective-permute-done((bf16[16,2048]{1,0:T(8,128)(2,1)S(1)}, bf16[16,2048]{1,0:T(8,128)(2,1)S(1)}, u32[]{:S(2)}, u32[]{:S(2)}) %collective-permute-start.23) | collective-permute-done | bytes 65568 | tf_op jit(solution)/shard_map/ppermute | solution.py:27
  105.8 2.2 %collective-permute-done.22.refs_2_ = bf16[16,2048]{1,0:T(8,128)(2,1)S(1)} collective-permute-done((bf16[16,2048]{1,0:T(8,128)(2,1)S(1)}, bf16[16,2048]{1,0:T(8,128)(2,1)S(1)}, u32[]{:S(2)}, u32[]{:S(2)}) %collective-permute-start.22) | collective-permute-done | bytes 65568 | tf_op jit(solution)/shard_map/ppermute | solution.py:27
  108.1 3.1 %layer.8 = (f32[16,2048]{1,0:T(8,128)S(1)}, bf16[16,2048]{1,0:T(8,128)(2,1)S(1)}, bf16[16,2048]{1,0:T(8,128)(2,1)S(1)}, bf16[16,2048]{1,0:T(8,128)(2,1)S(1)}) custom-call(bf16[16,2048]{1,0:T(8,128)(2,1)S(1)} %shard_map.105.refs_0_, bf16[16,2048]{1,0:T(8,128)(2,1)S(1)} %collective-permute-done.21.refs_1_, ...), custom_call_target="tpu_custom_call" | custom-call | flops 629145600 | bytes 9830400 | tf_op jit(solution)/shard_map/layer/pallas_call | solution.py:172
  111.1 2.0 %collective-permute-start.24 = (bf16[16,2048]{1,0:T(8,128)(2,1)S(1)}, bf16[16,2048]{1,0:T(8,128)(2,1)S(1)}, u32[]{:S(2)}, u32[]{:S(2)}) collective-permute-start(bf16[16,2048]{1,0:T(8,128)(2,1)S(1)} %get-tuple-element.58), channel_id=1, source_target_pairs={{0,6},{1,7},{2,4},{3,5},{4,2},{5,3},{6,0},{7,1},{8,14},{9,15},{10,... | collective-permute-start | bytes 196616 | tf_op jit(solution)/shard_map/ppermute | solution.py:27
  113.1 2.5 %collective-permute-start.26 = (bf16[16,2048]{1,0:T(8,128)(2,1)S(1)}, bf16[16,2048]{1,0:T(8,128)(2,1)S(1)}, u32[]{:S(2)}, u32[]{:S(2)}) collective-permute-start(bf16[16,2048]{1,0:T(8,128)(2,1)S(1)} %get-tuple-element.60), channel_id=1, source_target_pairs={{0,2},{1,3},{2,0},{3,1},{4,6},{5,7},{6,4},{7,5},{8,10},{9,11},{10,... | collective-permute-start | bytes 196616 | tf_op jit(solution)/shard_map/ppermute | solution.py:27
  115.6 1.8 %collective-permute-done.24.refs_1_ = bf16[16,2048]{1,0:T(8,128)(2,1)S(1)} collective-permute-done((bf16[16,2048]{1,0:T(8,128)(2,1)S(1)}, bf16[16,2048]{1,0:T(8,128)(2,1)S(1)}, u32[]{:S(2)}, u32[]{:S(2)}) %collective-permute-start.24) | collective-permute-done | bytes 65568 | tf_op jit(solution)/shard_map/ppermute | solution.py:27
  117.4 2.0 %collective-permute-done.25.refs_2_ = bf16[16,2048]{1,0:T(8,128)(2,1)S(1)} collective-permute-done((bf16[16,2048]{1,0:T(8,128)(2,1)S(1)}, bf16[16,2048]{1,0:T(8,128)(2,1)S(1)}, u32[]{:S(2)}, u32[]{:S(2)}) %collective-permute-start.25) | collective-permute-done | bytes 65568 | tf_op jit(solution)/shard_map/ppermute | solution.py:27
  119.6 2.0 %collective-permute-start.27 = (bf16[16,2048]{1,0:T(8,128)(2,1)S(1)}, bf16[16,2048]{1,0:T(8,128)(2,1)S(1)}, u32[]{:S(2)}, u32[]{:S(2)}) collective-permute-start(bf16[16,2048]{1,0:T(8,128)(2,1)S(1)} %shard_map.106), channel_id=1, source_target_pairs={{0,8},{1,9},{2,10},{3,11},{4,12},{5,13},{6,14},{7,15},{8,16},{9,17... | collective-permute-start | bytes 196616 | tf_op jit(solution)/shard_map/ppermute | solution.py:27
  121.6 2.9 %collective-permute-done.28.refs_1_ = bf16[16,2048]{1,0:T(8,128)(2,1)S(1)} collective-permute-done((bf16[16,2048]{1,0:T(8,128)(2,1)S(1)}, bf16[16,2048]{1,0:T(8,128)(2,1)S(1)}, u32[]{:S(2)}, u32[]{:S(2)}) %collective-permute-start.28) | collective-permute-done | bytes 65568 | tf_op jit(solution)/shard_map/ppermute | solution.py:27
  124.6 2.4 %collective-permute-start.31 = (bf16[16,2048]{1,0:T(8,128)(2,1)S(1)}, bf16[16,2048]{1,0:T(8,128)(2,1)S(1)}, u32[]{:S(2)}, u32[]{:S(2)}) collective-permute-start(bf16[16,2048]{1,0:T(8,128)(2,1)S(1)} %shard_map.107.refs_0_), channel_id=1, source_target_pairs={{0,6},{1,7},{2,4},{3,5},{4,2},{5,3},{6,0},{7,1},{8,14},{9,15},{10,... | collective-permute-start | bytes 196616 | tf_op jit(solution)/shard_map/ppermute | solution.py:27
  127.0 2.0 %collective-permute-start.29 = (bf16[16,2048]{1,0:T(8,128)(2,1)S(1)}, bf16[16,2048]{1,0:T(8,128)(2,1)S(1)}, u32[]{:S(2)}, u32[]{:S(2)}) collective-permute-start(bf16[16,2048]{1,0:T(8,128)(2,1)S(1)} %shard_map.107.refs_0_), channel_id=1, source_target_pairs={{0,2},{1,3},{2,0},{3,1},{4,6},{5,7},{6,4},{7,5},{8,10},{9,11},{10,... | collective-permute-start | bytes 196616 | tf_op jit(solution)/shard_map/ppermute | solution.py:27
  129.1 1.7 %collective-permute-done.31.refs_3_ = bf16[16,2048]{1,0:T(8,128)(2,1)S(1)} collective-permute-done((bf16[16,2048]{1,0:T(8,128)(2,1)S(1)}, bf16[16,2048]{1,0:T(8,128)(2,1)S(1)}, u32[]{:S(2)}, u32[]{:S(2)}) %collective-permute-start.31) | collective-permute-done | bytes 65568 | tf_op jit(solution)/shard_map/ppermute | solution.py:27
  130.7 2.3 %collective-permute-done.30.refs_2_ = bf16[16,2048]{1,0:T(8,128)(2,1)S(1)} collective-permute-done((bf16[16,2048]{1,0:T(8,128)(2,1)S(1)}, bf16[16,2048]{1,0:T(8,128)(2,1)S(1)}, u32[]{:S(2)}, u32[]{:S(2)}) %collective-permute-start.30) | collective-permute-done | bytes 65568 | tf_op jit(solution)/shard_map/ppermute | solution.py:27
  133.0 3.1 %layer.9 = (f32[16,2048]{1,0:T(8,128)S(1)}, bf16[16,2048]{1,0:T(8,128)(2,1)S(1)}, bf16[16,2048]{1,0:T(8,128)(2,1)S(1)}, bf16[16,2048]{1,0:T(8,128)(2,1)S(1)}) custom-call(bf16[16,2048]{1,0:T(8,128)(2,1)S(1)} %shard_map.107.refs_0_, bf16[16,2048]{1,0:T(8,128)(2,1)S(1)} %collective-permute-done.29.refs_1_, ...), custom_call_target="tpu_custom_call" | custom-call | flops 629145600 | bytes 9830400 | tf_op jit(solution)/shard_map/layer/pallas_call | solution.py:172
  136.1 2.0 %collective-permute-start.32 = (bf16[16,2048]{1,0:T(8,128)(2,1)S(1)}, bf16[16,2048]{1,0:T(8,128)(2,1)S(1)}, u32[]{:S(2)}, u32[]{:S(2)}) collective-permute-start(bf16[16,2048]{1,0:T(8,128)(2,1)S(1)} %get-tuple-element.62), channel_id=1, source_target_pairs={{0,6},{1,7},{2,4},{3,5},{4,2},{5,3},{6,0},{7,1},{8,14},{9,15},{10,... | collective-permute-start | bytes 196616 | tf_op jit(solution)/shard_map/ppermute | solution.py:27
  138.1 2.4 %collective-permute-start.34 = (bf16[16,2048]{1,0:T(8,128)(2,1)S(1)}, bf16[16,2048]{1,0:T(8,128)(2,1)S(1)}, u32[]{:S(2)}, u32[]{:S(2)}) collective-permute-start(bf16[16,2048]{1,0:T(8,128)(2,1)S(1)} %get-tuple-element.64), channel_id=1, source_target_pairs={{0,2},{1,3},{2,0},{3,1},{4,6},{5,7},{6,4},{7,5},{8,10},{9,11},{10,... | collective-permute-start | bytes 196616 | tf_op jit(solution)/shard_map/ppermute | solution.py:27
  140.5 1.9 %collective-permute-done.32 = bf16[16,2048]{1,0:T(8,128)(2,1)S(1)} collective-permute-done((bf16[16,2048]{1,0:T(8,128)(2,1)S(1)}, bf16[16,2048]{1,0:T(8,128)(2,1)S(1)}, u32[]{:S(2)}, u32[]{:S(2)}) %collective-permute-start.32) | collective-permute-done | bytes 65568 | tf_op jit(solution)/shard_map/ppermute | solution.py:27
  142.4 2.0 %collective-permute-done.33 = bf16[16,2048]{1,0:T(8,128)(2,1)S(1)} collective-permute-done((bf16[16,2048]{1,0:T(8,128)(2,1)S(1)}, bf16[16,2048]{1,0:T(8,128)(2,1)S(1)}, u32[]{:S(2)}, u32[]{:S(2)}) %collective-permute-start.33) | collective-permute-done | bytes 65568 | tf_op jit(solution)/shard_map/ppermute | solution.py:27
  144.8 3.6 %collective-permute-done.35 = bf16[8,2048]{1,0:T(8,128)(2,1)S(1)} collective-permute-done((bf16[8,2048]{1,0:T(8,128)(2,1)S(1)}, bf16[8,2048]{1,0:T(8,128)(2,1)S(1)}, u32[]{:S(2)}, u32[]{:S(2)}) %collective-permute-start.35) | collective-permute-done | bytes 32800 | tf_op jit(solution)/shard_map/ppermute | solution.py:27
  (52 shorter events, 14.3 us)
Async XLA Ops:
  1.1 0.8 copy-start.1
  1.9 0.7 copy-start.2
  2.6 0.7 copy-start.3
  3.5 4.9 %collective-permute-start = (bf16[8,2176]{1,0:T(8,128)(2,1)S(1)}, bf16[8,2176]{1,0:T(8,128)(2,1)S(1)}, u32[]{:S(2)}, u32[]{:S(2)}) collective-permute-start(bf16[8,2176]{1,0:T(8,128)(2,1)S(1)} %shard_map.100.first_ref), channel_id=1, source_target_pairs={{0,1},{1,0},{2,3},{3,2},{4,5},{5,4},{6,7},{7,6},{8,9},{9,8},{10,11... | collective-permute-start | bytes 104456 | tf_op jit(solution)/shard_map/ppermute | solution.py:27
  8.4 4.5 %collective-permute-start.1 = (bf16[16,2176]{1,0:T(8,128)(2,1)S(1)}, bf16[16,2176]{1,0:T(8,128)(2,1)S(1)}, u32[]{:S(2)}, u32[]{:S(2)}) collective-permute-start(bf16[16,2176]{1,0:T(8,128)(2,1)S(1)} %shard_map.101.refs_0_.refs_4_), channel_id=1, source_target_pairs={{0,2},{1,3},{2,0},{3,1},{4,6},{5,7},{6,4},{7,5},{8,10},{9,11},{10,... | collective-permute-start | bytes 208904 | tf_op jit(solution)/shard_map/ppermute | solution.py:27
  14.4 68.6 %collective-permute-start.15 = (bf16[3,160,2048]{2,1,0:T(8,128)(2,1)S(1)}, bf16[3,160,2048]{2,1,0:T(8,128)(2,1)S(1)}, u32[]{:S(2)}, u32[]{:S(2)}) collective-permute-start(bf16[3,160,2048]{2,1,0:T(8,128)(2,1)S(1)} %stack.1), channel_id=1, source_target_pairs={{0,24},{1,25},{2,26},{3,27},{4,28},{5,29},{6,30},{7,31},{8,0},{9,1... | collective-permute-start | bytes 5898248 | tf_op jit(solution)/shard_map/ppermute | solution.py:27
  14.4 29.2 %collective-permute-start.4 = (bf16[160,2048]{1,0:T(8,128)(2,1)S(1)}, bf16[160,2048]{1,0:T(8,128)(2,1)S(1)}, u32[]{:S(2)}, u32[]{:S(2)}) collective-permute-start(bf16[160,2048]{1,0:T(8,128)(2,1)S(1)} %fill.3), channel_id=1, source_target_pairs={{0,24},{1,25},{2,26},{3,27},{4,28},{5,29},{6,30},{7,31},{8,0},{9,1... | collective-permute-start | bytes 1966088 | tf_op jit(solution)/shard_map/ppermute | solution.py:27
  17.8 32.8 %collective-permute-start.5 = (bf16[160,2048]{1,0:T(8,128)(2,1)S(1)}, bf16[160,2048]{1,0:T(8,128)(2,1)S(1)}, u32[]{:S(2)}, u32[]{:S(2)}) collective-permute-start(bf16[160,2048]{1,0:T(8,128)(2,1)S(1)} %get-tuple-element.44), channel_id=1, source_target_pairs={{0,24},{1,25},{2,26},{3,27},{4,28},{5,29},{6,30},{7,31},{8,0},{9,1... | collective-permute-start | bytes 1966088 | tf_op jit(solution)/shard_map/ppermute | solution.py:27
  17.9 39.7 %collective-permute-start.6 = (bf16[160,2048]{1,0:T(8,128)(2,1)S(1)}, bf16[160,2048]{1,0:T(8,128)(2,1)S(1)}, u32[]{:S(2)}, u32[]{:S(2)}) collective-permute-start(bf16[160,2048]{1,0:T(8,128)(2,1)S(1)} %get-tuple-element.45), channel_id=1, source_target_pairs={{0,24},{1,25},{2,26},{3,27},{4,28},{5,29},{6,30},{7,31},{8,0},{9,1... | collective-permute-start | bytes 1966088 | tf_op jit(solution)/shard_map/ppermute | solution.py:27
  18.0 6.4 %collective-permute-start.3 = (bf16[16,2176]{1,0:T(8,128)(2,1)S(1)}, bf16[16,2176]{1,0:T(8,128)(2,1)S(1)}, u32[]{:S(2)}, u32[]{:S(2)}) collective-permute-start(bf16[16,2176]{1,0:T(8,128)(2,1)S(1)} %shard_map.101.refs_0_.refs_4_), channel_id=1, source_target_pairs={{0,6},{1,7},{2,4},{3,5},{4,2},{5,3},{6,0},{7,1},{8,14},{9,15},{10,... | collective-permute-start | bytes 208904 | tf_op jit(solution)/shard_map/ppermute | solution.py:27
  24.5 6.5 %collective-permute-start.2 = (bf16[16,2176]{1,0:T(8,128)(2,1)S(1)}, bf16[16,2176]{1,0:T(8,128)(2,1)S(1)}, u32[]{:S(2)}, u32[]{:S(2)}) collective-permute-start(bf16[16,2176]{1,0:T(8,128)(2,1)S(1)} %shard_map.101.refs_0_.refs_4_), channel_id=1, source_target_pairs={{0,4},{1,5},{2,6},{3,7},{4,0},{5,1},{6,2},{7,3},{8,12},{9,13},{10,... | collective-permute-start | bytes 208904 | tf_op jit(solution)/shard_map/ppermute | solution.py:27
  25.4 5.6 %copy-start = (f32[2,1,2048]{2,1,0:T(1,128)S(1)}, f32[2,1,2048]{2,1,0:T(1,128)}, u32[]{:S(2)}) copy-start(f32[2,1,2048]{2,1,0:T(1,128)} %refs_8_.9) | copy-start | bytes 49156
  58.5 6.5 %collective-permute-start.7 = (bf16[16,2048]{1,0:T(8,128)(2,1)S(1)}, bf16[16,2048]{1,0:T(8,128)(2,1)S(1)}, u32[]{:S(2)}, u32[]{:S(2)}) collective-permute-start(bf16[16,2048]{1,0:T(8,128)(2,1)S(1)} %get-tuple-element.47), channel_id=1, source_target_pairs={{0,6},{1,7},{2,4},{3,5},{4,2},{5,3},{6,0},{7,1},{8,14},{9,15},{10,... | collective-permute-start | bytes 196616 | tf_op jit(solution)/shard_map/ppermute | solution.py:27
  62.6 6.3 %collective-permute-start.8 = (bf16[16,2048]{1,0:T(8,128)(2,1)S(1)}, bf16[16,2048]{1,0:T(8,128)(2,1)S(1)}, u32[]{:S(2)}, u32[]{:S(2)}) collective-permute-start(bf16[16,2048]{1,0:T(8,128)(2,1)S(1)} %get-tuple-element.48), channel_id=1, source_target_pairs={{0,4},{1,5},{2,6},{3,7},{4,0},{5,1},{6,2},{7,3},{8,12},{9,13},{10,... | collective-permute-start | bytes 196616 | tf_op jit(solution)/shard_map/ppermute | solution.py:27
  62.6 6.3 %collective-permute-start.9 = (bf16[16,2048]{1,0:T(8,128)(2,1)S(1)}, bf16[16,2048]{1,0:T(8,128)(2,1)S(1)}, u32[]{:S(2)}, u32[]{:S(2)}) collective-permute-start(bf16[16,2048]{1,0:T(8,128)(2,1)S(1)} %get-tuple-element.49), channel_id=1, source_target_pairs={{0,2},{1,3},{2,0},{3,1},{4,6},{5,7},{6,4},{7,5},{8,10},{9,11},{10,... | collective-permute-start | bytes 196616 | tf_op jit(solution)/shard_map/ppermute | solution.py:27
  68.9 5.1 %collective-permute-start.11 = (bf16[16,2048]{1,0:T(8,128)(2,1)S(1)}, bf16[16,2048]{1,0:T(8,128)(2,1)S(1)}, u32[]{:S(2)}, u32[]{:S(2)}) collective-permute-start(bf16[16,2048]{1,0:T(8,128)(2,1)S(1)} %shard_map.102), channel_id=1, source_target_pairs={{0,9},{1,8},{2,11},{3,10},{4,13},{5,12},{6,15},{7,14},{8,17},{9,16... | collective-permute-start | bytes 196616 | tf_op jit(solution)/shard_map/ppermute | solution.py:27
  70.3 4.0 %collective-permute-start.10 = (bf16[16,2048]{1,0:T(8,128)(2,1)S(1)}, bf16[16,2048]{1,0:T(8,128)(2,1)S(1)}, u32[]{:S(2)}, u32[]{:S(2)}) collective-permute-start(bf16[16,2048]{1,0:T(8,128)(2,1)S(1)} %shard_map.102), channel_id=1, source_target_pairs={{0,8},{1,9},{2,10},{3,11},{4,12},{5,13},{6,14},{7,15},{8,16},{9,17... | collective-permute-start | bytes 196616 | tf_op jit(solution)/shard_map/ppermute | solution.py:27
  74.4 6.1 %collective-permute-start.14 = (bf16[16,2048]{1,0:T(8,128)(2,1)S(1)}, bf16[16,2048]{1,0:T(8,128)(2,1)S(1)}, u32[]{:S(2)}, u32[]{:S(2)}) collective-permute-start(bf16[16,2048]{1,0:T(8,128)(2,1)S(1)} %shard_map.103.refs_0_), channel_id=1, source_target_pairs={{0,6},{1,7},{2,4},{3,5},{4,2},{5,3},{6,0},{7,1},{8,14},{9,15},{10,... | collective-permute-start | bytes 196616 | tf_op jit(solution)/shard_map/ppermute | solution.py:27
  76.8 6.2 %collective-permute-start.13 = (bf16[16,2048]{1,0:T(8,128)(2,1)S(1)}, bf16[16,2048]{1,0:T(8,128)(2,1)S(1)}, u32[]{:S(2)}, u32[]{:S(2)}) collective-permute-start(bf16[16,2048]{1,0:T(8,128)(2,1)S(1)} %shard_map.103.refs_0_), channel_id=1, source_target_pairs={{0,4},{1,5},{2,6},{3,7},{4,0},{5,1},{6,2},{7,3},{8,12},{9,13},{10,... | collective-permute-start | bytes 196616 | tf_op jit(solution)/shard_map/ppermute | solution.py:27
  76.8 6.2 %collective-permute-start.12 = (bf16[16,2048]{1,0:T(8,128)(2,1)S(1)}, bf16[16,2048]{1,0:T(8,128)(2,1)S(1)}, u32[]{:S(2)}, u32[]{:S(2)}) collective-permute-start(bf16[16,2048]{1,0:T(8,128)(2,1)S(1)} %shard_map.103.refs_0_), channel_id=1, source_target_pairs={{0,2},{1,3},{2,0},{3,1},{4,6},{5,7},{6,4},{7,5},{8,10},{9,11},{10,... | collective-permute-start | bytes 196616 | tf_op jit(solution)/shard_map/ppermute | solution.py:27
  86.0 6.1 %collective-permute-start.16 = (bf16[16,2048]{1,0:T(8,128)(2,1)S(1)}, bf16[16,2048]{1,0:T(8,128)(2,1)S(1)}, u32[]{:S(2)}, u32[]{:S(2)}) collective-permute-start(bf16[16,2048]{1,0:T(8,128)(2,1)S(1)} %get-tuple-element.54), channel_id=1, source_target_pairs={{0,6},{1,7},{2,4},{3,5},{4,2},{5,3},{6,0},{7,1},{8,14},{9,15},{10,... | collective-permute-start | bytes 196616 | tf_op jit(solution)/shard_map/ppermute | solution.py:27
  88.4 5.7 %collective-permute-start.17 = (bf16[16,2048]{1,0:T(8,128)(2,1)S(1)}, bf16[16,2048]{1,0:T(8,128)(2,1)S(1)}, u32[]{:S(2)}, u32[]{:S(2)}) collective-permute-start(bf16[16,2048]{1,0:T(8,128)(2,1)S(1)} %get-tuple-element.55), channel_id=1, source_target_pairs={{0,4},{1,5},{2,6},{3,7},{4,0},{5,1},{6,2},{7,3},{8,12},{9,13},{10,... | collective-permute-start | bytes 196616 | tf_op jit(solution)/shard_map/ppermute | solution.py:27
  88.4 5.7 %collective-permute-start.18 = (bf16[16,2048]{1,0:T(8,128)(2,1)S(1)}, bf16[16,2048]{1,0:T(8,128)(2,1)S(1)}, u32[]{:S(2)}, u32[]{:S(2)}) collective-permute-start(bf16[16,2048]{1,0:T(8,128)(2,1)S(1)} %get-tuple-element.56), channel_id=1, source_target_pairs={{0,2},{1,3},{2,0},{3,1},{4,6},{5,7},{6,4},{7,5},{8,10},{9,11},{10,... | collective-permute-start | bytes 196616 | tf_op jit(solution)/shard_map/ppermute | solution.py:27
  94.2 5.2 %collective-permute-start.20 = (bf16[16,2048]{1,0:T(8,128)(2,1)S(1)}, bf16[16,2048]{1,0:T(8,128)(2,1)S(1)}, u32[]{:S(2)}, u32[]{:S(2)}) collective-permute-start(bf16[16,2048]{1,0:T(8,128)(2,1)S(1)} %shard_map.104), channel_id=1, source_target_pairs={{0,9},{1,8},{2,11},{3,10},{4,13},{5,12},{6,15},{7,14},{8,17},{9,16... | collective-permute-start | bytes 196616 | tf_op jit(solution)/shard_map/ppermute | solution.py:27
  94.9 4.5 %collective-permute-start.19 = (bf16[16,2048]{1,0:T(8,128)(2,1)S(1)}, bf16[16,2048]{1,0:T(8,128)(2,1)S(1)}, u32[]{:S(2)}, u32[]{:S(2)}) collective-permute-start(bf16[16,2048]{1,0:T(8,128)(2,1)S(1)} %shard_map.104), channel_id=1, source_target_pairs={{0,8},{1,9},{2,10},{3,11},{4,12},{5,13},{6,14},{7,15},{8,16},{9,17... | collective-permute-start | bytes 196616 | tf_op jit(solution)/shard_map/ppermute | solution.py:27
  99.4 6.4 %collective-permute-start.23 = (bf16[16,2048]{1,0:T(8,128)(2,1)S(1)}, bf16[16,2048]{1,0:T(8,128)(2,1)S(1)}, u32[]{:S(2)}, u32[]{:S(2)}) collective-permute-start(bf16[16,2048]{1,0:T(8,128)(2,1)S(1)} %shard_map.105.refs_0_), channel_id=1, source_target_pairs={{0,6},{1,7},{2,4},{3,5},{4,2},{5,3},{6,0},{7,1},{8,14},{9,15},{10,... | collective-permute-start | bytes 196616 | tf_op jit(solution)/shard_map/ppermute | solution.py:27
  102.0 6.0 %collective-permute-start.22 = (bf16[16,2048]{1,0:T(8,128)(2,1)S(1)}, bf16[16,2048]{1,0:T(8,128)(2,1)S(1)}, u32[]{:S(2)}, u32[]{:S(2)}) collective-permute-start(bf16[16,2048]{1,0:T(8,128)(2,1)S(1)} %shard_map.105.refs_0_), channel_id=1, source_target_pairs={{0,4},{1,5},{2,6},{3,7},{4,0},{5,1},{6,2},{7,3},{8,12},{9,13},{10,... | collective-permute-start | bytes 196616 | tf_op jit(solution)/shard_map/ppermute | solution.py:27
  102.1 6.0 %collective-permute-start.21 = (bf16[16,2048]{1,0:T(8,128)(2,1)S(1)}, bf16[16,2048]{1,0:T(8,128)(2,1)S(1)}, u32[]{:S(2)}, u32[]{:S(2)}) collective-permute-start(bf16[16,2048]{1,0:T(8,128)(2,1)S(1)} %shard_map.105.refs_0_), channel_id=1, source_target_pairs={{0,2},{1,3},{2,0},{3,1},{4,6},{5,7},{6,4},{7,5},{8,10},{9,11},{10,... | collective-permute-start | bytes 196616 | tf_op jit(solution)/shard_map/ppermute | solution.py:27
  111.1 6.2 %collective-permute-start.24 = (bf16[16,2048]{1,0:T(8,128)(2,1)S(1)}, bf16[16,2048]{1,0:T(8,128)(2,1)S(1)}, u32[]{:S(2)}, u32[]{:S(2)}) collective-permute-start(bf16[16,2048]{1,0:T(8,128)(2,1)S(1)} %get-tuple-element.58), channel_id=1, source_target_pairs={{0,6},{1,7},{2,4},{3,5},{4,2},{5,3},{6,0},{7,1},{8,14},{9,15},{10,... | collective-permute-start | bytes 196616 | tf_op jit(solution)/shard_map/ppermute | solution.py:27
  113.1 6.2 %collective-permute-start.25 = (bf16[16,2048]{1,0:T(8,128)(2,1)S(1)}, bf16[16,2048]{1,0:T(8,128)(2,1)S(1)}, u32[]{:S(2)}, u32[]{:S(2)}) collective-permute-start(bf16[16,2048]{1,0:T(8,128)(2,1)S(1)} %get-tuple-element.59), channel_id=1, source_target_pairs={{0,4},{1,5},{2,6},{3,7},{4,0},{5,1},{6,2},{7,3},{8,12},{9,13},{10,... | collective-permute-start | bytes 196616 | tf_op jit(solution)/shard_map/ppermute | solution.py:27
  113.1 6.2 %collective-permute-start.26 = (bf16[16,2048]{1,0:T(8,128)(2,1)S(1)}, bf16[16,2048]{1,0:T(8,128)(2,1)S(1)}, u32[]{:S(2)}, u32[]{:S(2)}) collective-permute-start(bf16[16,2048]{1,0:T(8,128)(2,1)S(1)} %get-tuple-element.60), channel_id=1, source_target_pairs={{0,2},{1,3},{2,0},{3,1},{4,6},{5,7},{6,4},{7,5},{8,10},{9,11},{10,... | collective-permute-start | bytes 196616 | tf_op jit(solution)/shard_map/ppermute | solution.py:27
  119.4 5.2 %collective-permute-start.28 = (bf16[16,2048]{1,0:T(8,128)(2,1)S(1)}, bf16[16,2048]{1,0:T(8,128)(2,1)S(1)}, u32[]{:S(2)}, u32[]{:S(2)}) collective-permute-start(bf16[16,2048]{1,0:T(8,128)(2,1)S(1)} %shard_map.106), channel_id=1, source_target_pairs={{0,9},{1,8},{2,11},{3,10},{4,13},{5,12},{6,15},{7,14},{8,17},{9,16... | collective-permute-start | bytes 196616 | tf_op jit(solution)/shard_map/ppermute | solution.py:27
  119.6 5.0 %collective-permute-start.27 = (bf16[16,2048]{1,0:T(8,128)(2,1)S(1)}, bf16[16,2048]{1,0:T(8,128)(2,1)S(1)}, u32[]{:S(2)}, u32[]{:S(2)}) collective-permute-start(bf16[16,2048]{1,0:T(8,128)(2,1)S(1)} %shard_map.106), channel_id=1, source_target_pairs={{0,8},{1,9},{2,10},{3,11},{4,12},{5,13},{6,14},{7,15},{8,16},{9,17... | collective-permute-start | bytes 196616 | tf_op jit(solution)/shard_map/ppermute | solution.py:27
  124.6 6.1 %collective-permute-start.31 = (bf16[16,2048]{1,0:T(8,128)(2,1)S(1)}, bf16[16,2048]{1,0:T(8,128)(2,1)S(1)}, u32[]{:S(2)}, u32[]{:S(2)}) collective-permute-start(bf16[16,2048]{1,0:T(8,128)(2,1)S(1)} %shard_map.107.refs_0_), channel_id=1, source_target_pairs={{0,6},{1,7},{2,4},{3,5},{4,2},{5,3},{6,0},{7,1},{8,14},{9,15},{10,... | collective-permute-start | bytes 196616 | tf_op jit(solution)/shard_map/ppermute | solution.py:27
  127.0 6.0 %collective-permute-start.30 = (bf16[16,2048]{1,0:T(8,128)(2,1)S(1)}, bf16[16,2048]{1,0:T(8,128)(2,1)S(1)}, u32[]{:S(2)}, u32[]{:S(2)}) collective-permute-start(bf16[16,2048]{1,0:T(8,128)(2,1)S(1)} %shard_map.107.refs_0_), channel_id=1, source_target_pairs={{0,4},{1,5},{2,6},{3,7},{4,0},{5,1},{6,2},{7,3},{8,12},{9,13},{10,... | collective-permute-start | bytes 196616 | tf_op jit(solution)/shard_map/ppermute | solution.py:27
  127.0 6.0 %collective-permute-start.29 = (bf16[16,2048]{1,0:T(8,128)(2,1)S(1)}, bf16[16,2048]{1,0:T(8,128)(2,1)S(1)}, u32[]{:S(2)}, u32[]{:S(2)}) collective-permute-start(bf16[16,2048]{1,0:T(8,128)(2,1)S(1)} %shard_map.107.refs_0_), channel_id=1, source_target_pairs={{0,2},{1,3},{2,0},{3,1},{4,6},{5,7},{6,4},{7,5},{8,10},{9,11},{10,... | collective-permute-start | bytes 196616 | tf_op jit(solution)/shard_map/ppermute | solution.py:27
  136.1 6.3 %collective-permute-start.32 = (bf16[16,2048]{1,0:T(8,128)(2,1)S(1)}, bf16[16,2048]{1,0:T(8,128)(2,1)S(1)}, u32[]{:S(2)}, u32[]{:S(2)}) collective-permute-start(bf16[16,2048]{1,0:T(8,128)(2,1)S(1)} %get-tuple-element.62), channel_id=1, source_target_pairs={{0,6},{1,7},{2,4},{3,5},{4,2},{5,3},{6,0},{7,1},{8,14},{9,15},{10,... | collective-permute-start | bytes 196616 | tf_op jit(solution)/shard_map/ppermute | solution.py:27
  138.1 6.3 %collective-permute-start.33 = (bf16[16,2048]{1,0:T(8,128)(2,1)S(1)}, bf16[16,2048]{1,0:T(8,128)(2,1)S(1)}, u32[]{:S(2)}, u32[]{:S(2)}) collective-permute-start(bf16[16,2048]{1,0:T(8,128)(2,1)S(1)} %get-tuple-element.63), channel_id=1, source_target_pairs={{0,4},{1,5},{2,6},{3,7},{4,0},{5,1},{6,2},{7,3},{8,12},{9,13},{10,... | collective-permute-start | bytes 196616 | tf_op jit(solution)/shard_map/ppermute | solution.py:27
  138.1 6.3 %collective-permute-start.34 = (bf16[16,2048]{1,0:T(8,128)(2,1)S(1)}, bf16[16,2048]{1,0:T(8,128)(2,1)S(1)}, u32[]{:S(2)}, u32[]{:S(2)}) collective-permute-start(bf16[16,2048]{1,0:T(8,128)(2,1)S(1)} %get-tuple-element.64), channel_id=1, source_target_pairs={{0,2},{1,3},{2,0},{3,1},{4,6},{5,7},{6,4},{7,5},{8,10},{9,11},{10,... | collective-permute-start | bytes 196616 | tf_op jit(solution)/shard_map/ppermute | solution.py:27
  144.4 4.0 %collective-permute-start.35 = (bf16[8,2048]{1,0:T(8,128)(2,1)S(1)}, bf16[8,2048]{1,0:T(8,128)(2,1)S(1)}, u32[]{:S(2)}, u32[]{:S(2)}) collective-permute-start(bf16[8,2048]{1,0:T(8,128)(2,1)S(1)} %slice.17), channel_id=1, source_target_pairs={{0,1},{1,0},{2,3},{3,2},{4,5},{5,4},{6,7},{7,6},{8,9},{9,8},{10,11... | collective-permute-start | bytes 98312 | tf_op jit(solution)/shard_map/ppermute | solution.py:27

commit v5 on v4

--- a/solution.py
+++ b/solution.py
@@ -93,21 +93,29 @@
     out_ref[...] = jnp.concatenate([first_ref[...], second_ref[...]], axis=0)
 
 
-def served(normed, gate, up, down):
-    contract = (((1,), (1,)), ((), ()))
+def served(normed, gate, up, down, turned):
+    contract = (((1,), (0 if turned else 1,)), ((), ()))
     gate_pre = lax.dot_general(normed, gate, contract, preferred_element_type=jnp.float32)
     up_pre = lax.dot_general(normed, up, contract, preferred_element_type=jnp.float32)
     hidden = (gate_pre / (1.0 + jnp.exp(-gate_pre)) * up_pre).astype(jnp.bfloat16)
     return jnp.dot(hidden, down, preferred_element_type=jnp.float32)
 
 
-def layer_kernel(*refs, tick_idx, blocks, spare_counts, tok_dev, width, carried, ends):
+def either(second, bodies):
+    if len(bodies) == 1:
+        bodies[0]()
+    elif bodies:
+        pl.when(jnp.logical_not(second))(bodies[0])
+        pl.when(second)(bodies[1])
+
+
+def layer_kernel(*refs, tick_idx, blocks, slot_count, spare_counts, tok_dev, width, carried, ends):
     x_refs, first_refs, refs = refs[:blocks], refs[blocks:2 * blocks], refs[2 * blocks:]
     gain_ref, refs = refs[0], refs[1:]
     if carried:
         carried_ref, refs = refs[0], refs[1:]
     else:
-        (gate_ref, up_ref, down_ref), refs = refs[:3], refs[3:]
+        slots, refs = [refs[3 * i:3 * i + 3] for i in range(slot_count)], refs[3 * slot_count:]
     spare_refs = []
     for count in spare_counts:
         spare_refs.append(refs[:count] if count > 1 else [refs[0].at[i] for i in range(refs[0].shape[0])])
@@ -130,18 +138,19 @@
     if carried:
         total_ref[...] = carried_ref[...]
     else:
-        share = column(tick_idx * (EXPERTS + 1) + expert)
-        total_ref[...] = share * served(normed, gate_ref[group], up_ref[group], down_ref[group])
-    for at, spare_ref in enumerate(spare_refs):
-
-        def add(spare_ref=spare_ref):
-            spill = column(tick_idx * (EXPERTS + 1) + EXPERTS)
-            total_ref[...] += spill * served(normed, *[ref[...] for ref in spare_ref])
-
-        if len(spare_refs) == 1:
-            add()
-        else:
-            pl.when(group == at)(add)
+
+        def put(slot):
+            share = column(tick_idx * (EXPERTS + 1) + expert)
+            total_ref[...] = share * served(normed, *[ref[...] for ref in slot], True)
+
+        home = group_of(lax.axis_index("segment"), 0, segments)
+        either(group != home, [functools.partial(put, slot) for slot in slots])
+
+    def add(spare_ref):
+        spill = column(tick_idx * (EXPERTS + 1) + EXPERTS)
+        total_ref[...] += spill * served(normed, *[ref[...] for ref in spare_ref], False)
+
+    either(group == 1, [functools.partial(add, spare_ref) for spare_ref in spare_refs])
     if not ends:
         return
     out_refs = refs[:blocks]
@@ -162,16 +171,16 @@
     per = 2 * tok_dev
     rows = per * blocks
     values = [*x_blocks, *first_blocks, gain]
-    values += [carried] if carried is not None else resident(weights)
+    values += [carried] if carried is not None else resident([one for slot in weights for one in slot])
     for spare in spares:
         values += resident(spare)
-    hidden = (0 if carried is not None else weights[0].shape[1]) + (spares[0][0].shape[0] if spares else 0)
+    hidden = (0 if carried is not None else weights[0][2].shape[0]) + (spares[0][0].shape[0] if spares else 0)
     whole = jax.ShapeDtypeStruct((rows, width), jnp.float32)
     parts = [jax.ShapeDtypeStruct((per, width), jnp.float32)]
     parts += [jax.ShapeDtypeStruct((per, width), jnp.bfloat16)] * (blocks - 1)
     return pl.pallas_call(
         functools.partial(
-            layer_kernel, tick_idx=tick_idx, blocks=blocks, spare_counts=[len(spare) for spare in spares],
+            layer_kernel, tick_idx=tick_idx, blocks=blocks, slot_count=len(weights), spare_counts=[len(spare) for spare in spares],
             tok_dev=tok_dev, width=width, carried=carried is not None, ends=ends,
         ),
         out_shape=parts if ends else whole,
@@ -226,6 +235,57 @@
     )(*[pltpu.with_memory_space_constraint(value, pltpu.HBM) for value in values])
 
 
+def load_kernel(*refs, turned, other):
+    count = len(turned)
+    ins, outs, (held, sems, straight) = refs[:count], refs[count:2 * count], refs[2 * count:]
+    group = group_of(lax.axis_index("segment"), 0, lax.axis_size("segment"))
+    group = 1 - group if other else group
+    depth, block = held.shape[:2]
+    work = [
+        (ins[i], outs[i], low) for i in range(count) if turned[i] for low in range(0, ins[i].shape[1], block)
+    ]
+
+    def copy_of(at):
+        source, _, low = work[at]
+        return pltpu.make_async_copy(source.at[group, pl.ds(low, block), :], held.at[at % depth], sems.at[at % depth])
+
+    for at in range(min(depth - 1, len(work))):
+        copy_of(at).start()
+    direct = [
+        pltpu.make_async_copy(ins[i].at[group], outs[i], straight.at[i]) for i in range(count) if not turned[i]
+    ]
+    for copy in direct:
+        copy.start()
+    for at, (_, out, low) in enumerate(work):
+        if at + depth - 1 < len(work):
+            copy_of(at + depth - 1).start()
+        copy_of(at).wait()
+        out[:, low:low + block] = held[at % depth].T
+    for copy in direct:
+        copy.wait()
+
+
+def loaded(values, turned, other):
+    hidden, width = values[0].shape[1:]
+    block = LANES if hidden % LANES == 0 else hidden
+    return pl.pallas_call(
+        functools.partial(load_kernel, turned=turned, other=other),
+        out_shape=[
+            pltpu.VMEM((width, hidden) if flip else (hidden, width), value.dtype)
+            for value, flip in zip(values, turned)
+        ],
+        in_specs=[pl.BlockSpec(memory_space=pltpu.HBM)] * len(values),
+        out_specs=[WHOLE] * len(values),
+        scratch_shapes=[
+            pltpu.VMEM((4, block, width), values[0].dtype),
+            pltpu.SemaphoreType.DMA((4,)),
+            pltpu.SemaphoreType.DMA((len(values),)),
+        ],
+        compiler_params=pltpu.CompilerParams(vmem_limit_bytes=6 * 1024 * 1024),
+        name="load",
+    )(*[pltpu.with_memory_space_constraint(value, pltpu.HBM) for value in values])
+
+
 def stack_kernel(*refs, group):
     ins, out, sems = refs[:-2], refs[-2], refs[-1]
     copies = [pltpu.make_async_copy(one.at[group], out.at[i], sems.at[i]) for i, one in enumerate(ins)]
@@ -289,10 +349,10 @@
     other = moved(own, 1, 0)
     pair = small(join_kernel, jax.ShapeDtypeStruct((2 * tok_dev, shape[1]), state.dtype), own, other)
     arrived = spread(pair)
-    weights = filled(weights)
+    slots = [loaded(weights, (True, True, False), False)]
     late = stacked(lax.optimization_barrier((*spare_all, arrived[1]))[:3], 1)
     before = run_layer(
-        arrived, arrived, norm_gain, weights, [], tick_idx=0, tok_dev=tok_dev, ends=False
+        arrived, arrived, norm_gain, slots, [], tick_idx=0, tok_dev=tok_dev, ends=False
     )
     late = moved(late, 0, -1)
     spares.append([late])
@@ -302,10 +362,13 @@
         used = sorted(groups_at(tick_idx, segments))
         assert used in ([0], [0, 1])
         parts = run_layer(
-            x_blocks, arrived, norm_gain, weights, spares[:len(used)], tick_idx=tick_idx, tok_dev=tok_dev,
+            x_blocks, arrived, norm_gain, slots, spares[:len(used)], tick_idx=tick_idx, tok_dev=tok_dev,
             carried=before if tick_idx == 0 else None,
         )
         got = [moved(parts[j], 2 * j, 0) for j in widest_first(outer)]
+        if tick_idx == 0:
+            tied = lax.optimization_barrier((*weights, parts[0]))[:3]
+            gate = loaded(tied[:1], (True,), True)
         if tick_idx + 1 == TICKS:
             total = added([parts[0]] + got)
             other = moved(total[tok_dev:].astype(jnp.bfloat16), 1, 0)
@@ -313,6 +376,9 @@
         total = summed([parts[0]] + got)
         across = moved(total, 1, 1)
         along = moved(total, 0, 1)
+        if tick_idx == 0:
+            tied = lax.optimization_barrier((*weights, total))[:3]
+            slots.append(gate + loaded(tied[1:], (True, False), True))
         x_blocks = spread(summed([along, across], swap=True))
 
 

time: 149 us -> 149 us (level)
  Pallas kernels: 22.2 us -> 24.3 us
  waiting for transfers between devices: 72.1 us -> 70.2 us
    pallas_call x0 -> x3, Pallas kernels: none -> 9.8 us  [loaded(): pl.pallas_call(functools.partial(load_kernel, turned=turned, other=other)...]
    pallas_call x3 -> x2, Pallas kernels: 7.97 us -> 2.4 us  [filled(): pl.pallas_call(functools.partial(fill_kernel, group=group), out_shape=[pl...]
    pallas_call x5, Pallas kernels: 12.3 us -> 10.2 us  [run_layer(): pl.pallas_call(functools.partial(layer_kernel, tick_idx=tick_idx, blocks=...]
    ppermute x36, waiting for transfers between devices: 72.1 us -> 70.2 us  [moved(): return lax.ppermute(value, BOTH, pairs)]
  transfers between devices with their start and end apart: 36 -> 36, of which waited for: 25 -> 23; matrix products, arithmetic and copies ran while one was open for 0% -> 0% of each run, Pallas kernels for 7% -> 9%
where the time goes in v5:
time: 149 us; the launch traced here: 148 us
  waiting for transfers between devices  70.2 us (47%)
  starting transfers between devices  50.8 us (34%)
  Pallas kernels  24.3 us (16%)
  local copies, waits for them, and re-layouts  2.14 us (1%)
    ppermute x36, waiting for transfers between devices, moved(): return lax.ppermute(value, BOTH, pairs)  70.2 us
    ppermute x36, starting transfers between devices, moved(): return lax.ppermute(value, BOTH, pairs)  50.8 us
    pallas_call x5, Pallas kernels, run_layer(): pl.pallas_call(functools.partial(layer_kernel, tick_idx=tick_idx, blocks=...  10.2 us
    pallas_call x3, Pallas kernels, loaded(): pl.pallas_call(functools.partial(load_kernel, turned=turned, other=other)...  9.8 us
  transfers between devices with their start and end apart: 36, of which 23 were waited for; matrix products, arithmetic and copies ran while one was open for 0% of the time, Pallas kernels for 9%

profile of v5, /device:TPU:0, one launch (start us, length us, event | category | flops | bytes accessed | tf_op | source)
XLA Modules:
  0.0 148.3 jit_solution(9976069294758408157)
XLA Ops:
  3.5 3.0 %collective-permute-start = (bf16[8,2176]{1,0:T(8,128)(2,1)S(1)}, bf16[8,2176]{1,0:T(8,128)(2,1)S(1)}, u32[]{:S(2)}, u32[]{:S(2)}) collective-permute-start(bf16[8,2176]{1,0:T(8,128)(2,1)S(1)} %shard_map.100.first_ref), channel_id=1, source_target_pairs={{0,1},{1,0},{2,3},{3,2},{4,5},{5,4},{6,7},{7,6},{8,9},{9,8},{10,11... | collective-permute-start | bytes 104456 | tf_op jit(solution)/shard_map/ppermute | solution.py:27
  6.5 1.9 %collective-permute-done.second_ref = bf16[8,2176]{1,0:T(8,128)(2,1)S(1)} collective-permute-done((bf16[8,2176]{1,0:T(8,128)(2,1)S(1)}, bf16[8,2176]{1,0:T(8,128)(2,1)S(1)}, u32[]{:S(2)}, u32[]{:S(2)}) %collective-permute-start) | collective-permute-done | bytes 34848 | tf_op jit(solution)/shard_map/ppermute | solution.py:27
  8.4 2.2 %collective-permute-start.1 = (bf16[16,2176]{1,0:T(8,128)(2,1)S(1)}, bf16[16,2176]{1,0:T(8,128)(2,1)S(1)}, u32[]{:S(2)}, u32[]{:S(2)}) collective-permute-start(bf16[16,2176]{1,0:T(8,128)(2,1)S(1)} %shard_map.101.refs_0_.refs_4_), channel_id=1, source_target_pairs={{0,2},{1,3},{2,0},{3,1},{4,6},{5,7},{6,4},{7,5},{8,10},{9,11},{10,... | collective-permute-start | bytes 208904 | tf_op jit(solution)/shard_map/ppermute | solution.py:27
  10.6 2.3 %collective-permute-done.1.refs_1_.refs_5_ = bf16[16,2176]{1,0:T(8,128)(2,1)S(1)} collective-permute-done((bf16[16,2176]{1,0:T(8,128)(2,1)S(1)}, bf16[16,2176]{1,0:T(8,128)(2,1)S(1)}, u32[]{:S(2)}, u32[]{:S(2)}) %collective-permute-start.1) | collective-permute-done | bytes 69664 | tf_op jit(solution)/shard_map/ppermute | solution.py:27
  12.9 1.5 %stack.1 = bf16[3,160,2048]{2,1,0:T(8,128)(2,1)S(1)} custom-call(bf16[2,160,2048]{2,1,0:T(8,128)(2,1)} %bitcast.29, bf16[2,160,2048]{2,1,0:T(8,128)(2,1)} %bitcast.24, bf16[2,160,2048]{2,1,0:T(8,128)(2,1)} %bitcast.26), custom_call_target="tpu_custom_call" | custom-call | tf_op jit(solution)/shard_map/stack/pallas_call | solution.py:300
  14.4 2.1 %collective-permute-start.4 = (bf16[160,2048]{1,0:T(8,128)(2,1)S(1)}, bf16[160,2048]{1,0:T(8,128)(2,1)S(1)}, u32[]{:S(2)}, u32[]{:S(2)}) collective-permute-start(bf16[160,2048]{1,0:T(8,128)(2,1)S(1)} %fill.2), channel_id=1, source_target_pairs={{0,24},{1,25},{2,26},{3,27},{4,28},{5,29},{6,30},{7,31},{8,0},{9,1... | collective-permute-start | bytes 1966088 | tf_op jit(solution)/shard_map/ppermute | solution.py:27
  18.0 4.0 %collective-permute-start.3 = (bf16[16,2176]{1,0:T(8,128)(2,1)S(1)}, bf16[16,2176]{1,0:T(8,128)(2,1)S(1)}, u32[]{:S(2)}, u32[]{:S(2)}) collective-permute-start(bf16[16,2176]{1,0:T(8,128)(2,1)S(1)} %shard_map.101.refs_0_.refs_4_), channel_id=1, source_target_pairs={{0,6},{1,7},{2,4},{3,5},{4,2},{5,3},{6,0},{7,1},{8,14},{9,15},{10,... | collective-permute-start | bytes 208904 | tf_op jit(solution)/shard_map/ppermute | solution.py:27
  22.1 2.4 %collective-permute-done.3.refs_3_.refs_7_ = bf16[16,2176]{1,0:T(8,128)(2,1)S(1)} collective-permute-done((bf16[16,2176]{1,0:T(8,128)(2,1)S(1)}, bf16[16,2176]{1,0:T(8,128)(2,1)S(1)}, u32[]{:S(2)}, u32[]{:S(2)}) %collective-permute-start.3) | collective-permute-done | bytes 69664 | tf_op jit(solution)/shard_map/ppermute | solution.py:27
  25.4 4.4 %load.3 = (bf16[2048,640]{1,0:T(8,128)(2,1)S(1)}, bf16[2048,640]{1,0:T(8,128)(2,1)S(1)}, bf16[640,2048]{1,0:T(8,128)(2,1)S(1)}) custom-call(bf16[2,640,2048]{2,1,0:T(8,128)(2,1)} %bitcast.22, bf16[2,640,2048]{2,1,0:T(8,128)(2,1)} %bitcast.18, bf16[2,640,2048]{2,1,0:T(8,128)(2,1)} %bitcast.20), custom_call_target="tpu_custom_call" | custom-call | tf_op jit(solution)/shard_map/load/pallas_call | solution.py:271
  29.8 1.6 %layer.5.refs_9_ = f32[64,2048]{1,0:T(8,128)S(1)} custom-call(bf16[16,2176]{1,0:T(8,128)(2,1)S(1)} %shard_map.101.refs_0_.refs_4_, bf16[16,2176]{1,0:T(8,128)(2,1)S(1)} %collective-permute-done.1.refs_1_.refs_5_, bf16[16,2176]{1,0:T(8,128)(2,1)S(1)} %collective-permute-done.2.refs_2_.refs_6_, bf16[16,2176]{1,0:T(8,128)(2,1)S(1)} %collective-permute-done.3.refs_3_.refs_7_, ...), custom_call_target="tpu_custom_call" | custom-call | flops 503316480 | bytes 7864320 | tf_op jit(solution)/shard_map/layer/pallas_call | solution.py:181
  31.4 12.2 %collective-permute-done.4.refs_10_.refs_15_ = bf16[160,2048]{1,0:T(8,128)(2,1)S(1)} collective-permute-done((bf16[160,2048]{1,0:T(8,128)(2,1)S(1)}, bf16[160,2048]{1,0:T(8,128)(2,1)S(1)}, u32[]{:S(2)}, u32[]{:S(2)}) %collective-permute-start.4) | collective-permute-done | bytes 655392 | tf_op jit(solution)/shard_map/ppermute | solution.py:27
  43.6 7.0 %collective-permute-done.5.refs_11_.refs_16_ = bf16[160,2048]{1,0:T(8,128)(2,1)S(1)} collective-permute-done((bf16[160,2048]{1,0:T(8,128)(2,1)S(1)}, bf16[160,2048]{1,0:T(8,128)(2,1)S(1)}, u32[]{:S(2)}, u32[]{:S(2)}) %collective-permute-start.5) | collective-permute-done | bytes 655392 | tf_op jit(solution)/shard_map/ppermute | solution.py:27
  50.6 7.0 %collective-permute-done.6.refs_12_.refs_17_ = bf16[160,2048]{1,0:T(8,128)(2,1)S(1)} collective-permute-done((bf16[160,2048]{1,0:T(8,128)(2,1)S(1)}, bf16[160,2048]{1,0:T(8,128)(2,1)S(1)}, u32[]{:S(2)}, u32[]{:S(2)}) %collective-permute-start.6) | collective-permute-done | bytes 655392 | tf_op jit(solution)/shard_map/ppermute | solution.py:27
  58.5 4.1 %collective-permute-start.7 = (bf16[16,2048]{1,0:T(8,128)(2,1)S(1)}, bf16[16,2048]{1,0:T(8,128)(2,1)S(1)}, u32[]{:S(2)}, u32[]{:S(2)}) collective-permute-start(bf16[16,2048]{1,0:T(8,128)(2,1)S(1)} %get-tuple-element.52), channel_id=1, source_target_pairs={{0,6},{1,7},{2,4},{3,5},{4,2},{5,3},{6,0},{7,1},{8,14},{9,15},{10,... | collective-permute-start | bytes 196616 | tf_op jit(solution)/shard_map/ppermute | solution.py:27
  63.3 1.7 %collective-permute-done.7.refs_1_ = bf16[16,2048]{1,0:T(8,128)(2,1)S(1)} collective-permute-done((bf16[16,2048]{1,0:T(8,128)(2,1)S(1)}, bf16[16,2048]{1,0:T(8,128)(2,1)S(1)}, u32[]{:S(2)}, u32[]{:S(2)}) %collective-permute-start.7) | collective-permute-done | bytes 65568 | tf_op jit(solution)/shard_map/ppermute | solution.py:27
  65.0 3.9 %collective-permute-done.8.refs_2_ = bf16[16,2048]{1,0:T(8,128)(2,1)S(1)} collective-permute-done((bf16[16,2048]{1,0:T(8,128)(2,1)S(1)}, bf16[16,2048]{1,0:T(8,128)(2,1)S(1)}, u32[]{:S(2)}, u32[]{:S(2)}) %collective-permute-start.8) | collective-permute-done | bytes 65568 | tf_op jit(solution)/shard_map/ppermute | solution.py:27
  68.9 1.4 collective-permute-start.11
  71.7 2.3 %collective-permute-done.11.refs_1_ = bf16[16,2048]{1,0:T(8,128)(2,1)S(1)} collective-permute-done((bf16[16,2048]{1,0:T(8,128)(2,1)S(1)}, bf16[16,2048]{1,0:T(8,128)(2,1)S(1)}, u32[]{:S(2)}, u32[]{:S(2)}) %collective-permute-start.11) | collective-permute-done | bytes 65568 | tf_op jit(solution)/shard_map/ppermute | solution.py:27
  74.3 2.4 %collective-permute-start.14 = (bf16[16,2048]{1,0:T(8,128)(2,1)S(1)}, bf16[16,2048]{1,0:T(8,128)(2,1)S(1)}, u32[]{:S(2)}, u32[]{:S(2)}) collective-permute-start(bf16[16,2048]{1,0:T(8,128)(2,1)S(1)} %shard_map.103.refs_0_), channel_id=1, source_target_pairs={{0,6},{1,7},{2,4},{3,5},{4,2},{5,3},{6,0},{7,1},{8,14},{9,15},{10,... | collective-permute-start | bytes 196616 | tf_op jit(solution)/shard_map/ppermute | solution.py:27
  76.8 2.0 %collective-permute-start.12 = (bf16[16,2048]{1,0:T(8,128)(2,1)S(1)}, bf16[16,2048]{1,0:T(8,128)(2,1)S(1)}, u32[]{:S(2)}, u32[]{:S(2)}) collective-permute-start(bf16[16,2048]{1,0:T(8,128)(2,1)S(1)} %shard_map.103.refs_0_), channel_id=1, source_target_pairs={{0,2},{1,3},{2,0},{3,1},{4,6},{5,7},{6,4},{7,5},{8,10},{9,11},{10,... | collective-permute-start | bytes 196616 | tf_op jit(solution)/shard_map/ppermute | solution.py:27
  78.8 2.5 %load.4.refs_12_ = bf16[2048,640]{1,0:T(8,128)(2,1)S(1)} custom-call(bf16[2,640,2048]{2,1,0:T(8,128)(2,1)} %bitcast.23), custom_call_target="tpu_custom_call" | custom-call | tf_op jit(solution)/shard_map/load/pallas_call | solution.py:271
  81.3 2.9 %load.5 = (bf16[2048,640]{1,0:T(8,128)(2,1)S(1)}, bf16[640,2048]{1,0:T(8,128)(2,1)S(1)}) custom-call(bf16[2,640,2048]{2,1,0:T(8,128)(2,1)} %bitcast.19, bf16[2,640,2048]{2,1,0:T(8,128)(2,1)} %bitcast.21), custom_call_target="tpu_custom_call" | custom-call | tf_op jit(solution)/shard_map/load/pallas_call | solution.py:271
  84.3 2.5 %layer.7 = (f32[16,2048]{1,0:T(8,128)S(1)}, bf16[16,2048]{1,0:T(8,128)(2,1)S(1)}, bf16[16,2048]{1,0:T(8,128)(2,1)S(1)}, bf16[16,2048]{1,0:T(8,128)(2,1)S(1)}) custom-call(bf16[16,2048]{1,0:T(8,128)(2,1)S(1)} %shard_map.103.refs_0_, bf16[16,2048]{1,0:T(8,128)(2,1)S(1)} %collective-permute-done.12.refs_1_, ...), custom_call_target="tpu_custom_call" | custom-call | flops 629145600 | bytes 9830400 | tf_op jit(solution)/shard_map/layer/pallas_call | solution.py:181
  86.8 2.4 %collective-permute-start.16 = (bf16[16,2048]{1,0:T(8,128)(2,1)S(1)}, bf16[16,2048]{1,0:T(8,128)(2,1)S(1)}, u32[]{:S(2)}, u32[]{:S(2)}) collective-permute-start(bf16[16,2048]{1,0:T(8,128)(2,1)S(1)} %get-tuple-element.64), channel_id=1, source_target_pairs={{0,6},{1,7},{2,4},{3,5},{4,2},{5,3},{6,0},{7,1},{8,14},{9,15},{10,... | collective-permute-start | bytes 196616 | tf_op jit(solution)/shard_map/ppermute | solution.py:27
  89.3 2.0 %collective-permute-start.18 = (bf16[16,2048]{1,0:T(8,128)(2,1)S(1)}, bf16[16,2048]{1,0:T(8,128)(2,1)S(1)}, u32[]{:S(2)}, u32[]{:S(2)}) collective-permute-start(bf16[16,2048]{1,0:T(8,128)(2,1)S(1)} %get-tuple-element.66), channel_id=1, source_target_pairs={{0,2},{1,3},{2,0},{3,1},{4,6},{5,7},{6,4},{7,5},{8,10},{9,11},{10,... | collective-permute-start | bytes 196616 | tf_op jit(solution)/shard_map/ppermute | solution.py:27
  91.3 2.5 %collective-permute-done.16.refs_1_ = bf16[16,2048]{1,0:T(8,128)(2,1)S(1)} collective-permute-done((bf16[16,2048]{1,0:T(8,128)(2,1)S(1)}, bf16[16,2048]{1,0:T(8,128)(2,1)S(1)}, u32[]{:S(2)}, u32[]{:S(2)}) %collective-permute-start.16) | collective-permute-done | bytes 65568 | tf_op jit(solution)/shard_map/ppermute | solution.py:27
  95.1 2.0 %collective-permute-start.19 = (bf16[16,2048]{1,0:T(8,128)(2,1)S(1)}, bf16[16,2048]{1,0:T(8,128)(2,1)S(1)}, u32[]{:S(2)}, u32[]{:S(2)}) collective-permute-start(bf16[16,2048]{1,0:T(8,128)(2,1)S(1)} %shard_map.104), channel_id=1, source_target_pairs={{0,8},{1,9},{2,10},{3,11},{4,12},{5,13},{6,14},{7,15},{8,16},{9,17... | collective-permute-start | bytes 196616 | tf_op jit(solution)/shard_map/ppermute | solution.py:27
  97.1 2.9 %collective-permute-done.20.refs_1_ = bf16[16,2048]{1,0:T(8,128)(2,1)S(1)} collective-permute-done((bf16[16,2048]{1,0:T(8,128)(2,1)S(1)}, bf16[16,2048]{1,0:T(8,128)(2,1)S(1)}, u32[]{:S(2)}, u32[]{:S(2)}) %collective-permute-start.20) | collective-permute-done | bytes 65568 | tf_op jit(solution)/shard_map/ppermute | solution.py:27
  100.1 2.2 %collective-permute-start.23 = (bf16[16,2048]{1,0:T(8,128)(2,1)S(1)}, bf16[16,2048]{1,0:T(8,128)(2,1)S(1)}, u32[]{:S(2)}, u32[]{:S(2)}) collective-permute-start(bf16[16,2048]{1,0:T(8,128)(2,1)S(1)} %shard_map.105.refs_0_), channel_id=1, source_target_pairs={{0,6},{1,7},{2,4},{3,5},{4,2},{5,3},{6,0},{7,1},{8,14},{9,15},{10,... | collective-permute-start | bytes 196616 | tf_op jit(solution)/shard_map/ppermute | solution.py:27
  102.3 2.2 %collective-permute-start.21 = (bf16[16,2048]{1,0:T(8,128)(2,1)S(1)}, bf16[16,2048]{1,0:T(8,128)(2,1)S(1)}, u32[]{:S(2)}, u32[]{:S(2)}) collective-permute-start(bf16[16,2048]{1,0:T(8,128)(2,1)S(1)} %shard_map.105.refs_0_), channel_id=1, source_target_pairs={{0,2},{1,3},{2,0},{3,1},{4,6},{5,7},{6,4},{7,5},{8,10},{9,11},{10,... | collective-permute-start | bytes 196616 | tf_op jit(solution)/shard_map/ppermute | solution.py:27
  104.6 2.1 %collective-permute-done.23.refs_3_ = bf16[16,2048]{1,0:T(8,128)(2,1)S(1)} collective-permute-done((bf16[16,2048]{1,0:T(8,128)(2,1)S(1)}, bf16[16,2048]{1,0:T(8,128)(2,1)S(1)}, u32[]{:S(2)}, u32[]{:S(2)}) %collective-permute-start.23) | collective-permute-done | bytes 65568 | tf_op jit(solution)/shard_map/ppermute | solution.py:27
  106.7 1.8 %collective-permute-done.22.refs_2_ = bf16[16,2048]{1,0:T(8,128)(2,1)S(1)} collective-permute-done((bf16[16,2048]{1,0:T(8,128)(2,1)S(1)}, bf16[16,2048]{1,0:T(8,128)(2,1)S(1)}, u32[]{:S(2)}, u32[]{:S(2)}) %collective-permute-start.22) | collective-permute-done | bytes 65568 | tf_op jit(solution)/shard_map/ppermute | solution.py:27
  108.4 2.7 %layer.8 = (f32[16,2048]{1,0:T(8,128)S(1)}, bf16[16,2048]{1,0:T(8,128)(2,1)S(1)}, bf16[16,2048]{1,0:T(8,128)(2,1)S(1)}, bf16[16,2048]{1,0:T(8,128)(2,1)S(1)}) custom-call(bf16[16,2048]{1,0:T(8,128)(2,1)S(1)} %shard_map.105.refs_0_, bf16[16,2048]{1,0:T(8,128)(2,1)S(1)} %collective-permute-done.21.refs_1_, ...), custom_call_target="tpu_custom_call" | custom-call | flops 629145600 | bytes 9830400 | tf_op jit(solution)/shard_map/layer/pallas_call | solution.py:181
  111.1 2.3 %collective-permute-start.24 = (bf16[16,2048]{1,0:T(8,128)(2,1)S(1)}, bf16[16,2048]{1,0:T(8,128)(2,1)S(1)}, u32[]{:S(2)}, u32[]{:S(2)}) collective-permute-start(bf16[16,2048]{1,0:T(8,128)(2,1)S(1)} %get-tuple-element.68), channel_id=1, source_target_pairs={{0,6},{1,7},{2,4},{3,5},{4,2},{5,3},{6,0},{7,1},{8,14},{9,15},{10,... | collective-permute-start | bytes 196616 | tf_op jit(solution)/shard_map/ppermute | solution.py:27
  113.5 2.1 %collective-permute-start.26 = (bf16[16,2048]{1,0:T(8,128)(2,1)S(1)}, bf16[16,2048]{1,0:T(8,128)(2,1)S(1)}, u32[]{:S(2)}, u32[]{:S(2)}) collective-permute-start(bf16[16,2048]{1,0:T(8,128)(2,1)S(1)} %get-tuple-element.70), channel_id=1, source_target_pairs={{0,2},{1,3},{2,0},{3,1},{4,6},{5,7},{6,4},{7,5},{8,10},{9,11},{10,... | collective-permute-start | bytes 196616 | tf_op jit(solution)/shard_map/ppermute | solution.py:27
  115.6 1.7 %collective-permute-done.24.refs_1_ = bf16[16,2048]{1,0:T(8,128)(2,1)S(1)} collective-permute-done((bf16[16,2048]{1,0:T(8,128)(2,1)S(1)}, bf16[16,2048]{1,0:T(8,128)(2,1)S(1)}, u32[]{:S(2)}, u32[]{:S(2)}) %collective-permute-start.24) | collective-permute-done | bytes 65568 | tf_op jit(solution)/shard_map/ppermute | solution.py:27
  117.3 2.2 %collective-permute-done.25.refs_2_ = bf16[16,2048]{1,0:T(8,128)(2,1)S(1)} collective-permute-done((bf16[16,2048]{1,0:T(8,128)(2,1)S(1)}, bf16[16,2048]{1,0:T(8,128)(2,1)S(1)}, u32[]{:S(2)}, u32[]{:S(2)}) %collective-permute-start.25) | collective-permute-done | bytes 65568 | tf_op jit(solution)/shard_map/ppermute | solution.py:27
  120.9 3.3 %collective-permute-done.28.refs_1_ = bf16[16,2048]{1,0:T(8,128)(2,1)S(1)} collective-permute-done((bf16[16,2048]{1,0:T(8,128)(2,1)S(1)}, bf16[16,2048]{1,0:T(8,128)(2,1)S(1)}, u32[]{:S(2)}, u32[]{:S(2)}) %collective-permute-start.28) | collective-permute-done | bytes 65568 | tf_op jit(solution)/shard_map/ppermute | solution.py:27
  124.2 2.6 %collective-permute-start.31 = (bf16[16,2048]{1,0:T(8,128)(2,1)S(1)}, bf16[16,2048]{1,0:T(8,128)(2,1)S(1)}, u32[]{:S(2)}, u32[]{:S(2)}) collective-permute-start(bf16[16,2048]{1,0:T(8,128)(2,1)S(1)} %shard_map.107.refs_0_), channel_id=1, source_target_pairs={{0,6},{1,7},{2,4},{3,5},{4,2},{5,3},{6,0},{7,1},{8,14},{9,15},{10,... | collective-permute-start | bytes 196616 | tf_op jit(solution)/shard_map/ppermute | solution.py:27
  126.8 1.9 %collective-permute-start.29 = (bf16[16,2048]{1,0:T(8,128)(2,1)S(1)}, bf16[16,2048]{1,0:T(8,128)(2,1)S(1)}, u32[]{:S(2)}, u32[]{:S(2)}) collective-permute-start(bf16[16,2048]{1,0:T(8,128)(2,1)S(1)} %shard_map.107.refs_0_), channel_id=1, source_target_pairs={{0,2},{1,3},{2,0},{3,1},{4,6},{5,7},{6,4},{7,5},{8,10},{9,11},{10,... | collective-permute-start | bytes 196616 | tf_op jit(solution)/shard_map/ppermute | solution.py:27
  128.7 2.1 %collective-permute-done.31.refs_3_ = bf16[16,2048]{1,0:T(8,128)(2,1)S(1)} collective-permute-done((bf16[16,2048]{1,0:T(8,128)(2,1)S(1)}, bf16[16,2048]{1,0:T(8,128)(2,1)S(1)}, u32[]{:S(2)}, u32[]{:S(2)}) %collective-permute-start.31) | collective-permute-done | bytes 65568 | tf_op jit(solution)/shard_map/ppermute | solution.py:27
  130.8 1.8 %collective-permute-done.30.refs_2_ = bf16[16,2048]{1,0:T(8,128)(2,1)S(1)} collective-permute-done((bf16[16,2048]{1,0:T(8,128)(2,1)S(1)}, bf16[16,2048]{1,0:T(8,128)(2,1)S(1)}, u32[]{:S(2)}, u32[]{:S(2)}) %collective-permute-start.30) | collective-permute-done | bytes 65568 | tf_op jit(solution)/shard_map/ppermute | solution.py:27
  132.5 2.5 %layer.9 = (f32[16,2048]{1,0:T(8,128)S(1)}, bf16[16,2048]{1,0:T(8,128)(2,1)S(1)}, bf16[16,2048]{1,0:T(8,128)(2,1)S(1)}, bf16[16,2048]{1,0:T(8,128)(2,1)S(1)}) custom-call(bf16[16,2048]{1,0:T(8,128)(2,1)S(1)} %shard_map.107.refs_0_, bf16[16,2048]{1,0:T(8,128)(2,1)S(1)} %collective-permute-done.29.refs_1_, ...), custom_call_target="tpu_custom_call" | custom-call | flops 629145600 | bytes 9830400 | tf_op jit(solution)/shard_map/layer/pallas_call | solution.py:181
  135.1 2.3 %collective-permute-start.32 = (bf16[16,2048]{1,0:T(8,128)(2,1)S(1)}, bf16[16,2048]{1,0:T(8,128)(2,1)S(1)}, u32[]{:S(2)}, u32[]{:S(2)}) collective-permute-start(bf16[16,2048]{1,0:T(8,128)(2,1)S(1)} %get-tuple-element.72), channel_id=1, source_target_pairs={{0,6},{1,7},{2,4},{3,5},{4,2},{5,3},{6,0},{7,1},{8,14},{9,15},{10,... | collective-permute-start | bytes 196616 | tf_op jit(solution)/shard_map/ppermute | solution.py:27
  137.4 2.1 %collective-permute-start.34 = (bf16[16,2048]{1,0:T(8,128)(2,1)S(1)}, bf16[16,2048]{1,0:T(8,128)(2,1)S(1)}, u32[]{:S(2)}, u32[]{:S(2)}) collective-permute-start(bf16[16,2048]{1,0:T(8,128)(2,1)S(1)} %get-tuple-element.74), channel_id=1, source_target_pairs={{0,2},{1,3},{2,0},{3,1},{4,6},{5,7},{6,4},{7,5},{8,10},{9,11},{10,... | collective-permute-start | bytes 196616 | tf_op jit(solution)/shard_map/ppermute | solution.py:27
  139.5 1.8 %collective-permute-done.32 = bf16[16,2048]{1,0:T(8,128)(2,1)S(1)} collective-permute-done((bf16[16,2048]{1,0:T(8,128)(2,1)S(1)}, bf16[16,2048]{1,0:T(8,128)(2,1)S(1)}, u32[]{:S(2)}, u32[]{:S(2)}) %collective-permute-start.32) | collective-permute-done | bytes 65568 | tf_op jit(solution)/shard_map/ppermute | solution.py:27
  141.3 2.4 %collective-permute-done.33 = bf16[16,2048]{1,0:T(8,128)(2,1)S(1)} collective-permute-done((bf16[16,2048]{1,0:T(8,128)(2,1)S(1)}, bf16[16,2048]{1,0:T(8,128)(2,1)S(1)}, u32[]{:S(2)}, u32[]{:S(2)}) %collective-permute-start.33) | collective-permute-done | bytes 65568 | tf_op jit(solution)/shard_map/ppermute | solution.py:27
  144.4 3.3 %collective-permute-done.35 = bf16[8,2048]{1,0:T(8,128)(2,1)S(1)} collective-permute-done((bf16[8,2048]{1,0:T(8,128)(2,1)S(1)}, bf16[8,2048]{1,0:T(8,128)(2,1)S(1)}, u32[]{:S(2)}, u32[]{:S(2)}) %collective-permute-start.35) | collective-permute-done | bytes 32800 | tf_op jit(solution)/shard_map/ppermute | solution.py:27
  (54 shorter events, 13.5 us)
Async XLA Ops:
  1.1 0.8 copy-start.1
  1.9 0.7 copy-start.2
  2.6 0.7 copy-start.3
  3.5 4.9 %collective-permute-start = (bf16[8,2176]{1,0:T(8,128)(2,1)S(1)}, bf16[8,2176]{1,0:T(8,128)(2,1)S(1)}, u32[]{:S(2)}, u32[]{:S(2)}) collective-permute-start(bf16[8,2176]{1,0:T(8,128)(2,1)S(1)} %shard_map.100.first_ref), channel_id=1, source_target_pairs={{0,1},{1,0},{2,3},{3,2},{4,5},{5,4},{6,7},{7,6},{8,9},{9,8},{10,11... | collective-permute-start | bytes 104456 | tf_op jit(solution)/shard_map/ppermute | solution.py:27
  8.4 4.5 %collective-permute-start.1 = (bf16[16,2176]{1,0:T(8,128)(2,1)S(1)}, bf16[16,2176]{1,0:T(8,128)(2,1)S(1)}, u32[]{:S(2)}, u32[]{:S(2)}) collective-permute-start(bf16[16,2176]{1,0:T(8,128)(2,1)S(1)} %shard_map.101.refs_0_.refs_4_), channel_id=1, source_target_pairs={{0,2},{1,3},{2,0},{3,1},{4,6},{5,7},{6,4},{7,5},{8,10},{9,11},{10,... | collective-permute-start | bytes 208904 | tf_op jit(solution)/shard_map/ppermute | solution.py:27
  14.4 69.9 %collective-permute-start.15 = (bf16[3,160,2048]{2,1,0:T(8,128)(2,1)S(1)}, bf16[3,160,2048]{2,1,0:T(8,128)(2,1)S(1)}, u32[]{:S(2)}, u32[]{:S(2)}) collective-permute-start(bf16[3,160,2048]{2,1,0:T(8,128)(2,1)S(1)} %stack.1), channel_id=1, source_target_pairs={{0,24},{1,25},{2,26},{3,27},{4,28},{5,29},{6,30},{7,31},{8,0},{9,1... | collective-permute-start | bytes 5898248 | tf_op jit(solution)/shard_map/ppermute | solution.py:27
  14.4 29.2 %collective-permute-start.4 = (bf16[160,2048]{1,0:T(8,128)(2,1)S(1)}, bf16[160,2048]{1,0:T(8,128)(2,1)S(1)}, u32[]{:S(2)}, u32[]{:S(2)}) collective-permute-start(bf16[160,2048]{1,0:T(8,128)(2,1)S(1)} %fill.2), channel_id=1, source_target_pairs={{0,24},{1,25},{2,26},{3,27},{4,28},{5,29},{6,30},{7,31},{8,0},{9,1... | collective-permute-start | bytes 1966088 | tf_op jit(solution)/shard_map/ppermute | solution.py:27
  17.8 32.8 %collective-permute-start.5 = (bf16[160,2048]{1,0:T(8,128)(2,1)S(1)}, bf16[160,2048]{1,0:T(8,128)(2,1)S(1)}, u32[]{:S(2)}, u32[]{:S(2)}) collective-permute-start(bf16[160,2048]{1,0:T(8,128)(2,1)S(1)} %get-tuple-element.49), channel_id=1, source_target_pairs={{0,24},{1,25},{2,26},{3,27},{4,28},{5,29},{6,30},{7,31},{8,0},{9,1... | collective-permute-start | bytes 1966088 | tf_op jit(solution)/shard_map/ppermute | solution.py:27
  17.9 39.7 %collective-permute-start.6 = (bf16[160,2048]{1,0:T(8,128)(2,1)S(1)}, bf16[160,2048]{1,0:T(8,128)(2,1)S(1)}, u32[]{:S(2)}, u32[]{:S(2)}) collective-permute-start(bf16[160,2048]{1,0:T(8,128)(2,1)S(1)} %get-tuple-element.50), channel_id=1, source_target_pairs={{0,24},{1,25},{2,26},{3,27},{4,28},{5,29},{6,30},{7,31},{8,0},{9,1... | collective-permute-start | bytes 1966088 | tf_op jit(solution)/shard_map/ppermute | solution.py:27
  18.0 6.4 %collective-permute-start.3 = (bf16[16,2176]{1,0:T(8,128)(2,1)S(1)}, bf16[16,2176]{1,0:T(8,128)(2,1)S(1)}, u32[]{:S(2)}, u32[]{:S(2)}) collective-permute-start(bf16[16,2176]{1,0:T(8,128)(2,1)S(1)} %shard_map.101.refs_0_.refs_4_), channel_id=1, source_target_pairs={{0,6},{1,7},{2,4},{3,5},{4,2},{5,3},{6,0},{7,1},{8,14},{9,15},{10,... | collective-permute-start | bytes 208904 | tf_op jit(solution)/shard_map/ppermute | solution.py:27
  24.5 5.3 %collective-permute-start.2 = (bf16[16,2176]{1,0:T(8,128)(2,1)S(1)}, bf16[16,2176]{1,0:T(8,128)(2,1)S(1)}, u32[]{:S(2)}, u32[]{:S(2)}) collective-permute-start(bf16[16,2176]{1,0:T(8,128)(2,1)S(1)} %shard_map.101.refs_0_.refs_4_), channel_id=1, source_target_pairs={{0,4},{1,5},{2,6},{3,7},{4,0},{5,1},{6,2},{7,3},{8,12},{9,13},{10,... | collective-permute-start | bytes 208904 | tf_op jit(solution)/shard_map/ppermute | solution.py:27
  25.4 4.4 %copy-start = (f32[2,1,2048]{2,1,0:T(1,128)S(1)}, f32[2,1,2048]{2,1,0:T(1,128)}, u32[]{:S(2)}) copy-start(f32[2,1,2048]{2,1,0:T(1,128)} %refs_8_.9) | copy-start | bytes 49156
  58.5 6.5 %collective-permute-start.7 = (bf16[16,2048]{1,0:T(8,128)(2,1)S(1)}, bf16[16,2048]{1,0:T(8,128)(2,1)S(1)}, u32[]{:S(2)}, u32[]{:S(2)}) collective-permute-start(bf16[16,2048]{1,0:T(8,128)(2,1)S(1)} %get-tuple-element.52), channel_id=1, source_target_pairs={{0,6},{1,7},{2,4},{3,5},{4,2},{5,3},{6,0},{7,1},{8,14},{9,15},{10,... | collective-permute-start | bytes 196616 | tf_op jit(solution)/shard_map/ppermute | solution.py:27
  62.6 6.3 %collective-permute-start.8 = (bf16[16,2048]{1,0:T(8,128)(2,1)S(1)}, bf16[16,2048]{1,0:T(8,128)(2,1)S(1)}, u32[]{:S(2)}, u32[]{:S(2)}) collective-permute-start(bf16[16,2048]{1,0:T(8,128)(2,1)S(1)} %get-tuple-element.53), channel_id=1, source_target_pairs={{0,4},{1,5},{2,6},{3,7},{4,0},{5,1},{6,2},{7,3},{8,12},{9,13},{10,... | collective-permute-start | bytes 196616 | tf_op jit(solution)/shard_map/ppermute | solution.py:27
  62.6 6.3 %collective-permute-start.9 = (bf16[16,2048]{1,0:T(8,128)(2,1)S(1)}, bf16[16,2048]{1,0:T(8,128)(2,1)S(1)}, u32[]{:S(2)}, u32[]{:S(2)}) collective-permute-start(bf16[16,2048]{1,0:T(8,128)(2,1)S(1)} %get-tuple-element.54), channel_id=1, source_target_pairs={{0,2},{1,3},{2,0},{3,1},{4,6},{5,7},{6,4},{7,5},{8,10},{9,11},{10,... | collective-permute-start | bytes 196616 | tf_op jit(solution)/shard_map/ppermute | solution.py:27
  68.9 5.0 %collective-permute-start.11 = (bf16[16,2048]{1,0:T(8,128)(2,1)S(1)}, bf16[16,2048]{1,0:T(8,128)(2,1)S(1)}, u32[]{:S(2)}, u32[]{:S(2)}) collective-permute-start(bf16[16,2048]{1,0:T(8,128)(2,1)S(1)} %shard_map.102), channel_id=1, source_target_pairs={{0,9},{1,8},{2,11},{3,10},{4,13},{5,12},{6,15},{7,14},{8,17},{9,16... | collective-permute-start | bytes 196616 | tf_op jit(solution)/shard_map/ppermute | solution.py:27
  70.3 4.0 %collective-permute-start.10 = (bf16[16,2048]{1,0:T(8,128)(2,1)S(1)}, bf16[16,2048]{1,0:T(8,128)(2,1)S(1)}, u32[]{:S(2)}, u32[]{:S(2)}) collective-permute-start(bf16[16,2048]{1,0:T(8,128)(2,1)S(1)} %shard_map.102), channel_id=1, source_target_pairs={{0,8},{1,9},{2,10},{3,11},{4,12},{5,13},{6,14},{7,15},{8,16},{9,17... | collective-permute-start | bytes 196616 | tf_op jit(solution)/shard_map/ppermute | solution.py:27
  74.3 9.9 %collective-permute-start.14 = (bf16[16,2048]{1,0:T(8,128)(2,1)S(1)}, bf16[16,2048]{1,0:T(8,128)(2,1)S(1)}, u32[]{:S(2)}, u32[]{:S(2)}) collective-permute-start(bf16[16,2048]{1,0:T(8,128)(2,1)S(1)} %shard_map.103.refs_0_), channel_id=1, source_target_pairs={{0,6},{1,7},{2,4},{3,5},{4,2},{5,3},{6,0},{7,1},{8,14},{9,15},{10,... | collective-permute-start | bytes 196616 | tf_op jit(solution)/shard_map/ppermute | solution.py:27
  76.8 7.5 %collective-permute-start.13 = (bf16[16,2048]{1,0:T(8,128)(2,1)S(1)}, bf16[16,2048]{1,0:T(8,128)(2,1)S(1)}, u32[]{:S(2)}, u32[]{:S(2)}) collective-permute-start(bf16[16,2048]{1,0:T(8,128)(2,1)S(1)} %shard_map.103.refs_0_), channel_id=1, source_target_pairs={{0,4},{1,5},{2,6},{3,7},{4,0},{5,1},{6,2},{7,3},{8,12},{9,13},{10,... | collective-permute-start | bytes 196616 | tf_op jit(solution)/shard_map/ppermute | solution.py:27
  76.8 7.5 %collective-permute-start.12 = (bf16[16,2048]{1,0:T(8,128)(2,1)S(1)}, bf16[16,2048]{1,0:T(8,128)(2,1)S(1)}, u32[]{:S(2)}, u32[]{:S(2)}) collective-permute-start(bf16[16,2048]{1,0:T(8,128)(2,1)S(1)} %shard_map.103.refs_0_), channel_id=1, source_target_pairs={{0,2},{1,3},{2,0},{3,1},{4,6},{5,7},{6,4},{7,5},{8,10},{9,11},{10,... | collective-permute-start | bytes 196616 | tf_op jit(solution)/shard_map/ppermute | solution.py:27
  86.8 6.9 %collective-permute-start.16 = (bf16[16,2048]{1,0:T(8,128)(2,1)S(1)}, bf16[16,2048]{1,0:T(8,128)(2,1)S(1)}, u32[]{:S(2)}, u32[]{:S(2)}) collective-permute-start(bf16[16,2048]{1,0:T(8,128)(2,1)S(1)} %get-tuple-element.64), channel_id=1, source_target_pairs={{0,6},{1,7},{2,4},{3,5},{4,2},{5,3},{6,0},{7,1},{8,14},{9,15},{10,... | collective-permute-start | bytes 196616 | tf_op jit(solution)/shard_map/ppermute | solution.py:27
  89.3 5.8 %collective-permute-start.17 = (bf16[16,2048]{1,0:T(8,128)(2,1)S(1)}, bf16[16,2048]{1,0:T(8,128)(2,1)S(1)}, u32[]{:S(2)}, u32[]{:S(2)}) collective-permute-start(bf16[16,2048]{1,0:T(8,128)(2,1)S(1)} %get-tuple-element.65), channel_id=1, source_target_pairs={{0,4},{1,5},{2,6},{3,7},{4,0},{5,1},{6,2},{7,3},{8,12},{9,13},{10,... | collective-permute-start | bytes 196616 | tf_op jit(solution)/shard_map/ppermute | solution.py:27
  89.3 5.8 %collective-permute-start.18 = (bf16[16,2048]{1,0:T(8,128)(2,1)S(1)}, bf16[16,2048]{1,0:T(8,128)(2,1)S(1)}, u32[]{:S(2)}, u32[]{:S(2)}) collective-permute-start(bf16[16,2048]{1,0:T(8,128)(2,1)S(1)} %get-tuple-element.66), channel_id=1, source_target_pairs={{0,2},{1,3},{2,0},{3,1},{4,6},{5,7},{6,4},{7,5},{8,10},{9,11},{10,... | collective-permute-start | bytes 196616 | tf_op jit(solution)/shard_map/ppermute | solution.py:27
  95.1 5.0 %collective-permute-start.20 = (bf16[16,2048]{1,0:T(8,128)(2,1)S(1)}, bf16[16,2048]{1,0:T(8,128)(2,1)S(1)}, u32[]{:S(2)}, u32[]{:S(2)}) collective-permute-start(bf16[16,2048]{1,0:T(8,128)(2,1)S(1)} %shard_map.104), channel_id=1, source_target_pairs={{0,9},{1,8},{2,11},{3,10},{4,13},{5,12},{6,15},{7,14},{8,17},{9,16... | collective-permute-start | bytes 196616 | tf_op jit(solution)/shard_map/ppermute | solution.py:27
  95.1 4.9 %collective-permute-start.19 = (bf16[16,2048]{1,0:T(8,128)(2,1)S(1)}, bf16[16,2048]{1,0:T(8,128)(2,1)S(1)}, u32[]{:S(2)}, u32[]{:S(2)}) collective-permute-start(bf16[16,2048]{1,0:T(8,128)(2,1)S(1)} %shard_map.104), channel_id=1, source_target_pairs={{0,8},{1,9},{2,10},{3,11},{4,12},{5,13},{6,14},{7,15},{8,16},{9,17... | collective-permute-start | bytes 196616 | tf_op jit(solution)/shard_map/ppermute | solution.py:27
  100.1 6.6 %collective-permute-start.23 = (bf16[16,2048]{1,0:T(8,128)(2,1)S(1)}, bf16[16,2048]{1,0:T(8,128)(2,1)S(1)}, u32[]{:S(2)}, u32[]{:S(2)}) collective-permute-start(bf16[16,2048]{1,0:T(8,128)(2,1)S(1)} %shard_map.105.refs_0_), channel_id=1, source_target_pairs={{0,6},{1,7},{2,4},{3,5},{4,2},{5,3},{6,0},{7,1},{8,14},{9,15},{10,... | collective-permute-start | bytes 196616 | tf_op jit(solution)/shard_map/ppermute | solution.py:27
  102.3 6.1 %collective-permute-start.22 = (bf16[16,2048]{1,0:T(8,128)(2,1)S(1)}, bf16[16,2048]{1,0:T(8,128)(2,1)S(1)}, u32[]{:S(2)}, u32[]{:S(2)}) collective-permute-start(bf16[16,2048]{1,0:T(8,128)(2,1)S(1)} %shard_map.105.refs_0_), channel_id=1, source_target_pairs={{0,4},{1,5},{2,6},{3,7},{4,0},{5,1},{6,2},{7,3},{8,12},{9,13},{10,... | collective-permute-start | bytes 196616 | tf_op jit(solution)/shard_map/ppermute | solution.py:27
  102.3 6.1 %collective-permute-start.21 = (bf16[16,2048]{1,0:T(8,128)(2,1)S(1)}, bf16[16,2048]{1,0:T(8,128)(2,1)S(1)}, u32[]{:S(2)}, u32[]{:S(2)}) collective-permute-start(bf16[16,2048]{1,0:T(8,128)(2,1)S(1)} %shard_map.105.refs_0_), channel_id=1, source_target_pairs={{0,2},{1,3},{2,0},{3,1},{4,6},{5,7},{6,4},{7,5},{8,10},{9,11},{10,... | collective-permute-start | bytes 196616 | tf_op jit(solution)/shard_map/ppermute | solution.py:27
  111.1 6.2 %collective-permute-start.24 = (bf16[16,2048]{1,0:T(8,128)(2,1)S(1)}, bf16[16,2048]{1,0:T(8,128)(2,1)S(1)}, u32[]{:S(2)}, u32[]{:S(2)}) collective-permute-start(bf16[16,2048]{1,0:T(8,128)(2,1)S(1)} %get-tuple-element.68), channel_id=1, source_target_pairs={{0,6},{1,7},{2,4},{3,5},{4,2},{5,3},{6,0},{7,1},{8,14},{9,15},{10,... | collective-permute-start | bytes 196616 | tf_op jit(solution)/shard_map/ppermute | solution.py:27
  113.5 6.0 %collective-permute-start.25 = (bf16[16,2048]{1,0:T(8,128)(2,1)S(1)}, bf16[16,2048]{1,0:T(8,128)(2,1)S(1)}, u32[]{:S(2)}, u32[]{:S(2)}) collective-permute-start(bf16[16,2048]{1,0:T(8,128)(2,1)S(1)} %get-tuple-element.69), channel_id=1, source_target_pairs={{0,4},{1,5},{2,6},{3,7},{4,0},{5,1},{6,2},{7,3},{8,12},{9,13},{10,... | collective-permute-start | bytes 196616 | tf_op jit(solution)/shard_map/ppermute | solution.py:27
  113.5 6.0 %collective-permute-start.26 = (bf16[16,2048]{1,0:T(8,128)(2,1)S(1)}, bf16[16,2048]{1,0:T(8,128)(2,1)S(1)}, u32[]{:S(2)}, u32[]{:S(2)}) collective-permute-start(bf16[16,2048]{1,0:T(8,128)(2,1)S(1)} %get-tuple-element.70), channel_id=1, source_target_pairs={{0,2},{1,3},{2,0},{3,1},{4,6},{5,7},{6,4},{7,5},{8,10},{9,11},{10,... | collective-permute-start | bytes 196616 | tf_op jit(solution)/shard_map/ppermute | solution.py:27
  119.5 4.6 %collective-permute-start.28 = (bf16[16,2048]{1,0:T(8,128)(2,1)S(1)}, bf16[16,2048]{1,0:T(8,128)(2,1)S(1)}, u32[]{:S(2)}, u32[]{:S(2)}) collective-permute-start(bf16[16,2048]{1,0:T(8,128)(2,1)S(1)} %shard_map.106), channel_id=1, source_target_pairs={{0,9},{1,8},{2,11},{3,10},{4,13},{5,12},{6,15},{7,14},{8,17},{9,16... | collective-permute-start | bytes 196616 | tf_op jit(solution)/shard_map/ppermute | solution.py:27
  119.6 4.6 %collective-permute-start.27 = (bf16[16,2048]{1,0:T(8,128)(2,1)S(1)}, bf16[16,2048]{1,0:T(8,128)(2,1)S(1)}, u32[]{:S(2)}, u32[]{:S(2)}) collective-permute-start(bf16[16,2048]{1,0:T(8,128)(2,1)S(1)} %shard_map.106), channel_id=1, source_target_pairs={{0,8},{1,9},{2,10},{3,11},{4,12},{5,13},{6,14},{7,15},{8,16},{9,17... | collective-permute-start | bytes 196616 | tf_op jit(solution)/shard_map/ppermute | solution.py:27
  124.2 6.5 %collective-permute-start.31 = (bf16[16,2048]{1,0:T(8,128)(2,1)S(1)}, bf16[16,2048]{1,0:T(8,128)(2,1)S(1)}, u32[]{:S(2)}, u32[]{:S(2)}) collective-permute-start(bf16[16,2048]{1,0:T(8,128)(2,1)S(1)} %shard_map.107.refs_0_), channel_id=1, source_target_pairs={{0,6},{1,7},{2,4},{3,5},{4,2},{5,3},{6,0},{7,1},{8,14},{9,15},{10,... | collective-permute-start | bytes 196616 | tf_op jit(solution)/shard_map/ppermute | solution.py:27
  126.8 5.8 %collective-permute-start.30 = (bf16[16,2048]{1,0:T(8,128)(2,1)S(1)}, bf16[16,2048]{1,0:T(8,128)(2,1)S(1)}, u32[]{:S(2)}, u32[]{:S(2)}) collective-permute-start(bf16[16,2048]{1,0:T(8,128)(2,1)S(1)} %shard_map.107.refs_0_), channel_id=1, source_target_pairs={{0,4},{1,5},{2,6},{3,7},{4,0},{5,1},{6,2},{7,3},{8,12},{9,13},{10,... | collective-permute-start | bytes 196616 | tf_op jit(solution)/shard_map/ppermute | solution.py:27
  126.8 5.8 %collective-permute-start.29 = (bf16[16,2048]{1,0:T(8,128)(2,1)S(1)}, bf16[16,2048]{1,0:T(8,128)(2,1)S(1)}, u32[]{:S(2)}, u32[]{:S(2)}) collective-permute-start(bf16[16,2048]{1,0:T(8,128)(2,1)S(1)} %shard_map.107.refs_0_), channel_id=1, source_target_pairs={{0,2},{1,3},{2,0},{3,1},{4,6},{5,7},{6,4},{7,5},{8,10},{9,11},{10,... | collective-permute-start | bytes 196616 | tf_op jit(solution)/shard_map/ppermute | solution.py:27
  135.1 6.2 %collective-permute-start.32 = (bf16[16,2048]{1,0:T(8,128)(2,1)S(1)}, bf16[16,2048]{1,0:T(8,128)(2,1)S(1)}, u32[]{:S(2)}, u32[]{:S(2)}) collective-permute-start(bf16[16,2048]{1,0:T(8,128)(2,1)S(1)} %get-tuple-element.72), channel_id=1, source_target_pairs={{0,6},{1,7},{2,4},{3,5},{4,2},{5,3},{6,0},{7,1},{8,14},{9,15},{10,... | collective-permute-start | bytes 196616 | tf_op jit(solution)/shard_map/ppermute | solution.py:27
  137.4 6.2 %collective-permute-start.33 = (bf16[16,2048]{1,0:T(8,128)(2,1)S(1)}, bf16[16,2048]{1,0:T(8,128)(2,1)S(1)}, u32[]{:S(2)}, u32[]{:S(2)}) collective-permute-start(bf16[16,2048]{1,0:T(8,128)(2,1)S(1)} %get-tuple-element.73), channel_id=1, source_target_pairs={{0,4},{1,5},{2,6},{3,7},{4,0},{5,1},{6,2},{7,3},{8,12},{9,13},{10,... | collective-permute-start | bytes 196616 | tf_op jit(solution)/shard_map/ppermute | solution.py:27
  137.4 6.2 %collective-permute-start.34 = (bf16[16,2048]{1,0:T(8,128)(2,1)S(1)}, bf16[16,2048]{1,0:T(8,128)(2,1)S(1)}, u32[]{:S(2)}, u32[]{:S(2)}) collective-permute-start(bf16[16,2048]{1,0:T(8,128)(2,1)S(1)} %get-tuple-element.74), channel_id=1, source_target_pairs={{0,2},{1,3},{2,0},{3,1},{4,6},{5,7},{6,4},{7,5},{8,10},{9,11},{10,... | collective-permute-start | bytes 196616 | tf_op jit(solution)/shard_map/ppermute | solution.py:27
  143.7 4.0 %collective-permute-start.35 = (bf16[8,2048]{1,0:T(8,128)(2,1)S(1)}, bf16[8,2048]{1,0:T(8,128)(2,1)S(1)}, u32[]{:S(2)}, u32[]{:S(2)}) collective-permute-start(bf16[8,2048]{1,0:T(8,128)(2,1)S(1)} %slice.17), channel_id=1, source_target_pairs={{0,1},{1,0},{2,3},{3,2},{4,5},{5,4},{6,7},{7,6},{8,9},{9,8},{10,11... | collective-permute-start | bytes 98312 | tf_op jit(solution)/shard_map/ppermute | solution.py:27

commit v6 on v5

--- a/solution.py
+++ b/solution.py
@@ -33,13 +33,29 @@
     return (first_group + jnp.where(start_segment + tick_idx >= segments, 1, 0)).astype(jnp.int32)
 
 
-def groups_at(tick_idx, segments):
+def later_users(tick_idx, segments):
     found = set()
     for section in range(segments):
         start = (section - tick_idx) % segments
         first = 1 if start % 2 == 1 and start + TICKS <= segments else 0
-        found.add(first + (1 if start + tick_idx >= segments else 0))
+        if first + (1 if start + tick_idx >= segments else 0) == 1:
+            found.add(section)
     return found
+
+
+def swapped(value, users):
+    segments, members = lax.axis_size("segment"), lax.axis_size("expert")
+    partner = {section: section for section in range(segments)}
+    for section in users:
+        behind = (section + 1) % segments
+        assert behind not in users
+        partner[section], partner[behind] = behind, section
+    pairs = [
+        (section * members + member, partner[section] * members + member)
+        for section in range(segments)
+        for member in range(members)
+    ]
+    return lax.ppermute(value, BOTH, pairs)
 
 
 WHOLE = pl.BlockSpec(memory_space=pltpu.VMEM)
@@ -323,7 +339,7 @@
     state, routes, gates, norm_gain, w_gate, w_up, w_down, spare_gate, spare_up, spare_down
 ):
     segments = lax.axis_size("segment")
-    members = lax.axis_size("expert")
+    segments, members = lax.axis_size("segment"), lax.axis_size("expert")
     outer = members // 2
     assert outer & (outer - 1) == 0
     tok_dev = state.shape[1]
@@ -354,19 +370,23 @@
     before = run_layer(
         arrived, arrived, norm_gain, slots, [], tick_idx=0, tok_dev=tok_dev, ends=False
     )
-    late = moved(late, 0, -1)
-    spares.append([late])
+
+    users = [later_users(tick_idx, segments) for tick_idx in range(TICKS)]
+    opening = min([tick_idx for tick_idx in range(TICKS) if users[tick_idx]], default=TICKS)
+    near = [swapped(late, users[opening])] if opening < TICKS else []
 
     x_blocks = arrived
     for tick_idx in range(TICKS):
-        used = sorted(groups_at(tick_idx, segments))
-        assert used in ([0], [0, 1])
+        used = [spares[0]]
+        if users[tick_idx]:
+            used.append(near if users[tick_idx] <= users[opening] else far)
         parts = run_layer(
-            x_blocks, arrived, norm_gain, slots, spares[:len(used)], tick_idx=tick_idx, tok_dev=tok_dev,
+            x_blocks, arrived, norm_gain, slots, used, tick_idx=tick_idx, tok_dev=tok_dev,
             carried=before if tick_idx == 0 else None,
         )
         got = [moved(parts[j], 2 * j, 0) for j in widest_first(outer)]
         if tick_idx == 0:
+            far = [moved(lax.optimization_barrier((late, parts[0]))[0], 0, -1)]
             tied = lax.optimization_barrier((*weights, parts[0]))[:3]
             gate = loaded(tied[:1], (True,), True)
         if tick_idx + 1 == TICKS:

time: 149 us -> 123 us (0.83)
  waiting for transfers between devices: 70.2 us -> 47.4 us
  local copies, waits for them, and re-layouts: 2.14 us -> 0.02 us
    ppermute x36, waiting for transfers between devices: 70.2 us -> 47.4 us  [moved(): return lax.ppermute(value, BOTH, pairs)]
    ppermute x36, starting transfers between devices: 50.8 us -> 47.8 us  [moved(): return lax.ppermute(value, BOTH, pairs)]
    unnamed x8, local copies, waits for them, and re-layouts: 2.13 us -> 0.01 us
    ppermute x0 -> x1, starting transfers between devices: none -> 1.92 us  [swapped(): return lax.ppermute(value, BOTH, pairs)]
  transfers between devices with their start and end apart: 36 -> 37, of which waited for: 23 -> 22; matrix products, arithmetic and copies ran while one was open for 0% -> 0% of each run, Pallas kernels for 9% -> 15%
where the time goes in v6:
time: 123 us; the launch traced here: 122 us
  starting transfers between devices  49.8 us (40%)
  waiting for transfers between devices  47.4 us (39%)
  Pallas kernels  24.4 us (20%)
    ppermute x36, starting transfers between devices, moved(): return lax.ppermute(value, BOTH, pairs)  47.8 us
    ppermute x36, waiting for transfers between devices, moved(): return lax.ppermute(value, BOTH, pairs)  47.4 us
    pallas_call x5, Pallas kernels, run_layer(): pl.pallas_call(functools.partial(layer_kernel, tick_idx=tick_idx, blocks=...  10.2 us
    pallas_call x3, Pallas kernels, loaded(): pl.pallas_call(functools.partial(load_kernel, turned=turned, other=other)...  9.8 us
  transfers between devices with their start and end apart: 37, of which 22 were waited for; matrix products, arithmetic and copies ran while one was open for 0% of the time, Pallas kernels for 15%

profile of v6, /device:TPU:0, one launch (start us, length us, event | category | flops | bytes accessed | tf_op | source)
XLA Modules:
  0.0 122.4 jit_solution(13211380433802907172)
XLA Ops:
  1.1 2.5 %collective-permute-start.4 = (bf16[160,2048]{1,0:T(8,128)(2,1)S(1)}, bf16[160,2048]{1,0:T(8,128)(2,1)S(1)}, u32[]{:S(2)}, u32[]{:S(2)}) collective-permute-start(bf16[160,2048]{1,0:T(8,128)(2,1)S(1)} %fill.2), channel_id=1, source_target_pairs={{0,24},{1,25},{2,26},{3,27},{4,28},{5,29},{6,30},{7,31},{8,0},{9,1... | collective-permute-start | bytes 1966088 | tf_op jit(solution)/shard_map/ppermute | solution.py:27
  6.0 1.5 %collective-permute-start = (bf16[8,2176]{1,0:T(8,128)(2,1)S(1)}, bf16[8,2176]{1,0:T(8,128)(2,1)S(1)}, u32[]{:S(2)}, u32[]{:S(2)}) collective-permute-start(bf16[8,2176]{1,0:T(8,128)(2,1)S(1)} %shard_map.100.first_ref), channel_id=1, source_target_pairs={{0,1},{1,0},{2,3},{3,2},{4,5},{5,4},{6,7},{7,6},{8,9},{9,8},{10,11... | collective-permute-start | bytes 104456 | tf_op jit(solution)/shard_map/ppermute | solution.py:27
  7.5 2.4 %collective-permute-done.second_ref = bf16[8,2176]{1,0:T(8,128)(2,1)S(1)} collective-permute-done((bf16[8,2176]{1,0:T(8,128)(2,1)S(1)}, bf16[8,2176]{1,0:T(8,128)(2,1)S(1)}, u32[]{:S(2)}, u32[]{:S(2)}) %collective-permute-start) | collective-permute-done | bytes 34848 | tf_op jit(solution)/shard_map/ppermute | solution.py:27
  10.0 1.6 %collective-permute-start.1 = (bf16[16,2176]{1,0:T(8,128)(2,1)S(1)}, bf16[16,2176]{1,0:T(8,128)(2,1)S(1)}, u32[]{:S(2)}, u32[]{:S(2)}) collective-permute-start(bf16[16,2176]{1,0:T(8,128)(2,1)S(1)} %shard_map.101.refs_0_.refs_4_), channel_id=1, source_target_pairs={{0,2},{1,3},{2,0},{3,1},{4,6},{5,7},{6,4},{7,5},{8,10},{9,11},{10,... | collective-permute-start | bytes 208904 | tf_op jit(solution)/shard_map/ppermute | solution.py:27
  11.6 2.7 %collective-permute-done.1.refs_1_.refs_5_ = bf16[16,2176]{1,0:T(8,128)(2,1)S(1)} collective-permute-done((bf16[16,2176]{1,0:T(8,128)(2,1)S(1)}, bf16[16,2176]{1,0:T(8,128)(2,1)S(1)}, u32[]{:S(2)}, u32[]{:S(2)}) %collective-permute-start.1) | collective-permute-done | bytes 69664 | tf_op jit(solution)/shard_map/ppermute | solution.py:27
  14.3 1.5 %stack.1 = bf16[3,160,2048]{2,1,0:T(8,128)(2,1)S(1)} custom-call(bf16[2,160,2048]{2,1,0:T(8,128)(2,1)} %bitcast.29, bf16[2,160,2048]{2,1,0:T(8,128)(2,1)} %bitcast.25, bf16[2,160,2048]{2,1,0:T(8,128)(2,1)} %bitcast.27), custom_call_target="tpu_custom_call" | custom-call | tf_op jit(solution)/shard_map/stack/pallas_call | solution.py:316
  15.9 1.9 %collective-permute-start.15 = (bf16[3,160,2048]{2,1,0:T(8,128)(2,1)S(1)}, bf16[3,160,2048]{2,1,0:T(8,128)(2,1)S(1)}, u32[]{:S(2)}, u32[]{:S(2)}) collective-permute-start(bf16[3,160,2048]{2,1,0:T(8,128)(2,1)S(1)} %stack.1), channel_id=1, source_target_pairs={{0,8},{1,9},{2,10},{3,11},{4,12},{5,13},{6,14},{7,15},{8,0},{9,1},... | collective-permute-start | bytes 5898248 | tf_op jit(solution)/shard_map/ppermute | solution.py:58
  17.8 3.7 %collective-permute-start.3 = (bf16[16,2176]{1,0:T(8,128)(2,1)S(1)}, bf16[16,2176]{1,0:T(8,128)(2,1)S(1)}, u32[]{:S(2)}, u32[]{:S(2)}) collective-permute-start(bf16[16,2176]{1,0:T(8,128)(2,1)S(1)} %shard_map.101.refs_0_.refs_4_), channel_id=1, source_target_pairs={{0,6},{1,7},{2,4},{3,5},{4,2},{5,3},{6,0},{7,1},{8,14},{9,15},{10,... | collective-permute-start | bytes 208904 | tf_op jit(solution)/shard_map/ppermute | solution.py:27
  21.5 2.9 %collective-permute-done.3.refs_3_.refs_7_ = bf16[16,2176]{1,0:T(8,128)(2,1)S(1)} collective-permute-done((bf16[16,2176]{1,0:T(8,128)(2,1)S(1)}, bf16[16,2176]{1,0:T(8,128)(2,1)S(1)}, u32[]{:S(2)}, u32[]{:S(2)}) %collective-permute-start.3) | collective-permute-done | bytes 69664 | tf_op jit(solution)/shard_map/ppermute | solution.py:27
  25.0 4.4 %load.3 = (bf16[2048,640]{1,0:T(8,128)(2,1)S(1)}, bf16[2048,640]{1,0:T(8,128)(2,1)S(1)}, bf16[640,2048]{1,0:T(8,128)(2,1)S(1)}) custom-call(bf16[2,640,2048]{2,1,0:T(8,128)(2,1)} %bitcast.22, bf16[2,640,2048]{2,1,0:T(8,128)(2,1)} %bitcast.18, bf16[2,640,2048]{2,1,0:T(8,128)(2,1)} %bitcast.20), custom_call_target="tpu_custom_call" | custom-call | tf_op jit(solution)/shard_map/load/pallas_call | solution.py:287
  30.6 1.6 %layer.5.refs_9_ = f32[64,2048]{1,0:T(8,128)S(1)} custom-call(bf16[16,2176]{1,0:T(8,128)(2,1)S(1)} %shard_map.101.refs_0_.refs_4_, bf16[16,2176]{1,0:T(8,128)(2,1)S(1)} %collective-permute-done.1.refs_1_.refs_5_, bf16[16,2176]{1,0:T(8,128)(2,1)S(1)} %collective-permute-done.2.refs_2_.refs_6_, bf16[16,2176]{1,0:T(8,128)(2,1)S(1)} %collective-permute-done.3.refs_3_.refs_7_, ...), custom_call_target="tpu_custom_call" | custom-call | flops 503316480 | bytes 7864320 | tf_op jit(solution)/shard_map/layer/pallas_call | solution.py:197
  33.1 2.6 %collective-permute-start.7 = (bf16[16,2048]{1,0:T(8,128)(2,1)S(1)}, bf16[16,2048]{1,0:T(8,128)(2,1)S(1)}, u32[]{:S(2)}, u32[]{:S(2)}) collective-permute-start(bf16[16,2048]{1,0:T(8,128)(2,1)S(1)} %get-tuple-element.53), channel_id=1, source_target_pairs={{0,6},{1,7},{2,4},{3,5},{4,2},{5,3},{6,0},{7,1},{8,14},{9,15},{10,... | collective-permute-start | bytes 196616 | tf_op jit(solution)/shard_map/ppermute | solution.py:27
  37.6 2.5 %collective-permute-done.7.refs_1_ = bf16[16,2048]{1,0:T(8,128)(2,1)S(1)} collective-permute-done((bf16[16,2048]{1,0:T(8,128)(2,1)S(1)}, bf16[16,2048]{1,0:T(8,128)(2,1)S(1)}, u32[]{:S(2)}, u32[]{:S(2)}) %collective-permute-start.7) | collective-permute-done | bytes 65568 | tf_op jit(solution)/shard_map/ppermute | solution.py:27
  40.1 3.4 %collective-permute-done.8.refs_2_ = bf16[16,2048]{1,0:T(8,128)(2,1)S(1)} collective-permute-done((bf16[16,2048]{1,0:T(8,128)(2,1)S(1)}, bf16[16,2048]{1,0:T(8,128)(2,1)S(1)}, u32[]{:S(2)}, u32[]{:S(2)}) %collective-permute-start.8) | collective-permute-done | bytes 65568 | tf_op jit(solution)/shard_map/ppermute | solution.py:27
  44.6 3.7 %collective-permute-done.11.refs_1_ = bf16[16,2048]{1,0:T(8,128)(2,1)S(1)} collective-permute-done((bf16[16,2048]{1,0:T(8,128)(2,1)S(1)}, bf16[16,2048]{1,0:T(8,128)(2,1)S(1)}, u32[]{:S(2)}, u32[]{:S(2)}) %collective-permute-start.11) | collective-permute-done | bytes 65568 | tf_op jit(solution)/shard_map/ppermute | solution.py:27
  48.3 1.4 %collective-permute-done.10.refs_0_ = bf16[16,2048]{1,0:T(8,128)(2,1)S(1)} collective-permute-done((bf16[16,2048]{1,0:T(8,128)(2,1)S(1)}, bf16[16,2048]{1,0:T(8,128)(2,1)S(1)}, u32[]{:S(2)}, u32[]{:S(2)}) %collective-permute-start.10) | collective-permute-done | bytes 65568 | tf_op jit(solution)/shard_map/ppermute | solution.py:27
  49.7 1.3 %collective-permute-start.14 = (bf16[16,2048]{1,0:T(8,128)(2,1)S(1)}, bf16[16,2048]{1,0:T(8,128)(2,1)S(1)}, u32[]{:S(2)}, u32[]{:S(2)}) collective-permute-start(bf16[16,2048]{1,0:T(8,128)(2,1)S(1)} %shard_map.103.refs_0_), channel_id=1, source_target_pairs={{0,6},{1,7},{2,4},{3,5},{4,2},{5,3},{6,0},{7,1},{8,14},{9,15},{10,... | collective-permute-start | bytes 196616 | tf_op jit(solution)/shard_map/ppermute | solution.py:27
  51.0 3.1 %collective-permute-start.12 = (bf16[16,2048]{1,0:T(8,128)(2,1)S(1)}, bf16[16,2048]{1,0:T(8,128)(2,1)S(1)}, u32[]{:S(2)}, u32[]{:S(2)}) collective-permute-start(bf16[16,2048]{1,0:T(8,128)(2,1)S(1)} %shard_map.103.refs_0_), channel_id=1, source_target_pairs={{0,2},{1,3},{2,0},{3,1},{4,6},{5,7},{6,4},{7,5},{8,10},{9,11},{10,... | collective-permute-start | bytes 196616 | tf_op jit(solution)/shard_map/ppermute | solution.py:27
  54.1 2.5 %load.4.refs_12_ = bf16[2048,640]{1,0:T(8,128)(2,1)S(1)} custom-call(bf16[2,640,2048]{2,1,0:T(8,128)(2,1)} %bitcast.23), custom_call_target="tpu_custom_call" | custom-call | tf_op jit(solution)/shard_map/load/pallas_call | solution.py:287
  56.7 2.9 %load.5 = (bf16[2048,640]{1,0:T(8,128)(2,1)S(1)}, bf16[640,2048]{1,0:T(8,128)(2,1)S(1)}) custom-call(bf16[2,640,2048]{2,1,0:T(8,128)(2,1)} %bitcast.19, bf16[2,640,2048]{2,1,0:T(8,128)(2,1)} %bitcast.21), custom_call_target="tpu_custom_call" | custom-call | tf_op jit(solution)/shard_map/load/pallas_call | solution.py:287
  59.6 2.5 %layer.7 = (f32[16,2048]{1,0:T(8,128)S(1)}, bf16[16,2048]{1,0:T(8,128)(2,1)S(1)}, bf16[16,2048]{1,0:T(8,128)(2,1)S(1)}, bf16[16,2048]{1,0:T(8,128)(2,1)S(1)}) custom-call(bf16[16,2048]{1,0:T(8,128)(2,1)S(1)} %shard_map.103.refs_0_, bf16[16,2048]{1,0:T(8,128)(2,1)S(1)} %collective-permute-done.12.refs_1_, ...), custom_call_target="tpu_custom_call" | custom-call | flops 629145600 | bytes 9830400 | tf_op jit(solution)/shard_map/layer/pallas_call | solution.py:197
  62.2 1.3 %collective-permute-start.16 = (bf16[16,2048]{1,0:T(8,128)(2,1)S(1)}, bf16[16,2048]{1,0:T(8,128)(2,1)S(1)}, u32[]{:S(2)}, u32[]{:S(2)}) collective-permute-start(bf16[16,2048]{1,0:T(8,128)(2,1)S(1)} %get-tuple-element.65), channel_id=1, source_target_pairs={{0,6},{1,7},{2,4},{3,5},{4,2},{5,3},{6,0},{7,1},{8,14},{9,15},{10,... | collective-permute-start | bytes 196616 | tf_op jit(solution)/shard_map/ppermute | solution.py:27
  63.7 2.9 %collective-permute-start.18 = (bf16[16,2048]{1,0:T(8,128)(2,1)S(1)}, bf16[16,2048]{1,0:T(8,128)(2,1)S(1)}, u32[]{:S(2)}, u32[]{:S(2)}) collective-permute-start(bf16[16,2048]{1,0:T(8,128)(2,1)S(1)} %get-tuple-element.67), channel_id=1, source_target_pairs={{0,2},{1,3},{2,0},{3,1},{4,6},{5,7},{6,4},{7,5},{8,10},{9,11},{10,... | collective-permute-start | bytes 196616 | tf_op jit(solution)/shard_map/ppermute | solution.py:27
  66.6 1.7 %collective-permute-done.16.refs_1_ = bf16[16,2048]{1,0:T(8,128)(2,1)S(1)} collective-permute-done((bf16[16,2048]{1,0:T(8,128)(2,1)S(1)}, bf16[16,2048]{1,0:T(8,128)(2,1)S(1)}, u32[]{:S(2)}, u32[]{:S(2)}) %collective-permute-start.16) | collective-permute-done | bytes 65568 | tf_op jit(solution)/shard_map/ppermute | solution.py:27
  68.3 1.4 %collective-permute-done.17.refs_2_ = bf16[16,2048]{1,0:T(8,128)(2,1)S(1)} collective-permute-done((bf16[16,2048]{1,0:T(8,128)(2,1)S(1)}, bf16[16,2048]{1,0:T(8,128)(2,1)S(1)}, u32[]{:S(2)}, u32[]{:S(2)}) %collective-permute-start.17) | collective-permute-done | bytes 65568 | tf_op jit(solution)/shard_map/ppermute | solution.py:27
  70.4 4.0 %collective-permute-done.20.refs_1_ = bf16[16,2048]{1,0:T(8,128)(2,1)S(1)} collective-permute-done((bf16[16,2048]{1,0:T(8,128)(2,1)S(1)}, bf16[16,2048]{1,0:T(8,128)(2,1)S(1)}, u32[]{:S(2)}, u32[]{:S(2)}) %collective-permute-start.20) | collective-permute-done | bytes 65568 | tf_op jit(solution)/shard_map/ppermute | solution.py:27
  74.4 1.6 %collective-permute-start.23 = (bf16[16,2048]{1,0:T(8,128)(2,1)S(1)}, bf16[16,2048]{1,0:T(8,128)(2,1)S(1)}, u32[]{:S(2)}, u32[]{:S(2)}) collective-permute-start(bf16[16,2048]{1,0:T(8,128)(2,1)S(1)} %shard_map.105.refs_0_), channel_id=1, source_target_pairs={{0,6},{1,7},{2,4},{3,5},{4,2},{5,3},{6,0},{7,1},{8,14},{9,15},{10,... | collective-permute-start | bytes 196616 | tf_op jit(solution)/shard_map/ppermute | solution.py:27
  77.1 1.7 %collective-permute-start.21 = (bf16[16,2048]{1,0:T(8,128)(2,1)S(1)}, bf16[16,2048]{1,0:T(8,128)(2,1)S(1)}, u32[]{:S(2)}, u32[]{:S(2)}) collective-permute-start(bf16[16,2048]{1,0:T(8,128)(2,1)S(1)} %shard_map.105.refs_0_), channel_id=1, source_target_pairs={{0,2},{1,3},{2,0},{3,1},{4,6},{5,7},{6,4},{7,5},{8,10},{9,11},{10,... | collective-permute-start | bytes 196616 | tf_op jit(solution)/shard_map/ppermute | solution.py:27
  78.9 1.8 %collective-permute-done.23.refs_3_ = bf16[16,2048]{1,0:T(8,128)(2,1)S(1)} collective-permute-done((bf16[16,2048]{1,0:T(8,128)(2,1)S(1)}, bf16[16,2048]{1,0:T(8,128)(2,1)S(1)}, u32[]{:S(2)}, u32[]{:S(2)}) %collective-permute-start.23) | collective-permute-done | bytes 65568 | tf_op jit(solution)/shard_map/ppermute | solution.py:27
  80.6 1.5 %collective-permute-done.22.refs_2_ = bf16[16,2048]{1,0:T(8,128)(2,1)S(1)} collective-permute-done((bf16[16,2048]{1,0:T(8,128)(2,1)S(1)}, bf16[16,2048]{1,0:T(8,128)(2,1)S(1)}, u32[]{:S(2)}, u32[]{:S(2)}) %collective-permute-start.22) | collective-permute-done | bytes 65568 | tf_op jit(solution)/shard_map/ppermute | solution.py:27
  82.2 2.7 %layer.8 = (f32[16,2048]{1,0:T(8,128)S(1)}, bf16[16,2048]{1,0:T(8,128)(2,1)S(1)}, bf16[16,2048]{1,0:T(8,128)(2,1)S(1)}, bf16[16,2048]{1,0:T(8,128)(2,1)S(1)}) custom-call(bf16[16,2048]{1,0:T(8,128)(2,1)S(1)} %shard_map.105.refs_0_, bf16[16,2048]{1,0:T(8,128)(2,1)S(1)} %collective-permute-done.21.refs_1_, ...), custom_call_target="tpu_custom_call" | custom-call | flops 629145600 | bytes 9830400 | tf_op jit(solution)/shard_map/layer/pallas_call | solution.py:197
  84.9 1.8 %collective-permute-start.25 = (bf16[16,2048]{1,0:T(8,128)(2,1)S(1)}, bf16[16,2048]{1,0:T(8,128)(2,1)S(1)}, u32[]{:S(2)}, u32[]{:S(2)}) collective-permute-start(bf16[16,2048]{1,0:T(8,128)(2,1)S(1)} %get-tuple-element.70), channel_id=1, source_target_pairs={{0,6},{1,7},{2,4},{3,5},{4,2},{5,3},{6,0},{7,1},{8,14},{9,15},{10,... | collective-permute-start | bytes 196616 | tf_op jit(solution)/shard_map/ppermute | solution.py:27
  87.4 2.0 %collective-permute-start.27 = (bf16[16,2048]{1,0:T(8,128)(2,1)S(1)}, bf16[16,2048]{1,0:T(8,128)(2,1)S(1)}, u32[]{:S(2)}, u32[]{:S(2)}) collective-permute-start(bf16[16,2048]{1,0:T(8,128)(2,1)S(1)} %get-tuple-element.72), channel_id=1, source_target_pairs={{0,2},{1,3},{2,0},{3,1},{4,6},{5,7},{6,4},{7,5},{8,10},{9,11},{10,... | collective-permute-start | bytes 196616 | tf_op jit(solution)/shard_map/ppermute | solution.py:27
  89.3 2.0 %collective-permute-done.25.refs_1_ = bf16[16,2048]{1,0:T(8,128)(2,1)S(1)} collective-permute-done((bf16[16,2048]{1,0:T(8,128)(2,1)S(1)}, bf16[16,2048]{1,0:T(8,128)(2,1)S(1)}, u32[]{:S(2)}, u32[]{:S(2)}) %collective-permute-start.25) | collective-permute-done | bytes 65568 | tf_op jit(solution)/shard_map/ppermute | solution.py:27
  91.3 1.4 %collective-permute-done.26.refs_2_ = bf16[16,2048]{1,0:T(8,128)(2,1)S(1)} collective-permute-done((bf16[16,2048]{1,0:T(8,128)(2,1)S(1)}, bf16[16,2048]{1,0:T(8,128)(2,1)S(1)}, u32[]{:S(2)}, u32[]{:S(2)}) %collective-permute-start.26) | collective-permute-done | bytes 65568 | tf_op jit(solution)/shard_map/ppermute | solution.py:27
  92.7 1.8 %collective-permute-start.29 = (bf16[16,2048]{1,0:T(8,128)(2,1)S(1)}, bf16[16,2048]{1,0:T(8,128)(2,1)S(1)}, u32[]{:S(2)}, u32[]{:S(2)}) collective-permute-start(bf16[16,2048]{1,0:T(8,128)(2,1)S(1)} %shard_map.106), channel_id=1, source_target_pairs={{0,9},{1,8},{2,11},{3,10},{4,13},{5,12},{6,15},{7,14},{8,17},{9,16... | collective-permute-start | bytes 196616 | tf_op jit(solution)/shard_map/ppermute | solution.py:27
  95.2 2.9 %collective-permute-done.29.refs_1_ = bf16[16,2048]{1,0:T(8,128)(2,1)S(1)} collective-permute-done((bf16[16,2048]{1,0:T(8,128)(2,1)S(1)}, bf16[16,2048]{1,0:T(8,128)(2,1)S(1)}, u32[]{:S(2)}, u32[]{:S(2)}) %collective-permute-start.29) | collective-permute-done | bytes 65568 | tf_op jit(solution)/shard_map/ppermute | solution.py:27
  98.6 1.8 %collective-permute-start.32 = (bf16[16,2048]{1,0:T(8,128)(2,1)S(1)}, bf16[16,2048]{1,0:T(8,128)(2,1)S(1)}, u32[]{:S(2)}, u32[]{:S(2)}) collective-permute-start(bf16[16,2048]{1,0:T(8,128)(2,1)S(1)} %shard_map.107.refs_0_), channel_id=1, source_target_pairs={{0,6},{1,7},{2,4},{3,5},{4,2},{5,3},{6,0},{7,1},{8,14},{9,15},{10,... | collective-permute-start | bytes 196616 | tf_op jit(solution)/shard_map/ppermute | solution.py:27
  100.8 2.2 %collective-permute-start.30 = (bf16[16,2048]{1,0:T(8,128)(2,1)S(1)}, bf16[16,2048]{1,0:T(8,128)(2,1)S(1)}, u32[]{:S(2)}, u32[]{:S(2)}) collective-permute-start(bf16[16,2048]{1,0:T(8,128)(2,1)S(1)} %shard_map.107.refs_0_), channel_id=1, source_target_pairs={{0,2},{1,3},{2,0},{3,1},{4,6},{5,7},{6,4},{7,5},{8,10},{9,11},{10,... | collective-permute-start | bytes 196616 | tf_op jit(solution)/shard_map/ppermute | solution.py:27
  103.0 2.3 %collective-permute-done.32.refs_3_ = bf16[16,2048]{1,0:T(8,128)(2,1)S(1)} collective-permute-done((bf16[16,2048]{1,0:T(8,128)(2,1)S(1)}, bf16[16,2048]{1,0:T(8,128)(2,1)S(1)}, u32[]{:S(2)}, u32[]{:S(2)}) %collective-permute-start.32) | collective-permute-done | bytes 65568 | tf_op jit(solution)/shard_map/ppermute | solution.py:27
  105.3 1.8 %collective-permute-done.31.refs_2_ = bf16[16,2048]{1,0:T(8,128)(2,1)S(1)} collective-permute-done((bf16[16,2048]{1,0:T(8,128)(2,1)S(1)}, bf16[16,2048]{1,0:T(8,128)(2,1)S(1)}, u32[]{:S(2)}, u32[]{:S(2)}) %collective-permute-start.31) | collective-permute-done | bytes 65568 | tf_op jit(solution)/shard_map/ppermute | solution.py:27
  107.1 2.5 %layer.9 = (f32[16,2048]{1,0:T(8,128)S(1)}, bf16[16,2048]{1,0:T(8,128)(2,1)S(1)}, bf16[16,2048]{1,0:T(8,128)(2,1)S(1)}, bf16[16,2048]{1,0:T(8,128)(2,1)S(1)}) custom-call(bf16[16,2048]{1,0:T(8,128)(2,1)S(1)} %shard_map.107.refs_0_, bf16[16,2048]{1,0:T(8,128)(2,1)S(1)} %collective-permute-done.30.refs_1_, ...), custom_call_target="tpu_custom_call" | custom-call | flops 629145600 | bytes 9830400 | tf_op jit(solution)/shard_map/layer/pallas_call | solution.py:197
  109.6 1.8 %collective-permute-start.33 = (bf16[16,2048]{1,0:T(8,128)(2,1)S(1)}, bf16[16,2048]{1,0:T(8,128)(2,1)S(1)}, u32[]{:S(2)}, u32[]{:S(2)}) collective-permute-start(bf16[16,2048]{1,0:T(8,128)(2,1)S(1)} %get-tuple-element.74), channel_id=1, source_target_pairs={{0,6},{1,7},{2,4},{3,5},{4,2},{5,3},{6,0},{7,1},{8,14},{9,15},{10,... | collective-permute-start | bytes 196616 | tf_op jit(solution)/shard_map/ppermute | solution.py:27
  111.5 2.6 %collective-permute-start.35 = (bf16[16,2048]{1,0:T(8,128)(2,1)S(1)}, bf16[16,2048]{1,0:T(8,128)(2,1)S(1)}, u32[]{:S(2)}, u32[]{:S(2)}) collective-permute-start(bf16[16,2048]{1,0:T(8,128)(2,1)S(1)} %get-tuple-element.76), channel_id=1, source_target_pairs={{0,2},{1,3},{2,0},{3,1},{4,6},{5,7},{6,4},{7,5},{8,10},{9,11},{10,... | collective-permute-start | bytes 196616 | tf_op jit(solution)/shard_map/ppermute | solution.py:27
  114.1 2.0 %collective-permute-done.33 = bf16[16,2048]{1,0:T(8,128)(2,1)S(1)} collective-permute-done((bf16[16,2048]{1,0:T(8,128)(2,1)S(1)}, bf16[16,2048]{1,0:T(8,128)(2,1)S(1)}, u32[]{:S(2)}, u32[]{:S(2)}) %collective-permute-start.33) | collective-permute-done | bytes 65568 | tf_op jit(solution)/shard_map/ppermute | solution.py:27
  116.1 1.7 %collective-permute-done.34 = bf16[16,2048]{1,0:T(8,128)(2,1)S(1)} collective-permute-done((bf16[16,2048]{1,0:T(8,128)(2,1)S(1)}, bf16[16,2048]{1,0:T(8,128)(2,1)S(1)}, u32[]{:S(2)}, u32[]{:S(2)}) %collective-permute-start.34) | collective-permute-done | bytes 65568 | tf_op jit(solution)/shard_map/ppermute | solution.py:27
  117.8 1.8 %collective-permute-start.36 = (bf16[8,2048]{1,0:T(8,128)(2,1)S(1)}, bf16[8,2048]{1,0:T(8,128)(2,1)S(1)}, u32[]{:S(2)}, u32[]{:S(2)}) collective-permute-start(bf16[8,2048]{1,0:T(8,128)(2,1)S(1)} %slice.17), channel_id=1, source_target_pairs={{0,1},{1,0},{2,3},{3,2},{4,5},{5,4},{6,7},{7,6},{8,9},{9,8},{10,11... | collective-permute-start | bytes 98312 | tf_op jit(solution)/shard_map/ppermute | solution.py:27
  119.6 2.2 %collective-permute-done.36 = bf16[8,2048]{1,0:T(8,128)(2,1)S(1)} collective-permute-done((bf16[8,2048]{1,0:T(8,128)(2,1)S(1)}, bf16[8,2048]{1,0:T(8,128)(2,1)S(1)}, u32[]{:S(2)}, u32[]{:S(2)}) %collective-permute-start.36) | collective-permute-done | bytes 32800 | tf_op jit(solution)/shard_map/ppermute | solution.py:27
  (56 shorter events, 14.2 us)
Async XLA Ops:
  0.0 5.7 %copy-start.3 = (f32[4,1,8,2]{2,3,1,0:T(2,128)S(1)}, f32[4,1,8,2]{2,3,1,0:T(2,128)}, u32[]{:S(2)}) copy-start(f32[4,1,8,2]{2,3,1,0:T(2,128)} %param.12) | copy-start | bytes 772
  0.0 5.7 %copy-start.2 = (s32[4,1,8,2]{2,3,1,0:T(2,128)S(1)}, s32[4,1,8,2]{2,3,1,0:T(2,128)}, u32[]{:S(2)}) copy-start(s32[4,1,8,2]{2,3,1,0:T(2,128)} %param.11) | copy-start | bytes 772
  0.0 5.7 %copy-start.1 = (bf16[1,8,2048]{2,1,0:T(8,128)(2,1)S(1)}, bf16[1,8,2048]{2,1,0:T(8,128)(2,1)}, u32[]{:S(2)}) copy-start(bf16[1,8,2048]{2,1,0:T(8,128)(2,1)} %param.10) | copy-start | bytes 98308
  1.1 31.0 %collective-permute-start.4 = (bf16[160,2048]{1,0:T(8,128)(2,1)S(1)}, bf16[160,2048]{1,0:T(8,128)(2,1)S(1)}, u32[]{:S(2)}, u32[]{:S(2)}) collective-permute-start(bf16[160,2048]{1,0:T(8,128)(2,1)S(1)} %fill.2), channel_id=1, source_target_pairs={{0,24},{1,25},{2,26},{3,27},{4,28},{5,29},{6,30},{7,31},{8,0},{9,1... | collective-permute-start | bytes 1966088 | tf_op jit(solution)/shard_map/ppermute | solution.py:27
  4.9 27.2 %collective-permute-start.5 = (bf16[160,2048]{1,0:T(8,128)(2,1)S(1)}, bf16[160,2048]{1,0:T(8,128)(2,1)S(1)}, u32[]{:S(2)}, u32[]{:S(2)}) collective-permute-start(bf16[160,2048]{1,0:T(8,128)(2,1)S(1)} %get-tuple-element.50), channel_id=1, source_target_pairs={{0,24},{1,25},{2,26},{3,27},{4,28},{5,29},{6,30},{7,31},{8,0},{9,1... | collective-permute-start | bytes 1966088 | tf_op jit(solution)/shard_map/ppermute | solution.py:27
  5.7 26.5 %collective-permute-start.6 = (bf16[160,2048]{1,0:T(8,128)(2,1)S(1)}, bf16[160,2048]{1,0:T(8,128)(2,1)S(1)}, u32[]{:S(2)}, u32[]{:S(2)}) collective-permute-start(bf16[160,2048]{1,0:T(8,128)(2,1)S(1)} %get-tuple-element.51), channel_id=1, source_target_pairs={{0,24},{1,25},{2,26},{3,27},{4,28},{5,29},{6,30},{7,31},{8,0},{9,1... | collective-permute-start | bytes 1966088 | tf_op jit(solution)/shard_map/ppermute | solution.py:27
  6.0 3.9 %collective-permute-start = (bf16[8,2176]{1,0:T(8,128)(2,1)S(1)}, bf16[8,2176]{1,0:T(8,128)(2,1)S(1)}, u32[]{:S(2)}, u32[]{:S(2)}) collective-permute-start(bf16[8,2176]{1,0:T(8,128)(2,1)S(1)} %shard_map.100.first_ref), channel_id=1, source_target_pairs={{0,1},{1,0},{2,3},{3,2},{4,5},{5,4},{6,7},{7,6},{8,9},{9,8},{10,11... | collective-permute-start | bytes 104456 | tf_op jit(solution)/shard_map/ppermute | solution.py:27
  10.0 4.4 %collective-permute-start.1 = (bf16[16,2176]{1,0:T(8,128)(2,1)S(1)}, bf16[16,2176]{1,0:T(8,128)(2,1)S(1)}, u32[]{:S(2)}, u32[]{:S(2)}) collective-permute-start(bf16[16,2176]{1,0:T(8,128)(2,1)S(1)} %shard_map.101.refs_0_.refs_4_), channel_id=1, source_target_pairs={{0,2},{1,3},{2,0},{3,1},{4,6},{5,7},{6,4},{7,5},{8,10},{9,11},{10,... | collective-permute-start | bytes 208904 | tf_op jit(solution)/shard_map/ppermute | solution.py:27
  15.9 43.8 %collective-permute-start.15 = (bf16[3,160,2048]{2,1,0:T(8,128)(2,1)S(1)}, bf16[3,160,2048]{2,1,0:T(8,128)(2,1)S(1)}, u32[]{:S(2)}, u32[]{:S(2)}) collective-permute-start(bf16[3,160,2048]{2,1,0:T(8,128)(2,1)S(1)} %stack.1), channel_id=1, source_target_pairs={{0,8},{1,9},{2,10},{3,11},{4,12},{5,13},{6,14},{7,15},{8,0},{9,1},... | collective-permute-start | bytes 5898248 | tf_op jit(solution)/shard_map/ppermute | solution.py:58
  17.8 6.6 %collective-permute-start.3 = (bf16[16,2176]{1,0:T(8,128)(2,1)S(1)}, bf16[16,2176]{1,0:T(8,128)(2,1)S(1)}, u32[]{:S(2)}, u32[]{:S(2)}) collective-permute-start(bf16[16,2176]{1,0:T(8,128)(2,1)S(1)} %shard_map.101.refs_0_.refs_4_), channel_id=1, source_target_pairs={{0,6},{1,7},{2,4},{3,5},{4,2},{5,3},{6,0},{7,1},{8,14},{9,15},{10,... | collective-permute-start | bytes 208904 | tf_op jit(solution)/shard_map/ppermute | solution.py:27
  24.4 6.2 %collective-permute-start.2 = (bf16[16,2176]{1,0:T(8,128)(2,1)S(1)}, bf16[16,2176]{1,0:T(8,128)(2,1)S(1)}, u32[]{:S(2)}, u32[]{:S(2)}) collective-permute-start(bf16[16,2176]{1,0:T(8,128)(2,1)S(1)} %shard_map.101.refs_0_.refs_4_), channel_id=1, source_target_pairs={{0,4},{1,5},{2,6},{3,7},{4,0},{5,1},{6,2},{7,3},{8,12},{9,13},{10,... | collective-permute-start | bytes 208904 | tf_op jit(solution)/shard_map/ppermute | solution.py:27
  25.0 5.5 %copy-start = (f32[2,1,2048]{2,1,0:T(1,128)S(1)}, f32[2,1,2048]{2,1,0:T(1,128)}, u32[]{:S(2)}) copy-start(f32[2,1,2048]{2,1,0:T(1,128)} %refs_8_.9) | copy-start | bytes 49156
  33.1 49.1 %collective-permute-start.24 = (bf16[3,160,2048]{2,1,0:T(8,128)(2,1)S(1)}, bf16[3,160,2048]{2,1,0:T(8,128)(2,1)S(1)}, u32[]{:S(2)}, u32[]{:S(2)}) collective-permute-start(bf16[3,160,2048]{2,1,0:T(8,128)(2,1)S(1)} %stack.1), channel_id=1, source_target_pairs={{0,24},{1,25},{2,26},{3,27},{4,28},{5,29},{6,30},{7,31},{8,0},{9,1... | collective-permute-start | bytes 5898248 | tf_op jit(solution)/shard_map/ppermute | solution.py:27
  33.1 6.9 %collective-permute-start.7 = (bf16[16,2048]{1,0:T(8,128)(2,1)S(1)}, bf16[16,2048]{1,0:T(8,128)(2,1)S(1)}, u32[]{:S(2)}, u32[]{:S(2)}) collective-permute-start(bf16[16,2048]{1,0:T(8,128)(2,1)S(1)} %get-tuple-element.53), channel_id=1, source_target_pairs={{0,6},{1,7},{2,4},{3,5},{4,2},{5,3},{6,0},{7,1},{8,14},{9,15},{10,... | collective-permute-start | bytes 196616 | tf_op jit(solution)/shard_map/ppermute | solution.py:27
  35.7 7.8 %collective-permute-start.8 = (bf16[16,2048]{1,0:T(8,128)(2,1)S(1)}, bf16[16,2048]{1,0:T(8,128)(2,1)S(1)}, u32[]{:S(2)}, u32[]{:S(2)}) collective-permute-start(bf16[16,2048]{1,0:T(8,128)(2,1)S(1)} %get-tuple-element.54), channel_id=1, source_target_pairs={{0,4},{1,5},{2,6},{3,7},{4,0},{5,1},{6,2},{7,3},{8,12},{9,13},{10,... | collective-permute-start | bytes 196616 | tf_op jit(solution)/shard_map/ppermute | solution.py:27
  36.9 6.6 %collective-permute-start.9 = (bf16[16,2048]{1,0:T(8,128)(2,1)S(1)}, bf16[16,2048]{1,0:T(8,128)(2,1)S(1)}, u32[]{:S(2)}, u32[]{:S(2)}) collective-permute-start(bf16[16,2048]{1,0:T(8,128)(2,1)S(1)} %get-tuple-element.55), channel_id=1, source_target_pairs={{0,2},{1,3},{2,0},{3,1},{4,6},{5,7},{6,4},{7,5},{8,10},{9,11},{10,... | collective-permute-start | bytes 196616 | tf_op jit(solution)/shard_map/ppermute | solution.py:27
  43.5 4.7 %collective-permute-start.11 = (bf16[16,2048]{1,0:T(8,128)(2,1)S(1)}, bf16[16,2048]{1,0:T(8,128)(2,1)S(1)}, u32[]{:S(2)}, u32[]{:S(2)}) collective-permute-start(bf16[16,2048]{1,0:T(8,128)(2,1)S(1)} %shard_map.102), channel_id=1, source_target_pairs={{0,9},{1,8},{2,11},{3,10},{4,13},{5,12},{6,15},{7,14},{8,17},{9,16... | collective-permute-start | bytes 196616 | tf_op jit(solution)/shard_map/ppermute | solution.py:27
  44.6 5.1 %collective-permute-start.10 = (bf16[16,2048]{1,0:T(8,128)(2,1)S(1)}, bf16[16,2048]{1,0:T(8,128)(2,1)S(1)}, u32[]{:S(2)}, u32[]{:S(2)}) collective-permute-start(bf16[16,2048]{1,0:T(8,128)(2,1)S(1)} %shard_map.102), channel_id=1, source_target_pairs={{0,8},{1,9},{2,10},{3,11},{4,12},{5,13},{6,14},{7,15},{8,16},{9,17... | collective-permute-start | bytes 196616 | tf_op jit(solution)/shard_map/ppermute | solution.py:27
  49.7 9.9 %collective-permute-start.14 = (bf16[16,2048]{1,0:T(8,128)(2,1)S(1)}, bf16[16,2048]{1,0:T(8,128)(2,1)S(1)}, u32[]{:S(2)}, u32[]{:S(2)}) collective-permute-start(bf16[16,2048]{1,0:T(8,128)(2,1)S(1)} %shard_map.103.refs_0_), channel_id=1, source_target_pairs={{0,6},{1,7},{2,4},{3,5},{4,2},{5,3},{6,0},{7,1},{8,14},{9,15},{10,... | collective-permute-start | bytes 196616 | tf_op jit(solution)/shard_map/ppermute | solution.py:27
  51.0 8.6 %collective-permute-start.13 = (bf16[16,2048]{1,0:T(8,128)(2,1)S(1)}, bf16[16,2048]{1,0:T(8,128)(2,1)S(1)}, u32[]{:S(2)}, u32[]{:S(2)}) collective-permute-start(bf16[16,2048]{1,0:T(8,128)(2,1)S(1)} %shard_map.103.refs_0_), channel_id=1, source_target_pairs={{0,4},{1,5},{2,6},{3,7},{4,0},{5,1},{6,2},{7,3},{8,12},{9,13},{10,... | collective-permute-start | bytes 196616 | tf_op jit(solution)/shard_map/ppermute | solution.py:27
  51.0 8.6 %collective-permute-start.12 = (bf16[16,2048]{1,0:T(8,128)(2,1)S(1)}, bf16[16,2048]{1,0:T(8,128)(2,1)S(1)}, u32[]{:S(2)}, u32[]{:S(2)}) collective-permute-start(bf16[16,2048]{1,0:T(8,128)(2,1)S(1)} %shard_map.103.refs_0_), channel_id=1, source_target_pairs={{0,2},{1,3},{2,0},{3,1},{4,6},{5,7},{6,4},{7,5},{8,10},{9,11},{10,... | collective-permute-start | bytes 196616 | tf_op jit(solution)/shard_map/ppermute | solution.py:27
  62.2 6.2 %collective-permute-start.16 = (bf16[16,2048]{1,0:T(8,128)(2,1)S(1)}, bf16[16,2048]{1,0:T(8,128)(2,1)S(1)}, u32[]{:S(2)}, u32[]{:S(2)}) collective-permute-start(bf16[16,2048]{1,0:T(8,128)(2,1)S(1)} %get-tuple-element.65), channel_id=1, source_target_pairs={{0,6},{1,7},{2,4},{3,5},{4,2},{5,3},{6,0},{7,1},{8,14},{9,15},{10,... | collective-permute-start | bytes 196616 | tf_op jit(solution)/shard_map/ppermute | solution.py:27
  63.5 6.2 %collective-permute-start.17 = (bf16[16,2048]{1,0:T(8,128)(2,1)S(1)}, bf16[16,2048]{1,0:T(8,128)(2,1)S(1)}, u32[]{:S(2)}, u32[]{:S(2)}) collective-permute-start(bf16[16,2048]{1,0:T(8,128)(2,1)S(1)} %get-tuple-element.66), channel_id=1, source_target_pairs={{0,4},{1,5},{2,6},{3,7},{4,0},{5,1},{6,2},{7,3},{8,12},{9,13},{10,... | collective-permute-start | bytes 196616 | tf_op jit(solution)/shard_map/ppermute | solution.py:27
  63.7 6.0 %collective-permute-start.18 = (bf16[16,2048]{1,0:T(8,128)(2,1)S(1)}, bf16[16,2048]{1,0:T(8,128)(2,1)S(1)}, u32[]{:S(2)}, u32[]{:S(2)}) collective-permute-start(bf16[16,2048]{1,0:T(8,128)(2,1)S(1)} %get-tuple-element.67), channel_id=1, source_target_pairs={{0,2},{1,3},{2,0},{3,1},{4,6},{5,7},{6,4},{7,5},{8,10},{9,11},{10,... | collective-permute-start | bytes 196616 | tf_op jit(solution)/shard_map/ppermute | solution.py:27
  69.7 4.6 %collective-permute-start.20 = (bf16[16,2048]{1,0:T(8,128)(2,1)S(1)}, bf16[16,2048]{1,0:T(8,128)(2,1)S(1)}, u32[]{:S(2)}, u32[]{:S(2)}) collective-permute-start(bf16[16,2048]{1,0:T(8,128)(2,1)S(1)} %shard_map.104), channel_id=1, source_target_pairs={{0,9},{1,8},{2,11},{3,10},{4,13},{5,12},{6,15},{7,14},{8,17},{9,16... | collective-permute-start | bytes 196616 | tf_op jit(solution)/shard_map/ppermute | solution.py:27
  69.8 4.6 %collective-permute-start.19 = (bf16[16,2048]{1,0:T(8,128)(2,1)S(1)}, bf16[16,2048]{1,0:T(8,128)(2,1)S(1)}, u32[]{:S(2)}, u32[]{:S(2)}) collective-permute-start(bf16[16,2048]{1,0:T(8,128)(2,1)S(1)} %shard_map.104), channel_id=1, source_target_pairs={{0,8},{1,9},{2,10},{3,11},{4,12},{5,13},{6,14},{7,15},{8,16},{9,17... | collective-permute-start | bytes 196616 | tf_op jit(solution)/shard_map/ppermute | solution.py:27
  74.4 6.2 %collective-permute-start.23 = (bf16[16,2048]{1,0:T(8,128)(2,1)S(1)}, bf16[16,2048]{1,0:T(8,128)(2,1)S(1)}, u32[]{:S(2)}, u32[]{:S(2)}) collective-permute-start(bf16[16,2048]{1,0:T(8,128)(2,1)S(1)} %shard_map.105.refs_0_), channel_id=1, source_target_pairs={{0,6},{1,7},{2,4},{3,5},{4,2},{5,3},{6,0},{7,1},{8,14},{9,15},{10,... | collective-permute-start | bytes 196616 | tf_op jit(solution)/shard_map/ppermute | solution.py:27
  76.0 6.2 %collective-permute-start.22 = (bf16[16,2048]{1,0:T(8,128)(2,1)S(1)}, bf16[16,2048]{1,0:T(8,128)(2,1)S(1)}, u32[]{:S(2)}, u32[]{:S(2)}) collective-permute-start(bf16[16,2048]{1,0:T(8,128)(2,1)S(1)} %shard_map.105.refs_0_), channel_id=1, source_target_pairs={{0,4},{1,5},{2,6},{3,7},{4,0},{5,1},{6,2},{7,3},{8,12},{9,13},{10,... | collective-permute-start | bytes 196616 | tf_op jit(solution)/shard_map/ppermute | solution.py:27
  77.1 5.0 %collective-permute-start.21 = (bf16[16,2048]{1,0:T(8,128)(2,1)S(1)}, bf16[16,2048]{1,0:T(8,128)(2,1)S(1)}, u32[]{:S(2)}, u32[]{:S(2)}) collective-permute-start(bf16[16,2048]{1,0:T(8,128)(2,1)S(1)} %shard_map.105.refs_0_), channel_id=1, source_target_pairs={{0,2},{1,3},{2,0},{3,1},{4,6},{5,7},{6,4},{7,5},{8,10},{9,11},{10,... | collective-permute-start | bytes 196616 | tf_op jit(solution)/shard_map/ppermute | solution.py:27
  84.9 6.4 %collective-permute-start.25 = (bf16[16,2048]{1,0:T(8,128)(2,1)S(1)}, bf16[16,2048]{1,0:T(8,128)(2,1)S(1)}, u32[]{:S(2)}, u32[]{:S(2)}) collective-permute-start(bf16[16,2048]{1,0:T(8,128)(2,1)S(1)} %get-tuple-element.70), channel_id=1, source_target_pairs={{0,6},{1,7},{2,4},{3,5},{4,2},{5,3},{6,0},{7,1},{8,14},{9,15},{10,... | collective-permute-start | bytes 196616 | tf_op jit(solution)/shard_map/ppermute | solution.py:27
  86.7 6.0 %collective-permute-start.26 = (bf16[16,2048]{1,0:T(8,128)(2,1)S(1)}, bf16[16,2048]{1,0:T(8,128)(2,1)S(1)}, u32[]{:S(2)}, u32[]{:S(2)}) collective-permute-start(bf16[16,2048]{1,0:T(8,128)(2,1)S(1)} %get-tuple-element.71), channel_id=1, source_target_pairs={{0,4},{1,5},{2,6},{3,7},{4,0},{5,1},{6,2},{7,3},{8,12},{9,13},{10,... | collective-permute-start | bytes 196616 | tf_op jit(solution)/shard_map/ppermute | solution.py:27
  87.4 5.3 %collective-permute-start.27 = (bf16[16,2048]{1,0:T(8,128)(2,1)S(1)}, bf16[16,2048]{1,0:T(8,128)(2,1)S(1)}, u32[]{:S(2)}, u32[]{:S(2)}) collective-permute-start(bf16[16,2048]{1,0:T(8,128)(2,1)S(1)} %get-tuple-element.72), channel_id=1, source_target_pairs={{0,2},{1,3},{2,0},{3,1},{4,6},{5,7},{6,4},{7,5},{8,10},{9,11},{10,... | collective-permute-start | bytes 196616 | tf_op jit(solution)/shard_map/ppermute | solution.py:27
  92.7 5.4 %collective-permute-start.29 = (bf16[16,2048]{1,0:T(8,128)(2,1)S(1)}, bf16[16,2048]{1,0:T(8,128)(2,1)S(1)}, u32[]{:S(2)}, u32[]{:S(2)}) collective-permute-start(bf16[16,2048]{1,0:T(8,128)(2,1)S(1)} %shard_map.106), channel_id=1, source_target_pairs={{0,9},{1,8},{2,11},{3,10},{4,13},{5,12},{6,15},{7,14},{8,17},{9,16... | collective-permute-start | bytes 196616 | tf_op jit(solution)/shard_map/ppermute | solution.py:27
  94.5 4.0 %collective-permute-start.28 = (bf16[16,2048]{1,0:T(8,128)(2,1)S(1)}, bf16[16,2048]{1,0:T(8,128)(2,1)S(1)}, u32[]{:S(2)}, u32[]{:S(2)}) collective-permute-start(bf16[16,2048]{1,0:T(8,128)(2,1)S(1)} %shard_map.106), channel_id=1, source_target_pairs={{0,8},{1,9},{2,10},{3,11},{4,12},{5,13},{6,14},{7,15},{8,16},{9,17... | collective-permute-start | bytes 196616 | tf_op jit(solution)/shard_map/ppermute | solution.py:27
  98.6 6.8 %collective-permute-start.32 = (bf16[16,2048]{1,0:T(8,128)(2,1)S(1)}, bf16[16,2048]{1,0:T(8,128)(2,1)S(1)}, u32[]{:S(2)}, u32[]{:S(2)}) collective-permute-start(bf16[16,2048]{1,0:T(8,128)(2,1)S(1)} %shard_map.107.refs_0_), channel_id=1, source_target_pairs={{0,6},{1,7},{2,4},{3,5},{4,2},{5,3},{6,0},{7,1},{8,14},{9,15},{10,... | collective-permute-start | bytes 196616 | tf_op jit(solution)/shard_map/ppermute | solution.py:27
  100.4 6.8 %collective-permute-start.31 = (bf16[16,2048]{1,0:T(8,128)(2,1)S(1)}, bf16[16,2048]{1,0:T(8,128)(2,1)S(1)}, u32[]{:S(2)}, u32[]{:S(2)}) collective-permute-start(bf16[16,2048]{1,0:T(8,128)(2,1)S(1)} %shard_map.107.refs_0_), channel_id=1, source_target_pairs={{0,4},{1,5},{2,6},{3,7},{4,0},{5,1},{6,2},{7,3},{8,12},{9,13},{10,... | collective-permute-start | bytes 196616 | tf_op jit(solution)/shard_map/ppermute | solution.py:27
  100.8 6.3 %collective-permute-start.30 = (bf16[16,2048]{1,0:T(8,128)(2,1)S(1)}, bf16[16,2048]{1,0:T(8,128)(2,1)S(1)}, u32[]{:S(2)}, u32[]{:S(2)}) collective-permute-start(bf16[16,2048]{1,0:T(8,128)(2,1)S(1)} %shard_map.107.refs_0_), channel_id=1, source_target_pairs={{0,2},{1,3},{2,0},{3,1},{4,6},{5,7},{6,4},{7,5},{8,10},{9,11},{10,... | collective-permute-start | bytes 196616 | tf_op jit(solution)/shard_map/ppermute | solution.py:27
  109.6 6.4 %collective-permute-start.33 = (bf16[16,2048]{1,0:T(8,128)(2,1)S(1)}, bf16[16,2048]{1,0:T(8,128)(2,1)S(1)}, u32[]{:S(2)}, u32[]{:S(2)}) collective-permute-start(bf16[16,2048]{1,0:T(8,128)(2,1)S(1)} %get-tuple-element.74), channel_id=1, source_target_pairs={{0,6},{1,7},{2,4},{3,5},{4,2},{5,3},{6,0},{7,1},{8,14},{9,15},{10,... | collective-permute-start | bytes 196616 | tf_op jit(solution)/shard_map/ppermute | solution.py:27
  111.5 6.3 %collective-permute-start.34 = (bf16[16,2048]{1,0:T(8,128)(2,1)S(1)}, bf16[16,2048]{1,0:T(8,128)(2,1)S(1)}, u32[]{:S(2)}, u32[]{:S(2)}) collective-permute-start(bf16[16,2048]{1,0:T(8,128)(2,1)S(1)} %get-tuple-element.75), channel_id=1, source_target_pairs={{0,4},{1,5},{2,6},{3,7},{4,0},{5,1},{6,2},{7,3},{8,12},{9,13},{10,... | collective-permute-start | bytes 196616 | tf_op jit(solution)/shard_map/ppermute | solution.py:27
  111.5 6.3 %collective-permute-start.35 = (bf16[16,2048]{1,0:T(8,128)(2,1)S(1)}, bf16[16,2048]{1,0:T(8,128)(2,1)S(1)}, u32[]{:S(2)}, u32[]{:S(2)}) collective-permute-start(bf16[16,2048]{1,0:T(8,128)(2,1)S(1)} %get-tuple-element.76), channel_id=1, source_target_pairs={{0,2},{1,3},{2,0},{3,1},{4,6},{5,7},{6,4},{7,5},{8,10},{9,11},{10,... | collective-permute-start | bytes 196616 | tf_op jit(solution)/shard_map/ppermute | solution.py:27
  117.8 4.0 %collective-permute-start.36 = (bf16[8,2048]{1,0:T(8,128)(2,1)S(1)}, bf16[8,2048]{1,0:T(8,128)(2,1)S(1)}, u32[]{:S(2)}, u32[]{:S(2)}) collective-permute-start(bf16[8,2048]{1,0:T(8,128)(2,1)S(1)} %slice.17), channel_id=1, source_target_pairs={{0,1},{1,0},{2,3},{3,2},{4,5},{5,4},{6,7},{7,6},{8,9},{9,8},{10,11... | collective-permute-start | bytes 98312 | tf_op jit(solution)/shard_map/ppermute | solution.py:27

commit v7 on v6

--- a/solution.py
+++ b/solution.py
@@ -125,7 +125,7 @@
         pl.when(second)(bodies[1])
 
 
-def layer_kernel(*refs, tick_idx, blocks, slot_count, spare_counts, tok_dev, width, carried, ends):
+def layer_kernel(*refs, tick_idx, blocks, slot_count, spare_counts, tok_dev, width, carried, ends, lead):
     x_refs, first_refs, refs = refs[:blocks], refs[blocks:2 * blocks], refs[2 * blocks:]
     gain_ref, refs = refs[0], refs[1:]
     if carried:
@@ -172,16 +172,18 @@
     out_refs = refs[:blocks]
     per = 2 * tok_dev
     row = lax.broadcasted_iota(jnp.int32, (per, 1), 0)
-    out_refs[0][...] = total_ref[0:per, :] + jnp.where(row < tok_dev, values[0:per], 0.0)
-    for i in range(1, blocks):
-        out_refs[i][...] = total_ref[i * per:(i + 1) * per, :].astype(jnp.bfloat16)
+    for i in range(blocks):
+        part = total_ref[i * per:(i + 1) * per, :]
+        if lead and i == 0:
+            part = part + jnp.where(row < tok_dev, values[0:per], 0.0)
+        out_refs[i][...] = part.astype(out_refs[i].dtype)
 
 
 def resident(values):
     return [pltpu.with_memory_space_constraint(value, pltpu.VMEM) for value in values]
 
 
-def run_layer(x_blocks, first_blocks, gain, weights, spares, *, tick_idx, tok_dev, carried=None, ends=True):
+def run_layer(x_blocks, first_blocks, gain, weights, spares, *, tick_idx, tok_dev, carried=None, ends=True, lead=True):
     blocks = len(x_blocks)
     width = gain.shape[-1]
     per = 2 * tok_dev
@@ -192,12 +194,13 @@
         values += resident(spare)
     hidden = (0 if carried is not None else weights[0][2].shape[0]) + (spares[0][0].shape[0] if spares else 0)
     whole = jax.ShapeDtypeStruct((rows, width), jnp.float32)
-    parts = [jax.ShapeDtypeStruct((per, width), jnp.float32)]
-    parts += [jax.ShapeDtypeStruct((per, width), jnp.bfloat16)] * (blocks - 1)
+    parts = [
+        jax.ShapeDtypeStruct((per, width), jnp.float32 if lead and i == 0 else jnp.bfloat16) for i in range(blocks)
+    ]
     return pl.pallas_call(
         functools.partial(
             layer_kernel, tick_idx=tick_idx, blocks=blocks, slot_count=len(weights), spare_counts=[len(spare) for spare in spares],
-            tok_dev=tok_dev, width=width, carried=carried is not None, ends=ends,
+            tok_dev=tok_dev, width=width, carried=carried is not None, ends=ends, lead=lead,
         ),
         out_shape=parts if ends else whole,
         in_specs=[WHOLE] * len(values),
@@ -354,9 +357,13 @@
     def fetched(values):
         return [moved(value, 0, -1) for value in values]
 
+    users = [later_users(tick_idx, segments) for tick_idx in range(TICKS)]
+    opening = min([tick_idx for tick_idx in range(TICKS) if users[tick_idx]], default=TICKS)
+    last = outer // 2
+    here = [j for j in range(outer) if j != last]
     head = filled(spare_all[:1], 0)
     head, rest, state, routes, gates = lax.optimization_barrier((head, spare_all[1:], state, routes, gates))
-    spares = [fetched(head + filled(rest, 0))]
+    spares = fetched(head + filled(rest, 0))
     shape = (tok_dev, state.shape[2] + LANES)
     own = small(
         prepare_kernel, jax.ShapeDtypeStruct(shape, state.dtype), state[0],
@@ -367,23 +374,27 @@
     arrived = spread(pair)
     slots = [loaded(weights, (True, True, False), False)]
     late = stacked(lax.optimization_barrier((*spare_all, arrived[1]))[:3], 1)
+    near = [swapped(late, users[opening])] if opening < TICKS else []
     before = run_layer(
         arrived, arrived, norm_gain, slots, [], tick_idx=0, tok_dev=tok_dev, ends=False
     )
 
-    users = [later_users(tick_idx, segments) for tick_idx in range(TICKS)]
-    opening = min([tick_idx for tick_idx in range(TICKS) if users[tick_idx]], default=TICKS)
-    near = [swapped(late, users[opening])] if opening < TICKS else []
-
     x_blocks = arrived
     for tick_idx in range(TICKS):
-        used = [spares[0]]
+        if tick_idx > 0:
+            x_blocks = spread(total)
+        used = [spares]
         if users[tick_idx]:
             used.append(near if users[tick_idx] <= users[opening] else far)
-        parts = run_layer(
-            x_blocks, arrived, norm_gain, slots, used, tick_idx=tick_idx, tok_dev=tok_dev,
-            carried=before if tick_idx == 0 else None,
-        )
+        layer = functools.partial(run_layer, tick_idx=tick_idx, tok_dev=tok_dev)
+        if tick_idx == 0:
+            parts = layer(x_blocks, arrived, norm_gain, slots, used, carried=before)
+        else:
+            most = layer(
+                [x_blocks[j] for j in here], [arrived[j] for j in here], norm_gain, slots, used
+            )
+            rest = layer(x_blocks[last:last + 1], arrived[last:last + 1], norm_gain, slots, used, lead=False)
+            parts = most[:last] + rest + most[last:]
         got = [moved(parts[j], 2 * j, 0) for j in widest_first(outer)]
         if tick_idx == 0:
             far = [moved(lax.optimization_barrier((late, parts[0]))[0], 0, -1)]
@@ -399,7 +410,7 @@
         if tick_idx == 0:
             tied = lax.optimization_barrier((*weights, total))[:3]
             slots.append(gate + loaded(tied[1:], (True, False), True))
-        x_blocks = spread(summed([along, across], swap=True))
+        total = summed([along, across], swap=True)
 
 
 def solution(mesh):

time: 123 us -> 124 us (level)
  Pallas kernels: 24.4 us -> 29.9 us
  starting transfers between devices: 49.8 us -> 44.6 us
    pallas_call x5 -> x8, Pallas kernels: 10.2 us -> 15.7 us  [run_layer(): pl.pallas_call(functools.partial(layer_kernel, tick_idx=tick_idx, blocks=...]
    ppermute x36, starting transfers between devices: 47.8 us -> 42.7 us  [moved(): return lax.ppermute(value, BOTH, pairs)]
  transfers between devices with their start and end apart: 37 -> 37, of which waited for: 22 -> 20; matrix products, arithmetic and copies ran while one was open for 0% -> 0% of each run, Pallas kernels for 15% -> 23%
where the time goes in v7:
time: 124 us
  waiting for transfers between devices  48.1 us (39%)
  starting transfers between devices  44.6 us (36%)
  Pallas kernels  29.9 us (24%)
    ppermute x36, waiting for transfers between devices, moved(): return lax.ppermute(value, BOTH, pairs)  48.1 us
    ppermute x36, starting transfers between devices, moved(): return lax.ppermute(value, BOTH, pairs)  42.7 us
    pallas_call x8, Pallas kernels, run_layer(): pl.pallas_call(functools.partial(layer_kernel, tick_idx=tick_idx, blocks=...  15.7 us
    pallas_call x3, Pallas kernels, loaded(): pl.pallas_call(functools.partial(load_kernel, turned=turned, other=other)...  9.8 us
  transfers between devices with their start and end apart: 37, of which 20 were waited for; matrix products, arithmetic and copies ran while one was open for 0% of the time, Pallas kernels for 23%

profile of v7, /device:TPU:0, one launch (start us, length us, event | category | flops | bytes accessed | tf_op | source)
XLA Modules:
  0.0 123.5 jit_solution(7332925133413007262)
XLA Ops:
  0.0 1.1 fill.2
  1.1 2.5 %collective-permute-start.4 = (bf16[160,2048]{1,0:T(8,128)(2,1)S(1)}, bf16[160,2048]{1,0:T(8,128)(2,1)S(1)}, u32[]{:S(2)}, u32[]{:S(2)}) collective-permute-start(bf16[160,2048]{1,0:T(8,128)(2,1)S(1)} %fill.2), channel_id=1, source_target_pairs={{0,24},{1,25},{2,26},{3,27},{4,28},{5,29},{6,30},{7,31},{8,0},{9,1... | collective-permute-start | bytes 1966088 | tf_op jit(solution)/shard_map/ppermute | solution.py:27
  3.6 1.3 %fill.3 = (bf16[160,2048]{1,0:T(8,128)(2,1)S(1)}, bf16[160,2048]{1,0:T(8,128)(2,1)S(1)}) custom-call(bf16[2,160,2048]{2,1,0:T(8,128)(2,1)} %bitcast.24, bf16[2,160,2048]{2,1,0:T(8,128)(2,1)} %bitcast.26), custom_call_target="tpu_custom_call" | custom-call | tf_op jit(solution)/shard_map/fill/pallas_call | solution.py:246
  6.0 1.5 %collective-permute-start = (bf16[8,2176]{1,0:T(8,128)(2,1)S(1)}, bf16[8,2176]{1,0:T(8,128)(2,1)S(1)}, u32[]{:S(2)}, u32[]{:S(2)}) collective-permute-start(bf16[8,2176]{1,0:T(8,128)(2,1)S(1)} %shard_map.100.first_ref), channel_id=1, source_target_pairs={{0,1},{1,0},{2,3},{3,2},{4,5},{5,4},{6,7},{7,6},{8,9},{9,8},{10,11... | collective-permute-start | bytes 104456 | tf_op jit(solution)/shard_map/ppermute | solution.py:27
  7.5 2.4 %collective-permute-done.second_ref = bf16[8,2176]{1,0:T(8,128)(2,1)S(1)} collective-permute-done((bf16[8,2176]{1,0:T(8,128)(2,1)S(1)}, bf16[8,2176]{1,0:T(8,128)(2,1)S(1)}, u32[]{:S(2)}, u32[]{:S(2)}) %collective-permute-start) | collective-permute-done | bytes 34848 | tf_op jit(solution)/shard_map/ppermute | solution.py:27
  10.0 1.6 %collective-permute-start.1 = (bf16[16,2176]{1,0:T(8,128)(2,1)S(1)}, bf16[16,2176]{1,0:T(8,128)(2,1)S(1)}, u32[]{:S(2)}, u32[]{:S(2)}) collective-permute-start(bf16[16,2176]{1,0:T(8,128)(2,1)S(1)} %shard_map.101.refs_0_.refs_4_.refs_3_), channel_id=1, source_target_pairs={{0,2},{1,3},{2,0},{3,1},{4,6},{5,7},{6,4},{7,5},{8,10},{9,11},{10,... | collective-permute-start | bytes 208904 | tf_op jit(solution)/shard_map/ppermute | solution.py:27
  11.6 2.7 %collective-permute-done.1.refs_1_.refs_5_.refs_4_ = bf16[16,2176]{1,0:T(8,128)(2,1)S(1)} collective-permute-done((bf16[16,2176]{1,0:T(8,128)(2,1)S(1)}, bf16[16,2176]{1,0:T(8,128)(2,1)S(1)}, u32[]{:S(2)}, u32[]{:S(2)}) %collective-permute-start.1) | collective-permute-done | bytes 69664 | tf_op jit(solution)/shard_map/ppermute | solution.py:27
  14.3 1.5 %stack.1 = bf16[3,160,2048]{2,1,0:T(8,128)(2,1)S(1)} custom-call(bf16[2,160,2048]{2,1,0:T(8,128)(2,1)} %bitcast.29, bf16[2,160,2048]{2,1,0:T(8,128)(2,1)} %bitcast.25, bf16[2,160,2048]{2,1,0:T(8,128)(2,1)} %bitcast.27), custom_call_target="tpu_custom_call" | custom-call | tf_op jit(solution)/shard_map/stack/pallas_call | solution.py:319
  15.9 1.9 %collective-permute-start.14 = (bf16[3,160,2048]{2,1,0:T(8,128)(2,1)S(1)}, bf16[3,160,2048]{2,1,0:T(8,128)(2,1)S(1)}, u32[]{:S(2)}, u32[]{:S(2)}) collective-permute-start(bf16[3,160,2048]{2,1,0:T(8,128)(2,1)S(1)} %stack.1), channel_id=1, source_target_pairs={{0,8},{1,9},{2,10},{3,11},{4,12},{5,13},{6,14},{7,15},{8,0},{9,1},... | collective-permute-start | bytes 5898248 | tf_op jit(solution)/shard_map/ppermute | solution.py:58
  17.8 3.7 %collective-permute-start.3 = (bf16[16,2176]{1,0:T(8,128)(2,1)S(1)}, bf16[16,2176]{1,0:T(8,128)(2,1)S(1)}, u32[]{:S(2)}, u32[]{:S(2)}) collective-permute-start(bf16[16,2176]{1,0:T(8,128)(2,1)S(1)} %shard_map.101.refs_0_.refs_4_.refs_3_), channel_id=1, source_target_pairs={{0,6},{1,7},{2,4},{3,5},{4,2},{5,3},{6,0},{7,1},{8,14},{9,15},{10,... | collective-permute-start | bytes 208904 | tf_op jit(solution)/shard_map/ppermute | solution.py:27
  21.5 2.9 %collective-permute-done.3.refs_3_.refs_7_.refs_5_ = bf16[16,2176]{1,0:T(8,128)(2,1)S(1)} collective-permute-done((bf16[16,2176]{1,0:T(8,128)(2,1)S(1)}, bf16[16,2176]{1,0:T(8,128)(2,1)S(1)}, u32[]{:S(2)}, u32[]{:S(2)}) %collective-permute-start.3) | collective-permute-done | bytes 69664 | tf_op jit(solution)/shard_map/ppermute | solution.py:27
  25.0 4.4 %load.3 = (bf16[2048,640]{1,0:T(8,128)(2,1)S(1)}, bf16[2048,640]{1,0:T(8,128)(2,1)S(1)}, bf16[640,2048]{1,0:T(8,128)(2,1)S(1)}) custom-call(bf16[2,640,2048]{2,1,0:T(8,128)(2,1)} %bitcast.22, bf16[2,640,2048]{2,1,0:T(8,128)(2,1)} %bitcast.18, bf16[2,640,2048]{2,1,0:T(8,128)(2,1)} %bitcast.20), custom_call_target="tpu_custom_call" | custom-call | tf_op jit(solution)/shard_map/load/pallas_call | solution.py:290
  29.4 1.2 collective-permute-done.2.refs_2_.refs_6_.refs_1_
  30.6 1.6 %layer.8.refs_9_ = f32[64,2048]{1,0:T(8,128)S(1)} custom-call(bf16[16,2176]{1,0:T(8,128)(2,1)S(1)} %shard_map.101.refs_0_.refs_4_.refs_3_, bf16[16,2176]{1,0:T(8,128)(2,1)S(1)} %collective-permute-done.1.refs_1_.refs_5_.refs_4_, bf16[16,2176]{1,0:T(8,128)(2,1)S(1)} %collective-permute-done.2.refs_2_.refs_6_.refs_1_, ...), custom_call_target="tpu_custom_call" | custom-call | flops 503316480 | bytes 7864320 | tf_op jit(solution)/shard_map/layer/pallas_call | solution.py:200
  33.1 2.5 %collective-permute-start.7 = (bf16[16,2048]{1,0:T(8,128)(2,1)S(1)}, bf16[16,2048]{1,0:T(8,128)(2,1)S(1)}, u32[]{:S(2)}, u32[]{:S(2)}) collective-permute-start(bf16[16,2048]{1,0:T(8,128)(2,1)S(1)} %get-tuple-element.50), channel_id=1, source_target_pairs={{0,6},{1,7},{2,4},{3,5},{4,2},{5,3},{6,0},{7,1},{8,14},{9,15},{10,... | collective-permute-start | bytes 196616 | tf_op jit(solution)/shard_map/ppermute | solution.py:27
  35.7 1.2 collective-permute-start.8
  37.6 2.5 %collective-permute-done.7.refs_1_ = bf16[16,2048]{1,0:T(8,128)(2,1)S(1)} collective-permute-done((bf16[16,2048]{1,0:T(8,128)(2,1)S(1)}, bf16[16,2048]{1,0:T(8,128)(2,1)S(1)}, u32[]{:S(2)}, u32[]{:S(2)}) %collective-permute-start.7) | collective-permute-done | bytes 65568 | tf_op jit(solution)/shard_map/ppermute | solution.py:27
  40.1 3.4 %collective-permute-done.8.refs_2_ = bf16[16,2048]{1,0:T(8,128)(2,1)S(1)} collective-permute-done((bf16[16,2048]{1,0:T(8,128)(2,1)S(1)}, bf16[16,2048]{1,0:T(8,128)(2,1)S(1)}, u32[]{:S(2)}, u32[]{:S(2)}) %collective-permute-start.8) | collective-permute-done | bytes 65568 | tf_op jit(solution)/shard_map/ppermute | solution.py:27
  44.6 3.7 %collective-permute-done.11.refs_1_ = bf16[16,2048]{1,0:T(8,128)(2,1)S(1)} collective-permute-done((bf16[16,2048]{1,0:T(8,128)(2,1)S(1)}, bf16[16,2048]{1,0:T(8,128)(2,1)S(1)}, u32[]{:S(2)}, u32[]{:S(2)}) %collective-permute-start.11) | collective-permute-done | bytes 65568 | tf_op jit(solution)/shard_map/ppermute | solution.py:27
  48.3 1.4 %collective-permute-done.10.refs_0_ = bf16[16,2048]{1,0:T(8,128)(2,1)S(1)} collective-permute-done((bf16[16,2048]{1,0:T(8,128)(2,1)S(1)}, bf16[16,2048]{1,0:T(8,128)(2,1)S(1)}, u32[]{:S(2)}, u32[]{:S(2)}) %collective-permute-start.10) | collective-permute-done | bytes 65568 | tf_op jit(solution)/shard_map/ppermute | solution.py:27
  49.7 1.3 %collective-permute-start.13 = (bf16[16,2048]{1,0:T(8,128)(2,1)S(1)}, bf16[16,2048]{1,0:T(8,128)(2,1)S(1)}, u32[]{:S(2)}, u32[]{:S(2)}) collective-permute-start(bf16[16,2048]{1,0:T(8,128)(2,1)S(1)} %shard_map.103.refs_0_), channel_id=1, source_target_pairs={{0,6},{1,7},{2,4},{3,5},{4,2},{5,3},{6,0},{7,1},{8,14},{9,15},{10,... | collective-permute-start | bytes 196616 | tf_op jit(solution)/shard_map/ppermute | solution.py:27
  51.0 3.1 %collective-permute-start.16 = (bf16[16,2048]{1,0:T(8,128)(2,1)S(1)}, bf16[16,2048]{1,0:T(8,128)(2,1)S(1)}, u32[]{:S(2)}, u32[]{:S(2)}) collective-permute-start(bf16[16,2048]{1,0:T(8,128)(2,1)S(1)} %shard_map.103.refs_0_), channel_id=1, source_target_pairs={{0,4},{1,5},{2,6},{3,7},{4,0},{5,1},{6,2},{7,3},{8,12},{9,13},{10,... | collective-permute-start | bytes 196616 | tf_op jit(solution)/shard_map/ppermute | solution.py:27
  54.1 2.5 %load.4.refs_10_.refs_6_ = bf16[2048,640]{1,0:T(8,128)(2,1)S(1)} custom-call(bf16[2,640,2048]{2,1,0:T(8,128)(2,1)} %bitcast.23), custom_call_target="tpu_custom_call" | custom-call | tf_op jit(solution)/shard_map/load/pallas_call | solution.py:290
  56.7 2.9 %load.5 = (bf16[2048,640]{1,0:T(8,128)(2,1)S(1)}, bf16[640,2048]{1,0:T(8,128)(2,1)S(1)}) custom-call(bf16[2,640,2048]{2,1,0:T(8,128)(2,1)} %bitcast.19, bf16[2,640,2048]{2,1,0:T(8,128)(2,1)} %bitcast.21), custom_call_target="tpu_custom_call" | custom-call | tf_op jit(solution)/shard_map/load/pallas_call | solution.py:290
  59.6 2.5 %layer.10 = (f32[16,2048]{1,0:T(8,128)S(1)}, bf16[16,2048]{1,0:T(8,128)(2,1)S(1)}, bf16[16,2048]{1,0:T(8,128)(2,1)S(1)}) custom-call(bf16[16,2048]{1,0:T(8,128)(2,1)S(1)} %shard_map.103.refs_0_, bf16[16,2048]{1,0:T(8,128)(2,1)S(1)} %collective-permute-done.12.refs_1_, bf16[16,2048]{1,0:T(8,128)(2,1)S(1)} %collective-permute-done.13.refs_2_, ...), custom_call_target="tpu_custom_call" | custom-call | flops 471859200 | bytes 9830400 | tf_op jit(solution)/shard_map/layer/pallas_call | solution.py:200
  62.1 1.3 %collective-permute-start.15 = (bf16[16,2048]{1,0:T(8,128)(2,1)S(1)}, bf16[16,2048]{1,0:T(8,128)(2,1)S(1)}, u32[]{:S(2)}, u32[]{:S(2)}) collective-permute-start(bf16[16,2048]{1,0:T(8,128)(2,1)S(1)} %get-tuple-element.62), channel_id=1, source_target_pairs={{0,6},{1,7},{2,4},{3,5},{4,2},{5,3},{6,0},{7,1},{8,14},{9,15},{10,... | collective-permute-start | bytes 196616 | tf_op jit(solution)/shard_map/ppermute | solution.py:27
  63.4 2.0 %layer.11 = bf16[16,2048]{1,0:T(8,128)(2,1)S(1)} custom-call(bf16[16,2048]{1,0:T(8,128)(2,1)S(1)} %collective-permute-done.16.refs_0_, bf16[16,2176]{1,0:T(8,128)(2,1)S(1)} %collective-permute-done.2.refs_2_.refs_6_.refs_1_, f32[2,1,2048]{2,1,0:T(1,128)S(1)} %copy-done, bf16[2048,640]{1,0:T(8,128)(2,1)S(1)} %get-tuple-element.41.refs_9_.refs_7_.refs_3_, ...), custom_call_target="tpu_custom_call" | custom-call | flops 157286400 | bytes 9830400 | tf_op jit(solution)/shard_map/layer/pallas_call | solution.py:200
  65.4 3.2 %collective-permute-start.17 = (bf16[16,2048]{1,0:T(8,128)(2,1)S(1)}, bf16[16,2048]{1,0:T(8,128)(2,1)S(1)}, u32[]{:S(2)}, u32[]{:S(2)}) collective-permute-start(bf16[16,2048]{1,0:T(8,128)(2,1)S(1)} %layer.11), channel_id=1, source_target_pairs={{0,4},{1,5},{2,6},{3,7},{4,0},{5,1},{6,2},{7,3},{8,12},{9,13},{10,... | collective-permute-start | bytes 196616 | tf_op jit(solution)/shard_map/ppermute | solution.py:27
  68.8 2.1 %collective-permute-done.17.refs_2_ = bf16[16,2048]{1,0:T(8,128)(2,1)S(1)} collective-permute-done((bf16[16,2048]{1,0:T(8,128)(2,1)S(1)}, bf16[16,2048]{1,0:T(8,128)(2,1)S(1)}, u32[]{:S(2)}, u32[]{:S(2)}) %collective-permute-start.17) | collective-permute-done | bytes 65568 | tf_op jit(solution)/shard_map/ppermute | solution.py:27
  71.3 4.3 %collective-permute-done.20.refs_1_ = bf16[16,2048]{1,0:T(8,128)(2,1)S(1)} collective-permute-done((bf16[16,2048]{1,0:T(8,128)(2,1)S(1)}, bf16[16,2048]{1,0:T(8,128)(2,1)S(1)}, u32[]{:S(2)}, u32[]{:S(2)}) %collective-permute-start.20) | collective-permute-done | bytes 65568 | tf_op jit(solution)/shard_map/ppermute | solution.py:27
  75.6 3.0 %collective-permute-start.25 = (bf16[16,2048]{1,0:T(8,128)(2,1)S(1)}, bf16[16,2048]{1,0:T(8,128)(2,1)S(1)}, u32[]{:S(2)}, u32[]{:S(2)}) collective-permute-start(bf16[16,2048]{1,0:T(8,128)(2,1)S(1)} %shard_map.105.refs_0_), channel_id=1, source_target_pairs={{0,4},{1,5},{2,6},{3,7},{4,0},{5,1},{6,2},{7,3},{8,12},{9,13},{10,... | collective-permute-start | bytes 196616 | tf_op jit(solution)/shard_map/ppermute | solution.py:27
  78.6 1.2 %collective-permute-start.22 = (bf16[16,2048]{1,0:T(8,128)(2,1)S(1)}, bf16[16,2048]{1,0:T(8,128)(2,1)S(1)}, u32[]{:S(2)}, u32[]{:S(2)}) collective-permute-start(bf16[16,2048]{1,0:T(8,128)(2,1)S(1)} %shard_map.105.refs_0_), channel_id=1, source_target_pairs={{0,6},{1,7},{2,4},{3,5},{4,2},{5,3},{6,0},{7,1},{8,14},{9,15},{10,... | collective-permute-start | bytes 196616 | tf_op jit(solution)/shard_map/ppermute | solution.py:27
  79.8 1.4 %collective-permute-done.25.refs_0_ = bf16[16,2048]{1,0:T(8,128)(2,1)S(1)} collective-permute-done((bf16[16,2048]{1,0:T(8,128)(2,1)S(1)}, bf16[16,2048]{1,0:T(8,128)(2,1)S(1)}, u32[]{:S(2)}, u32[]{:S(2)}) %collective-permute-start.25) | collective-permute-done | bytes 65568 | tf_op jit(solution)/shard_map/ppermute | solution.py:27
  81.2 1.9 %layer.13 = bf16[16,2048]{1,0:T(8,128)(2,1)S(1)} custom-call(bf16[16,2048]{1,0:T(8,128)(2,1)S(1)} %collective-permute-done.25.refs_0_, bf16[16,2176]{1,0:T(8,128)(2,1)S(1)} %collective-permute-done.2.refs_2_.refs_6_.refs_1_, f32[2,1,2048]{2,1,0:T(1,128)S(1)} %copy-done, bf16[2048,640]{1,0:T(8,128)(2,1)S(1)} %get-tuple-element.41.refs_9_.refs_7_.refs_3_, ...), custom_call_target="tpu_custom_call" | custom-call | flops 157286400 | bytes 9830400 | tf_op jit(solution)/shard_map/layer/pallas_call | solution.py:200
  83.1 2.7 %collective-permute-start.26 = (bf16[16,2048]{1,0:T(8,128)(2,1)S(1)}, bf16[16,2048]{1,0:T(8,128)(2,1)S(1)}, u32[]{:S(2)}, u32[]{:S(2)}) collective-permute-start(bf16[16,2048]{1,0:T(8,128)(2,1)S(1)} %layer.13), channel_id=1, source_target_pairs={{0,4},{1,5},{2,6},{3,7},{4,0},{5,1},{6,2},{7,3},{8,12},{9,13},{10,... | collective-permute-start | bytes 196616 | tf_op jit(solution)/shard_map/ppermute | solution.py:27
  85.9 2.4 %layer.12 = (f32[16,2048]{1,0:T(8,128)S(1)}, bf16[16,2048]{1,0:T(8,128)(2,1)S(1)}, bf16[16,2048]{1,0:T(8,128)(2,1)S(1)}) custom-call(bf16[16,2048]{1,0:T(8,128)(2,1)S(1)} %shard_map.105.refs_0_, bf16[16,2048]{1,0:T(8,128)(2,1)S(1)} %collective-permute-done.21.refs_1_, bf16[16,2048]{1,0:T(8,128)(2,1)S(1)} %collective-permute-done.22.refs_2_, ...), custom_call_target="tpu_custom_call" | custom-call | flops 471859200 | bytes 9830400 | tf_op jit(solution)/shard_map/layer/pallas_call | solution.py:200
  88.3 1.8 %collective-permute-start.24 = (bf16[16,2048]{1,0:T(8,128)(2,1)S(1)}, bf16[16,2048]{1,0:T(8,128)(2,1)S(1)}, u32[]{:S(2)}, u32[]{:S(2)}) collective-permute-start(bf16[16,2048]{1,0:T(8,128)(2,1)S(1)} %get-tuple-element.66), channel_id=1, source_target_pairs={{0,6},{1,7},{2,4},{3,5},{4,2},{5,3},{6,0},{7,1},{8,14},{9,15},{10,... | collective-permute-start | bytes 196616 | tf_op jit(solution)/shard_map/ppermute | solution.py:27
  90.1 4.4 %collective-permute-done.24.refs_1_ = bf16[16,2048]{1,0:T(8,128)(2,1)S(1)} collective-permute-done((bf16[16,2048]{1,0:T(8,128)(2,1)S(1)}, bf16[16,2048]{1,0:T(8,128)(2,1)S(1)}, u32[]{:S(2)}, u32[]{:S(2)}) %collective-permute-start.24) | collective-permute-done | bytes 65568 | tf_op jit(solution)/shard_map/ppermute | solution.py:27
  95.9 3.9 %collective-permute-done.29.refs_1_ = bf16[16,2048]{1,0:T(8,128)(2,1)S(1)} collective-permute-done((bf16[16,2048]{1,0:T(8,128)(2,1)S(1)}, bf16[16,2048]{1,0:T(8,128)(2,1)S(1)}, u32[]{:S(2)}, u32[]{:S(2)}) %collective-permute-start.29) | collective-permute-done | bytes 65568 | tf_op jit(solution)/shard_map/ppermute | solution.py:27
  101.2 1.6 %collective-permute-start.31 = (bf16[16,2048]{1,0:T(8,128)(2,1)S(1)}, bf16[16,2048]{1,0:T(8,128)(2,1)S(1)}, u32[]{:S(2)}, u32[]{:S(2)}) collective-permute-start(bf16[16,2048]{1,0:T(8,128)(2,1)S(1)} %shard_map.107.refs_0_), channel_id=1, source_target_pairs={{0,6},{1,7},{2,4},{3,5},{4,2},{5,3},{6,0},{7,1},{8,14},{9,15},{10,... | collective-permute-start | bytes 196616 | tf_op jit(solution)/shard_map/ppermute | solution.py:27
  102.8 1.1 collective-permute-start.30
  103.9 3.6 %collective-permute-done.33.refs_0_ = bf16[16,2048]{1,0:T(8,128)(2,1)S(1)} collective-permute-done((bf16[16,2048]{1,0:T(8,128)(2,1)S(1)}, bf16[16,2048]{1,0:T(8,128)(2,1)S(1)}, u32[]{:S(2)}, u32[]{:S(2)}) %collective-permute-start.33) | collective-permute-done | bytes 65568 | tf_op jit(solution)/shard_map/ppermute | solution.py:27
  107.5 1.9 %layer.15 = bf16[16,2048]{1,0:T(8,128)(2,1)S(1)} custom-call(bf16[16,2048]{1,0:T(8,128)(2,1)S(1)} %collective-permute-done.33.refs_0_, bf16[16,2176]{1,0:T(8,128)(2,1)S(1)} %collective-permute-done.2.refs_2_.refs_6_.refs_1_, f32[2,1,2048]{2,1,0:T(1,128)S(1)} %copy-done, bf16[2048,640]{1,0:T(8,128)(2,1)S(1)} %get-tuple-element.41.refs_9_.refs_7_.refs_3_, ...), custom_call_target="tpu_custom_call" | custom-call | flops 157286400 | bytes 9830400 | tf_op jit(solution)/shard_map/layer/pallas_call | solution.py:200
  109.6 2.4 %layer.14 = (f32[16,2048]{1,0:T(8,128)S(1)}, bf16[16,2048]{1,0:T(8,128)(2,1)S(1)}, bf16[16,2048]{1,0:T(8,128)(2,1)S(1)}) custom-call(bf16[16,2048]{1,0:T(8,128)(2,1)S(1)} %shard_map.107.refs_0_, bf16[16,2048]{1,0:T(8,128)(2,1)S(1)} %collective-permute-done.30.refs_1_, bf16[16,2048]{1,0:T(8,128)(2,1)S(1)} %collective-permute-done.31.refs_2_, ...), custom_call_target="tpu_custom_call" | custom-call | flops 471859200 | bytes 9830400 | tf_op jit(solution)/shard_map/layer/pallas_call | solution.py:200
  112.0 2.1 %collective-permute-start.32 = (bf16[16,2048]{1,0:T(8,128)(2,1)S(1)}, bf16[16,2048]{1,0:T(8,128)(2,1)S(1)}, u32[]{:S(2)}, u32[]{:S(2)}) collective-permute-start(bf16[16,2048]{1,0:T(8,128)(2,1)S(1)} %get-tuple-element.69), channel_id=1, source_target_pairs={{0,6},{1,7},{2,4},{3,5},{4,2},{5,3},{6,0},{7,1},{8,14},{9,15},{10,... | collective-permute-start | bytes 196616 | tf_op jit(solution)/shard_map/ppermute | solution.py:27
  114.1 1.4 %collective-permute-start.35 = (bf16[16,2048]{1,0:T(8,128)(2,1)S(1)}, bf16[16,2048]{1,0:T(8,128)(2,1)S(1)}, u32[]{:S(2)}, u32[]{:S(2)}) collective-permute-start(bf16[16,2048]{1,0:T(8,128)(2,1)S(1)} %get-tuple-element.70), channel_id=1, source_target_pairs={{0,2},{1,3},{2,0},{3,1},{4,6},{5,7},{6,4},{7,5},{8,10},{9,11},{10,... | collective-permute-start | bytes 196616 | tf_op jit(solution)/shard_map/ppermute | solution.py:27
  115.5 2.7 %collective-permute-done.32 = bf16[16,2048]{1,0:T(8,128)(2,1)S(1)} collective-permute-done((bf16[16,2048]{1,0:T(8,128)(2,1)S(1)}, bf16[16,2048]{1,0:T(8,128)(2,1)S(1)}, u32[]{:S(2)}, u32[]{:S(2)}) %collective-permute-start.32) | collective-permute-done | bytes 65568 | tf_op jit(solution)/shard_map/ppermute | solution.py:27
  119.3 3.6 %collective-permute-done.36 = bf16[8,2048]{1,0:T(8,128)(2,1)S(1)} collective-permute-done((bf16[8,2048]{1,0:T(8,128)(2,1)S(1)}, bf16[8,2048]{1,0:T(8,128)(2,1)S(1)}, u32[]{:S(2)}, u32[]{:S(2)}) %collective-permute-start.36) | collective-permute-done | bytes 32800 | tf_op jit(solution)/shard_map/ppermute | solution.py:27
  (59 shorter events, 9.5 us)
Async XLA Ops:
  0.0 5.7 %copy-start.3 = (f32[4,1,8,2]{2,3,1,0:T(2,128)S(1)}, f32[4,1,8,2]{2,3,1,0:T(2,128)}, u32[]{:S(2)}) copy-start(f32[4,1,8,2]{2,3,1,0:T(2,128)} %param.12) | copy-start | bytes 772
  0.0 5.7 %copy-start.2 = (s32[4,1,8,2]{2,3,1,0:T(2,128)S(1)}, s32[4,1,8,2]{2,3,1,0:T(2,128)}, u32[]{:S(2)}) copy-start(s32[4,1,8,2]{2,3,1,0:T(2,128)} %param.11) | copy-start | bytes 772
  0.0 5.7 %copy-start.1 = (bf16[1,8,2048]{2,1,0:T(8,128)(2,1)S(1)}, bf16[1,8,2048]{2,1,0:T(8,128)(2,1)}, u32[]{:S(2)}) copy-start(bf16[1,8,2048]{2,1,0:T(8,128)(2,1)} %param.10) | copy-start | bytes 98308
  1.1 31.0 %collective-permute-start.4 = (bf16[160,2048]{1,0:T(8,128)(2,1)S(1)}, bf16[160,2048]{1,0:T(8,128)(2,1)S(1)}, u32[]{:S(2)}, u32[]{:S(2)}) collective-permute-start(bf16[160,2048]{1,0:T(8,128)(2,1)S(1)} %fill.2), channel_id=1, source_target_pairs={{0,24},{1,25},{2,26},{3,27},{4,28},{5,29},{6,30},{7,31},{8,0},{9,1... | collective-permute-start | bytes 1966088 | tf_op jit(solution)/shard_map/ppermute | solution.py:27
  4.9 27.2 %collective-permute-start.5 = (bf16[160,2048]{1,0:T(8,128)(2,1)S(1)}, bf16[160,2048]{1,0:T(8,128)(2,1)S(1)}, u32[]{:S(2)}, u32[]{:S(2)}) collective-permute-start(bf16[160,2048]{1,0:T(8,128)(2,1)S(1)} %get-tuple-element.47), channel_id=1, source_target_pairs={{0,24},{1,25},{2,26},{3,27},{4,28},{5,29},{6,30},{7,31},{8,0},{9,1... | collective-permute-start | bytes 1966088 | tf_op jit(solution)/shard_map/ppermute | solution.py:27
  5.7 26.5 %collective-permute-start.6 = (bf16[160,2048]{1,0:T(8,128)(2,1)S(1)}, bf16[160,2048]{1,0:T(8,128)(2,1)S(1)}, u32[]{:S(2)}, u32[]{:S(2)}) collective-permute-start(bf16[160,2048]{1,0:T(8,128)(2,1)S(1)} %get-tuple-element.48), channel_id=1, source_target_pairs={{0,24},{1,25},{2,26},{3,27},{4,28},{5,29},{6,30},{7,31},{8,0},{9,1... | collective-permute-start | bytes 1966088 | tf_op jit(solution)/shard_map/ppermute | solution.py:27
  6.0 3.9 %collective-permute-start = (bf16[8,2176]{1,0:T(8,128)(2,1)S(1)}, bf16[8,2176]{1,0:T(8,128)(2,1)S(1)}, u32[]{:S(2)}, u32[]{:S(2)}) collective-permute-start(bf16[8,2176]{1,0:T(8,128)(2,1)S(1)} %shard_map.100.first_ref), channel_id=1, source_target_pairs={{0,1},{1,0},{2,3},{3,2},{4,5},{5,4},{6,7},{7,6},{8,9},{9,8},{10,11... | collective-permute-start | bytes 104456 | tf_op jit(solution)/shard_map/ppermute | solution.py:27
  10.0 4.4 %collective-permute-start.1 = (bf16[16,2176]{1,0:T(8,128)(2,1)S(1)}, bf16[16,2176]{1,0:T(8,128)(2,1)S(1)}, u32[]{:S(2)}, u32[]{:S(2)}) collective-permute-start(bf16[16,2176]{1,0:T(8,128)(2,1)S(1)} %shard_map.101.refs_0_.refs_4_.refs_3_), channel_id=1, source_target_pairs={{0,2},{1,3},{2,0},{3,1},{4,6},{5,7},{6,4},{7,5},{8,10},{9,11},{10,... | collective-permute-start | bytes 208904 | tf_op jit(solution)/shard_map/ppermute | solution.py:27
  15.9 43.8 %collective-permute-start.14 = (bf16[3,160,2048]{2,1,0:T(8,128)(2,1)S(1)}, bf16[3,160,2048]{2,1,0:T(8,128)(2,1)S(1)}, u32[]{:S(2)}, u32[]{:S(2)}) collective-permute-start(bf16[3,160,2048]{2,1,0:T(8,128)(2,1)S(1)} %stack.1), channel_id=1, source_target_pairs={{0,8},{1,9},{2,10},{3,11},{4,12},{5,13},{6,14},{7,15},{8,0},{9,1},... | collective-permute-start | bytes 5898248 | tf_op jit(solution)/shard_map/ppermute | solution.py:58
  17.8 6.6 %collective-permute-start.3 = (bf16[16,2176]{1,0:T(8,128)(2,1)S(1)}, bf16[16,2176]{1,0:T(8,128)(2,1)S(1)}, u32[]{:S(2)}, u32[]{:S(2)}) collective-permute-start(bf16[16,2176]{1,0:T(8,128)(2,1)S(1)} %shard_map.101.refs_0_.refs_4_.refs_3_), channel_id=1, source_target_pairs={{0,6},{1,7},{2,4},{3,5},{4,2},{5,3},{6,0},{7,1},{8,14},{9,15},{10,... | collective-permute-start | bytes 208904 | tf_op jit(solution)/shard_map/ppermute | solution.py:27
  24.4 6.2 %collective-permute-start.2 = (bf16[16,2176]{1,0:T(8,128)(2,1)S(1)}, bf16[16,2176]{1,0:T(8,128)(2,1)S(1)}, u32[]{:S(2)}, u32[]{:S(2)}) collective-permute-start(bf16[16,2176]{1,0:T(8,128)(2,1)S(1)} %shard_map.101.refs_0_.refs_4_.refs_3_), channel_id=1, source_target_pairs={{0,4},{1,5},{2,6},{3,7},{4,0},{5,1},{6,2},{7,3},{8,12},{9,13},{10,... | collective-permute-start | bytes 208904 | tf_op jit(solution)/shard_map/ppermute | solution.py:27
  25.0 5.5 %copy-start = (f32[2,1,2048]{2,1,0:T(1,128)S(1)}, f32[2,1,2048]{2,1,0:T(1,128)}, u32[]{:S(2)}) copy-start(f32[2,1,2048]{2,1,0:T(1,128)} %refs_2_.5) | copy-start | bytes 49156
  33.1 48.1 %collective-permute-start.23 = (bf16[3,160,2048]{2,1,0:T(8,128)(2,1)S(1)}, bf16[3,160,2048]{2,1,0:T(8,128)(2,1)S(1)}, u32[]{:S(2)}, u32[]{:S(2)}) collective-permute-start(bf16[3,160,2048]{2,1,0:T(8,128)(2,1)S(1)} %stack.1), channel_id=1, source_target_pairs={{0,24},{1,25},{2,26},{3,27},{4,28},{5,29},{6,30},{7,31},{8,0},{9,1... | collective-permute-start | bytes 5898248 | tf_op jit(solution)/shard_map/ppermute | solution.py:27
  33.1 6.9 %collective-permute-start.7 = (bf16[16,2048]{1,0:T(8,128)(2,1)S(1)}, bf16[16,2048]{1,0:T(8,128)(2,1)S(1)}, u32[]{:S(2)}, u32[]{:S(2)}) collective-permute-start(bf16[16,2048]{1,0:T(8,128)(2,1)S(1)} %get-tuple-element.50), channel_id=1, source_target_pairs={{0,6},{1,7},{2,4},{3,5},{4,2},{5,3},{6,0},{7,1},{8,14},{9,15},{10,... | collective-permute-start | bytes 196616 | tf_op jit(solution)/shard_map/ppermute | solution.py:27
  35.7 7.8 %collective-permute-start.8 = (bf16[16,2048]{1,0:T(8,128)(2,1)S(1)}, bf16[16,2048]{1,0:T(8,128)(2,1)S(1)}, u32[]{:S(2)}, u32[]{:S(2)}) collective-permute-start(bf16[16,2048]{1,0:T(8,128)(2,1)S(1)} %get-tuple-element.51), channel_id=1, source_target_pairs={{0,4},{1,5},{2,6},{3,7},{4,0},{5,1},{6,2},{7,3},{8,12},{9,13},{10,... | collective-permute-start | bytes 196616 | tf_op jit(solution)/shard_map/ppermute | solution.py:27
  36.9 6.6 %collective-permute-start.9 = (bf16[16,2048]{1,0:T(8,128)(2,1)S(1)}, bf16[16,2048]{1,0:T(8,128)(2,1)S(1)}, u32[]{:S(2)}, u32[]{:S(2)}) collective-permute-start(bf16[16,2048]{1,0:T(8,128)(2,1)S(1)} %get-tuple-element.52), channel_id=1, source_target_pairs={{0,2},{1,3},{2,0},{3,1},{4,6},{5,7},{6,4},{7,5},{8,10},{9,11},{10,... | collective-permute-start | bytes 196616 | tf_op jit(solution)/shard_map/ppermute | solution.py:27
  43.6 4.7 %collective-permute-start.11 = (bf16[16,2048]{1,0:T(8,128)(2,1)S(1)}, bf16[16,2048]{1,0:T(8,128)(2,1)S(1)}, u32[]{:S(2)}, u32[]{:S(2)}) collective-permute-start(bf16[16,2048]{1,0:T(8,128)(2,1)S(1)} %shard_map.102), channel_id=1, source_target_pairs={{0,9},{1,8},{2,11},{3,10},{4,13},{5,12},{6,15},{7,14},{8,17},{9,16... | collective-permute-start | bytes 196616 | tf_op jit(solution)/shard_map/ppermute | solution.py:27
  44.6 5.1 %collective-permute-start.10 = (bf16[16,2048]{1,0:T(8,128)(2,1)S(1)}, bf16[16,2048]{1,0:T(8,128)(2,1)S(1)}, u32[]{:S(2)}, u32[]{:S(2)}) collective-permute-start(bf16[16,2048]{1,0:T(8,128)(2,1)S(1)} %shard_map.102), channel_id=1, source_target_pairs={{0,8},{1,9},{2,10},{3,11},{4,12},{5,13},{6,14},{7,15},{8,16},{9,17... | collective-permute-start | bytes 196616 | tf_op jit(solution)/shard_map/ppermute | solution.py:27
  49.7 9.9 %collective-permute-start.13 = (bf16[16,2048]{1,0:T(8,128)(2,1)S(1)}, bf16[16,2048]{1,0:T(8,128)(2,1)S(1)}, u32[]{:S(2)}, u32[]{:S(2)}) collective-permute-start(bf16[16,2048]{1,0:T(8,128)(2,1)S(1)} %shard_map.103.refs_0_), channel_id=1, source_target_pairs={{0,6},{1,7},{2,4},{3,5},{4,2},{5,3},{6,0},{7,1},{8,14},{9,15},{10,... | collective-permute-start | bytes 196616 | tf_op jit(solution)/shard_map/ppermute | solution.py:27
  51.0 8.6 %collective-permute-start.12 = (bf16[16,2048]{1,0:T(8,128)(2,1)S(1)}, bf16[16,2048]{1,0:T(8,128)(2,1)S(1)}, u32[]{:S(2)}, u32[]{:S(2)}) collective-permute-start(bf16[16,2048]{1,0:T(8,128)(2,1)S(1)} %shard_map.103.refs_0_), channel_id=1, source_target_pairs={{0,2},{1,3},{2,0},{3,1},{4,6},{5,7},{6,4},{7,5},{8,10},{9,11},{10,... | collective-permute-start | bytes 196616 | tf_op jit(solution)/shard_map/ppermute | solution.py:27
  51.0 12.4 %collective-permute-start.16 = (bf16[16,2048]{1,0:T(8,128)(2,1)S(1)}, bf16[16,2048]{1,0:T(8,128)(2,1)S(1)}, u32[]{:S(2)}, u32[]{:S(2)}) collective-permute-start(bf16[16,2048]{1,0:T(8,128)(2,1)S(1)} %shard_map.103.refs_0_), channel_id=1, source_target_pairs={{0,4},{1,5},{2,6},{3,7},{4,0},{5,1},{6,2},{7,3},{8,12},{9,13},{10,... | collective-permute-start | bytes 196616 | tf_op jit(solution)/shard_map/ppermute | solution.py:27
  62.1 6.7 %collective-permute-start.15 = (bf16[16,2048]{1,0:T(8,128)(2,1)S(1)}, bf16[16,2048]{1,0:T(8,128)(2,1)S(1)}, u32[]{:S(2)}, u32[]{:S(2)}) collective-permute-start(bf16[16,2048]{1,0:T(8,128)(2,1)S(1)} %get-tuple-element.62), channel_id=1, source_target_pairs={{0,6},{1,7},{2,4},{3,5},{4,2},{5,3},{6,0},{7,1},{8,14},{9,15},{10,... | collective-permute-start | bytes 196616 | tf_op jit(solution)/shard_map/ppermute | solution.py:27
  63.4 5.4 %collective-permute-start.18 = (bf16[16,2048]{1,0:T(8,128)(2,1)S(1)}, bf16[16,2048]{1,0:T(8,128)(2,1)S(1)}, u32[]{:S(2)}, u32[]{:S(2)}) collective-permute-start(bf16[16,2048]{1,0:T(8,128)(2,1)S(1)} %get-tuple-element.63), channel_id=1, source_target_pairs={{0,2},{1,3},{2,0},{3,1},{4,6},{5,7},{6,4},{7,5},{8,10},{9,11},{10,... | collective-permute-start | bytes 196616 | tf_op jit(solution)/shard_map/ppermute | solution.py:27
  65.4 5.5 %collective-permute-start.17 = (bf16[16,2048]{1,0:T(8,128)(2,1)S(1)}, bf16[16,2048]{1,0:T(8,128)(2,1)S(1)}, u32[]{:S(2)}, u32[]{:S(2)}) collective-permute-start(bf16[16,2048]{1,0:T(8,128)(2,1)S(1)} %layer.11), channel_id=1, source_target_pairs={{0,4},{1,5},{2,6},{3,7},{4,0},{5,1},{6,2},{7,3},{8,12},{9,13},{10,... | collective-permute-start | bytes 196616 | tf_op jit(solution)/shard_map/ppermute | solution.py:27
  70.9 4.6 %collective-permute-start.20 = (bf16[16,2048]{1,0:T(8,128)(2,1)S(1)}, bf16[16,2048]{1,0:T(8,128)(2,1)S(1)}, u32[]{:S(2)}, u32[]{:S(2)}) collective-permute-start(bf16[16,2048]{1,0:T(8,128)(2,1)S(1)} %shard_map.104), channel_id=1, source_target_pairs={{0,9},{1,8},{2,11},{3,10},{4,13},{5,12},{6,15},{7,14},{8,17},{9,16... | collective-permute-start | bytes 196616 | tf_op jit(solution)/shard_map/ppermute | solution.py:27
  71.0 4.6 %collective-permute-start.19 = (bf16[16,2048]{1,0:T(8,128)(2,1)S(1)}, bf16[16,2048]{1,0:T(8,128)(2,1)S(1)}, u32[]{:S(2)}, u32[]{:S(2)}) collective-permute-start(bf16[16,2048]{1,0:T(8,128)(2,1)S(1)} %shard_map.104), channel_id=1, source_target_pairs={{0,8},{1,9},{2,10},{3,11},{4,12},{5,13},{6,14},{7,15},{8,16},{9,17... | collective-permute-start | bytes 196616 | tf_op jit(solution)/shard_map/ppermute | solution.py:27
  75.6 5.6 %collective-permute-start.25 = (bf16[16,2048]{1,0:T(8,128)(2,1)S(1)}, bf16[16,2048]{1,0:T(8,128)(2,1)S(1)}, u32[]{:S(2)}, u32[]{:S(2)}) collective-permute-start(bf16[16,2048]{1,0:T(8,128)(2,1)S(1)} %shard_map.105.refs_0_), channel_id=1, source_target_pairs={{0,4},{1,5},{2,6},{3,7},{4,0},{5,1},{6,2},{7,3},{8,12},{9,13},{10,... | collective-permute-start | bytes 196616 | tf_op jit(solution)/shard_map/ppermute | solution.py:27
  78.6 7.3 %collective-permute-start.22 = (bf16[16,2048]{1,0:T(8,128)(2,1)S(1)}, bf16[16,2048]{1,0:T(8,128)(2,1)S(1)}, u32[]{:S(2)}, u32[]{:S(2)}) collective-permute-start(bf16[16,2048]{1,0:T(8,128)(2,1)S(1)} %shard_map.105.refs_0_), channel_id=1, source_target_pairs={{0,6},{1,7},{2,4},{3,5},{4,2},{5,3},{6,0},{7,1},{8,14},{9,15},{10,... | collective-permute-start | bytes 196616 | tf_op jit(solution)/shard_map/ppermute | solution.py:27
  79.8 6.0 %collective-permute-start.21 = (bf16[16,2048]{1,0:T(8,128)(2,1)S(1)}, bf16[16,2048]{1,0:T(8,128)(2,1)S(1)}, u32[]{:S(2)}, u32[]{:S(2)}) collective-permute-start(bf16[16,2048]{1,0:T(8,128)(2,1)S(1)} %shard_map.105.refs_0_), channel_id=1, source_target_pairs={{0,2},{1,3},{2,0},{3,1},{4,6},{5,7},{6,4},{7,5},{8,10},{9,11},{10,... | collective-permute-start | bytes 196616 | tf_op jit(solution)/shard_map/ppermute | solution.py:27
  83.1 7.0 %collective-permute-start.26 = (bf16[16,2048]{1,0:T(8,128)(2,1)S(1)}, bf16[16,2048]{1,0:T(8,128)(2,1)S(1)}, u32[]{:S(2)}, u32[]{:S(2)}) collective-permute-start(bf16[16,2048]{1,0:T(8,128)(2,1)S(1)} %layer.13), channel_id=1, source_target_pairs={{0,4},{1,5},{2,6},{3,7},{4,0},{5,1},{6,2},{7,3},{8,12},{9,13},{10,... | collective-permute-start | bytes 196616 | tf_op jit(solution)/shard_map/ppermute | solution.py:27
  88.3 6.2 %collective-permute-start.24 = (bf16[16,2048]{1,0:T(8,128)(2,1)S(1)}, bf16[16,2048]{1,0:T(8,128)(2,1)S(1)}, u32[]{:S(2)}, u32[]{:S(2)}) collective-permute-start(bf16[16,2048]{1,0:T(8,128)(2,1)S(1)} %get-tuple-element.66), channel_id=1, source_target_pairs={{0,6},{1,7},{2,4},{3,5},{4,2},{5,3},{6,0},{7,1},{8,14},{9,15},{10,... | collective-permute-start | bytes 196616 | tf_op jit(solution)/shard_map/ppermute | solution.py:27
  90.1 5.0 %collective-permute-start.27 = (bf16[16,2048]{1,0:T(8,128)(2,1)S(1)}, bf16[16,2048]{1,0:T(8,128)(2,1)S(1)}, u32[]{:S(2)}, u32[]{:S(2)}) collective-permute-start(bf16[16,2048]{1,0:T(8,128)(2,1)S(1)} %get-tuple-element.67), channel_id=1, source_target_pairs={{0,2},{1,3},{2,0},{3,1},{4,6},{5,7},{6,4},{7,5},{8,10},{9,11},{10,... | collective-permute-start | bytes 196616 | tf_op jit(solution)/shard_map/ppermute | solution.py:27
  95.1 4.7 %collective-permute-start.29 = (bf16[16,2048]{1,0:T(8,128)(2,1)S(1)}, bf16[16,2048]{1,0:T(8,128)(2,1)S(1)}, u32[]{:S(2)}, u32[]{:S(2)}) collective-permute-start(bf16[16,2048]{1,0:T(8,128)(2,1)S(1)} %shard_map.106), channel_id=1, source_target_pairs={{0,9},{1,8},{2,11},{3,10},{4,13},{5,12},{6,15},{7,14},{8,17},{9,16... | collective-permute-start | bytes 196616 | tf_op jit(solution)/shard_map/ppermute | solution.py:27
  95.2 5.2 %collective-permute-start.28 = (bf16[16,2048]{1,0:T(8,128)(2,1)S(1)}, bf16[16,2048]{1,0:T(8,128)(2,1)S(1)}, u32[]{:S(2)}, u32[]{:S(2)}) collective-permute-start(bf16[16,2048]{1,0:T(8,128)(2,1)S(1)} %shard_map.106), channel_id=1, source_target_pairs={{0,8},{1,9},{2,10},{3,11},{4,12},{5,13},{6,14},{7,15},{8,16},{9,17... | collective-permute-start | bytes 196616 | tf_op jit(solution)/shard_map/ppermute | solution.py:27
  100.4 7.1 %collective-permute-start.33 = (bf16[16,2048]{1,0:T(8,128)(2,1)S(1)}, bf16[16,2048]{1,0:T(8,128)(2,1)S(1)}, u32[]{:S(2)}, u32[]{:S(2)}) collective-permute-start(bf16[16,2048]{1,0:T(8,128)(2,1)S(1)} %shard_map.107.refs_0_), channel_id=1, source_target_pairs={{0,4},{1,5},{2,6},{3,7},{4,0},{5,1},{6,2},{7,3},{8,12},{9,13},{10,... | collective-permute-start | bytes 196616 | tf_op jit(solution)/shard_map/ppermute | solution.py:27
  101.2 8.4 %collective-permute-start.31 = (bf16[16,2048]{1,0:T(8,128)(2,1)S(1)}, bf16[16,2048]{1,0:T(8,128)(2,1)S(1)}, u32[]{:S(2)}, u32[]{:S(2)}) collective-permute-start(bf16[16,2048]{1,0:T(8,128)(2,1)S(1)} %shard_map.107.refs_0_), channel_id=1, source_target_pairs={{0,6},{1,7},{2,4},{3,5},{4,2},{5,3},{6,0},{7,1},{8,14},{9,15},{10,... | collective-permute-start | bytes 196616 | tf_op jit(solution)/shard_map/ppermute | solution.py:27
  102.8 6.7 %collective-permute-start.30 = (bf16[16,2048]{1,0:T(8,128)(2,1)S(1)}, bf16[16,2048]{1,0:T(8,128)(2,1)S(1)}, u32[]{:S(2)}, u32[]{:S(2)}) collective-permute-start(bf16[16,2048]{1,0:T(8,128)(2,1)S(1)} %shard_map.107.refs_0_), channel_id=1, source_target_pairs={{0,2},{1,3},{2,0},{3,1},{4,6},{5,7},{6,4},{7,5},{8,10},{9,11},{10,... | collective-permute-start | bytes 196616 | tf_op jit(solution)/shard_map/ppermute | solution.py:27
  109.5 6.1 %collective-permute-start.34 = (bf16[16,2048]{1,0:T(8,128)(2,1)S(1)}, bf16[16,2048]{1,0:T(8,128)(2,1)S(1)}, u32[]{:S(2)}, u32[]{:S(2)}) collective-permute-start(bf16[16,2048]{1,0:T(8,128)(2,1)S(1)} %layer.15), channel_id=1, source_target_pairs={{0,4},{1,5},{2,6},{3,7},{4,0},{5,1},{6,2},{7,3},{8,12},{9,13},{10,... | collective-permute-start | bytes 196616 | tf_op jit(solution)/shard_map/ppermute | solution.py:27
  112.0 6.2 %collective-permute-start.32 = (bf16[16,2048]{1,0:T(8,128)(2,1)S(1)}, bf16[16,2048]{1,0:T(8,128)(2,1)S(1)}, u32[]{:S(2)}, u32[]{:S(2)}) collective-permute-start(bf16[16,2048]{1,0:T(8,128)(2,1)S(1)} %get-tuple-element.69), channel_id=1, source_target_pairs={{0,6},{1,7},{2,4},{3,5},{4,2},{5,3},{6,0},{7,1},{8,14},{9,15},{10,... | collective-permute-start | bytes 196616 | tf_op jit(solution)/shard_map/ppermute | solution.py:27
  114.1 4.7 %collective-permute-start.35 = (bf16[16,2048]{1,0:T(8,128)(2,1)S(1)}, bf16[16,2048]{1,0:T(8,128)(2,1)S(1)}, u32[]{:S(2)}, u32[]{:S(2)}) collective-permute-start(bf16[16,2048]{1,0:T(8,128)(2,1)S(1)} %get-tuple-element.70), channel_id=1, source_target_pairs={{0,2},{1,3},{2,0},{3,1},{4,6},{5,7},{6,4},{7,5},{8,10},{9,11},{10,... | collective-permute-start | bytes 196616 | tf_op jit(solution)/shard_map/ppermute | solution.py:27
  118.9 4.0 %collective-permute-start.36 = (bf16[8,2048]{1,0:T(8,128)(2,1)S(1)}, bf16[8,2048]{1,0:T(8,128)(2,1)S(1)}, u32[]{:S(2)}, u32[]{:S(2)}) collective-permute-start(bf16[8,2048]{1,0:T(8,128)(2,1)S(1)} %slice.17), channel_id=1, source_target_pairs={{0,1},{1,0},{2,3},{3,2},{4,5},{5,4},{6,7},{7,6},{8,9},{9,8},{10,11... | collective-permute-start | bytes 98312 | tf_op jit(solution)/shard_map/ppermute | solution.py:27

commit v8 on v6

--- a/solution.py
+++ b/solution.py
@@ -66,12 +66,18 @@
         kernel,
         out_shape=out_shape,
         in_specs=[WHOLE] * len(values),
-        out_specs=WHOLE,
+        out_specs=[WHOLE] * len(out_shape) if isinstance(out_shape, list) else WHOLE,
         compiler_params=pltpu.CompilerParams(vmem_limit_bytes=2 * 1024 * 1024),
     )(*values)
 
 
-def prepare_kernel(state_ref, routes_ref, gates_ref, out_ref):
+def normed_rows(values, gain_ref, tick_idx):
+    group = group_of(lax.axis_index("segment"), tick_idx, lax.axis_size("segment"))
+    row_scale = lax.rsqrt(jnp.mean(values * values, axis=-1, keepdims=True) + EPSILON)
+    return (values * row_scale * gain_ref[group]).astype(jnp.bfloat16)
+
+
+def prepare_kernel(state_ref, routes_ref, gates_ref, gain_ref, out_ref):
     rows, width = state_ref.shape
     lane = lax.broadcasted_iota(jnp.int32, (rows, LANES), 1)
     columns = EXPERTS + 1
@@ -101,7 +107,7 @@
         table = jnp.where(lane == low + EXPERTS, spill, table)
     high = table.astype(jnp.bfloat16).astype(jnp.float32)
     both = high + pltpu.roll(table - high, TICKS * columns, 1)
-    out_ref[:, :width] = state_ref[...]
+    out_ref[:, :width] = normed_rows(state_ref[...].astype(jnp.float32), gain_ref, 0)
     out_ref[:, width:] = both.astype(jnp.bfloat16)
 
 
@@ -125,104 +131,102 @@
         pl.when(second)(bodies[1])
 
 
-def layer_kernel(*refs, tick_idx, blocks, slot_count, spare_counts, tok_dev, width, carried, ends):
-    x_refs, first_refs, refs = refs[:blocks], refs[blocks:2 * blocks], refs[2 * blocks:]
-    gain_ref, refs = refs[0], refs[1:]
+def layer_kernel(*refs, tick_idx, blocks, layer_counts, tok_dev, width, carried, ends):
+    row_refs, table_refs, refs = refs[:blocks], refs[blocks:2 * blocks], refs[2 * blocks:]
+    own_ref, refs = refs[0], refs[1:]
     if carried:
         carried_ref, refs = refs[0], refs[1:]
-    else:
-        slots, refs = [refs[3 * i:3 * i + 3] for i in range(slot_count)], refs[3 * slot_count:]
-    spare_refs = []
-    for count in spare_counts:
-        spare_refs.append(refs[:count] if count > 1 else [refs[0].at[i] for i in range(refs[0].shape[0])])
-        refs = refs[count:]
+    choices = []
+    for slot_count, spare_count in layer_counts:
+        slot, spare, refs = refs[:slot_count], refs[slot_count:slot_count + spare_count], refs[slot_count + spare_count:]
+        choices.append((slot, [spare[0].at[i] for i in range(3)] if spare_count == 1 else spare))
     segments, members = lax.axis_size("segment"), lax.axis_size("expert")
     group = group_of(lax.axis_index("segment"), tick_idx, segments)
     expert = lax.axis_index("expert") // (members // EXPERTS)
-    x = jnp.concatenate([x_ref[:, :width] for x_ref in x_refs], axis=0)
-    values = x.astype(jnp.float32)
-    row_scale = lax.rsqrt(jnp.mean(values * values, axis=-1, keepdims=True) + EPSILON)
-    normed = (values * row_scale * gain_ref[group]).astype(jnp.bfloat16)
-    table = jnp.concatenate([ref[:, width:] for ref in first_refs], axis=0).astype(jnp.float32)
+    normed = jnp.concatenate([ref[:, :width] for ref in row_refs], axis=0)
+    table = jnp.concatenate([ref[:, width:] for ref in table_refs], axis=0).astype(jnp.float32)
     lane = lax.broadcasted_iota(jnp.int32, table.shape, 1)
     columns = TICKS * (EXPERTS + 1)
 
     def column(at):
         return jnp.sum(jnp.where((lane == at) | (lane == at + columns), table, 0.0), axis=1, keepdims=True)
 
-    total_ref = refs[0] if not ends else refs[-1]
-    if carried:
-        total_ref[...] = carried_ref[...]
-    else:
-
-        def put(slot):
-            share = column(tick_idx * (EXPERTS + 1) + expert)
-            total_ref[...] = share * served(normed, *[ref[...] for ref in slot], True)
-
-        home = group_of(lax.axis_index("segment"), 0, segments)
-        either(group != home, [functools.partial(put, slot) for slot in slots])
-
-    def add(spare_ref):
-        spill = column(tick_idx * (EXPERTS + 1) + EXPERTS)
-        total_ref[...] += spill * served(normed, *[ref[...] for ref in spare_ref], False)
-
-    either(group == 1, [functools.partial(add, spare_ref) for spare_ref in spare_refs])
-    if not ends:
-        return
-    out_refs = refs[:blocks]
+    share = column(tick_idx * (EXPERTS + 1) + expert)
+    spill = column(tick_idx * (EXPERTS + 1) + EXPERTS)
     per = 2 * tok_dev
-    row = lax.broadcasted_iota(jnp.int32, (per, 1), 0)
-    out_refs[0][...] = total_ref[0:per, :] + jnp.where(row < tok_dev, values[0:per], 0.0)
-    for i in range(1, blocks):
-        out_refs[i][...] = total_ref[i * per:(i + 1) * per, :].astype(jnp.bfloat16)
+
+    def run(slot, spare):
+        total = carried_ref[...] if carried else share * served(normed, *[ref[...] for ref in slot], True)
+        if spare:
+            total = total + spill * served(normed, *[ref[...] for ref in spare], False)
+        if not ends:
+            refs[0][...] = total
+            return
+        own = jnp.concatenate([own_ref[...].astype(jnp.float32), jnp.zeros((tok_dev, width), jnp.float32)], axis=0)
+        refs[0][...] = total[0:per] + own
+        for i in range(1, blocks):
+            refs[i][...] = total[i * per:(i + 1) * per].astype(jnp.bfloat16)
+
+    either(group == 1, [functools.partial(run, *choice) for choice in choices])
 
 
 def resident(values):
     return [pltpu.with_memory_space_constraint(value, pltpu.VMEM) for value in values]
 
 
-def run_layer(x_blocks, first_blocks, gain, weights, spares, *, tick_idx, tok_dev, carried=None, ends=True):
-    blocks = len(x_blocks)
-    width = gain.shape[-1]
+def run_layer(rows, tables, own, layers, *, tick_idx, tok_dev, carried=None, ends=True):
+    blocks = len(rows)
+    width = own.shape[-1]
     per = 2 * tok_dev
-    rows = per * blocks
-    values = [*x_blocks, *first_blocks, gain]
-    values += [carried] if carried is not None else resident([one for slot in weights for one in slot])
-    for spare in spares:
-        values += resident(spare)
-    hidden = (0 if carried is not None else weights[0][2].shape[0]) + (spares[0][0].shape[0] if spares else 0)
-    whole = jax.ShapeDtypeStruct((rows, width), jnp.float32)
+    values = [*rows, *tables, own]
+    if carried is not None:
+        values.append(carried)
+    for slot, spare in layers:
+        values += resident([*slot, *spare])
+    slot, spare = layers[0]
+    hidden = (slot[2].shape[0] if slot else 0) + (spare[-1].shape[-2] if spare else 0)
+    whole = jax.ShapeDtypeStruct((per * blocks, width), jnp.float32)
     parts = [jax.ShapeDtypeStruct((per, width), jnp.float32)]
     parts += [jax.ShapeDtypeStruct((per, width), jnp.bfloat16)] * (blocks - 1)
     return pl.pallas_call(
         functools.partial(
-            layer_kernel, tick_idx=tick_idx, blocks=blocks, slot_count=len(weights), spare_counts=[len(spare) for spare in spares],
-            tok_dev=tok_dev, width=width, carried=carried is not None, ends=ends,
+            layer_kernel, tick_idx=tick_idx, blocks=blocks, tok_dev=tok_dev, width=width, ends=ends,
+            layer_counts=[(len(slot), len(spare)) for slot, spare in layers], carried=carried is not None,
         ),
         out_shape=parts if ends else whole,
         in_specs=[WHOLE] * len(values),
         out_specs=[WHOLE] * blocks if ends else WHOLE,
-        scratch_shapes=[pltpu.VMEM((rows, width), jnp.float32)] if ends else [],
         compiler_params=pltpu.CompilerParams(vmem_limit_bytes=12 * 1024 * 1024),
         cost_estimate=pl.CostEstimate(
-            flops=6 * rows * hidden * width, bytes_accessed=6 * hidden * width, transcendentals=rows * hidden
+            flops=6 * per * blocks * hidden * width, bytes_accessed=6 * hidden * width,
+            transcendentals=per * blocks * hidden,
         ),
         name="layer",
     )(*values)
 
 
-def sum_kernel(*refs, swap):
-    total = refs[0][...].astype(jnp.float32)
-    half = total.shape[0] // 2
-    for ref in refs[1:-1]:
-        value = ref[...].astype(jnp.float32)
-        total = total + (jnp.concatenate([value[half:], value[:half]], axis=0) if swap else value)
-    refs[-1][...] = total.astype(jnp.bfloat16)
-
-
-def summed(values, swap=False):
+def sum_kernel(*refs):
+    refs[-1][...] = added([ref[...] for ref in refs[:-1]]).astype(jnp.bfloat16)
+
+
+def summed(values):
     shape = jax.ShapeDtypeStruct(values[0].shape, jnp.bfloat16)
-    return small(functools.partial(sum_kernel, swap=swap), shape, *values)
+    return small(sum_kernel, shape, *values)
+
+
+def arrive_kernel(along_ref, across_ref, gain_ref, own_ref, normed_ref, *, tick_idx):
+    across = across_ref[...].astype(jnp.float32)
+    half = across.shape[0] // 2
+    total = along_ref[...].astype(jnp.float32) + jnp.concatenate([across[half:], across[:half]], axis=0)
+    total = total.astype(jnp.bfloat16)
+    own_ref[...] = total[:half]
+    normed_ref[...] = normed_rows(total.astype(jnp.float32), gain_ref, tick_idx)
+
+
+def arriving(along, across, gain, tick_idx):
+    rows, width = along.shape
+    shapes = [jax.ShapeDtypeStruct((count, width), jnp.bfloat16) for count in (rows // 2, rows)]
+    return small(functools.partial(arrive_kernel, tick_idx=tick_idx), shapes, along, across, gain)
 
 
 def fill_kernel(*refs, group):
@@ -251,11 +255,9 @@
     )(*[pltpu.with_memory_space_constraint(value, pltpu.HBM) for value in values])
 
 
-def load_kernel(*refs, turned, other):
+def load_kernel(*refs, turned, group):
     count = len(turned)
     ins, outs, (held, sems, straight) = refs[:count], refs[count:2 * count], refs[2 * count:]
-    group = group_of(lax.axis_index("segment"), 0, lax.axis_size("segment"))
-    group = 1 - group if other else group
     depth, block = held.shape[:2]
     work = [
         (ins[i], outs[i], low) for i in range(count) if turned[i] for low in range(0, ins[i].shape[1], block)
@@ -281,11 +283,11 @@
         copy.wait()
 
 
-def loaded(values, turned, other):
+def loaded(values, turned, group):
     hidden, width = values[0].shape[1:]
     block = LANES if hidden % LANES == 0 else hidden
     return pl.pallas_call(
-        functools.partial(load_kernel, turned=turned, other=other),
+        functools.partial(load_kernel, turned=turned, group=group),
         out_shape=[
             pltpu.VMEM((width, hidden) if flip else (hidden, width), value.dtype)
             for value, flip in zip(values, turned)
@@ -360,35 +362,36 @@
     shape = (tok_dev, state.shape[2] + LANES)
     own = small(
         prepare_kernel, jax.ShapeDtypeStruct(shape, state.dtype), state[0],
-        jnp.transpose(routes[:, 0], (0, 2, 1)), jnp.transpose(gates[:, 0], (0, 2, 1)),
+        jnp.transpose(routes[:, 0], (0, 2, 1)), jnp.transpose(gates[:, 0], (0, 2, 1)), norm_gain,
     )
     other = moved(own, 1, 0)
     pair = small(join_kernel, jax.ShapeDtypeStruct((2 * tok_dev, shape[1]), state.dtype), own, other)
     arrived = spread(pair)
-    slots = [loaded(weights, (True, True, False), False)]
-    late = stacked(lax.optimization_barrier((*spare_all, arrived[1]))[:3], 1)
-    before = run_layer(
-        arrived, arrived, norm_gain, slots, [], tick_idx=0, tok_dev=tok_dev, ends=False
-    )
-
     users = [later_users(tick_idx, segments) for tick_idx in range(TICKS)]
     opening = min([tick_idx for tick_idx in range(TICKS) if users[tick_idx]], default=TICKS)
+    slots = [loaded(weights, (True, True, False), 0)]
+    if users[0]:
+        slots.append(loaded(weights, (True, True, False), 1))
+    late = stacked(lax.optimization_barrier((*spare_all, arrived[1]))[:3], 1)
     near = [swapped(late, users[opening])] if opening < TICKS else []
-
-    x_blocks = arrived
+    own = state[0]
+    before = run_layer(arrived, arrived, own, [(slot, []) for slot in slots], tick_idx=0, tok_dev=tok_dev, ends=False)
+
+    rows = arrived
     for tick_idx in range(TICKS):
-        used = [spares[0]]
+        layers = [(slots[0], spares[0])]
         if users[tick_idx]:
-            used.append(near if users[tick_idx] <= users[opening] else far)
+            layers.append((slots[1], near if users[tick_idx] <= users[opening] else far))
+        if tick_idx == 0:
+            layers = [([], spare) for _, spare in layers]
         parts = run_layer(
-            x_blocks, arrived, norm_gain, slots, used, tick_idx=tick_idx, tok_dev=tok_dev,
+            rows, arrived, own, layers, tick_idx=tick_idx, tok_dev=tok_dev,
             carried=before if tick_idx == 0 else None,
         )
         got = [moved(parts[j], 2 * j, 0) for j in widest_first(outer)]
-        if tick_idx == 0:
-            far = [moved(lax.optimization_barrier((late, parts[0]))[0], 0, -1)]
+        if tick_idx == 0 and not users[0]:
             tied = lax.optimization_barrier((*weights, parts[0]))[:3]
-            gate = loaded(tied[:1], (True,), True)
+            gate = loaded(tied[:1], (True,), 1)
         if tick_idx + 1 == TICKS:
             total = added([parts[0]] + got)
             other = moved(total[tok_dev:].astype(jnp.bfloat16), 1, 0)
@@ -397,9 +400,12 @@
         across = moved(total, 1, 1)
         along = moved(total, 0, 1)
         if tick_idx == 0:
-            tied = lax.optimization_barrier((*weights, total))[:3]
-            slots.append(gate + loaded(tied[1:], (True, False), True))
-        x_blocks = spread(summed([along, across], swap=True))
+            far = [moved(lax.optimization_barrier((late, total))[0], 0, -1)]
+            if not users[0]:
+                tied = lax.optimization_barrier((*weights, total))[:3]
+                slots.append(gate + loaded(tied[1:], (True, False), 1))
+        own, normed = arriving(along, across, norm_gain, tick_idx + 1)
+        rows = spread(normed)
 
 
 def solution(mesh):

time: 123 us -> 117 us (0.951)
  waiting for transfers between devices: 47.4 us -> 40.1 us
  starting transfers between devices: 49.8 us -> 51.8 us
    ppermute x36, waiting for transfers between devices: 47.4 us -> 40.1 us  [moved(): return lax.ppermute(value, BOTH, pairs)]
    ppermute x36, starting transfers between devices: 47.8 us -> 49.9 us  [moved(): return lax.ppermute(value, BOTH, pairs)]
  transfers between devices with their start and end apart: 37 -> 37, of which waited for: 22 -> 21; matrix products, arithmetic and copies ran while one was open for 0% -> 0% of each run, Pallas kernels for 15% -> 15%
where the time goes in v8:
time: 117 us
  starting transfers between devices  51.8 us (44%)
  waiting for transfers between devices  40.1 us (34%)
  Pallas kernels  23.8 us (20%)
    ppermute x36, starting transfers between devices, moved(): return lax.ppermute(value, BOTH, pairs)  49.9 us
    ppermute x36, waiting for transfers between devices, moved(): return lax.ppermute(value, BOTH, pairs)  40.1 us
    pallas_call x3, Pallas kernels, loaded(): pl.pallas_call(functools.partial(load_kernel, turned=turned, group=group)...  9.77 us
    pallas_call x5, Pallas kernels, run_layer(): pl.pallas_call(functools.partial(layer_kernel, tick_idx=tick_idx, blocks=...  9.36 us
    pallas_call x2, Pallas kernels, filled(): pl.pallas_call(functools.partial(fill_kernel, group=group), out_shape=[pl...  2.43 us
  transfers between devices with their start and end apart: 37, of which 21 were waited for; matrix products, arithmetic and copies ran while one was open for 0% of the time, Pallas kernels for 15%

profile of v8, /device:TPU:0, one launch (start us, length us, event | category | flops | bytes accessed | tf_op | source)
XLA Modules:
  0.0 116.7 jit_solution(7191709309864208838)
XLA Ops:
  1.1 2.5 %collective-permute-start.4 = (bf16[160,2048]{1,0:T(8,128)(2,1)S(1)}, bf16[160,2048]{1,0:T(8,128)(2,1)S(1)}, u32[]{:S(2)}, u32[]{:S(2)}) collective-permute-start(bf16[160,2048]{1,0:T(8,128)(2,1)S(1)} %fill.2), channel_id=1, source_target_pairs={{0,24},{1,25},{2,26},{3,27},{4,28},{5,29},{6,30},{7,31},{8,0},{9,1... | collective-permute-start | bytes 1966088 | tf_op jit(solution)/shard_map/ppermute | solution.py:27
  3.7 1.3 %fill.3 = (bf16[160,2048]{1,0:T(8,128)(2,1)S(1)}, bf16[160,2048]{1,0:T(8,128)(2,1)S(1)}) custom-call(bf16[2,160,2048]{2,1,0:T(8,128)(2,1)} %bitcast.26, bf16[2,160,2048]{2,1,0:T(8,128)(2,1)} %bitcast.28), custom_call_target="tpu_custom_call" | custom-call | tf_op jit(solution)/shard_map/fill/pallas_call | solution.py:247
  6.0 1.5 %collective-permute-start = (bf16[8,2176]{1,0:T(8,128)(2,1)S(1)}, bf16[8,2176]{1,0:T(8,128)(2,1)S(1)}, u32[]{:S(2)}, u32[]{:S(2)}) collective-permute-start(bf16[8,2176]{1,0:T(8,128)(2,1)S(1)} %shard_map.100.first_ref), channel_id=1, source_target_pairs={{0,1},{1,0},{2,3},{3,2},{4,5},{5,4},{6,7},{7,6},{8,9},{9,8},{10,11... | collective-permute-start | bytes 104456 | tf_op jit(solution)/shard_map/ppermute | solution.py:27
  7.5 2.4 %collective-permute-done.second_ref = bf16[8,2176]{1,0:T(8,128)(2,1)S(1)} collective-permute-done((bf16[8,2176]{1,0:T(8,128)(2,1)S(1)}, bf16[8,2176]{1,0:T(8,128)(2,1)S(1)}, u32[]{:S(2)}, u32[]{:S(2)}) %collective-permute-start) | collective-permute-done | bytes 34848 | tf_op jit(solution)/shard_map/ppermute | solution.py:27
  10.0 1.6 %collective-permute-start.1 = (bf16[16,2176]{1,0:T(8,128)(2,1)S(1)}, bf16[16,2176]{1,0:T(8,128)(2,1)S(1)}, u32[]{:S(2)}, u32[]{:S(2)}) collective-permute-start(bf16[16,2176]{1,0:T(8,128)(2,1)S(1)} %shard_map.101.refs_0_.refs_4_), channel_id=1, source_target_pairs={{0,2},{1,3},{2,0},{3,1},{4,6},{5,7},{6,4},{7,5},{8,10},{9,11},{10,... | collective-permute-start | bytes 208904 | tf_op jit(solution)/shard_map/ppermute | solution.py:27
  11.6 2.5 %collective-permute-start.3 = (bf16[16,2176]{1,0:T(8,128)(2,1)S(1)}, bf16[16,2176]{1,0:T(8,128)(2,1)S(1)}, u32[]{:S(2)}, u32[]{:S(2)}) collective-permute-start(bf16[16,2176]{1,0:T(8,128)(2,1)S(1)} %shard_map.101.refs_0_.refs_4_), channel_id=1, source_target_pairs={{0,6},{1,7},{2,4},{3,5},{4,2},{5,3},{6,0},{7,1},{8,14},{9,15},{10,... | collective-permute-start | bytes 208904 | tf_op jit(solution)/shard_map/ppermute | solution.py:27
  14.4 1.5 %stack.1 = bf16[3,160,2048]{2,1,0:T(8,128)(2,1)S(1)} custom-call(bf16[2,160,2048]{2,1,0:T(8,128)(2,1)} %bitcast.31, bf16[2,160,2048]{2,1,0:T(8,128)(2,1)} %bitcast.27, bf16[2,160,2048]{2,1,0:T(8,128)(2,1)} %bitcast.29), custom_call_target="tpu_custom_call" | custom-call | tf_op jit(solution)/shard_map/stack/pallas_call | solution.py:318
  15.9 1.9 %collective-permute-start.15 = (bf16[3,160,2048]{2,1,0:T(8,128)(2,1)S(1)}, bf16[3,160,2048]{2,1,0:T(8,128)(2,1)S(1)}, u32[]{:S(2)}, u32[]{:S(2)}) collective-permute-start(bf16[3,160,2048]{2,1,0:T(8,128)(2,1)S(1)} %stack.1), channel_id=1, source_target_pairs={{0,8},{1,9},{2,10},{3,11},{4,12},{5,13},{6,14},{7,15},{8,0},{9,1},... | collective-permute-start | bytes 5898248 | tf_op jit(solution)/shard_map/ppermute | solution.py:58
  17.8 2.8 %collective-permute-start.2 = (bf16[16,2176]{1,0:T(8,128)(2,1)S(1)}, bf16[16,2176]{1,0:T(8,128)(2,1)S(1)}, u32[]{:S(2)}, u32[]{:S(2)}) collective-permute-start(bf16[16,2176]{1,0:T(8,128)(2,1)S(1)} %shard_map.101.refs_0_.refs_4_), channel_id=1, source_target_pairs={{0,4},{1,5},{2,6},{3,7},{4,0},{5,1},{6,2},{7,3},{8,12},{9,13},{10,... | collective-permute-start | bytes 208904 | tf_op jit(solution)/shard_map/ppermute | solution.py:27
  20.6 4.3 %load.3 = (bf16[2048,640]{1,0:T(8,128)(2,1)S(1)}, bf16[2048,640]{1,0:T(8,128)(2,1)S(1)}, bf16[640,2048]{1,0:T(8,128)(2,1)S(1)}) custom-call(bf16[2,640,2048]{2,1,0:T(8,128)(2,1)} %bitcast.24, bf16[2,640,2048]{2,1,0:T(8,128)(2,1)} %bitcast.20, bf16[2,640,2048]{2,1,0:T(8,128)(2,1)} %bitcast.22), custom_call_target="tpu_custom_call" | custom-call | tf_op jit(solution)/shard_map/load/pallas_call | solution.py:289
  25.0 1.5 %layer.5.refs_9_ = f32[64,2048]{1,0:T(8,128)S(1)} custom-call(bf16[16,2176]{1,0:T(8,128)(2,1)S(1)} %shard_map.101.refs_0_.refs_4_, bf16[16,2176]{1,0:T(8,128)(2,1)S(1)} %collective-permute-done.1.refs_1_.refs_5_, bf16[16,2176]{1,0:T(8,128)(2,1)S(1)} %collective-permute-done.2.refs_2_.refs_6_, bf16[16,2176]{1,0:T(8,128)(2,1)S(1)} %collective-permute-done.3.refs_3_.refs_7_, ...), custom_call_target="tpu_custom_call" | custom-call | flops 503316480 | bytes 7864320 | tf_op jit(solution)/shard_map/layer/pallas_call | solution.py:191
  27.4 3.6 %collective-permute-start.7 = (bf16[16,2048]{1,0:T(8,128)(2,1)S(1)}, bf16[16,2048]{1,0:T(8,128)(2,1)S(1)}, u32[]{:S(2)}, u32[]{:S(2)}) collective-permute-start(bf16[16,2048]{1,0:T(8,128)(2,1)S(1)} %get-tuple-element.59), channel_id=1, source_target_pairs={{0,6},{1,7},{2,4},{3,5},{4,2},{5,3},{6,0},{7,1},{8,14},{9,15},{10,... | collective-permute-start | bytes 196616 | tf_op jit(solution)/shard_map/ppermute | solution.py:27
  31.8 1.9 %collective-permute-done.7.refs_1_ = bf16[16,2048]{1,0:T(8,128)(2,1)S(1)} collective-permute-done((bf16[16,2048]{1,0:T(8,128)(2,1)S(1)}, bf16[16,2048]{1,0:T(8,128)(2,1)S(1)}, u32[]{:S(2)}, u32[]{:S(2)}) %collective-permute-start.7) | collective-permute-done | bytes 65568 | tf_op jit(solution)/shard_map/ppermute | solution.py:27
  33.7 3.8 %collective-permute-done.8.refs_2_ = bf16[16,2048]{1,0:T(8,128)(2,1)S(1)} collective-permute-done((bf16[16,2048]{1,0:T(8,128)(2,1)S(1)}, bf16[16,2048]{1,0:T(8,128)(2,1)S(1)}, u32[]{:S(2)}, u32[]{:S(2)}) %collective-permute-start.8) | collective-permute-done | bytes 65568 | tf_op jit(solution)/shard_map/ppermute | solution.py:27
  37.6 1.5 %collective-permute-start.11 = (bf16[16,2048]{1,0:T(8,128)(2,1)S(1)}, bf16[16,2048]{1,0:T(8,128)(2,1)S(1)}, u32[]{:S(2)}, u32[]{:S(2)}) collective-permute-start(bf16[16,2048]{1,0:T(8,128)(2,1)S(1)} %shard_map.102), channel_id=1, source_target_pairs={{0,9},{1,8},{2,11},{3,10},{4,13},{5,12},{6,15},{7,14},{8,17},{9,16... | collective-permute-start | bytes 196616 | tf_op jit(solution)/shard_map/ppermute | solution.py:27
  40.1 2.9 %collective-permute-done.11.across_ref = bf16[16,2048]{1,0:T(8,128)(2,1)S(1)} collective-permute-done((bf16[16,2048]{1,0:T(8,128)(2,1)S(1)}, bf16[16,2048]{1,0:T(8,128)(2,1)S(1)}, u32[]{:S(2)}, u32[]{:S(2)}) %collective-permute-start.11) | collective-permute-done | bytes 65568 | tf_op jit(solution)/shard_map/ppermute | solution.py:27
  44.1 1.9 %collective-permute-start.14 = (bf16[16,2048]{1,0:T(8,128)(2,1)S(1)}, bf16[16,2048]{1,0:T(8,128)(2,1)S(1)}, u32[]{:S(2)}, u32[]{:S(2)}) collective-permute-start(bf16[16,2048]{1,0:T(8,128)(2,1)S(1)} %get-tuple-element.62.refs_0_), channel_id=1, source_target_pairs={{0,6},{1,7},{2,4},{3,5},{4,2},{5,3},{6,0},{7,1},{8,14},{9,15},{10,... | collective-permute-start | bytes 196616 | tf_op jit(solution)/shard_map/ppermute | solution.py:27
  46.0 2.5 %collective-permute-start.12 = (bf16[16,2048]{1,0:T(8,128)(2,1)S(1)}, bf16[16,2048]{1,0:T(8,128)(2,1)S(1)}, u32[]{:S(2)}, u32[]{:S(2)}) collective-permute-start(bf16[16,2048]{1,0:T(8,128)(2,1)S(1)} %get-tuple-element.62.refs_0_), channel_id=1, source_target_pairs={{0,2},{1,3},{2,0},{3,1},{4,6},{5,7},{6,4},{7,5},{8,10},{9,11},{10,... | collective-permute-start | bytes 196616 | tf_op jit(solution)/shard_map/ppermute | solution.py:27
  48.5 2.5 %load.4.refs_15_ = bf16[2048,640]{1,0:T(8,128)(2,1)S(1)} custom-call(bf16[2,640,2048]{2,1,0:T(8,128)(2,1)} %bitcast.25), custom_call_target="tpu_custom_call" | custom-call | tf_op jit(solution)/shard_map/load/pallas_call | solution.py:289
  51.1 2.9 %load.5 = (bf16[2048,640]{1,0:T(8,128)(2,1)S(1)}, bf16[640,2048]{1,0:T(8,128)(2,1)S(1)}) custom-call(bf16[2,640,2048]{2,1,0:T(8,128)(2,1)} %bitcast.21, bf16[2,640,2048]{2,1,0:T(8,128)(2,1)} %bitcast.23), custom_call_target="tpu_custom_call" | custom-call | tf_op jit(solution)/shard_map/load/pallas_call | solution.py:289
  54.0 2.3 %layer.7 = (f32[16,2048]{1,0:T(8,128)S(1)}, bf16[16,2048]{1,0:T(8,128)(2,1)S(1)}, bf16[16,2048]{1,0:T(8,128)(2,1)S(1)}, bf16[16,2048]{1,0:T(8,128)(2,1)S(1)}) custom-call(bf16[16,2048]{1,0:T(8,128)(2,1)S(1)} %get-tuple-element.62.refs_0_, bf16[16,2048]{1,0:T(8,128)(2,1)S(1)} %collective-permute-done.12.refs_1_, ...), custom_call_target="tpu_custom_call" | custom-call | flops 629145600 | bytes 9830400 | tf_op jit(solution)/shard_map/layer/pallas_call | solution.py:191
  56.3 1.9 %collective-permute-start.16 = (bf16[16,2048]{1,0:T(8,128)(2,1)S(1)}, bf16[16,2048]{1,0:T(8,128)(2,1)S(1)}, u32[]{:S(2)}, u32[]{:S(2)}) collective-permute-start(bf16[16,2048]{1,0:T(8,128)(2,1)S(1)} %get-tuple-element.73), channel_id=1, source_target_pairs={{0,6},{1,7},{2,4},{3,5},{4,2},{5,3},{6,0},{7,1},{8,14},{9,15},{10,... | collective-permute-start | bytes 196616 | tf_op jit(solution)/shard_map/ppermute | solution.py:27
  58.3 2.5 %collective-permute-start.18 = (bf16[16,2048]{1,0:T(8,128)(2,1)S(1)}, bf16[16,2048]{1,0:T(8,128)(2,1)S(1)}, u32[]{:S(2)}, u32[]{:S(2)}) collective-permute-start(bf16[16,2048]{1,0:T(8,128)(2,1)S(1)} %get-tuple-element.75), channel_id=1, source_target_pairs={{0,2},{1,3},{2,0},{3,1},{4,6},{5,7},{6,4},{7,5},{8,10},{9,11},{10,... | collective-permute-start | bytes 196616 | tf_op jit(solution)/shard_map/ppermute | solution.py:27
  60.8 1.7 %collective-permute-done.16.refs_1_ = bf16[16,2048]{1,0:T(8,128)(2,1)S(1)} collective-permute-done((bf16[16,2048]{1,0:T(8,128)(2,1)S(1)}, bf16[16,2048]{1,0:T(8,128)(2,1)S(1)}, u32[]{:S(2)}, u32[]{:S(2)}) %collective-permute-start.16) | collective-permute-done | bytes 65568 | tf_op jit(solution)/shard_map/ppermute | solution.py:27
  62.5 1.4 %collective-permute-done.17.refs_2_ = bf16[16,2048]{1,0:T(8,128)(2,1)S(1)} collective-permute-done((bf16[16,2048]{1,0:T(8,128)(2,1)S(1)}, bf16[16,2048]{1,0:T(8,128)(2,1)S(1)}, u32[]{:S(2)}, u32[]{:S(2)}) %collective-permute-start.17) | collective-permute-done | bytes 65568 | tf_op jit(solution)/shard_map/ppermute | solution.py:27
  64.1 1.2 %collective-permute-start.19 = (bf16[16,2048]{1,0:T(8,128)(2,1)S(1)}, bf16[16,2048]{1,0:T(8,128)(2,1)S(1)}, u32[]{:S(2)}, u32[]{:S(2)}) collective-permute-start(bf16[16,2048]{1,0:T(8,128)(2,1)S(1)} %shard_map.104), channel_id=1, source_target_pairs={{0,8},{1,9},{2,10},{3,11},{4,12},{5,13},{6,14},{7,15},{8,16},{9,17... | collective-permute-start | bytes 196616 | tf_op jit(solution)/shard_map/ppermute | solution.py:27
  65.3 3.4 %collective-permute-done.20.across_ref = bf16[16,2048]{1,0:T(8,128)(2,1)S(1)} collective-permute-done((bf16[16,2048]{1,0:T(8,128)(2,1)S(1)}, bf16[16,2048]{1,0:T(8,128)(2,1)S(1)}, u32[]{:S(2)}, u32[]{:S(2)}) %collective-permute-start.20) | collective-permute-done | bytes 65568 | tf_op jit(solution)/shard_map/ppermute | solution.py:27
  69.0 1.8 %collective-permute-start.23 = (bf16[16,2048]{1,0:T(8,128)(2,1)S(1)}, bf16[16,2048]{1,0:T(8,128)(2,1)S(1)}, u32[]{:S(2)}, u32[]{:S(2)}) collective-permute-start(bf16[16,2048]{1,0:T(8,128)(2,1)S(1)} %get-tuple-element.76.refs_0_), channel_id=1, source_target_pairs={{0,6},{1,7},{2,4},{3,5},{4,2},{5,3},{6,0},{7,1},{8,14},{9,15},{10,... | collective-permute-start | bytes 196616 | tf_op jit(solution)/shard_map/ppermute | solution.py:27
  71.5 2.0 %collective-permute-start.21 = (bf16[16,2048]{1,0:T(8,128)(2,1)S(1)}, bf16[16,2048]{1,0:T(8,128)(2,1)S(1)}, u32[]{:S(2)}, u32[]{:S(2)}) collective-permute-start(bf16[16,2048]{1,0:T(8,128)(2,1)S(1)} %get-tuple-element.76.refs_0_), channel_id=1, source_target_pairs={{0,2},{1,3},{2,0},{3,1},{4,6},{5,7},{6,4},{7,5},{8,10},{9,11},{10,... | collective-permute-start | bytes 196616 | tf_op jit(solution)/shard_map/ppermute | solution.py:27
  73.5 1.8 %collective-permute-done.23.refs_3_ = bf16[16,2048]{1,0:T(8,128)(2,1)S(1)} collective-permute-done((bf16[16,2048]{1,0:T(8,128)(2,1)S(1)}, bf16[16,2048]{1,0:T(8,128)(2,1)S(1)}, u32[]{:S(2)}, u32[]{:S(2)}) %collective-permute-start.23) | collective-permute-done | bytes 65568 | tf_op jit(solution)/shard_map/ppermute | solution.py:27
  75.2 1.4 %collective-permute-done.22.refs_2_ = bf16[16,2048]{1,0:T(8,128)(2,1)S(1)} collective-permute-done((bf16[16,2048]{1,0:T(8,128)(2,1)S(1)}, bf16[16,2048]{1,0:T(8,128)(2,1)S(1)}, u32[]{:S(2)}, u32[]{:S(2)}) %collective-permute-start.22) | collective-permute-done | bytes 65568 | tf_op jit(solution)/shard_map/ppermute | solution.py:27
  76.6 2.4 %layer.8 = (f32[16,2048]{1,0:T(8,128)S(1)}, bf16[16,2048]{1,0:T(8,128)(2,1)S(1)}, bf16[16,2048]{1,0:T(8,128)(2,1)S(1)}, bf16[16,2048]{1,0:T(8,128)(2,1)S(1)}) custom-call(bf16[16,2048]{1,0:T(8,128)(2,1)S(1)} %get-tuple-element.76.refs_0_, bf16[16,2048]{1,0:T(8,128)(2,1)S(1)} %collective-permute-done.21.refs_1_, ...), custom_call_target="tpu_custom_call" | custom-call | flops 629145600 | bytes 9830400 | tf_op jit(solution)/shard_map/layer/pallas_call | solution.py:191
  79.1 1.8 %collective-permute-start.25 = (bf16[16,2048]{1,0:T(8,128)(2,1)S(1)}, bf16[16,2048]{1,0:T(8,128)(2,1)S(1)}, u32[]{:S(2)}, u32[]{:S(2)}) collective-permute-start(bf16[16,2048]{1,0:T(8,128)(2,1)S(1)} %get-tuple-element.80), channel_id=1, source_target_pairs={{0,6},{1,7},{2,4},{3,5},{4,2},{5,3},{6,0},{7,1},{8,14},{9,15},{10,... | collective-permute-start | bytes 196616 | tf_op jit(solution)/shard_map/ppermute | solution.py:27
  81.7 1.8 %collective-permute-start.27 = (bf16[16,2048]{1,0:T(8,128)(2,1)S(1)}, bf16[16,2048]{1,0:T(8,128)(2,1)S(1)}, u32[]{:S(2)}, u32[]{:S(2)}) collective-permute-start(bf16[16,2048]{1,0:T(8,128)(2,1)S(1)} %get-tuple-element.82), channel_id=1, source_target_pairs={{0,2},{1,3},{2,0},{3,1},{4,6},{5,7},{6,4},{7,5},{8,10},{9,11},{10,... | collective-permute-start | bytes 196616 | tf_op jit(solution)/shard_map/ppermute | solution.py:27
  83.5 1.7 %collective-permute-done.25.refs_1_ = bf16[16,2048]{1,0:T(8,128)(2,1)S(1)} collective-permute-done((bf16[16,2048]{1,0:T(8,128)(2,1)S(1)}, bf16[16,2048]{1,0:T(8,128)(2,1)S(1)}, u32[]{:S(2)}, u32[]{:S(2)}) %collective-permute-start.25) | collective-permute-done | bytes 65568 | tf_op jit(solution)/shard_map/ppermute | solution.py:27
  85.2 1.5 %collective-permute-done.26.refs_2_ = bf16[16,2048]{1,0:T(8,128)(2,1)S(1)} collective-permute-done((bf16[16,2048]{1,0:T(8,128)(2,1)S(1)}, bf16[16,2048]{1,0:T(8,128)(2,1)S(1)}, u32[]{:S(2)}, u32[]{:S(2)}) %collective-permute-start.26) | collective-permute-done | bytes 65568 | tf_op jit(solution)/shard_map/ppermute | solution.py:27
  86.7 1.6 %collective-permute-start.29 = (bf16[16,2048]{1,0:T(8,128)(2,1)S(1)}, bf16[16,2048]{1,0:T(8,128)(2,1)S(1)}, u32[]{:S(2)}, u32[]{:S(2)}) collective-permute-start(bf16[16,2048]{1,0:T(8,128)(2,1)S(1)} %shard_map.106), channel_id=1, source_target_pairs={{0,9},{1,8},{2,11},{3,10},{4,13},{5,12},{6,15},{7,14},{8,17},{9,16... | collective-permute-start | bytes 196616 | tf_op jit(solution)/shard_map/ppermute | solution.py:27
  88.9 2.8 %collective-permute-done.29.across_ref = bf16[16,2048]{1,0:T(8,128)(2,1)S(1)} collective-permute-done((bf16[16,2048]{1,0:T(8,128)(2,1)S(1)}, bf16[16,2048]{1,0:T(8,128)(2,1)S(1)}, u32[]{:S(2)}, u32[]{:S(2)}) %collective-permute-start.29) | collective-permute-done | bytes 65568 | tf_op jit(solution)/shard_map/ppermute | solution.py:27
  92.5 1.8 %collective-permute-start.32 = (bf16[16,2048]{1,0:T(8,128)(2,1)S(1)}, bf16[16,2048]{1,0:T(8,128)(2,1)S(1)}, u32[]{:S(2)}, u32[]{:S(2)}) collective-permute-start(bf16[16,2048]{1,0:T(8,128)(2,1)S(1)} %get-tuple-element.83.refs_0_), channel_id=1, source_target_pairs={{0,6},{1,7},{2,4},{3,5},{4,2},{5,3},{6,0},{7,1},{8,14},{9,15},{10,... | collective-permute-start | bytes 196616 | tf_op jit(solution)/shard_map/ppermute | solution.py:27
  94.8 2.1 %collective-permute-start.30 = (bf16[16,2048]{1,0:T(8,128)(2,1)S(1)}, bf16[16,2048]{1,0:T(8,128)(2,1)S(1)}, u32[]{:S(2)}, u32[]{:S(2)}) collective-permute-start(bf16[16,2048]{1,0:T(8,128)(2,1)S(1)} %get-tuple-element.83.refs_0_), channel_id=1, source_target_pairs={{0,2},{1,3},{2,0},{3,1},{4,6},{5,7},{6,4},{7,5},{8,10},{9,11},{10,... | collective-permute-start | bytes 196616 | tf_op jit(solution)/shard_map/ppermute | solution.py:27
  97.0 1.9 %collective-permute-done.32.refs_3_ = bf16[16,2048]{1,0:T(8,128)(2,1)S(1)} collective-permute-done((bf16[16,2048]{1,0:T(8,128)(2,1)S(1)}, bf16[16,2048]{1,0:T(8,128)(2,1)S(1)}, u32[]{:S(2)}, u32[]{:S(2)}) %collective-permute-start.32) | collective-permute-done | bytes 65568 | tf_op jit(solution)/shard_map/ppermute | solution.py:27
  98.9 2.4 %collective-permute-done.31.refs_2_ = bf16[16,2048]{1,0:T(8,128)(2,1)S(1)} collective-permute-done((bf16[16,2048]{1,0:T(8,128)(2,1)S(1)}, bf16[16,2048]{1,0:T(8,128)(2,1)S(1)}, u32[]{:S(2)}, u32[]{:S(2)}) %collective-permute-start.31) | collective-permute-done | bytes 65568 | tf_op jit(solution)/shard_map/ppermute | solution.py:27
  101.3 2.3 %layer.9 = (f32[16,2048]{1,0:T(8,128)S(1)}, bf16[16,2048]{1,0:T(8,128)(2,1)S(1)}, bf16[16,2048]{1,0:T(8,128)(2,1)S(1)}, bf16[16,2048]{1,0:T(8,128)(2,1)S(1)}) custom-call(bf16[16,2048]{1,0:T(8,128)(2,1)S(1)} %get-tuple-element.83.refs_0_, bf16[16,2048]{1,0:T(8,128)(2,1)S(1)} %collective-permute-done.30.refs_1_, ...), custom_call_target="tpu_custom_call" | custom-call | flops 629145600 | bytes 9830400 | tf_op jit(solution)/shard_map/layer/pallas_call | solution.py:191
  103.6 1.9 %collective-permute-start.33 = (bf16[16,2048]{1,0:T(8,128)(2,1)S(1)}, bf16[16,2048]{1,0:T(8,128)(2,1)S(1)}, u32[]{:S(2)}, u32[]{:S(2)}) collective-permute-start(bf16[16,2048]{1,0:T(8,128)(2,1)S(1)} %get-tuple-element.86), channel_id=1, source_target_pairs={{0,6},{1,7},{2,4},{3,5},{4,2},{5,3},{6,0},{7,1},{8,14},{9,15},{10,... | collective-permute-start | bytes 196616 | tf_op jit(solution)/shard_map/ppermute | solution.py:27
  105.5 2.6 %collective-permute-start.35 = (bf16[16,2048]{1,0:T(8,128)(2,1)S(1)}, bf16[16,2048]{1,0:T(8,128)(2,1)S(1)}, u32[]{:S(2)}, u32[]{:S(2)}) collective-permute-start(bf16[16,2048]{1,0:T(8,128)(2,1)S(1)} %get-tuple-element.88), channel_id=1, source_target_pairs={{0,2},{1,3},{2,0},{3,1},{4,6},{5,7},{6,4},{7,5},{8,10},{9,11},{10,... | collective-permute-start | bytes 196616 | tf_op jit(solution)/shard_map/ppermute | solution.py:27
  108.0 2.0 %collective-permute-done.33 = bf16[16,2048]{1,0:T(8,128)(2,1)S(1)} collective-permute-done((bf16[16,2048]{1,0:T(8,128)(2,1)S(1)}, bf16[16,2048]{1,0:T(8,128)(2,1)S(1)}, u32[]{:S(2)}, u32[]{:S(2)}) %collective-permute-start.33) | collective-permute-done | bytes 65568 | tf_op jit(solution)/shard_map/ppermute | solution.py:27
  110.0 2.0 %collective-permute-done.34 = bf16[16,2048]{1,0:T(8,128)(2,1)S(1)} collective-permute-done((bf16[16,2048]{1,0:T(8,128)(2,1)S(1)}, bf16[16,2048]{1,0:T(8,128)(2,1)S(1)}, u32[]{:S(2)}, u32[]{:S(2)}) %collective-permute-start.34) | collective-permute-done | bytes 65568 | tf_op jit(solution)/shard_map/ppermute | solution.py:27
  113.0 3.0 %collective-permute-done.36 = bf16[8,2048]{1,0:T(8,128)(2,1)S(1)} collective-permute-done((bf16[8,2048]{1,0:T(8,128)(2,1)S(1)}, bf16[8,2048]{1,0:T(8,128)(2,1)S(1)}, u32[]{:S(2)}, u32[]{:S(2)}) %collective-permute-start.36) | collective-permute-done | bytes 32800 | tf_op jit(solution)/shard_map/ppermute | solution.py:27
  (56 shorter events, 11.9 us)
Async XLA Ops:
  0.0 5.8 %copy-start.3 = (f32[4,1,8,2]{2,3,1,0:T(2,128)S(1)}, f32[4,1,8,2]{2,3,1,0:T(2,128)}, u32[]{:S(2)}) copy-start(f32[4,1,8,2]{2,3,1,0:T(2,128)} %param.12) | copy-start | bytes 772
  0.0 5.8 %copy-start.2 = (s32[4,1,8,2]{2,3,1,0:T(2,128)S(1)}, s32[4,1,8,2]{2,3,1,0:T(2,128)}, u32[]{:S(2)}) copy-start(s32[4,1,8,2]{2,3,1,0:T(2,128)} %param.11) | copy-start | bytes 772
  0.0 5.8 %copy-start = (bf16[1,8,2048]{2,1,0:T(8,128)(2,1)S(1)}, bf16[1,8,2048]{2,1,0:T(8,128)(2,1)}, u32[]{:S(2)}) copy-start(bf16[1,8,2048]{2,1,0:T(8,128)(2,1)} %param.10) | copy-start | bytes 98308
  0.0 5.8 %copy-start.1 = (f32[2,1,2048]{2,1,0:T(1,128)S(1)}, f32[2,1,2048]{2,1,0:T(1,128)}, u32[]{:S(2)}) copy-start(f32[2,1,2048]{2,1,0:T(1,128)} %gain_ref.7) | copy-start | bytes 49156
  1.1 25.4 %collective-permute-start.4 = (bf16[160,2048]{1,0:T(8,128)(2,1)S(1)}, bf16[160,2048]{1,0:T(8,128)(2,1)S(1)}, u32[]{:S(2)}, u32[]{:S(2)}) collective-permute-start(bf16[160,2048]{1,0:T(8,128)(2,1)S(1)} %fill.2), channel_id=1, source_target_pairs={{0,24},{1,25},{2,26},{3,27},{4,28},{5,29},{6,30},{7,31},{8,0},{9,1... | collective-permute-start | bytes 1966088 | tf_op jit(solution)/shard_map/ppermute | solution.py:27
  5.0 21.6 %collective-permute-start.5 = (bf16[160,2048]{1,0:T(8,128)(2,1)S(1)}, bf16[160,2048]{1,0:T(8,128)(2,1)S(1)}, u32[]{:S(2)}, u32[]{:S(2)}) collective-permute-start(bf16[160,2048]{1,0:T(8,128)(2,1)S(1)} %get-tuple-element.56), channel_id=1, source_target_pairs={{0,24},{1,25},{2,26},{3,27},{4,28},{5,29},{6,30},{7,31},{8,0},{9,1... | collective-permute-start | bytes 1966088 | tf_op jit(solution)/shard_map/ppermute | solution.py:27
  5.7 20.9 %collective-permute-start.6 = (bf16[160,2048]{1,0:T(8,128)(2,1)S(1)}, bf16[160,2048]{1,0:T(8,128)(2,1)S(1)}, u32[]{:S(2)}, u32[]{:S(2)}) collective-permute-start(bf16[160,2048]{1,0:T(8,128)(2,1)S(1)} %get-tuple-element.57), channel_id=1, source_target_pairs={{0,24},{1,25},{2,26},{3,27},{4,28},{5,29},{6,30},{7,31},{8,0},{9,1... | collective-permute-start | bytes 1966088 | tf_op jit(solution)/shard_map/ppermute | solution.py:27
  6.0 4.0 %collective-permute-start = (bf16[8,2176]{1,0:T(8,128)(2,1)S(1)}, bf16[8,2176]{1,0:T(8,128)(2,1)S(1)}, u32[]{:S(2)}, u32[]{:S(2)}) collective-permute-start(bf16[8,2176]{1,0:T(8,128)(2,1)S(1)} %shard_map.100.first_ref), channel_id=1, source_target_pairs={{0,1},{1,0},{2,3},{3,2},{4,5},{5,4},{6,7},{7,6},{8,9},{9,8},{10,11... | collective-permute-start | bytes 104456 | tf_op jit(solution)/shard_map/ppermute | solution.py:27
  10.0 4.4 %collective-permute-start.1 = (bf16[16,2176]{1,0:T(8,128)(2,1)S(1)}, bf16[16,2176]{1,0:T(8,128)(2,1)S(1)}, u32[]{:S(2)}, u32[]{:S(2)}) collective-permute-start(bf16[16,2176]{1,0:T(8,128)(2,1)S(1)} %shard_map.101.refs_0_.refs_4_), channel_id=1, source_target_pairs={{0,2},{1,3},{2,0},{3,1},{4,6},{5,7},{6,4},{7,5},{8,10},{9,11},{10,... | collective-permute-start | bytes 208904 | tf_op jit(solution)/shard_map/ppermute | solution.py:27
  11.6 6.2 %collective-permute-start.3 = (bf16[16,2176]{1,0:T(8,128)(2,1)S(1)}, bf16[16,2176]{1,0:T(8,128)(2,1)S(1)}, u32[]{:S(2)}, u32[]{:S(2)}) collective-permute-start(bf16[16,2176]{1,0:T(8,128)(2,1)S(1)} %shard_map.101.refs_0_.refs_4_), channel_id=1, source_target_pairs={{0,6},{1,7},{2,4},{3,5},{4,2},{5,3},{6,0},{7,1},{8,14},{9,15},{10,... | collective-permute-start | bytes 208904 | tf_op jit(solution)/shard_map/ppermute | solution.py:27
  15.9 38.1 %collective-permute-start.15 = (bf16[3,160,2048]{2,1,0:T(8,128)(2,1)S(1)}, bf16[3,160,2048]{2,1,0:T(8,128)(2,1)S(1)}, u32[]{:S(2)}, u32[]{:S(2)}) collective-permute-start(bf16[3,160,2048]{2,1,0:T(8,128)(2,1)S(1)} %stack.1), channel_id=1, source_target_pairs={{0,8},{1,9},{2,10},{3,11},{4,12},{5,13},{6,14},{7,15},{8,0},{9,1},... | collective-permute-start | bytes 5898248 | tf_op jit(solution)/shard_map/ppermute | solution.py:58
  17.8 7.2 %collective-permute-start.2 = (bf16[16,2176]{1,0:T(8,128)(2,1)S(1)}, bf16[16,2176]{1,0:T(8,128)(2,1)S(1)}, u32[]{:S(2)}, u32[]{:S(2)}) collective-permute-start(bf16[16,2176]{1,0:T(8,128)(2,1)S(1)} %shard_map.101.refs_0_.refs_4_), channel_id=1, source_target_pairs={{0,4},{1,5},{2,6},{3,7},{4,0},{5,1},{6,2},{7,3},{8,12},{9,13},{10,... | collective-permute-start | bytes 208904 | tf_op jit(solution)/shard_map/ppermute | solution.py:27
  27.4 6.4 %collective-permute-start.7 = (bf16[16,2048]{1,0:T(8,128)(2,1)S(1)}, bf16[16,2048]{1,0:T(8,128)(2,1)S(1)}, u32[]{:S(2)}, u32[]{:S(2)}) collective-permute-start(bf16[16,2048]{1,0:T(8,128)(2,1)S(1)} %get-tuple-element.59), channel_id=1, source_target_pairs={{0,6},{1,7},{2,4},{3,5},{4,2},{5,3},{6,0},{7,1},{8,14},{9,15},{10,... | collective-permute-start | bytes 196616 | tf_op jit(solution)/shard_map/ppermute | solution.py:27
  30.9 6.5 %collective-permute-start.8 = (bf16[16,2048]{1,0:T(8,128)(2,1)S(1)}, bf16[16,2048]{1,0:T(8,128)(2,1)S(1)}, u32[]{:S(2)}, u32[]{:S(2)}) collective-permute-start(bf16[16,2048]{1,0:T(8,128)(2,1)S(1)} %get-tuple-element.60), channel_id=1, source_target_pairs={{0,4},{1,5},{2,6},{3,7},{4,0},{5,1},{6,2},{7,3},{8,12},{9,13},{10,... | collective-permute-start | bytes 196616 | tf_op jit(solution)/shard_map/ppermute | solution.py:27
  31.1 6.4 %collective-permute-start.9 = (bf16[16,2048]{1,0:T(8,128)(2,1)S(1)}, bf16[16,2048]{1,0:T(8,128)(2,1)S(1)}, u32[]{:S(2)}, u32[]{:S(2)}) collective-permute-start(bf16[16,2048]{1,0:T(8,128)(2,1)S(1)} %get-tuple-element.61), channel_id=1, source_target_pairs={{0,2},{1,3},{2,0},{3,1},{4,6},{5,7},{6,4},{7,5},{8,10},{9,11},{10,... | collective-permute-start | bytes 196616 | tf_op jit(solution)/shard_map/ppermute | solution.py:27
  37.5 39.1 %collective-permute-start.24 = (bf16[3,160,2048]{2,1,0:T(8,128)(2,1)S(1)}, bf16[3,160,2048]{2,1,0:T(8,128)(2,1)S(1)}, u32[]{:S(2)}, u32[]{:S(2)}) collective-permute-start(bf16[3,160,2048]{2,1,0:T(8,128)(2,1)S(1)} %stack.1), channel_id=1, source_target_pairs={{0,24},{1,25},{2,26},{3,27},{4,28},{5,29},{6,30},{7,31},{8,0},{9,1... | collective-permute-start | bytes 5898248 | tf_op jit(solution)/shard_map/ppermute | solution.py:27
  37.6 5.4 %collective-permute-start.11 = (bf16[16,2048]{1,0:T(8,128)(2,1)S(1)}, bf16[16,2048]{1,0:T(8,128)(2,1)S(1)}, u32[]{:S(2)}, u32[]{:S(2)}) collective-permute-start(bf16[16,2048]{1,0:T(8,128)(2,1)S(1)} %shard_map.102), channel_id=1, source_target_pairs={{0,9},{1,8},{2,11},{3,10},{4,13},{5,12},{6,15},{7,14},{8,17},{9,16... | collective-permute-start | bytes 196616 | tf_op jit(solution)/shard_map/ppermute | solution.py:27
  39.2 4.8 %collective-permute-start.10 = (bf16[16,2048]{1,0:T(8,128)(2,1)S(1)}, bf16[16,2048]{1,0:T(8,128)(2,1)S(1)}, u32[]{:S(2)}, u32[]{:S(2)}) collective-permute-start(bf16[16,2048]{1,0:T(8,128)(2,1)S(1)} %shard_map.102), channel_id=1, source_target_pairs={{0,8},{1,9},{2,10},{3,11},{4,12},{5,13},{6,14},{7,15},{8,16},{9,17... | collective-permute-start | bytes 196616 | tf_op jit(solution)/shard_map/ppermute | solution.py:27
  44.1 9.9 %collective-permute-start.14 = (bf16[16,2048]{1,0:T(8,128)(2,1)S(1)}, bf16[16,2048]{1,0:T(8,128)(2,1)S(1)}, u32[]{:S(2)}, u32[]{:S(2)}) collective-permute-start(bf16[16,2048]{1,0:T(8,128)(2,1)S(1)} %get-tuple-element.62.refs_0_), channel_id=1, source_target_pairs={{0,6},{1,7},{2,4},{3,5},{4,2},{5,3},{6,0},{7,1},{8,14},{9,15},{10,... | collective-permute-start | bytes 196616 | tf_op jit(solution)/shard_map/ppermute | solution.py:27
  46.0 8.0 %collective-permute-start.13 = (bf16[16,2048]{1,0:T(8,128)(2,1)S(1)}, bf16[16,2048]{1,0:T(8,128)(2,1)S(1)}, u32[]{:S(2)}, u32[]{:S(2)}) collective-permute-start(bf16[16,2048]{1,0:T(8,128)(2,1)S(1)} %get-tuple-element.62.refs_0_), channel_id=1, source_target_pairs={{0,4},{1,5},{2,6},{3,7},{4,0},{5,1},{6,2},{7,3},{8,12},{9,13},{10,... | collective-permute-start | bytes 196616 | tf_op jit(solution)/shard_map/ppermute | solution.py:27
  46.0 8.0 %collective-permute-start.12 = (bf16[16,2048]{1,0:T(8,128)(2,1)S(1)}, bf16[16,2048]{1,0:T(8,128)(2,1)S(1)}, u32[]{:S(2)}, u32[]{:S(2)}) collective-permute-start(bf16[16,2048]{1,0:T(8,128)(2,1)S(1)} %get-tuple-element.62.refs_0_), channel_id=1, source_target_pairs={{0,2},{1,3},{2,0},{3,1},{4,6},{5,7},{6,4},{7,5},{8,10},{9,11},{10,... | collective-permute-start | bytes 196616 | tf_op jit(solution)/shard_map/ppermute | solution.py:27
  56.3 6.1 %collective-permute-start.16 = (bf16[16,2048]{1,0:T(8,128)(2,1)S(1)}, bf16[16,2048]{1,0:T(8,128)(2,1)S(1)}, u32[]{:S(2)}, u32[]{:S(2)}) collective-permute-start(bf16[16,2048]{1,0:T(8,128)(2,1)S(1)} %get-tuple-element.73), channel_id=1, source_target_pairs={{0,6},{1,7},{2,4},{3,5},{4,2},{5,3},{6,0},{7,1},{8,14},{9,15},{10,... | collective-permute-start | bytes 196616 | tf_op jit(solution)/shard_map/ppermute | solution.py:27
  58.3 5.6 %collective-permute-start.17 = (bf16[16,2048]{1,0:T(8,128)(2,1)S(1)}, bf16[16,2048]{1,0:T(8,128)(2,1)S(1)}, u32[]{:S(2)}, u32[]{:S(2)}) collective-permute-start(bf16[16,2048]{1,0:T(8,128)(2,1)S(1)} %get-tuple-element.74), channel_id=1, source_target_pairs={{0,4},{1,5},{2,6},{3,7},{4,0},{5,1},{6,2},{7,3},{8,12},{9,13},{10,... | collective-permute-start | bytes 196616 | tf_op jit(solution)/shard_map/ppermute | solution.py:27
  58.3 5.6 %collective-permute-start.18 = (bf16[16,2048]{1,0:T(8,128)(2,1)S(1)}, bf16[16,2048]{1,0:T(8,128)(2,1)S(1)}, u32[]{:S(2)}, u32[]{:S(2)}) collective-permute-start(bf16[16,2048]{1,0:T(8,128)(2,1)S(1)} %get-tuple-element.75), channel_id=1, source_target_pairs={{0,2},{1,3},{2,0},{3,1},{4,6},{5,7},{6,4},{7,5},{8,10},{9,11},{10,... | collective-permute-start | bytes 196616 | tf_op jit(solution)/shard_map/ppermute | solution.py:27
  63.9 4.7 %collective-permute-start.20 = (bf16[16,2048]{1,0:T(8,128)(2,1)S(1)}, bf16[16,2048]{1,0:T(8,128)(2,1)S(1)}, u32[]{:S(2)}, u32[]{:S(2)}) collective-permute-start(bf16[16,2048]{1,0:T(8,128)(2,1)S(1)} %shard_map.104), channel_id=1, source_target_pairs={{0,9},{1,8},{2,11},{3,10},{4,13},{5,12},{6,15},{7,14},{8,17},{9,16... | collective-permute-start | bytes 196616 | tf_op jit(solution)/shard_map/ppermute | solution.py:27
  64.1 4.8 %collective-permute-start.19 = (bf16[16,2048]{1,0:T(8,128)(2,1)S(1)}, bf16[16,2048]{1,0:T(8,128)(2,1)S(1)}, u32[]{:S(2)}, u32[]{:S(2)}) collective-permute-start(bf16[16,2048]{1,0:T(8,128)(2,1)S(1)} %shard_map.104), channel_id=1, source_target_pairs={{0,8},{1,9},{2,10},{3,11},{4,12},{5,13},{6,14},{7,15},{8,16},{9,17... | collective-permute-start | bytes 196616 | tf_op jit(solution)/shard_map/ppermute | solution.py:27
  69.0 6.2 %collective-permute-start.23 = (bf16[16,2048]{1,0:T(8,128)(2,1)S(1)}, bf16[16,2048]{1,0:T(8,128)(2,1)S(1)}, u32[]{:S(2)}, u32[]{:S(2)}) collective-permute-start(bf16[16,2048]{1,0:T(8,128)(2,1)S(1)} %get-tuple-element.76.refs_0_), channel_id=1, source_target_pairs={{0,6},{1,7},{2,4},{3,5},{4,2},{5,3},{6,0},{7,1},{8,14},{9,15},{10,... | collective-permute-start | bytes 196616 | tf_op jit(solution)/shard_map/ppermute | solution.py:27
  70.8 5.8 %collective-permute-start.22 = (bf16[16,2048]{1,0:T(8,128)(2,1)S(1)}, bf16[16,2048]{1,0:T(8,128)(2,1)S(1)}, u32[]{:S(2)}, u32[]{:S(2)}) collective-permute-start(bf16[16,2048]{1,0:T(8,128)(2,1)S(1)} %get-tuple-element.76.refs_0_), channel_id=1, source_target_pairs={{0,4},{1,5},{2,6},{3,7},{4,0},{5,1},{6,2},{7,3},{8,12},{9,13},{10,... | collective-permute-start | bytes 196616 | tf_op jit(solution)/shard_map/ppermute | solution.py:27
  71.5 5.1 %collective-permute-start.21 = (bf16[16,2048]{1,0:T(8,128)(2,1)S(1)}, bf16[16,2048]{1,0:T(8,128)(2,1)S(1)}, u32[]{:S(2)}, u32[]{:S(2)}) collective-permute-start(bf16[16,2048]{1,0:T(8,128)(2,1)S(1)} %get-tuple-element.76.refs_0_), channel_id=1, source_target_pairs={{0,2},{1,3},{2,0},{3,1},{4,6},{5,7},{6,4},{7,5},{8,10},{9,11},{10,... | collective-permute-start | bytes 196616 | tf_op jit(solution)/shard_map/ppermute | solution.py:27
  79.1 6.1 %collective-permute-start.25 = (bf16[16,2048]{1,0:T(8,128)(2,1)S(1)}, bf16[16,2048]{1,0:T(8,128)(2,1)S(1)}, u32[]{:S(2)}, u32[]{:S(2)}) collective-permute-start(bf16[16,2048]{1,0:T(8,128)(2,1)S(1)} %get-tuple-element.80), channel_id=1, source_target_pairs={{0,6},{1,7},{2,4},{3,5},{4,2},{5,3},{6,0},{7,1},{8,14},{9,15},{10,... | collective-permute-start | bytes 196616 | tf_op jit(solution)/shard_map/ppermute | solution.py:27
  80.9 5.8 %collective-permute-start.26 = (bf16[16,2048]{1,0:T(8,128)(2,1)S(1)}, bf16[16,2048]{1,0:T(8,128)(2,1)S(1)}, u32[]{:S(2)}, u32[]{:S(2)}) collective-permute-start(bf16[16,2048]{1,0:T(8,128)(2,1)S(1)} %get-tuple-element.81), channel_id=1, source_target_pairs={{0,4},{1,5},{2,6},{3,7},{4,0},{5,1},{6,2},{7,3},{8,12},{9,13},{10,... | collective-permute-start | bytes 196616 | tf_op jit(solution)/shard_map/ppermute | solution.py:27
  81.7 5.0 %collective-permute-start.27 = (bf16[16,2048]{1,0:T(8,128)(2,1)S(1)}, bf16[16,2048]{1,0:T(8,128)(2,1)S(1)}, u32[]{:S(2)}, u32[]{:S(2)}) collective-permute-start(bf16[16,2048]{1,0:T(8,128)(2,1)S(1)} %get-tuple-element.82), channel_id=1, source_target_pairs={{0,2},{1,3},{2,0},{3,1},{4,6},{5,7},{6,4},{7,5},{8,10},{9,11},{10,... | collective-permute-start | bytes 196616 | tf_op jit(solution)/shard_map/ppermute | solution.py:27
  86.7 5.0 %collective-permute-start.29 = (bf16[16,2048]{1,0:T(8,128)(2,1)S(1)}, bf16[16,2048]{1,0:T(8,128)(2,1)S(1)}, u32[]{:S(2)}, u32[]{:S(2)}) collective-permute-start(bf16[16,2048]{1,0:T(8,128)(2,1)S(1)} %shard_map.106), channel_id=1, source_target_pairs={{0,9},{1,8},{2,11},{3,10},{4,13},{5,12},{6,15},{7,14},{8,17},{9,16... | collective-permute-start | bytes 196616 | tf_op jit(solution)/shard_map/ppermute | solution.py:27
  88.3 4.1 %collective-permute-start.28 = (bf16[16,2048]{1,0:T(8,128)(2,1)S(1)}, bf16[16,2048]{1,0:T(8,128)(2,1)S(1)}, u32[]{:S(2)}, u32[]{:S(2)}) collective-permute-start(bf16[16,2048]{1,0:T(8,128)(2,1)S(1)} %shard_map.106), channel_id=1, source_target_pairs={{0,8},{1,9},{2,10},{3,11},{4,12},{5,13},{6,14},{7,15},{8,16},{9,17... | collective-permute-start | bytes 196616 | tf_op jit(solution)/shard_map/ppermute | solution.py:27
  92.5 6.4 %collective-permute-start.32 = (bf16[16,2048]{1,0:T(8,128)(2,1)S(1)}, bf16[16,2048]{1,0:T(8,128)(2,1)S(1)}, u32[]{:S(2)}, u32[]{:S(2)}) collective-permute-start(bf16[16,2048]{1,0:T(8,128)(2,1)S(1)} %get-tuple-element.83.refs_0_), channel_id=1, source_target_pairs={{0,6},{1,7},{2,4},{3,5},{4,2},{5,3},{6,0},{7,1},{8,14},{9,15},{10,... | collective-permute-start | bytes 196616 | tf_op jit(solution)/shard_map/ppermute | solution.py:27
  94.4 6.9 %collective-permute-start.31 = (bf16[16,2048]{1,0:T(8,128)(2,1)S(1)}, bf16[16,2048]{1,0:T(8,128)(2,1)S(1)}, u32[]{:S(2)}, u32[]{:S(2)}) collective-permute-start(bf16[16,2048]{1,0:T(8,128)(2,1)S(1)} %get-tuple-element.83.refs_0_), channel_id=1, source_target_pairs={{0,4},{1,5},{2,6},{3,7},{4,0},{5,1},{6,2},{7,3},{8,12},{9,13},{10,... | collective-permute-start | bytes 196616 | tf_op jit(solution)/shard_map/ppermute | solution.py:27
  94.8 6.5 %collective-permute-start.30 = (bf16[16,2048]{1,0:T(8,128)(2,1)S(1)}, bf16[16,2048]{1,0:T(8,128)(2,1)S(1)}, u32[]{:S(2)}, u32[]{:S(2)}) collective-permute-start(bf16[16,2048]{1,0:T(8,128)(2,1)S(1)} %get-tuple-element.83.refs_0_), channel_id=1, source_target_pairs={{0,2},{1,3},{2,0},{3,1},{4,6},{5,7},{6,4},{7,5},{8,10},{9,11},{10,... | collective-permute-start | bytes 196616 | tf_op jit(solution)/shard_map/ppermute | solution.py:27
  103.6 6.4 %collective-permute-start.33 = (bf16[16,2048]{1,0:T(8,128)(2,1)S(1)}, bf16[16,2048]{1,0:T(8,128)(2,1)S(1)}, u32[]{:S(2)}, u32[]{:S(2)}) collective-permute-start(bf16[16,2048]{1,0:T(8,128)(2,1)S(1)} %get-tuple-element.86), channel_id=1, source_target_pairs={{0,6},{1,7},{2,4},{3,5},{4,2},{5,3},{6,0},{7,1},{8,14},{9,15},{10,... | collective-permute-start | bytes 196616 | tf_op jit(solution)/shard_map/ppermute | solution.py:27
  105.4 6.6 %collective-permute-start.34 = (bf16[16,2048]{1,0:T(8,128)(2,1)S(1)}, bf16[16,2048]{1,0:T(8,128)(2,1)S(1)}, u32[]{:S(2)}, u32[]{:S(2)}) collective-permute-start(bf16[16,2048]{1,0:T(8,128)(2,1)S(1)} %get-tuple-element.87), channel_id=1, source_target_pairs={{0,4},{1,5},{2,6},{3,7},{4,0},{5,1},{6,2},{7,3},{8,12},{9,13},{10,... | collective-permute-start | bytes 196616 | tf_op jit(solution)/shard_map/ppermute | solution.py:27
  105.5 6.6 %collective-permute-start.35 = (bf16[16,2048]{1,0:T(8,128)(2,1)S(1)}, bf16[16,2048]{1,0:T(8,128)(2,1)S(1)}, u32[]{:S(2)}, u32[]{:S(2)}) collective-permute-start(bf16[16,2048]{1,0:T(8,128)(2,1)S(1)} %get-tuple-element.88), channel_id=1, source_target_pairs={{0,2},{1,3},{2,0},{3,1},{4,6},{5,7},{6,4},{7,5},{8,10},{9,11},{10,... | collective-permute-start | bytes 196616 | tf_op jit(solution)/shard_map/ppermute | solution.py:27
  112.1 4.0 %collective-permute-start.36 = (bf16[8,2048]{1,0:T(8,128)(2,1)S(1)}, bf16[8,2048]{1,0:T(8,128)(2,1)S(1)}, u32[]{:S(2)}, u32[]{:S(2)}) collective-permute-start(bf16[8,2048]{1,0:T(8,128)(2,1)S(1)} %slice.17), channel_id=1, source_target_pairs={{0,1},{1,0},{2,3},{3,2},{4,5},{5,4},{6,7},{7,6},{8,9},{9,8},{10,11... | collective-permute-start | bytes 98312 | tf_op jit(solution)/shard_map/ppermute | solution.py:27

commit v9 on v8

--- a/solution.py
+++ b/solution.py
@@ -327,7 +327,11 @@
 
 
 def widest_first(outer):
-    return range(outer - 1, 0, -1)
+    return list(range(outer - 1, 0, -1))
+
+
+def half_first(outer):
+    return [outer // 2] + [j for j in widest_first(outer) if j != outer // 2]
 
 
 def added(values):
@@ -347,7 +351,7 @@
     tok_dev = state.shape[1]
 
     def spread(value):
-        got = {j: moved(value, 2 * j, 0) for j in widest_first(outer)}
+        got = {j: moved(value, 2 * j, 0) for j in half_first(outer)}
         return [value] + [got[j] for j in range(1, outer)]
 
     weights = [w_gate[:, 0], w_up[:, 0], w_down[:, 0]]

time: 117 us -> 117 us (level)
  no operation moved by 1% of the time
where the time goes in v9:
time: 117 us
  starting transfers between devices  51.8 us (44%)
  waiting for transfers between devices  40.1 us (34%)
  Pallas kernels  23.8 us (20%)
    ppermute x36, starting transfers between devices, moved(): return lax.ppermute(value, BOTH, pairs)  49.9 us
    ppermute x36, waiting for transfers between devices, moved(): return lax.ppermute(value, BOTH, pairs)  40.1 us
    pallas_call x3, Pallas kernels, loaded(): pl.pallas_call(functools.partial(load_kernel, turned=turned, group=group)...  9.77 us
    pallas_call x5, Pallas kernels, run_layer(): pl.pallas_call(functools.partial(layer_kernel, tick_idx=tick_idx, blocks=...  9.36 us
    pallas_call x2, Pallas kernels, filled(): pl.pallas_call(functools.partial(fill_kernel, group=group), out_shape=[pl...  2.43 us
  transfers between devices with their start and end apart: 37, of which 21 were waited for; matrix products, arithmetic and copies ran while one was open for 0% of the time, Pallas kernels for 15%

profile of v9, /device:TPU:0, one launch (start us, length us, event | category | flops | bytes accessed | tf_op | source)
XLA Modules:
  0.0 116.7 jit_solution(7191709309864208838)
XLA Ops:
  1.1 2.5 %collective-permute-start.4 = (bf16[160,2048]{1,0:T(8,128)(2,1)S(1)}, bf16[160,2048]{1,0:T(8,128)(2,1)S(1)}, u32[]{:S(2)}, u32[]{:S(2)}) collective-permute-start(bf16[160,2048]{1,0:T(8,128)(2,1)S(1)} %fill.2), channel_id=1, source_target_pairs={{0,24},{1,25},{2,26},{3,27},{4,28},{5,29},{6,30},{7,31},{8,0},{9,1... | collective-permute-start | bytes 1966088 | tf_op jit(solution)/shard_map/ppermute | solution.py:27
  3.7 1.3 %fill.3 = (bf16[160,2048]{1,0:T(8,128)(2,1)S(1)}, bf16[160,2048]{1,0:T(8,128)(2,1)S(1)}) custom-call(bf16[2,160,2048]{2,1,0:T(8,128)(2,1)} %bitcast.26, bf16[2,160,2048]{2,1,0:T(8,128)(2,1)} %bitcast.28), custom_call_target="tpu_custom_call" | custom-call | tf_op jit(solution)/shard_map/fill/pallas_call | solution.py:247
  6.0 1.5 %collective-permute-start = (bf16[8,2176]{1,0:T(8,128)(2,1)S(1)}, bf16[8,2176]{1,0:T(8,128)(2,1)S(1)}, u32[]{:S(2)}, u32[]{:S(2)}) collective-permute-start(bf16[8,2176]{1,0:T(8,128)(2,1)S(1)} %shard_map.100.first_ref), channel_id=1, source_target_pairs={{0,1},{1,0},{2,3},{3,2},{4,5},{5,4},{6,7},{7,6},{8,9},{9,8},{10,11... | collective-permute-start | bytes 104456 | tf_op jit(solution)/shard_map/ppermute | solution.py:27
  7.5 2.4 %collective-permute-done.second_ref = bf16[8,2176]{1,0:T(8,128)(2,1)S(1)} collective-permute-done((bf16[8,2176]{1,0:T(8,128)(2,1)S(1)}, bf16[8,2176]{1,0:T(8,128)(2,1)S(1)}, u32[]{:S(2)}, u32[]{:S(2)}) %collective-permute-start) | collective-permute-done | bytes 34848 | tf_op jit(solution)/shard_map/ppermute | solution.py:27
  10.0 1.6 %collective-permute-start.1 = (bf16[16,2176]{1,0:T(8,128)(2,1)S(1)}, bf16[16,2176]{1,0:T(8,128)(2,1)S(1)}, u32[]{:S(2)}, u32[]{:S(2)}) collective-permute-start(bf16[16,2176]{1,0:T(8,128)(2,1)S(1)} %shard_map.101.refs_0_.refs_4_), channel_id=1, source_target_pairs={{0,2},{1,3},{2,0},{3,1},{4,6},{5,7},{6,4},{7,5},{8,10},{9,11},{10,... | collective-permute-start | bytes 208904 | tf_op jit(solution)/shard_map/ppermute | solution.py:27
  11.6 2.5 %collective-permute-start.3 = (bf16[16,2176]{1,0:T(8,128)(2,1)S(1)}, bf16[16,2176]{1,0:T(8,128)(2,1)S(1)}, u32[]{:S(2)}, u32[]{:S(2)}) collective-permute-start(bf16[16,2176]{1,0:T(8,128)(2,1)S(1)} %shard_map.101.refs_0_.refs_4_), channel_id=1, source_target_pairs={{0,6},{1,7},{2,4},{3,5},{4,2},{5,3},{6,0},{7,1},{8,14},{9,15},{10,... | collective-permute-start | bytes 208904 | tf_op jit(solution)/shard_map/ppermute | solution.py:27
  14.4 1.5 %stack.1 = bf16[3,160,2048]{2,1,0:T(8,128)(2,1)S(1)} custom-call(bf16[2,160,2048]{2,1,0:T(8,128)(2,1)} %bitcast.31, bf16[2,160,2048]{2,1,0:T(8,128)(2,1)} %bitcast.27, bf16[2,160,2048]{2,1,0:T(8,128)(2,1)} %bitcast.29), custom_call_target="tpu_custom_call" | custom-call | tf_op jit(solution)/shard_map/stack/pallas_call | solution.py:318
  15.9 1.9 %collective-permute-start.15 = (bf16[3,160,2048]{2,1,0:T(8,128)(2,1)S(1)}, bf16[3,160,2048]{2,1,0:T(8,128)(2,1)S(1)}, u32[]{:S(2)}, u32[]{:S(2)}) collective-permute-start(bf16[3,160,2048]{2,1,0:T(8,128)(2,1)S(1)} %stack.1), channel_id=1, source_target_pairs={{0,8},{1,9},{2,10},{3,11},{4,12},{5,13},{6,14},{7,15},{8,0},{9,1},... | collective-permute-start | bytes 5898248 | tf_op jit(solution)/shard_map/ppermute | solution.py:58
  17.8 2.8 %collective-permute-start.2 = (bf16[16,2176]{1,0:T(8,128)(2,1)S(1)}, bf16[16,2176]{1,0:T(8,128)(2,1)S(1)}, u32[]{:S(2)}, u32[]{:S(2)}) collective-permute-start(bf16[16,2176]{1,0:T(8,128)(2,1)S(1)} %shard_map.101.refs_0_.refs_4_), channel_id=1, source_target_pairs={{0,4},{1,5},{2,6},{3,7},{4,0},{5,1},{6,2},{7,3},{8,12},{9,13},{10,... | collective-permute-start | bytes 208904 | tf_op jit(solution)/shard_map/ppermute | solution.py:27
  20.6 4.3 %load.3 = (bf16[2048,640]{1,0:T(8,128)(2,1)S(1)}, bf16[2048,640]{1,0:T(8,128)(2,1)S(1)}, bf16[640,2048]{1,0:T(8,128)(2,1)S(1)}) custom-call(bf16[2,640,2048]{2,1,0:T(8,128)(2,1)} %bitcast.24, bf16[2,640,2048]{2,1,0:T(8,128)(2,1)} %bitcast.20, bf16[2,640,2048]{2,1,0:T(8,128)(2,1)} %bitcast.22), custom_call_target="tpu_custom_call" | custom-call | tf_op jit(solution)/shard_map/load/pallas_call | solution.py:289
  25.0 1.5 %layer.5.refs_9_ = f32[64,2048]{1,0:T(8,128)S(1)} custom-call(bf16[16,2176]{1,0:T(8,128)(2,1)S(1)} %shard_map.101.refs_0_.refs_4_, bf16[16,2176]{1,0:T(8,128)(2,1)S(1)} %collective-permute-done.1.refs_1_.refs_5_, bf16[16,2176]{1,0:T(8,128)(2,1)S(1)} %collective-permute-done.2.refs_2_.refs_6_, bf16[16,2176]{1,0:T(8,128)(2,1)S(1)} %collective-permute-done.3.refs_3_.refs_7_, ...), custom_call_target="tpu_custom_call" | custom-call | flops 503316480 | bytes 7864320 | tf_op jit(solution)/shard_map/layer/pallas_call | solution.py:191
  27.4 3.6 %collective-permute-start.7 = (bf16[16,2048]{1,0:T(8,128)(2,1)S(1)}, bf16[16,2048]{1,0:T(8,128)(2,1)S(1)}, u32[]{:S(2)}, u32[]{:S(2)}) collective-permute-start(bf16[16,2048]{1,0:T(8,128)(2,1)S(1)} %get-tuple-element.59), channel_id=1, source_target_pairs={{0,6},{1,7},{2,4},{3,5},{4,2},{5,3},{6,0},{7,1},{8,14},{9,15},{10,... | collective-permute-start | bytes 196616 | tf_op jit(solution)/shard_map/ppermute | solution.py:27
  31.8 1.9 %collective-permute-done.7.refs_1_ = bf16[16,2048]{1,0:T(8,128)(2,1)S(1)} collective-permute-done((bf16[16,2048]{1,0:T(8,128)(2,1)S(1)}, bf16[16,2048]{1,0:T(8,128)(2,1)S(1)}, u32[]{:S(2)}, u32[]{:S(2)}) %collective-permute-start.7) | collective-permute-done | bytes 65568 | tf_op jit(solution)/shard_map/ppermute | solution.py:27
  33.7 3.8 %collective-permute-done.8.refs_2_ = bf16[16,2048]{1,0:T(8,128)(2,1)S(1)} collective-permute-done((bf16[16,2048]{1,0:T(8,128)(2,1)S(1)}, bf16[16,2048]{1,0:T(8,128)(2,1)S(1)}, u32[]{:S(2)}, u32[]{:S(2)}) %collective-permute-start.8) | collective-permute-done | bytes 65568 | tf_op jit(solution)/shard_map/ppermute | solution.py:27
  37.6 1.5 %collective-permute-start.11 = (bf16[16,2048]{1,0:T(8,128)(2,1)S(1)}, bf16[16,2048]{1,0:T(8,128)(2,1)S(1)}, u32[]{:S(2)}, u32[]{:S(2)}) collective-permute-start(bf16[16,2048]{1,0:T(8,128)(2,1)S(1)} %shard_map.102), channel_id=1, source_target_pairs={{0,9},{1,8},{2,11},{3,10},{4,13},{5,12},{6,15},{7,14},{8,17},{9,16... | collective-permute-start | bytes 196616 | tf_op jit(solution)/shard_map/ppermute | solution.py:27
  40.1 2.9 %collective-permute-done.11.across_ref = bf16[16,2048]{1,0:T(8,128)(2,1)S(1)} collective-permute-done((bf16[16,2048]{1,0:T(8,128)(2,1)S(1)}, bf16[16,2048]{1,0:T(8,128)(2,1)S(1)}, u32[]{:S(2)}, u32[]{:S(2)}) %collective-permute-start.11) | collective-permute-done | bytes 65568 | tf_op jit(solution)/shard_map/ppermute | solution.py:27
  44.1 1.9 %collective-permute-start.14 = (bf16[16,2048]{1,0:T(8,128)(2,1)S(1)}, bf16[16,2048]{1,0:T(8,128)(2,1)S(1)}, u32[]{:S(2)}, u32[]{:S(2)}) collective-permute-start(bf16[16,2048]{1,0:T(8,128)(2,1)S(1)} %get-tuple-element.62.refs_0_), channel_id=1, source_target_pairs={{0,6},{1,7},{2,4},{3,5},{4,2},{5,3},{6,0},{7,1},{8,14},{9,15},{10,... | collective-permute-start | bytes 196616 | tf_op jit(solution)/shard_map/ppermute | solution.py:27
  46.0 2.5 %collective-permute-start.12 = (bf16[16,2048]{1,0:T(8,128)(2,1)S(1)}, bf16[16,2048]{1,0:T(8,128)(2,1)S(1)}, u32[]{:S(2)}, u32[]{:S(2)}) collective-permute-start(bf16[16,2048]{1,0:T(8,128)(2,1)S(1)} %get-tuple-element.62.refs_0_), channel_id=1, source_target_pairs={{0,2},{1,3},{2,0},{3,1},{4,6},{5,7},{6,4},{7,5},{8,10},{9,11},{10,... | collective-permute-start | bytes 196616 | tf_op jit(solution)/shard_map/ppermute | solution.py:27
  48.5 2.5 %load.4.refs_15_ = bf16[2048,640]{1,0:T(8,128)(2,1)S(1)} custom-call(bf16[2,640,2048]{2,1,0:T(8,128)(2,1)} %bitcast.25), custom_call_target="tpu_custom_call" | custom-call | tf_op jit(solution)/shard_map/load/pallas_call | solution.py:289
  51.1 2.9 %load.5 = (bf16[2048,640]{1,0:T(8,128)(2,1)S(1)}, bf16[640,2048]{1,0:T(8,128)(2,1)S(1)}) custom-call(bf16[2,640,2048]{2,1,0:T(8,128)(2,1)} %bitcast.21, bf16[2,640,2048]{2,1,0:T(8,128)(2,1)} %bitcast.23), custom_call_target="tpu_custom_call" | custom-call | tf_op jit(solution)/shard_map/load/pallas_call | solution.py:289
  54.0 2.3 %layer.7 = (f32[16,2048]{1,0:T(8,128)S(1)}, bf16[16,2048]{1,0:T(8,128)(2,1)S(1)}, bf16[16,2048]{1,0:T(8,128)(2,1)S(1)}, bf16[16,2048]{1,0:T(8,128)(2,1)S(1)}) custom-call(bf16[16,2048]{1,0:T(8,128)(2,1)S(1)} %get-tuple-element.62.refs_0_, bf16[16,2048]{1,0:T(8,128)(2,1)S(1)} %collective-permute-done.12.refs_1_, ...), custom_call_target="tpu_custom_call" | custom-call | flops 629145600 | bytes 9830400 | tf_op jit(solution)/shard_map/layer/pallas_call | solution.py:191
  56.3 1.9 %collective-permute-start.16 = (bf16[16,2048]{1,0:T(8,128)(2,1)S(1)}, bf16[16,2048]{1,0:T(8,128)(2,1)S(1)}, u32[]{:S(2)}, u32[]{:S(2)}) collective-permute-start(bf16[16,2048]{1,0:T(8,128)(2,1)S(1)} %get-tuple-element.73), channel_id=1, source_target_pairs={{0,6},{1,7},{2,4},{3,5},{4,2},{5,3},{6,0},{7,1},{8,14},{9,15},{10,... | collective-permute-start | bytes 196616 | tf_op jit(solution)/shard_map/ppermute | solution.py:27
  58.3 2.5 %collective-permute-start.18 = (bf16[16,2048]{1,0:T(8,128)(2,1)S(1)}, bf16[16,2048]{1,0:T(8,128)(2,1)S(1)}, u32[]{:S(2)}, u32[]{:S(2)}) collective-permute-start(bf16[16,2048]{1,0:T(8,128)(2,1)S(1)} %get-tuple-element.75), channel_id=1, source_target_pairs={{0,2},{1,3},{2,0},{3,1},{4,6},{5,7},{6,4},{7,5},{8,10},{9,11},{10,... | collective-permute-start | bytes 196616 | tf_op jit(solution)/shard_map/ppermute | solution.py:27
  60.8 1.7 %collective-permute-done.16.refs_1_ = bf16[16,2048]{1,0:T(8,128)(2,1)S(1)} collective-permute-done((bf16[16,2048]{1,0:T(8,128)(2,1)S(1)}, bf16[16,2048]{1,0:T(8,128)(2,1)S(1)}, u32[]{:S(2)}, u32[]{:S(2)}) %collective-permute-start.16) | collective-permute-done | bytes 65568 | tf_op jit(solution)/shard_map/ppermute | solution.py:27
  62.5 1.4 %collective-permute-done.17.refs_2_ = bf16[16,2048]{1,0:T(8,128)(2,1)S(1)} collective-permute-done((bf16[16,2048]{1,0:T(8,128)(2,1)S(1)}, bf16[16,2048]{1,0:T(8,128)(2,1)S(1)}, u32[]{:S(2)}, u32[]{:S(2)}) %collective-permute-start.17) | collective-permute-done | bytes 65568 | tf_op jit(solution)/shard_map/ppermute | solution.py:27
  64.1 1.2 %collective-permute-start.19 = (bf16[16,2048]{1,0:T(8,128)(2,1)S(1)}, bf16[16,2048]{1,0:T(8,128)(2,1)S(1)}, u32[]{:S(2)}, u32[]{:S(2)}) collective-permute-start(bf16[16,2048]{1,0:T(8,128)(2,1)S(1)} %shard_map.104), channel_id=1, source_target_pairs={{0,8},{1,9},{2,10},{3,11},{4,12},{5,13},{6,14},{7,15},{8,16},{9,17... | collective-permute-start | bytes 196616 | tf_op jit(solution)/shard_map/ppermute | solution.py:27
  65.3 3.4 %collective-permute-done.20.across_ref = bf16[16,2048]{1,0:T(8,128)(2,1)S(1)} collective-permute-done((bf16[16,2048]{1,0:T(8,128)(2,1)S(1)}, bf16[16,2048]{1,0:T(8,128)(2,1)S(1)}, u32[]{:S(2)}, u32[]{:S(2)}) %collective-permute-start.20) | collective-permute-done | bytes 65568 | tf_op jit(solution)/shard_map/ppermute | solution.py:27
  69.0 1.8 %collective-permute-start.23 = (bf16[16,2048]{1,0:T(8,128)(2,1)S(1)}, bf16[16,2048]{1,0:T(8,128)(2,1)S(1)}, u32[]{:S(2)}, u32[]{:S(2)}) collective-permute-start(bf16[16,2048]{1,0:T(8,128)(2,1)S(1)} %get-tuple-element.76.refs_0_), channel_id=1, source_target_pairs={{0,6},{1,7},{2,4},{3,5},{4,2},{5,3},{6,0},{7,1},{8,14},{9,15},{10,... | collective-permute-start | bytes 196616 | tf_op jit(solution)/shard_map/ppermute | solution.py:27
  71.5 2.0 %collective-permute-start.21 = (bf16[16,2048]{1,0:T(8,128)(2,1)S(1)}, bf16[16,2048]{1,0:T(8,128)(2,1)S(1)}, u32[]{:S(2)}, u32[]{:S(2)}) collective-permute-start(bf16[16,2048]{1,0:T(8,128)(2,1)S(1)} %get-tuple-element.76.refs_0_), channel_id=1, source_target_pairs={{0,2},{1,3},{2,0},{3,1},{4,6},{5,7},{6,4},{7,5},{8,10},{9,11},{10,... | collective-permute-start | bytes 196616 | tf_op jit(solution)/shard_map/ppermute | solution.py:27
  73.5 1.8 %collective-permute-done.23.refs_3_ = bf16[16,2048]{1,0:T(8,128)(2,1)S(1)} collective-permute-done((bf16[16,2048]{1,0:T(8,128)(2,1)S(1)}, bf16[16,2048]{1,0:T(8,128)(2,1)S(1)}, u32[]{:S(2)}, u32[]{:S(2)}) %collective-permute-start.23) | collective-permute-done | bytes 65568 | tf_op jit(solution)/shard_map/ppermute | solution.py:27
  75.2 1.4 %collective-permute-done.22.refs_2_ = bf16[16,2048]{1,0:T(8,128)(2,1)S(1)} collective-permute-done((bf16[16,2048]{1,0:T(8,128)(2,1)S(1)}, bf16[16,2048]{1,0:T(8,128)(2,1)S(1)}, u32[]{:S(2)}, u32[]{:S(2)}) %collective-permute-start.22) | collective-permute-done | bytes 65568 | tf_op jit(solution)/shard_map/ppermute | solution.py:27
  76.6 2.4 %layer.8 = (f32[16,2048]{1,0:T(8,128)S(1)}, bf16[16,2048]{1,0:T(8,128)(2,1)S(1)}, bf16[16,2048]{1,0:T(8,128)(2,1)S(1)}, bf16[16,2048]{1,0:T(8,128)(2,1)S(1)}) custom-call(bf16[16,2048]{1,0:T(8,128)(2,1)S(1)} %get-tuple-element.76.refs_0_, bf16[16,2048]{1,0:T(8,128)(2,1)S(1)} %collective-permute-done.21.refs_1_, ...), custom_call_target="tpu_custom_call" | custom-call | flops 629145600 | bytes 9830400 | tf_op jit(solution)/shard_map/layer/pallas_call | solution.py:191
  79.1 1.8 %collective-permute-start.25 = (bf16[16,2048]{1,0:T(8,128)(2,1)S(1)}, bf16[16,2048]{1,0:T(8,128)(2,1)S(1)}, u32[]{:S(2)}, u32[]{:S(2)}) collective-permute-start(bf16[16,2048]{1,0:T(8,128)(2,1)S(1)} %get-tuple-element.80), channel_id=1, source_target_pairs={{0,6},{1,7},{2,4},{3,5},{4,2},{5,3},{6,0},{7,1},{8,14},{9,15},{10,... | collective-permute-start | bytes 196616 | tf_op jit(solution)/shard_map/ppermute | solution.py:27
  81.7 1.8 %collective-permute-start.27 = (bf16[16,2048]{1,0:T(8,128)(2,1)S(1)}, bf16[16,2048]{1,0:T(8,128)(2,1)S(1)}, u32[]{:S(2)}, u32[]{:S(2)}) collective-permute-start(bf16[16,2048]{1,0:T(8,128)(2,1)S(1)} %get-tuple-element.82), channel_id=1, source_target_pairs={{0,2},{1,3},{2,0},{3,1},{4,6},{5,7},{6,4},{7,5},{8,10},{9,11},{10,... | collective-permute-start | bytes 196616 | tf_op jit(solution)/shard_map/ppermute | solution.py:27
  83.5 1.7 %collective-permute-done.25.refs_1_ = bf16[16,2048]{1,0:T(8,128)(2,1)S(1)} collective-permute-done((bf16[16,2048]{1,0:T(8,128)(2,1)S(1)}, bf16[16,2048]{1,0:T(8,128)(2,1)S(1)}, u32[]{:S(2)}, u32[]{:S(2)}) %collective-permute-start.25) | collective-permute-done | bytes 65568 | tf_op jit(solution)/shard_map/ppermute | solution.py:27
  85.2 1.5 %collective-permute-done.26.refs_2_ = bf16[16,2048]{1,0:T(8,128)(2,1)S(1)} collective-permute-done((bf16[16,2048]{1,0:T(8,128)(2,1)S(1)}, bf16[16,2048]{1,0:T(8,128)(2,1)S(1)}, u32[]{:S(2)}, u32[]{:S(2)}) %collective-permute-start.26) | collective-permute-done | bytes 65568 | tf_op jit(solution)/shard_map/ppermute | solution.py:27
  86.7 1.6 %collective-permute-start.29 = (bf16[16,2048]{1,0:T(8,128)(2,1)S(1)}, bf16[16,2048]{1,0:T(8,128)(2,1)S(1)}, u32[]{:S(2)}, u32[]{:S(2)}) collective-permute-start(bf16[16,2048]{1,0:T(8,128)(2,1)S(1)} %shard_map.106), channel_id=1, source_target_pairs={{0,9},{1,8},{2,11},{3,10},{4,13},{5,12},{6,15},{7,14},{8,17},{9,16... | collective-permute-start | bytes 196616 | tf_op jit(solution)/shard_map/ppermute | solution.py:27
  88.9 2.8 %collective-permute-done.29.across_ref = bf16[16,2048]{1,0:T(8,128)(2,1)S(1)} collective-permute-done((bf16[16,2048]{1,0:T(8,128)(2,1)S(1)}, bf16[16,2048]{1,0:T(8,128)(2,1)S(1)}, u32[]{:S(2)}, u32[]{:S(2)}) %collective-permute-start.29) | collective-permute-done | bytes 65568 | tf_op jit(solution)/shard_map/ppermute | solution.py:27
  92.5 1.8 %collective-permute-start.32 = (bf16[16,2048]{1,0:T(8,128)(2,1)S(1)}, bf16[16,2048]{1,0:T(8,128)(2,1)S(1)}, u32[]{:S(2)}, u32[]{:S(2)}) collective-permute-start(bf16[16,2048]{1,0:T(8,128)(2,1)S(1)} %get-tuple-element.83.refs_0_), channel_id=1, source_target_pairs={{0,6},{1,7},{2,4},{3,5},{4,2},{5,3},{6,0},{7,1},{8,14},{9,15},{10,... | collective-permute-start | bytes 196616 | tf_op jit(solution)/shard_map/ppermute | solution.py:27
  94.8 2.1 %collective-permute-start.30 = (bf16[16,2048]{1,0:T(8,128)(2,1)S(1)}, bf16[16,2048]{1,0:T(8,128)(2,1)S(1)}, u32[]{:S(2)}, u32[]{:S(2)}) collective-permute-start(bf16[16,2048]{1,0:T(8,128)(2,1)S(1)} %get-tuple-element.83.refs_0_), channel_id=1, source_target_pairs={{0,2},{1,3},{2,0},{3,1},{4,6},{5,7},{6,4},{7,5},{8,10},{9,11},{10,... | collective-permute-start | bytes 196616 | tf_op jit(solution)/shard_map/ppermute | solution.py:27
  97.0 1.9 %collective-permute-done.32.refs_3_ = bf16[16,2048]{1,0:T(8,128)(2,1)S(1)} collective-permute-done((bf16[16,2048]{1,0:T(8,128)(2,1)S(1)}, bf16[16,2048]{1,0:T(8,128)(2,1)S(1)}, u32[]{:S(2)}, u32[]{:S(2)}) %collective-permute-start.32) | collective-permute-done | bytes 65568 | tf_op jit(solution)/shard_map/ppermute | solution.py:27
  98.9 2.4 %collective-permute-done.31.refs_2_ = bf16[16,2048]{1,0:T(8,128)(2,1)S(1)} collective-permute-done((bf16[16,2048]{1,0:T(8,128)(2,1)S(1)}, bf16[16,2048]{1,0:T(8,128)(2,1)S(1)}, u32[]{:S(2)}, u32[]{:S(2)}) %collective-permute-start.31) | collective-permute-done | bytes 65568 | tf_op jit(solution)/shard_map/ppermute | solution.py:27
  101.3 2.3 %layer.9 = (f32[16,2048]{1,0:T(8,128)S(1)}, bf16[16,2048]{1,0:T(8,128)(2,1)S(1)}, bf16[16,2048]{1,0:T(8,128)(2,1)S(1)}, bf16[16,2048]{1,0:T(8,128)(2,1)S(1)}) custom-call(bf16[16,2048]{1,0:T(8,128)(2,1)S(1)} %get-tuple-element.83.refs_0_, bf16[16,2048]{1,0:T(8,128)(2,1)S(1)} %collective-permute-done.30.refs_1_, ...), custom_call_target="tpu_custom_call" | custom-call | flops 629145600 | bytes 9830400 | tf_op jit(solution)/shard_map/layer/pallas_call | solution.py:191
  103.6 1.9 %collective-permute-start.33 = (bf16[16,2048]{1,0:T(8,128)(2,1)S(1)}, bf16[16,2048]{1,0:T(8,128)(2,1)S(1)}, u32[]{:S(2)}, u32[]{:S(2)}) collective-permute-start(bf16[16,2048]{1,0:T(8,128)(2,1)S(1)} %get-tuple-element.86), channel_id=1, source_target_pairs={{0,6},{1,7},{2,4},{3,5},{4,2},{5,3},{6,0},{7,1},{8,14},{9,15},{10,... | collective-permute-start | bytes 196616 | tf_op jit(solution)/shard_map/ppermute | solution.py:27
  105.5 2.6 %collective-permute-start.35 = (bf16[16,2048]{1,0:T(8,128)(2,1)S(1)}, bf16[16,2048]{1,0:T(8,128)(2,1)S(1)}, u32[]{:S(2)}, u32[]{:S(2)}) collective-permute-start(bf16[16,2048]{1,0:T(8,128)(2,1)S(1)} %get-tuple-element.88), channel_id=1, source_target_pairs={{0,2},{1,3},{2,0},{3,1},{4,6},{5,7},{6,4},{7,5},{8,10},{9,11},{10,... | collective-permute-start | bytes 196616 | tf_op jit(solution)/shard_map/ppermute | solution.py:27
  108.0 2.0 %collective-permute-done.33 = bf16[16,2048]{1,0:T(8,128)(2,1)S(1)} collective-permute-done((bf16[16,2048]{1,0:T(8,128)(2,1)S(1)}, bf16[16,2048]{1,0:T(8,128)(2,1)S(1)}, u32[]{:S(2)}, u32[]{:S(2)}) %collective-permute-start.33) | collective-permute-done | bytes 65568 | tf_op jit(solution)/shard_map/ppermute | solution.py:27
  110.0 2.0 %collective-permute-done.34 = bf16[16,2048]{1,0:T(8,128)(2,1)S(1)} collective-permute-done((bf16[16,2048]{1,0:T(8,128)(2,1)S(1)}, bf16[16,2048]{1,0:T(8,128)(2,1)S(1)}, u32[]{:S(2)}, u32[]{:S(2)}) %collective-permute-start.34) | collective-permute-done | bytes 65568 | tf_op jit(solution)/shard_map/ppermute | solution.py:27
  113.0 3.0 %collective-permute-done.36 = bf16[8,2048]{1,0:T(8,128)(2,1)S(1)} collective-permute-done((bf16[8,2048]{1,0:T(8,128)(2,1)S(1)}, bf16[8,2048]{1,0:T(8,128)(2,1)S(1)}, u32[]{:S(2)}, u32[]{:S(2)}) %collective-permute-start.36) | collective-permute-done | bytes 32800 | tf_op jit(solution)/shard_map/ppermute | solution.py:27
  (56 shorter events, 11.9 us)
Async XLA Ops:
  0.0 5.8 %copy-start.3 = (f32[4,1,8,2]{2,3,1,0:T(2,128)S(1)}, f32[4,1,8,2]{2,3,1,0:T(2,128)}, u32[]{:S(2)}) copy-start(f32[4,1,8,2]{2,3,1,0:T(2,128)} %param.12) | copy-start | bytes 772
  0.0 5.8 %copy-start.2 = (s32[4,1,8,2]{2,3,1,0:T(2,128)S(1)}, s32[4,1,8,2]{2,3,1,0:T(2,128)}, u32[]{:S(2)}) copy-start(s32[4,1,8,2]{2,3,1,0:T(2,128)} %param.11) | copy-start | bytes 772
  0.0 5.8 %copy-start = (bf16[1,8,2048]{2,1,0:T(8,128)(2,1)S(1)}, bf16[1,8,2048]{2,1,0:T(8,128)(2,1)}, u32[]{:S(2)}) copy-start(bf16[1,8,2048]{2,1,0:T(8,128)(2,1)} %param.10) | copy-start | bytes 98308
  0.0 5.8 %copy-start.1 = (f32[2,1,2048]{2,1,0:T(1,128)S(1)}, f32[2,1,2048]{2,1,0:T(1,128)}, u32[]{:S(2)}) copy-start(f32[2,1,2048]{2,1,0:T(1,128)} %gain_ref.7) | copy-start | bytes 49156
  1.1 25.4 %collective-permute-start.4 = (bf16[160,2048]{1,0:T(8,128)(2,1)S(1)}, bf16[160,2048]{1,0:T(8,128)(2,1)S(1)}, u32[]{:S(2)}, u32[]{:S(2)}) collective-permute-start(bf16[160,2048]{1,0:T(8,128)(2,1)S(1)} %fill.2), channel_id=1, source_target_pairs={{0,24},{1,25},{2,26},{3,27},{4,28},{5,29},{6,30},{7,31},{8,0},{9,1... | collective-permute-start | bytes 1966088 | tf_op jit(solution)/shard_map/ppermute | solution.py:27
  5.0 21.6 %collective-permute-start.5 = (bf16[160,2048]{1,0:T(8,128)(2,1)S(1)}, bf16[160,2048]{1,0:T(8,128)(2,1)S(1)}, u32[]{:S(2)}, u32[]{:S(2)}) collective-permute-start(bf16[160,2048]{1,0:T(8,128)(2,1)S(1)} %get-tuple-element.56), channel_id=1, source_target_pairs={{0,24},{1,25},{2,26},{3,27},{4,28},{5,29},{6,30},{7,31},{8,0},{9,1... | collective-permute-start | bytes 1966088 | tf_op jit(solution)/shard_map/ppermute | solution.py:27
  5.7 20.9 %collective-permute-start.6 = (bf16[160,2048]{1,0:T(8,128)(2,1)S(1)}, bf16[160,2048]{1,0:T(8,128)(2,1)S(1)}, u32[]{:S(2)}, u32[]{:S(2)}) collective-permute-start(bf16[160,2048]{1,0:T(8,128)(2,1)S(1)} %get-tuple-element.57), channel_id=1, source_target_pairs={{0,24},{1,25},{2,26},{3,27},{4,28},{5,29},{6,30},{7,31},{8,0},{9,1... | collective-permute-start | bytes 1966088 | tf_op jit(solution)/shard_map/ppermute | solution.py:27
  6.0 4.0 %collective-permute-start = (bf16[8,2176]{1,0:T(8,128)(2,1)S(1)}, bf16[8,2176]{1,0:T(8,128)(2,1)S(1)}, u32[]{:S(2)}, u32[]{:S(2)}) collective-permute-start(bf16[8,2176]{1,0:T(8,128)(2,1)S(1)} %shard_map.100.first_ref), channel_id=1, source_target_pairs={{0,1},{1,0},{2,3},{3,2},{4,5},{5,4},{6,7},{7,6},{8,9},{9,8},{10,11... | collective-permute-start | bytes 104456 | tf_op jit(solution)/shard_map/ppermute | solution.py:27
  10.0 4.4 %collective-permute-start.1 = (bf16[16,2176]{1,0:T(8,128)(2,1)S(1)}, bf16[16,2176]{1,0:T(8,128)(2,1)S(1)}, u32[]{:S(2)}, u32[]{:S(2)}) collective-permute-start(bf16[16,2176]{1,0:T(8,128)(2,1)S(1)} %shard_map.101.refs_0_.refs_4_), channel_id=1, source_target_pairs={{0,2},{1,3},{2,0},{3,1},{4,6},{5,7},{6,4},{7,5},{8,10},{9,11},{10,... | collective-permute-start | bytes 208904 | tf_op jit(solution)/shard_map/ppermute | solution.py:27
  11.6 6.2 %collective-permute-start.3 = (bf16[16,2176]{1,0:T(8,128)(2,1)S(1)}, bf16[16,2176]{1,0:T(8,128)(2,1)S(1)}, u32[]{:S(2)}, u32[]{:S(2)}) collective-permute-start(bf16[16,2176]{1,0:T(8,128)(2,1)S(1)} %shard_map.101.refs_0_.refs_4_), channel_id=1, source_target_pairs={{0,6},{1,7},{2,4},{3,5},{4,2},{5,3},{6,0},{7,1},{8,14},{9,15},{10,... | collective-permute-start | bytes 208904 | tf_op jit(solution)/shard_map/ppermute | solution.py:27
  15.9 38.1 %collective-permute-start.15 = (bf16[3,160,2048]{2,1,0:T(8,128)(2,1)S(1)}, bf16[3,160,2048]{2,1,0:T(8,128)(2,1)S(1)}, u32[]{:S(2)}, u32[]{:S(2)}) collective-permute-start(bf16[3,160,2048]{2,1,0:T(8,128)(2,1)S(1)} %stack.1), channel_id=1, source_target_pairs={{0,8},{1,9},{2,10},{3,11},{4,12},{5,13},{6,14},{7,15},{8,0},{9,1},... | collective-permute-start | bytes 5898248 | tf_op jit(solution)/shard_map/ppermute | solution.py:58
  17.8 7.2 %collective-permute-start.2 = (bf16[16,2176]{1,0:T(8,128)(2,1)S(1)}, bf16[16,2176]{1,0:T(8,128)(2,1)S(1)}, u32[]{:S(2)}, u32[]{:S(2)}) collective-permute-start(bf16[16,2176]{1,0:T(8,128)(2,1)S(1)} %shard_map.101.refs_0_.refs_4_), channel_id=1, source_target_pairs={{0,4},{1,5},{2,6},{3,7},{4,0},{5,1},{6,2},{7,3},{8,12},{9,13},{10,... | collective-permute-start | bytes 208904 | tf_op jit(solution)/shard_map/ppermute | solution.py:27
  27.4 6.4 %collective-permute-start.7 = (bf16[16,2048]{1,0:T(8,128)(2,1)S(1)}, bf16[16,2048]{1,0:T(8,128)(2,1)S(1)}, u32[]{:S(2)}, u32[]{:S(2)}) collective-permute-start(bf16[16,2048]{1,0:T(8,128)(2,1)S(1)} %get-tuple-element.59), channel_id=1, source_target_pairs={{0,6},{1,7},{2,4},{3,5},{4,2},{5,3},{6,0},{7,1},{8,14},{9,15},{10,... | collective-permute-start | bytes 196616 | tf_op jit(solution)/shard_map/ppermute | solution.py:27
  30.9 6.5 %collective-permute-start.8 = (bf16[16,2048]{1,0:T(8,128)(2,1)S(1)}, bf16[16,2048]{1,0:T(8,128)(2,1)S(1)}, u32[]{:S(2)}, u32[]{:S(2)}) collective-permute-start(bf16[16,2048]{1,0:T(8,128)(2,1)S(1)} %get-tuple-element.60), channel_id=1, source_target_pairs={{0,4},{1,5},{2,6},{3,7},{4,0},{5,1},{6,2},{7,3},{8,12},{9,13},{10,... | collective-permute-start | bytes 196616 | tf_op jit(solution)/shard_map/ppermute | solution.py:27
  31.1 6.4 %collective-permute-start.9 = (bf16[16,2048]{1,0:T(8,128)(2,1)S(1)}, bf16[16,2048]{1,0:T(8,128)(2,1)S(1)}, u32[]{:S(2)}, u32[]{:S(2)}) collective-permute-start(bf16[16,2048]{1,0:T(8,128)(2,1)S(1)} %get-tuple-element.61), channel_id=1, source_target_pairs={{0,2},{1,3},{2,0},{3,1},{4,6},{5,7},{6,4},{7,5},{8,10},{9,11},{10,... | collective-permute-start | bytes 196616 | tf_op jit(solution)/shard_map/ppermute | solution.py:27
  37.5 39.1 %collective-permute-start.24 = (bf16[3,160,2048]{2,1,0:T(8,128)(2,1)S(1)}, bf16[3,160,2048]{2,1,0:T(8,128)(2,1)S(1)}, u32[]{:S(2)}, u32[]{:S(2)}) collective-permute-start(bf16[3,160,2048]{2,1,0:T(8,128)(2,1)S(1)} %stack.1), channel_id=1, source_target_pairs={{0,24},{1,25},{2,26},{3,27},{4,28},{5,29},{6,30},{7,31},{8,0},{9,1... | collective-permute-start | bytes 5898248 | tf_op jit(solution)/shard_map/ppermute | solution.py:27
  37.6 5.4 %collective-permute-start.11 = (bf16[16,2048]{1,0:T(8,128)(2,1)S(1)}, bf16[16,2048]{1,0:T(8,128)(2,1)S(1)}, u32[]{:S(2)}, u32[]{:S(2)}) collective-permute-start(bf16[16,2048]{1,0:T(8,128)(2,1)S(1)} %shard_map.102), channel_id=1, source_target_pairs={{0,9},{1,8},{2,11},{3,10},{4,13},{5,12},{6,15},{7,14},{8,17},{9,16... | collective-permute-start | bytes 196616 | tf_op jit(solution)/shard_map/ppermute | solution.py:27
  39.2 4.8 %collective-permute-start.10 = (bf16[16,2048]{1,0:T(8,128)(2,1)S(1)}, bf16[16,2048]{1,0:T(8,128)(2,1)S(1)}, u32[]{:S(2)}, u32[]{:S(2)}) collective-permute-start(bf16[16,2048]{1,0:T(8,128)(2,1)S(1)} %shard_map.102), channel_id=1, source_target_pairs={{0,8},{1,9},{2,10},{3,11},{4,12},{5,13},{6,14},{7,15},{8,16},{9,17... | collective-permute-start | bytes 196616 | tf_op jit(solution)/shard_map/ppermute | solution.py:27
  44.1 9.9 %collective-permute-start.14 = (bf16[16,2048]{1,0:T(8,128)(2,1)S(1)}, bf16[16,2048]{1,0:T(8,128)(2,1)S(1)}, u32[]{:S(2)}, u32[]{:S(2)}) collective-permute-start(bf16[16,2048]{1,0:T(8,128)(2,1)S(1)} %get-tuple-element.62.refs_0_), channel_id=1, source_target_pairs={{0,6},{1,7},{2,4},{3,5},{4,2},{5,3},{6,0},{7,1},{8,14},{9,15},{10,... | collective-permute-start | bytes 196616 | tf_op jit(solution)/shard_map/ppermute | solution.py:27
  46.0 8.0 %collective-permute-start.13 = (bf16[16,2048]{1,0:T(8,128)(2,1)S(1)}, bf16[16,2048]{1,0:T(8,128)(2,1)S(1)}, u32[]{:S(2)}, u32[]{:S(2)}) collective-permute-start(bf16[16,2048]{1,0:T(8,128)(2,1)S(1)} %get-tuple-element.62.refs_0_), channel_id=1, source_target_pairs={{0,4},{1,5},{2,6},{3,7},{4,0},{5,1},{6,2},{7,3},{8,12},{9,13},{10,... | collective-permute-start | bytes 196616 | tf_op jit(solution)/shard_map/ppermute | solution.py:27
  46.0 8.0 %collective-permute-start.12 = (bf16[16,2048]{1,0:T(8,128)(2,1)S(1)}, bf16[16,2048]{1,0:T(8,128)(2,1)S(1)}, u32[]{:S(2)}, u32[]{:S(2)}) collective-permute-start(bf16[16,2048]{1,0:T(8,128)(2,1)S(1)} %get-tuple-element.62.refs_0_), channel_id=1, source_target_pairs={{0,2},{1,3},{2,0},{3,1},{4,6},{5,7},{6,4},{7,5},{8,10},{9,11},{10,... | collective-permute-start | bytes 196616 | tf_op jit(solution)/shard_map/ppermute | solution.py:27
  56.3 6.1 %collective-permute-start.16 = (bf16[16,2048]{1,0:T(8,128)(2,1)S(1)}, bf16[16,2048]{1,0:T(8,128)(2,1)S(1)}, u32[]{:S(2)}, u32[]{:S(2)}) collective-permute-start(bf16[16,2048]{1,0:T(8,128)(2,1)S(1)} %get-tuple-element.73), channel_id=1, source_target_pairs={{0,6},{1,7},{2,4},{3,5},{4,2},{5,3},{6,0},{7,1},{8,14},{9,15},{10,... | collective-permute-start | bytes 196616 | tf_op jit(solution)/shard_map/ppermute | solution.py:27
  58.3 5.6 %collective-permute-start.17 = (bf16[16,2048]{1,0:T(8,128)(2,1)S(1)}, bf16[16,2048]{1,0:T(8,128)(2,1)S(1)}, u32[]{:S(2)}, u32[]{:S(2)}) collective-permute-start(bf16[16,2048]{1,0:T(8,128)(2,1)S(1)} %get-tuple-element.74), channel_id=1, source_target_pairs={{0,4},{1,5},{2,6},{3,7},{4,0},{5,1},{6,2},{7,3},{8,12},{9,13},{10,... | collective-permute-start | bytes 196616 | tf_op jit(solution)/shard_map/ppermute | solution.py:27
  58.3 5.6 %collective-permute-start.18 = (bf16[16,2048]{1,0:T(8,128)(2,1)S(1)}, bf16[16,2048]{1,0:T(8,128)(2,1)S(1)}, u32[]{:S(2)}, u32[]{:S(2)}) collective-permute-start(bf16[16,2048]{1,0:T(8,128)(2,1)S(1)} %get-tuple-element.75), channel_id=1, source_target_pairs={{0,2},{1,3},{2,0},{3,1},{4,6},{5,7},{6,4},{7,5},{8,10},{9,11},{10,... | collective-permute-start | bytes 196616 | tf_op jit(solution)/shard_map/ppermute | solution.py:27
  63.9 4.7 %collective-permute-start.20 = (bf16[16,2048]{1,0:T(8,128)(2,1)S(1)}, bf16[16,2048]{1,0:T(8,128)(2,1)S(1)}, u32[]{:S(2)}, u32[]{:S(2)}) collective-permute-start(bf16[16,2048]{1,0:T(8,128)(2,1)S(1)} %shard_map.104), channel_id=1, source_target_pairs={{0,9},{1,8},{2,11},{3,10},{4,13},{5,12},{6,15},{7,14},{8,17},{9,16... | collective-permute-start | bytes 196616 | tf_op jit(solution)/shard_map/ppermute | solution.py:27
  64.1 4.8 %collective-permute-start.19 = (bf16[16,2048]{1,0:T(8,128)(2,1)S(1)}, bf16[16,2048]{1,0:T(8,128)(2,1)S(1)}, u32[]{:S(2)}, u32[]{:S(2)}) collective-permute-start(bf16[16,2048]{1,0:T(8,128)(2,1)S(1)} %shard_map.104), channel_id=1, source_target_pairs={{0,8},{1,9},{2,10},{3,11},{4,12},{5,13},{6,14},{7,15},{8,16},{9,17... | collective-permute-start | bytes 196616 | tf_op jit(solution)/shard_map/ppermute | solution.py:27
  69.0 6.2 %collective-permute-start.23 = (bf16[16,2048]{1,0:T(8,128)(2,1)S(1)}, bf16[16,2048]{1,0:T(8,128)(2,1)S(1)}, u32[]{:S(2)}, u32[]{:S(2)}) collective-permute-start(bf16[16,2048]{1,0:T(8,128)(2,1)S(1)} %get-tuple-element.76.refs_0_), channel_id=1, source_target_pairs={{0,6},{1,7},{2,4},{3,5},{4,2},{5,3},{6,0},{7,1},{8,14},{9,15},{10,... | collective-permute-start | bytes 196616 | tf_op jit(solution)/shard_map/ppermute | solution.py:27
  70.8 5.8 %collective-permute-start.22 = (bf16[16,2048]{1,0:T(8,128)(2,1)S(1)}, bf16[16,2048]{1,0:T(8,128)(2,1)S(1)}, u32[]{:S(2)}, u32[]{:S(2)}) collective-permute-start(bf16[16,2048]{1,0:T(8,128)(2,1)S(1)} %get-tuple-element.76.refs_0_), channel_id=1, source_target_pairs={{0,4},{1,5},{2,6},{3,7},{4,0},{5,1},{6,2},{7,3},{8,12},{9,13},{10,... | collective-permute-start | bytes 196616 | tf_op jit(solution)/shard_map/ppermute | solution.py:27
  71.5 5.1 %collective-permute-start.21 = (bf16[16,2048]{1,0:T(8,128)(2,1)S(1)}, bf16[16,2048]{1,0:T(8,128)(2,1)S(1)}, u32[]{:S(2)}, u32[]{:S(2)}) collective-permute-start(bf16[16,2048]{1,0:T(8,128)(2,1)S(1)} %get-tuple-element.76.refs_0_), channel_id=1, source_target_pairs={{0,2},{1,3},{2,0},{3,1},{4,6},{5,7},{6,4},{7,5},{8,10},{9,11},{10,... | collective-permute-start | bytes 196616 | tf_op jit(solution)/shard_map/ppermute | solution.py:27
  79.1 6.1 %collective-permute-start.25 = (bf16[16,2048]{1,0:T(8,128)(2,1)S(1)}, bf16[16,2048]{1,0:T(8,128)(2,1)S(1)}, u32[]{:S(2)}, u32[]{:S(2)}) collective-permute-start(bf16[16,2048]{1,0:T(8,128)(2,1)S(1)} %get-tuple-element.80), channel_id=1, source_target_pairs={{0,6},{1,7},{2,4},{3,5},{4,2},{5,3},{6,0},{7,1},{8,14},{9,15},{10,... | collective-permute-start | bytes 196616 | tf_op jit(solution)/shard_map/ppermute | solution.py:27
  80.9 5.8 %collective-permute-start.26 = (bf16[16,2048]{1,0:T(8,128)(2,1)S(1)}, bf16[16,2048]{1,0:T(8,128)(2,1)S(1)}, u32[]{:S(2)}, u32[]{:S(2)}) collective-permute-start(bf16[16,2048]{1,0:T(8,128)(2,1)S(1)} %get-tuple-element.81), channel_id=1, source_target_pairs={{0,4},{1,5},{2,6},{3,7},{4,0},{5,1},{6,2},{7,3},{8,12},{9,13},{10,... | collective-permute-start | bytes 196616 | tf_op jit(solution)/shard_map/ppermute | solution.py:27
  81.7 5.0 %collective-permute-start.27 = (bf16[16,2048]{1,0:T(8,128)(2,1)S(1)}, bf16[16,2048]{1,0:T(8,128)(2,1)S(1)}, u32[]{:S(2)}, u32[]{:S(2)}) collective-permute-start(bf16[16,2048]{1,0:T(8,128)(2,1)S(1)} %get-tuple-element.82), channel_id=1, source_target_pairs={{0,2},{1,3},{2,0},{3,1},{4,6},{5,7},{6,4},{7,5},{8,10},{9,11},{10,... | collective-permute-start | bytes 196616 | tf_op jit(solution)/shard_map/ppermute | solution.py:27
  86.7 5.0 %collective-permute-start.29 = (bf16[16,2048]{1,0:T(8,128)(2,1)S(1)}, bf16[16,2048]{1,0:T(8,128)(2,1)S(1)}, u32[]{:S(2)}, u32[]{:S(2)}) collective-permute-start(bf16[16,2048]{1,0:T(8,128)(2,1)S(1)} %shard_map.106), channel_id=1, source_target_pairs={{0,9},{1,8},{2,11},{3,10},{4,13},{5,12},{6,15},{7,14},{8,17},{9,16... | collective-permute-start | bytes 196616 | tf_op jit(solution)/shard_map/ppermute | solution.py:27
  88.3 4.1 %collective-permute-start.28 = (bf16[16,2048]{1,0:T(8,128)(2,1)S(1)}, bf16[16,2048]{1,0:T(8,128)(2,1)S(1)}, u32[]{:S(2)}, u32[]{:S(2)}) collective-permute-start(bf16[16,2048]{1,0:T(8,128)(2,1)S(1)} %shard_map.106), channel_id=1, source_target_pairs={{0,8},{1,9},{2,10},{3,11},{4,12},{5,13},{6,14},{7,15},{8,16},{9,17... | collective-permute-start | bytes 196616 | tf_op jit(solution)/shard_map/ppermute | solution.py:27
  92.5 6.4 %collective-permute-start.32 = (bf16[16,2048]{1,0:T(8,128)(2,1)S(1)}, bf16[16,2048]{1,0:T(8,128)(2,1)S(1)}, u32[]{:S(2)}, u32[]{:S(2)}) collective-permute-start(bf16[16,2048]{1,0:T(8,128)(2,1)S(1)} %get-tuple-element.83.refs_0_), channel_id=1, source_target_pairs={{0,6},{1,7},{2,4},{3,5},{4,2},{5,3},{6,0},{7,1},{8,14},{9,15},{10,... | collective-permute-start | bytes 196616 | tf_op jit(solution)/shard_map/ppermute | solution.py:27
  94.4 6.9 %collective-permute-start.31 = (bf16[16,2048]{1,0:T(8,128)(2,1)S(1)}, bf16[16,2048]{1,0:T(8,128)(2,1)S(1)}, u32[]{:S(2)}, u32[]{:S(2)}) collective-permute-start(bf16[16,2048]{1,0:T(8,128)(2,1)S(1)} %get-tuple-element.83.refs_0_), channel_id=1, source_target_pairs={{0,4},{1,5},{2,6},{3,7},{4,0},{5,1},{6,2},{7,3},{8,12},{9,13},{10,... | collective-permute-start | bytes 196616 | tf_op jit(solution)/shard_map/ppermute | solution.py:27
  94.8 6.5 %collective-permute-start.30 = (bf16[16,2048]{1,0:T(8,128)(2,1)S(1)}, bf16[16,2048]{1,0:T(8,128)(2,1)S(1)}, u32[]{:S(2)}, u32[]{:S(2)}) collective-permute-start(bf16[16,2048]{1,0:T(8,128)(2,1)S(1)} %get-tuple-element.83.refs_0_), channel_id=1, source_target_pairs={{0,2},{1,3},{2,0},{3,1},{4,6},{5,7},{6,4},{7,5},{8,10},{9,11},{10,... | collective-permute-start | bytes 196616 | tf_op jit(solution)/shard_map/ppermute | solution.py:27
  103.6 6.4 %collective-permute-start.33 = (bf16[16,2048]{1,0:T(8,128)(2,1)S(1)}, bf16[16,2048]{1,0:T(8,128)(2,1)S(1)}, u32[]{:S(2)}, u32[]{:S(2)}) collective-permute-start(bf16[16,2048]{1,0:T(8,128)(2,1)S(1)} %get-tuple-element.86), channel_id=1, source_target_pairs={{0,6},{1,7},{2,4},{3,5},{4,2},{5,3},{6,0},{7,1},{8,14},{9,15},{10,... | collective-permute-start | bytes 196616 | tf_op jit(solution)/shard_map/ppermute | solution.py:27
  105.4 6.6 %collective-permute-start.34 = (bf16[16,2048]{1,0:T(8,128)(2,1)S(1)}, bf16[16,2048]{1,0:T(8,128)(2,1)S(1)}, u32[]{:S(2)}, u32[]{:S(2)}) collective-permute-start(bf16[16,2048]{1,0:T(8,128)(2,1)S(1)} %get-tuple-element.87), channel_id=1, source_target_pairs={{0,4},{1,5},{2,6},{3,7},{4,0},{5,1},{6,2},{7,3},{8,12},{9,13},{10,... | collective-permute-start | bytes 196616 | tf_op jit(solution)/shard_map/ppermute | solution.py:27
  105.5 6.6 %collective-permute-start.35 = (bf16[16,2048]{1,0:T(8,128)(2,1)S(1)}, bf16[16,2048]{1,0:T(8,128)(2,1)S(1)}, u32[]{:S(2)}, u32[]{:S(2)}) collective-permute-start(bf16[16,2048]{1,0:T(8,128)(2,1)S(1)} %get-tuple-element.88), channel_id=1, source_target_pairs={{0,2},{1,3},{2,0},{3,1},{4,6},{5,7},{6,4},{7,5},{8,10},{9,11},{10,... | collective-permute-start | bytes 196616 | tf_op jit(solution)/shard_map/ppermute | solution.py:27
  112.1 4.0 %collective-permute-start.36 = (bf16[8,2048]{1,0:T(8,128)(2,1)S(1)}, bf16[8,2048]{1,0:T(8,128)(2,1)S(1)}, u32[]{:S(2)}, u32[]{:S(2)}) collective-permute-start(bf16[8,2048]{1,0:T(8,128)(2,1)S(1)} %slice.17), channel_id=1, source_target_pairs={{0,1},{1,0},{2,3},{3,2},{4,5},{5,4},{6,7},{7,6},{8,9},{9,8},{10,11... | collective-permute-start | bytes 98312 | tf_op jit(solution)/shard_map/ppermute | solution.py:27

commit v10 on v8

--- a/solution.py
+++ b/solution.py
@@ -326,8 +326,8 @@
     )(*[pltpu.with_memory_space_constraint(value, pltpu.HBM) for value in values])
 
 
-def widest_first(outer):
-    return range(outer - 1, 0, -1)
+def both_first(outer):
+    return [outer - 1, *range(1, outer - 1)]
 
 
 def added(values):
@@ -347,7 +347,7 @@
     tok_dev = state.shape[1]
 
     def spread(value):
-        got = {j: moved(value, 2 * j, 0) for j in widest_first(outer)}
+        got = {j: moved(value, j, 0) for j in both_first(outer)}
         return [value] + [got[j] for j in range(1, outer)]
 
     weights = [w_gate[:, 0], w_up[:, 0], w_down[:, 0]]
@@ -364,7 +364,7 @@
         prepare_kernel, jax.ShapeDtypeStruct(shape, state.dtype), state[0],
         jnp.transpose(routes[:, 0], (0, 2, 1)), jnp.transpose(gates[:, 0], (0, 2, 1)), norm_gain,
     )
-    other = moved(own, 1, 0)
+    other = moved(own, outer, 0)
     pair = small(join_kernel, jax.ShapeDtypeStruct((2 * tok_dev, shape[1]), state.dtype), own, other)
     arrived = spread(pair)
     users = [later_users(tick_idx, segments) for tick_idx in range(TICKS)]
@@ -372,7 +372,7 @@
     slots = [loaded(weights, (True, True, False), 0)]
     if users[0]:
         slots.append(loaded(weights, (True, True, False), 1))
-    late = stacked(lax.optimization_barrier((*spare_all, arrived[1]))[:3], 1)
+    late = stacked(lax.optimization_barrier((*spare_all, arrived[both_first(outer)[-1]]))[:3], 1)
     near = [swapped(late, users[opening])] if opening < TICKS else []
     own = state[0]
     before = run_layer(arrived, arrived, own, [(slot, []) for slot in slots], tick_idx=0, tok_dev=tok_dev, ends=False)
@@ -388,16 +388,16 @@
             rows, arrived, own, layers, tick_idx=tick_idx, tok_dev=tok_dev,
             carried=before if tick_idx == 0 else None,
         )
-        got = [moved(parts[j], 2 * j, 0) for j in widest_first(outer)]
+        got = [moved(parts[j], j, 0) for j in both_first(outer)]
         if tick_idx == 0 and not users[0]:
             tied = lax.optimization_barrier((*weights, parts[0]))[:3]
             gate = loaded(tied[:1], (True,), 1)
         if tick_idx + 1 == TICKS:
             total = added([parts[0]] + got)
-            other = moved(total[tok_dev:].astype(jnp.bfloat16), 1, 0)
+            other = moved(total[tok_dev:].astype(jnp.bfloat16), outer, 0)
             return added([total[:tok_dev], other]).astype(jnp.bfloat16)[None]
         total = summed([parts[0]] + got)
-        across = moved(total, 1, 1)
+        across = moved(total, outer, 1)
         along = moved(total, 0, 1)
         if tick_idx == 0:
             far = [moved(lax.optimization_barrier((late, total))[0], 0, -1)]

time: 117 us -> 111 us (0.949)
  waiting for transfers between devices: 40.1 us -> 36.7 us
  starting transfers between devices: 51.8 us -> 49.1 us
    ppermute x36, waiting for transfers between devices: 40.1 us -> 36.7 us  [moved(): return lax.ppermute(value, BOTH, pairs)]
    ppermute x36, starting transfers between devices: 49.9 us -> 47.2 us  [moved(): return lax.ppermute(value, BOTH, pairs)]
  transfers between devices with their start and end apart: 37 -> 37, of which waited for: 21 -> 26; matrix products, arithmetic and copies ran while one was open for 0% -> 0% of each run, Pallas kernels for 15% -> 16%
where the time goes in v10:
time: 111 us
  starting transfers between devices  49.1 us (44%)
  waiting for transfers between devices  36.7 us (33%)
  Pallas kernels  23.8 us (21%)
    ppermute x36, starting transfers between devices, moved(): return lax.ppermute(value, BOTH, pairs)  47.2 us
    ppermute x36, waiting for transfers between devices, moved(): return lax.ppermute(value, BOTH, pairs)  36.7 us
    pallas_call x3, Pallas kernels, loaded(): pl.pallas_call(functools.partial(load_kernel, turned=turned, group=group)...  9.77 us
    pallas_call x5, Pallas kernels, run_layer(): pl.pallas_call(functools.partial(layer_kernel, tick_idx=tick_idx, blocks=...  9.35 us
    pallas_call x2, Pallas kernels, filled(): pl.pallas_call(functools.partial(fill_kernel, group=group), out_shape=[pl...  2.43 us
  transfers between devices with their start and end apart: 37, of which 26 were waited for; matrix products, arithmetic and copies ran while one was open for 0% of the time, Pallas kernels for 16%

profile of v10, /device:TPU:0, one launch (start us, length us, event | category | flops | bytes accessed | tf_op | source)
XLA Modules:
  0.0 110.6 jit_solution(3494142921560278838)
XLA Ops:
  0.0 1.1 %fill.2 = bf16[160,2048]{1,0:T(8,128)(2,1)S(1)} custom-call(bf16[2,160,2048]{2,1,0:T(8,128)(2,1)} %bitcast.30), custom_call_target="tpu_custom_call" | custom-call | tf_op jit(solution)/shard_map/fill/pallas_call | solution.py:247
  1.1 2.5 %collective-permute-start.4 = (bf16[160,2048]{1,0:T(8,128)(2,1)S(1)}, bf16[160,2048]{1,0:T(8,128)(2,1)S(1)}, u32[]{:S(2)}, u32[]{:S(2)}) collective-permute-start(bf16[160,2048]{1,0:T(8,128)(2,1)S(1)} %fill.2), channel_id=1, source_target_pairs={{0,24},{1,25},{2,26},{3,27},{4,28},{5,29},{6,30},{7,31},{8,0},{9,1... | collective-permute-start | bytes 1966088 | tf_op jit(solution)/shard_map/ppermute | solution.py:27
  3.7 1.3 %fill.3 = (bf16[160,2048]{1,0:T(8,128)(2,1)S(1)}, bf16[160,2048]{1,0:T(8,128)(2,1)S(1)}) custom-call(bf16[2,160,2048]{2,1,0:T(8,128)(2,1)} %bitcast.26, bf16[2,160,2048]{2,1,0:T(8,128)(2,1)} %bitcast.28), custom_call_target="tpu_custom_call" | custom-call | tf_op jit(solution)/shard_map/fill/pallas_call | solution.py:247
  6.0 2.6 %collective-permute-start = (bf16[8,2176]{1,0:T(8,128)(2,1)S(1)}, bf16[8,2176]{1,0:T(8,128)(2,1)S(1)}, u32[]{:S(2)}, u32[]{:S(2)}) collective-permute-start(bf16[8,2176]{1,0:T(8,128)(2,1)S(1)} %shard_map.100.first_ref), channel_id=1, source_target_pairs={{0,4},{1,5},{2,6},{3,7},{4,0},{5,1},{6,2},{7,3},{8,12},{9,13},{10,... | collective-permute-start | bytes 104456 | tf_op jit(solution)/shard_map/ppermute | solution.py:27
  8.6 2.2 %collective-permute-done.second_ref = bf16[8,2176]{1,0:T(8,128)(2,1)S(1)} collective-permute-done((bf16[8,2176]{1,0:T(8,128)(2,1)S(1)}, bf16[8,2176]{1,0:T(8,128)(2,1)S(1)}, u32[]{:S(2)}, u32[]{:S(2)}) %collective-permute-start) | collective-permute-done | bytes 34848 | tf_op jit(solution)/shard_map/ppermute | solution.py:27
  10.9 1.6 %collective-permute-start.2 = (bf16[16,2176]{1,0:T(8,128)(2,1)S(1)}, bf16[16,2176]{1,0:T(8,128)(2,1)S(1)}, u32[]{:S(2)}, u32[]{:S(2)}) collective-permute-start(bf16[16,2176]{1,0:T(8,128)(2,1)S(1)} %shard_map.101.refs_0_.refs_4_), channel_id=1, source_target_pairs={{0,2},{1,3},{2,0},{3,1},{4,6},{5,7},{6,4},{7,5},{8,10},{9,11},{10,... | collective-permute-start | bytes 208904 | tf_op jit(solution)/shard_map/ppermute | solution.py:27
  12.5 1.4 %collective-permute-start.3 = (bf16[16,2176]{1,0:T(8,128)(2,1)S(1)}, bf16[16,2176]{1,0:T(8,128)(2,1)S(1)}, u32[]{:S(2)}, u32[]{:S(2)}) collective-permute-start(bf16[16,2176]{1,0:T(8,128)(2,1)S(1)} %shard_map.101.refs_0_.refs_4_), channel_id=1, source_target_pairs={{0,3},{1,2},{2,1},{3,0},{4,7},{5,6},{6,5},{7,4},{8,11},{9,10},{10,... | collective-permute-start | bytes 208904 | tf_op jit(solution)/shard_map/ppermute | solution.py:27
  13.9 1.4 %collective-permute-done.2.refs_2_.refs_6_ = bf16[16,2176]{1,0:T(8,128)(2,1)S(1)} collective-permute-done((bf16[16,2176]{1,0:T(8,128)(2,1)S(1)}, bf16[16,2176]{1,0:T(8,128)(2,1)S(1)}, u32[]{:S(2)}, u32[]{:S(2)}) %collective-permute-start.2) | collective-permute-done | bytes 69664 | tf_op jit(solution)/shard_map/ppermute | solution.py:27
  15.3 1.5 %stack.1 = bf16[3,160,2048]{2,1,0:T(8,128)(2,1)S(1)} custom-call(bf16[2,160,2048]{2,1,0:T(8,128)(2,1)} %bitcast.31, bf16[2,160,2048]{2,1,0:T(8,128)(2,1)} %bitcast.27, bf16[2,160,2048]{2,1,0:T(8,128)(2,1)} %bitcast.29), custom_call_target="tpu_custom_call" | custom-call | tf_op jit(solution)/shard_map/stack/pallas_call | solution.py:318
  16.8 1.9 %collective-permute-start.15 = (bf16[3,160,2048]{2,1,0:T(8,128)(2,1)S(1)}, bf16[3,160,2048]{2,1,0:T(8,128)(2,1)S(1)}, u32[]{:S(2)}, u32[]{:S(2)}) collective-permute-start(bf16[3,160,2048]{2,1,0:T(8,128)(2,1)S(1)} %stack.1), channel_id=1, source_target_pairs={{0,8},{1,9},{2,10},{3,11},{4,12},{5,13},{6,14},{7,15},{8,0},{9,1},... | collective-permute-start | bytes 5898248 | tf_op jit(solution)/shard_map/ppermute | solution.py:58
  18.7 2.1 %collective-permute-start.1 = (bf16[16,2176]{1,0:T(8,128)(2,1)S(1)}, bf16[16,2176]{1,0:T(8,128)(2,1)S(1)}, u32[]{:S(2)}, u32[]{:S(2)}) collective-permute-start(bf16[16,2176]{1,0:T(8,128)(2,1)S(1)} %shard_map.101.refs_0_.refs_4_), channel_id=1, source_target_pairs={{0,1},{1,0},{2,3},{3,2},{4,5},{5,4},{6,7},{7,6},{8,9},{9,8},{10,11... | collective-permute-start | bytes 208904 | tf_op jit(solution)/shard_map/ppermute | solution.py:27
  20.8 4.3 %load.3 = (bf16[2048,640]{1,0:T(8,128)(2,1)S(1)}, bf16[2048,640]{1,0:T(8,128)(2,1)S(1)}, bf16[640,2048]{1,0:T(8,128)(2,1)S(1)}) custom-call(bf16[2,640,2048]{2,1,0:T(8,128)(2,1)} %bitcast.24, bf16[2,640,2048]{2,1,0:T(8,128)(2,1)} %bitcast.20, bf16[2,640,2048]{2,1,0:T(8,128)(2,1)} %bitcast.22), custom_call_target="tpu_custom_call" | custom-call | tf_op jit(solution)/shard_map/load/pallas_call | solution.py:289
  25.2 1.5 %layer.5.refs_9_ = f32[64,2048]{1,0:T(8,128)S(1)} custom-call(bf16[16,2176]{1,0:T(8,128)(2,1)S(1)} %shard_map.101.refs_0_.refs_4_, bf16[16,2176]{1,0:T(8,128)(2,1)S(1)} %collective-permute-done.1.refs_1_.refs_5_, bf16[16,2176]{1,0:T(8,128)(2,1)S(1)} %collective-permute-done.2.refs_2_.refs_6_, bf16[16,2176]{1,0:T(8,128)(2,1)S(1)} %collective-permute-done.3.refs_3_.refs_7_, ...), custom_call_target="tpu_custom_call" | custom-call | flops 503316480 | bytes 7864320 | tf_op jit(solution)/shard_map/layer/pallas_call | solution.py:191
  27.6 1.6 %collective-permute-start.7 = (bf16[16,2048]{1,0:T(8,128)(2,1)S(1)}, bf16[16,2048]{1,0:T(8,128)(2,1)S(1)}, u32[]{:S(2)}, u32[]{:S(2)}) collective-permute-start(bf16[16,2048]{1,0:T(8,128)(2,1)S(1)} %get-tuple-element.59), channel_id=1, source_target_pairs={{0,3},{1,2},{2,1},{3,0},{4,7},{5,6},{6,5},{7,4},{8,11},{9,10},{10,... | collective-permute-start | bytes 196616 | tf_op jit(solution)/shard_map/ppermute | solution.py:27
  29.2 1.0 collective-permute-start.8
  31.1 1.7 %collective-permute-done.7.refs_1_ = bf16[16,2048]{1,0:T(8,128)(2,1)S(1)} collective-permute-done((bf16[16,2048]{1,0:T(8,128)(2,1)S(1)}, bf16[16,2048]{1,0:T(8,128)(2,1)S(1)}, u32[]{:S(2)}, u32[]{:S(2)}) %collective-permute-start.7) | collective-permute-done | bytes 65568 | tf_op jit(solution)/shard_map/ppermute | solution.py:27
  32.8 1.4 %collective-permute-done.8.refs_2_ = bf16[16,2048]{1,0:T(8,128)(2,1)S(1)} collective-permute-done((bf16[16,2048]{1,0:T(8,128)(2,1)S(1)}, bf16[16,2048]{1,0:T(8,128)(2,1)S(1)}, u32[]{:S(2)}, u32[]{:S(2)}) %collective-permute-start.8) | collective-permute-done | bytes 65568 | tf_op jit(solution)/shard_map/ppermute | solution.py:27
  35.1 3.1 %collective-permute-start.11 = (bf16[16,2048]{1,0:T(8,128)(2,1)S(1)}, bf16[16,2048]{1,0:T(8,128)(2,1)S(1)}, u32[]{:S(2)}, u32[]{:S(2)}) collective-permute-start(bf16[16,2048]{1,0:T(8,128)(2,1)S(1)} %shard_map.102), channel_id=1, source_target_pairs={{0,12},{1,13},{2,14},{3,15},{4,8},{5,9},{6,10},{7,11},{8,20},{9,21... | collective-permute-start | bytes 196616 | tf_op jit(solution)/shard_map/ppermute | solution.py:27
  38.2 4.2 %collective-permute-done.11.across_ref = bf16[16,2048]{1,0:T(8,128)(2,1)S(1)} collective-permute-done((bf16[16,2048]{1,0:T(8,128)(2,1)S(1)}, bf16[16,2048]{1,0:T(8,128)(2,1)S(1)}, u32[]{:S(2)}, u32[]{:S(2)}) %collective-permute-start.11) | collective-permute-done | bytes 65568 | tf_op jit(solution)/shard_map/ppermute | solution.py:27
  43.9 1.8 %collective-permute-start.13 = (bf16[16,2048]{1,0:T(8,128)(2,1)S(1)}, bf16[16,2048]{1,0:T(8,128)(2,1)S(1)}, u32[]{:S(2)}, u32[]{:S(2)}) collective-permute-start(bf16[16,2048]{1,0:T(8,128)(2,1)S(1)} %get-tuple-element.62.refs_0_), channel_id=1, source_target_pairs={{0,2},{1,3},{2,0},{3,1},{4,6},{5,7},{6,4},{7,5},{8,10},{9,11},{10,... | collective-permute-start | bytes 196616 | tf_op jit(solution)/shard_map/ppermute | solution.py:27
  45.7 1.2 %collective-permute-start.12 = (bf16[16,2048]{1,0:T(8,128)(2,1)S(1)}, bf16[16,2048]{1,0:T(8,128)(2,1)S(1)}, u32[]{:S(2)}, u32[]{:S(2)}) collective-permute-start(bf16[16,2048]{1,0:T(8,128)(2,1)S(1)} %get-tuple-element.62.refs_0_), channel_id=1, source_target_pairs={{0,1},{1,0},{2,3},{3,2},{4,5},{5,4},{6,7},{7,6},{8,9},{9,8},{10,11... | collective-permute-start | bytes 196616 | tf_op jit(solution)/shard_map/ppermute | solution.py:27
  46.9 2.5 %load.4.refs_15_ = bf16[2048,640]{1,0:T(8,128)(2,1)S(1)} custom-call(bf16[2,640,2048]{2,1,0:T(8,128)(2,1)} %bitcast.25), custom_call_target="tpu_custom_call" | custom-call | tf_op jit(solution)/shard_map/load/pallas_call | solution.py:289
  49.4 2.9 %load.5 = (bf16[2048,640]{1,0:T(8,128)(2,1)S(1)}, bf16[640,2048]{1,0:T(8,128)(2,1)S(1)}) custom-call(bf16[2,640,2048]{2,1,0:T(8,128)(2,1)} %bitcast.21, bf16[2,640,2048]{2,1,0:T(8,128)(2,1)} %bitcast.23), custom_call_target="tpu_custom_call" | custom-call | tf_op jit(solution)/shard_map/load/pallas_call | solution.py:289
  52.4 2.3 %layer.7 = (f32[16,2048]{1,0:T(8,128)S(1)}, bf16[16,2048]{1,0:T(8,128)(2,1)S(1)}, bf16[16,2048]{1,0:T(8,128)(2,1)S(1)}, bf16[16,2048]{1,0:T(8,128)(2,1)S(1)}) custom-call(bf16[16,2048]{1,0:T(8,128)(2,1)S(1)} %get-tuple-element.62.refs_0_, bf16[16,2048]{1,0:T(8,128)(2,1)S(1)} %collective-permute-done.12.refs_1_, ...), custom_call_target="tpu_custom_call" | custom-call | flops 629145600 | bytes 9830400 | tf_op jit(solution)/shard_map/layer/pallas_call | solution.py:191
  55.2 1.0 collective-permute-start.17
  56.2 2.0 %collective-permute-start.18 = (bf16[16,2048]{1,0:T(8,128)(2,1)S(1)}, bf16[16,2048]{1,0:T(8,128)(2,1)S(1)}, u32[]{:S(2)}, u32[]{:S(2)}) collective-permute-start(bf16[16,2048]{1,0:T(8,128)(2,1)S(1)} %get-tuple-element.75), channel_id=1, source_target_pairs={{0,2},{1,3},{2,0},{3,1},{4,6},{5,7},{6,4},{7,5},{8,10},{9,11},{10,... | collective-permute-start | bytes 196616 | tf_op jit(solution)/shard_map/ppermute | solution.py:27
  58.3 1.8 %collective-permute-done.16.refs_1_ = bf16[16,2048]{1,0:T(8,128)(2,1)S(1)} collective-permute-done((bf16[16,2048]{1,0:T(8,128)(2,1)S(1)}, bf16[16,2048]{1,0:T(8,128)(2,1)S(1)}, u32[]{:S(2)}, u32[]{:S(2)}) %collective-permute-start.16) | collective-permute-done | bytes 65568 | tf_op jit(solution)/shard_map/ppermute | solution.py:27
  60.9 2.9 %collective-permute-start.19 = (bf16[16,2048]{1,0:T(8,128)(2,1)S(1)}, bf16[16,2048]{1,0:T(8,128)(2,1)S(1)}, u32[]{:S(2)}, u32[]{:S(2)}) collective-permute-start(bf16[16,2048]{1,0:T(8,128)(2,1)S(1)} %shard_map.104), channel_id=1, source_target_pairs={{0,8},{1,9},{2,10},{3,11},{4,12},{5,13},{6,14},{7,15},{8,16},{9,17... | collective-permute-start | bytes 196616 | tf_op jit(solution)/shard_map/ppermute | solution.py:27
  63.8 3.0 %collective-permute-done.20.across_ref = bf16[16,2048]{1,0:T(8,128)(2,1)S(1)} collective-permute-done((bf16[16,2048]{1,0:T(8,128)(2,1)S(1)}, bf16[16,2048]{1,0:T(8,128)(2,1)S(1)}, u32[]{:S(2)}, u32[]{:S(2)}) %collective-permute-start.20) | collective-permute-done | bytes 65568 | tf_op jit(solution)/shard_map/ppermute | solution.py:27
  67.1 1.4 %collective-permute-start.23 = (bf16[16,2048]{1,0:T(8,128)(2,1)S(1)}, bf16[16,2048]{1,0:T(8,128)(2,1)S(1)}, u32[]{:S(2)}, u32[]{:S(2)}) collective-permute-start(bf16[16,2048]{1,0:T(8,128)(2,1)S(1)} %get-tuple-element.76.refs_0_), channel_id=1, source_target_pairs={{0,3},{1,2},{2,1},{3,0},{4,7},{5,6},{6,5},{7,4},{8,11},{9,10},{10,... | collective-permute-start | bytes 196616 | tf_op jit(solution)/shard_map/ppermute | solution.py:27
  68.6 1.2 %collective-permute-start.22 = (bf16[16,2048]{1,0:T(8,128)(2,1)S(1)}, bf16[16,2048]{1,0:T(8,128)(2,1)S(1)}, u32[]{:S(2)}, u32[]{:S(2)}) collective-permute-start(bf16[16,2048]{1,0:T(8,128)(2,1)S(1)} %get-tuple-element.76.refs_0_), channel_id=1, source_target_pairs={{0,2},{1,3},{2,0},{3,1},{4,6},{5,7},{6,4},{7,5},{8,10},{9,11},{10,... | collective-permute-start | bytes 196616 | tf_op jit(solution)/shard_map/ppermute | solution.py:27
  70.7 2.2 %collective-permute-done.23.refs_3_ = bf16[16,2048]{1,0:T(8,128)(2,1)S(1)} collective-permute-done((bf16[16,2048]{1,0:T(8,128)(2,1)S(1)}, bf16[16,2048]{1,0:T(8,128)(2,1)S(1)}, u32[]{:S(2)}, u32[]{:S(2)}) %collective-permute-start.23) | collective-permute-done | bytes 65568 | tf_op jit(solution)/shard_map/ppermute | solution.py:27
  74.0 2.4 %layer.8 = (f32[16,2048]{1,0:T(8,128)S(1)}, bf16[16,2048]{1,0:T(8,128)(2,1)S(1)}, bf16[16,2048]{1,0:T(8,128)(2,1)S(1)}, bf16[16,2048]{1,0:T(8,128)(2,1)S(1)}) custom-call(bf16[16,2048]{1,0:T(8,128)(2,1)S(1)} %get-tuple-element.76.refs_0_, bf16[16,2048]{1,0:T(8,128)(2,1)S(1)} %collective-permute-done.21.refs_1_, ...), custom_call_target="tpu_custom_call" | custom-call | flops 629145600 | bytes 9830400 | tf_op jit(solution)/shard_map/layer/pallas_call | solution.py:191
  76.4 1.6 %collective-permute-start.25 = (bf16[16,2048]{1,0:T(8,128)(2,1)S(1)}, bf16[16,2048]{1,0:T(8,128)(2,1)S(1)}, u32[]{:S(2)}, u32[]{:S(2)}) collective-permute-start(bf16[16,2048]{1,0:T(8,128)(2,1)S(1)} %get-tuple-element.80), channel_id=1, source_target_pairs={{0,3},{1,2},{2,1},{3,0},{4,7},{5,6},{6,5},{7,4},{8,11},{9,10},{10,... | collective-permute-start | bytes 196616 | tf_op jit(solution)/shard_map/ppermute | solution.py:27
  78.8 1.2 %collective-permute-start.27 = (bf16[16,2048]{1,0:T(8,128)(2,1)S(1)}, bf16[16,2048]{1,0:T(8,128)(2,1)S(1)}, u32[]{:S(2)}, u32[]{:S(2)}) collective-permute-start(bf16[16,2048]{1,0:T(8,128)(2,1)S(1)} %get-tuple-element.82), channel_id=1, source_target_pairs={{0,2},{1,3},{2,0},{3,1},{4,6},{5,7},{6,4},{7,5},{8,10},{9,11},{10,... | collective-permute-start | bytes 196616 | tf_op jit(solution)/shard_map/ppermute | solution.py:27
  80.0 1.7 %collective-permute-done.25.refs_1_ = bf16[16,2048]{1,0:T(8,128)(2,1)S(1)} collective-permute-done((bf16[16,2048]{1,0:T(8,128)(2,1)S(1)}, bf16[16,2048]{1,0:T(8,128)(2,1)S(1)}, u32[]{:S(2)}, u32[]{:S(2)}) %collective-permute-start.25) | collective-permute-done | bytes 65568 | tf_op jit(solution)/shard_map/ppermute | solution.py:27
  83.2 1.9 %collective-permute-start.28 = (bf16[16,2048]{1,0:T(8,128)(2,1)S(1)}, bf16[16,2048]{1,0:T(8,128)(2,1)S(1)}, u32[]{:S(2)}, u32[]{:S(2)}) collective-permute-start(bf16[16,2048]{1,0:T(8,128)(2,1)S(1)} %shard_map.106), channel_id=1, source_target_pairs={{0,8},{1,9},{2,10},{3,11},{4,12},{5,13},{6,14},{7,15},{8,16},{9,17... | collective-permute-start | bytes 196616 | tf_op jit(solution)/shard_map/ppermute | solution.py:27
  85.1 4.3 %collective-permute-done.29.across_ref = bf16[16,2048]{1,0:T(8,128)(2,1)S(1)} collective-permute-done((bf16[16,2048]{1,0:T(8,128)(2,1)S(1)}, bf16[16,2048]{1,0:T(8,128)(2,1)S(1)}, u32[]{:S(2)}, u32[]{:S(2)}) %collective-permute-start.29) | collective-permute-done | bytes 65568 | tf_op jit(solution)/shard_map/ppermute | solution.py:27
  89.6 1.1 collective-permute-start.32
  90.6 1.6 %collective-permute-start.31 = (bf16[16,2048]{1,0:T(8,128)(2,1)S(1)}, bf16[16,2048]{1,0:T(8,128)(2,1)S(1)}, u32[]{:S(2)}, u32[]{:S(2)}) collective-permute-start(bf16[16,2048]{1,0:T(8,128)(2,1)S(1)} %get-tuple-element.83.refs_0_), channel_id=1, source_target_pairs={{0,2},{1,3},{2,0},{3,1},{4,6},{5,7},{6,4},{7,5},{8,10},{9,11},{10,... | collective-permute-start | bytes 196616 | tf_op jit(solution)/shard_map/ppermute | solution.py:27
  93.1 1.7 %collective-permute-done.32.refs_3_ = bf16[16,2048]{1,0:T(8,128)(2,1)S(1)} collective-permute-done((bf16[16,2048]{1,0:T(8,128)(2,1)S(1)}, bf16[16,2048]{1,0:T(8,128)(2,1)S(1)}, u32[]{:S(2)}, u32[]{:S(2)}) %collective-permute-start.32) | collective-permute-done | bytes 65568 | tf_op jit(solution)/shard_map/ppermute | solution.py:27
  95.2 1.3 %collective-permute-done.30.refs_1_ = bf16[16,2048]{1,0:T(8,128)(2,1)S(1)} collective-permute-done((bf16[16,2048]{1,0:T(8,128)(2,1)S(1)}, bf16[16,2048]{1,0:T(8,128)(2,1)S(1)}, u32[]{:S(2)}, u32[]{:S(2)}) %collective-permute-start.30) | collective-permute-done | bytes 65568 | tf_op jit(solution)/shard_map/ppermute | solution.py:27
  96.5 2.3 %layer.9 = (f32[16,2048]{1,0:T(8,128)S(1)}, bf16[16,2048]{1,0:T(8,128)(2,1)S(1)}, bf16[16,2048]{1,0:T(8,128)(2,1)S(1)}, bf16[16,2048]{1,0:T(8,128)(2,1)S(1)}) custom-call(bf16[16,2048]{1,0:T(8,128)(2,1)S(1)} %get-tuple-element.83.refs_0_, bf16[16,2048]{1,0:T(8,128)(2,1)S(1)} %collective-permute-done.30.refs_1_, ...), custom_call_target="tpu_custom_call" | custom-call | flops 629145600 | bytes 9830400 | tf_op jit(solution)/shard_map/layer/pallas_call | solution.py:191
  98.8 1.1 collective-permute-start.33
  100.8 1.6 %collective-permute-start.35 = (bf16[16,2048]{1,0:T(8,128)(2,1)S(1)}, bf16[16,2048]{1,0:T(8,128)(2,1)S(1)}, u32[]{:S(2)}, u32[]{:S(2)}) collective-permute-start(bf16[16,2048]{1,0:T(8,128)(2,1)S(1)} %get-tuple-element.88), channel_id=1, source_target_pairs={{0,2},{1,3},{2,0},{3,1},{4,6},{5,7},{6,4},{7,5},{8,10},{9,11},{10,... | collective-permute-start | bytes 196616 | tf_op jit(solution)/shard_map/ppermute | solution.py:27
  102.4 1.7 %collective-permute-done.33 = bf16[16,2048]{1,0:T(8,128)(2,1)S(1)} collective-permute-done((bf16[16,2048]{1,0:T(8,128)(2,1)S(1)}, bf16[16,2048]{1,0:T(8,128)(2,1)S(1)}, u32[]{:S(2)}, u32[]{:S(2)}) %collective-permute-start.33) | collective-permute-done | bytes 65568 | tf_op jit(solution)/shard_map/ppermute | solution.py:27
  105.1 2.3 %collective-permute-start.36 = (bf16[8,2048]{1,0:T(8,128)(2,1)S(1)}, bf16[8,2048]{1,0:T(8,128)(2,1)S(1)}, u32[]{:S(2)}, u32[]{:S(2)}) collective-permute-start(bf16[8,2048]{1,0:T(8,128)(2,1)S(1)} %slice.17), channel_id=1, source_target_pairs={{0,4},{1,5},{2,6},{3,7},{4,0},{5,1},{6,2},{7,3},{8,12},{9,13},{10,... | collective-permute-start | bytes 98312 | tf_op jit(solution)/shard_map/ppermute | solution.py:27
  107.4 2.5 %collective-permute-done.36 = bf16[8,2048]{1,0:T(8,128)(2,1)S(1)} collective-permute-done((bf16[8,2048]{1,0:T(8,128)(2,1)S(1)}, bf16[8,2048]{1,0:T(8,128)(2,1)S(1)}, u32[]{:S(2)}, u32[]{:S(2)}) %collective-permute-start.36) | collective-permute-done | bytes 32800 | tf_op jit(solution)/shard_map/ppermute | solution.py:27
  (56 shorter events, 15.2 us)
Async XLA Ops:
  0.0 5.8 %copy-start.3 = (f32[4,1,8,2]{2,3,1,0:T(2,128)S(1)}, f32[4,1,8,2]{2,3,1,0:T(2,128)}, u32[]{:S(2)}) copy-start(f32[4,1,8,2]{2,3,1,0:T(2,128)} %param.12) | copy-start | bytes 772
  0.0 5.8 %copy-start.2 = (s32[4,1,8,2]{2,3,1,0:T(2,128)S(1)}, s32[4,1,8,2]{2,3,1,0:T(2,128)}, u32[]{:S(2)}) copy-start(s32[4,1,8,2]{2,3,1,0:T(2,128)} %param.11) | copy-start | bytes 772
  0.0 5.8 %copy-start = (bf16[1,8,2048]{2,1,0:T(8,128)(2,1)S(1)}, bf16[1,8,2048]{2,1,0:T(8,128)(2,1)}, u32[]{:S(2)}) copy-start(bf16[1,8,2048]{2,1,0:T(8,128)(2,1)} %param.10) | copy-start | bytes 98308
  0.0 5.8 %copy-start.1 = (f32[2,1,2048]{2,1,0:T(1,128)S(1)}, f32[2,1,2048]{2,1,0:T(1,128)}, u32[]{:S(2)}) copy-start(f32[2,1,2048]{2,1,0:T(1,128)} %gain_ref.7) | copy-start | bytes 49156
  1.1 25.6 %collective-permute-start.4 = (bf16[160,2048]{1,0:T(8,128)(2,1)S(1)}, bf16[160,2048]{1,0:T(8,128)(2,1)S(1)}, u32[]{:S(2)}, u32[]{:S(2)}) collective-permute-start(bf16[160,2048]{1,0:T(8,128)(2,1)S(1)} %fill.2), channel_id=1, source_target_pairs={{0,24},{1,25},{2,26},{3,27},{4,28},{5,29},{6,30},{7,31},{8,0},{9,1... | collective-permute-start | bytes 1966088 | tf_op jit(solution)/shard_map/ppermute | solution.py:27
  5.0 21.8 %collective-permute-start.5 = (bf16[160,2048]{1,0:T(8,128)(2,1)S(1)}, bf16[160,2048]{1,0:T(8,128)(2,1)S(1)}, u32[]{:S(2)}, u32[]{:S(2)}) collective-permute-start(bf16[160,2048]{1,0:T(8,128)(2,1)S(1)} %get-tuple-element.56), channel_id=1, source_target_pairs={{0,24},{1,25},{2,26},{3,27},{4,28},{5,29},{6,30},{7,31},{8,0},{9,1... | collective-permute-start | bytes 1966088 | tf_op jit(solution)/shard_map/ppermute | solution.py:27
  5.7 21.1 %collective-permute-start.6 = (bf16[160,2048]{1,0:T(8,128)(2,1)S(1)}, bf16[160,2048]{1,0:T(8,128)(2,1)S(1)}, u32[]{:S(2)}, u32[]{:S(2)}) collective-permute-start(bf16[160,2048]{1,0:T(8,128)(2,1)S(1)} %get-tuple-element.57), channel_id=1, source_target_pairs={{0,24},{1,25},{2,26},{3,27},{4,28},{5,29},{6,30},{7,31},{8,0},{9,1... | collective-permute-start | bytes 1966088 | tf_op jit(solution)/shard_map/ppermute | solution.py:27
  6.0 4.9 %collective-permute-start = (bf16[8,2176]{1,0:T(8,128)(2,1)S(1)}, bf16[8,2176]{1,0:T(8,128)(2,1)S(1)}, u32[]{:S(2)}, u32[]{:S(2)}) collective-permute-start(bf16[8,2176]{1,0:T(8,128)(2,1)S(1)} %shard_map.100.first_ref), channel_id=1, source_target_pairs={{0,4},{1,5},{2,6},{3,7},{4,0},{5,1},{6,2},{7,3},{8,12},{9,13},{10,... | collective-permute-start | bytes 104456 | tf_op jit(solution)/shard_map/ppermute | solution.py:27
  10.9 4.4 %collective-permute-start.2 = (bf16[16,2176]{1,0:T(8,128)(2,1)S(1)}, bf16[16,2176]{1,0:T(8,128)(2,1)S(1)}, u32[]{:S(2)}, u32[]{:S(2)}) collective-permute-start(bf16[16,2176]{1,0:T(8,128)(2,1)S(1)} %shard_map.101.refs_0_.refs_4_), channel_id=1, source_target_pairs={{0,2},{1,3},{2,0},{3,1},{4,6},{5,7},{6,4},{7,5},{8,10},{9,11},{10,... | collective-permute-start | bytes 208904 | tf_op jit(solution)/shard_map/ppermute | solution.py:27
  12.5 6.2 %collective-permute-start.3 = (bf16[16,2176]{1,0:T(8,128)(2,1)S(1)}, bf16[16,2176]{1,0:T(8,128)(2,1)S(1)}, u32[]{:S(2)}, u32[]{:S(2)}) collective-permute-start(bf16[16,2176]{1,0:T(8,128)(2,1)S(1)} %shard_map.101.refs_0_.refs_4_), channel_id=1, source_target_pairs={{0,3},{1,2},{2,1},{3,0},{4,7},{5,6},{6,5},{7,4},{8,11},{9,10},{10,... | collective-permute-start | bytes 208904 | tf_op jit(solution)/shard_map/ppermute | solution.py:27
  16.8 35.6 %collective-permute-start.15 = (bf16[3,160,2048]{2,1,0:T(8,128)(2,1)S(1)}, bf16[3,160,2048]{2,1,0:T(8,128)(2,1)S(1)}, u32[]{:S(2)}, u32[]{:S(2)}) collective-permute-start(bf16[3,160,2048]{2,1,0:T(8,128)(2,1)S(1)} %stack.1), channel_id=1, source_target_pairs={{0,8},{1,9},{2,10},{3,11},{4,12},{5,13},{6,14},{7,15},{8,0},{9,1},... | collective-permute-start | bytes 5898248 | tf_op jit(solution)/shard_map/ppermute | solution.py:58
  18.7 6.5 %collective-permute-start.1 = (bf16[16,2176]{1,0:T(8,128)(2,1)S(1)}, bf16[16,2176]{1,0:T(8,128)(2,1)S(1)}, u32[]{:S(2)}, u32[]{:S(2)}) collective-permute-start(bf16[16,2176]{1,0:T(8,128)(2,1)S(1)} %shard_map.101.refs_0_.refs_4_), channel_id=1, source_target_pairs={{0,1},{1,0},{2,3},{3,2},{4,5},{5,4},{6,7},{7,6},{8,9},{9,8},{10,11... | collective-permute-start | bytes 208904 | tf_op jit(solution)/shard_map/ppermute | solution.py:27
  27.6 5.3 %collective-permute-start.7 = (bf16[16,2048]{1,0:T(8,128)(2,1)S(1)}, bf16[16,2048]{1,0:T(8,128)(2,1)S(1)}, u32[]{:S(2)}, u32[]{:S(2)}) collective-permute-start(bf16[16,2048]{1,0:T(8,128)(2,1)S(1)} %get-tuple-element.59), channel_id=1, source_target_pairs={{0,3},{1,2},{2,1},{3,0},{4,7},{5,6},{6,5},{7,4},{8,11},{9,10},{10,... | collective-permute-start | bytes 196616 | tf_op jit(solution)/shard_map/ppermute | solution.py:27
  29.2 5.0 %collective-permute-start.8 = (bf16[16,2048]{1,0:T(8,128)(2,1)S(1)}, bf16[16,2048]{1,0:T(8,128)(2,1)S(1)}, u32[]{:S(2)}, u32[]{:S(2)}) collective-permute-start(bf16[16,2048]{1,0:T(8,128)(2,1)S(1)} %get-tuple-element.60), channel_id=1, source_target_pairs={{0,1},{1,0},{2,3},{3,2},{4,5},{5,4},{6,7},{7,6},{8,9},{9,8},{10,11... | collective-permute-start | bytes 196616 | tf_op jit(solution)/shard_map/ppermute | solution.py:27
  30.2 4.3 %collective-permute-start.9 = (bf16[16,2048]{1,0:T(8,128)(2,1)S(1)}, bf16[16,2048]{1,0:T(8,128)(2,1)S(1)}, u32[]{:S(2)}, u32[]{:S(2)}) collective-permute-start(bf16[16,2048]{1,0:T(8,128)(2,1)S(1)} %get-tuple-element.61), channel_id=1, source_target_pairs={{0,2},{1,3},{2,0},{3,1},{4,6},{5,7},{6,4},{7,5},{8,10},{9,11},{10,... | collective-permute-start | bytes 196616 | tf_op jit(solution)/shard_map/ppermute | solution.py:27
  34.5 39.5 %collective-permute-start.24 = (bf16[3,160,2048]{2,1,0:T(8,128)(2,1)S(1)}, bf16[3,160,2048]{2,1,0:T(8,128)(2,1)S(1)}, u32[]{:S(2)}, u32[]{:S(2)}) collective-permute-start(bf16[3,160,2048]{2,1,0:T(8,128)(2,1)S(1)} %stack.1), channel_id=1, source_target_pairs={{0,24},{1,25},{2,26},{3,27},{4,28},{5,29},{6,30},{7,31},{8,0},{9,1... | collective-permute-start | bytes 5898248 | tf_op jit(solution)/shard_map/ppermute | solution.py:27
  35.1 7.3 %collective-permute-start.11 = (bf16[16,2048]{1,0:T(8,128)(2,1)S(1)}, bf16[16,2048]{1,0:T(8,128)(2,1)S(1)}, u32[]{:S(2)}, u32[]{:S(2)}) collective-permute-start(bf16[16,2048]{1,0:T(8,128)(2,1)S(1)} %shard_map.102), channel_id=1, source_target_pairs={{0,12},{1,13},{2,14},{3,15},{4,8},{5,9},{6,10},{7,11},{8,20},{9,21... | collective-permute-start | bytes 196616 | tf_op jit(solution)/shard_map/ppermute | solution.py:27
  38.2 5.1 %collective-permute-start.10 = (bf16[16,2048]{1,0:T(8,128)(2,1)S(1)}, bf16[16,2048]{1,0:T(8,128)(2,1)S(1)}, u32[]{:S(2)}, u32[]{:S(2)}) collective-permute-start(bf16[16,2048]{1,0:T(8,128)(2,1)S(1)} %shard_map.102), channel_id=1, source_target_pairs={{0,8},{1,9},{2,10},{3,11},{4,12},{5,13},{6,14},{7,15},{8,16},{9,17... | collective-permute-start | bytes 196616 | tf_op jit(solution)/shard_map/ppermute | solution.py:27
  43.3 9.0 %collective-permute-start.14 = (bf16[16,2048]{1,0:T(8,128)(2,1)S(1)}, bf16[16,2048]{1,0:T(8,128)(2,1)S(1)}, u32[]{:S(2)}, u32[]{:S(2)}) collective-permute-start(bf16[16,2048]{1,0:T(8,128)(2,1)S(1)} %get-tuple-element.62.refs_0_), channel_id=1, source_target_pairs={{0,3},{1,2},{2,1},{3,0},{4,7},{5,6},{6,5},{7,4},{8,11},{9,10},{10,... | collective-permute-start | bytes 196616 | tf_op jit(solution)/shard_map/ppermute | solution.py:27
  43.9 8.5 %collective-permute-start.13 = (bf16[16,2048]{1,0:T(8,128)(2,1)S(1)}, bf16[16,2048]{1,0:T(8,128)(2,1)S(1)}, u32[]{:S(2)}, u32[]{:S(2)}) collective-permute-start(bf16[16,2048]{1,0:T(8,128)(2,1)S(1)} %get-tuple-element.62.refs_0_), channel_id=1, source_target_pairs={{0,2},{1,3},{2,0},{3,1},{4,6},{5,7},{6,4},{7,5},{8,10},{9,11},{10,... | collective-permute-start | bytes 196616 | tf_op jit(solution)/shard_map/ppermute | solution.py:27
  45.7 6.7 %collective-permute-start.12 = (bf16[16,2048]{1,0:T(8,128)(2,1)S(1)}, bf16[16,2048]{1,0:T(8,128)(2,1)S(1)}, u32[]{:S(2)}, u32[]{:S(2)}) collective-permute-start(bf16[16,2048]{1,0:T(8,128)(2,1)S(1)} %get-tuple-element.62.refs_0_), channel_id=1, source_target_pairs={{0,1},{1,0},{2,3},{3,2},{4,5},{5,4},{6,7},{7,6},{8,9},{9,8},{10,11... | collective-permute-start | bytes 196616 | tf_op jit(solution)/shard_map/ppermute | solution.py:27
  54.7 5.3 %collective-permute-start.16 = (bf16[16,2048]{1,0:T(8,128)(2,1)S(1)}, bf16[16,2048]{1,0:T(8,128)(2,1)S(1)}, u32[]{:S(2)}, u32[]{:S(2)}) collective-permute-start(bf16[16,2048]{1,0:T(8,128)(2,1)S(1)} %get-tuple-element.73), channel_id=1, source_target_pairs={{0,3},{1,2},{2,1},{3,0},{4,7},{5,6},{6,5},{7,4},{8,11},{9,10},{10,... | collective-permute-start | bytes 196616 | tf_op jit(solution)/shard_map/ppermute | solution.py:27
  55.2 5.0 %collective-permute-start.17 = (bf16[16,2048]{1,0:T(8,128)(2,1)S(1)}, bf16[16,2048]{1,0:T(8,128)(2,1)S(1)}, u32[]{:S(2)}, u32[]{:S(2)}) collective-permute-start(bf16[16,2048]{1,0:T(8,128)(2,1)S(1)} %get-tuple-element.74), channel_id=1, source_target_pairs={{0,1},{1,0},{2,3},{3,2},{4,5},{5,4},{6,7},{7,6},{8,9},{9,8},{10,11... | collective-permute-start | bytes 196616 | tf_op jit(solution)/shard_map/ppermute | solution.py:27
  56.2 4.3 %collective-permute-start.18 = (bf16[16,2048]{1,0:T(8,128)(2,1)S(1)}, bf16[16,2048]{1,0:T(8,128)(2,1)S(1)}, u32[]{:S(2)}, u32[]{:S(2)}) collective-permute-start(bf16[16,2048]{1,0:T(8,128)(2,1)S(1)} %get-tuple-element.75), channel_id=1, source_target_pairs={{0,2},{1,3},{2,0},{3,1},{4,6},{5,7},{6,4},{7,5},{8,10},{9,11},{10,... | collective-permute-start | bytes 196616 | tf_op jit(solution)/shard_map/ppermute | solution.py:27
  60.5 6.2 %collective-permute-start.20 = (bf16[16,2048]{1,0:T(8,128)(2,1)S(1)}, bf16[16,2048]{1,0:T(8,128)(2,1)S(1)}, u32[]{:S(2)}, u32[]{:S(2)}) collective-permute-start(bf16[16,2048]{1,0:T(8,128)(2,1)S(1)} %shard_map.104), channel_id=1, source_target_pairs={{0,12},{1,13},{2,14},{3,15},{4,8},{5,9},{6,10},{7,11},{8,20},{9,21... | collective-permute-start | bytes 196616 | tf_op jit(solution)/shard_map/ppermute | solution.py:27
  60.9 6.1 %collective-permute-start.19 = (bf16[16,2048]{1,0:T(8,128)(2,1)S(1)}, bf16[16,2048]{1,0:T(8,128)(2,1)S(1)}, u32[]{:S(2)}, u32[]{:S(2)}) collective-permute-start(bf16[16,2048]{1,0:T(8,128)(2,1)S(1)} %shard_map.104), channel_id=1, source_target_pairs={{0,8},{1,9},{2,10},{3,11},{4,12},{5,13},{6,14},{7,15},{8,16},{9,17... | collective-permute-start | bytes 196616 | tf_op jit(solution)/shard_map/ppermute | solution.py:27
  67.1 5.8 %collective-permute-start.23 = (bf16[16,2048]{1,0:T(8,128)(2,1)S(1)}, bf16[16,2048]{1,0:T(8,128)(2,1)S(1)}, u32[]{:S(2)}, u32[]{:S(2)}) collective-permute-start(bf16[16,2048]{1,0:T(8,128)(2,1)S(1)} %get-tuple-element.76.refs_0_), channel_id=1, source_target_pairs={{0,3},{1,2},{2,1},{3,0},{4,7},{5,6},{6,5},{7,4},{8,11},{9,10},{10,... | collective-permute-start | bytes 196616 | tf_op jit(solution)/shard_map/ppermute | solution.py:27
  68.6 4.6 %collective-permute-start.22 = (bf16[16,2048]{1,0:T(8,128)(2,1)S(1)}, bf16[16,2048]{1,0:T(8,128)(2,1)S(1)}, u32[]{:S(2)}, u32[]{:S(2)}) collective-permute-start(bf16[16,2048]{1,0:T(8,128)(2,1)S(1)} %get-tuple-element.76.refs_0_), channel_id=1, source_target_pairs={{0,2},{1,3},{2,0},{3,1},{4,6},{5,7},{6,4},{7,5},{8,10},{9,11},{10,... | collective-permute-start | bytes 196616 | tf_op jit(solution)/shard_map/ppermute | solution.py:27
  69.7 4.3 %collective-permute-start.21 = (bf16[16,2048]{1,0:T(8,128)(2,1)S(1)}, bf16[16,2048]{1,0:T(8,128)(2,1)S(1)}, u32[]{:S(2)}, u32[]{:S(2)}) collective-permute-start(bf16[16,2048]{1,0:T(8,128)(2,1)S(1)} %get-tuple-element.76.refs_0_), channel_id=1, source_target_pairs={{0,1},{1,0},{2,3},{3,2},{4,5},{5,4},{6,7},{7,6},{8,9},{9,8},{10,11... | collective-permute-start | bytes 196616 | tf_op jit(solution)/shard_map/ppermute | solution.py:27
  76.4 5.2 %collective-permute-start.25 = (bf16[16,2048]{1,0:T(8,128)(2,1)S(1)}, bf16[16,2048]{1,0:T(8,128)(2,1)S(1)}, u32[]{:S(2)}, u32[]{:S(2)}) collective-permute-start(bf16[16,2048]{1,0:T(8,128)(2,1)S(1)} %get-tuple-element.80), channel_id=1, source_target_pairs={{0,3},{1,2},{2,1},{3,0},{4,7},{5,6},{6,5},{7,4},{8,11},{9,10},{10,... | collective-permute-start | bytes 196616 | tf_op jit(solution)/shard_map/ppermute | solution.py:27
  78.0 4.4 %collective-permute-start.26 = (bf16[16,2048]{1,0:T(8,128)(2,1)S(1)}, bf16[16,2048]{1,0:T(8,128)(2,1)S(1)}, u32[]{:S(2)}, u32[]{:S(2)}) collective-permute-start(bf16[16,2048]{1,0:T(8,128)(2,1)S(1)} %get-tuple-element.81), channel_id=1, source_target_pairs={{0,1},{1,0},{2,3},{3,2},{4,5},{5,4},{6,7},{7,6},{8,9},{9,8},{10,11... | collective-permute-start | bytes 196616 | tf_op jit(solution)/shard_map/ppermute | solution.py:27
  78.8 4.3 %collective-permute-start.27 = (bf16[16,2048]{1,0:T(8,128)(2,1)S(1)}, bf16[16,2048]{1,0:T(8,128)(2,1)S(1)}, u32[]{:S(2)}, u32[]{:S(2)}) collective-permute-start(bf16[16,2048]{1,0:T(8,128)(2,1)S(1)} %get-tuple-element.82), channel_id=1, source_target_pairs={{0,2},{1,3},{2,0},{3,1},{4,6},{5,7},{6,4},{7,5},{8,10},{9,11},{10,... | collective-permute-start | bytes 196616 | tf_op jit(solution)/shard_map/ppermute | solution.py:27
  83.1 6.3 %collective-permute-start.29 = (bf16[16,2048]{1,0:T(8,128)(2,1)S(1)}, bf16[16,2048]{1,0:T(8,128)(2,1)S(1)}, u32[]{:S(2)}, u32[]{:S(2)}) collective-permute-start(bf16[16,2048]{1,0:T(8,128)(2,1)S(1)} %shard_map.106), channel_id=1, source_target_pairs={{0,12},{1,13},{2,14},{3,15},{4,8},{5,9},{6,10},{7,11},{8,20},{9,21... | collective-permute-start | bytes 196616 | tf_op jit(solution)/shard_map/ppermute | solution.py:27
  83.2 6.2 %collective-permute-start.28 = (bf16[16,2048]{1,0:T(8,128)(2,1)S(1)}, bf16[16,2048]{1,0:T(8,128)(2,1)S(1)}, u32[]{:S(2)}, u32[]{:S(2)}) collective-permute-start(bf16[16,2048]{1,0:T(8,128)(2,1)S(1)} %shard_map.106), channel_id=1, source_target_pairs={{0,8},{1,9},{2,10},{3,11},{4,12},{5,13},{6,14},{7,15},{8,16},{9,17... | collective-permute-start | bytes 196616 | tf_op jit(solution)/shard_map/ppermute | solution.py:27
  89.6 5.2 %collective-permute-start.32 = (bf16[16,2048]{1,0:T(8,128)(2,1)S(1)}, bf16[16,2048]{1,0:T(8,128)(2,1)S(1)}, u32[]{:S(2)}, u32[]{:S(2)}) collective-permute-start(bf16[16,2048]{1,0:T(8,128)(2,1)S(1)} %get-tuple-element.83.refs_0_), channel_id=1, source_target_pairs={{0,3},{1,2},{2,1},{3,0},{4,7},{5,6},{6,5},{7,4},{8,11},{9,10},{10,... | collective-permute-start | bytes 196616 | tf_op jit(solution)/shard_map/ppermute | solution.py:27
  90.6 4.6 %collective-permute-start.31 = (bf16[16,2048]{1,0:T(8,128)(2,1)S(1)}, bf16[16,2048]{1,0:T(8,128)(2,1)S(1)}, u32[]{:S(2)}, u32[]{:S(2)}) collective-permute-start(bf16[16,2048]{1,0:T(8,128)(2,1)S(1)} %get-tuple-element.83.refs_0_), channel_id=1, source_target_pairs={{0,2},{1,3},{2,0},{3,1},{4,6},{5,7},{6,4},{7,5},{8,10},{9,11},{10,... | collective-permute-start | bytes 196616 | tf_op jit(solution)/shard_map/ppermute | solution.py:27
  92.3 4.3 %collective-permute-start.30 = (bf16[16,2048]{1,0:T(8,128)(2,1)S(1)}, bf16[16,2048]{1,0:T(8,128)(2,1)S(1)}, u32[]{:S(2)}, u32[]{:S(2)}) collective-permute-start(bf16[16,2048]{1,0:T(8,128)(2,1)S(1)} %get-tuple-element.83.refs_0_), channel_id=1, source_target_pairs={{0,1},{1,0},{2,3},{3,2},{4,5},{5,4},{6,7},{7,6},{8,9},{9,8},{10,11... | collective-permute-start | bytes 196616 | tf_op jit(solution)/shard_map/ppermute | solution.py:27
  98.8 5.3 %collective-permute-start.33 = (bf16[16,2048]{1,0:T(8,128)(2,1)S(1)}, bf16[16,2048]{1,0:T(8,128)(2,1)S(1)}, u32[]{:S(2)}, u32[]{:S(2)}) collective-permute-start(bf16[16,2048]{1,0:T(8,128)(2,1)S(1)} %get-tuple-element.86), channel_id=1, source_target_pairs={{0,3},{1,2},{2,1},{3,0},{4,7},{5,6},{6,5},{7,4},{8,11},{9,10},{10,... | collective-permute-start | bytes 196616 | tf_op jit(solution)/shard_map/ppermute | solution.py:27
  99.9 4.9 %collective-permute-start.34 = (bf16[16,2048]{1,0:T(8,128)(2,1)S(1)}, bf16[16,2048]{1,0:T(8,128)(2,1)S(1)}, u32[]{:S(2)}, u32[]{:S(2)}) collective-permute-start(bf16[16,2048]{1,0:T(8,128)(2,1)S(1)} %get-tuple-element.87), channel_id=1, source_target_pairs={{0,1},{1,0},{2,3},{3,2},{4,5},{5,4},{6,7},{7,6},{8,9},{9,8},{10,11... | collective-permute-start | bytes 196616 | tf_op jit(solution)/shard_map/ppermute | solution.py:27
  100.8 4.3 %collective-permute-start.35 = (bf16[16,2048]{1,0:T(8,128)(2,1)S(1)}, bf16[16,2048]{1,0:T(8,128)(2,1)S(1)}, u32[]{:S(2)}, u32[]{:S(2)}) collective-permute-start(bf16[16,2048]{1,0:T(8,128)(2,1)S(1)} %get-tuple-element.88), channel_id=1, source_target_pairs={{0,2},{1,3},{2,0},{3,1},{4,6},{5,7},{6,4},{7,5},{8,10},{9,11},{10,... | collective-permute-start | bytes 196616 | tf_op jit(solution)/shard_map/ppermute | solution.py:27
  105.1 4.9 %collective-permute-start.36 = (bf16[8,2048]{1,0:T(8,128)(2,1)S(1)}, bf16[8,2048]{1,0:T(8,128)(2,1)S(1)}, u32[]{:S(2)}, u32[]{:S(2)}) collective-permute-start(bf16[8,2048]{1,0:T(8,128)(2,1)S(1)} %slice.17), channel_id=1, source_target_pairs={{0,4},{1,5},{2,6},{3,7},{4,0},{5,1},{6,2},{7,3},{8,12},{9,13},{10,... | collective-permute-start | bytes 98312 | tf_op jit(solution)/shard_map/ppermute | solution.py:27

commit v11 on v10

--- a/solution.py
+++ b/solution.py
@@ -232,9 +232,12 @@
 def fill_kernel(*refs, group):
     count = len(refs) // 2
     ins, outs, sems = refs[:count], refs[count:2 * count], refs[2 * count]
+    pieces = sems.shape[1]
+    rows = outs[0].shape[0] // pieces
     copies = [
-        pltpu.make_async_copy(one if group is None else one.at[group], out, sems.at[i])
+        pltpu.make_async_copy(one.at[group, pl.ds(at * rows, rows)], out.at[pl.ds(at * rows, rows)], sems.at[i, at])
         for i, (one, out) in enumerate(zip(ins, outs))
+        for at in range(pieces)
     ]
     for copy in copies:
         copy.start()
@@ -242,14 +245,15 @@
         copy.wait()
 
 
-def filled(values, group=None):
-    shapes = [value.shape if group is None else value.shape[1:] for value in values]
+def filled(values, group):
+    shapes = [value.shape[1:] for value in values]
+    pieces = 4 if shapes[0][0] % 32 == 0 else 1
     return pl.pallas_call(
         functools.partial(fill_kernel, group=group),
         out_shape=[pltpu.VMEM(shape, value.dtype) for shape, value in zip(shapes, values)],
         in_specs=[pl.BlockSpec(memory_space=pltpu.HBM)] * len(values),
         out_specs=[WHOLE] * len(values),
-        scratch_shapes=[pltpu.SemaphoreType.DMA((len(values),))],
+        scratch_shapes=[pltpu.SemaphoreType.DMA((len(values), pieces))],
         compiler_params=pltpu.CompilerParams(vmem_limit_bytes=1024 * 1024),
         name="fill",
     )(*[pltpu.with_memory_space_constraint(value, pltpu.HBM) for value in values])
@@ -304,28 +308,6 @@
     )(*[pltpu.with_memory_space_constraint(value, pltpu.HBM) for value in values])
 
 
-def stack_kernel(*refs, group):
-    ins, out, sems = refs[:-2], refs[-2], refs[-1]
-    copies = [pltpu.make_async_copy(one.at[group], out.at[i], sems.at[i]) for i, one in enumerate(ins)]
-    for copy in copies:
-        copy.start()
-    for copy in copies:
-        copy.wait()
-
-
-def stacked(values, group):
-    shape = (len(values),) + values[0].shape[1:]
-    return pl.pallas_call(
-        functools.partial(stack_kernel, group=group),
-        out_shape=pltpu.VMEM(shape, values[0].dtype),
-        in_specs=[pl.BlockSpec(memory_space=pltpu.HBM)] * len(values),
-        out_specs=WHOLE,
-        scratch_shapes=[pltpu.SemaphoreType.DMA((len(values),))],
-        compiler_params=pltpu.CompilerParams(vmem_limit_bytes=6 * 1024 * 1024),
-        name="stack",
-    )(*[pltpu.with_memory_space_constraint(value, pltpu.HBM) for value in values])
-
-
 def both_first(outer):
     return [outer - 1, *range(1, outer - 1)]
 
@@ -372,8 +354,8 @@
     slots = [loaded(weights, (True, True, False), 0)]
     if users[0]:
         slots.append(loaded(weights, (True, True, False), 1))
-    late = stacked(lax.optimization_barrier((*spare_all, arrived[both_first(outer)[-1]]))[:3], 1)
-    near = [swapped(late, users[opening])] if opening < TICKS else []
+    late = filled(lax.optimization_barrier((*spare_all, arrived[both_first(outer)[-1]]))[:3], 1)
+    near = [swapped(one, users[opening]) for one in late] if opening < TICKS else []
     own = state[0]
     before = run_layer(arrived, arrived, own, [(slot, []) for slot in slots], tick_idx=0, tok_dev=tok_dev, ends=False)
 
@@ -389,6 +371,8 @@
             carried=before if tick_idx == 0 else None,
         )
         got = [moved(parts[j], j, 0) for j in both_first(outer)]
+        if tick_idx == 0:
+            far = [moved(lax.optimization_barrier((late[0], parts[0]))[0], 0, -1)]
         if tick_idx == 0 and not users[0]:
             tied = lax.optimization_barrier((*weights, parts[0]))[:3]
             gate = loaded(tied[:1], (True,), 1)
@@ -400,11 +384,13 @@
         across = moved(total, outer, 1)
         along = moved(total, 0, 1)
         if tick_idx == 0:
-            far = [moved(lax.optimization_barrier((late, total))[0], 0, -1)]
             if not users[0]:
                 tied = lax.optimization_barrier((*weights, total))[:3]
                 slots.append(gate + loaded(tied[1:], (True, False), 1))
         own, normed = arriving(along, across, norm_gain, tick_idx + 1)
+        if tick_idx == 0:
+            later = lax.optimization_barrier((*late[1:], normed))[:2]
+            far += [moved(one, 0, -1) for one in later]
         rows = spread(normed)
 
 

time: 111 us -> 130 us (1.17)
  waiting for transfers between devices: 36.7 us -> 49.4 us
  starting transfers between devices: 49.1 us -> 55.3 us
    ppermute x36 -> x38, waiting for transfers between devices: 36.7 us -> 49.3 us  [moved(): return lax.ppermute(value, BOTH, pairs)]
    ppermute x1 -> x3, starting transfers between devices: 1.92 us -> 6.24 us  [swapped(): return lax.ppermute(value, BOTH, pairs)]
    pallas_call x2 -> x3, Pallas kernels: 2.43 us -> 4.35 us  [filled(): pl.pallas_call(functools.partial(fill_kernel, group=group), out_shape=[pl...]
    ppermute x36 -> x38, starting transfers between devices: 47.2 us -> 49.1 us  [moved(): return lax.ppermute(value, BOTH, pairs)]
    pallas_call x1 -> x0, Pallas kernels: 1.51 us -> none  [stacked(): pl.pallas_call(functools.partial(stack_kernel, group=group), out_shape=pl...]
  transfers between devices with their start and end apart: 37 -> 41, of which waited for: 26 -> 23; matrix products, arithmetic and copies ran while one was open for 0% -> 0% of each run, Pallas kernels for 16% -> 14%
where the time goes in v11:
time: 130 us
  starting transfers between devices  55.3 us (43%)
  waiting for transfers between devices  49.4 us (38%)
  Pallas kernels  24.2 us (19%)
    ppermute x38, waiting for transfers between devices, moved(): return lax.ppermute(value, BOTH, pairs)  49.3 us
    ppermute x38, starting transfers between devices, moved(): return lax.ppermute(value, BOTH, pairs)  49.1 us
    pallas_call x3, Pallas kernels, loaded(): pl.pallas_call(functools.partial(load_kernel, turned=turned, group=group)...  9.78 us
    pallas_call x5, Pallas kernels, run_layer(): pl.pallas_call(functools.partial(layer_kernel, tick_idx=tick_idx, blocks=...  9.37 us
    ppermute x3, starting transfers between devices, swapped(): return lax.ppermute(value, BOTH, pairs)  6.24 us
    pallas_call x3, Pallas kernels, filled(): pl.pallas_call(functools.partial(fill_kernel, group=group), out_shape=[pl...  4.35 us
  transfers between devices with their start and end apart: 41, of which 23 were waited for; matrix products, arithmetic and copies ran while one was open for 0% of the time, Pallas kernels for 14%

profile of v11, /device:TPU:0, one launch (start us, length us, event | category | flops | bytes accessed | tf_op | source)
XLA Modules:
  0.0 129.9 jit_solution(15093247892275332099)
XLA Ops:
  1.2 2.5 %collective-permute-start.4 = (bf16[160,2048]{1,0:T(8,128)(2,1)S(1)}, bf16[160,2048]{1,0:T(8,128)(2,1)S(1)}, u32[]{:S(2)}, u32[]{:S(2)}) collective-permute-start(bf16[160,2048]{1,0:T(8,128)(2,1)S(1)} %fill.3), channel_id=1, source_target_pairs={{0,24},{1,25},{2,26},{3,27},{4,28},{5,29},{6,30},{7,31},{8,0},{9,1... | collective-permute-start | bytes 1966088 | tf_op jit(solution)/shard_map/ppermute | solution.py:27
  3.7 1.5 %fill.4 = (bf16[160,2048]{1,0:T(8,128)(2,1)S(1)}, bf16[160,2048]{1,0:T(8,128)(2,1)S(1)}) custom-call(bf16[2,160,2048]{2,1,0:T(8,128)(2,1)} %bitcast.26, bf16[2,160,2048]{2,1,0:T(8,128)(2,1)} %bitcast.28), custom_call_target="tpu_custom_call" | custom-call | tf_op jit(solution)/shard_map/fill/pallas_call | solution.py:251
  6.3 2.6 %collective-permute-start = (bf16[8,2176]{1,0:T(8,128)(2,1)S(1)}, bf16[8,2176]{1,0:T(8,128)(2,1)S(1)}, u32[]{:S(2)}, u32[]{:S(2)}) collective-permute-start(bf16[8,2176]{1,0:T(8,128)(2,1)S(1)} %shard_map.100.first_ref), channel_id=1, source_target_pairs={{0,4},{1,5},{2,6},{3,7},{4,0},{5,1},{6,2},{7,3},{8,12},{9,13},{10,... | collective-permute-start | bytes 104456 | tf_op jit(solution)/shard_map/ppermute | solution.py:27
  8.9 2.2 %collective-permute-done.second_ref = bf16[8,2176]{1,0:T(8,128)(2,1)S(1)} collective-permute-done((bf16[8,2176]{1,0:T(8,128)(2,1)S(1)}, bf16[8,2176]{1,0:T(8,128)(2,1)S(1)}, u32[]{:S(2)}, u32[]{:S(2)}) %collective-permute-start) | collective-permute-done | bytes 34848 | tf_op jit(solution)/shard_map/ppermute | solution.py:27
  11.1 1.6 %collective-permute-start.2 = (bf16[16,2176]{1,0:T(8,128)(2,1)S(1)}, bf16[16,2176]{1,0:T(8,128)(2,1)S(1)}, u32[]{:S(2)}, u32[]{:S(2)}) collective-permute-start(bf16[16,2176]{1,0:T(8,128)(2,1)S(1)} %shard_map.101.refs_0_.refs_4_), channel_id=1, source_target_pairs={{0,2},{1,3},{2,0},{3,1},{4,6},{5,7},{6,4},{7,5},{8,10},{9,11},{10,... | collective-permute-start | bytes 208904 | tf_op jit(solution)/shard_map/ppermute | solution.py:27
  12.8 1.4 %collective-permute-start.3 = (bf16[16,2176]{1,0:T(8,128)(2,1)S(1)}, bf16[16,2176]{1,0:T(8,128)(2,1)S(1)}, u32[]{:S(2)}, u32[]{:S(2)}) collective-permute-start(bf16[16,2176]{1,0:T(8,128)(2,1)S(1)} %shard_map.101.refs_0_.refs_4_), channel_id=1, source_target_pairs={{0,3},{1,2},{2,1},{3,0},{4,7},{5,6},{6,5},{7,4},{8,11},{9,10},{10,... | collective-permute-start | bytes 208904 | tf_op jit(solution)/shard_map/ppermute | solution.py:27
  14.2 1.4 %collective-permute-done.2.refs_2_.refs_6_ = bf16[16,2176]{1,0:T(8,128)(2,1)S(1)} collective-permute-done((bf16[16,2176]{1,0:T(8,128)(2,1)S(1)}, bf16[16,2176]{1,0:T(8,128)(2,1)S(1)}, u32[]{:S(2)}, u32[]{:S(2)}) %collective-permute-start.2) | collective-permute-done | bytes 69664 | tf_op jit(solution)/shard_map/ppermute | solution.py:27
  15.5 1.7 %fill.5 = (bf16[160,2048]{1,0:T(8,128)(2,1)S(1)}, bf16[160,2048]{1,0:T(8,128)(2,1)S(1)}, bf16[160,2048]{1,0:T(8,128)(2,1)S(1)}) custom-call(bf16[2,160,2048]{2,1,0:T(8,128)(2,1)} %bitcast.31, bf16[2,160,2048]{2,1,0:T(8,128)(2,1)} %bitcast.27, bf16[2,160,2048]{2,1,0:T(8,128)(2,1)} %bitcast.29), custom_call_target="tpu_custom_call" | custom-call | tf_op jit(solution)/shard_map/fill/pallas_call | solution.py:251
  17.2 1.9 %collective-permute-start.15 = (bf16[160,2048]{1,0:T(8,128)(2,1)S(1)}, bf16[160,2048]{1,0:T(8,128)(2,1)S(1)}, u32[]{:S(2)}, u32[]{:S(2)}) collective-permute-start(bf16[160,2048]{1,0:T(8,128)(2,1)S(1)} %get-tuple-element.86), channel_id=1, source_target_pairs={{0,8},{1,9},{2,10},{3,11},{4,12},{5,13},{6,14},{7,15},{8,0},{9,1},... | collective-permute-start | bytes 1966088 | tf_op jit(solution)/shard_map/ppermute | solution.py:58
  19.1 2.1 %collective-permute-start.1 = (bf16[16,2176]{1,0:T(8,128)(2,1)S(1)}, bf16[16,2176]{1,0:T(8,128)(2,1)S(1)}, u32[]{:S(2)}, u32[]{:S(2)}) collective-permute-start(bf16[16,2176]{1,0:T(8,128)(2,1)S(1)} %shard_map.101.refs_0_.refs_4_), channel_id=1, source_target_pairs={{0,1},{1,0},{2,3},{3,2},{4,5},{5,4},{6,7},{7,6},{8,9},{9,8},{10,11... | collective-permute-start | bytes 208904 | tf_op jit(solution)/shard_map/ppermute | solution.py:27
  21.3 2.8 %collective-permute-done.1.refs_1_.refs_5_ = bf16[16,2176]{1,0:T(8,128)(2,1)S(1)} collective-permute-done((bf16[16,2176]{1,0:T(8,128)(2,1)S(1)}, bf16[16,2176]{1,0:T(8,128)(2,1)S(1)}, u32[]{:S(2)}, u32[]{:S(2)}) %collective-permute-start.1) | collective-permute-done | bytes 69664 | tf_op jit(solution)/shard_map/ppermute | solution.py:27
  24.1 1.9 %collective-permute-start.16 = (bf16[160,2048]{1,0:T(8,128)(2,1)S(1)}, bf16[160,2048]{1,0:T(8,128)(2,1)S(1)}, u32[]{:S(2)}, u32[]{:S(2)}) collective-permute-start(bf16[160,2048]{1,0:T(8,128)(2,1)S(1)} %get-tuple-element.87), channel_id=1, source_target_pairs={{0,8},{1,9},{2,10},{3,11},{4,12},{5,13},{6,14},{7,15},{8,0},{9,1},... | collective-permute-start | bytes 1966088 | tf_op jit(solution)/shard_map/ppermute | solution.py:58
  26.0 2.4 %collective-permute-start.17 = (bf16[160,2048]{1,0:T(8,128)(2,1)S(1)}, bf16[160,2048]{1,0:T(8,128)(2,1)S(1)}, u32[]{:S(2)}, u32[]{:S(2)}) collective-permute-start(bf16[160,2048]{1,0:T(8,128)(2,1)S(1)} %get-tuple-element.88), channel_id=1, source_target_pairs={{0,8},{1,9},{2,10},{3,11},{4,12},{5,13},{6,14},{7,15},{8,0},{9,1},... | collective-permute-start | bytes 1966088 | tf_op jit(solution)/shard_map/ppermute | solution.py:58
  28.4 4.4 %load.3 = (bf16[2048,640]{1,0:T(8,128)(2,1)S(1)}, bf16[2048,640]{1,0:T(8,128)(2,1)S(1)}, bf16[640,2048]{1,0:T(8,128)(2,1)S(1)}) custom-call(bf16[2,640,2048]{2,1,0:T(8,128)(2,1)} %bitcast.24, bf16[2,640,2048]{2,1,0:T(8,128)(2,1)} %bitcast.20, bf16[2,640,2048]{2,1,0:T(8,128)(2,1)} %bitcast.22), custom_call_target="tpu_custom_call" | custom-call | tf_op jit(solution)/shard_map/load/pallas_call | solution.py:293
  32.8 1.5 %layer.5.refs_9_ = f32[64,2048]{1,0:T(8,128)S(1)} custom-call(bf16[16,2176]{1,0:T(8,128)(2,1)S(1)} %shard_map.101.refs_0_.refs_4_, bf16[16,2176]{1,0:T(8,128)(2,1)S(1)} %collective-permute-done.1.refs_1_.refs_5_, bf16[16,2176]{1,0:T(8,128)(2,1)S(1)} %collective-permute-done.2.refs_2_.refs_6_, bf16[16,2176]{1,0:T(8,128)(2,1)S(1)} %collective-permute-done.3.refs_3_.refs_7_, ...), custom_call_target="tpu_custom_call" | custom-call | flops 503316480 | bytes 7864320 | tf_op jit(solution)/shard_map/layer/pallas_call | solution.py:191
  35.2 2.3 %collective-permute-start.7 = (bf16[16,2048]{1,0:T(8,128)(2,1)S(1)}, bf16[16,2048]{1,0:T(8,128)(2,1)S(1)}, u32[]{:S(2)}, u32[]{:S(2)}) collective-permute-start(bf16[16,2048]{1,0:T(8,128)(2,1)S(1)} %get-tuple-element.64), channel_id=1, source_target_pairs={{0,3},{1,2},{2,1},{3,0},{4,7},{5,6},{6,5},{7,4},{8,11},{9,10},{10,... | collective-permute-start | bytes 196616 | tf_op jit(solution)/shard_map/ppermute | solution.py:27
  38.3 2.2 %collective-permute-done.7.refs_1_ = bf16[16,2048]{1,0:T(8,128)(2,1)S(1)} collective-permute-done((bf16[16,2048]{1,0:T(8,128)(2,1)S(1)}, bf16[16,2048]{1,0:T(8,128)(2,1)S(1)}, u32[]{:S(2)}, u32[]{:S(2)}) %collective-permute-start.7) | collective-permute-done | bytes 65568 | tf_op jit(solution)/shard_map/ppermute | solution.py:27
  40.5 1.5 %collective-permute-start.9 = (bf16[16,2048]{1,0:T(8,128)(2,1)S(1)}, bf16[16,2048]{1,0:T(8,128)(2,1)S(1)}, u32[]{:S(2)}, u32[]{:S(2)}) collective-permute-start(bf16[16,2048]{1,0:T(8,128)(2,1)S(1)} %get-tuple-element.66), channel_id=1, source_target_pairs={{0,2},{1,3},{2,0},{3,1},{4,6},{5,7},{6,4},{7,5},{8,10},{9,11},{10,... | collective-permute-start | bytes 196616 | tf_op jit(solution)/shard_map/ppermute | solution.py:27
  42.0 2.8 %collective-permute-done.9.refs_3_ = bf16[16,2048]{1,0:T(8,128)(2,1)S(1)} collective-permute-done((bf16[16,2048]{1,0:T(8,128)(2,1)S(1)}, bf16[16,2048]{1,0:T(8,128)(2,1)S(1)}, u32[]{:S(2)}, u32[]{:S(2)}) %collective-permute-start.9) | collective-permute-done | bytes 65568 | tf_op jit(solution)/shard_map/ppermute | solution.py:27
  45.5 4.8 %collective-permute-done.11.across_ref = bf16[16,2048]{1,0:T(8,128)(2,1)S(1)} collective-permute-done((bf16[16,2048]{1,0:T(8,128)(2,1)S(1)}, bf16[16,2048]{1,0:T(8,128)(2,1)S(1)}, u32[]{:S(2)}, u32[]{:S(2)}) %collective-permute-start.11) | collective-permute-done | bytes 65568 | tf_op jit(solution)/shard_map/ppermute | solution.py:27
  52.1 2.4 %collective-permute-start.14 = (bf16[16,2048]{1,0:T(8,128)(2,1)S(1)}, bf16[16,2048]{1,0:T(8,128)(2,1)S(1)}, u32[]{:S(2)}, u32[]{:S(2)}) collective-permute-start(bf16[16,2048]{1,0:T(8,128)(2,1)S(1)} %get-tuple-element.67.refs_0_), channel_id=1, source_target_pairs={{0,3},{1,2},{2,1},{3,0},{4,7},{5,6},{6,5},{7,4},{8,11},{9,10},{10,... | collective-permute-start | bytes 196616 | tf_op jit(solution)/shard_map/ppermute | solution.py:27
  54.8 2.8 %collective-permute-done.14.refs_3_ = bf16[16,2048]{1,0:T(8,128)(2,1)S(1)} collective-permute-done((bf16[16,2048]{1,0:T(8,128)(2,1)S(1)}, bf16[16,2048]{1,0:T(8,128)(2,1)S(1)}, u32[]{:S(2)}, u32[]{:S(2)}) %collective-permute-start.14) | collective-permute-done | bytes 65568 | tf_op jit(solution)/shard_map/ppermute | solution.py:27
  58.8 2.5 %load.4.refs_15_ = bf16[2048,640]{1,0:T(8,128)(2,1)S(1)} custom-call(bf16[2,640,2048]{2,1,0:T(8,128)(2,1)} %bitcast.25), custom_call_target="tpu_custom_call" | custom-call | tf_op jit(solution)/shard_map/load/pallas_call | solution.py:293
  61.3 2.9 %load.5 = (bf16[2048,640]{1,0:T(8,128)(2,1)S(1)}, bf16[640,2048]{1,0:T(8,128)(2,1)S(1)}) custom-call(bf16[2,640,2048]{2,1,0:T(8,128)(2,1)} %bitcast.21, bf16[2,640,2048]{2,1,0:T(8,128)(2,1)} %bitcast.23), custom_call_target="tpu_custom_call" | custom-call | tf_op jit(solution)/shard_map/load/pallas_call | solution.py:293
  64.3 2.3 %layer.7 = (f32[16,2048]{1,0:T(8,128)S(1)}, bf16[16,2048]{1,0:T(8,128)(2,1)S(1)}, bf16[16,2048]{1,0:T(8,128)(2,1)S(1)}, bf16[16,2048]{1,0:T(8,128)(2,1)S(1)}) custom-call(bf16[16,2048]{1,0:T(8,128)(2,1)S(1)} %get-tuple-element.67.refs_0_, bf16[16,2048]{1,0:T(8,128)(2,1)S(1)} %collective-permute-done.12.refs_1_, ...), custom_call_target="tpu_custom_call" | custom-call | flops 629145600 | bytes 9830400 | tf_op jit(solution)/shard_map/layer/pallas_call | solution.py:191
  66.6 2.1 %collective-permute-start.18 = (bf16[16,2048]{1,0:T(8,128)(2,1)S(1)}, bf16[16,2048]{1,0:T(8,128)(2,1)S(1)}, u32[]{:S(2)}, u32[]{:S(2)}) collective-permute-start(bf16[16,2048]{1,0:T(8,128)(2,1)S(1)} %get-tuple-element.81), channel_id=1, source_target_pairs={{0,3},{1,2},{2,1},{3,0},{4,7},{5,6},{6,5},{7,4},{8,11},{9,10},{10,... | collective-permute-start | bytes 196616 | tf_op jit(solution)/shard_map/ppermute | solution.py:27
  69.9 2.0 %collective-permute-done.18.refs_1_ = bf16[16,2048]{1,0:T(8,128)(2,1)S(1)} collective-permute-done((bf16[16,2048]{1,0:T(8,128)(2,1)S(1)}, bf16[16,2048]{1,0:T(8,128)(2,1)S(1)}, u32[]{:S(2)}, u32[]{:S(2)}) %collective-permute-start.18) | collective-permute-done | bytes 65568 | tf_op jit(solution)/shard_map/ppermute | solution.py:27
  71.9 1.8 %collective-permute-start.20 = (bf16[16,2048]{1,0:T(8,128)(2,1)S(1)}, bf16[16,2048]{1,0:T(8,128)(2,1)S(1)}, u32[]{:S(2)}, u32[]{:S(2)}) collective-permute-start(bf16[16,2048]{1,0:T(8,128)(2,1)S(1)} %get-tuple-element.83), channel_id=1, source_target_pairs={{0,2},{1,3},{2,0},{3,1},{4,6},{5,7},{6,4},{7,5},{8,10},{9,11},{10,... | collective-permute-start | bytes 196616 | tf_op jit(solution)/shard_map/ppermute | solution.py:27
  73.8 2.4 %collective-permute-done.20.refs_3_ = bf16[16,2048]{1,0:T(8,128)(2,1)S(1)} collective-permute-done((bf16[16,2048]{1,0:T(8,128)(2,1)S(1)}, bf16[16,2048]{1,0:T(8,128)(2,1)S(1)}, u32[]{:S(2)}, u32[]{:S(2)}) %collective-permute-start.20) | collective-permute-done | bytes 65568 | tf_op jit(solution)/shard_map/ppermute | solution.py:27
  76.3 3.6 %collective-permute-start.21 = (bf16[16,2048]{1,0:T(8,128)(2,1)S(1)}, bf16[16,2048]{1,0:T(8,128)(2,1)S(1)}, u32[]{:S(2)}, u32[]{:S(2)}) collective-permute-start(bf16[16,2048]{1,0:T(8,128)(2,1)S(1)} %shard_map.104), channel_id=1, source_target_pairs={{0,8},{1,9},{2,10},{3,11},{4,12},{5,13},{6,14},{7,15},{8,16},{9,17... | collective-permute-start | bytes 196616 | tf_op jit(solution)/shard_map/ppermute | solution.py:27
  79.9 2.4 %collective-permute-done.22.across_ref = bf16[16,2048]{1,0:T(8,128)(2,1)S(1)} collective-permute-done((bf16[16,2048]{1,0:T(8,128)(2,1)S(1)}, bf16[16,2048]{1,0:T(8,128)(2,1)S(1)}, u32[]{:S(2)}, u32[]{:S(2)}) %collective-permute-start.22) | collective-permute-done | bytes 65568 | tf_op jit(solution)/shard_map/ppermute | solution.py:27
  82.4 2.1 %collective-permute-start.25 = (bf16[16,2048]{1,0:T(8,128)(2,1)S(1)}, bf16[16,2048]{1,0:T(8,128)(2,1)S(1)}, u32[]{:S(2)}, u32[]{:S(2)}) collective-permute-start(bf16[16,2048]{1,0:T(8,128)(2,1)S(1)} %get-tuple-element.84.refs_0_), channel_id=1, source_target_pairs={{0,3},{1,2},{2,1},{3,0},{4,7},{5,6},{6,5},{7,4},{8,11},{9,10},{10,... | collective-permute-start | bytes 196616 | tf_op jit(solution)/shard_map/ppermute | solution.py:27
  84.5 3.5 %collective-permute-done.25.refs_3_ = bf16[16,2048]{1,0:T(8,128)(2,1)S(1)} collective-permute-done((bf16[16,2048]{1,0:T(8,128)(2,1)S(1)}, bf16[16,2048]{1,0:T(8,128)(2,1)S(1)}, u32[]{:S(2)}, u32[]{:S(2)}) %collective-permute-start.25) | collective-permute-done | bytes 65568 | tf_op jit(solution)/shard_map/ppermute | solution.py:27
  88.8 3.5 %collective-permute-done.23.refs_1_ = bf16[16,2048]{1,0:T(8,128)(2,1)S(1)} collective-permute-done((bf16[16,2048]{1,0:T(8,128)(2,1)S(1)}, bf16[16,2048]{1,0:T(8,128)(2,1)S(1)}, u32[]{:S(2)}, u32[]{:S(2)}) %collective-permute-start.23) | collective-permute-done | bytes 65568 | tf_op jit(solution)/shard_map/ppermute | solution.py:27
  92.3 2.4 %layer.8 = (f32[16,2048]{1,0:T(8,128)S(1)}, bf16[16,2048]{1,0:T(8,128)(2,1)S(1)}, bf16[16,2048]{1,0:T(8,128)(2,1)S(1)}, bf16[16,2048]{1,0:T(8,128)(2,1)S(1)}) custom-call(bf16[16,2048]{1,0:T(8,128)(2,1)S(1)} %get-tuple-element.84.refs_0_, bf16[16,2048]{1,0:T(8,128)(2,1)S(1)} %collective-permute-done.23.refs_1_, ...), custom_call_target="tpu_custom_call" | custom-call | flops 629145600 | bytes 9830400 | tf_op jit(solution)/shard_map/layer/pallas_call | solution.py:191
  94.8 1.7 %collective-permute-start.29 = (bf16[16,2048]{1,0:T(8,128)(2,1)S(1)}, bf16[16,2048]{1,0:T(8,128)(2,1)S(1)}, u32[]{:S(2)}, u32[]{:S(2)}) collective-permute-start(bf16[16,2048]{1,0:T(8,128)(2,1)S(1)} %get-tuple-element.90), channel_id=1, source_target_pairs={{0,3},{1,2},{2,1},{3,0},{4,7},{5,6},{6,5},{7,4},{8,11},{9,10},{10,... | collective-permute-start | bytes 196616 | tf_op jit(solution)/shard_map/ppermute | solution.py:27
  96.5 1.3 %collective-permute-start.30 = (bf16[16,2048]{1,0:T(8,128)(2,1)S(1)}, bf16[16,2048]{1,0:T(8,128)(2,1)S(1)}, u32[]{:S(2)}, u32[]{:S(2)}) collective-permute-start(bf16[16,2048]{1,0:T(8,128)(2,1)S(1)} %get-tuple-element.91), channel_id=1, source_target_pairs={{0,1},{1,0},{2,3},{3,2},{4,5},{5,4},{6,7},{7,6},{8,9},{9,8},{10,11... | collective-permute-start | bytes 196616 | tf_op jit(solution)/shard_map/ppermute | solution.py:27
  98.3 1.7 %collective-permute-done.29.refs_1_ = bf16[16,2048]{1,0:T(8,128)(2,1)S(1)} collective-permute-done((bf16[16,2048]{1,0:T(8,128)(2,1)S(1)}, bf16[16,2048]{1,0:T(8,128)(2,1)S(1)}, u32[]{:S(2)}, u32[]{:S(2)}) %collective-permute-start.29) | collective-permute-done | bytes 65568 | tf_op jit(solution)/shard_map/ppermute | solution.py:27
  102.2 3.3 %collective-permute-start.32 = (bf16[16,2048]{1,0:T(8,128)(2,1)S(1)}, bf16[16,2048]{1,0:T(8,128)(2,1)S(1)}, u32[]{:S(2)}, u32[]{:S(2)}) collective-permute-start(bf16[16,2048]{1,0:T(8,128)(2,1)S(1)} %shard_map.106), channel_id=1, source_target_pairs={{0,8},{1,9},{2,10},{3,11},{4,12},{5,13},{6,14},{7,15},{8,16},{9,17... | collective-permute-start | bytes 196616 | tf_op jit(solution)/shard_map/ppermute | solution.py:27
  105.5 4.1 %collective-permute-done.33.across_ref = bf16[16,2048]{1,0:T(8,128)(2,1)S(1)} collective-permute-done((bf16[16,2048]{1,0:T(8,128)(2,1)S(1)}, bf16[16,2048]{1,0:T(8,128)(2,1)S(1)}, u32[]{:S(2)}, u32[]{:S(2)}) %collective-permute-start.33) | collective-permute-done | bytes 65568 | tf_op jit(solution)/shard_map/ppermute | solution.py:27
  109.8 1.9 %collective-permute-start.35 = (bf16[16,2048]{1,0:T(8,128)(2,1)S(1)}, bf16[16,2048]{1,0:T(8,128)(2,1)S(1)}, u32[]{:S(2)}, u32[]{:S(2)}) collective-permute-start(bf16[16,2048]{1,0:T(8,128)(2,1)S(1)} %get-tuple-element.93.refs_0_), channel_id=1, source_target_pairs={{0,2},{1,3},{2,0},{3,1},{4,6},{5,7},{6,4},{7,5},{8,10},{9,11},{10,... | collective-permute-start | bytes 196616 | tf_op jit(solution)/shard_map/ppermute | solution.py:27
  111.8 1.5 %collective-permute-start.34 = (bf16[16,2048]{1,0:T(8,128)(2,1)S(1)}, bf16[16,2048]{1,0:T(8,128)(2,1)S(1)}, u32[]{:S(2)}, u32[]{:S(2)}) collective-permute-start(bf16[16,2048]{1,0:T(8,128)(2,1)S(1)} %get-tuple-element.93.refs_0_), channel_id=1, source_target_pairs={{0,1},{1,0},{2,3},{3,2},{4,5},{5,4},{6,7},{7,6},{8,9},{9,8},{10,11... | collective-permute-start | bytes 196616 | tf_op jit(solution)/shard_map/ppermute | solution.py:27
  113.3 1.7 %collective-permute-done.36.refs_3_ = bf16[16,2048]{1,0:T(8,128)(2,1)S(1)} collective-permute-done((bf16[16,2048]{1,0:T(8,128)(2,1)S(1)}, bf16[16,2048]{1,0:T(8,128)(2,1)S(1)}, u32[]{:S(2)}, u32[]{:S(2)}) %collective-permute-start.36) | collective-permute-done | bytes 65568 | tf_op jit(solution)/shard_map/ppermute | solution.py:27
  116.0 2.3 %layer.9 = (f32[16,2048]{1,0:T(8,128)S(1)}, bf16[16,2048]{1,0:T(8,128)(2,1)S(1)}, bf16[16,2048]{1,0:T(8,128)(2,1)S(1)}, bf16[16,2048]{1,0:T(8,128)(2,1)S(1)}) custom-call(bf16[16,2048]{1,0:T(8,128)(2,1)S(1)} %get-tuple-element.93.refs_0_, bf16[16,2048]{1,0:T(8,128)(2,1)S(1)} %collective-permute-done.34.refs_1_, ...), custom_call_target="tpu_custom_call" | custom-call | flops 629145600 | bytes 9830400 | tf_op jit(solution)/shard_map/layer/pallas_call | solution.py:191
  120.0 1.9 %collective-permute-start.39 = (bf16[16,2048]{1,0:T(8,128)(2,1)S(1)}, bf16[16,2048]{1,0:T(8,128)(2,1)S(1)}, u32[]{:S(2)}, u32[]{:S(2)}) collective-permute-start(bf16[16,2048]{1,0:T(8,128)(2,1)S(1)} %get-tuple-element.98), channel_id=1, source_target_pairs={{0,2},{1,3},{2,0},{3,1},{4,6},{5,7},{6,4},{7,5},{8,10},{9,11},{10,... | collective-permute-start | bytes 196616 | tf_op jit(solution)/shard_map/ppermute | solution.py:27
  121.9 2.0 %collective-permute-done.37 = bf16[16,2048]{1,0:T(8,128)(2,1)S(1)} collective-permute-done((bf16[16,2048]{1,0:T(8,128)(2,1)S(1)}, bf16[16,2048]{1,0:T(8,128)(2,1)S(1)}, u32[]{:S(2)}, u32[]{:S(2)}) %collective-permute-start.37) | collective-permute-done | bytes 65568 | tf_op jit(solution)/shard_map/ppermute | solution.py:27
  124.4 2.2 %collective-permute-start.40 = (bf16[8,2048]{1,0:T(8,128)(2,1)S(1)}, bf16[8,2048]{1,0:T(8,128)(2,1)S(1)}, u32[]{:S(2)}, u32[]{:S(2)}) collective-permute-start(bf16[8,2048]{1,0:T(8,128)(2,1)S(1)} %slice.17), channel_id=1, source_target_pairs={{0,4},{1,5},{2,6},{3,7},{4,0},{5,1},{6,2},{7,3},{8,12},{9,13},{10,... | collective-permute-start | bytes 98312 | tf_op jit(solution)/shard_map/ppermute | solution.py:27
  126.5 2.7 %collective-permute-done.40 = bf16[8,2048]{1,0:T(8,128)(2,1)S(1)} collective-permute-done((bf16[8,2048]{1,0:T(8,128)(2,1)S(1)}, bf16[8,2048]{1,0:T(8,128)(2,1)S(1)}, u32[]{:S(2)}, u32[]{:S(2)}) %collective-permute-start.40) | collective-permute-done | bytes 32800 | tf_op jit(solution)/shard_map/ppermute | solution.py:27
  (64 shorter events, 16.9 us)
Async XLA Ops:
  0.0 6.0 %copy-start.3 = (f32[4,1,8,2]{2,3,1,0:T(2,128)S(1)}, f32[4,1,8,2]{2,3,1,0:T(2,128)}, u32[]{:S(2)}) copy-start(f32[4,1,8,2]{2,3,1,0:T(2,128)} %param.12) | copy-start | bytes 772
  0.0 6.0 %copy-start.2 = (s32[4,1,8,2]{2,3,1,0:T(2,128)S(1)}, s32[4,1,8,2]{2,3,1,0:T(2,128)}, u32[]{:S(2)}) copy-start(s32[4,1,8,2]{2,3,1,0:T(2,128)} %param.11) | copy-start | bytes 772
  0.0 6.0 %copy-start = (bf16[1,8,2048]{2,1,0:T(8,128)(2,1)S(1)}, bf16[1,8,2048]{2,1,0:T(8,128)(2,1)}, u32[]{:S(2)}) copy-start(bf16[1,8,2048]{2,1,0:T(8,128)(2,1)} %param.10) | copy-start | bytes 98308
  0.0 6.0 %copy-start.1 = (f32[2,1,2048]{2,1,0:T(1,128)S(1)}, f32[2,1,2048]{2,1,0:T(1,128)}, u32[]{:S(2)}) copy-start(f32[2,1,2048]{2,1,0:T(1,128)} %gain_ref.7) | copy-start | bytes 49156
  1.2 24.8 %collective-permute-start.4 = (bf16[160,2048]{1,0:T(8,128)(2,1)S(1)}, bf16[160,2048]{1,0:T(8,128)(2,1)S(1)}, u32[]{:S(2)}, u32[]{:S(2)}) collective-permute-start(bf16[160,2048]{1,0:T(8,128)(2,1)S(1)} %fill.3), channel_id=1, source_target_pairs={{0,24},{1,25},{2,26},{3,27},{4,28},{5,29},{6,30},{7,31},{8,0},{9,1... | collective-permute-start | bytes 1966088 | tf_op jit(solution)/shard_map/ppermute | solution.py:27
  5.2 29.1 %collective-permute-start.5 = (bf16[160,2048]{1,0:T(8,128)(2,1)S(1)}, bf16[160,2048]{1,0:T(8,128)(2,1)S(1)}, u32[]{:S(2)}, u32[]{:S(2)}) collective-permute-start(bf16[160,2048]{1,0:T(8,128)(2,1)S(1)} %get-tuple-element.61), channel_id=1, source_target_pairs={{0,24},{1,25},{2,26},{3,27},{4,28},{5,29},{6,30},{7,31},{8,0},{9,1... | collective-permute-start | bytes 1966088 | tf_op jit(solution)/shard_map/ppermute | solution.py:27
  5.9 28.4 %collective-permute-start.6 = (bf16[160,2048]{1,0:T(8,128)(2,1)S(1)}, bf16[160,2048]{1,0:T(8,128)(2,1)S(1)}, u32[]{:S(2)}, u32[]{:S(2)}) collective-permute-start(bf16[160,2048]{1,0:T(8,128)(2,1)S(1)} %get-tuple-element.62), channel_id=1, source_target_pairs={{0,24},{1,25},{2,26},{3,27},{4,28},{5,29},{6,30},{7,31},{8,0},{9,1... | collective-permute-start | bytes 1966088 | tf_op jit(solution)/shard_map/ppermute | solution.py:27
  6.3 4.9 %collective-permute-start = (bf16[8,2176]{1,0:T(8,128)(2,1)S(1)}, bf16[8,2176]{1,0:T(8,128)(2,1)S(1)}, u32[]{:S(2)}, u32[]{:S(2)}) collective-permute-start(bf16[8,2176]{1,0:T(8,128)(2,1)S(1)} %shard_map.100.first_ref), channel_id=1, source_target_pairs={{0,4},{1,5},{2,6},{3,7},{4,0},{5,1},{6,2},{7,3},{8,12},{9,13},{10,... | collective-permute-start | bytes 104456 | tf_op jit(solution)/shard_map/ppermute | solution.py:27
  11.1 4.4 %collective-permute-start.2 = (bf16[16,2176]{1,0:T(8,128)(2,1)S(1)}, bf16[16,2176]{1,0:T(8,128)(2,1)S(1)}, u32[]{:S(2)}, u32[]{:S(2)}) collective-permute-start(bf16[16,2176]{1,0:T(8,128)(2,1)S(1)} %shard_map.101.refs_0_.refs_4_), channel_id=1, source_target_pairs={{0,2},{1,3},{2,0},{3,1},{4,6},{5,7},{6,4},{7,5},{8,10},{9,11},{10,... | collective-permute-start | bytes 208904 | tf_op jit(solution)/shard_map/ppermute | solution.py:27
  12.8 6.4 %collective-permute-start.3 = (bf16[16,2176]{1,0:T(8,128)(2,1)S(1)}, bf16[16,2176]{1,0:T(8,128)(2,1)S(1)}, u32[]{:S(2)}, u32[]{:S(2)}) collective-permute-start(bf16[16,2176]{1,0:T(8,128)(2,1)S(1)} %shard_map.101.refs_0_.refs_4_), channel_id=1, source_target_pairs={{0,3},{1,2},{2,1},{3,0},{4,7},{5,6},{6,5},{7,4},{8,11},{9,10},{10,... | collective-permute-start | bytes 208904 | tf_op jit(solution)/shard_map/ppermute | solution.py:27
  17.2 34.0 %collective-permute-start.15 = (bf16[160,2048]{1,0:T(8,128)(2,1)S(1)}, bf16[160,2048]{1,0:T(8,128)(2,1)S(1)}, u32[]{:S(2)}, u32[]{:S(2)}) collective-permute-start(bf16[160,2048]{1,0:T(8,128)(2,1)S(1)} %get-tuple-element.86), channel_id=1, source_target_pairs={{0,8},{1,9},{2,10},{3,11},{4,12},{5,13},{6,14},{7,15},{8,0},{9,1},... | collective-permute-start | bytes 1966088 | tf_op jit(solution)/shard_map/ppermute | solution.py:58
  19.1 5.0 %collective-permute-start.1 = (bf16[16,2176]{1,0:T(8,128)(2,1)S(1)}, bf16[16,2176]{1,0:T(8,128)(2,1)S(1)}, u32[]{:S(2)}, u32[]{:S(2)}) collective-permute-start(bf16[16,2176]{1,0:T(8,128)(2,1)S(1)} %shard_map.101.refs_0_.refs_4_), channel_id=1, source_target_pairs={{0,1},{1,0},{2,3},{3,2},{4,5},{5,4},{6,7},{7,6},{8,9},{9,8},{10,11... | collective-permute-start | bytes 208904 | tf_op jit(solution)/shard_map/ppermute | solution.py:27
  24.1 28.0 %collective-permute-start.16 = (bf16[160,2048]{1,0:T(8,128)(2,1)S(1)}, bf16[160,2048]{1,0:T(8,128)(2,1)S(1)}, u32[]{:S(2)}, u32[]{:S(2)}) collective-permute-start(bf16[160,2048]{1,0:T(8,128)(2,1)S(1)} %get-tuple-element.87), channel_id=1, source_target_pairs={{0,8},{1,9},{2,10},{3,11},{4,12},{5,13},{6,14},{7,15},{8,0},{9,1},... | collective-permute-start | bytes 1966088 | tf_op jit(solution)/shard_map/ppermute | solution.py:58
  26.0 28.5 %collective-permute-start.17 = (bf16[160,2048]{1,0:T(8,128)(2,1)S(1)}, bf16[160,2048]{1,0:T(8,128)(2,1)S(1)}, u32[]{:S(2)}, u32[]{:S(2)}) collective-permute-start(bf16[160,2048]{1,0:T(8,128)(2,1)S(1)} %get-tuple-element.88), channel_id=1, source_target_pairs={{0,8},{1,9},{2,10},{3,11},{4,12},{5,13},{6,14},{7,15},{8,0},{9,1},... | collective-permute-start | bytes 1966088 | tf_op jit(solution)/shard_map/ppermute | solution.py:58
  35.2 5.3 %collective-permute-start.7 = (bf16[16,2048]{1,0:T(8,128)(2,1)S(1)}, bf16[16,2048]{1,0:T(8,128)(2,1)S(1)}, u32[]{:S(2)}, u32[]{:S(2)}) collective-permute-start(bf16[16,2048]{1,0:T(8,128)(2,1)S(1)} %get-tuple-element.64), channel_id=1, source_target_pairs={{0,3},{1,2},{2,1},{3,0},{4,7},{5,6},{6,5},{7,4},{8,11},{9,10},{10,... | collective-permute-start | bytes 196616 | tf_op jit(solution)/shard_map/ppermute | solution.py:27
  37.5 4.5 %collective-permute-start.8 = (bf16[16,2048]{1,0:T(8,128)(2,1)S(1)}, bf16[16,2048]{1,0:T(8,128)(2,1)S(1)}, u32[]{:S(2)}, u32[]{:S(2)}) collective-permute-start(bf16[16,2048]{1,0:T(8,128)(2,1)S(1)} %get-tuple-element.65), channel_id=1, source_target_pairs={{0,1},{1,0},{2,3},{3,2},{4,5},{5,4},{6,7},{7,6},{8,9},{9,8},{10,11... | collective-permute-start | bytes 196616 | tf_op jit(solution)/shard_map/ppermute | solution.py:27
  40.5 4.3 %collective-permute-start.9 = (bf16[16,2048]{1,0:T(8,128)(2,1)S(1)}, bf16[16,2048]{1,0:T(8,128)(2,1)S(1)}, u32[]{:S(2)}, u32[]{:S(2)}) collective-permute-start(bf16[16,2048]{1,0:T(8,128)(2,1)S(1)} %get-tuple-element.66), channel_id=1, source_target_pairs={{0,2},{1,3},{2,0},{3,1},{4,6},{5,7},{6,4},{7,5},{8,10},{9,11},{10,... | collective-permute-start | bytes 196616 | tf_op jit(solution)/shard_map/ppermute | solution.py:27
  44.8 5.5 %collective-permute-start.11 = (bf16[16,2048]{1,0:T(8,128)(2,1)S(1)}, bf16[16,2048]{1,0:T(8,128)(2,1)S(1)}, u32[]{:S(2)}, u32[]{:S(2)}) collective-permute-start(bf16[16,2048]{1,0:T(8,128)(2,1)S(1)} %shard_map.102), channel_id=1, source_target_pairs={{0,12},{1,13},{2,14},{3,15},{4,8},{5,9},{6,10},{7,11},{8,20},{9,21... | collective-permute-start | bytes 196616 | tf_op jit(solution)/shard_map/ppermute | solution.py:27
  45.5 5.5 %collective-permute-start.10 = (bf16[16,2048]{1,0:T(8,128)(2,1)S(1)}, bf16[16,2048]{1,0:T(8,128)(2,1)S(1)}, u32[]{:S(2)}, u32[]{:S(2)}) collective-permute-start(bf16[16,2048]{1,0:T(8,128)(2,1)S(1)} %shard_map.102), channel_id=1, source_target_pairs={{0,8},{1,9},{2,10},{3,11},{4,12},{5,13},{6,14},{7,15},{8,16},{9,17... | collective-permute-start | bytes 196616 | tf_op jit(solution)/shard_map/ppermute | solution.py:27
  50.3 42.0 %collective-permute-start.26 = (bf16[160,2048]{1,0:T(8,128)(2,1)S(1)}, bf16[160,2048]{1,0:T(8,128)(2,1)S(1)}, u32[]{:S(2)}, u32[]{:S(2)}) collective-permute-start(bf16[160,2048]{1,0:T(8,128)(2,1)S(1)} %get-tuple-element.86), channel_id=1, source_target_pairs={{0,24},{1,25},{2,26},{3,27},{4,28},{5,29},{6,30},{7,31},{8,0},{9,1... | collective-permute-start | bytes 1966088 | tf_op jit(solution)/shard_map/ppermute | solution.py:27
  51.1 41.2 %collective-permute-start.27 = (bf16[160,2048]{1,0:T(8,128)(2,1)S(1)}, bf16[160,2048]{1,0:T(8,128)(2,1)S(1)}, u32[]{:S(2)}, u32[]{:S(2)}) collective-permute-start(bf16[160,2048]{1,0:T(8,128)(2,1)S(1)} %get-tuple-element.87), channel_id=1, source_target_pairs={{0,24},{1,25},{2,26},{3,27},{4,28},{5,29},{6,30},{7,31},{8,0},{9,1... | collective-permute-start | bytes 1966088 | tf_op jit(solution)/shard_map/ppermute | solution.py:27
  51.2 41.1 %collective-permute-start.28 = (bf16[160,2048]{1,0:T(8,128)(2,1)S(1)}, bf16[160,2048]{1,0:T(8,128)(2,1)S(1)}, u32[]{:S(2)}, u32[]{:S(2)}) collective-permute-start(bf16[160,2048]{1,0:T(8,128)(2,1)S(1)} %get-tuple-element.88), channel_id=1, source_target_pairs={{0,24},{1,25},{2,26},{3,27},{4,28},{5,29},{6,30},{7,31},{8,0},{9,1... | collective-permute-start | bytes 1966088 | tf_op jit(solution)/shard_map/ppermute | solution.py:27
  52.1 5.5 %collective-permute-start.14 = (bf16[16,2048]{1,0:T(8,128)(2,1)S(1)}, bf16[16,2048]{1,0:T(8,128)(2,1)S(1)}, u32[]{:S(2)}, u32[]{:S(2)}) collective-permute-start(bf16[16,2048]{1,0:T(8,128)(2,1)S(1)} %get-tuple-element.67.refs_0_), channel_id=1, source_target_pairs={{0,3},{1,2},{2,1},{3,0},{4,7},{5,6},{6,5},{7,4},{8,11},{9,10},{10,... | collective-permute-start | bytes 196616 | tf_op jit(solution)/shard_map/ppermute | solution.py:27
  54.5 9.7 %collective-permute-start.13 = (bf16[16,2048]{1,0:T(8,128)(2,1)S(1)}, bf16[16,2048]{1,0:T(8,128)(2,1)S(1)}, u32[]{:S(2)}, u32[]{:S(2)}) collective-permute-start(bf16[16,2048]{1,0:T(8,128)(2,1)S(1)} %get-tuple-element.67.refs_0_), channel_id=1, source_target_pairs={{0,2},{1,3},{2,0},{3,1},{4,6},{5,7},{6,4},{7,5},{8,10},{9,11},{10,... | collective-permute-start | bytes 196616 | tf_op jit(solution)/shard_map/ppermute | solution.py:27
  57.6 6.7 %collective-permute-start.12 = (bf16[16,2048]{1,0:T(8,128)(2,1)S(1)}, bf16[16,2048]{1,0:T(8,128)(2,1)S(1)}, u32[]{:S(2)}, u32[]{:S(2)}) collective-permute-start(bf16[16,2048]{1,0:T(8,128)(2,1)S(1)} %get-tuple-element.67.refs_0_), channel_id=1, source_target_pairs={{0,1},{1,0},{2,3},{3,2},{4,5},{5,4},{6,7},{7,6},{8,9},{9,8},{10,11... | collective-permute-start | bytes 196616 | tf_op jit(solution)/shard_map/ppermute | solution.py:27
  66.6 5.3 %collective-permute-start.18 = (bf16[16,2048]{1,0:T(8,128)(2,1)S(1)}, bf16[16,2048]{1,0:T(8,128)(2,1)S(1)}, u32[]{:S(2)}, u32[]{:S(2)}) collective-permute-start(bf16[16,2048]{1,0:T(8,128)(2,1)S(1)} %get-tuple-element.81), channel_id=1, source_target_pairs={{0,3},{1,2},{2,1},{3,0},{4,7},{5,6},{6,5},{7,4},{8,11},{9,10},{10,... | collective-permute-start | bytes 196616 | tf_op jit(solution)/shard_map/ppermute | solution.py:27
  68.6 5.1 %collective-permute-start.19 = (bf16[16,2048]{1,0:T(8,128)(2,1)S(1)}, bf16[16,2048]{1,0:T(8,128)(2,1)S(1)}, u32[]{:S(2)}, u32[]{:S(2)}) collective-permute-start(bf16[16,2048]{1,0:T(8,128)(2,1)S(1)} %get-tuple-element.82), channel_id=1, source_target_pairs={{0,1},{1,0},{2,3},{3,2},{4,5},{5,4},{6,7},{7,6},{8,9},{9,8},{10,11... | collective-permute-start | bytes 196616 | tf_op jit(solution)/shard_map/ppermute | solution.py:27
  71.9 4.3 %collective-permute-start.20 = (bf16[16,2048]{1,0:T(8,128)(2,1)S(1)}, bf16[16,2048]{1,0:T(8,128)(2,1)S(1)}, u32[]{:S(2)}, u32[]{:S(2)}) collective-permute-start(bf16[16,2048]{1,0:T(8,128)(2,1)S(1)} %get-tuple-element.83), channel_id=1, source_target_pairs={{0,2},{1,3},{2,0},{3,1},{4,6},{5,7},{6,4},{7,5},{8,10},{9,11},{10,... | collective-permute-start | bytes 196616 | tf_op jit(solution)/shard_map/ppermute | solution.py:27
  76.2 6.0 %collective-permute-start.22 = (bf16[16,2048]{1,0:T(8,128)(2,1)S(1)}, bf16[16,2048]{1,0:T(8,128)(2,1)S(1)}, u32[]{:S(2)}, u32[]{:S(2)}) collective-permute-start(bf16[16,2048]{1,0:T(8,128)(2,1)S(1)} %shard_map.104), channel_id=1, source_target_pairs={{0,12},{1,13},{2,14},{3,15},{4,8},{5,9},{6,10},{7,11},{8,20},{9,21... | collective-permute-start | bytes 196616 | tf_op jit(solution)/shard_map/ppermute | solution.py:27
  76.3 6.0 %collective-permute-start.21 = (bf16[16,2048]{1,0:T(8,128)(2,1)S(1)}, bf16[16,2048]{1,0:T(8,128)(2,1)S(1)}, u32[]{:S(2)}, u32[]{:S(2)}) collective-permute-start(bf16[16,2048]{1,0:T(8,128)(2,1)S(1)} %shard_map.104), channel_id=1, source_target_pairs={{0,8},{1,9},{2,10},{3,11},{4,12},{5,13},{6,14},{7,15},{8,16},{9,17... | collective-permute-start | bytes 196616 | tf_op jit(solution)/shard_map/ppermute | solution.py:27
  82.4 5.7 %collective-permute-start.25 = (bf16[16,2048]{1,0:T(8,128)(2,1)S(1)}, bf16[16,2048]{1,0:T(8,128)(2,1)S(1)}, u32[]{:S(2)}, u32[]{:S(2)}) collective-permute-start(bf16[16,2048]{1,0:T(8,128)(2,1)S(1)} %get-tuple-element.84.refs_0_), channel_id=1, source_target_pairs={{0,3},{1,2},{2,1},{3,0},{4,7},{5,6},{6,5},{7,4},{8,11},{9,10},{10,... | collective-permute-start | bytes 196616 | tf_op jit(solution)/shard_map/ppermute | solution.py:27
  84.5 4.3 %collective-permute-start.24 = (bf16[16,2048]{1,0:T(8,128)(2,1)S(1)}, bf16[16,2048]{1,0:T(8,128)(2,1)S(1)}, u32[]{:S(2)}, u32[]{:S(2)}) collective-permute-start(bf16[16,2048]{1,0:T(8,128)(2,1)S(1)} %get-tuple-element.84.refs_0_), channel_id=1, source_target_pairs={{0,2},{1,3},{2,0},{3,1},{4,6},{5,7},{6,4},{7,5},{8,10},{9,11},{10,... | collective-permute-start | bytes 196616 | tf_op jit(solution)/shard_map/ppermute | solution.py:27
  88.1 4.3 %collective-permute-start.23 = (bf16[16,2048]{1,0:T(8,128)(2,1)S(1)}, bf16[16,2048]{1,0:T(8,128)(2,1)S(1)}, u32[]{:S(2)}, u32[]{:S(2)}) collective-permute-start(bf16[16,2048]{1,0:T(8,128)(2,1)S(1)} %get-tuple-element.84.refs_0_), channel_id=1, source_target_pairs={{0,1},{1,0},{2,3},{3,2},{4,5},{5,4},{6,7},{7,6},{8,9},{9,8},{10,11... | collective-permute-start | bytes 196616 | tf_op jit(solution)/shard_map/ppermute | solution.py:27
  94.8 5.2 %collective-permute-start.29 = (bf16[16,2048]{1,0:T(8,128)(2,1)S(1)}, bf16[16,2048]{1,0:T(8,128)(2,1)S(1)}, u32[]{:S(2)}, u32[]{:S(2)}) collective-permute-start(bf16[16,2048]{1,0:T(8,128)(2,1)S(1)} %get-tuple-element.90), channel_id=1, source_target_pairs={{0,3},{1,2},{2,1},{3,0},{4,7},{5,6},{6,5},{7,4},{8,11},{9,10},{10,... | collective-permute-start | bytes 196616 | tf_op jit(solution)/shard_map/ppermute | solution.py:27
  96.5 4.3 %collective-permute-start.30 = (bf16[16,2048]{1,0:T(8,128)(2,1)S(1)}, bf16[16,2048]{1,0:T(8,128)(2,1)S(1)}, u32[]{:S(2)}, u32[]{:S(2)}) collective-permute-start(bf16[16,2048]{1,0:T(8,128)(2,1)S(1)} %get-tuple-element.91), channel_id=1, source_target_pairs={{0,1},{1,0},{2,3},{3,2},{4,5},{5,4},{6,7},{7,6},{8,9},{9,8},{10,11... | collective-permute-start | bytes 196616 | tf_op jit(solution)/shard_map/ppermute | solution.py:27
  97.8 4.3 %collective-permute-start.31 = (bf16[16,2048]{1,0:T(8,128)(2,1)S(1)}, bf16[16,2048]{1,0:T(8,128)(2,1)S(1)}, u32[]{:S(2)}, u32[]{:S(2)}) collective-permute-start(bf16[16,2048]{1,0:T(8,128)(2,1)S(1)} %get-tuple-element.92), channel_id=1, source_target_pairs={{0,2},{1,3},{2,0},{3,1},{4,6},{5,7},{6,4},{7,5},{8,10},{9,11},{10,... | collective-permute-start | bytes 196616 | tf_op jit(solution)/shard_map/ppermute | solution.py:27
  102.2 7.5 %collective-permute-start.33 = (bf16[16,2048]{1,0:T(8,128)(2,1)S(1)}, bf16[16,2048]{1,0:T(8,128)(2,1)S(1)}, u32[]{:S(2)}, u32[]{:S(2)}) collective-permute-start(bf16[16,2048]{1,0:T(8,128)(2,1)S(1)} %shard_map.106), channel_id=1, source_target_pairs={{0,12},{1,13},{2,14},{3,15},{4,8},{5,9},{6,10},{7,11},{8,20},{9,21... | collective-permute-start | bytes 196616 | tf_op jit(solution)/shard_map/ppermute | solution.py:27
  102.2 7.4 %collective-permute-start.32 = (bf16[16,2048]{1,0:T(8,128)(2,1)S(1)}, bf16[16,2048]{1,0:T(8,128)(2,1)S(1)}, u32[]{:S(2)}, u32[]{:S(2)}) collective-permute-start(bf16[16,2048]{1,0:T(8,128)(2,1)S(1)} %shard_map.106), channel_id=1, source_target_pairs={{0,8},{1,9},{2,10},{3,11},{4,12},{5,13},{6,14},{7,15},{8,16},{9,17... | collective-permute-start | bytes 196616 | tf_op jit(solution)/shard_map/ppermute | solution.py:27
  109.7 5.2 %collective-permute-start.36 = (bf16[16,2048]{1,0:T(8,128)(2,1)S(1)}, bf16[16,2048]{1,0:T(8,128)(2,1)S(1)}, u32[]{:S(2)}, u32[]{:S(2)}) collective-permute-start(bf16[16,2048]{1,0:T(8,128)(2,1)S(1)} %get-tuple-element.93.refs_0_), channel_id=1, source_target_pairs={{0,3},{1,2},{2,1},{3,0},{4,7},{5,6},{6,5},{7,4},{8,11},{9,10},{10,... | collective-permute-start | bytes 196616 | tf_op jit(solution)/shard_map/ppermute | solution.py:27
  109.8 5.2 %collective-permute-start.35 = (bf16[16,2048]{1,0:T(8,128)(2,1)S(1)}, bf16[16,2048]{1,0:T(8,128)(2,1)S(1)}, u32[]{:S(2)}, u32[]{:S(2)}) collective-permute-start(bf16[16,2048]{1,0:T(8,128)(2,1)S(1)} %get-tuple-element.93.refs_0_), channel_id=1, source_target_pairs={{0,2},{1,3},{2,0},{3,1},{4,6},{5,7},{6,4},{7,5},{8,10},{9,11},{10,... | collective-permute-start | bytes 196616 | tf_op jit(solution)/shard_map/ppermute | solution.py:27
  111.8 4.3 %collective-permute-start.34 = (bf16[16,2048]{1,0:T(8,128)(2,1)S(1)}, bf16[16,2048]{1,0:T(8,128)(2,1)S(1)}, u32[]{:S(2)}, u32[]{:S(2)}) collective-permute-start(bf16[16,2048]{1,0:T(8,128)(2,1)S(1)} %get-tuple-element.93.refs_0_), channel_id=1, source_target_pairs={{0,1},{1,0},{2,3},{3,2},{4,5},{5,4},{6,7},{7,6},{8,9},{9,8},{10,11... | collective-permute-start | bytes 196616 | tf_op jit(solution)/shard_map/ppermute | solution.py:27
  118.3 5.6 %collective-permute-start.37 = (bf16[16,2048]{1,0:T(8,128)(2,1)S(1)}, bf16[16,2048]{1,0:T(8,128)(2,1)S(1)}, u32[]{:S(2)}, u32[]{:S(2)}) collective-permute-start(bf16[16,2048]{1,0:T(8,128)(2,1)S(1)} %get-tuple-element.96), channel_id=1, source_target_pairs={{0,3},{1,2},{2,1},{3,0},{4,7},{5,6},{6,5},{7,4},{8,11},{9,10},{10,... | collective-permute-start | bytes 196616 | tf_op jit(solution)/shard_map/ppermute | solution.py:27
  119.4 4.9 %collective-permute-start.38 = (bf16[16,2048]{1,0:T(8,128)(2,1)S(1)}, bf16[16,2048]{1,0:T(8,128)(2,1)S(1)}, u32[]{:S(2)}, u32[]{:S(2)}) collective-permute-start(bf16[16,2048]{1,0:T(8,128)(2,1)S(1)} %get-tuple-element.97), channel_id=1, source_target_pairs={{0,1},{1,0},{2,3},{3,2},{4,5},{5,4},{6,7},{7,6},{8,9},{9,8},{10,11... | collective-permute-start | bytes 196616 | tf_op jit(solution)/shard_map/ppermute | solution.py:27
  120.0 4.3 %collective-permute-start.39 = (bf16[16,2048]{1,0:T(8,128)(2,1)S(1)}, bf16[16,2048]{1,0:T(8,128)(2,1)S(1)}, u32[]{:S(2)}, u32[]{:S(2)}) collective-permute-start(bf16[16,2048]{1,0:T(8,128)(2,1)S(1)} %get-tuple-element.98), channel_id=1, source_target_pairs={{0,2},{1,3},{2,0},{3,1},{4,6},{5,7},{6,4},{7,5},{8,10},{9,11},{10,... | collective-permute-start | bytes 196616 | tf_op jit(solution)/shard_map/ppermute | solution.py:27
  124.4 4.9 %collective-permute-start.40 = (bf16[8,2048]{1,0:T(8,128)(2,1)S(1)}, bf16[8,2048]{1,0:T(8,128)(2,1)S(1)}, u32[]{:S(2)}, u32[]{:S(2)}) collective-permute-start(bf16[8,2048]{1,0:T(8,128)(2,1)S(1)} %slice.17), channel_id=1, source_target_pairs={{0,4},{1,5},{2,6},{3,7},{4,0},{5,1},{6,2},{7,3},{8,12},{9,13},{10,... | collective-permute-start | bytes 98312 | tf_op jit(solution)/shard_map/ppermute | solution.py:27

commit v12 on v10

--- a/solution.py
+++ b/solution.py
@@ -139,7 +139,10 @@
     choices = []
     for slot_count, spare_count in layer_counts:
         slot, spare, refs = refs[:slot_count], refs[slot_count:slot_count + spare_count], refs[slot_count + spare_count:]
-        choices.append((slot, [spare[0].at[i] for i in range(3)] if spare_count == 1 else spare))
+        whole = []
+        for ref in spare:
+            whole += [ref.at[i] for i in range(ref.shape[0])] if len(ref.shape) == 3 else [ref]
+        choices.append((slot, whole))
     segments, members = lax.axis_size("segment"), lax.axis_size("expert")
     group = group_of(lax.axis_index("segment"), tick_idx, segments)
     expert = lax.axis_index("expert") // (members // EXPERTS)
@@ -373,6 +376,7 @@
     if users[0]:
         slots.append(loaded(weights, (True, True, False), 1))
     late = stacked(lax.optimization_barrier((*spare_all, arrived[both_first(outer)[-1]]))[:3], 1)
+    first_late = filled(lax.optimization_barrier((*spare_all, arrived[both_first(outer)[-1]]))[:1], 1)[0]
     near = [swapped(late, users[opening])] if opening < TICKS else []
     own = state[0]
     before = run_layer(arrived, arrived, own, [(slot, []) for slot in slots], tick_idx=0, tok_dev=tok_dev, ends=False)
@@ -389,6 +393,9 @@
             carried=before if tick_idx == 0 else None,
         )
         got = [moved(parts[j], j, 0) for j in both_first(outer)]
+        if tick_idx == 0:
+            far = [moved(lax.optimization_barrier((first_late, parts[0]))[0], 0, -1)]
+            rest_late = stacked(lax.optimization_barrier((*spare_all[1:], parts[0]))[:2], 1)
         if tick_idx == 0 and not users[0]:
             tied = lax.optimization_barrier((*weights, parts[0]))[:3]
             gate = loaded(tied[:1], (True,), 1)
@@ -400,11 +407,12 @@
         across = moved(total, outer, 1)
         along = moved(total, 0, 1)
         if tick_idx == 0:
-            far = [moved(lax.optimization_barrier((late, total))[0], 0, -1)]
             if not users[0]:
-                tied = lax.optimization_barrier((*weights, total))[:3]
+                tied = lax.optimization_barrier((*weights, parts[0]))[:3]
                 slots.append(gate + loaded(tied[1:], (True, False), 1))
         own, normed = arriving(along, across, norm_gain, tick_idx + 1)
+        if tick_idx == 0:
+            far.append(moved(lax.optimization_barrier((rest_late, normed))[0], 0, -1))
         rows = spread(normed)
 
 

time: 111 us -> 135 us (1.22)
  waiting for transfers between devices: 36.7 us -> 56.1 us
  local copies, waits for them, and re-layouts: 0.02 us -> 2.86 us
  Pallas kernels: 23.8 us -> 26.2 us
    ppermute x36 -> x37, waiting for transfers between devices: 36.7 us -> 56.1 us  [moved(): return lax.ppermute(value, BOTH, pairs)]
    unnamed x8 -> x12, local copies, waits for them, and re-layouts: 0.01 us -> 2.85 us
    pallas_call x1 -> x2, Pallas kernels: 1.51 us -> 2.81 us  [stacked(): pl.pallas_call(functools.partial(stack_kernel, group=group), out_shape=pl...]
    pallas_call x2 -> x3, Pallas kernels: 2.43 us -> 3.49 us  [filled(): pl.pallas_call(functools.partial(fill_kernel, group=group), out_shape=[pl...]
    ppermute x36 -> x37, starting transfers between devices: 47.2 us -> 46.6 us  [moved(): return lax.ppermute(value, BOTH, pairs)]
  transfers between devices with their start and end apart: 37 -> 38, of which waited for: 26 -> 28; matrix products, arithmetic and copies ran while one was open for 0% -> 0% of each run, Pallas kernels for 16% -> 14%
where the time goes in v12:
time: 135 us
  waiting for transfers between devices  56.1 us (42%)
  starting transfers between devices  48.5 us (36%)
  Pallas kernels  26.2 us (19%)
  local copies, waits for them, and re-layouts  2.86 us (2%)
    ppermute x37, waiting for transfers between devices, moved(): return lax.ppermute(value, BOTH, pairs)  56.1 us
    ppermute x37, starting transfers between devices, moved(): return lax.ppermute(value, BOTH, pairs)  46.6 us
    pallas_call x3, Pallas kernels, loaded(): pl.pallas_call(functools.partial(load_kernel, turned=turned, group=group)...  9.78 us
    pallas_call x5, Pallas kernels, run_layer(): pl.pallas_call(functools.partial(layer_kernel, tick_idx=tick_idx, blocks=...  9.36 us
    pallas_call x3, Pallas kernels, filled(): pl.pallas_call(functools.partial(fill_kernel, group=group), out_shape=[pl...  3.49 us
    unnamed x12, local copies, waits for them, and re-layouts  2.85 us
    pallas_call x2, Pallas kernels, stacked(): pl.pallas_call(functools.partial(stack_kernel, group=group), out_shape=pl...  2.81 us
  transfers between devices with their start and end apart: 38, of which 28 were waited for; matrix products, arithmetic and copies ran while one was open for 0% of the time, Pallas kernels for 14%

profile of v12, /device:TPU:0, one launch (start us, length us, event | category | flops | bytes accessed | tf_op | source)
XLA Modules:
  0.0 134.6 jit_solution(13128584763593538175)
XLA Ops:
  4.2 4.1 %collective-permute-start = (bf16[8,2176]{1,0:T(8,128)(2,1)S(1)}, bf16[8,2176]{1,0:T(8,128)(2,1)S(1)}, u32[]{:S(2)}, u32[]{:S(2)}) collective-permute-start(bf16[8,2176]{1,0:T(8,128)(2,1)S(1)} %shard_map.100.first_ref), channel_id=1, source_target_pairs={{0,4},{1,5},{2,6},{3,7},{4,0},{5,1},{6,2},{7,3},{8,12},{9,13},{10,... | collective-permute-start | bytes 104456 | tf_op jit(solution)/shard_map/ppermute | solution.py:27
  8.3 2.3 %collective-permute-done.second_ref = bf16[8,2176]{1,0:T(8,128)(2,1)S(1)} collective-permute-done((bf16[8,2176]{1,0:T(8,128)(2,1)S(1)}, bf16[8,2176]{1,0:T(8,128)(2,1)S(1)}, u32[]{:S(2)}, u32[]{:S(2)}) %collective-permute-start) | collective-permute-done | bytes 34848 | tf_op jit(solution)/shard_map/ppermute | solution.py:27
  10.6 1.6 %collective-permute-start.2 = (bf16[16,2176]{1,0:T(8,128)(2,1)S(1)}, bf16[16,2176]{1,0:T(8,128)(2,1)S(1)}, u32[]{:S(2)}, u32[]{:S(2)}) collective-permute-start(bf16[16,2176]{1,0:T(8,128)(2,1)S(1)} %shard_map.101.refs_0_.refs_4_), channel_id=1, source_target_pairs={{0,2},{1,3},{2,0},{3,1},{4,6},{5,7},{6,4},{7,5},{8,10},{9,11},{10,... | collective-permute-start | bytes 208904 | tf_op jit(solution)/shard_map/ppermute | solution.py:27
  12.2 2.8 %collective-permute-done.2.refs_2_.refs_6_ = bf16[16,2176]{1,0:T(8,128)(2,1)S(1)} collective-permute-done((bf16[16,2176]{1,0:T(8,128)(2,1)S(1)}, bf16[16,2176]{1,0:T(8,128)(2,1)S(1)}, u32[]{:S(2)}, u32[]{:S(2)}) %collective-permute-start.2) | collective-permute-done | bytes 69664 | tf_op jit(solution)/shard_map/ppermute | solution.py:27
  15.0 1.5 %stack.2 = bf16[3,160,2048]{2,1,0:T(8,128)(2,1)S(1)} custom-call(bf16[2,160,2048]{2,1,0:T(8,128)(2,1)} %bitcast.33, bf16[2,160,2048]{2,1,0:T(8,128)(2,1)} %bitcast.26, bf16[2,160,2048]{2,1,0:T(8,128)(2,1)} %bitcast.29), custom_call_target="tpu_custom_call" | custom-call | tf_op jit(solution)/shard_map/stack/pallas_call | solution.py:321
  16.5 1.9 %collective-permute-start.15 = (bf16[3,160,2048]{2,1,0:T(8,128)(2,1)S(1)}, bf16[3,160,2048]{2,1,0:T(8,128)(2,1)S(1)}, u32[]{:S(2)}, u32[]{:S(2)}) collective-permute-start(bf16[3,160,2048]{2,1,0:T(8,128)(2,1)S(1)} %stack.2), channel_id=1, source_target_pairs={{0,8},{1,9},{2,10},{3,11},{4,12},{5,13},{6,14},{7,15},{8,0},{9,1},... | collective-permute-start | bytes 5898248 | tf_op jit(solution)/shard_map/ppermute | solution.py:58
  18.5 1.3 fill.4
  20.5 1.5 %collective-permute-start.6 = (bf16[160,2048]{1,0:T(8,128)(2,1)S(1)}, bf16[160,2048]{1,0:T(8,128)(2,1)S(1)}, u32[]{:S(2)}, u32[]{:S(2)}) collective-permute-start(bf16[160,2048]{1,0:T(8,128)(2,1)S(1)} %get-tuple-element.60), channel_id=1, source_target_pairs={{0,24},{1,25},{2,26},{3,27},{4,28},{5,29},{6,30},{7,31},{8,0},{9,1... | collective-permute-start | bytes 1966088 | tf_op jit(solution)/shard_map/ppermute | solution.py:27
  22.1 1.7 %collective-permute-start.1 = (bf16[16,2176]{1,0:T(8,128)(2,1)S(1)}, bf16[16,2176]{1,0:T(8,128)(2,1)S(1)}, u32[]{:S(2)}, u32[]{:S(2)}) collective-permute-start(bf16[16,2176]{1,0:T(8,128)(2,1)S(1)} %shard_map.101.refs_0_.refs_4_), channel_id=1, source_target_pairs={{0,1},{1,0},{2,3},{3,2},{4,5},{5,4},{6,7},{7,6},{8,9},{9,8},{10,11... | collective-permute-start | bytes 208904 | tf_op jit(solution)/shard_map/ppermute | solution.py:27
  23.8 2.6 %collective-permute-done.1.refs_1_.refs_5_ = bf16[16,2176]{1,0:T(8,128)(2,1)S(1)} collective-permute-done((bf16[16,2176]{1,0:T(8,128)(2,1)S(1)}, bf16[16,2176]{1,0:T(8,128)(2,1)S(1)}, u32[]{:S(2)}, u32[]{:S(2)}) %collective-permute-start.1) | collective-permute-done | bytes 69664 | tf_op jit(solution)/shard_map/ppermute | solution.py:27
  26.4 2.5 %collective-permute-start.3 = (bf16[16,2176]{1,0:T(8,128)(2,1)S(1)}, bf16[16,2176]{1,0:T(8,128)(2,1)S(1)}, u32[]{:S(2)}, u32[]{:S(2)}) collective-permute-start(bf16[16,2176]{1,0:T(8,128)(2,1)S(1)} %shard_map.101.refs_0_.refs_4_), channel_id=1, source_target_pairs={{0,3},{1,2},{2,1},{3,0},{4,7},{5,6},{6,5},{7,4},{8,11},{9,10},{10,... | collective-permute-start | bytes 208904 | tf_op jit(solution)/shard_map/ppermute | solution.py:27
  28.9 4.4 %load.3 = (bf16[2048,640]{1,0:T(8,128)(2,1)S(1)}, bf16[2048,640]{1,0:T(8,128)(2,1)S(1)}, bf16[640,2048]{1,0:T(8,128)(2,1)S(1)}) custom-call(bf16[2,640,2048]{2,1,0:T(8,128)(2,1)} %bitcast.24, bf16[2,640,2048]{2,1,0:T(8,128)(2,1)} %bitcast.20, bf16[2,640,2048]{2,1,0:T(8,128)(2,1)} %bitcast.22), custom_call_target="tpu_custom_call" | custom-call | tf_op jit(solution)/shard_map/load/pallas_call | solution.py:292
  33.2 1.5 %layer.5.refs_9_ = f32[64,2048]{1,0:T(8,128)S(1)} custom-call(bf16[16,2176]{1,0:T(8,128)(2,1)S(1)} %shard_map.101.refs_0_.refs_4_, bf16[16,2176]{1,0:T(8,128)(2,1)S(1)} %collective-permute-done.1.refs_1_.refs_5_, bf16[16,2176]{1,0:T(8,128)(2,1)S(1)} %collective-permute-done.2.refs_2_.refs_6_, bf16[16,2176]{1,0:T(8,128)(2,1)S(1)} %collective-permute-done.3.refs_3_.refs_7_, ...), custom_call_target="tpu_custom_call" | custom-call | flops 503316480 | bytes 7864320 | tf_op jit(solution)/shard_map/layer/pallas_call | solution.py:194
  34.8 5.8 %collective-permute-done.6.refs_12_.refs_14_ = bf16[160,2048]{1,0:T(8,128)(2,1)S(1)} collective-permute-done((bf16[160,2048]{1,0:T(8,128)(2,1)S(1)}, bf16[160,2048]{1,0:T(8,128)(2,1)S(1)}, u32[]{:S(2)}, u32[]{:S(2)}) %collective-permute-start.6) | collective-permute-done | bytes 655392 | tf_op jit(solution)/shard_map/ppermute | solution.py:27
  41.4 2.5 %collective-permute-start.7 = (bf16[16,2048]{1,0:T(8,128)(2,1)S(1)}, bf16[16,2048]{1,0:T(8,128)(2,1)S(1)}, u32[]{:S(2)}, u32[]{:S(2)}) collective-permute-start(bf16[16,2048]{1,0:T(8,128)(2,1)S(1)} %get-tuple-element.62), channel_id=1, source_target_pairs={{0,3},{1,2},{2,1},{3,0},{4,7},{5,6},{6,5},{7,4},{8,11},{9,10},{10,... | collective-permute-start | bytes 196616 | tf_op jit(solution)/shard_map/ppermute | solution.py:27
  45.0 1.7 %collective-permute-done.7.refs_1_ = bf16[16,2048]{1,0:T(8,128)(2,1)S(1)} collective-permute-done((bf16[16,2048]{1,0:T(8,128)(2,1)S(1)}, bf16[16,2048]{1,0:T(8,128)(2,1)S(1)}, u32[]{:S(2)}, u32[]{:S(2)}) %collective-permute-start.7) | collective-permute-done | bytes 65568 | tf_op jit(solution)/shard_map/ppermute | solution.py:27
  46.7 2.3 %collective-permute-done.8.refs_2_ = bf16[16,2048]{1,0:T(8,128)(2,1)S(1)} collective-permute-done((bf16[16,2048]{1,0:T(8,128)(2,1)S(1)}, bf16[16,2048]{1,0:T(8,128)(2,1)S(1)}, u32[]{:S(2)}, u32[]{:S(2)}) %collective-permute-start.8) | collective-permute-done | bytes 65568 | tf_op jit(solution)/shard_map/ppermute | solution.py:27
  49.7 3.9 %collective-permute-start.11 = (bf16[16,2048]{1,0:T(8,128)(2,1)S(1)}, bf16[16,2048]{1,0:T(8,128)(2,1)S(1)}, u32[]{:S(2)}, u32[]{:S(2)}) collective-permute-start(bf16[16,2048]{1,0:T(8,128)(2,1)S(1)} %shard_map.102), channel_id=1, source_target_pairs={{0,12},{1,13},{2,14},{3,15},{4,8},{5,9},{6,10},{7,11},{8,20},{9,21... | collective-permute-start | bytes 196616 | tf_op jit(solution)/shard_map/ppermute | solution.py:27
  54.9 1.9 %collective-permute-done.11.across_ref = bf16[16,2048]{1,0:T(8,128)(2,1)S(1)} collective-permute-done((bf16[16,2048]{1,0:T(8,128)(2,1)S(1)}, bf16[16,2048]{1,0:T(8,128)(2,1)S(1)}, u32[]{:S(2)}, u32[]{:S(2)}) %collective-permute-start.11) | collective-permute-done | bytes 65568 | tf_op jit(solution)/shard_map/ppermute | solution.py:27
  58.8 1.4 %collective-permute-start.24 = (bf16[160,2048]{1,0:T(8,128)(2,1)S(1)}, bf16[160,2048]{1,0:T(8,128)(2,1)S(1)}, u32[]{:S(2)}, u32[]{:S(2)}) collective-permute-start(bf16[160,2048]{1,0:T(8,128)(2,1)S(1)} %fill.5), channel_id=1, source_target_pairs={{0,24},{1,25},{2,26},{3,27},{4,28},{5,29},{6,30},{7,31},{8,0},{9,1... | collective-permute-start | bytes 1966088 | tf_op jit(solution)/shard_map/ppermute | solution.py:27
  60.2 1.5 %collective-permute-start.12 = (bf16[16,2048]{1,0:T(8,128)(2,1)S(1)}, bf16[16,2048]{1,0:T(8,128)(2,1)S(1)}, u32[]{:S(2)}, u32[]{:S(2)}) collective-permute-start(bf16[16,2048]{1,0:T(8,128)(2,1)S(1)} %get-tuple-element.65.refs_0_), channel_id=1, source_target_pairs={{0,1},{1,0},{2,3},{3,2},{4,5},{5,4},{6,7},{7,6},{8,9},{9,8},{10,11... | collective-permute-start | bytes 196616 | tf_op jit(solution)/shard_map/ppermute | solution.py:27
  61.7 2.8 %collective-permute-done.12.refs_1_ = bf16[16,2048]{1,0:T(8,128)(2,1)S(1)} collective-permute-done((bf16[16,2048]{1,0:T(8,128)(2,1)S(1)}, bf16[16,2048]{1,0:T(8,128)(2,1)S(1)}, u32[]{:S(2)}, u32[]{:S(2)}) %collective-permute-start.12) | collective-permute-done | bytes 65568 | tf_op jit(solution)/shard_map/ppermute | solution.py:27
  64.5 2.5 %load.4.refs_15_ = bf16[2048,640]{1,0:T(8,128)(2,1)S(1)} custom-call(bf16[2,640,2048]{2,1,0:T(8,128)(2,1)} %bitcast.25), custom_call_target="tpu_custom_call" | custom-call | tf_op jit(solution)/shard_map/load/pallas_call | solution.py:292
  67.0 2.9 %load.5 = (bf16[2048,640]{1,0:T(8,128)(2,1)S(1)}, bf16[640,2048]{1,0:T(8,128)(2,1)S(1)}) custom-call(bf16[2,640,2048]{2,1,0:T(8,128)(2,1)} %bitcast.21, bf16[2,640,2048]{2,1,0:T(8,128)(2,1)} %bitcast.23), custom_call_target="tpu_custom_call" | custom-call | tf_op jit(solution)/shard_map/load/pallas_call | solution.py:292
  70.0 2.3 %layer.7 = (f32[16,2048]{1,0:T(8,128)S(1)}, bf16[16,2048]{1,0:T(8,128)(2,1)S(1)}, bf16[16,2048]{1,0:T(8,128)(2,1)S(1)}, bf16[16,2048]{1,0:T(8,128)(2,1)S(1)}) custom-call(bf16[16,2048]{1,0:T(8,128)(2,1)S(1)} %get-tuple-element.65.refs_0_, bf16[16,2048]{1,0:T(8,128)(2,1)S(1)} %collective-permute-done.12.refs_1_, ...), custom_call_target="tpu_custom_call" | custom-call | flops 629145600 | bytes 9830400 | tf_op jit(solution)/shard_map/layer/pallas_call | solution.py:194
  72.3 3.0 %collective-permute-start.16 = (bf16[16,2048]{1,0:T(8,128)(2,1)S(1)}, bf16[16,2048]{1,0:T(8,128)(2,1)S(1)}, u32[]{:S(2)}, u32[]{:S(2)}) collective-permute-start(bf16[16,2048]{1,0:T(8,128)(2,1)S(1)} %get-tuple-element.76), channel_id=1, source_target_pairs={{0,3},{1,2},{2,1},{3,0},{4,7},{5,6},{6,5},{7,4},{8,11},{9,10},{10,... | collective-permute-start | bytes 196616 | tf_op jit(solution)/shard_map/ppermute | solution.py:27
  75.3 1.5 %collective-permute-start.17 = (bf16[16,2048]{1,0:T(8,128)(2,1)S(1)}, bf16[16,2048]{1,0:T(8,128)(2,1)S(1)}, u32[]{:S(2)}, u32[]{:S(2)}) collective-permute-start(bf16[16,2048]{1,0:T(8,128)(2,1)S(1)} %get-tuple-element.77), channel_id=1, source_target_pairs={{0,1},{1,0},{2,3},{3,2},{4,5},{5,4},{6,7},{7,6},{8,9},{9,8},{10,11... | collective-permute-start | bytes 196616 | tf_op jit(solution)/shard_map/ppermute | solution.py:27
  77.9 1.6 %collective-permute-done.17.refs_2_ = bf16[16,2048]{1,0:T(8,128)(2,1)S(1)} collective-permute-done((bf16[16,2048]{1,0:T(8,128)(2,1)S(1)}, bf16[16,2048]{1,0:T(8,128)(2,1)S(1)}, u32[]{:S(2)}, u32[]{:S(2)}) %collective-permute-start.17) | collective-permute-done | bytes 65568 | tf_op jit(solution)/shard_map/ppermute | solution.py:27
  79.5 1.5 %collective-permute-done.18.refs_3_ = bf16[16,2048]{1,0:T(8,128)(2,1)S(1)} collective-permute-done((bf16[16,2048]{1,0:T(8,128)(2,1)S(1)}, bf16[16,2048]{1,0:T(8,128)(2,1)S(1)}, u32[]{:S(2)}, u32[]{:S(2)}) %collective-permute-start.18) | collective-permute-done | bytes 65568 | tf_op jit(solution)/shard_map/ppermute | solution.py:27
  81.1 1.5 %collective-permute-start.20 = (bf16[16,2048]{1,0:T(8,128)(2,1)S(1)}, bf16[16,2048]{1,0:T(8,128)(2,1)S(1)}, u32[]{:S(2)}, u32[]{:S(2)}) collective-permute-start(bf16[16,2048]{1,0:T(8,128)(2,1)S(1)} %shard_map.104), channel_id=1, source_target_pairs={{0,12},{1,13},{2,14},{3,15},{4,8},{5,9},{6,10},{7,11},{8,20},{9,21... | collective-permute-start | bytes 196616 | tf_op jit(solution)/shard_map/ppermute | solution.py:27
  82.6 2.2 %collective-permute-done.19.along_ref = bf16[16,2048]{1,0:T(8,128)(2,1)S(1)} collective-permute-done((bf16[16,2048]{1,0:T(8,128)(2,1)S(1)}, bf16[16,2048]{1,0:T(8,128)(2,1)S(1)}, u32[]{:S(2)}, u32[]{:S(2)}) %collective-permute-start.19) | collective-permute-done | bytes 65568 | tf_op jit(solution)/shard_map/ppermute | solution.py:27
  84.8 3.3 %collective-permute-done.20.across_ref = bf16[16,2048]{1,0:T(8,128)(2,1)S(1)} collective-permute-done((bf16[16,2048]{1,0:T(8,128)(2,1)S(1)}, bf16[16,2048]{1,0:T(8,128)(2,1)S(1)}, u32[]{:S(2)}, u32[]{:S(2)}) %collective-permute-start.20) | collective-permute-done | bytes 65568 | tf_op jit(solution)/shard_map/ppermute | solution.py:27
  89.0 2.8 %collective-permute-start.23 = (bf16[16,2048]{1,0:T(8,128)(2,1)S(1)}, bf16[16,2048]{1,0:T(8,128)(2,1)S(1)}, u32[]{:S(2)}, u32[]{:S(2)}) collective-permute-start(bf16[16,2048]{1,0:T(8,128)(2,1)S(1)} %get-tuple-element.79.refs_0_), channel_id=1, source_target_pairs={{0,3},{1,2},{2,1},{3,0},{4,7},{5,6},{6,5},{7,4},{8,11},{9,10},{10,... | collective-permute-start | bytes 196616 | tf_op jit(solution)/shard_map/ppermute | solution.py:27
  91.8 1.5 %collective-permute-done.21.refs_1_ = bf16[16,2048]{1,0:T(8,128)(2,1)S(1)} collective-permute-done((bf16[16,2048]{1,0:T(8,128)(2,1)S(1)}, bf16[16,2048]{1,0:T(8,128)(2,1)S(1)}, u32[]{:S(2)}, u32[]{:S(2)}) %collective-permute-start.21) | collective-permute-done | bytes 65568 | tf_op jit(solution)/shard_map/ppermute | solution.py:27
  93.3 1.5 %collective-permute-done.23.refs_3_ = bf16[16,2048]{1,0:T(8,128)(2,1)S(1)} collective-permute-done((bf16[16,2048]{1,0:T(8,128)(2,1)S(1)}, bf16[16,2048]{1,0:T(8,128)(2,1)S(1)}, u32[]{:S(2)}, u32[]{:S(2)}) %collective-permute-start.23) | collective-permute-done | bytes 65568 | tf_op jit(solution)/shard_map/ppermute | solution.py:27
  94.7 2.4 %layer.8 = (f32[16,2048]{1,0:T(8,128)S(1)}, bf16[16,2048]{1,0:T(8,128)(2,1)S(1)}, bf16[16,2048]{1,0:T(8,128)(2,1)S(1)}, bf16[16,2048]{1,0:T(8,128)(2,1)S(1)}) custom-call(bf16[16,2048]{1,0:T(8,128)(2,1)S(1)} %get-tuple-element.79.refs_0_, bf16[16,2048]{1,0:T(8,128)(2,1)S(1)} %collective-permute-done.21.refs_1_, ...), custom_call_target="tpu_custom_call" | custom-call | flops 629145600 | bytes 9830400 | tf_op jit(solution)/shard_map/layer/pallas_call | solution.py:194
  97.2 2.3 %collective-permute-start.26 = (bf16[16,2048]{1,0:T(8,128)(2,1)S(1)}, bf16[16,2048]{1,0:T(8,128)(2,1)S(1)}, u32[]{:S(2)}, u32[]{:S(2)}) collective-permute-start(bf16[16,2048]{1,0:T(8,128)(2,1)S(1)} %get-tuple-element.86), channel_id=1, source_target_pairs={{0,3},{1,2},{2,1},{3,0},{4,7},{5,6},{6,5},{7,4},{8,11},{9,10},{10,... | collective-permute-start | bytes 196616 | tf_op jit(solution)/shard_map/ppermute | solution.py:27
  100.7 1.7 %collective-permute-done.26.refs_1_ = bf16[16,2048]{1,0:T(8,128)(2,1)S(1)} collective-permute-done((bf16[16,2048]{1,0:T(8,128)(2,1)S(1)}, bf16[16,2048]{1,0:T(8,128)(2,1)S(1)}, u32[]{:S(2)}, u32[]{:S(2)}) %collective-permute-start.26) | collective-permute-done | bytes 65568 | tf_op jit(solution)/shard_map/ppermute | solution.py:27
  102.4 1.3 collective-permute-done.27.refs_2_
  104.5 1.9 %collective-permute-start.30 = (bf16[16,2048]{1,0:T(8,128)(2,1)S(1)}, bf16[16,2048]{1,0:T(8,128)(2,1)S(1)}, u32[]{:S(2)}, u32[]{:S(2)}) collective-permute-start(bf16[16,2048]{1,0:T(8,128)(2,1)S(1)} %shard_map.106), channel_id=1, source_target_pairs={{0,12},{1,13},{2,14},{3,15},{4,8},{5,9},{6,10},{7,11},{8,20},{9,21... | collective-permute-start | bytes 196616 | tf_op jit(solution)/shard_map/ppermute | solution.py:27
  106.4 1.8 %collective-permute-done.29.along_ref = bf16[16,2048]{1,0:T(8,128)(2,1)S(1)} collective-permute-done((bf16[16,2048]{1,0:T(8,128)(2,1)S(1)}, bf16[16,2048]{1,0:T(8,128)(2,1)S(1)}, u32[]{:S(2)}, u32[]{:S(2)}) %collective-permute-start.29) | collective-permute-done | bytes 65568 | tf_op jit(solution)/shard_map/ppermute | solution.py:27
  108.2 3.9 %collective-permute-done.30.across_ref = bf16[16,2048]{1,0:T(8,128)(2,1)S(1)} collective-permute-done((bf16[16,2048]{1,0:T(8,128)(2,1)S(1)}, bf16[16,2048]{1,0:T(8,128)(2,1)S(1)}, u32[]{:S(2)}, u32[]{:S(2)}) %collective-permute-start.30) | collective-permute-done | bytes 65568 | tf_op jit(solution)/shard_map/ppermute | solution.py:27
  113.0 2.7 %collective-permute-start.33 = (bf16[16,2048]{1,0:T(8,128)(2,1)S(1)}, bf16[16,2048]{1,0:T(8,128)(2,1)S(1)}, u32[]{:S(2)}, u32[]{:S(2)}) collective-permute-start(bf16[16,2048]{1,0:T(8,128)(2,1)S(1)} %get-tuple-element.89.refs_0_), channel_id=1, source_target_pairs={{0,3},{1,2},{2,1},{3,0},{4,7},{5,6},{6,5},{7,4},{8,11},{9,10},{10,... | collective-permute-start | bytes 196616 | tf_op jit(solution)/shard_map/ppermute | solution.py:27
  115.7 1.5 %collective-permute-done.31.refs_1_ = bf16[16,2048]{1,0:T(8,128)(2,1)S(1)} collective-permute-done((bf16[16,2048]{1,0:T(8,128)(2,1)S(1)}, bf16[16,2048]{1,0:T(8,128)(2,1)S(1)}, u32[]{:S(2)}, u32[]{:S(2)}) %collective-permute-start.31) | collective-permute-done | bytes 65568 | tf_op jit(solution)/shard_map/ppermute | solution.py:27
  118.7 2.3 %layer.9 = (f32[16,2048]{1,0:T(8,128)S(1)}, bf16[16,2048]{1,0:T(8,128)(2,1)S(1)}, bf16[16,2048]{1,0:T(8,128)(2,1)S(1)}, bf16[16,2048]{1,0:T(8,128)(2,1)S(1)}) custom-call(bf16[16,2048]{1,0:T(8,128)(2,1)S(1)} %get-tuple-element.89.refs_0_, bf16[16,2048]{1,0:T(8,128)(2,1)S(1)} %collective-permute-done.31.refs_1_, ...), custom_call_target="tpu_custom_call" | custom-call | flops 629145600 | bytes 9830400 | tf_op jit(solution)/shard_map/layer/pallas_call | solution.py:194
  121.0 1.6 %collective-permute-start.36 = (bf16[16,2048]{1,0:T(8,128)(2,1)S(1)}, bf16[16,2048]{1,0:T(8,128)(2,1)S(1)}, u32[]{:S(2)}, u32[]{:S(2)}) collective-permute-start(bf16[16,2048]{1,0:T(8,128)(2,1)S(1)} %get-tuple-element.94), channel_id=1, source_target_pairs={{0,2},{1,3},{2,0},{3,1},{4,6},{5,7},{6,4},{7,5},{8,10},{9,11},{10,... | collective-permute-start | bytes 196616 | tf_op jit(solution)/shard_map/ppermute | solution.py:27
  126.8 2.2 %collective-permute-done.34 = bf16[16,2048]{1,0:T(8,128)(2,1)S(1)} collective-permute-done((bf16[16,2048]{1,0:T(8,128)(2,1)S(1)}, bf16[16,2048]{1,0:T(8,128)(2,1)S(1)}, u32[]{:S(2)}, u32[]{:S(2)}) %collective-permute-start.34) | collective-permute-done | bytes 65568 | tf_op jit(solution)/shard_map/ppermute | solution.py:27
  129.7 4.2 %collective-permute-done.37 = bf16[8,2048]{1,0:T(8,128)(2,1)S(1)} collective-permute-done((bf16[8,2048]{1,0:T(8,128)(2,1)S(1)}, bf16[8,2048]{1,0:T(8,128)(2,1)S(1)}, u32[]{:S(2)}, u32[]{:S(2)}) %collective-permute-start.37) | collective-permute-done | bytes 32800 | tf_op jit(solution)/shard_map/ppermute | solution.py:27
  (64 shorter events, 23.1 us)
Async XLA Ops:
  1.1 0.8 copy-start
  1.9 0.7 copy-start.2
  2.6 0.7 copy-start.4
  3.3 0.7 copy-start.5
  4.2 6.4 %collective-permute-start = (bf16[8,2176]{1,0:T(8,128)(2,1)S(1)}, bf16[8,2176]{1,0:T(8,128)(2,1)S(1)}, u32[]{:S(2)}, u32[]{:S(2)}) collective-permute-start(bf16[8,2176]{1,0:T(8,128)(2,1)S(1)} %shard_map.100.first_ref), channel_id=1, source_target_pairs={{0,4},{1,5},{2,6},{3,7},{4,0},{5,1},{6,2},{7,3},{8,12},{9,13},{10,... | collective-permute-start | bytes 104456 | tf_op jit(solution)/shard_map/ppermute | solution.py:27
  10.6 4.4 %collective-permute-start.2 = (bf16[16,2176]{1,0:T(8,128)(2,1)S(1)}, bf16[16,2176]{1,0:T(8,128)(2,1)S(1)}, u32[]{:S(2)}, u32[]{:S(2)}) collective-permute-start(bf16[16,2176]{1,0:T(8,128)(2,1)S(1)} %shard_map.101.refs_0_.refs_4_), channel_id=1, source_target_pairs={{0,2},{1,3},{2,0},{3,1},{4,6},{5,7},{6,4},{7,5},{8,10},{9,11},{10,... | collective-permute-start | bytes 208904 | tf_op jit(solution)/shard_map/ppermute | solution.py:27
  16.5 53.4 %collective-permute-start.15 = (bf16[3,160,2048]{2,1,0:T(8,128)(2,1)S(1)}, bf16[3,160,2048]{2,1,0:T(8,128)(2,1)S(1)}, u32[]{:S(2)}, u32[]{:S(2)}) collective-permute-start(bf16[3,160,2048]{2,1,0:T(8,128)(2,1)S(1)} %stack.2), channel_id=1, source_target_pairs={{0,8},{1,9},{2,10},{3,11},{4,12},{5,13},{6,14},{7,15},{8,0},{9,1},... | collective-permute-start | bytes 5898248 | tf_op jit(solution)/shard_map/ppermute | solution.py:58
  18.4 16.4 %collective-permute-start.4 = (bf16[160,2048]{1,0:T(8,128)(2,1)S(1)}, bf16[160,2048]{1,0:T(8,128)(2,1)S(1)}, u32[]{:S(2)}, u32[]{:S(2)}) collective-permute-start(bf16[160,2048]{1,0:T(8,128)(2,1)S(1)} %fill.3), channel_id=1, source_target_pairs={{0,24},{1,25},{2,26},{3,27},{4,28},{5,29},{6,30},{7,31},{8,0},{9,1... | collective-permute-start | bytes 1966088 | tf_op jit(solution)/shard_map/ppermute | solution.py:27
  19.8 15.0 %collective-permute-start.5 = (bf16[160,2048]{1,0:T(8,128)(2,1)S(1)}, bf16[160,2048]{1,0:T(8,128)(2,1)S(1)}, u32[]{:S(2)}, u32[]{:S(2)}) collective-permute-start(bf16[160,2048]{1,0:T(8,128)(2,1)S(1)} %get-tuple-element.59), channel_id=1, source_target_pairs={{0,24},{1,25},{2,26},{3,27},{4,28},{5,29},{6,30},{7,31},{8,0},{9,1... | collective-permute-start | bytes 1966088 | tf_op jit(solution)/shard_map/ppermute | solution.py:27
  20.5 20.1 %collective-permute-start.6 = (bf16[160,2048]{1,0:T(8,128)(2,1)S(1)}, bf16[160,2048]{1,0:T(8,128)(2,1)S(1)}, u32[]{:S(2)}, u32[]{:S(2)}) collective-permute-start(bf16[160,2048]{1,0:T(8,128)(2,1)S(1)} %get-tuple-element.60), channel_id=1, source_target_pairs={{0,24},{1,25},{2,26},{3,27},{4,28},{5,29},{6,30},{7,31},{8,0},{9,1... | collective-permute-start | bytes 1966088 | tf_op jit(solution)/shard_map/ppermute | solution.py:27
  22.1 4.3 %collective-permute-start.1 = (bf16[16,2176]{1,0:T(8,128)(2,1)S(1)}, bf16[16,2176]{1,0:T(8,128)(2,1)S(1)}, u32[]{:S(2)}, u32[]{:S(2)}) collective-permute-start(bf16[16,2176]{1,0:T(8,128)(2,1)S(1)} %shard_map.101.refs_0_.refs_4_), channel_id=1, source_target_pairs={{0,1},{1,0},{2,3},{3,2},{4,5},{5,4},{6,7},{7,6},{8,9},{9,8},{10,11... | collective-permute-start | bytes 208904 | tf_op jit(solution)/shard_map/ppermute | solution.py:27
  26.4 6.8 %collective-permute-start.3 = (bf16[16,2176]{1,0:T(8,128)(2,1)S(1)}, bf16[16,2176]{1,0:T(8,128)(2,1)S(1)}, u32[]{:S(2)}, u32[]{:S(2)}) collective-permute-start(bf16[16,2176]{1,0:T(8,128)(2,1)S(1)} %shard_map.101.refs_0_.refs_4_), channel_id=1, source_target_pairs={{0,3},{1,2},{2,1},{3,0},{4,7},{5,6},{6,5},{7,4},{8,11},{9,10},{10,... | collective-permute-start | bytes 208904 | tf_op jit(solution)/shard_map/ppermute | solution.py:27
  28.9 4.4 %copy-start.1 = (bf16[1,8,2048]{2,1,0:T(8,128)(2,1)S(1)}, bf16[1,8,2048]{2,1,0:T(8,128)(2,1)}, u32[]{:S(2)}) copy-start(bf16[1,8,2048]{2,1,0:T(8,128)(2,1)} %param.10) | copy-start | bytes 98308
  41.4 15.4 %copy-start.3 = (f32[2,1,2048]{2,1,0:T(1,128)S(1)}, f32[2,1,2048]{2,1,0:T(1,128)}, u32[]{:S(2)}) copy-start(f32[2,1,2048]{2,1,0:T(1,128)} %gain_ref.7) | copy-start | bytes 49156
  41.4 5.2 %collective-permute-start.7 = (bf16[16,2048]{1,0:T(8,128)(2,1)S(1)}, bf16[16,2048]{1,0:T(8,128)(2,1)S(1)}, u32[]{:S(2)}, u32[]{:S(2)}) collective-permute-start(bf16[16,2048]{1,0:T(8,128)(2,1)S(1)} %get-tuple-element.62), channel_id=1, source_target_pairs={{0,3},{1,2},{2,1},{3,0},{4,7},{5,6},{6,5},{7,4},{8,11},{9,10},{10,... | collective-permute-start | bytes 196616 | tf_op jit(solution)/shard_map/ppermute | solution.py:27
  44.0 5.0 %collective-permute-start.8 = (bf16[16,2048]{1,0:T(8,128)(2,1)S(1)}, bf16[16,2048]{1,0:T(8,128)(2,1)S(1)}, u32[]{:S(2)}, u32[]{:S(2)}) collective-permute-start(bf16[16,2048]{1,0:T(8,128)(2,1)S(1)} %get-tuple-element.63), channel_id=1, source_target_pairs={{0,1},{1,0},{2,3},{3,2},{4,5},{5,4},{6,7},{7,6},{8,9},{9,8},{10,11... | collective-permute-start | bytes 196616 | tf_op jit(solution)/shard_map/ppermute | solution.py:27
  44.5 4.6 %collective-permute-start.9 = (bf16[16,2048]{1,0:T(8,128)(2,1)S(1)}, bf16[16,2048]{1,0:T(8,128)(2,1)S(1)}, u32[]{:S(2)}, u32[]{:S(2)}) collective-permute-start(bf16[16,2048]{1,0:T(8,128)(2,1)S(1)} %get-tuple-element.64), channel_id=1, source_target_pairs={{0,2},{1,3},{2,0},{3,1},{4,6},{5,7},{6,4},{7,5},{8,10},{9,11},{10,... | collective-permute-start | bytes 196616 | tf_op jit(solution)/shard_map/ppermute | solution.py:27
  49.2 5.7 %collective-permute-start.10 = (bf16[16,2048]{1,0:T(8,128)(2,1)S(1)}, bf16[16,2048]{1,0:T(8,128)(2,1)S(1)}, u32[]{:S(2)}, u32[]{:S(2)}) collective-permute-start(bf16[16,2048]{1,0:T(8,128)(2,1)S(1)} %shard_map.102), channel_id=1, source_target_pairs={{0,8},{1,9},{2,10},{3,11},{4,12},{5,13},{6,14},{7,15},{8,16},{9,17... | collective-permute-start | bytes 196616 | tf_op jit(solution)/shard_map/ppermute | solution.py:27
  49.7 7.2 %collective-permute-start.11 = (bf16[16,2048]{1,0:T(8,128)(2,1)S(1)}, bf16[16,2048]{1,0:T(8,128)(2,1)S(1)}, u32[]{:S(2)}, u32[]{:S(2)}) collective-permute-start(bf16[16,2048]{1,0:T(8,128)(2,1)S(1)} %shard_map.102), channel_id=1, source_target_pairs={{0,12},{1,13},{2,14},{3,15},{4,8},{5,9},{6,10},{7,11},{8,20},{9,21... | collective-permute-start | bytes 196616 | tf_op jit(solution)/shard_map/ppermute | solution.py:27
  56.9 34.8 %collective-permute-start.25 = (bf16[2,160,2048]{2,1,0:T(8,128)(2,1)S(1)}, bf16[2,160,2048]{2,1,0:T(8,128)(2,1)S(1)}, u32[]{:S(2)}, u32[]{:S(2)}) collective-permute-start(bf16[2,160,2048]{2,1,0:T(8,128)(2,1)S(1)} %stack.3), channel_id=1, source_target_pairs={{0,24},{1,25},{2,26},{3,27},{4,28},{5,29},{6,30},{7,31},{8,0},{9,1... | collective-permute-start | bytes 3932168 | tf_op jit(solution)/shard_map/ppermute | solution.py:27
  58.8 33.0 %collective-permute-start.24 = (bf16[160,2048]{1,0:T(8,128)(2,1)S(1)}, bf16[160,2048]{1,0:T(8,128)(2,1)S(1)}, u32[]{:S(2)}, u32[]{:S(2)}) collective-permute-start(bf16[160,2048]{1,0:T(8,128)(2,1)S(1)} %fill.5), channel_id=1, source_target_pairs={{0,24},{1,25},{2,26},{3,27},{4,28},{5,29},{6,30},{7,31},{8,0},{9,1... | collective-permute-start | bytes 1966088 | tf_op jit(solution)/shard_map/ppermute | solution.py:27
  60.2 4.3 %collective-permute-start.12 = (bf16[16,2048]{1,0:T(8,128)(2,1)S(1)}, bf16[16,2048]{1,0:T(8,128)(2,1)S(1)}, u32[]{:S(2)}, u32[]{:S(2)}) collective-permute-start(bf16[16,2048]{1,0:T(8,128)(2,1)S(1)} %get-tuple-element.65.refs_0_), channel_id=1, source_target_pairs={{0,1},{1,0},{2,3},{3,2},{4,5},{5,4},{6,7},{7,6},{8,9},{9,8},{10,11... | collective-permute-start | bytes 196616 | tf_op jit(solution)/shard_map/ppermute | solution.py:27
  61.7 8.2 %collective-permute-start.13 = (bf16[16,2048]{1,0:T(8,128)(2,1)S(1)}, bf16[16,2048]{1,0:T(8,128)(2,1)S(1)}, u32[]{:S(2)}, u32[]{:S(2)}) collective-permute-start(bf16[16,2048]{1,0:T(8,128)(2,1)S(1)} %get-tuple-element.65.refs_0_), channel_id=1, source_target_pairs={{0,2},{1,3},{2,0},{3,1},{4,6},{5,7},{6,4},{7,5},{8,10},{9,11},{10,... | collective-permute-start | bytes 196616 | tf_op jit(solution)/shard_map/ppermute | solution.py:27
  64.5 5.5 %collective-permute-start.14 = (bf16[16,2048]{1,0:T(8,128)(2,1)S(1)}, bf16[16,2048]{1,0:T(8,128)(2,1)S(1)}, u32[]{:S(2)}, u32[]{:S(2)}) collective-permute-start(bf16[16,2048]{1,0:T(8,128)(2,1)S(1)} %get-tuple-element.65.refs_0_), channel_id=1, source_target_pairs={{0,3},{1,2},{2,1},{3,0},{4,7},{5,6},{6,5},{7,4},{8,11},{9,10},{10,... | collective-permute-start | bytes 196616 | tf_op jit(solution)/shard_map/ppermute | solution.py:27
  72.3 5.6 %collective-permute-start.16 = (bf16[16,2048]{1,0:T(8,128)(2,1)S(1)}, bf16[16,2048]{1,0:T(8,128)(2,1)S(1)}, u32[]{:S(2)}, u32[]{:S(2)}) collective-permute-start(bf16[16,2048]{1,0:T(8,128)(2,1)S(1)} %get-tuple-element.76), channel_id=1, source_target_pairs={{0,3},{1,2},{2,1},{3,0},{4,7},{5,6},{6,5},{7,4},{8,11},{9,10},{10,... | collective-permute-start | bytes 196616 | tf_op jit(solution)/shard_map/ppermute | solution.py:27
  75.3 4.3 %collective-permute-start.17 = (bf16[16,2048]{1,0:T(8,128)(2,1)S(1)}, bf16[16,2048]{1,0:T(8,128)(2,1)S(1)}, u32[]{:S(2)}, u32[]{:S(2)}) collective-permute-start(bf16[16,2048]{1,0:T(8,128)(2,1)S(1)} %get-tuple-element.77), channel_id=1, source_target_pairs={{0,1},{1,0},{2,3},{3,2},{4,5},{5,4},{6,7},{7,6},{8,9},{9,8},{10,11... | collective-permute-start | bytes 196616 | tf_op jit(solution)/shard_map/ppermute | solution.py:27
  76.7 4.3 %collective-permute-start.18 = (bf16[16,2048]{1,0:T(8,128)(2,1)S(1)}, bf16[16,2048]{1,0:T(8,128)(2,1)S(1)}, u32[]{:S(2)}, u32[]{:S(2)}) collective-permute-start(bf16[16,2048]{1,0:T(8,128)(2,1)S(1)} %get-tuple-element.78), channel_id=1, source_target_pairs={{0,2},{1,3},{2,0},{3,1},{4,6},{5,7},{6,4},{7,5},{8,10},{9,11},{10,... | collective-permute-start | bytes 196616 | tf_op jit(solution)/shard_map/ppermute | solution.py:27
  81.0 3.7 %collective-permute-start.19 = (bf16[16,2048]{1,0:T(8,128)(2,1)S(1)}, bf16[16,2048]{1,0:T(8,128)(2,1)S(1)}, u32[]{:S(2)}, u32[]{:S(2)}) collective-permute-start(bf16[16,2048]{1,0:T(8,128)(2,1)S(1)} %shard_map.104), channel_id=1, source_target_pairs={{0,8},{1,9},{2,10},{3,11},{4,12},{5,13},{6,14},{7,15},{8,16},{9,17... | collective-permute-start | bytes 196616 | tf_op jit(solution)/shard_map/ppermute | solution.py:27
  81.1 7.0 %collective-permute-start.20 = (bf16[16,2048]{1,0:T(8,128)(2,1)S(1)}, bf16[16,2048]{1,0:T(8,128)(2,1)S(1)}, u32[]{:S(2)}, u32[]{:S(2)}) collective-permute-start(bf16[16,2048]{1,0:T(8,128)(2,1)S(1)} %shard_map.104), channel_id=1, source_target_pairs={{0,12},{1,13},{2,14},{3,15},{4,8},{5,9},{6,10},{7,11},{8,20},{9,21... | collective-permute-start | bytes 196616 | tf_op jit(solution)/shard_map/ppermute | solution.py:27
  88.2 5.0 %collective-permute-start.21 = (bf16[16,2048]{1,0:T(8,128)(2,1)S(1)}, bf16[16,2048]{1,0:T(8,128)(2,1)S(1)}, u32[]{:S(2)}, u32[]{:S(2)}) collective-permute-start(bf16[16,2048]{1,0:T(8,128)(2,1)S(1)} %get-tuple-element.79.refs_0_), channel_id=1, source_target_pairs={{0,1},{1,0},{2,3},{3,2},{4,5},{5,4},{6,7},{7,6},{8,9},{9,8},{10,11... | collective-permute-start | bytes 196616 | tf_op jit(solution)/shard_map/ppermute | solution.py:27
  89.0 4.3 %collective-permute-start.22 = (bf16[16,2048]{1,0:T(8,128)(2,1)S(1)}, bf16[16,2048]{1,0:T(8,128)(2,1)S(1)}, u32[]{:S(2)}, u32[]{:S(2)}) collective-permute-start(bf16[16,2048]{1,0:T(8,128)(2,1)S(1)} %get-tuple-element.79.refs_0_), channel_id=1, source_target_pairs={{0,2},{1,3},{2,0},{3,1},{4,6},{5,7},{6,4},{7,5},{8,10},{9,11},{10,... | collective-permute-start | bytes 196616 | tf_op jit(solution)/shard_map/ppermute | solution.py:27
  89.0 5.7 %collective-permute-start.23 = (bf16[16,2048]{1,0:T(8,128)(2,1)S(1)}, bf16[16,2048]{1,0:T(8,128)(2,1)S(1)}, u32[]{:S(2)}, u32[]{:S(2)}) collective-permute-start(bf16[16,2048]{1,0:T(8,128)(2,1)S(1)} %get-tuple-element.79.refs_0_), channel_id=1, source_target_pairs={{0,3},{1,2},{2,1},{3,0},{4,7},{5,6},{6,5},{7,4},{8,11},{9,10},{10,... | collective-permute-start | bytes 196616 | tf_op jit(solution)/shard_map/ppermute | solution.py:27
  97.2 5.2 %collective-permute-start.26 = (bf16[16,2048]{1,0:T(8,128)(2,1)S(1)}, bf16[16,2048]{1,0:T(8,128)(2,1)S(1)}, u32[]{:S(2)}, u32[]{:S(2)}) collective-permute-start(bf16[16,2048]{1,0:T(8,128)(2,1)S(1)} %get-tuple-element.86), channel_id=1, source_target_pairs={{0,3},{1,2},{2,1},{3,0},{4,7},{5,6},{6,5},{7,4},{8,11},{9,10},{10,... | collective-permute-start | bytes 196616 | tf_op jit(solution)/shard_map/ppermute | solution.py:27
  99.4 4.3 %collective-permute-start.27 = (bf16[16,2048]{1,0:T(8,128)(2,1)S(1)}, bf16[16,2048]{1,0:T(8,128)(2,1)S(1)}, u32[]{:S(2)}, u32[]{:S(2)}) collective-permute-start(bf16[16,2048]{1,0:T(8,128)(2,1)S(1)} %get-tuple-element.87), channel_id=1, source_target_pairs={{0,1},{1,0},{2,3},{3,2},{4,5},{5,4},{6,7},{7,6},{8,9},{9,8},{10,11... | collective-permute-start | bytes 196616 | tf_op jit(solution)/shard_map/ppermute | solution.py:27
  100.2 4.3 %collective-permute-start.28 = (bf16[16,2048]{1,0:T(8,128)(2,1)S(1)}, bf16[16,2048]{1,0:T(8,128)(2,1)S(1)}, u32[]{:S(2)}, u32[]{:S(2)}) collective-permute-start(bf16[16,2048]{1,0:T(8,128)(2,1)S(1)} %get-tuple-element.88), channel_id=1, source_target_pairs={{0,2},{1,3},{2,0},{3,1},{4,6},{5,7},{6,4},{7,5},{8,10},{9,11},{10,... | collective-permute-start | bytes 196616 | tf_op jit(solution)/shard_map/ppermute | solution.py:27
  104.5 3.7 %collective-permute-start.29 = (bf16[16,2048]{1,0:T(8,128)(2,1)S(1)}, bf16[16,2048]{1,0:T(8,128)(2,1)S(1)}, u32[]{:S(2)}, u32[]{:S(2)}) collective-permute-start(bf16[16,2048]{1,0:T(8,128)(2,1)S(1)} %shard_map.106), channel_id=1, source_target_pairs={{0,8},{1,9},{2,10},{3,11},{4,12},{5,13},{6,14},{7,15},{8,16},{9,17... | collective-permute-start | bytes 196616 | tf_op jit(solution)/shard_map/ppermute | solution.py:27
  104.5 7.5 %collective-permute-start.30 = (bf16[16,2048]{1,0:T(8,128)(2,1)S(1)}, bf16[16,2048]{1,0:T(8,128)(2,1)S(1)}, u32[]{:S(2)}, u32[]{:S(2)}) collective-permute-start(bf16[16,2048]{1,0:T(8,128)(2,1)S(1)} %shard_map.106), channel_id=1, source_target_pairs={{0,12},{1,13},{2,14},{3,15},{4,8},{5,9},{6,10},{7,11},{8,20},{9,21... | collective-permute-start | bytes 196616 | tf_op jit(solution)/shard_map/ppermute | solution.py:27
  112.2 5.0 %collective-permute-start.31 = (bf16[16,2048]{1,0:T(8,128)(2,1)S(1)}, bf16[16,2048]{1,0:T(8,128)(2,1)S(1)}, u32[]{:S(2)}, u32[]{:S(2)}) collective-permute-start(bf16[16,2048]{1,0:T(8,128)(2,1)S(1)} %get-tuple-element.89.refs_0_), channel_id=1, source_target_pairs={{0,1},{1,0},{2,3},{3,2},{4,5},{5,4},{6,7},{7,6},{8,9},{9,8},{10,11... | collective-permute-start | bytes 196616 | tf_op jit(solution)/shard_map/ppermute | solution.py:27
  113.0 4.4 %collective-permute-start.32 = (bf16[16,2048]{1,0:T(8,128)(2,1)S(1)}, bf16[16,2048]{1,0:T(8,128)(2,1)S(1)}, u32[]{:S(2)}, u32[]{:S(2)}) collective-permute-start(bf16[16,2048]{1,0:T(8,128)(2,1)S(1)} %get-tuple-element.89.refs_0_), channel_id=1, source_target_pairs={{0,2},{1,3},{2,0},{3,1},{4,6},{5,7},{6,4},{7,5},{8,10},{9,11},{10,... | collective-permute-start | bytes 196616 | tf_op jit(solution)/shard_map/ppermute | solution.py:27
  113.0 5.7 %collective-permute-start.33 = (bf16[16,2048]{1,0:T(8,128)(2,1)S(1)}, bf16[16,2048]{1,0:T(8,128)(2,1)S(1)}, u32[]{:S(2)}, u32[]{:S(2)}) collective-permute-start(bf16[16,2048]{1,0:T(8,128)(2,1)S(1)} %get-tuple-element.89.refs_0_), channel_id=1, source_target_pairs={{0,3},{1,2},{2,1},{3,0},{4,7},{5,6},{6,5},{7,4},{8,11},{9,10},{10,... | collective-permute-start | bytes 196616 | tf_op jit(solution)/shard_map/ppermute | solution.py:27
  121.0 4.8 %collective-permute-start.36 = (bf16[16,2048]{1,0:T(8,128)(2,1)S(1)}, bf16[16,2048]{1,0:T(8,128)(2,1)S(1)}, u32[]{:S(2)}, u32[]{:S(2)}) collective-permute-start(bf16[16,2048]{1,0:T(8,128)(2,1)S(1)} %get-tuple-element.94), channel_id=1, source_target_pairs={{0,2},{1,3},{2,0},{3,1},{4,6},{5,7},{6,4},{7,5},{8,10},{9,11},{10,... | collective-permute-start | bytes 196616 | tf_op jit(solution)/shard_map/ppermute | solution.py:27
  122.6 4.3 %collective-permute-start.35 = (bf16[16,2048]{1,0:T(8,128)(2,1)S(1)}, bf16[16,2048]{1,0:T(8,128)(2,1)S(1)}, u32[]{:S(2)}, u32[]{:S(2)}) collective-permute-start(bf16[16,2048]{1,0:T(8,128)(2,1)S(1)} %get-tuple-element.93), channel_id=1, source_target_pairs={{0,1},{1,0},{2,3},{3,2},{4,5},{5,4},{6,7},{7,6},{8,9},{9,8},{10,11... | collective-permute-start | bytes 196616 | tf_op jit(solution)/shard_map/ppermute | solution.py:27
  123.8 5.2 %collective-permute-start.34 = (bf16[16,2048]{1,0:T(8,128)(2,1)S(1)}, bf16[16,2048]{1,0:T(8,128)(2,1)S(1)}, u32[]{:S(2)}, u32[]{:S(2)}) collective-permute-start(bf16[16,2048]{1,0:T(8,128)(2,1)S(1)} %get-tuple-element.92), channel_id=1, source_target_pairs={{0,3},{1,2},{2,1},{3,0},{4,7},{5,6},{6,5},{7,4},{8,11},{9,10},{10,... | collective-permute-start | bytes 196616 | tf_op jit(solution)/shard_map/ppermute | solution.py:27
  129.1 4.9 %collective-permute-start.37 = (bf16[8,2048]{1,0:T(8,128)(2,1)S(1)}, bf16[8,2048]{1,0:T(8,128)(2,1)S(1)}, u32[]{:S(2)}, u32[]{:S(2)}) collective-permute-start(bf16[8,2048]{1,0:T(8,128)(2,1)S(1)} %slice.17), channel_id=1, source_target_pairs={{0,4},{1,5},{2,6},{3,7},{4,0},{5,1},{6,2},{7,3},{8,12},{9,13},{10,... | collective-permute-start | bytes 98312 | tf_op jit(solution)/shard_map/ppermute | solution.py:27

commit v13 on v10

--- a/solution.py
+++ b/solution.py
@@ -389,6 +389,8 @@
             carried=before if tick_idx == 0 else None,
         )
         got = [moved(parts[j], j, 0) for j in both_first(outer)]
+        if tick_idx == 0:
+            far = [moved(lax.optimization_barrier((late, parts[0]))[0], 0, -1)]
         if tick_idx == 0 and not users[0]:
             tied = lax.optimization_barrier((*weights, parts[0]))[:3]
             gate = loaded(tied[:1], (True,), 1)
@@ -400,9 +402,8 @@
         across = moved(total, outer, 1)
         along = moved(total, 0, 1)
         if tick_idx == 0:
-            far = [moved(lax.optimization_barrier((late, total))[0], 0, -1)]
             if not users[0]:
-                tied = lax.optimization_barrier((*weights, total))[:3]
+                tied = lax.optimization_barrier((*weights, parts[0]))[:3]
                 slots.append(gate + loaded(tied[1:], (True, False), 1))
         own, normed = arriving(along, across, norm_gain, tick_idx + 1)
         rows = spread(normed)

time: 111 us -> 116 us (1.045)
  waiting for transfers between devices: 36.7 us -> 42.6 us
    ppermute x36, waiting for transfers between devices: 36.7 us -> 42.6 us  [moved(): return lax.ppermute(value, BOTH, pairs)]
  transfers between devices with their start and end apart: 37 -> 37, of which waited for: 26 -> 24; matrix products, arithmetic and copies ran while one was open for 0% -> 0% of each run, Pallas kernels for 16% -> 15%
where the time goes in v13:
time: 116 us
  starting transfers between devices  48.4 us (42%)
  waiting for transfers between devices  42.6 us (37%)
  Pallas kernels  23.8 us (21%)
    ppermute x36, starting transfers between devices, moved(): return lax.ppermute(value, BOTH, pairs)  46.4 us
    ppermute x36, waiting for transfers between devices, moved(): return lax.ppermute(value, BOTH, pairs)  42.6 us
    pallas_call x3, Pallas kernels, loaded(): pl.pallas_call(functools.partial(load_kernel, turned=turned, group=group)...  9.77 us
    pallas_call x5, Pallas kernels, run_layer(): pl.pallas_call(functools.partial(layer_kernel, tick_idx=tick_idx, blocks=...  9.35 us
    pallas_call x2, Pallas kernels, filled(): pl.pallas_call(functools.partial(fill_kernel, group=group), out_shape=[pl...  2.43 us
  transfers between devices with their start and end apart: 37, of which 24 were waited for; matrix products, arithmetic and copies ran while one was open for 0% of the time, Pallas kernels for 15%

profile of v13, /device:TPU:0, one launch (start us, length us, event | category | flops | bytes accessed | tf_op | source)
XLA Modules:
  0.0 115.8 jit_solution(1744484276313436420)
XLA Ops:
  0.0 1.1 fill.2
  1.1 2.5 %collective-permute-start.4 = (bf16[160,2048]{1,0:T(8,128)(2,1)S(1)}, bf16[160,2048]{1,0:T(8,128)(2,1)S(1)}, u32[]{:S(2)}, u32[]{:S(2)}) collective-permute-start(bf16[160,2048]{1,0:T(8,128)(2,1)S(1)} %fill.2), channel_id=1, source_target_pairs={{0,24},{1,25},{2,26},{3,27},{4,28},{5,29},{6,30},{7,31},{8,0},{9,1... | collective-permute-start | bytes 1966088 | tf_op jit(solution)/shard_map/ppermute | solution.py:27
  3.7 1.3 %fill.3 = (bf16[160,2048]{1,0:T(8,128)(2,1)S(1)}, bf16[160,2048]{1,0:T(8,128)(2,1)S(1)}) custom-call(bf16[2,160,2048]{2,1,0:T(8,128)(2,1)} %bitcast.26, bf16[2,160,2048]{2,1,0:T(8,128)(2,1)} %bitcast.28), custom_call_target="tpu_custom_call" | custom-call | tf_op jit(solution)/shard_map/fill/pallas_call | solution.py:247
  6.0 2.6 %collective-permute-start = (bf16[8,2176]{1,0:T(8,128)(2,1)S(1)}, bf16[8,2176]{1,0:T(8,128)(2,1)S(1)}, u32[]{:S(2)}, u32[]{:S(2)}) collective-permute-start(bf16[8,2176]{1,0:T(8,128)(2,1)S(1)} %shard_map.100.first_ref), channel_id=1, source_target_pairs={{0,4},{1,5},{2,6},{3,7},{4,0},{5,1},{6,2},{7,3},{8,12},{9,13},{10,... | collective-permute-start | bytes 104456 | tf_op jit(solution)/shard_map/ppermute | solution.py:27
  8.6 2.2 %collective-permute-done.second_ref = bf16[8,2176]{1,0:T(8,128)(2,1)S(1)} collective-permute-done((bf16[8,2176]{1,0:T(8,128)(2,1)S(1)}, bf16[8,2176]{1,0:T(8,128)(2,1)S(1)}, u32[]{:S(2)}, u32[]{:S(2)}) %collective-permute-start) | collective-permute-done | bytes 34848 | tf_op jit(solution)/shard_map/ppermute | solution.py:27
  10.9 1.6 %collective-permute-start.2 = (bf16[16,2176]{1,0:T(8,128)(2,1)S(1)}, bf16[16,2176]{1,0:T(8,128)(2,1)S(1)}, u32[]{:S(2)}, u32[]{:S(2)}) collective-permute-start(bf16[16,2176]{1,0:T(8,128)(2,1)S(1)} %shard_map.101.refs_0_.refs_4_), channel_id=1, source_target_pairs={{0,2},{1,3},{2,0},{3,1},{4,6},{5,7},{6,4},{7,5},{8,10},{9,11},{10,... | collective-permute-start | bytes 208904 | tf_op jit(solution)/shard_map/ppermute | solution.py:27
  12.5 2.7 %collective-permute-done.2.refs_2_.refs_6_ = bf16[16,2176]{1,0:T(8,128)(2,1)S(1)} collective-permute-done((bf16[16,2176]{1,0:T(8,128)(2,1)S(1)}, bf16[16,2176]{1,0:T(8,128)(2,1)S(1)}, u32[]{:S(2)}, u32[]{:S(2)}) %collective-permute-start.2) | collective-permute-done | bytes 69664 | tf_op jit(solution)/shard_map/ppermute | solution.py:27
  15.3 1.5 %stack.1 = bf16[3,160,2048]{2,1,0:T(8,128)(2,1)S(1)} custom-call(bf16[2,160,2048]{2,1,0:T(8,128)(2,1)} %bitcast.31, bf16[2,160,2048]{2,1,0:T(8,128)(2,1)} %bitcast.27, bf16[2,160,2048]{2,1,0:T(8,128)(2,1)} %bitcast.29), custom_call_target="tpu_custom_call" | custom-call | tf_op jit(solution)/shard_map/stack/pallas_call | solution.py:318
  16.8 1.9 %collective-permute-start.15 = (bf16[3,160,2048]{2,1,0:T(8,128)(2,1)S(1)}, bf16[3,160,2048]{2,1,0:T(8,128)(2,1)S(1)}, u32[]{:S(2)}, u32[]{:S(2)}) collective-permute-start(bf16[3,160,2048]{2,1,0:T(8,128)(2,1)S(1)} %stack.1), channel_id=1, source_target_pairs={{0,8},{1,9},{2,10},{3,11},{4,12},{5,13},{6,14},{7,15},{8,0},{9,1},... | collective-permute-start | bytes 5898248 | tf_op jit(solution)/shard_map/ppermute | solution.py:58
  18.7 2.6 %collective-permute-start.3 = (bf16[16,2176]{1,0:T(8,128)(2,1)S(1)}, bf16[16,2176]{1,0:T(8,128)(2,1)S(1)}, u32[]{:S(2)}, u32[]{:S(2)}) collective-permute-start(bf16[16,2176]{1,0:T(8,128)(2,1)S(1)} %shard_map.101.refs_0_.refs_4_), channel_id=1, source_target_pairs={{0,3},{1,2},{2,1},{3,0},{4,7},{5,6},{6,5},{7,4},{8,11},{9,10},{10,... | collective-permute-start | bytes 208904 | tf_op jit(solution)/shard_map/ppermute | solution.py:27
  21.3 3.0 %collective-permute-done.3.refs_3_.refs_7_ = bf16[16,2176]{1,0:T(8,128)(2,1)S(1)} collective-permute-done((bf16[16,2176]{1,0:T(8,128)(2,1)S(1)}, bf16[16,2176]{1,0:T(8,128)(2,1)S(1)}, u32[]{:S(2)}, u32[]{:S(2)}) %collective-permute-start.3) | collective-permute-done | bytes 69664 | tf_op jit(solution)/shard_map/ppermute | solution.py:27
  24.3 1.5 %collective-permute-start.1 = (bf16[16,2176]{1,0:T(8,128)(2,1)S(1)}, bf16[16,2176]{1,0:T(8,128)(2,1)S(1)}, u32[]{:S(2)}, u32[]{:S(2)}) collective-permute-start(bf16[16,2176]{1,0:T(8,128)(2,1)S(1)} %shard_map.101.refs_0_.refs_4_), channel_id=1, source_target_pairs={{0,1},{1,0},{2,3},{3,2},{4,5},{5,4},{6,7},{7,6},{8,9},{9,8},{10,11... | collective-permute-start | bytes 208904 | tf_op jit(solution)/shard_map/ppermute | solution.py:27
  25.8 4.3 %load.3 = (bf16[2048,640]{1,0:T(8,128)(2,1)S(1)}, bf16[2048,640]{1,0:T(8,128)(2,1)S(1)}, bf16[640,2048]{1,0:T(8,128)(2,1)S(1)}) custom-call(bf16[2,640,2048]{2,1,0:T(8,128)(2,1)} %bitcast.24, bf16[2,640,2048]{2,1,0:T(8,128)(2,1)} %bitcast.20, bf16[2,640,2048]{2,1,0:T(8,128)(2,1)} %bitcast.22), custom_call_target="tpu_custom_call" | custom-call | tf_op jit(solution)/shard_map/load/pallas_call | solution.py:289
  30.1 1.5 %layer.5.refs_9_ = f32[64,2048]{1,0:T(8,128)S(1)} custom-call(bf16[16,2176]{1,0:T(8,128)(2,1)S(1)} %shard_map.101.refs_0_.refs_4_, bf16[16,2176]{1,0:T(8,128)(2,1)S(1)} %collective-permute-done.1.refs_1_.refs_5_, bf16[16,2176]{1,0:T(8,128)(2,1)S(1)} %collective-permute-done.2.refs_2_.refs_6_, bf16[16,2176]{1,0:T(8,128)(2,1)S(1)} %collective-permute-done.3.refs_3_.refs_7_, ...), custom_call_target="tpu_custom_call" | custom-call | flops 503316480 | bytes 7864320 | tf_op jit(solution)/shard_map/layer/pallas_call | solution.py:191
  32.6 1.6 %collective-permute-start.7 = (bf16[16,2048]{1,0:T(8,128)(2,1)S(1)}, bf16[16,2048]{1,0:T(8,128)(2,1)S(1)}, u32[]{:S(2)}, u32[]{:S(2)}) collective-permute-start(bf16[16,2048]{1,0:T(8,128)(2,1)S(1)} %get-tuple-element.59), channel_id=1, source_target_pairs={{0,3},{1,2},{2,1},{3,0},{4,7},{5,6},{6,5},{7,4},{8,11},{9,10},{10,... | collective-permute-start | bytes 196616 | tf_op jit(solution)/shard_map/ppermute | solution.py:27
  34.2 1.5 %collective-permute-start.8 = (bf16[16,2048]{1,0:T(8,128)(2,1)S(1)}, bf16[16,2048]{1,0:T(8,128)(2,1)S(1)}, u32[]{:S(2)}, u32[]{:S(2)}) collective-permute-start(bf16[16,2048]{1,0:T(8,128)(2,1)S(1)} %get-tuple-element.60), channel_id=1, source_target_pairs={{0,1},{1,0},{2,3},{3,2},{4,5},{5,4},{6,7},{7,6},{8,9},{9,8},{10,11... | collective-permute-start | bytes 196616 | tf_op jit(solution)/shard_map/ppermute | solution.py:27
  36.1 1.9 %collective-permute-done.7.refs_1_ = bf16[16,2048]{1,0:T(8,128)(2,1)S(1)} collective-permute-done((bf16[16,2048]{1,0:T(8,128)(2,1)S(1)}, bf16[16,2048]{1,0:T(8,128)(2,1)S(1)}, u32[]{:S(2)}, u32[]{:S(2)}) %collective-permute-start.7) | collective-permute-done | bytes 65568 | tf_op jit(solution)/shard_map/ppermute | solution.py:27
  38.0 1.3 %collective-permute-done.8.refs_2_ = bf16[16,2048]{1,0:T(8,128)(2,1)S(1)} collective-permute-done((bf16[16,2048]{1,0:T(8,128)(2,1)S(1)}, bf16[16,2048]{1,0:T(8,128)(2,1)S(1)}, u32[]{:S(2)}, u32[]{:S(2)}) %collective-permute-start.8) | collective-permute-done | bytes 65568 | tf_op jit(solution)/shard_map/ppermute | solution.py:27
  40.0 1.7 %collective-permute-start.11 = (bf16[16,2048]{1,0:T(8,128)(2,1)S(1)}, bf16[16,2048]{1,0:T(8,128)(2,1)S(1)}, u32[]{:S(2)}, u32[]{:S(2)}) collective-permute-start(bf16[16,2048]{1,0:T(8,128)(2,1)S(1)} %shard_map.102), channel_id=1, source_target_pairs={{0,12},{1,13},{2,14},{3,15},{4,8},{5,9},{6,10},{7,11},{8,20},{9,21... | collective-permute-start | bytes 196616 | tf_op jit(solution)/shard_map/ppermute | solution.py:27
  41.7 1.8 %collective-permute-start.10 = (bf16[16,2048]{1,0:T(8,128)(2,1)S(1)}, bf16[16,2048]{1,0:T(8,128)(2,1)S(1)}, u32[]{:S(2)}, u32[]{:S(2)}) collective-permute-start(bf16[16,2048]{1,0:T(8,128)(2,1)S(1)} %shard_map.102), channel_id=1, source_target_pairs={{0,8},{1,9},{2,10},{3,11},{4,12},{5,13},{6,14},{7,15},{8,16},{9,17... | collective-permute-start | bytes 196616 | tf_op jit(solution)/shard_map/ppermute | solution.py:27
  43.5 3.7 %collective-permute-done.11.across_ref = bf16[16,2048]{1,0:T(8,128)(2,1)S(1)} collective-permute-done((bf16[16,2048]{1,0:T(8,128)(2,1)S(1)}, bf16[16,2048]{1,0:T(8,128)(2,1)S(1)}, u32[]{:S(2)}, u32[]{:S(2)}) %collective-permute-start.11) | collective-permute-done | bytes 65568 | tf_op jit(solution)/shard_map/ppermute | solution.py:27
  48.5 1.1 collective-permute-start.13
  49.6 1.6 %collective-permute-start.12 = (bf16[16,2048]{1,0:T(8,128)(2,1)S(1)}, bf16[16,2048]{1,0:T(8,128)(2,1)S(1)}, u32[]{:S(2)}, u32[]{:S(2)}) collective-permute-start(bf16[16,2048]{1,0:T(8,128)(2,1)S(1)} %get-tuple-element.62.refs_0_), channel_id=1, source_target_pairs={{0,1},{1,0},{2,3},{3,2},{4,5},{5,4},{6,7},{7,6},{8,9},{9,8},{10,11... | collective-permute-start | bytes 196616 | tf_op jit(solution)/shard_map/ppermute | solution.py:27
  51.3 2.5 %load.4.refs_15_ = bf16[2048,640]{1,0:T(8,128)(2,1)S(1)} custom-call(bf16[2,640,2048]{2,1,0:T(8,128)(2,1)} %bitcast.25), custom_call_target="tpu_custom_call" | custom-call | tf_op jit(solution)/shard_map/load/pallas_call | solution.py:289
  53.8 2.9 %load.5 = (bf16[2048,640]{1,0:T(8,128)(2,1)S(1)}, bf16[640,2048]{1,0:T(8,128)(2,1)S(1)}) custom-call(bf16[2,640,2048]{2,1,0:T(8,128)(2,1)} %bitcast.21, bf16[2,640,2048]{2,1,0:T(8,128)(2,1)} %bitcast.23), custom_call_target="tpu_custom_call" | custom-call | tf_op jit(solution)/shard_map/load/pallas_call | solution.py:289
  56.8 2.3 %layer.7 = (f32[16,2048]{1,0:T(8,128)S(1)}, bf16[16,2048]{1,0:T(8,128)(2,1)S(1)}, bf16[16,2048]{1,0:T(8,128)(2,1)S(1)}, bf16[16,2048]{1,0:T(8,128)(2,1)S(1)}) custom-call(bf16[16,2048]{1,0:T(8,128)(2,1)S(1)} %get-tuple-element.62.refs_0_, bf16[16,2048]{1,0:T(8,128)(2,1)S(1)} %collective-permute-done.12.refs_1_, ...), custom_call_target="tpu_custom_call" | custom-call | flops 629145600 | bytes 9830400 | tf_op jit(solution)/shard_map/layer/pallas_call | solution.py:191
  60.6 2.0 %collective-permute-start.18 = (bf16[16,2048]{1,0:T(8,128)(2,1)S(1)}, bf16[16,2048]{1,0:T(8,128)(2,1)S(1)}, u32[]{:S(2)}, u32[]{:S(2)}) collective-permute-start(bf16[16,2048]{1,0:T(8,128)(2,1)S(1)} %get-tuple-element.75), channel_id=1, source_target_pairs={{0,2},{1,3},{2,0},{3,1},{4,6},{5,7},{6,4},{7,5},{8,10},{9,11},{10,... | collective-permute-start | bytes 196616 | tf_op jit(solution)/shard_map/ppermute | solution.py:27
  62.6 1.8 %collective-permute-done.16.refs_1_ = bf16[16,2048]{1,0:T(8,128)(2,1)S(1)} collective-permute-done((bf16[16,2048]{1,0:T(8,128)(2,1)S(1)}, bf16[16,2048]{1,0:T(8,128)(2,1)S(1)}, u32[]{:S(2)}, u32[]{:S(2)}) %collective-permute-start.16) | collective-permute-done | bytes 65568 | tf_op jit(solution)/shard_map/ppermute | solution.py:27
  65.0 3.1 %collective-permute-start.19 = (bf16[16,2048]{1,0:T(8,128)(2,1)S(1)}, bf16[16,2048]{1,0:T(8,128)(2,1)S(1)}, u32[]{:S(2)}, u32[]{:S(2)}) collective-permute-start(bf16[16,2048]{1,0:T(8,128)(2,1)S(1)} %shard_map.104), channel_id=1, source_target_pairs={{0,8},{1,9},{2,10},{3,11},{4,12},{5,13},{6,14},{7,15},{8,16},{9,17... | collective-permute-start | bytes 196616 | tf_op jit(solution)/shard_map/ppermute | solution.py:27
  68.1 4.1 %collective-permute-done.20.across_ref = bf16[16,2048]{1,0:T(8,128)(2,1)S(1)} collective-permute-done((bf16[16,2048]{1,0:T(8,128)(2,1)S(1)}, bf16[16,2048]{1,0:T(8,128)(2,1)S(1)}, u32[]{:S(2)}, u32[]{:S(2)}) %collective-permute-start.20) | collective-permute-done | bytes 65568 | tf_op jit(solution)/shard_map/ppermute | solution.py:27
  72.6 2.1 %collective-permute-start.22 = (bf16[16,2048]{1,0:T(8,128)(2,1)S(1)}, bf16[16,2048]{1,0:T(8,128)(2,1)S(1)}, u32[]{:S(2)}, u32[]{:S(2)}) collective-permute-start(bf16[16,2048]{1,0:T(8,128)(2,1)S(1)} %get-tuple-element.76.refs_0_), channel_id=1, source_target_pairs={{0,2},{1,3},{2,0},{3,1},{4,6},{5,7},{6,4},{7,5},{8,10},{9,11},{10,... | collective-permute-start | bytes 196616 | tf_op jit(solution)/shard_map/ppermute | solution.py:27
  74.7 1.2 %collective-permute-start.21 = (bf16[16,2048]{1,0:T(8,128)(2,1)S(1)}, bf16[16,2048]{1,0:T(8,128)(2,1)S(1)}, u32[]{:S(2)}, u32[]{:S(2)}) collective-permute-start(bf16[16,2048]{1,0:T(8,128)(2,1)S(1)} %get-tuple-element.76.refs_0_), channel_id=1, source_target_pairs={{0,1},{1,0},{2,3},{3,2},{4,5},{5,4},{6,7},{7,6},{8,9},{9,8},{10,11... | collective-permute-start | bytes 196616 | tf_op jit(solution)/shard_map/ppermute | solution.py:27
  75.9 1.7 %collective-permute-done.23.refs_3_ = bf16[16,2048]{1,0:T(8,128)(2,1)S(1)} collective-permute-done((bf16[16,2048]{1,0:T(8,128)(2,1)S(1)}, bf16[16,2048]{1,0:T(8,128)(2,1)S(1)}, u32[]{:S(2)}, u32[]{:S(2)}) %collective-permute-start.23) | collective-permute-done | bytes 65568 | tf_op jit(solution)/shard_map/ppermute | solution.py:27
  77.6 1.3 %collective-permute-done.21.refs_1_ = bf16[16,2048]{1,0:T(8,128)(2,1)S(1)} collective-permute-done((bf16[16,2048]{1,0:T(8,128)(2,1)S(1)}, bf16[16,2048]{1,0:T(8,128)(2,1)S(1)}, u32[]{:S(2)}, u32[]{:S(2)}) %collective-permute-start.21) | collective-permute-done | bytes 65568 | tf_op jit(solution)/shard_map/ppermute | solution.py:27
  79.0 2.4 %layer.8 = (f32[16,2048]{1,0:T(8,128)S(1)}, bf16[16,2048]{1,0:T(8,128)(2,1)S(1)}, bf16[16,2048]{1,0:T(8,128)(2,1)S(1)}, bf16[16,2048]{1,0:T(8,128)(2,1)S(1)}) custom-call(bf16[16,2048]{1,0:T(8,128)(2,1)S(1)} %get-tuple-element.76.refs_0_, bf16[16,2048]{1,0:T(8,128)(2,1)S(1)} %collective-permute-done.21.refs_1_, ...), custom_call_target="tpu_custom_call" | custom-call | flops 629145600 | bytes 9830400 | tf_op jit(solution)/shard_map/layer/pallas_call | solution.py:191
  82.9 2.0 %collective-permute-start.27 = (bf16[16,2048]{1,0:T(8,128)(2,1)S(1)}, bf16[16,2048]{1,0:T(8,128)(2,1)S(1)}, u32[]{:S(2)}, u32[]{:S(2)}) collective-permute-start(bf16[16,2048]{1,0:T(8,128)(2,1)S(1)} %get-tuple-element.82), channel_id=1, source_target_pairs={{0,2},{1,3},{2,0},{3,1},{4,6},{5,7},{6,4},{7,5},{8,10},{9,11},{10,... | collective-permute-start | bytes 196616 | tf_op jit(solution)/shard_map/ppermute | solution.py:27
  85.0 1.7 %collective-permute-done.25.refs_1_ = bf16[16,2048]{1,0:T(8,128)(2,1)S(1)} collective-permute-done((bf16[16,2048]{1,0:T(8,128)(2,1)S(1)}, bf16[16,2048]{1,0:T(8,128)(2,1)S(1)}, u32[]{:S(2)}, u32[]{:S(2)}) %collective-permute-start.25) | collective-permute-done | bytes 65568 | tf_op jit(solution)/shard_map/ppermute | solution.py:27
  87.5 1.8 %collective-permute-start.28 = (bf16[16,2048]{1,0:T(8,128)(2,1)S(1)}, bf16[16,2048]{1,0:T(8,128)(2,1)S(1)}, u32[]{:S(2)}, u32[]{:S(2)}) collective-permute-start(bf16[16,2048]{1,0:T(8,128)(2,1)S(1)} %shard_map.106), channel_id=1, source_target_pairs={{0,8},{1,9},{2,10},{3,11},{4,12},{5,13},{6,14},{7,15},{8,16},{9,17... | collective-permute-start | bytes 196616 | tf_op jit(solution)/shard_map/ppermute | solution.py:27
  89.3 4.2 %collective-permute-done.29.across_ref = bf16[16,2048]{1,0:T(8,128)(2,1)S(1)} collective-permute-done((bf16[16,2048]{1,0:T(8,128)(2,1)S(1)}, bf16[16,2048]{1,0:T(8,128)(2,1)S(1)}, u32[]{:S(2)}, u32[]{:S(2)}) %collective-permute-start.29) | collective-permute-done | bytes 65568 | tf_op jit(solution)/shard_map/ppermute | solution.py:27
  93.6 2.0 %collective-permute-start.32 = (bf16[16,2048]{1,0:T(8,128)(2,1)S(1)}, bf16[16,2048]{1,0:T(8,128)(2,1)S(1)}, u32[]{:S(2)}, u32[]{:S(2)}) collective-permute-start(bf16[16,2048]{1,0:T(8,128)(2,1)S(1)} %get-tuple-element.83.refs_0_), channel_id=1, source_target_pairs={{0,3},{1,2},{2,1},{3,0},{4,7},{5,6},{6,5},{7,4},{8,11},{9,10},{10,... | collective-permute-start | bytes 196616 | tf_op jit(solution)/shard_map/ppermute | solution.py:27
  97.1 1.7 %collective-permute-done.32.refs_3_ = bf16[16,2048]{1,0:T(8,128)(2,1)S(1)} collective-permute-done((bf16[16,2048]{1,0:T(8,128)(2,1)S(1)}, bf16[16,2048]{1,0:T(8,128)(2,1)S(1)}, u32[]{:S(2)}, u32[]{:S(2)}) %collective-permute-start.32) | collective-permute-done | bytes 65568 | tf_op jit(solution)/shard_map/ppermute | solution.py:27
  100.3 2.3 %layer.9 = (f32[16,2048]{1,0:T(8,128)S(1)}, bf16[16,2048]{1,0:T(8,128)(2,1)S(1)}, bf16[16,2048]{1,0:T(8,128)(2,1)S(1)}, bf16[16,2048]{1,0:T(8,128)(2,1)S(1)}) custom-call(bf16[16,2048]{1,0:T(8,128)(2,1)S(1)} %get-tuple-element.83.refs_0_, bf16[16,2048]{1,0:T(8,128)(2,1)S(1)} %collective-permute-done.30.refs_1_, ...), custom_call_target="tpu_custom_call" | custom-call | flops 629145600 | bytes 9830400 | tf_op jit(solution)/shard_map/layer/pallas_call | solution.py:191
  102.6 2.0 %collective-permute-start.33 = (bf16[16,2048]{1,0:T(8,128)(2,1)S(1)}, bf16[16,2048]{1,0:T(8,128)(2,1)S(1)}, u32[]{:S(2)}, u32[]{:S(2)}) collective-permute-start(bf16[16,2048]{1,0:T(8,128)(2,1)S(1)} %get-tuple-element.86), channel_id=1, source_target_pairs={{0,3},{1,2},{2,1},{3,0},{4,7},{5,6},{6,5},{7,4},{8,11},{9,10},{10,... | collective-permute-start | bytes 196616 | tf_op jit(solution)/shard_map/ppermute | solution.py:27
  104.6 1.2 %collective-permute-start.34 = (bf16[16,2048]{1,0:T(8,128)(2,1)S(1)}, bf16[16,2048]{1,0:T(8,128)(2,1)S(1)}, u32[]{:S(2)}, u32[]{:S(2)}) collective-permute-start(bf16[16,2048]{1,0:T(8,128)(2,1)S(1)} %get-tuple-element.87), channel_id=1, source_target_pairs={{0,1},{1,0},{2,3},{3,2},{4,5},{5,4},{6,7},{7,6},{8,9},{9,8},{10,11... | collective-permute-start | bytes 196616 | tf_op jit(solution)/shard_map/ppermute | solution.py:27
  106.2 1.7 %collective-permute-done.33 = bf16[16,2048]{1,0:T(8,128)(2,1)S(1)} collective-permute-done((bf16[16,2048]{1,0:T(8,128)(2,1)S(1)}, bf16[16,2048]{1,0:T(8,128)(2,1)S(1)}, u32[]{:S(2)}, u32[]{:S(2)}) %collective-permute-start.33) | collective-permute-done | bytes 65568 | tf_op jit(solution)/shard_map/ppermute | solution.py:27
  108.8 1.2 %collective-permute-done.35 = bf16[16,2048]{1,0:T(8,128)(2,1)S(1)} collective-permute-done((bf16[16,2048]{1,0:T(8,128)(2,1)S(1)}, bf16[16,2048]{1,0:T(8,128)(2,1)S(1)}, u32[]{:S(2)}, u32[]{:S(2)}) %collective-permute-start.35) | collective-permute-done | bytes 65568 | tf_op jit(solution)/shard_map/ppermute | solution.py:27
  110.1 1.3 %collective-permute-start.36 = (bf16[8,2048]{1,0:T(8,128)(2,1)S(1)}, bf16[8,2048]{1,0:T(8,128)(2,1)S(1)}, u32[]{:S(2)}, u32[]{:S(2)}) collective-permute-start(bf16[8,2048]{1,0:T(8,128)(2,1)S(1)} %slice.17), channel_id=1, source_target_pairs={{0,4},{1,5},{2,6},{3,7},{4,0},{5,1},{6,2},{7,3},{8,12},{9,13},{10,... | collective-permute-start | bytes 98312 | tf_op jit(solution)/shard_map/ppermute | solution.py:27
  111.4 3.7 %collective-permute-done.36 = bf16[8,2048]{1,0:T(8,128)(2,1)S(1)} collective-permute-done((bf16[8,2048]{1,0:T(8,128)(2,1)S(1)}, bf16[8,2048]{1,0:T(8,128)(2,1)S(1)}, u32[]{:S(2)}, u32[]{:S(2)}) %collective-permute-start.36) | collective-permute-done | bytes 32800 | tf_op jit(solution)/shard_map/ppermute | solution.py:27
  (56 shorter events, 14.3 us)
Async XLA Ops:
  0.0 5.8 %copy-start.3 = (f32[4,1,8,2]{2,3,1,0:T(2,128)S(1)}, f32[4,1,8,2]{2,3,1,0:T(2,128)}, u32[]{:S(2)}) copy-start(f32[4,1,8,2]{2,3,1,0:T(2,128)} %param.12) | copy-start | bytes 772
  0.0 5.8 %copy-start.2 = (s32[4,1,8,2]{2,3,1,0:T(2,128)S(1)}, s32[4,1,8,2]{2,3,1,0:T(2,128)}, u32[]{:S(2)}) copy-start(s32[4,1,8,2]{2,3,1,0:T(2,128)} %param.11) | copy-start | bytes 772
  0.0 5.8 %copy-start = (bf16[1,8,2048]{2,1,0:T(8,128)(2,1)S(1)}, bf16[1,8,2048]{2,1,0:T(8,128)(2,1)}, u32[]{:S(2)}) copy-start(bf16[1,8,2048]{2,1,0:T(8,128)(2,1)} %param.10) | copy-start | bytes 98308
  0.0 5.8 %copy-start.1 = (f32[2,1,2048]{2,1,0:T(1,128)S(1)}, f32[2,1,2048]{2,1,0:T(1,128)}, u32[]{:S(2)}) copy-start(f32[2,1,2048]{2,1,0:T(1,128)} %gain_ref.7) | copy-start | bytes 49156
  1.1 30.5 %collective-permute-start.4 = (bf16[160,2048]{1,0:T(8,128)(2,1)S(1)}, bf16[160,2048]{1,0:T(8,128)(2,1)S(1)}, u32[]{:S(2)}, u32[]{:S(2)}) collective-permute-start(bf16[160,2048]{1,0:T(8,128)(2,1)S(1)} %fill.2), channel_id=1, source_target_pairs={{0,24},{1,25},{2,26},{3,27},{4,28},{5,29},{6,30},{7,31},{8,0},{9,1... | collective-permute-start | bytes 1966088 | tf_op jit(solution)/shard_map/ppermute | solution.py:27
  5.0 26.7 %collective-permute-start.5 = (bf16[160,2048]{1,0:T(8,128)(2,1)S(1)}, bf16[160,2048]{1,0:T(8,128)(2,1)S(1)}, u32[]{:S(2)}, u32[]{:S(2)}) collective-permute-start(bf16[160,2048]{1,0:T(8,128)(2,1)S(1)} %get-tuple-element.56), channel_id=1, source_target_pairs={{0,24},{1,25},{2,26},{3,27},{4,28},{5,29},{6,30},{7,31},{8,0},{9,1... | collective-permute-start | bytes 1966088 | tf_op jit(solution)/shard_map/ppermute | solution.py:27
  5.7 26.0 %collective-permute-start.6 = (bf16[160,2048]{1,0:T(8,128)(2,1)S(1)}, bf16[160,2048]{1,0:T(8,128)(2,1)S(1)}, u32[]{:S(2)}, u32[]{:S(2)}) collective-permute-start(bf16[160,2048]{1,0:T(8,128)(2,1)S(1)} %get-tuple-element.57), channel_id=1, source_target_pairs={{0,24},{1,25},{2,26},{3,27},{4,28},{5,29},{6,30},{7,31},{8,0},{9,1... | collective-permute-start | bytes 1966088 | tf_op jit(solution)/shard_map/ppermute | solution.py:27
  6.0 4.9 %collective-permute-start = (bf16[8,2176]{1,0:T(8,128)(2,1)S(1)}, bf16[8,2176]{1,0:T(8,128)(2,1)S(1)}, u32[]{:S(2)}, u32[]{:S(2)}) collective-permute-start(bf16[8,2176]{1,0:T(8,128)(2,1)S(1)} %shard_map.100.first_ref), channel_id=1, source_target_pairs={{0,4},{1,5},{2,6},{3,7},{4,0},{5,1},{6,2},{7,3},{8,12},{9,13},{10,... | collective-permute-start | bytes 104456 | tf_op jit(solution)/shard_map/ppermute | solution.py:27
  10.9 4.4 %collective-permute-start.2 = (bf16[16,2176]{1,0:T(8,128)(2,1)S(1)}, bf16[16,2176]{1,0:T(8,128)(2,1)S(1)}, u32[]{:S(2)}, u32[]{:S(2)}) collective-permute-start(bf16[16,2176]{1,0:T(8,128)(2,1)S(1)} %shard_map.101.refs_0_.refs_4_), channel_id=1, source_target_pairs={{0,2},{1,3},{2,0},{3,1},{4,6},{5,7},{6,4},{7,5},{8,10},{9,11},{10,... | collective-permute-start | bytes 208904 | tf_op jit(solution)/shard_map/ppermute | solution.py:27
  16.8 40.0 %collective-permute-start.15 = (bf16[3,160,2048]{2,1,0:T(8,128)(2,1)S(1)}, bf16[3,160,2048]{2,1,0:T(8,128)(2,1)S(1)}, u32[]{:S(2)}, u32[]{:S(2)}) collective-permute-start(bf16[3,160,2048]{2,1,0:T(8,128)(2,1)S(1)} %stack.1), channel_id=1, source_target_pairs={{0,8},{1,9},{2,10},{3,11},{4,12},{5,13},{6,14},{7,15},{8,0},{9,1},... | collective-permute-start | bytes 5898248 | tf_op jit(solution)/shard_map/ppermute | solution.py:58
  18.7 5.5 %collective-permute-start.3 = (bf16[16,2176]{1,0:T(8,128)(2,1)S(1)}, bf16[16,2176]{1,0:T(8,128)(2,1)S(1)}, u32[]{:S(2)}, u32[]{:S(2)}) collective-permute-start(bf16[16,2176]{1,0:T(8,128)(2,1)S(1)} %shard_map.101.refs_0_.refs_4_), channel_id=1, source_target_pairs={{0,3},{1,2},{2,1},{3,0},{4,7},{5,6},{6,5},{7,4},{8,11},{9,10},{10,... | collective-permute-start | bytes 208904 | tf_op jit(solution)/shard_map/ppermute | solution.py:27
  24.3 5.8 %collective-permute-start.1 = (bf16[16,2176]{1,0:T(8,128)(2,1)S(1)}, bf16[16,2176]{1,0:T(8,128)(2,1)S(1)}, u32[]{:S(2)}, u32[]{:S(2)}) collective-permute-start(bf16[16,2176]{1,0:T(8,128)(2,1)S(1)} %shard_map.101.refs_0_.refs_4_), channel_id=1, source_target_pairs={{0,1},{1,0},{2,3},{3,2},{4,5},{5,4},{6,7},{7,6},{8,9},{9,8},{10,11... | collective-permute-start | bytes 208904 | tf_op jit(solution)/shard_map/ppermute | solution.py:27
  32.5 46.5 %collective-permute-start.24 = (bf16[3,160,2048]{2,1,0:T(8,128)(2,1)S(1)}, bf16[3,160,2048]{2,1,0:T(8,128)(2,1)S(1)}, u32[]{:S(2)}, u32[]{:S(2)}) collective-permute-start(bf16[3,160,2048]{2,1,0:T(8,128)(2,1)S(1)} %stack.1), channel_id=1, source_target_pairs={{0,24},{1,25},{2,26},{3,27},{4,28},{5,29},{6,30},{7,31},{8,0},{9,1... | collective-permute-start | bytes 5898248 | tf_op jit(solution)/shard_map/ppermute | solution.py:27
  32.6 5.5 %collective-permute-start.7 = (bf16[16,2048]{1,0:T(8,128)(2,1)S(1)}, bf16[16,2048]{1,0:T(8,128)(2,1)S(1)}, u32[]{:S(2)}, u32[]{:S(2)}) collective-permute-start(bf16[16,2048]{1,0:T(8,128)(2,1)S(1)} %get-tuple-element.59), channel_id=1, source_target_pairs={{0,3},{1,2},{2,1},{3,0},{4,7},{5,6},{6,5},{7,4},{8,11},{9,10},{10,... | collective-permute-start | bytes 196616 | tf_op jit(solution)/shard_map/ppermute | solution.py:27
  34.2 5.2 %collective-permute-start.8 = (bf16[16,2048]{1,0:T(8,128)(2,1)S(1)}, bf16[16,2048]{1,0:T(8,128)(2,1)S(1)}, u32[]{:S(2)}, u32[]{:S(2)}) collective-permute-start(bf16[16,2048]{1,0:T(8,128)(2,1)S(1)} %get-tuple-element.60), channel_id=1, source_target_pairs={{0,1},{1,0},{2,3},{3,2},{4,5},{5,4},{6,7},{7,6},{8,9},{9,8},{10,11... | collective-permute-start | bytes 196616 | tf_op jit(solution)/shard_map/ppermute | solution.py:27
  35.7 4.3 %collective-permute-start.9 = (bf16[16,2048]{1,0:T(8,128)(2,1)S(1)}, bf16[16,2048]{1,0:T(8,128)(2,1)S(1)}, u32[]{:S(2)}, u32[]{:S(2)}) collective-permute-start(bf16[16,2048]{1,0:T(8,128)(2,1)S(1)} %get-tuple-element.61), channel_id=1, source_target_pairs={{0,2},{1,3},{2,0},{3,1},{4,6},{5,7},{6,4},{7,5},{8,10},{9,11},{10,... | collective-permute-start | bytes 196616 | tf_op jit(solution)/shard_map/ppermute | solution.py:27
  40.0 7.3 %collective-permute-start.11 = (bf16[16,2048]{1,0:T(8,128)(2,1)S(1)}, bf16[16,2048]{1,0:T(8,128)(2,1)S(1)}, u32[]{:S(2)}, u32[]{:S(2)}) collective-permute-start(bf16[16,2048]{1,0:T(8,128)(2,1)S(1)} %shard_map.102), channel_id=1, source_target_pairs={{0,12},{1,13},{2,14},{3,15},{4,8},{5,9},{6,10},{7,11},{8,20},{9,21... | collective-permute-start | bytes 196616 | tf_op jit(solution)/shard_map/ppermute | solution.py:27
  41.7 5.9 %collective-permute-start.10 = (bf16[16,2048]{1,0:T(8,128)(2,1)S(1)}, bf16[16,2048]{1,0:T(8,128)(2,1)S(1)}, u32[]{:S(2)}, u32[]{:S(2)}) collective-permute-start(bf16[16,2048]{1,0:T(8,128)(2,1)S(1)} %shard_map.102), channel_id=1, source_target_pairs={{0,8},{1,9},{2,10},{3,11},{4,12},{5,13},{6,14},{7,15},{8,16},{9,17... | collective-permute-start | bytes 196616 | tf_op jit(solution)/shard_map/ppermute | solution.py:27
  47.7 9.0 %collective-permute-start.14 = (bf16[16,2048]{1,0:T(8,128)(2,1)S(1)}, bf16[16,2048]{1,0:T(8,128)(2,1)S(1)}, u32[]{:S(2)}, u32[]{:S(2)}) collective-permute-start(bf16[16,2048]{1,0:T(8,128)(2,1)S(1)} %get-tuple-element.62.refs_0_), channel_id=1, source_target_pairs={{0,3},{1,2},{2,1},{3,0},{4,7},{5,6},{6,5},{7,4},{8,11},{9,10},{10,... | collective-permute-start | bytes 196616 | tf_op jit(solution)/shard_map/ppermute | solution.py:27
  48.5 8.2 %collective-permute-start.13 = (bf16[16,2048]{1,0:T(8,128)(2,1)S(1)}, bf16[16,2048]{1,0:T(8,128)(2,1)S(1)}, u32[]{:S(2)}, u32[]{:S(2)}) collective-permute-start(bf16[16,2048]{1,0:T(8,128)(2,1)S(1)} %get-tuple-element.62.refs_0_), channel_id=1, source_target_pairs={{0,2},{1,3},{2,0},{3,1},{4,6},{5,7},{6,4},{7,5},{8,10},{9,11},{10,... | collective-permute-start | bytes 196616 | tf_op jit(solution)/shard_map/ppermute | solution.py:27
  49.6 7.1 %collective-permute-start.12 = (bf16[16,2048]{1,0:T(8,128)(2,1)S(1)}, bf16[16,2048]{1,0:T(8,128)(2,1)S(1)}, u32[]{:S(2)}, u32[]{:S(2)}) collective-permute-start(bf16[16,2048]{1,0:T(8,128)(2,1)S(1)} %get-tuple-element.62.refs_0_), channel_id=1, source_target_pairs={{0,1},{1,0},{2,3},{3,2},{4,5},{5,4},{6,7},{7,6},{8,9},{9,8},{10,11... | collective-permute-start | bytes 196616 | tf_op jit(solution)/shard_map/ppermute | solution.py:27
  59.1 5.3 %collective-permute-start.16 = (bf16[16,2048]{1,0:T(8,128)(2,1)S(1)}, bf16[16,2048]{1,0:T(8,128)(2,1)S(1)}, u32[]{:S(2)}, u32[]{:S(2)}) collective-permute-start(bf16[16,2048]{1,0:T(8,128)(2,1)S(1)} %get-tuple-element.73), channel_id=1, source_target_pairs={{0,3},{1,2},{2,1},{3,0},{4,7},{5,6},{6,5},{7,4},{8,11},{9,10},{10,... | collective-permute-start | bytes 196616 | tf_op jit(solution)/shard_map/ppermute | solution.py:27
  59.9 5.0 %collective-permute-start.17 = (bf16[16,2048]{1,0:T(8,128)(2,1)S(1)}, bf16[16,2048]{1,0:T(8,128)(2,1)S(1)}, u32[]{:S(2)}, u32[]{:S(2)}) collective-permute-start(bf16[16,2048]{1,0:T(8,128)(2,1)S(1)} %get-tuple-element.74), channel_id=1, source_target_pairs={{0,1},{1,0},{2,3},{3,2},{4,5},{5,4},{6,7},{7,6},{8,9},{9,8},{10,11... | collective-permute-start | bytes 196616 | tf_op jit(solution)/shard_map/ppermute | solution.py:27
  60.6 4.3 %collective-permute-start.18 = (bf16[16,2048]{1,0:T(8,128)(2,1)S(1)}, bf16[16,2048]{1,0:T(8,128)(2,1)S(1)}, u32[]{:S(2)}, u32[]{:S(2)}) collective-permute-start(bf16[16,2048]{1,0:T(8,128)(2,1)S(1)} %get-tuple-element.75), channel_id=1, source_target_pairs={{0,2},{1,3},{2,0},{3,1},{4,6},{5,7},{6,4},{7,5},{8,10},{9,11},{10,... | collective-permute-start | bytes 196616 | tf_op jit(solution)/shard_map/ppermute | solution.py:27
  64.9 7.3 %collective-permute-start.20 = (bf16[16,2048]{1,0:T(8,128)(2,1)S(1)}, bf16[16,2048]{1,0:T(8,128)(2,1)S(1)}, u32[]{:S(2)}, u32[]{:S(2)}) collective-permute-start(bf16[16,2048]{1,0:T(8,128)(2,1)S(1)} %shard_map.104), channel_id=1, source_target_pairs={{0,12},{1,13},{2,14},{3,15},{4,8},{5,9},{6,10},{7,11},{8,20},{9,21... | collective-permute-start | bytes 196616 | tf_op jit(solution)/shard_map/ppermute | solution.py:27
  65.0 7.2 %collective-permute-start.19 = (bf16[16,2048]{1,0:T(8,128)(2,1)S(1)}, bf16[16,2048]{1,0:T(8,128)(2,1)S(1)}, u32[]{:S(2)}, u32[]{:S(2)}) collective-permute-start(bf16[16,2048]{1,0:T(8,128)(2,1)S(1)} %shard_map.104), channel_id=1, source_target_pairs={{0,8},{1,9},{2,10},{3,11},{4,12},{5,13},{6,14},{7,15},{8,16},{9,17... | collective-permute-start | bytes 196616 | tf_op jit(solution)/shard_map/ppermute | solution.py:27
  72.3 5.3 %collective-permute-start.23 = (bf16[16,2048]{1,0:T(8,128)(2,1)S(1)}, bf16[16,2048]{1,0:T(8,128)(2,1)S(1)}, u32[]{:S(2)}, u32[]{:S(2)}) collective-permute-start(bf16[16,2048]{1,0:T(8,128)(2,1)S(1)} %get-tuple-element.76.refs_0_), channel_id=1, source_target_pairs={{0,3},{1,2},{2,1},{3,0},{4,7},{5,6},{6,5},{7,4},{8,11},{9,10},{10,... | collective-permute-start | bytes 196616 | tf_op jit(solution)/shard_map/ppermute | solution.py:27
  72.6 5.0 %collective-permute-start.22 = (bf16[16,2048]{1,0:T(8,128)(2,1)S(1)}, bf16[16,2048]{1,0:T(8,128)(2,1)S(1)}, u32[]{:S(2)}, u32[]{:S(2)}) collective-permute-start(bf16[16,2048]{1,0:T(8,128)(2,1)S(1)} %get-tuple-element.76.refs_0_), channel_id=1, source_target_pairs={{0,2},{1,3},{2,0},{3,1},{4,6},{5,7},{6,4},{7,5},{8,10},{9,11},{10,... | collective-permute-start | bytes 196616 | tf_op jit(solution)/shard_map/ppermute | solution.py:27
  74.7 4.3 %collective-permute-start.21 = (bf16[16,2048]{1,0:T(8,128)(2,1)S(1)}, bf16[16,2048]{1,0:T(8,128)(2,1)S(1)}, u32[]{:S(2)}, u32[]{:S(2)}) collective-permute-start(bf16[16,2048]{1,0:T(8,128)(2,1)S(1)} %get-tuple-element.76.refs_0_), channel_id=1, source_target_pairs={{0,1},{1,0},{2,3},{3,2},{4,5},{5,4},{6,7},{7,6},{8,9},{9,8},{10,11... | collective-permute-start | bytes 196616 | tf_op jit(solution)/shard_map/ppermute | solution.py:27
  81.4 5.3 %collective-permute-start.25 = (bf16[16,2048]{1,0:T(8,128)(2,1)S(1)}, bf16[16,2048]{1,0:T(8,128)(2,1)S(1)}, u32[]{:S(2)}, u32[]{:S(2)}) collective-permute-start(bf16[16,2048]{1,0:T(8,128)(2,1)S(1)} %get-tuple-element.80), channel_id=1, source_target_pairs={{0,3},{1,2},{2,1},{3,0},{4,7},{5,6},{6,5},{7,4},{8,11},{9,10},{10,... | collective-permute-start | bytes 196616 | tf_op jit(solution)/shard_map/ppermute | solution.py:27
  82.5 4.9 %collective-permute-start.26 = (bf16[16,2048]{1,0:T(8,128)(2,1)S(1)}, bf16[16,2048]{1,0:T(8,128)(2,1)S(1)}, u32[]{:S(2)}, u32[]{:S(2)}) collective-permute-start(bf16[16,2048]{1,0:T(8,128)(2,1)S(1)} %get-tuple-element.81), channel_id=1, source_target_pairs={{0,1},{1,0},{2,3},{3,2},{4,5},{5,4},{6,7},{7,6},{8,9},{9,8},{10,11... | collective-permute-start | bytes 196616 | tf_op jit(solution)/shard_map/ppermute | solution.py:27
  82.9 4.4 %collective-permute-start.27 = (bf16[16,2048]{1,0:T(8,128)(2,1)S(1)}, bf16[16,2048]{1,0:T(8,128)(2,1)S(1)}, u32[]{:S(2)}, u32[]{:S(2)}) collective-permute-start(bf16[16,2048]{1,0:T(8,128)(2,1)S(1)} %get-tuple-element.82), channel_id=1, source_target_pairs={{0,2},{1,3},{2,0},{3,1},{4,6},{5,7},{6,4},{7,5},{8,10},{9,11},{10,... | collective-permute-start | bytes 196616 | tf_op jit(solution)/shard_map/ppermute | solution.py:27
  87.4 6.1 %collective-permute-start.29 = (bf16[16,2048]{1,0:T(8,128)(2,1)S(1)}, bf16[16,2048]{1,0:T(8,128)(2,1)S(1)}, u32[]{:S(2)}, u32[]{:S(2)}) collective-permute-start(bf16[16,2048]{1,0:T(8,128)(2,1)S(1)} %shard_map.106), channel_id=1, source_target_pairs={{0,12},{1,13},{2,14},{3,15},{4,8},{5,9},{6,10},{7,11},{8,20},{9,21... | collective-permute-start | bytes 196616 | tf_op jit(solution)/shard_map/ppermute | solution.py:27
  87.5 6.0 %collective-permute-start.28 = (bf16[16,2048]{1,0:T(8,128)(2,1)S(1)}, bf16[16,2048]{1,0:T(8,128)(2,1)S(1)}, u32[]{:S(2)}, u32[]{:S(2)}) collective-permute-start(bf16[16,2048]{1,0:T(8,128)(2,1)S(1)} %shard_map.106), channel_id=1, source_target_pairs={{0,8},{1,9},{2,10},{3,11},{4,12},{5,13},{6,14},{7,15},{8,16},{9,17... | collective-permute-start | bytes 196616 | tf_op jit(solution)/shard_map/ppermute | solution.py:27
  93.6 5.2 %collective-permute-start.32 = (bf16[16,2048]{1,0:T(8,128)(2,1)S(1)}, bf16[16,2048]{1,0:T(8,128)(2,1)S(1)}, u32[]{:S(2)}, u32[]{:S(2)}) collective-permute-start(bf16[16,2048]{1,0:T(8,128)(2,1)S(1)} %get-tuple-element.83.refs_0_), channel_id=1, source_target_pairs={{0,3},{1,2},{2,1},{3,0},{4,7},{5,6},{6,5},{7,4},{8,11},{9,10},{10,... | collective-permute-start | bytes 196616 | tf_op jit(solution)/shard_map/ppermute | solution.py:27
  95.6 4.3 %collective-permute-start.31 = (bf16[16,2048]{1,0:T(8,128)(2,1)S(1)}, bf16[16,2048]{1,0:T(8,128)(2,1)S(1)}, u32[]{:S(2)}, u32[]{:S(2)}) collective-permute-start(bf16[16,2048]{1,0:T(8,128)(2,1)S(1)} %get-tuple-element.83.refs_0_), channel_id=1, source_target_pairs={{0,2},{1,3},{2,0},{3,1},{4,6},{5,7},{6,4},{7,5},{8,10},{9,11},{10,... | collective-permute-start | bytes 196616 | tf_op jit(solution)/shard_map/ppermute | solution.py:27
  96.0 4.3 %collective-permute-start.30 = (bf16[16,2048]{1,0:T(8,128)(2,1)S(1)}, bf16[16,2048]{1,0:T(8,128)(2,1)S(1)}, u32[]{:S(2)}, u32[]{:S(2)}) collective-permute-start(bf16[16,2048]{1,0:T(8,128)(2,1)S(1)} %get-tuple-element.83.refs_0_), channel_id=1, source_target_pairs={{0,1},{1,0},{2,3},{3,2},{4,5},{5,4},{6,7},{7,6},{8,9},{9,8},{10,11... | collective-permute-start | bytes 196616 | tf_op jit(solution)/shard_map/ppermute | solution.py:27
  102.6 5.2 %collective-permute-start.33 = (bf16[16,2048]{1,0:T(8,128)(2,1)S(1)}, bf16[16,2048]{1,0:T(8,128)(2,1)S(1)}, u32[]{:S(2)}, u32[]{:S(2)}) collective-permute-start(bf16[16,2048]{1,0:T(8,128)(2,1)S(1)} %get-tuple-element.86), channel_id=1, source_target_pairs={{0,3},{1,2},{2,1},{3,0},{4,7},{5,6},{6,5},{7,4},{8,11},{9,10},{10,... | collective-permute-start | bytes 196616 | tf_op jit(solution)/shard_map/ppermute | solution.py:27
  104.6 4.3 %collective-permute-start.34 = (bf16[16,2048]{1,0:T(8,128)(2,1)S(1)}, bf16[16,2048]{1,0:T(8,128)(2,1)S(1)}, u32[]{:S(2)}, u32[]{:S(2)}) collective-permute-start(bf16[16,2048]{1,0:T(8,128)(2,1)S(1)} %get-tuple-element.87), channel_id=1, source_target_pairs={{0,1},{1,0},{2,3},{3,2},{4,5},{5,4},{6,7},{7,6},{8,9},{9,8},{10,11... | collective-permute-start | bytes 196616 | tf_op jit(solution)/shard_map/ppermute | solution.py:27
  105.7 4.3 %collective-permute-start.35 = (bf16[16,2048]{1,0:T(8,128)(2,1)S(1)}, bf16[16,2048]{1,0:T(8,128)(2,1)S(1)}, u32[]{:S(2)}, u32[]{:S(2)}) collective-permute-start(bf16[16,2048]{1,0:T(8,128)(2,1)S(1)} %get-tuple-element.88), channel_id=1, source_target_pairs={{0,2},{1,3},{2,0},{3,1},{4,6},{5,7},{6,4},{7,5},{8,10},{9,11},{10,... | collective-permute-start | bytes 196616 | tf_op jit(solution)/shard_map/ppermute | solution.py:27
  110.1 5.1 %collective-permute-start.36 = (bf16[8,2048]{1,0:T(8,128)(2,1)S(1)}, bf16[8,2048]{1,0:T(8,128)(2,1)S(1)}, u32[]{:S(2)}, u32[]{:S(2)}) collective-permute-start(bf16[8,2048]{1,0:T(8,128)(2,1)S(1)} %slice.17), channel_id=1, source_target_pairs={{0,4},{1,5},{2,6},{3,7},{4,0},{5,1},{6,2},{7,3},{8,12},{9,13},{10,... | collective-permute-start | bytes 98312 | tf_op jit(solution)/shard_map/ppermute | solution.py:27
